TPU v7x, 32 devices: a whole 2x2x4 slice. The times are simulated.
32 devices in a mesh: dp: 4 (over x, core), ctx: 2 (over y), tensor: 4 (over z).
Axes of the slice: x: 2, y: 2, z: 4, core: 2. Of those that a mesh axis runs over, the one named last changes fastest.
Arguments:
- block_input: bfloat16 [8, 1024, 2048], P('dp', 'ctx'), may hold values from -6 to 6
- out_grad: bfloat16 [8, 1024, 2048], P('dp', 'ctx'), may hold values from -6 to 6
- lengths: int32 [8], P('dp'), may hold values from 256 to 1024, as said below
- attn_gain: float32 [2048], replicated, may hold values from 0.5 to 1.5
- attn_shift: float32 [2048], replicated, may hold values from -2 to 2
- ffn_gain: float32 [2048], replicated, may hold values from 0.5 to 1.5
- ffn_shift: float32 [2048], replicated, may hold values from -2 to 2
- w_qkv: float32 [2048, 6144], P(('dp', 'ctx'), 'tensor'), may hold values from -0.125 to 0.125
- b_qkv: float32 [6144], P('tensor'), may hold values from -2 to 2
- w_proj: float32 [2048, 2048], P('tensor', ('dp', 'ctx')), may hold values from -0.5 to 0.5
- b_proj: float32 [2048], replicated, may hold values from -2 to 2
- w_in: float32 [2048, 8192], P(('dp', 'ctx'), 'tensor'), may hold values from -0.125 to 0.125
- b_in: float32 [8192], P('tensor'), may hold values from -2 to 2
- w_out: float32 [8192, 2048], P('tensor', ('dp', 'ctx')), may hold values from -0.0625 to 0.0625
- b_out: float32 [2048], replicated, may hold values from -2 to 2
Outputs:
- block_output: bfloat16 [8, 1024, 2048], P('dp', 'ctx')
- input_grad: bfloat16 [8, 1024, 2048], P('dp', 'ctx')
- grad_attn_gain: float32 [2048], replicated
- grad_attn_shift: float32 [2048], replicated
- grad_ffn_gain: float32 [2048], replicated
- grad_ffn_shift: float32 [2048], replicated
- grad_w_qkv: float32 [2048, 6144], P(('dp', 'ctx'), 'tensor')
- grad_b_qkv: float32 [6144], P('tensor')
- grad_w_proj: float32 [2048, 2048], P('tensor', ('dp', 'ctx'))
- grad_b_proj: float32 [2048], replicated
- grad_w_in: float32 [2048, 8192], P(('dp', 'ctx'), 'tensor')
- grad_b_in: float32 [8192], P('tensor')
- grad_w_out: float32 [8192, 2048], P('tensor', ('dp', 'ctx'))
- grad_b_out: float32 [2048], replicated
Inputs may be any that keep to these rules, and one draw needn't show every extreme that they name: `lengths`: one slot has exactly 1024 valid positions and one exactly a quarter of 1024.
All inputs are finite; a program needn't handle non-finite values.
Results may differ from a plain program's by a relative error of at most 0.014.
Values may be sent and summed in bfloat16 or wider, within the bound.
No kernel may reach another device: no remote copies, remote signals or barrier semaphores. Data moves between devices by JAX's collectives and lax.ppermute only.
A program may use at most 256 MiB of HBM per device.

v0:
```python
import math

import jax
import jax.numpy as jnp
from jax import lax
from jax.sharding import PartitionSpec as P

HD = 256
ROT = 64


neg_big = -1e30
inv_sqrt_two = 0.7071067811865476
inv_sqrt_tau = 0.3989422804014327


def rotary_tables(positions):
    half_rot = ROT // 2
    exponent = jnp.arange(half_rot, dtype=jnp.float32) * (2.0 / ROT)
    inv_freq = jnp.exp(-math.log(10000.0) * exponent)
    angles = positions[:, None] * inv_freq[None, :]
    return (jnp.cos(angles), jnp.sin(angles))


def rotate(values, cos_tab, sine_tab):
    half_rot = ROT // 2
    first_half = values[..., :half_rot]
    second = values[..., half_rot:ROT]
    cos_b = cos_tab[:, None, :]
    sin_b = sine_tab[:, None, :]
    return jnp.concatenate(
        [
            first_half * cos_b - second * sin_b,
            second * cos_b + first_half * sin_b,
            values[..., ROT:],
        ],
        axis=-1,
    )


def unrotate(grad_vals, cos_tab, sine_tab):
    half_rot = ROT // 2
    first_half = grad_vals[..., :half_rot]
    second = grad_vals[..., half_rot:ROT]
    cos_b = cos_tab[:, None, :]
    sin_b = sine_tab[:, None, :]
    return jnp.concatenate(
        [
            first_half * cos_b + second * sin_b,
            second * cos_b - first_half * sin_b,
            grad_vals[..., ROT:],
        ],
        axis=-1,
    )


def dot_last(left_side, right_side):
    return lax.dot_general(
        left_side, right_side, (((1,), (1,)), ((), ())), preferred_element_type=jnp.float32
    )


def dot_rows(left_side, right_side):
    return lax.dot_general(
        left_side, right_side, (((0,), (0,)), ((), ())), preferred_element_type=jnp.float32
    )


def local(
    block_input,
    out_grad,
    lengths,
    attn_gain,
    attn_shift,
    ffn_gain,
    ffn_shift,
    w_qkv,
    b_qkv,
    w_proj,
    b_proj,
    w_in,
    b_in,
    w_out,
    b_out,
):
    slots_dev, local_len, model_width = block_input.shape
    n_ctx = lax.axis_size("ctx")
    n_tensor = lax.axis_size("tensor")
    seq_len = local_len * n_ctx
    row_count = slots_dev * local_len
    heads_dev = b_qkv.shape[0] // (3 * HD)
    feat_dev = heads_dev * HD
    score_scale = 1.0 / math.sqrt(HD)
    part_len = local_len // n_tensor
    tensor_index = lax.axis_index("tensor")
    row_start = tensor_index * part_len
    first_pos = lax.axis_index("ctx") * local_len
    positions = first_pos + jnp.arange(local_len, dtype=jnp.int32)
    last_pos = first_pos + local_len - 1
    longest = jnp.max(lengths)
    valid_mask = (positions[None, :] < lengths[:, None]).astype(jnp.float32)
    mask_three = valid_mask[..., None]
    weights_low = (
        w_qkv.astype(jnp.bfloat16),
        w_proj.astype(jnp.bfloat16),
        w_in.astype(jnp.bfloat16),
        w_out.astype(jnp.bfloat16),
    )
    gathered = (
        lax.all_gather(weights_low[0], ("dp", "ctx"), axis=0, tiled=True),
        lax.all_gather(weights_low[1], ("dp", "ctx"), axis=1, tiled=True),
        lax.all_gather(weights_low[2], ("dp", "ctx"), axis=0, tiled=True),
        lax.all_gather(weights_low[3], ("dp", "ctx"), axis=1, tiled=True),
    )
    qkv_full, proj_full, in_full, out_full = gathered
    inputs = block_input.astype(jnp.float32)
    row_mean = jnp.mean(inputs, axis=-1, keepdims=True)
    centered = inputs - row_mean
    inv_std = lax.rsqrt(jnp.mean(centered * centered, axis=-1, keepdims=True) + 1e-05)
    normed = centered * inv_std
    attn_in = (normed * attn_gain + attn_shift).astype(jnp.bfloat16).reshape(row_count, model_width)
    ffn_in = (normed * ffn_gain + ffn_shift).astype(jnp.bfloat16).reshape(row_count, model_width)
    qkv = (jnp.dot(attn_in, qkv_full, preferred_element_type=jnp.float32) + b_qkv).reshape(
        slots_dev, local_len, heads_dev, 3, HD
    )
    cos_tab, sine_tab = rotary_tables(positions.astype(jnp.float32))
    queries = rotate(qkv[:, :, :, 0], cos_tab, sine_tab).astype(jnp.bfloat16)
    keys_b = rotate(qkv[:, :, :, 1], cos_tab, sine_tab).astype(jnp.bfloat16)
    values_b = qkv[:, :, :, 2].astype(jnp.bfloat16)
    keys_flat = keys_b.reshape(slots_dev, local_len, feat_dev)
    values_flat = values_b.reshape(slots_dev, local_len, feat_dev)
    start_state = (
        jnp.full((slots_dev, heads_dev, local_len), neg_big, jnp.float32),
        jnp.zeros((slots_dev, heads_dev, local_len), jnp.float32),
        jnp.zeros((slots_dev, heads_dev, local_len, HD), jnp.float32),
    )
    running = start_state
    key_part = lax.all_gather(keys_flat, "ctx", axis=1, tiled=True)
    value_part = lax.all_gather(values_flat, "ctx", axis=1, tiled=True)
    piece_len = key_part.shape[1]
    fold_block_len = math.gcd(piece_len, 512)
    block_count = piece_len // fold_block_len
    key_blocks = jnp.moveaxis(
        key_part.reshape(slots_dev, block_count, fold_block_len, heads_dev, HD), 1, 0
    )
    value_blocks = jnp.moveaxis(
        value_part.reshape(slots_dev, block_count, fold_block_len, heads_dev, HD), 1, 0
    )
    offsets = jnp.arange(block_count, dtype=jnp.int32) * fold_block_len

    def step_block(state_in, scanned):
        key_blk, value_blk, offset = scanned
        block_first = offset

        def step_compute(state_now):
            top_prev, sum_prev, acc_prev = state_now
            key_pos = block_first + jnp.arange(fold_block_len, dtype=jnp.int32)
            allowed = (key_pos[None, None, :] <= positions[None, :, None]) & (
                key_pos[None, None, :] < lengths[:, None, None]
            )
            allowed = allowed[:, None]
            scores = (
                jnp.einsum("sqhd,skhd->shqk", queries, key_blk, preferred_element_type=jnp.float32)
                * score_scale
            )
            masked = jnp.where(allowed, scores, neg_big)
            top_new = jnp.maximum(top_prev, jnp.max(masked, axis=-1))
            expo_vals = jnp.where(allowed, jnp.exp(masked - top_new[..., None]), 0.0)
            rescale = jnp.exp(top_prev - top_new)
            sum_new = sum_prev * rescale + jnp.sum(expo_vals, axis=-1)
            acc_new = acc_prev * rescale[..., None] + jnp.einsum(
                "shqk,skhd->shqd",
                expo_vals.astype(jnp.bfloat16),
                value_blk,
                preferred_element_type=jnp.float32,
            )
            return (top_new, sum_new, acc_new)

        needed = (block_first <= last_pos) & (block_first < longest)
        return (lax.cond(needed, step_compute, lambda state_now: state_now, state_in), None)

    running, no_output = lax.scan(step_block, running, (key_blocks, value_blocks, offsets))
    row_top, row_total, row_acc = running
    attended = row_acc / row_total[..., None]
    log_sum = row_top + jnp.log(row_total)
    att_low = (
        jnp.transpose(attended, (0, 2, 1, 3)).reshape(row_count, feat_dev).astype(jnp.bfloat16)
    )
    hidden = jnp.dot(ffn_in, in_full, preferred_element_type=jnp.float32) + b_in
    activated = jax.nn.gelu(hidden, approximate=False).astype(jnp.bfloat16)
    partial_out = jnp.dot(att_low, proj_full, preferred_element_type=jnp.float32) + jnp.dot(
        activated, out_full, preferred_element_type=jnp.float32
    )
    bias_sum = b_proj + b_out
    summed = (
        lax.psum(partial_out.astype(jnp.bfloat16), "tensor")
        .astype(jnp.float32)
        .reshape(slots_dev, local_len, model_width)
    )
    block_output = (mask_three * (inputs + summed + bias_sum)).astype(jnp.bfloat16)
    mask_grad = out_grad.astype(jnp.float32) * mask_three
    grad_low = mask_grad.astype(jnp.bfloat16).reshape(row_count, model_width)
    qkv_back, proj_back, in_back, out_back = gathered
    grad_w_out_local = dot_rows(activated, grad_low)
    grad_act = dot_last(grad_low, out_back)
    normal_cdf = 0.5 * (1.0 + lax.erf(hidden * inv_sqrt_two))
    normal_pdf = jnp.exp(-0.5 * hidden * hidden) * inv_sqrt_tau
    grad_hidden = (grad_act * (normal_cdf + hidden * normal_pdf)).astype(jnp.bfloat16)
    grad_b_in_local = jnp.sum(grad_hidden, axis=0, dtype=jnp.float32)
    grad_w_in_local = dot_rows(ffn_in, grad_hidden)
    grad_ffn_in = dot_last(grad_hidden, in_back)
    grad_w_proj_local = dot_rows(att_low, grad_low)
    grad_att = (
        dot_last(grad_low, proj_back)
        .astype(jnp.bfloat16)
        .reshape(slots_dev, local_len, heads_dev, HD)
    )
    row_delta = jnp.einsum("sqhd,shqd->shq", grad_att.astype(jnp.float32), attended)
    keys_all, values_all = (
        lax.all_gather(keys_flat, "ctx", axis=1, tiled=True),
        lax.all_gather(values_flat, "ctx", axis=1, tiled=True),
    )
    block_len = math.gcd(seq_len, 512)
    block_count = seq_len // block_len
    key_blocks = jnp.moveaxis(
        keys_all.reshape(slots_dev, block_count, block_len, heads_dev, HD), 1, 0
    )
    value_blocks = jnp.moveaxis(
        values_all.reshape(slots_dev, block_count, block_len, heads_dev, HD), 1, 0
    )
    offsets = jnp.arange(block_count, dtype=jnp.int32) * block_len

    def back_block(grad_q, scanned):
        key_blk, value_blk, offset = scanned

        def back_compute(grad_now):
            key_pos = offset + jnp.arange(block_len, dtype=jnp.int32)
            allowed = (key_pos[None, None, :] <= positions[None, :, None]) & (
                key_pos[None, None, :] < lengths[:, None, None]
            )
            allowed = allowed[:, None]
            scores = (
                jnp.einsum("sqhd,skhd->shqk", queries, key_blk, preferred_element_type=jnp.float32)
                * score_scale
            )
            probs_f = jnp.where(
                allowed, jnp.exp(jnp.where(allowed, scores - log_sum[..., None], neg_big)), 0.0
            )
            grad_probs = jnp.einsum(
                "sqhd,skhd->shqk", grad_att, value_blk, preferred_element_type=jnp.float32
            )
            grad_scores = (probs_f * (grad_probs - row_delta[..., None])).astype(jnp.bfloat16)
            grad_q_new = (
                grad_now
                + jnp.einsum(
                    "shqk,skhd->shqd", grad_scores, key_blk, preferred_element_type=jnp.float32
                )
                * score_scale
            )
            grad_k = (
                jnp.einsum(
                    "shqk,sqhd->skhd", grad_scores, queries, preferred_element_type=jnp.float32
                )
                * score_scale
            )
            grad_v = jnp.einsum(
                "shqk,sqhd->skhd",
                probs_f.astype(jnp.bfloat16),
                grad_att,
                preferred_element_type=jnp.float32,
            )
            return (grad_q_new, (grad_k, grad_v))

        def skip(grad_now):
            zero_blk = jnp.zeros((slots_dev, block_len, heads_dev, HD), jnp.float32)
            return (grad_now, (zero_blk, zero_blk))

        needed = (offset <= last_pos) & (offset < longest)
        return lax.cond(needed, back_compute, skip, grad_q)

    grad_q_start = jnp.zeros((slots_dev, heads_dev, local_len, HD), jnp.float32)
    grad_q, kv_terms = lax.scan(
        lambda carry, scanned: back_block(carry, scanned),
        grad_q_start,
        (key_blocks, value_blocks, offsets),
    )
    grad_k_all = jnp.moveaxis(kv_terms[0], 0, 1).reshape(slots_dev, seq_len, feat_dev)
    grad_v_all = jnp.moveaxis(kv_terms[1], 0, 1).reshape(slots_dev, seq_len, feat_dev)
    grad_k_own, grad_v_own = (
        lax.psum_scatter(
            grad_k_all.astype(jnp.bfloat16), "ctx", scatter_dimension=1, tiled=True
        ).astype(jnp.float32),
        lax.psum_scatter(
            grad_v_all.astype(jnp.bfloat16), "ctx", scatter_dimension=1, tiled=True
        ).astype(jnp.float32),
    )
    grad_k_rows = grad_k_own.reshape(slots_dev, local_len, heads_dev, HD)
    grad_v_rows = grad_v_own.reshape(slots_dev, local_len, heads_dev, HD)
    grad_q_rows = jnp.transpose(grad_q, (0, 2, 1, 3))
    grad_qkv = jnp.stack(
        [
            unrotate(grad_q_rows, cos_tab, sine_tab),
            unrotate(grad_k_rows, cos_tab, sine_tab),
            grad_v_rows,
        ],
        axis=3,
    )
    grad_qkv = grad_qkv.astype(jnp.bfloat16).reshape(row_count, 3 * feat_dev)
    grad_b_qkv_local = jnp.sum(grad_qkv, axis=0, dtype=jnp.float32)
    grad_w_qkv_local = dot_rows(attn_in, grad_qkv)
    grad_attn_in = dot_last(grad_qkv, qkv_back)
    attn_three = grad_attn_in.reshape(slots_dev, local_len, model_width)
    ffn_three = grad_ffn_in.reshape(slots_dev, local_len, model_width)
    attn_full, ffn_full = (
        lax.psum(attn_three.astype(jnp.bfloat16), "tensor").astype(jnp.float32),
        lax.psum(ffn_three.astype(jnp.bfloat16), "tensor").astype(jnp.float32),
    )
    grad_normed = attn_full * attn_gain + ffn_full * ffn_gain
    mean_one = jnp.mean(grad_normed, axis=-1, keepdims=True)
    mean_two = jnp.mean(grad_normed * normed, axis=-1, keepdims=True)
    input_grad = (mask_grad + inv_std * (grad_normed - mean_one - normed * mean_two)).astype(
        jnp.bfloat16
    )
    attn_part = lax.dynamic_slice_in_dim(attn_full, row_start, part_len, 1)
    ffn_part = lax.dynamic_slice_in_dim(ffn_full, row_start, part_len, 1)
    normed_rows = lax.dynamic_slice_in_dim(normed, row_start, part_len, 1)
    qkv_bias_len = grad_b_qkv_local.shape[0]
    in_bias_len = grad_b_in_local.shape[0]
    qkv_bias_wide = lax.dynamic_update_slice_in_dim(
        jnp.zeros((qkv_bias_len * n_tensor,), jnp.float32),
        grad_b_qkv_local,
        tensor_index * qkv_bias_len,
        0,
    )
    in_bias_wide = lax.dynamic_update_slice_in_dim(
        jnp.zeros((in_bias_len * n_tensor,), jnp.float32),
        grad_b_in_local,
        tensor_index * in_bias_len,
        0,
    )
    gain_attn, shift_attn, gain_ffn, shift_ffn, bias_grad, qkv_bias_sum, in_bias_sum = lax.psum(
        (
            jnp.sum(attn_part * normed_rows, axis=(0, 1)),
            jnp.sum(attn_part, axis=(0, 1)),
            jnp.sum(ffn_part * normed_rows, axis=(0, 1)),
            jnp.sum(ffn_part, axis=(0, 1)),
            jnp.sum(lax.dynamic_slice_in_dim(mask_grad, row_start, part_len, 1), axis=(0, 1)),
            qkv_bias_wide,
            in_bias_wide,
        ),
        ("dp", "ctx", "tensor"),
    )
    grad_b_qkv = lax.dynamic_slice_in_dim(
        qkv_bias_sum, tensor_index * qkv_bias_len, qkv_bias_len, 0
    )
    grad_b_in = lax.dynamic_slice_in_dim(in_bias_sum, tensor_index * in_bias_len, in_bias_len, 0)
    grad_w_qkv, grad_w_proj, grad_w_in, grad_w_out = (
        lax.psum_scatter(
            grad_w_qkv_local.astype(jnp.bfloat16), ("dp", "ctx"), scatter_dimension=0, tiled=True
        ).astype(jnp.float32),
        lax.psum_scatter(
            grad_w_proj_local.astype(jnp.bfloat16), ("dp", "ctx"), scatter_dimension=1, tiled=True
        ).astype(jnp.float32),
        lax.psum_scatter(
            grad_w_in_local.astype(jnp.bfloat16), ("dp", "ctx"), scatter_dimension=0, tiled=True
        ).astype(jnp.float32),
        lax.psum_scatter(
            grad_w_out_local.astype(jnp.bfloat16), ("dp", "ctx"), scatter_dimension=1, tiled=True
        ).astype(jnp.float32),
    )
    return (
        block_output,
        input_grad,
        gain_attn,
        shift_attn,
        gain_ffn,
        shift_ffn,
        grad_w_qkv,
        grad_b_qkv,
        grad_w_proj,
        bias_grad,
        grad_w_in,
        grad_b_in,
        grad_w_out,
        bias_grad,
    )


def solution(mesh):
    placed = (
        P("dp", "ctx", None),
        P("dp", "ctx", None),
        P("dp"),
        P(),
        P(),
        P(),
        P(),
        P(("dp", "ctx"), "tensor"),
        P("tensor"),
        P("tensor", ("dp", "ctx")),
        P(),
        P(("dp", "ctx"), "tensor"),
        P("tensor"),
        P("tensor", ("dp", "ctx")),
        P(),
    )
    return jax.shard_map(
        local,
        mesh=mesh,
        in_specs=placed,
        out_specs=(
            P("dp", "ctx", None),
            P("dp", "ctx", None),
            P(),
            P(),
            P(),
            P(),
            P(("dp", "ctx"), "tensor"),
            P("tensor"),
            P("tensor", ("dp", "ctx")),
            P(),
            P(("dp", "ctx"), "tensor"),
            P("tensor"),
            P("tensor", ("dp", "ctx")),
            P(),
        ),
        check_vma=False,
    )
```

profile of v0, /device:TPU:0, one launch (start us, length us, event | category | flops | bytes accessed | tf_op | source)
XLA Modules:
  0.0 1265.5 jit_solution(16969775963921930338)
XLA Ops:
  7.2 2.4 convert_element_type.191
  11.6 3.0 convert_reduce_fusion
  16.9 7.6 fusion.53
  24.4 34.2 %all-gather.7.cloned.1.call-done = bf16[2048,1536]{1,0:T(8,128)(2,1)} async-done(((bf16[256,1536]{1,0:T(8,128)(2,1)}), bf16[2048,1536]{1,0:T(8,128)(2,1)}) %all-gather.7.cloned.1.call-update) | async-done | bytes 6291472 | tf_op jit(solution)/shard_map/all_gather | solution.py:110
  58.6 11.8 convolution_add_fusion
  70.3 6.5 copy.65
  76.9 9.2 reshape.353
  86.1 2.3 slice.95
  91.0 3.7 slice_bitcast_fusion
  98.4 7.9 convert_multiply_fusion
  106.3 6.2 convolution_convert_fusion.5
  114.9 2.0 bitcast_convert_fusion
  120.0 3.8 all-gather.11.cloned.1.call-done
  123.9 3.3 reshape.371
  127.2 4.1 copy.73
  131.3 27.7 %all-gather.9.cloned.1.call-done = bf16[2,1024,512]{1,2,0:T(8,128)(2,1)} async-done(((bf16[2,512,512]{1,2,0:T(8,128)(2,1)}), bf16[2,1024,512]{1,2,0:T(8,128)(2,1)}) %all-gather.9.cloned.1.call-update) | async-done | bytes 2097168 | tf_op jit(solution)/shard_map/all_gather | solution.py:138
  159.0 3.3 reshape.370
  162.3 4.1 copy.71
  167.9 14.2 %while.33 = (s32[]{:T(128)}, f32[2,2,512]{2,1,0:T(2,128)S(1)}, f32[2,2,512]{2,1,0:T(2,128)S(1)}, f32[2,2,512,256]{3,2,1,0:T(8,128)}, s32[2]{0:T(128)S(1)}, /*ind...) while((s32[]{:T(128)}, f32[2,2,512]{2,1,0:T(2,128)S(1)}, ...), condition=%wide.region_8.9_spmd.clone, body=%wide.region_3.8_spmd.clone.sunk | while | flops 1089214464 | bytes 47858592 | solution.py:182
  170.5 9.1 conditional.6
  171.7 2.2 fusion.4
  176.2 2.1 multiply_add_fusion
  182.1 2.9 multiply_reduce_fusion.1
  186.6 27.5 %while.34 = (s32[]{:T(128)}, f32[2,2,512,256]{3,2,1,0:T(8,128)}, bf16[2,2,512,2,256]{4,2,3,1,0:T(8,128)(2,1)}, bf16[2,2,512,2,256]{4,2,3,1,0:T(8,128)(2,1)}, s32...) while((s32[]{:T(128)}, f32[2,2,512,256]{3,2,1,0:T(8,128)}, ...), condition=%wide.region_13.14_spmd.clone, body=%wide.region_10.13_spmd.clone.sunk | while | flops 2699823104 | bytes 68200384 | solution.py:282
  197.5 10.8 conditional.7
  204.3 2.8 multiply_add_fusion.2
  214.0 3.7 copy.80
  217.8 2.6 convert_element_type.210
  220.5 3.7 copy.85
  224.3 2.6 convert_element_type.213
  227.0 2.8 convert_element_type.200
  230.2 2.8 convert_element_type.202
  235.5 2.3 copy.79
  239.7 6.2 convolution_convert_fusion.4
  246.0 26.2 %reduce-scatter.7.cloned.1.call-done = bf16[2,512,512]{2,1,0:T(8,128)(2,1)} async-done(((bf16[2,1024,512]{2,1,0:T(8,128)(2,1)}), bf16[2,512,512]{2,1,0:T(8,128)(2,1)}) %reduce-scatter.7.cloned.1.call-update) | async-done | bytes 1048592 | tf_op jit(solution)/shard_map/reduce_scatter | solution.py:290
  276.4 2.8 maximum_bitcast_fusion
  279.3 27.6 %reduce-scatter.9.cloned.1.call-done = bf16[2,512,512]{2,1,0:T(8,128)(2,1)} async-done(((bf16[2,1024,512]{2,1,0:T(8,128)(2,1)}), bf16[2,512,512]{2,1,0:T(8,128)(2,1)}) %reduce-scatter.9.cloned.1.call-update) | async-done | bytes 1048592 | tf_op jit(solution)/shard_map/reduce_scatter | solution.py:293
  309.4 12.5 convert_reduce_fusion.2
  322.0 2.2 copy.90
  326.3 9.1 convolution_convert_fusion.2
  335.5 28.1 %all-gather.15.cloned.1.call-done = bf16[2048,2048]{1,0:T(8,128)(2,1)} async-done(((bf16[256,2048]{1,0:T(8,128)(2,1)}), bf16[2048,2048]{1,0:T(8,128)(2,1)}) %all-gather.15.cloned.1.call-update) | async-done | bytes 8388624 | tf_op jit(solution)/shard_map/all_gather | solution.py:112
  363.6 30.6 %fusion.61 = (bf16[1024,2048]{1,0:T(8,128)(2,1)S(1)}, f32[1024,2048]{1,0:T(8,128)}) fusion(f32[2048]{0:T(1024)S(1)} %copy-done.40, bf16[1024,2048]{1,0:T(8,128)(2,1)} %bitcast.153, bf16[2048,2048]{1,0:T(8,128)(2,1)} %all-gather.15.cloned.1.call-done), kind=kOutput, calls=%fused_computation.79 | convolution fusion | flops 8728346624 | bytes 25174016 | tf_op jit(solution)/shard_map/dot_general | solution.py:189
  394.2 2.0 copy-done.41
  396.2 11.4 convolution_convert_fusion
  407.7 13.6 %all-gather.17.cloned.1.call-done = bf16[2048,2048]{1,0:T(8,128)(2,1)} async-done(((bf16[2048,256]{1,0:T(8,128)(2,1)}), bf16[2048,2048]{1,0:T(8,128)(2,1)}) %all-gather.17.cloned.1.call-update) | async-done | bytes 8388624 | tf_op jit(solution)/shard_map/all_gather | solution.py:113
  421.4 16.6 %convert_reduce_fusion.1 = (f32[2048]{0:T(1024)S(1)}, bf16[1024,2048]{1,0:T(8,128)(2,1)S(1)}) fusion(f32[1024,2048]{1,0:T(8,128)} %get-tuple-element.598, f32[2048]{0:T(1024)S(1)} %copy-done.40, bf16[1024,2048]{1,0:T(8,128)(2,1)} %bitcast.159, bf16[2048,2048]{1,0:T(8,128)(2,1)} %all-gather.17.cloned.1.call-done), kind=kOutput, calls=%fused_computation.86 | convolution fusion | flops 8617195520 | bytes 25182208 | tf_op jit(solution)/shard_map/dot_general | solution.py:58
  439.9 11.4 convolution_convert_fusion.1
  451.5 13.3 %fusion.84 = f32[1024,2048]{1,0:T(8,128)S(1)} fusion(bf16[1024,2048]{1,0:T(8,128)(2,1)} %copy-done.41, bf16[2048,2048]{1,0:T(8,128)(2,1)} %all-gather.17.cloned.1.call-done), kind=kOutput, calls=%fused_computation.164 | convolution fusion | flops 8589934592 | bytes 20971520 | tf_op jit(solution)/shard_map/dot_general | solution.py:191
  464.8 4.4 add_convert_fusion.1
  469.1 12.7 %convolution_convert_fusion.3 = bf16[1024,2048]{1,0:T(8,128)(2,1)} fusion(bf16[1024,2048]{1,0:T(8,128)(2,1)S(1)} %copy-done.43, bf16[2048,2048]{1,0:T(8,128)(2,1)} %all-gather.15.cloned.1.call-done), kind=kOutput, calls=%fused_computation.118 | convolution fusion | flops 8592031744 | bytes 16777216 | tf_op jit(solution)/shard_map/dot_general | solution.py:58
  482.5 8.5 fusion.77
  491.7 2.6 dynamic-slice_reduce_fusion
  496.6 34.2 %reduce-scatter.11.cloned.1.call-done = bf16[256,1536]{1,0:T(8,128)(2,1)} async-done(((bf16[2048,1536]{1,0:T(8,128)(2,1)}), bf16[256,1536]{1,0:T(8,128)(2,1)}) %reduce-scatter.11.cloned.1.call-update) | async-done | bytes 786448 | tf_op jit(solution)/shard_map/reduce_scatter | solution.py:358
  530.8 2.5 convert_element_type.225
  533.3 72.4 %reduce-scatter.17.cloned.1.call-done = bf16[2048,256]{1,0:T(8,128)(2,1)} async-done(((bf16[2048,2048]{1,0:T(8,128)(2,1)}), bf16[2048,256]{1,0:T(8,128)(2,1)}) %reduce-scatter.17.cloned.1.call-update) | async-done | bytes 1048592 | tf_op jit(solution)/shard_map/reduce_scatter | solution.py:367
  605.7 2.8 convert_element_type.233
  608.4 72.1 %reduce-scatter.15.cloned.1.call-done = bf16[256,2048]{1,0:T(8,128)(2,1)} async-done(((bf16[2048,2048]{1,0:T(8,128)(2,1)}), bf16[256,2048]{1,0:T(8,128)(2,1)}) %reduce-scatter.15.cloned.1.call-update) | async-done | bytes 1048592 | tf_op jit(solution)/shard_map/reduce_scatter | solution.py:364
  680.5 2.8 convert_element_type.230
  683.3 426.7 %all-reduce.7.cloned.1.call-done = (bf16[2,512,2048]{2,1,0:T(8,128)(2,1)}, bf16[2,512,2048]{2,1,0:T(8,128)(2,1)}, bf16[2,512,2048]{2,1,0:T(8,128)(2,1)}) async-done(((bf16[2,512,2048]{2,1,0:T(8,128)(2,1)}, bf16[2,512,2048]{2,1,0:T(8,128)(2,1)}, bf16[2,512,2048]{2,1,0:T(8,128)(2,1)}), (bf16[2,512,2048]{2,1,0:T(8,128)(2,1)}, bf16[2,512,2048]{2,1,0:T(8,128)(2,1)}, ...) | async-done | bytes 12582928 | tf_op jit(solution)/shard_map/psum | solution.py:196
  1110.1 3.4 convert_element_type.217
  1116.0 3.4 fusion.81
  1120.5 2.8 dynamic-slice_reduce_fusion.1
  1123.3 13.8 %add_convert_fusion = (bf16[2,512,2048]{2,1,0:T(8,128)(2,1)}, bf16[2,512,2048]{2,1,0:T(8,128)(2,1)}) fusion(bf16[2,512,2048]{2,1,0:T(8,128)(2,1)} %param.23, f32[2,512]{1,0:T(2,128)S(1)} %broadcast_multiply_fusion, f32[2,512]{1,0:T(2,128)S(1)} %broadcast_multiply_fusion.1, f32[2,512]{1,0:T(2,128)S(1)} %copy-done.29, f32[2,512]{1,0:T(2,128)S(1)} %copy-done.22, ...), kind=kLoop, calls=%fused_computation.87 | loop fusion | flops 44040192 | bytes 29405184 | tf_op jit(solution)/shard_map/convert_element_type | solution.py:321
  1137.2 111.2 %all-reduce.5.cloned.1.call-done = (f32[2048]{0:T(1024)}, f32[2048]{0:T(1024)}, f32[2048]{0:T(1024)}, f32[2048]{0:T(1024)}, f32[6144]{0:T(1024)}, /*index=5*/f32[2048]{0:T(1024)}, f32[8192]{0:T(1024)}) async-done(((f32[2048]{0:T(1024)}, f32[2048]{0:T(1024)}, f32[2048]{0:T(1024)}, f32[2048]{0:T(1024)}, f32[6144]{0:T(1024)}, /*index=5*/f32[2048]{0:T(1024)}, f32[8192]{0:T(1024)}), (f32[2048]{0:T(1024)}, ...) | async-done | bytes 98320 | tf_op jit(solution)/shard_map/psum | solution.py:341
  (211 shorter events, 71.0 us)
Async XLA Ops:
  7.2 51.4 %all-gather.7.cloned.1.call-start = ((), (), s32[]{:S(2)}) async-start(), calls=%async_computation.6 | async-start | bytes 7077888 | tf_op jit(solution)/shard_map/all_gather | solution.py:110
  9.6 96.7 %all-gather.13.cloned.1.call-start = ((), (), s32[]{:S(2)}) async-start(), calls=%async_computation.9 | async-start | bytes 2359296 | tf_op jit(solution)/shard_map/all_gather | solution.py:111
  11.5 5.4 copy-start.24
  11.5 112.4 %all-gather.11.cloned.1.call-start = ((), (), s32[]{:S(2)}) async-start(), calls=%async_computation.8 | async-start | bytes 3145728 | tf_op jit(solution)/shard_map/all_gather | solution.py:139
  11.5 3.5 copy-start
  11.5 5.3 copy-start.26
  11.6 5.3 copy-start.34
  11.6 5.3 copy-start.35
  15.0 1.3 copy-start.21
  16.2 0.6 copy-start.28
  16.8 41.7 %copy-start.39 = (f32[1536]{0:T(1024)S(1)}, f32[1536]{0:T(1024)}, u32[]{:S(2)}) copy-start(f32[1536]{0:T(1024)} %param.31) | copy-start | bytes 18436
  86.1 3.9 copy-start.30
  89.6 69.4 %all-gather.9.cloned.1.call-start = ((), (), s32[]{:S(2)}) async-start(), calls=%async_computation.7 | async-start | bytes 3145728 | tf_op jit(solution)/shard_map/all_gather | solution.py:138
  90.7 7.8 copy-start.31
  98.4 173.9 %reduce-scatter.7.cloned.1.call-start = ((), (), s32[]{:S(2)}) async-start(), calls=%async_computation.12 | async-start | bytes 3145728 | tf_op jit(solution)/shard_map/reduce_scatter | solution.py:290
  167.9 14.2 %copy-start.9 = (f32[2,2,512,256]{3,1,2,0:T(2,128)S(1)}, f32[2,2,512,256]{3,1,2,0:T(2,128)}, u32[]{:S(2)}) copy-start(f32[2,2,512,256]{3,1,2,0:T(2,128)} %bitcast_convert_fusion) | copy-start | bytes 6291460
  173.9 1.6 copy-start.10
  173.9 2.2 copy-start.16
  178.2 1.3 copy-start.11
  197.5 3.4 copy-start.17
  197.6 3.4 copy-start.18
  202.7 1.6 copy-start.2
  207.0 1.3 copy-start.3
  220.5 86.4 %reduce-scatter.9.cloned.1.call-start = ((), (), s32[]{:S(2)}) async-start(), calls=%async_computation.13 | async-start | bytes 3145728 | tf_op jit(solution)/shard_map/reduce_scatter | solution.py:293
  226.9 6.3 copy-start.15
  226.9 136.7 %all-gather.15.cloned.1.call-start = ((), (), s32[]{:S(2)}) async-start(), calls=%async_computation.10 | async-start | bytes 9437184 | tf_op jit(solution)/shard_map/all_gather | solution.py:112
  229.8 5.7 copy-start.4
  229.8 191.6 %all-gather.17.cloned.1.call-start = ((), (), s32[]{:S(2)}) async-start(), calls=%async_computation.11 | async-start | bytes 9437184 | tf_op jit(solution)/shard_map/all_gather | solution.py:113
  233.1 261.4 %reduce-scatter.13.cloned.1.call-start = ((), (), s32[]{:S(2)}) async-start(), calls=%async_computation.15 | async-start | bytes 2359296 | tf_op jit(solution)/shard_map/reduce_scatter | solution.py:361
  245.9 284.9 %reduce-scatter.11.cloned.1.call-start = ((), (), s32[]{:S(2)}) async-start(), calls=%async_computation.14 | async-start | bytes 7077888 | tf_op jit(solution)/shard_map/reduce_scatter | solution.py:358
  322.0 3.0 copy-start.7
  324.1 2.2 copy-start.13
  335.4 28.1 %copy-start.40 = (f32[2048]{0:T(1024)S(1)}, f32[2048]{0:T(1024)}, u32[]{:S(2)}) copy-start(f32[2048]{0:T(1024)} %param.35) | copy-start | bytes 24580
  335.5 270.2 %reduce-scatter.17.cloned.1.call-start = ((), (), s32[]{:S(2)}) async-start(), calls=%async_computation.17 | async-start | bytes 9437184 | tf_op jit(solution)/shard_map/reduce_scatter | solution.py:367
  363.6 32.6 %copy-start.14 = (bf16[2,512,2048]{2,1,0:T(8,128)(2,1)S(1)}, bf16[2,512,2048]{2,1,0:T(8,128)(2,1)}, u32[]{:S(2)}) copy-start(bf16[2,512,2048]{2,1,0:T(8,128)(2,1)} %get-tuple-element.576) | copy-start | bytes 12582916
  394.2 2.0 copy-start.41
  407.7 272.9 %reduce-scatter.15.cloned.1.call-start = ((), (), s32[]{:S(2)}) async-start(), calls=%async_computation.16 | async-start | bytes 9437184 | tf_op jit(solution)/shard_map/reduce_scatter | solution.py:364
  421.4 18.6 %copy-start.12 = (bf16[2,512,2048]{2,1,0:T(8,128)(2,1)S(1)}, bf16[2,512,2048]{2,1,0:T(8,128)(2,1)}, u32[]{:S(2)}) copy-start(bf16[2,512,2048]{2,1,0:T(8,128)(2,1)} %get-tuple-element.574) | copy-start | bytes 12582916
  438.0 2.0 copy-start.42
  451.4 13.3 %copy-start.19 = (bf16[128,8,2,256]{3,1,2,0:T(8,128)(2,1)S(1)}, bf16[128,8,2,256]{3,1,2,0:T(8,128)(2,1)}, u32[]{:S(2)}) copy-start(bf16[128,8,2,256]{3,1,2,0:T(8,128)(2,1)} %copy.110) | copy-start | bytes 3145732
  451.4 13.3 %copy-start.38 = (bf16[512,2048]{1,0:T(8,128)(2,1)S(1)}, bf16[512,2048]{1,0:T(8,128)(2,1)}, u32[]{:S(2)}) copy-start(bf16[512,2048]{1,0:T(8,128)(2,1)} %all-gather.13.cloned.1.call-done) | copy-start | bytes 6291460
  451.4 658.6 %all-reduce.7.cloned.1.call-start = ((), (), s32[]{:S(2)}) async-start(), calls=%async_computation.19 | async-start | bytes 25165824 | tf_op jit(solution)/shard_map/psum | solution.py:196
  464.8 4.4 copy-start.43
  464.8 17.7 %slice-start = ((s8[6291456]{0:T(1024)(128)(4,1)}), s8[4194304]{0:T(1024)(128)(4,1)S(1)}, s32[]{:S(2)}) async-start(s8[6291456]{0:T(1024)(128)(4,1)} %bitcast.173), calls=%async_computation.20 | async-start | bytes 8388608
  469.1 12.7 %copy-start.8 = (bf16[2,512,2,3,256]{1,0,4,2,3:T(2,128)(2,1)S(1)}, bf16[2,512,2,3,256]{1,0,4,2,3:T(2,128)(2,1)}, u32[]{:S(2)}) copy-start(bf16[2,512,2,3,256]{1,0,4,2,3:T(2,128)(2,1)} %copy-done.7) | copy-start | bytes 9437188
  469.1 13.3 %slice-start.1 = ((s8[6291456]{0:T(1024)(128)(4,1)}), s8[2097152]{0:T(1024)(128)(4,1)S(1)}, s32[]{:S(2)}) async-start(s8[6291456]{0:T(1024)(128)(4,1)} %bitcast.173), calls=%async_computation.21 | async-start | bytes 4194304
  491.0 0.7 copy-start.36
  491.0 0.7 copy-start.37
  491.0 5.3 copy-start.33
  491.0 757.3 %all-reduce.5.cloned.1.call-start = ((), (), s32[]{:S(2)}) async-start(), calls=%async_computation.18 | async-start | bytes 196608 | tf_op jit(solution)/shard_map/psum | solution.py:341
  494.5 188.9 %copy-start.20 = (f32[8192]{0:T(1024)}, f32[8192]{0:T(1024)S(1)}, u32[]{:S(2)}) copy-start(f32[8192]{0:T(1024)S(1)} %dynamic_update_slice.14) | copy-start | bytes 98308
  496.6 186.7 %copy-start.23 = (f32[6144]{0:T(1024)}, f32[6144]{0:T(1024)S(1)}, u32[]{:S(2)}) copy-start(f32[6144]{0:T(1024)S(1)} %dynamic_update_slice.13) | copy-start | bytes 73732
  605.7 507.8 %copy-start.22 = (f32[2,512]{1,0:T(2,128)S(1)}, f32[2,512]{1,0:T(2,128)}, u32[]{:S(2)}) copy-start(f32[2,512]{1,0:T(2,128)} %copy-done.21) | copy-start | bytes 12292
  605.7 507.8 %copy-start.25 = (f32[2048]{0:T(1024)S(1)}, f32[2048]{0:T(1024)}, u32[]{:S(2)}) copy-start(f32[2048]{0:T(1024)} %param.28) | copy-start | bytes 24580
  605.7 507.8 %copy-start.27 = (f32[2048]{0:T(1024)S(1)}, f32[2048]{0:T(1024)}, u32[]{:S(2)}) copy-start(f32[2048]{0:T(1024)} %param.26) | copy-start | bytes 24580
  605.7 507.9 %copy-start.29 = (f32[2,512]{1,0:T(2,128)S(1)}, f32[2,512]{1,0:T(2,128)}, u32[]{:S(2)}) copy-start(f32[2,512]{1,0:T(2,128)} %copy-done.28) | copy-start | bytes 12292
  1110.1 3.5 copy-start.1
  1110.1 4.7 copy-start.5
  1110.1 5.9 copy-start.6
  1120.5 2.9 copy-start.32
Sparse Core Ops, SparseCore 0:
  10.4 48.1 all-gather.6
  61.0 28.0 all-gather.12
  90.7 33.0 all-gather.10
  125.8 33.0 all-gather.8
  220.6 51.6 reduce-scatter.6
  274.9 31.8 reduce-scatter.8
  309.3 54.2 all-gather.14
  365.5 55.8 all-gather.16
  424.7 41.1 reduce-scatter.12
  469.0 61.7 reduce-scatter.10
  534.3 71.3 reduce-scatter.16
  609.0 71.5 reduce-scatter.14
  683.9 426.1 all-reduce.6
  1123.5 124.8 all-reduce.4
where the time goes:
time: 1270 us
  waiting for transfers between devices  878 us (69%)
  matrix products  155 us (12%)
  local copies, waits for them, and re-layouts  104 us (8%)
  other arithmetic  96.6 us (8%)
  loops' own time  16.5 us (1%)
  between operations  14.7 us (1%)
    psum x1, waiting for transfers between devices, local(): lax.psum(partial_out.astype(jnp.bfloat16), 'tensor').astype(jnp.float32)  427 us
    psum x1, waiting for transfers between devices, local(): lax.psum((jnp.sum(attn_part * normed_rows, axis=(0, 1)), jnp.sum(attn_par...  111 us
    reduce_scatter x1, waiting for transfers between devices, local(): lax.psum_scatter(grad_w_out_local.astype(jnp.bfloat16), ('dp', 'ctx'), sc...  72.4 us
    reduce_scatter x1, waiting for transfers between devices, local(): lax.psum_scatter(grad_w_in_local.astype(jnp.bfloat16), ('dp', 'ctx'), sca...  72.1 us
    dot_general x4, matrix products, dot_last(): lax.dot_general(left_side, right_side, (((1,), (1,)), ((), ())), preferre...  44 us
    dot_general x4, matrix products, dot_rows(): lax.dot_general(left_side, right_side, (((0,), (0,)), ((), ())), preferre...  38.2 us
    reduce_scatter x1, waiting for transfers between devices, local(): lax.psum_scatter(grad_w_qkv_local.astype(jnp.bfloat16), ('dp', 'ctx'), sc...  34.2 us
    all_gather x1, waiting for transfers between devices, local(): lax.all_gather(weights_low[0], ('dp', 'ctx'), axis=0, tiled=True)  34.2 us
  transfers between devices with their start and end apart: 14, of which 12 were waited for; matrix products, arithmetic and copies ran while one was open for 22% of the time, Pallas kernels for 0%

commit v1 on v0

v1 whole, which is shorter than its diff:
```python
import functools
import math

import jax
import jax.numpy as jnp
from jax import lax
from jax.experimental import pallas as pl
from jax.experimental.pallas import tpu as pltpu
from jax.sharding import PartitionSpec as P

HD = 256
ROT = 64
NBLK = 8
BF = jnp.bfloat16
F32 = jnp.float32

neg_big = -1e30
inv_sqrt_two = 0.7071067811865476
inv_sqrt_tau = 0.3989422804014327


def cost(flops, nbytes, trans=0):
    return pl.CostEstimate(flops=int(flops), bytes_accessed=int(nbytes), transcendentals=int(trans))


def params(n, mb=60):
    return pltpu.CompilerParams(
        dimension_semantics=("arbitrary",) * n, vmem_limit_bytes=int(mb * 1024 * 1024)
    )


def nn(a, b):
    return lax.dot_general(a, b, (((1,), (0,)), ((), ())), preferred_element_type=F32)


def nt(a, b):
    return lax.dot_general(a, b, (((1,), (1,)), ((), ())), preferred_element_type=F32)


def tn(a, b):
    return lax.dot_general(a, b, (((0,), (0,)), ((), ())), preferred_element_type=F32)


def block_cols(r):
    return pl.ds(pl.multiple_of(r, 128), 256)


def row_valid(meta, row0, rows, local_len):
    slot = row0 // local_len
    pos = meta[0] * local_len + row0 % local_len + lax.broadcasted_iota(jnp.int32, (rows, 1), 0)
    return (pos < meta[2 + NBLK + slot]).astype(F32)


def norm_kernel(local_len, meta, x_ref, g_ref, ga, sa, gf, sf, h1_ref, h2_ref, g_out, st_ref, gs_ref):
    rows = x_ref.shape[0]
    i = pl.program_id(0)
    x = x_ref[...].astype(F32)
    mean = jnp.mean(x, axis=-1, keepdims=True)
    cen = x - mean
    inv = lax.rsqrt(jnp.mean(cen * cen, axis=-1, keepdims=True) + 1e-05)
    mask = row_valid(meta, i * rows, rows, local_len)
    lane = lax.broadcasted_iota(jnp.int32, (rows, 128), 1)
    st_ref[...] = jnp.where(lane == 0, mean, inv)
    for r in range(NBLK):
        src = block_cols(meta[1 + r] * 256)
        dst = slice(r * 256, (r + 1) * 256)
        xh = (x_ref[:, src].astype(F32) - mean) * inv
        h1_ref[:, dst] = (xh * ga[:, src] + sa[:, src]).astype(BF)
        h2_ref[:, dst] = (xh * gf[:, src] + sf[:, src]).astype(BF)
        gm = g_ref[:, src].astype(F32) * mask
        g_out[:, dst] = gm.astype(BF)
        part = jnp.sum(gm, axis=0, keepdims=True)

        @pl.when(i == 0)
        def _():
            gs_ref[:, src] = part

        @pl.when(i > 0)
        def _():
            gs_ref[:, src] = gs_ref[:, src] + part


def norm_call(meta, x2, g2, ga, sa, gf, sf, local_len):
    m, d = x2.shape
    rows = 256
    row_spec = pl.BlockSpec((rows, d), lambda i, mt: (i, 0))
    vec = pl.BlockSpec((1, d), lambda i, mt: (0, 0))
    return pl.pallas_call(
        functools.partial(norm_kernel, local_len),
        name="norm",
        grid_spec=pltpu.PrefetchScalarGridSpec(
            num_scalar_prefetch=1,
            grid=(m // rows,),
            in_specs=[row_spec, row_spec, vec, vec, vec, vec],
            out_specs=[row_spec, row_spec, row_spec, pl.BlockSpec((rows, 128), lambda i, mt: (i, 0)), vec],
        ),
        out_shape=[jax.ShapeDtypeStruct((m, d), BF)] * 3
        + [jax.ShapeDtypeStruct((m, 128), F32), jax.ShapeDtypeStruct((1, d), F32)],
        compiler_params=params(1),
        cost_estimate=cost(20 * m * d, 10 * m * d),
    )(meta, x2, g2, ga, sa, gf, sf)


def rotate_tile(y, cosf, s1, s2, sign):
    head = y[:, :128]
    rot = (
        head * cosf
        + pltpu.roll(head, 96, 1) * (s1 * sign)
        + pltpu.roll(head, 32, 1) * (s2 * sign)
    )
    return rot, y[:, 128:]


def rotated(out, y, cosf, s1, s2):
    local_len = cosf.shape[0]
    for s in range(y.shape[0] // local_len):
        rows = slice(s * local_len, (s + 1) * local_len)
        rot, rest = rotate_tile(y[rows], cosf[...], s1[...], s2[...], 1.0)
        out[rows, :128] = rot.astype(BF)
        out[rows, 128:] = rest.astype(BF)


def kv_kernel(h1, wa, wb, b_ref, cosf, s1, s2, kv_ref):
    half = wa.shape[0]
    part = lax.rem(pl.program_id(0), 2)
    y = nn(h1[:, :half], wa[...]) + nn(h1[:, half:], wb[...]) + b_ref[...]

    @pl.when(part == 0)
    def _():
        rotated(kv_ref, y, cosf, s1, s2)

    @pl.when(part == 1)
    def _():
        kv_ref[...] = y.astype(BF)


def kv_call(h1, wa, wb, b_qkv, tabs, nheads):
    m, d = h1.shape
    local_len = tabs[0].shape[0]

    def src(j):
        return (0, (j // 2) * 3 + 1 + j % 2)

    tab = pl.BlockSpec((local_len, 128), lambda j: (0, 0))
    return pl.pallas_call(
        kv_kernel,
        name="kv",
        grid=(2 * nheads,),
        in_specs=[
            pl.BlockSpec((m, d), lambda j: (0, 0)),
            pl.BlockSpec((d // 2, HD), src),
            pl.BlockSpec((d // 2, HD), src),
            pl.BlockSpec((1, HD), src),
            tab,
            tab,
            tab,
        ],
        out_specs=pl.BlockSpec((m, HD), lambda j: (0, j)),
        out_shape=jax.ShapeDtypeStruct((m, 2 * nheads * HD), BF),
        compiler_params=params(1),
        cost_estimate=cost(4 * m * d * nheads * HD, 2 * (m * d + 2 * d * nheads * HD + 2 * m * nheads * HD)),
    )(h1, wa, wb, b_qkv, *tabs)


def qd_kernel(nheads, h1, g, wa, wb, b_ref, cosf, s1, s2, q_ref, dob_ref):
    j = pl.program_id(0)
    half = wa.shape[0]

    @pl.when(j < nheads)
    def _():
        rotated(q_ref, nn(h1[:, :half], wa[...]) + nn(h1[:, half:], wb[...]) + b_ref[...], cosf, s1, s2)

    @pl.when(j >= nheads)
    def _():
        dob_ref[...] = (nn(g[:, :half], wa[...]) + nn(g[:, half:], wb[...])).astype(BF)


def qd_call(h1, g, wa, wb, b_qkv, tabs, nheads):
    m, d = h1.shape
    local_len = tabs[0].shape[0]
    full = pl.BlockSpec((m, d), lambda j: (0, 0))
    w_spec = pl.BlockSpec((d // 2, HD), lambda j: (0, jnp.where(j < nheads, 3 * j, 2 * nheads + j)))
    tab = pl.BlockSpec((local_len, 128), lambda j: (0, 0))
    return pl.pallas_call(
        functools.partial(qd_kernel, nheads),
        name="qd",
        grid=(2 * nheads,),
        in_specs=[
            full,
            full,
            w_spec,
            w_spec,
            pl.BlockSpec((1, HD), lambda j: (0, 3 * jnp.minimum(j, nheads - 1))),
            tab,
            tab,
            tab,
        ],
        out_specs=[
            pl.BlockSpec((m, HD), lambda j: (0, jnp.minimum(j, nheads - 1))),
            pl.BlockSpec((m, HD), lambda j: (0, jnp.maximum(j - nheads, 0))),
        ],
        out_shape=[jax.ShapeDtypeStruct((m, nheads * HD), BF)] * 2,
        compiler_params=params(1),
        cost_estimate=cost(4 * m * d * nheads * HD, 2 * (2 * m * d + 2 * d * nheads * HD + 2 * m * nheads * HD)),
    )(h1, g, wa, wb, b_qkv, *tabs)


def attn_kernel(nprev, local_len, meta, q_ref, kv_ref, pv_ref, dob_ref, cosf, s1, s2, ob_ref, dq_ref, dkv_ref, dpv_ref, sc_ref, dq_acc):
    slot = pl.program_id(0)
    ctx = meta[0]
    length = meta[2 + NBLK + slot]
    scale = 1.0 / math.sqrt(HD)
    n_vis = jnp.minimum(ctx, (length + local_len - 1) // local_len)
    q = q_ref[...]
    dob = dob_ref[...]
    own_k = kv_ref[:, :HD]
    own_v = kv_ref[:, HD:]

    ri = lax.broadcasted_iota(jnp.int32, (local_len, local_len), 0)
    ci = lax.broadcasted_iota(jnp.int32, (local_len, local_len), 1)
    s_own = nt(q, own_k) * scale
    s_own = jnp.where((ci <= ri) & (ci < length - ctx * local_len), s_own, neg_big)
    sc_ref[nprev] = s_own

    def prev_rows(jb):
        return pl.ds(pl.multiple_of(jb * local_len, local_len), local_len)

    def score(jb, top):
        s = nt(q, pv_ref[prev_rows(jb), :HD]) * scale
        s = jnp.where(ci[:1] < length - jb * local_len, s, neg_big)
        sc_ref[jb] = s
        return jnp.maximum(top, jnp.max(s, axis=1, keepdims=True))

    top = lax.fori_loop(0, n_vis, score, jnp.max(s_own, axis=1, keepdims=True))

    e_own = jnp.exp(sc_ref[nprev] - top)
    sc_ref[nprev] = e_own

    def expo(jb, tot):
        e = jnp.exp(sc_ref[jb] - top)
        sc_ref[jb] = e
        return tot + jnp.sum(e, axis=1, keepdims=True)

    tot = lax.fori_loop(0, n_vis, expo, jnp.sum(e_own, axis=1, keepdims=True))
    inv = 1.0 / tot
    att = nn((sc_ref[nprev] * inv).astype(BF), own_v)

    def out_step(jb, acc):
        return acc + nn((sc_ref[jb] * inv).astype(BF), pv_ref[prev_rows(jb), HD:])

    att = lax.fori_loop(0, n_vis, out_step, att)
    ob_ref[...] = att.astype(BF)
    delta = jnp.sum(dob.astype(F32) * att, axis=1, keepdims=True)

    def back(p, k, v):
        pb = p.astype(BF)
        ds = (p * (nt(dob, v) - delta)).astype(BF)
        return nn(ds, k) * scale, tn(ds, q) * scale, tn(pb, dob)

    dq, dk, dv = back(sc_ref[nprev] * inv, own_k, own_v)
    dq_acc[...] = dq
    dkv_ref[:, :HD] = dk
    dkv_ref[:, HD:] = dv

    def back_step(jb, carry):
        rows = prev_rows(jb)
        dqp, dkp, dvp = back(sc_ref[jb] * inv, pv_ref[rows, :HD], pv_ref[rows, HD:])
        dq_acc[...] += dqp
        dpv_ref[rows, :HD] = dkp.astype(BF)
        dpv_ref[rows, HD:] = dvp.astype(BF)
        return carry

    lax.fori_loop(0, n_vis, back_step, 0)

    def clear(jb, carry):
        dpv_ref[prev_rows(jb), :] = jnp.zeros((local_len, 2 * HD), BF)
        return carry

    lax.fori_loop(n_vis, nprev, clear, 0)
    rot, rest = rotate_tile(dq_acc[...], cosf[...], s1[...], s2[...], -1.0)
    dq_ref[:, :128] = rot.astype(BF)
    dq_ref[:, 128:] = rest.astype(BF)


def attn_call(meta, q, kv, pv, dob, tabs, nheads):
    local_len = tabs[0].shape[0]
    slots = q.shape[0] // local_len
    nprev = pv.shape[0] // q.shape[0]
    one = pl.BlockSpec((local_len, HD), lambda s, h, mt: (s, h))
    two = pl.BlockSpec((local_len, 2 * HD), lambda s, h, mt: (s, h))
    prev = pl.BlockSpec((nprev * local_len, 2 * HD), lambda s, h, mt: (s, h))
    tab = pl.BlockSpec((local_len, 128), lambda s, h, mt: (0, 0))
    m = q.shape[0]
    return pl.pallas_call(
        functools.partial(attn_kernel, nprev, local_len),
        name="attn",
        grid_spec=pltpu.PrefetchScalarGridSpec(
            num_scalar_prefetch=1,
            grid=(slots, nheads),
            in_specs=[one, two, prev, one, tab, tab, tab],
            out_specs=[one, one, two, prev],
            scratch_shapes=[
                pltpu.VMEM((nprev + 1, local_len, local_len), F32),
                pltpu.VMEM((local_len, HD), F32),
            ],
        ),
        out_shape=[
            jax.ShapeDtypeStruct((m, nheads * HD), BF),
            jax.ShapeDtypeStruct((m, nheads * HD), BF),
            jax.ShapeDtypeStruct((m, 2 * nheads * HD), F32),
            jax.ShapeDtypeStruct((nprev * m, 2 * nheads * HD), BF),
        ],
        compiler_params=params(2),
        cost_estimate=cost(12 * m * nheads * HD * (nprev + 1) * local_len, 20 * m * nheads * HD, m * nheads * (nprev + 1) * local_len),
    )(meta, q, kv, pv, dob, *tabs)


def join_kernel(nheads, dq_ref, dkv_ref, rv_ref, cosf, s1, s2, out_ref, sum_ref):
    i = pl.program_id(0)

    @pl.when(i == 0)
    def _():
        sum_ref[...] = jnp.zeros_like(sum_ref)

    for h in range(nheads):
        base = h * 3 * HD
        out_ref[:, base : base + HD] = dq_ref[:, h * HD : (h + 1) * HD]
        kc = slice(h * 2 * HD, h * 2 * HD + HD)
        vc = slice(h * 2 * HD + HD, (h + 1) * 2 * HD)
        dk = dkv_ref[:, kc] + rv_ref[:, kc].astype(F32)
        rot, rest = rotate_tile(dk, cosf[...], s1[...], s2[...], -1.0)
        out_ref[:, base + HD : base + HD + 128] = rot.astype(BF)
        out_ref[:, base + HD + 128 : base + 2 * HD] = rest.astype(BF)
        out_ref[:, base + 2 * HD : base + 3 * HD] = (dkv_ref[:, vc] + rv_ref[:, vc].astype(F32)).astype(BF)
    sum_ref[...] += jnp.sum(out_ref[...].astype(F32), axis=0, keepdims=True)


def join_call(dq, dkv, rv, tabs, nheads):
    m = dq.shape[0]
    local_len = tabs[0].shape[0]
    rows = 256
    per = local_len // rows

    def spec(c):
        return pl.BlockSpec((rows, c), lambda i: (i, 0))

    tab = pl.BlockSpec((rows, 128), lambda i: (i % per, 0))
    n = 3 * nheads * HD
    return pl.pallas_call(
        functools.partial(join_kernel, nheads),
        name="join",
        grid=(m // rows,),
        in_specs=[spec(nheads * HD), spec(2 * nheads * HD), spec(2 * nheads * HD), tab, tab, tab],
        out_specs=[spec(n), pl.BlockSpec((1, n), lambda i: (0, 0))],
        out_shape=[jax.ShapeDtypeStruct((m, n), BF), jax.ShapeDtypeStruct((1, n), F32)],
        compiler_params=params(1),
        cost_estimate=cost(10 * m * n, 8 * m * n),
    )(dq, dkv, rv, *tabs)


def hidden_kernel(h2, wa, wb, b_ref, gb_ref, dg_ref):
    half = wa.shape[0]
    u = nn(h2[:, :half], wa[...]) + nn(h2[:, half:], wb[...]) + b_ref[...]
    cdf = 0.5 * (1.0 + lax.erf(u * inv_sqrt_two))
    gb_ref[...] = (u * cdf).astype(BF)
    dg_ref[...] = (cdf + u * (jnp.exp(-0.5 * u * u) * inv_sqrt_tau)).astype(BF)


def hidden_call(h2, wa, wb, b_in):
    m, d = h2.shape
    f = wa.shape[1]
    t = 256
    col = pl.BlockSpec((m, t), lambda j: (0, j))
    w_spec = pl.BlockSpec((d // 2, t), lambda j: (0, j))
    return pl.pallas_call(
        hidden_kernel,
        name="hidden",
        grid=(f // t,),
        in_specs=[pl.BlockSpec((m, d), lambda j: (0, 0)), w_spec, w_spec, pl.BlockSpec((1, t), lambda j: (0, j))],
        out_specs=[col, col],
        out_shape=[jax.ShapeDtypeStruct((m, f), BF)] * 2,
        compiler_params=params(1),
        cost_estimate=cost(2 * m * d * f, 2 * (m * d + d * f + 2 * m * f), 2 * m * f),
    )(h2, wa, wb, b_in)


def dhid_kernel(g, w0, w1, w2, w3, dg_ref, du_ref, sum_ref):
    n = w0.shape[0]
    a = nn(g[:, :n], w0[...]) + nn(g[:, n : 2 * n], w1[...])
    a += nn(g[:, 2 * n : 3 * n], w2[...]) + nn(g[:, 3 * n :], w3[...])
    du = (a * dg_ref[...].astype(F32)).astype(BF)
    du_ref[...] = du
    sum_ref[...] = jnp.sum(du.astype(F32), axis=0, keepdims=True)


def dhid_call(g, quarters, dg):
    m, d = g.shape
    f = dg.shape[1]
    t = 256
    col = pl.BlockSpec((m, t), lambda j: (0, j))
    w_spec = pl.BlockSpec((d // 4, t), lambda j: (0, j))
    return pl.pallas_call(
        dhid_kernel,
        name="dhid",
        grid=(f // t,),
        in_specs=[pl.BlockSpec((m, d), lambda j: (0, 0))] + [w_spec] * 4 + [col],
        out_specs=[col, pl.BlockSpec((1, t), lambda j: (0, j))],
        out_shape=[jax.ShapeDtypeStruct((m, f), BF), jax.ShapeDtypeStruct((1, f), F32)],
        compiler_params=params(1),
        cost_estimate=cost(2 * m * d * f, 2 * (m * d + d * f + 2 * m * f)),
    )(g, *quarters, dg)


def out_kernel(ob, gb, wp, wo, y_ref):
    y_ref[...] = (nt(ob[...], wp[...]) + nt(gb[...], wo[...])).astype(BF)


def out_call(ob, gb, g1, quarter, c):
    m, f = gb.shape
    nf = ob.shape[1]
    n = quarter.shape[0]
    rows = 512
    last = g1.shape[1] // nf - 1
    return pl.pallas_call(
        out_kernel,
        name="outp",
        grid=(m // rows,),
        in_specs=[
            pl.BlockSpec((rows, nf), lambda i: (i, 0)),
            pl.BlockSpec((rows, f), lambda i: (i, 0)),
            pl.BlockSpec((n, nf), lambda i: (c % 2, last)),
            pl.BlockSpec((n, f), lambda i: (0, 0)),
        ],
        out_specs=pl.BlockSpec((rows, n), lambda i: (i, 0)),
        out_shape=jax.ShapeDtypeStruct((m, n), BF),
        compiler_params=params(1),
        cost_estimate=cost(2 * m * n * (f + nf), 2 * (m * f + m * nf + n * (f + nf) + m * n)),
    )(ob, gb, g1, quarter)


def back_kernel(c, meta, dqkv, du, w1, w2, x_ref, st_ref, ga, gf, prev, dn_ref, sums_ref):
    i = pl.program_id(0)
    dh1 = nt(dqkv[...], w1[...])
    dh2 = nt(du[...], w2[...])
    for k in range(2):
        src = block_cols(lax.rem(meta[1 + 2 * c + k], 2) * 256)
        dst = slice(k * 256, (k + 1) * 256)
        a, b = dh1[:, dst], dh2[:, dst]
        xh = (x_ref[:, src].astype(F32) - st_ref[:, 0:1]) * st_ref[:, 1:2]
        dn_ref[:, dst] = (a * ga[:, src] + b * gf[:, src]).astype(BF)
        for j, v in enumerate((a * xh, a, b * xh, b)):
            part = jnp.sum(v, axis=0, keepdims=True)

            @pl.when(i == 0)
            def _():
                sums_ref[j : j + 1, src] = part

            @pl.when(i > 0)
            def _():
                sums_ref[j : j + 1, src] = sums_ref[j : j + 1, src] + part


def back_call(meta, dqkv, du, g1, g2, x2, st, ga, gf, sums, c):
    m, d = x2.shape
    nq = dqkv.shape[1]
    f = du.shape[1]
    n = d // 4
    rows = 512

    def absolute(r, at):
        return pl.BlockSpec((r, n), lambda i, mt: (i if at else 0, mt[1 + 2 * c] // 2))

    return pl.pallas_call(
        functools.partial(back_kernel, c),
        name="backn",
        grid_spec=pltpu.PrefetchScalarGridSpec(
            num_scalar_prefetch=1,
            grid=(m // rows,),
            in_specs=[
                pl.BlockSpec((rows, nq), lambda i, mt: (i, 0)),
                pl.BlockSpec((rows, f), lambda i, mt: (i, 0)),
                pl.BlockSpec((n, nq), lambda i, mt: (c % 2, 0)),
                pl.BlockSpec((n, f), lambda i, mt: (c % 2, 0)),
                absolute(rows, True),
                pl.BlockSpec((rows, 128), lambda i, mt: (i, 0)),
                absolute(1, False),
                absolute(1, False),
                pl.BlockSpec(memory_space=pl.ANY),
            ],
            out_specs=[pl.BlockSpec((rows, n), lambda i, mt: (i, 0)), absolute(4, False)],
        ),
        out_shape=[jax.ShapeDtypeStruct((m, n), BF), jax.ShapeDtypeStruct((4, d), F32)],
        input_output_aliases={9: 1},
        compiler_params=params(1),
        cost_estimate=cost(2 * m * n * (f + nq), 2 * (m * f + m * nq + n * (f + nq) + 2 * m * n)),
    )(meta, dqkv, du, g1, g2, x2, st, ga, gf, sums)


def wgrad_kernel(pairs, adds, split, *refs):
    j = pl.program_id(0)
    half_way = sum(pairs) // 2
    start = 0
    for p, count in enumerate(pairs):
        a, b = refs[2 * p], refs[2 * p + 1]

        @pl.when((j >= start) & (j < start + count))
        def _():
            y = tn(a[...], b[...])
            if adds:
                y = y + refs[2 * len(pairs)][...].astype(F32)
            y = y.astype(BF)
            if not split:
                refs[-1][...] = y
                return
            keep_x, send_x, keep_y, send_y = refs[-4:]
            n = y.shape[0] // 4

            @pl.when(j < half_way)
            def _():
                keep_x[...] = y[: 2 * n]
                send_x[...] = y[2 * n :]

            @pl.when(j >= half_way)
            def _():
                keep_y[:n] = y[:n]
                send_y[:n] = y[n : 2 * n]
                keep_y[n:] = y[2 * n : 3 * n]
                send_y[n:] = y[3 * n :]

        start += count


def wgrad_call(*flat, half, add=None, split=False):
    pairs = list(zip(flat[::2], flat[1::2]))
    m, d = pairs[0][0].shape
    t = 512
    counts = tuple(b.shape[1] // t for _, b in pairs)
    total = sum(counts)
    in_specs, ops, start = [], [], 0
    for (a, b), c in zip(pairs, counts):
        in_specs.append(pl.BlockSpec((m, d // 2), lambda j: (0, half)))
        in_specs.append(
            pl.BlockSpec((m, t), lambda j, s=start, c=c: (0, jnp.clip(j - s, 0, c - 1)))
        )
        ops += [a, b]
        start += c
    col = pl.BlockSpec((d // 2, t), lambda j: (0, j))
    if add is not None:
        in_specs.append(col)
        ops.append(add)
    if split:
        h = total // 2
        left = pl.BlockSpec((d // 4, t), lambda j: (0, jnp.minimum(j, h - 1)))
        right = pl.BlockSpec((d // 4, t), lambda j: (0, jnp.maximum(j - h, 0)))
        out_specs = [left, left, right, right]
        out_shape = [jax.ShapeDtypeStruct((d // 4, h * t), BF)] * 4
    else:
        out_specs = col
        out_shape = jax.ShapeDtypeStruct((d // 2, total * t), BF)
    return pl.pallas_call(
        functools.partial(wgrad_kernel, counts, add is not None, split),
        name="wgrad",
        grid=(total,),
        in_specs=in_specs,
        out_specs=out_specs,
        out_shape=out_shape,
        compiler_params=params(1),
        cost_estimate=cost(m * d * total * t, 2 * (m * d // 2 * len(pairs) + m * total * t + d * total * t)),
    )(*ops)


def pack_kernel(*refs):
    out, at = refs[-1], 0
    for ref in refs[:-1]:
        n = ref.shape[0]
        out[at : at + n] = ref[...]
        at += n


def pack_call(*pieces):
    rows = sum(p.shape[0] for p in pieces)
    cols = pieces[0].shape[1]
    t = 512
    return pl.pallas_call(
        pack_kernel,
        name="pack",
        grid=(cols // t,),
        in_specs=[pl.BlockSpec((p.shape[0], t), lambda j: (0, j)) for p in pieces],
        out_specs=pl.BlockSpec((rows, t), lambda j: (0, j)),
        out_shape=jax.ShapeDtypeStruct((rows, cols), BF),
        compiler_params=params(1),
        cost_estimate=cost(0, 4 * rows * cols),
    )(*pieces)


def half_sum_kernel(keep_x, got_x, keep_y, got_y, mid_x, send_y, mid_y, send_x):
    n = mid_x.shape[0]
    for keep, got, mid, send in ((keep_x, got_x, mid_x, send_y), (keep_y, got_y, mid_y, send_x)):
        mid[...] = keep[:n].astype(F32) + got[:n].astype(F32)
        send[...] = (keep[n:].astype(F32) + got[n:].astype(F32)).astype(BF)


def half_sum_call(*ops):
    rows, cols = ops[0].shape
    t = 512
    n = rows // 2
    small = pl.BlockSpec((n, t), lambda j: (0, j))
    return pl.pallas_call(
        half_sum_kernel,
        name="hsum",
        grid=(cols // t,),
        in_specs=[pl.BlockSpec((rows, t), lambda j: (0, j))] * 4,
        out_specs=[small] * 4,
        out_shape=[jax.ShapeDtypeStruct((n, cols), F32), jax.ShapeDtypeStruct((n, cols), BF)] * 2,
        compiler_params=params(1),
        cost_estimate=cost(8 * n * cols, 28 * n * cols),
    )(*ops)


def last_sum_kernel(plan, mid_x, got_y, mid_y, got_x, *outs):
    j = pl.program_id(0)
    half = sum(c for c, _ in plan) // 2
    at = 0
    for (count, turned), out in zip(plan, outs):
        for k in range(at, at + count):
            mid, got = (mid_x, got_y) if k < half else (mid_y, got_x)

            @pl.when(j == k)
            def _():
                v = mid[...] + got[...].astype(F32)
                out[...] = v.T if turned else v

        at += count


def last_sum_call(*ops, plan):
    n, cols = ops[0].shape
    t = 512
    h = cols // t
    left = pl.BlockSpec((n, t), lambda j: (0, jnp.minimum(j, h - 1)))
    right = pl.BlockSpec((n, t), lambda j: (0, jnp.maximum(j - h, 0)))
    out_specs, out_shape, at = [], [], 0
    for count, turned in plan:
        def place(j, at=at, count=count):
            return jnp.clip(j - at, 0, count - 1)

        if turned:
            out_specs.append(pl.BlockSpec((t, n), lambda j, f=place: (f(j), 0)))
            out_shape.append(jax.ShapeDtypeStruct((count * t, n), F32))
        else:
            out_specs.append(pl.BlockSpec((n, t), lambda j, f=place: (0, f(j))))
            out_shape.append(jax.ShapeDtypeStruct((n, count * t), F32))
        at += count
    return pl.pallas_call(
        functools.partial(last_sum_kernel, plan),
        name="lsum",
        grid=(2 * h,),
        in_specs=[left, left, right, right],
        out_specs=out_specs,
        out_shape=out_shape,
        compiler_params=params(1),
        cost_estimate=cost(4 * n * cols, 20 * n * cols),
    )(*ops)


def total_of(meta, refs, c, cols):
    here, sent = refs[2 * c], refs[2 * c + 1]
    return jnp.where(meta[1 + NBLK] > 0, here[:, cols].astype(F32), sent[:, cols].astype(F32))


def block_out_kernel(local_len, meta, x_ref, b_ref, *refs):
    y_ref = refs[-1]
    rows = x_ref.shape[0]
    mask = row_valid(meta, pl.program_id(0) * rows, rows, local_len)
    for r in range(NBLK):
        col = block_cols(meta[1 + r] * 256)
        k = r % 2 * 256
        s = total_of(meta, refs, r // 2, slice(k, k + 256))
        y_ref[:, col] = (mask * (x_ref[:, col].astype(F32) + s + b_ref[:, col])).astype(BF)


def input_grad_kernel(local_len, meta, x_ref, g_ref, st_ref, *refs):
    y_ref = refs[-1]
    rows = x_ref.shape[0]
    mask = row_valid(meta, pl.program_id(0) * rows, rows, local_len)
    mean = st_ref[:, 0:1]
    inv = st_ref[:, 1:2]
    one = jnp.zeros((rows, 1), F32)
    two = jnp.zeros((rows, 1), F32)
    for r in range(NBLK):
        col = block_cols(meta[1 + r] * 256)
        k = r % 2 * 256
        dn = total_of(meta, refs, r // 2, slice(k, k + 256))
        one += jnp.sum(dn, axis=1, keepdims=True)
        two += jnp.sum(dn * ((x_ref[:, col].astype(F32) - mean) * inv), axis=1, keepdims=True)
    d = x_ref.shape[1]
    one = one / d
    two = two / d
    for r in range(NBLK):
        col = block_cols(meta[1 + r] * 256)
        k = r % 2 * 256
        dn = total_of(meta, refs, r // 2, slice(k, k + 256))
        xh = (x_ref[:, col].astype(F32) - mean) * inv
        y_ref[:, col] = (g_ref[:, col].astype(F32) * mask + inv * (dn - one - xh * two)).astype(BF)


def rows_call(meta, *ops, body, name, specs):
    rows = 256
    m, d = ops[0].shape
    made = {
        "row": pl.BlockSpec((rows, d), lambda i, mt: (i, 0)),
        "part": pl.BlockSpec((rows, d // 4), lambda i, mt: (i, 0)),
        "stat": pl.BlockSpec((rows, 128), lambda i, mt: (i, 0)),
        "vec": pl.BlockSpec((1, d), lambda i, mt: (0, 0)),
    }
    return pl.pallas_call(
        body,
        name=name,
        grid_spec=pltpu.PrefetchScalarGridSpec(
            num_scalar_prefetch=1,
            grid=(m // rows,),
            in_specs=[made[s] for s in specs],
            out_specs=made["row"],
        ),
        out_shape=jax.ShapeDtypeStruct((m, d), BF),
        compiler_params=params(1),
        cost_estimate=cost(10 * m * d, 8 * m * d),
    )(meta, *ops)


def after(v, *others):
    return lax.optimization_barrier((v,) + others)[0]


class Order:
    def __init__(self):
        self.last = ()

    def __call__(self, f, first, *rest, **named):
        out = f(after(first, *self.last), *rest, **named)
        self.last = (jax.tree.leaves(out)[0],)
        return out


def add_bf(a, b):
    return lax.optimization_barrier((a.astype(F32) + b.astype(F32)).astype(BF))


def pick_bf(a, b, middle, other):
    total = (a.astype(F32) + b.astype(F32)).astype(BF)
    return lax.optimization_barrier(jnp.where(middle > 0, total, other))


class Pipe:
    LAG = 3

    def __init__(self, run, middle, count):
        self.run, self.middle, self.count = run, middle, count
        self.parts, self.got, self.sums, self.crossed = [], [], [], []
        self.here, self.sent = [], []

    def send(self, part=None):
        step = len(self.got)
        back = step - self.LAG
        pairs = []
        v = part
        if part is not None:
            self.parts.append(part)
            pairs += [(0, 1), (3, 2)]
        if back >= 0:
            pairs += [(1, 0), (2, 3)]
            a, b = self.sums[back], self.crossed[back]
            if part is None:
                v = self.run(add_bf, a, b)
            else:
                v = self.run(pick_bf, a, b, self.middle, part)
        got = lax.ppermute(v, "tensor", pairs)
        self.got.append(got)
        if back >= 0:
            self.here.append(v)
            self.sent.append(got)

    def cross(self):
        k = len(self.sums)
        v = self.run(add_bf, self.parts[k], self.got[k])
        self.sums.append(v)
        self.crossed.append(lax.ppermute(v, "tensor", [(1, 2), (2, 1)]))


class PlainPipe:
    def __init__(self, run, middle, count):
        self.here, self.sent = [], []

    def send(self, part=None):
        if part is not None:
            total = lax.psum(part, "tensor")
            self.here.append(total)
            self.sent.append(total)

    def cross(self):
        pass


class SmallMesh:
    def x(self, v):
        return lax.ppermute(v, "dp", [(0, 2), (2, 0), (1, 3), (3, 1)])

    def core(self, v):
        return lax.ppermute(v, "dp", [(0, 1), (1, 0), (2, 3), (3, 2)])

    def y(self, v):
        return lax.ppermute(v, "ctx", [(0, 1), (1, 0)])

    def perm(self):
        r = jnp.arange(NBLK, dtype=jnp.int32)
        dp = lax.axis_index("dp") ^ (((r >> 1) & 1) * 2 + (r >> 2))
        return dp * 2 + (lax.axis_index("ctx") ^ (r & 1))

    def middle(self):
        z = lax.axis_index("tensor")
        return ((z == 1) | (z == 2)).astype(jnp.int32)

    pipe = Pipe

    def first_hop(self, own):
        return self.x(own), self.y(own)

    def diagonal(self, own, hop):
        n = own.shape[0] // 2
        return [self.x(hop[1][:n]), self.y(hop[0][n:])]

    def diagonal_x(self, own, hop):
        return [self.x(hop[1])]

    def pack(self, run, own, hop, diag):
        return run(pack_call, own, hop[1], hop[0], *diag)

    def both(self, near):
        return near, self.core(near)

    def quarters_near(self, run, own, hop):
        return self.both(run(pack_call, own, hop[1]))

    def quarters_far(self, run, hop, diag):
        return self.both(run(pack_call, hop[0], *diag))

    def scatter_cross(self, theirs):
        return self.core(theirs)

    def scatter_own(self, run, pairs, got):
        keep_x, send_x, keep_y, send_y = run(wgrad_call, *pairs, half=0, add=got, split=True)
        return keep_x, self.x(send_x), keep_y, self.y(send_y)

    def scatter_half(self, run, parts):
        mid_x, to_y, mid_y, to_x = run(half_sum_call, *parts)
        return mid_x, self.y(to_y), mid_y, self.x(to_x)

    def scatter_last(self, run, plan, parts):
        return run(last_sum_call, *parts, plan=plan)

    def previous(self, kv, slots):
        return lax.ppermute(kv, "ctx", [(0, 1)])

    def give_back(self, dpv, dkv, slots):
        return dkv, lax.ppermute(dpv, "ctx", [(1, 0)])

    def small_sum(self, group, everywhere):
        n = group.shape[0]
        v = jnp.concatenate([group, everywhere])
        v = v + self.core(v)
        v = v + self.x(v)
        v = v + self.y(v)
        w = v[n:]
        w = w + lax.ppermute(w, "tensor", [(0, 1), (1, 0), (2, 3), (3, 2)])
        w = w + lax.ppermute(w, "tensor", [(0, 2), (2, 0), (1, 3), (3, 1)])
        return v[:n], w


class AnyMesh:
    def perm(self):
        return jnp.arange(NBLK, dtype=jnp.int32)

    def middle(self):
        return jnp.ones((), jnp.int32)

    pipe = PlainPipe

    def first_hop(self, own):
        return lax.all_gather(own, ("dp", "ctx"), axis=0, tiled=True)

    def diagonal(self, own, hop):
        return ()

    diagonal_x = diagonal

    def both(self, full):
        n = full.shape[0] // 2
        return full[:n], full[n:]

    def pack(self, run, own, hop, diag):
        return hop

    def quarters_near(self, run, own, hop):
        n = hop.shape[0] // 4
        return hop[:n], hop[2 * n : 3 * n]

    def quarters_far(self, run, hop, diag):
        n = hop.shape[0] // 4
        return hop[n : 2 * n], hop[3 * n :]

    def scatter_cross(self, theirs):
        return theirs

    def scatter_own(self, run, pairs, got):
        full = jnp.concatenate([run(wgrad_call, *pairs, half=0), got], axis=0)
        return lax.psum_scatter(full, ("dp", "ctx"), scatter_dimension=0, tiled=True).astype(F32)

    def scatter_half(self, run, parts):
        return parts

    def scatter_last(self, run, plan, parts):
        outs, at = [], 0
        for count, turned in plan:
            v = parts[:, at * 512 : (at + count) * 512]
            outs.append(v.T if turned else v)
            at += count
        return outs

    def previous(self, kv, slots):
        own = kv.reshape(slots, -1, kv.shape[1])
        full = lax.all_gather(own, "ctx", axis=1, tiled=True)
        return full.reshape(-1, kv.shape[1])

    def give_back(self, dpv, dkv, slots):
        cols = dkv.shape[1]
        full = dpv.reshape(slots, -1, cols)
        got = lax.psum_scatter(full, "ctx", scatter_dimension=1, tiled=True)
        return dkv, got.reshape(-1, cols)

    def small_sum(self, group, everywhere):
        return lax.psum(group, ("dp", "ctx")), lax.psum(everywhere, ("dp", "ctx", "tensor"))


def rotary_tables(positions):
    half_rot = ROT // 2
    lane = jnp.arange(128, dtype=jnp.int32)
    exponent = (lane % half_rot).astype(F32) * (2.0 / ROT)
    angles = positions[:, None] * jnp.exp(-math.log(10000.0) * exponent)[None, :]
    cos_all, sin_all = jnp.cos(angles), jnp.sin(angles)
    cosf = jnp.where(lane < ROT, cos_all, 1.0)
    s1 = jnp.where(lane < half_rot, -sin_all, 0.0)
    s2 = jnp.where((lane >= half_rot) & (lane < ROT), sin_all, 0.0)
    return cosf, s1, s2


def local(small, block_input, out_grad, lengths, attn_gain, attn_shift, ffn_gain, ffn_shift, w_qkv, b_qkv, w_proj, b_proj, w_in, b_in, w_out, b_out):
    comm = SmallMesh() if small else AnyMesh()
    slots, local_len, d = block_input.shape
    m = slots * local_len
    nheads = b_qkv.shape[0] // (3 * HD)
    nq = 3 * nheads * HD
    ctx = lax.axis_index("ctx")
    meta = jnp.concatenate([ctx[None].astype(jnp.int32), comm.perm(), comm.middle()[None], lengths])

    run = Order()
    x2 = block_input.reshape(m, d)
    og2 = out_grad.reshape(m, d)
    ga, sa, gf, sf = (v.reshape(1, d) for v in (attn_gain, attn_shift, ffn_gain, ffn_shift))
    bq = b_qkv.reshape(1, nq)
    positions = ctx * local_len + jnp.arange(local_len, dtype=jnp.int32)
    tabs = rotary_tables(positions.astype(F32))

    own1 = jnp.concatenate([w_qkv, w_proj.T], axis=1).astype(BF)
    hop1 = comm.first_hop(own1)
    run.last = (own1,)
    h1, h2, g, stats, g_sum = run(norm_call, meta, x2, og2, ga, sa, gf, sf, local_len)
    own2 = w_in.astype(BF)
    own3 = w_out.T.astype(BF)
    diag1 = comm.diagonal(own1, hop1)
    hop2 = comm.first_hop(own2)
    near1 = comm.pack(run, own1, hop1, diag1)
    g1 = comm.both(near1)
    kv = run(kv_call, h1, *g1, bq, tabs, nheads)
    pv = comm.previous(kv, slots)
    diag2 = comm.diagonal_x(own2, hop2)
    hop3 = comm.first_hop(own3)
    q, dob = run(qd_call, h1, g, *g1, bq, tabs, nheads)
    near2 = comm.pack(run, own2, hop2, diag2)
    g2 = comm.both(near2)
    diag3 = comm.diagonal_x(own3, hop3)
    gb, dg = run(hidden_call, h2, *g2, b_in.reshape(1, -1))
    cross3 = comm.scatter_cross(run(wgrad_call, g, gb, half=1))
    one, three = comm.quarters_near(run, own3, hop3)
    ob, dq, dkv, dpv = run(attn_call, meta, q, kv, pv, dob, tabs, nheads)
    dkv, rv = comm.give_back(dpv, dkv, slots)

    pipe = comm.pipe(run, meta[1 + NBLK], 8)

    def out_part(c, quarter):
        return run(out_call, ob, gb, g1[c // 2], quarter, c)

    pipe.send(out_part(0, one))
    two, four = comm.quarters_far(run, hop3, diag3)
    pipe.send(out_part(2, three))
    pipe.send(out_part(1, two))
    last_out = out_part(3, four)
    pipe.cross()
    du, bin_sum = run(dhid_call, g, (one, two, three, four), dg)
    dqkv, bqkv_sum = run(join_call, dq, dkv, rv, tabs, nheads)
    pipe.cross()
    gain_sums = jnp.zeros((4, d), F32)
    dn_parts = []

    def back_part(c):
        nonlocal gain_sums
        part, gain_sums = run(back_call, meta, dqkv, du, g1[c // 2], g2[c // 2], x2, stats, ga, gf, gain_sums, c)
        dn_parts.append(part)

    ff = du.shape[1] // 512
    back_part(0)
    pipe.send(last_out)
    back_part(1)
    state3 = comm.scatter_own(run, (g, gb), cross3)
    pipe.cross()
    pipe.send(dn_parts[0])
    back_part(2)
    cross2 = comm.scatter_cross(run(wgrad_call, h2, du, half=1))
    pipe.cross()
    pipe.send(dn_parts[1])
    back_part(3)
    state3 = comm.scatter_half(run, state3)
    state2 = comm.scatter_own(run, (h2, du), cross2)
    pipe.cross()
    pipe.send(dn_parts[2])
    group, gains = comm.small_sum(
        jnp.concatenate([g_sum.reshape(-1), bqkv_sum.reshape(-1), bin_sum.reshape(-1)]),
        gain_sums.reshape(-1),
    )
    gains = gains.reshape(4, d)
    bias_grad = group[:d]
    (grad_out,) = comm.scatter_last(run, ((ff, True),), state3)
    cross1 = comm.scatter_cross(run(wgrad_call, h1, dqkv, g, ob, half=1))
    state2 = comm.scatter_half(run, state2)
    pipe.cross()
    pipe.send(dn_parts[3])
    state1 = comm.scatter_own(run, (h1, dqkv, g, ob), cross1)
    (grad_in,) = comm.scatter_last(run, ((ff, False),), state2)
    pipe.cross()
    pipe.send()
    state1 = comm.scatter_half(run, state1)
    order = (0, 2, 1, 3)

    def sums_of(first, order):
        return [v for c in order for v in (pipe.here[first + c], pipe.sent[first + c])]

    block_output = run(
        rows_call, meta, x2, (b_proj + b_out).reshape(1, d), *sums_of(0, order),
        body=functools.partial(block_out_kernel, local_len), name="bout", specs=("row", "vec") + ("part",) * 8,
    ).reshape(slots, local_len, d)
    pipe.cross()
    pipe.send()
    grad_qkv, grad_proj = comm.scatter_last(
        run, ((nq // 512, False), (nheads * HD // 512, True)), state1
    )
    pipe.send()
    input_grad = run(
        rows_call, meta, x2, og2, stats, *sums_of(4, range(4)),
        body=functools.partial(input_grad_kernel, local_len), name="igrad", specs=("row", "row", "stat") + ("part",) * 8,
    ).reshape(slots, local_len, d)
    return (
        block_output,
        input_grad,
        gains[0],
        gains[1],
        gains[2],
        gains[3],
        grad_qkv,
        group[d : d + nq],
        grad_proj,
        bias_grad,
        grad_in,
        group[d + nq :],
        grad_out,
        bias_grad,
    )


def solution(mesh):
    small = mesh.shape["dp"] == 4 and mesh.shape["ctx"] == 2 and mesh.shape["tensor"] == 4
    placed = (
        P("dp", "ctx", None),
        P("dp", "ctx", None),
        P("dp"),
        P(),
        P(),
        P(),
        P(),
        P(("dp", "ctx"), "tensor"),
        P("tensor"),
        P("tensor", ("dp", "ctx")),
        P(),
        P(("dp", "ctx"), "tensor"),
        P("tensor"),
        P("tensor", ("dp", "ctx")),
        P(),
    )
    return jax.shard_map(
        functools.partial(local, small),
        mesh=mesh,
        in_specs=placed,
        out_specs=(
            P("dp", "ctx", None),
            P("dp", "ctx", None),
            P(),
            P(),
            P(),
            P(),
            P(("dp", "ctx"), "tensor"),
            P("tensor"),
            P("tensor", ("dp", "ctx")),
            P(),
            P(("dp", "ctx"), "tensor"),
            P("tensor"),
            P("tensor", ("dp", "ctx")),
            P(),
        ),
        check_vma=False,
    )
```

time: 1270 us -> 606 us (0.48)
  waiting for transfers between devices: 878 us -> 194 us
  Pallas kernels: 0 us -> 273 us
  matrix products: 155 us -> 0 us
  local copies, waits for them, and re-layouts: 104 us -> 10.3 us
  starting transfers between devices: 1.25 us -> 80.1 us
  other arithmetic: 96.6 us -> 38.5 us
  loops' own time: 16.5 us -> 0 us
  between operations: 14.7 us -> 1.82 us
    psum x2 -> x0, waiting for transfers between devices: 538 us -> none  [the longest x1 427 us: local(): lax.psum(partial_out.astype(jnp.bfloat16), 'tensor').astype(jnp.float32)]
    pallas_call x0 -> x33, Pallas kernels: none -> 273 us  [the longest x6 57.4 us: wgrad_call(): pl.pallas_call(functools.partial(wgrad_kernel, counts, add is not None, s...]
    reduce_scatter x6 -> x0, waiting for transfers between devices: 233 us -> none  [the longest x1 72.4 us: local(): lax.psum_scatter(grad_w_out_local.astype(jnp.bfloat16), ('dp', 'ctx'), sc...]
    ppermute x0 -> x55, waiting for transfers between devices: none -> 194 us  [the longest x11 75.8 us: y(): return lax.ppermute(v, 'ctx', [(0, 1), (1, 0)])]
    dot_general x19 -> x0, matrix products: 155 us -> none  [the longest x4 44 us: dot_last(): lax.dot_general(left_side, right_side, (((1,), (1,)), ((), ())), preferre...]
    all_gather x6 -> x0, waiting for transfers between devices: 107 us -> none  [the longest x1 34.2 us: local(): lax.all_gather(weights_low[0], ('dp', 'ctx'), axis=0, tiled=True)]
    ppermute x0 -> x55, starting transfers between devices: none -> 80.1 us  [the longest x11 27.4 us: send(): got = lax.ppermute(v, 'tensor', pairs)]
    reduce_sum x7 -> x0, other arithmetic: 26.6 us -> none  [the longest x1 12.5 us: local(): grad_b_qkv_local = jnp.sum(grad_qkv, axis=0, dtype=jnp.float32)]
  transfers between devices with their start and end apart: 14 -> 55, of which waited for: 12 -> 15; matrix products, arithmetic and copies ran while one was open for 22% -> 7% of each run, Pallas kernels for 0% -> 36%
where the time goes in v1:
time: 606 us; the launch traced here: 598 us
  Pallas kernels  273 us (45%)
  waiting for transfers between devices  194 us (32%)
  starting transfers between devices  80.1 us (13%)
  other arithmetic  38.5 us (6%)
  local copies, waits for them, and re-layouts  10.3 us (2%)
    ppermute x11, waiting for transfers between devices, y(): return lax.ppermute(v, 'ctx', [(0, 1), (1, 0)])  75.8 us
    pallas_call x6, Pallas kernels, wgrad_call(): pl.pallas_call(functools.partial(wgrad_kernel, counts, add is not None, s...  57.4 us
    pallas_call x4, Pallas kernels, back_call(): pl.pallas_call(functools.partial(back_kernel, c), name='backn', grid_spec...  45.8 us
    ppermute x1, waiting for transfers between devices, small_sum(): w = w + lax.ppermute(w, 'tensor', [(0, 1), (1, 0), (2, 3), (3, 2)])  38.3 us
    ppermute x13, waiting for transfers between devices, x(): return lax.ppermute(v, 'dp', [(0, 2), (2, 0), (1, 3), (3, 1)])  32.4 us
    ppermute x11, starting transfers between devices, send(): got = lax.ppermute(v, 'tensor', pairs)  27.4 us
    pallas_call x4, Pallas kernels, out_call(): pl.pallas_call(out_kernel, name='outp', grid=(m // rows,), in_specs=[pl.B...  26 us
    convert_element_type x11, other arithmetic, add_bf(): return lax.optimization_barrier((a.astype(F32) + b.astype(F32)).astype(BF))  24.2 us
  transfers between devices with their start and end apart: 55, of which 15 were waited for; matrix products, arithmetic and copies ran while one was open for 7% of the time, Pallas kernels for 36%

profile of v1, /device:TPU:0, one launch (start us, length us, event | category | flops | bytes accessed | tf_op | source)
XLA Modules:
  0.0 597.9 jit_solution(4060641776934760998)
XLA Ops:
  2.5 3.1 collective-permute-start
  7.1 21.7 %collective-permute-done.refs_1_ = bf16[256,2048]{1,0:T(8,128)(2,1)S(1)} collective-permute-done((bf16[256,2048]{1,0:T(8,128)(2,1)S(1)}, bf16[256,2048]{1,0:T(8,128)(2,1)S(1)}, u32[]{:S(2)}, u32[]{:S(2)}) %collective-permute-start) | collective-permute-done | bytes 1048608 | tf_op jit(solution)/shard_map/ppermute | solution.py:812
  34.5 11.8 %norm.1 = (bf16[1024,2048]{1,0:T(8,128)(2,1)}, bf16[1024,2048]{1,0:T(8,128)(2,1)}, bf16[1024,2048]{1,0:T(8,128)(2,1)}, f32[1024,128]{1,0:T(8,128)}, f32[1,2048]{1,0:T(1,128)}) custom-call(s32[12]{0:T(128)} %pad_add_fusion.meta, bf16[1024,2048]{1,0:T(8,128)(2,1)} %bitcast.22, bf16[1024,2048]{1,0:T(8,128)(2,1)} %bitcast.29, f32[1,2048]{1,0:T(1,128)} %bitcast.40, ...), custom_call_target="tpu_custom_call" | custom-call | flops 41943040 | bytes 20971520 | tf_op jit(solution)/shard_map/norm/pallas_call | solution.py:88
  46.4 5.0 pack.4.wa.wp.w1
  53.0 24.2 %collective-permute-done.5.refs_1_ = bf16[256,2048]{1,0:T(8,128)(2,1)} collective-permute-done((bf16[256,2048]{1,0:T(8,128)(2,1)S(1)}, bf16[256,2048]{1,0:T(8,128)(2,1)}, u32[]{:S(2)}, u32[]{:S(2)}) %collective-permute-start.5) | collective-permute-done | bytes 1048608 | tf_op jit(solution)/shard_map/ppermute | solution.py:812
  79.6 9.8 %kv.1.kv_ref = bf16[1024,1024]{1,0:T(8,128)(2,1)} custom-call(bf16[1024,2048]{1,0:T(8,128)(2,1)} %get-tuple-element.186.h1.refs_0_, bf16[1024,2048]{1,0:T(8,128)(2,1)} %pack.4.wa.wp.w1, bf16[1024,2048]{1,0:T(8,128)(2,1)} %collective-permute-done.4.wb.wp.w1, f32[1,1536]{1,0:T(1,128)} %reshape.105.b_ref, f32[512,128]{1,0:T(8,128)} %get-tuple-element.222.cosf, ...), custom_call_target="tpu_custom_call" | custom-call | flops 4294967296 | bytes 10485760 | tf_op jit(solution)/shard_map/kv/pallas_call | solution.py:145
  89.4 10.5 %qd.1 = (bf16[1024,512]{1,0:T(8,128)(2,1)}, bf16[1024,512]{1,0:T(8,128)(2,1)}) custom-call(bf16[1024,2048]{1,0:T(8,128)(2,1)} %get-tuple-element.186.h1.refs_0_, bf16[1024,2048]{1,0:T(8,128)(2,1)} %get-tuple-element.152.g.refs_0_.refs_2_, bf16[1024,2048]{1,0:T(8,128)(2,1)} %pack.4.wa.wp.w1, bf16[1024,2048]{1,0:T(8,128)(2,1)} %collective-permute-done.4.wb.wp.w1, ...), custom_call_target="tpu_custom_call" | custom-call | flops 4294967296 | bytes 14680064 | tf_op jit(solution)/shard_map/qd/pallas_call | solution.py:184
  99.9 2.4 collective-permute-done.7.refs_3_
  102.3 4.7 pack.5.wa.w2
  108.2 5.2 collective-permute-start.10
  114.0 19.4 %collective-permute-done.9.refs_1_ = bf16[256,2048]{1,0:T(8,128)(2,1)} collective-permute-done((bf16[256,2048]{1,0:T(8,128)(2,1)S(1)}, bf16[256,2048]{1,0:T(8,128)(2,1)}, u32[]{:S(2)}, u32[]{:S(2)}) %collective-permute-start.9) | collective-permute-done | bytes 1048608 | tf_op jit(solution)/shard_map/ppermute | solution.py:812
  133.9 16.4 %hidden.1 = (bf16[1024,2048]{1,0:T(8,128)(2,1)}, bf16[1024,2048]{1,0:T(8,128)(2,1)}) custom-call(bf16[1024,2048]{1,0:T(8,128)(2,1)} %get-tuple-element.170.h2.refs_0_, bf16[1024,2048]{1,0:T(8,128)(2,1)} %pack.5.wa.w2, bf16[1024,2048]{1,0:T(8,128)(2,1)} %collective-permute-done.8.wb.w2, f32[1,2048]{1,0:T(1,128)} %bitcast.57), custom_call_target="tpu_custom_call" | custom-call | flops 8589934592 | bytes 20971520 | tf_op jit(solution)/shard_map/hidden/pallas_call | solution.py:375
  150.2 8.6 %wgrad.6 = bf16[1024,2048]{1,0:T(8,128)(2,1)} custom-call(bf16[1024,2048]{1,0:T(8,128)(2,1)} %get-tuple-element.152.g.refs_0_.refs_2_, bf16[1024,2048]{1,0:T(8,128)(2,1)} %get-tuple-element.124.refs_1_.gb), custom_call_target="tpu_custom_call" | custom-call | flops 4294967296 | bytes 14680064 | tf_op jit(solution)/shard_map/wgrad/pallas_call | solution.py:560
  158.8 3.9 pack.6.wo.w0
  162.7 13.6 %collective-permute-done.10.pv_ref = bf16[1024,1024]{1,0:T(8,128)(2,1)} collective-permute-done((bf16[1024,1024]{1,0:T(8,128)(2,1)}, bf16[1024,1024]{1,0:T(8,128)(2,1)}, u32[]{:S(2)}, u32[]{:S(2)}) %collective-permute-start.10) | collective-permute-done | bytes 2097184 | tf_op jit(solution)/shard_map/ppermute | solution.py:862
  176.3 12.5 %attn.1 = (bf16[1024,512]{1,0:T(8,128)(2,1)}, bf16[1024,512]{1,0:T(8,128)(2,1)}, f32[1024,1024]{1,0:T(8,128)}, bf16[1024,1024]{1,0:T(8,128)(2,1)}) custom-call(s32[12]{0:T(128)} %pad_add_fusion.meta, bf16[1024,512]{1,0:T(8,128)(2,1)} %get-tuple-element.121.q_ref, bf16[1024,1024]{1,0:T(8,128)(2,1)} %kv.1.kv_ref, ...), custom_call_target="tpu_custom_call" | custom-call | flops 6442450944 | bytes 10485760 | tf_op jit(solution)/shard_map/attn/pallas_call | solution.py:294
  188.8 6.5 %outp.4 = bf16[1024,512]{1,0:T(8,128)(2,1)} custom-call(bf16[1024,512]{1,0:T(8,128)(2,1)} %get-tuple-element.135.ob.refs_3_, bf16[1024,2048]{1,0:T(8,128)(2,1)} %get-tuple-element.124.refs_1_.gb, bf16[1024,2048]{1,0:T(8,128)(2,1)} %pack.4.wa.wp.w1, bf16[512,2048]{1,0:T(8,128)(2,1)} %pack.6.wo.w0), custom_call_target="tpu_custom_call" | custom-call | flops 2684354560 | bytes 8912896 | tf_op jit(solution)/shard_map/outp/pallas_call | solution.py:424
  195.3 3.8 pack.7.wo.w1
  199.6 4.5 collective-permute-start.15
  206.7 6.5 %outp.5 = bf16[1024,512]{1,0:T(8,128)(2,1)} custom-call(bf16[1024,512]{1,0:T(8,128)(2,1)} %get-tuple-element.135.ob.refs_3_, bf16[1024,2048]{1,0:T(8,128)(2,1)} %get-tuple-element.124.refs_1_.gb, bf16[1024,2048]{1,0:T(8,128)(2,1)} %collective-permute-done.4.wb.wp.w1, bf16[512,2048]{1,0:T(8,128)(2,1)} %copy-done.27), custom_call_target="tpu_custom_call" | custom-call | flops 2684354560 | bytes 8912896 | tf_op jit(solution)/shard_map/outp/pallas_call | solution.py:424
  213.2 2.3 collective-permute-start.17
  215.4 6.5 %outp.6 = bf16[1024,512]{1,0:T(8,128)(2,1)} custom-call(bf16[1024,512]{1,0:T(8,128)(2,1)} %get-tuple-element.135.ob.refs_3_, bf16[1024,2048]{1,0:T(8,128)(2,1)} %get-tuple-element.124.refs_1_.gb, bf16[1024,2048]{1,0:T(8,128)(2,1)} %pack.4.wa.wp.w1, bf16[512,2048]{1,0:T(8,128)(2,1)} %pack.7.wo.w1), custom_call_target="tpu_custom_call" | custom-call | flops 2684354560 | bytes 8912896 | tf_op jit(solution)/shard_map/outp/pallas_call | solution.py:424
  221.9 6.5 %outp.7 = bf16[1024,512]{1,0:T(8,128)(2,1)} custom-call(bf16[1024,512]{1,0:T(8,128)(2,1)} %get-tuple-element.135.ob.refs_3_, bf16[1024,2048]{1,0:T(8,128)(2,1)} %get-tuple-element.124.refs_1_.gb, bf16[1024,2048]{1,0:T(8,128)(2,1)} %collective-permute-done.4.wb.wp.w1, bf16[512,2048]{1,0:T(8,128)(2,1)} %collective-permute-done.14.wo.w3), custom_call_target="tpu_custom_call" | custom-call | flops 2684354560 | bytes 8912896 | tf_op jit(solution)/shard_map/outp/pallas_call | solution.py:424
  232.1 5.7 collective-permute-start.20
  237.8 15.0 %dhid.1 = (bf16[1024,2048]{1,0:T(8,128)(2,1)}, f32[1,2048]{1,0:T(1,128)}) custom-call(bf16[1024,2048]{1,0:T(8,128)(2,1)} %get-tuple-element.152.g.refs_0_.refs_2_, bf16[512,2048]{1,0:T(8,128)(2,1)} %pack.6.wo.w0, bf16[512,2048]{1,0:T(8,128)(2,1)} %pack.7.wo.w1, bf16[512,2048]{1,0:T(8,128)(2,1)} %copy-done.27, ...), custom_call_target="tpu_custom_call" | custom-call | flops 8589934592 | bytes 20971520 | tf_op jit(solution)/shard_map/dhid/pallas_call | solution.py:402
  252.8 8.5 %collective-permute-done.16.rv_ref = bf16[1024,1024]{1,0:T(8,128)(2,1)} collective-permute-done((bf16[1024,1024]{1,0:T(8,128)(2,1)}, bf16[1024,1024]{1,0:T(8,128)(2,1)}, u32[]{:S(2)}, u32[]{:S(2)}) %collective-permute-start.16) | collective-permute-done | bytes 2097184 | tf_op jit(solution)/shard_map/ppermute | solution.py:865
  261.3 6.0 join.1
  267.3 2.5 add_convert_fusion.14
  272.0 11.5 %backn.4 = (bf16[1024,512]{1,0:T(8,128)(2,1)}, f32[4,2048]{1,0:T(4,128)}) custom-call(s32[12]{0:T(128)} %pad_add_fusion.meta, bf16[1024,1536]{1,0:T(8,128)(2,1)} %get-tuple-element.143.dqkv.refs_1_, bf16[1024,2048]{1,0:T(8,128)(2,1)} %get-tuple-element.139.du.refs_1_, bf16[1024,2048]{1,0:T(8,128)(2,1)} %pack.4.wa.wp.w1, ...), custom_call_target="tpu_custom_call", output_to_operand_aliasing={{1}: (9, {})} | custom-call | flops 3758096384 | bytes 13107200 | tf_op jit(solution)/shard_map/backn/pallas_call | solution.py:473
  285.6 11.4 %backn.5 = (bf16[1024,512]{1,0:T(8,128)(2,1)}, f32[4,2048]{1,0:T(4,128)}) custom-call(s32[12]{0:T(128)} %pad_add_fusion.meta, bf16[1024,1536]{1,0:T(8,128)(2,1)} %get-tuple-element.143.dqkv.refs_1_, bf16[1024,2048]{1,0:T(8,128)(2,1)} %get-tuple-element.139.du.refs_1_, bf16[1024,2048]{1,0:T(8,128)(2,1)} %pack.4.wa.wp.w1, ...), custom_call_target="tpu_custom_call", output_to_operand_aliasing={{1}: (9, {})} | custom-call | flops 3758096384 | bytes 13107200 | tf_op jit(solution)/shard_map/backn/pallas_call | solution.py:473
  297.0 9.8 %wgrad.7 = (bf16[512,1024]{1,0:T(8,128)(2,1)}, bf16[512,1024]{1,0:T(8,128)(2,1)}, bf16[512,1024]{1,0:T(8,128)(2,1)}, bf16[512,1024]{1,0:T(8,128)(2,1)}) custom-call(bf16[1024,2048]{1,0:T(8,128)(2,1)} %get-tuple-element.152.g.refs_0_.refs_2_, bf16[1024,2048]{1,0:T(8,128)(2,1)} %get-tuple-element.124.refs_1_.gb, bf16[1024,2048]{1,0:T(8,128)(2,1)} %collective-permute-done.19.refs_2_), custom_call_target="tpu_custom_call" | custom-call | flops 4294967296 | bytes 14680064 | tf_op jit(solution)/shard_map/wgrad/pallas_call | solution.py:560
  306.8 2.6 add_convert_fusion.12
  311.4 11.4 %backn.6 = (bf16[1024,512]{1,0:T(8,128)(2,1)}, f32[4,2048]{1,0:T(4,128)}) custom-call(s32[12]{0:T(128)} %pad_add_fusion.meta, bf16[1024,1536]{1,0:T(8,128)(2,1)} %get-tuple-element.143.dqkv.refs_1_, bf16[1024,2048]{1,0:T(8,128)(2,1)} %get-tuple-element.139.du.refs_1_, ...), custom_call_target="tpu_custom_call", output_to_operand_aliasing={{1}: (9, {})} | custom-call | flops 3758096384 | bytes 13107200 | tf_op jit(solution)/shard_map/backn/pallas_call | solution.py:473
  322.8 8.6 %wgrad.8 = bf16[1024,2048]{1,0:T(8,128)(2,1)} custom-call(bf16[1024,2048]{1,0:T(8,128)(2,1)} %get-tuple-element.170.h2.refs_0_, bf16[1024,2048]{1,0:T(8,128)(2,1)} %get-tuple-element.139.du.refs_1_), custom_call_target="tpu_custom_call" | custom-call | flops 4294967296 | bytes 14680064 | tf_op jit(solution)/shard_map/wgrad/pallas_call | solution.py:560
  334.7 22.3 %collective-permute-done.22.refs_1_ = bf16[1024,512]{1,0:T(8,128)(2,1)S(1)} collective-permute-done((bf16[1024,512]{1,0:T(8,128)(2,1)S(1)}, bf16[1024,512]{1,0:T(8,128)(2,1)S(1)}, u32[]{:S(2)}, u32[]{:S(2)}) %collective-permute-start.22) | collective-permute-done | bytes 1048608 | tf_op jit(solution)/shard_map/ppermute | solution.py:777
  361.0 11.4 %backn.7 = (bf16[1024,512]{1,0:T(8,128)(2,1)}, f32[4,2048]{1,0:T(4,128)}) custom-call(s32[12]{0:T(128)} %pad_add_fusion.meta, bf16[1024,1536]{1,0:T(8,128)(2,1)} %get-tuple-element.143.dqkv.refs_1_, bf16[1024,2048]{1,0:T(8,128)(2,1)} %get-tuple-element.139.du.refs_1_, ...), custom_call_target="tpu_custom_call", output_to_operand_aliasing={{1}: (9, {})} | custom-call | flops 3758096384 | bytes 13107200 | tf_op jit(solution)/shard_map/backn/pallas_call | solution.py:473
  372.5 3.5 hsum.3
  378.1 9.9 %wgrad.9 = (bf16[512,1024]{1,0:T(8,128)(2,1)}, bf16[512,1024]{1,0:T(8,128)(2,1)}, bf16[512,1024]{1,0:T(8,128)(2,1)}, bf16[512,1024]{1,0:T(8,128)(2,1)}) custom-call(bf16[1024,2048]{1,0:T(8,128)(2,1)} %get-tuple-element.170.h2.refs_0_, bf16[1024,2048]{1,0:T(8,128)(2,1)} %get-tuple-element.139.du.refs_1_, bf16[1024,2048]{1,0:T(8,128)(2,1)} %collective-permute-done.26.refs_2_), custom_call_target="tpu_custom_call" | custom-call | flops 4294967296 | bytes 14680064 | tf_op jit(solution)/shard_map/wgrad/pallas_call | solution.py:560
  388.0 2.9 add_convert_fusion.8
  390.9 2.9 fusion.3.refs_6_
  394.6 4.5 lsum.3
  399.1 9.4 %wgrad.10 = bf16[1024,2048]{1,0:T(8,128)(2,1)} custom-call(bf16[1024,2048]{1,0:T(8,128)(2,1)} %get-tuple-element.186.h1.refs_0_, bf16[1024,1536]{1,0:T(8,128)(2,1)} %get-tuple-element.143.dqkv.refs_1_, bf16[1024,2048]{1,0:T(8,128)(2,1)} %get-tuple-element.152.g.refs_0_.refs_2_, bf16[1024,512]{1,0:T(8,128)(2,1)} %get-tuple-element.135.ob.refs_3_), custom_call_target="tpu_custom_call" | custom-call | flops 4294967296 | bytes 16777216 | tf_op jit(solution)/shard_map/wgrad/pallas_call | solution.py:560
  410.5 3.9 collective-permute-start.33
  416.1 18.2 %collective-permute-done.31.got_x = bf16[512,1024]{1,0:T(8,128)(2,1)S(1)} collective-permute-done((bf16[512,1024]{1,0:T(8,128)(2,1)}, bf16[512,1024]{1,0:T(8,128)(2,1)S(1)}, u32[]{:S(2)}, u32[]{:S(2)}) %collective-permute-start.31) | collective-permute-done | bytes 1048608 | tf_op jit(solution)/shard_map/ppermute | solution.py:806
  434.3 3.0 collective-permute-start.38
  438.3 3.6 hsum.4
  441.9 2.6 add_convert_fusion.6
  449.4 2.0 fusion.4.refs_0_
  451.4 11.1 %wgrad.11 = (bf16[512,1024]{1,0:T(8,128)(2,1)}, bf16[512,1024]{1,0:T(8,128)(2,1)}, bf16[512,1024]{1,0:T(8,128)(2,1)}, bf16[512,1024]{1,0:T(8,128)(2,1)}) custom-call(bf16[1024,2048]{1,0:T(8,128)(2,1)} %get-tuple-element.186.h1.refs_0_, bf16[1024,1536]{1,0:T(8,128)(2,1)} %get-tuple-element.143.dqkv.refs_1_, ...), custom_call_target="tpu_custom_call" | custom-call | flops 4294967296 | bytes 16777216 | tf_op jit(solution)/shard_map/wgrad/pallas_call | solution.py:560
  463.7 3.0 collective-permute-start.42
  467.3 4.4 lsum.4
  471.8 2.5 add_convert_fusion.4
  477.7 9.1 %collective-permute-done.40.got_x = bf16[512,1024]{1,0:T(8,128)(2,1)} collective-permute-done((bf16[512,1024]{1,0:T(8,128)(2,1)}, bf16[512,1024]{1,0:T(8,128)(2,1)}, u32[]{:S(2)}, u32[]{:S(2)}) %collective-permute-start.40) | collective-permute-done | bytes 1048608 | tf_op jit(solution)/shard_map/ppermute | solution.py:806
  487.1 3.5 hsum.5
  490.6 8.8 %bout.1 = bf16[1024,2048]{1,0:T(8,128)(2,1)} custom-call(s32[12]{0:T(128)} %pad_add_fusion.meta, bf16[1024,2048]{1,0:T(8,128)(2,1)} %bitcast.27, f32[1,2048]{1,0:T(1,128)} %bitcast.50, bf16[1024,512]{1,0:T(8,128)(2,1)} %copy-done.1, bf16[1024,512]{1,0:T(8,128)(2,1)} %copy-done.3, bf16[1024,512]{1,0:T(8,128)(2,1)} %copy-done.9, ...), custom_call_target="tpu_custom_call" | custom-call | flops 20971520 | bytes 16777216 | tf_op jit(solution)/shard_map/bout/pallas_call | solution.py:716
  499.5 2.5 add_convert_fusion.2
  509.0 6.6 %collective-permute-done.44.got_y = bf16[256,1024]{1,0:T(8,128)(2,1)S(1)} collective-permute-done((bf16[256,1024]{1,0:T(8,128)(2,1)}, bf16[256,1024]{1,0:T(8,128)(2,1)S(1)}, u32[]{:S(2)}, u32[]{:S(2)}) %collective-permute-start.44) | collective-permute-done | bytes 524320 | tf_op jit(solution)/shard_map/ppermute | solution.py:812
  517.7 4.5 lsum.5
  526.8 2.7 collective-permute-done.51
  530.2 3.6 collective-permute-done.52
  533.8 7.3 %collective-permute-start.53 = (f32[8192]{0:T(1024)S(1)}, f32[8192]{0:T(1024)S(1)}, u32[]{:S(2)}, u32[]{:S(2)}) collective-permute-start(f32[8192]{0:T(1024)S(1)} %slice.50), channel_id=1, source_target_pairs={{0,1},{1,0},{2,3},{3,2},{4,5},{5,4},{6,7},{7,6},{8,9},{9,8},{10,11... | collective-permute-start | bytes 98312 | tf_op jit(solution)/shard_map/ppermute | solution.py:874
  541.1 38.3 %collective-permute-done.53 = f32[8192]{0:T(1024)S(1)} collective-permute-done((f32[8192]{0:T(1024)S(1)}, f32[8192]{0:T(1024)S(1)}, u32[]{:S(2)}, u32[]{:S(2)}) %collective-permute-start.53) | collective-permute-done | bytes 32800 | tf_op jit(solution)/shard_map/ppermute | solution.py:874
  581.2 3.1 collective-permute-done.54
  584.9 12.0 %igrad.1 = bf16[1024,2048]{1,0:T(8,128)(2,1)} custom-call(s32[12]{0:T(128)} %pad_add_fusion.meta, bf16[1024,2048]{1,0:T(8,128)(2,1)} %bitcast.28, bf16[1024,2048]{1,0:T(8,128)(2,1)} %bitcast.30, f32[1024,128]{1,0:T(8,128)} %get-tuple-element.146.st_ref, bf16[1024,512]{1,0:T(8,128)(2,1)} %copy-done.4, bf16[1024,512]{1,0:T(8,128)(2,1)} %collective-permute-done.42.refs_1_, ...), custom_call_target="tpu_custom_call" | custom-call | flops 20971520 | bytes 16777216 | tf_op jit(solution)/shard_map/igrad/pallas_call | solution.py:716
  (217 shorter events, 70.7 us)
Async XLA Ops:
  2.4 31.5 %copy-start.44 = (s32[2]{0:T(128)S(1)}, s32[2]{0:T(128)}, u32[]{:S(2)}) copy-start(s32[2]{0:T(128)} %param.17) | copy-start | bytes 28
  2.5 43.8 %copy-start.22 = (bf16[256,2048]{1,0:T(8,128)(2,1)}, bf16[256,2048]{1,0:T(8,128)(2,1)S(1)}, u32[]{:S(2)}) copy-start(bf16[256,2048]{1,0:T(8,128)(2,1)S(1)} %pad_maximum_fusion.refs_0_) | copy-start | bytes 3145732
  2.5 26.2 %collective-permute-start = (bf16[256,2048]{1,0:T(8,128)(2,1)S(1)}, bf16[256,2048]{1,0:T(8,128)(2,1)S(1)}, u32[]{:S(2)}, u32[]{:S(2)}) collective-permute-start(bf16[256,2048]{1,0:T(8,128)(2,1)S(1)} %pad_maximum_fusion.refs_0_), channel_id=1, source_target_pairs={{0,4},{4,0},{1,5},{5,1},{2,6},{6,2},{3,7},{7,3},{8,12},{12,8},{9,1... | collective-permute-start | bytes 3145736 | tf_op jit(solution)/shard_map/ppermute | solution.py:812
  5.6 25.8 %collective-permute-start.1 = (bf16[256,2048]{1,0:T(8,128)(2,1)S(1)}, bf16[256,2048]{1,0:T(8,128)(2,1)S(1)}, u32[]{:S(2)}, u32[]{:S(2)}) collective-permute-start(bf16[256,2048]{1,0:T(8,128)(2,1)S(1)} %pad_maximum_fusion.refs_0_), channel_id=1, source_target_pairs={{0,16},{16,0},{8,24},{24,8},{1,17},{17,1},{9,25},{25,9},{2,18},{18... | collective-permute-start | bytes 3145736 | tf_op jit(solution)/shard_map/ppermute | solution.py:806
  29.7 16.7 %collective-permute-start.2 = (bf16[128,2048]{1,0:T(8,128)(2,1)}, bf16[128,2048]{1,0:T(8,128)(2,1)}, u32[]{:S(2)}, u32[]{:S(2)}) collective-permute-start(bf16[128,2048]{1,0:T(8,128)(2,1)} %slice.48), channel_id=1, source_target_pairs={{0,16},{16,0},{8,24},{24,8},{1,17},{17,1},{9,25},{25,9},{2,18},{18... | collective-permute-start | bytes 1572872 | tf_op jit(solution)/shard_map/ppermute | solution.py:806
  32.3 14.1 %collective-permute-start.3 = (bf16[128,2048]{1,0:T(8,128)(2,1)}, bf16[128,2048]{1,0:T(8,128)(2,1)}, u32[]{:S(2)}, u32[]{:S(2)}) collective-permute-start(bf16[128,2048]{1,0:T(8,128)(2,1)} %slice.49), channel_id=1, source_target_pairs={{0,4},{4,0},{1,5},{5,1},{2,6},{6,2},{3,7},{7,3},{8,12},{12,8},{9,1... | collective-permute-start | bytes 1572872 | tf_op jit(solution)/shard_map/ppermute | solution.py:812
  51.4 28.2 %collective-permute-start.4 = (bf16[1024,2048]{1,0:T(8,128)(2,1)}, bf16[1024,2048]{1,0:T(8,128)(2,1)}, u32[]{:S(2)}, u32[]{:S(2)}) collective-permute-start(bf16[1024,2048]{1,0:T(8,128)(2,1)} %pack.4.wa.wp.w1), channel_id=1, source_target_pairs={{0,8},{8,0},{16,24},{24,16},{1,9},{9,1},{17,25},{25,17},{2,10},{10... | collective-permute-start | bytes 12582920 | tf_op jit(solution)/shard_map/ppermute | solution.py:809
  51.5 37.9 %copy-start.21 = (bf16[256,2048]{1,0:T(8,128)(2,1)}, bf16[256,2048]{1,0:T(8,128)(2,1)S(1)}, u32[]{:S(2)}) copy-start(bf16[256,2048]{1,0:T(8,128)(2,1)S(1)} %convert_element_type.174.refs_0_) | copy-start | bytes 3145732
  51.5 25.7 %collective-permute-start.5 = (bf16[256,2048]{1,0:T(8,128)(2,1)S(1)}, bf16[256,2048]{1,0:T(8,128)(2,1)}, u32[]{:S(2)}, u32[]{:S(2)}) collective-permute-start(bf16[256,2048]{1,0:T(8,128)(2,1)S(1)} %convert_element_type.174.refs_0_), channel_id=1, source_target_pairs={{0,4},{4,0},{1,5},{5,1},{2,6},{6,2},{3,7},{7,3},{8,12},{12,8},{9,1... | collective-permute-start | bytes 3145736 | tf_op jit(solution)/shard_map/ppermute | solution.py:812
  52.0 47.9 %collective-permute-start.6 = (bf16[256,2048]{1,0:T(8,128)(2,1)S(1)}, bf16[256,2048]{1,0:T(8,128)(2,1)}, u32[]{:S(2)}, u32[]{:S(2)}) collective-permute-start(bf16[256,2048]{1,0:T(8,128)(2,1)S(1)} %convert_element_type.174.refs_0_), channel_id=1, source_target_pairs={{0,16},{16,0},{8,24},{24,8},{1,17},{17,1},{9,25},{25,9},{2,18},{18... | collective-permute-start | bytes 3145736 | tf_op jit(solution)/shard_map/ppermute | solution.py:806
  77.3 25.0 %collective-permute-start.7 = (bf16[256,2048]{1,0:T(8,128)(2,1)}, bf16[256,2048]{1,0:T(8,128)(2,1)}, u32[]{:S(2)}, u32[]{:S(2)}) collective-permute-start(bf16[256,2048]{1,0:T(8,128)(2,1)} %collective-permute-done.5.refs_1_), channel_id=1, source_target_pairs={{0,16},{16,0},{8,24},{24,8},{1,17},{17,1},{9,25},{25,9},{2,18},{18... | collective-permute-start | bytes 3145736 | tf_op jit(solution)/shard_map/ppermute | solution.py:806
  107.0 26.8 %collective-permute-start.8 = (bf16[1024,2048]{1,0:T(8,128)(2,1)}, bf16[1024,2048]{1,0:T(8,128)(2,1)}, u32[]{:S(2)}, u32[]{:S(2)}) collective-permute-start(bf16[1024,2048]{1,0:T(8,128)(2,1)} %pack.5.wa.w2), channel_id=1, source_target_pairs={{0,8},{8,0},{16,24},{24,16},{1,9},{9,1},{17,25},{25,17},{2,10},{10... | collective-permute-start | bytes 12582920 | tf_op jit(solution)/shard_map/ppermute | solution.py:809
  107.6 42.6 %copy-start.20 = (bf16[2048,256]{0,1:T(8,128)(2,1)}, bf16[2048,256]{0,1:T(8,128)(2,1)S(1)}, u32[]{:S(2)}) copy-start(bf16[2048,256]{0,1:T(8,128)(2,1)S(1)} %copy.34) | copy-start | bytes 3145732
  107.7 25.7 %collective-permute-start.9 = (bf16[256,2048]{1,0:T(8,128)(2,1)S(1)}, bf16[256,2048]{1,0:T(8,128)(2,1)}, u32[]{:S(2)}, u32[]{:S(2)}) collective-permute-start(bf16[256,2048]{1,0:T(8,128)(2,1)S(1)} %bitcast.32), channel_id=1, source_target_pairs={{0,4},{4,0},{1,5},{5,1},{2,6},{6,2},{3,7},{7,3},{8,12},{12,8},{9,1... | collective-permute-start | bytes 3145736 | tf_op jit(solution)/shard_map/ppermute | solution.py:812
  108.2 68.1 %collective-permute-start.10 = (bf16[1024,1024]{1,0:T(8,128)(2,1)}, bf16[1024,1024]{1,0:T(8,128)(2,1)}, u32[]{:S(2)}, u32[]{:S(2)}) collective-permute-start(bf16[1024,1024]{1,0:T(8,128)(2,1)} %kv.1.kv_ref), channel_id=1, source_target_pairs={{0,4},{1,5},{2,6},{3,7},{8,12},{9,13},{10,14},{11,15},{16,20},{17,... | collective-permute-start | bytes 6291464 | tf_op jit(solution)/shard_map/ppermute | solution.py:862
  113.4 81.9 %collective-permute-start.11 = (bf16[256,2048]{1,0:T(8,128)(2,1)S(1)}, bf16[256,2048]{1,0:T(8,128)(2,1)}, u32[]{:S(2)}, u32[]{:S(2)}) collective-permute-start(bf16[256,2048]{1,0:T(8,128)(2,1)S(1)} %bitcast.33), channel_id=1, source_target_pairs={{0,16},{16,0},{8,24},{24,8},{1,17},{17,1},{9,25},{25,9},{2,18},{18... | collective-permute-start | bytes 3145736 | tf_op jit(solution)/shard_map/ppermute | solution.py:806
  133.4 61.9 %collective-permute-start.12 = (bf16[256,2048]{1,0:T(8,128)(2,1)}, bf16[256,2048]{1,0:T(8,128)(2,1)}, u32[]{:S(2)}, u32[]{:S(2)}) collective-permute-start(bf16[256,2048]{1,0:T(8,128)(2,1)} %collective-permute-done.9.refs_1_), channel_id=1, source_target_pairs={{0,16},{16,0},{8,24},{24,8},{1,17},{17,1},{9,25},{25,9},{2,18},{18... | collective-permute-start | bytes 3145736 | tf_op jit(solution)/shard_map/ppermute | solution.py:806
  162.7 42.6 %collective-permute-start.13 = (bf16[512,2048]{1,0:T(8,128)(2,1)}, bf16[512,2048]{1,0:T(8,128)(2,1)S(1)}, u32[]{:S(2)}, u32[]{:S(2)}) collective-permute-start(bf16[512,2048]{1,0:T(8,128)(2,1)} %pack.6.wo.w0), channel_id=1, source_target_pairs={{0,8},{8,0},{16,24},{24,16},{1,9},{9,1},{17,25},{25,17},{2,10},{10... | collective-permute-start | bytes 6291464 | tf_op jit(solution)/shard_map/ppermute | solution.py:809
  199.1 22.9 %collective-permute-start.14 = (bf16[512,2048]{1,0:T(8,128)(2,1)}, bf16[512,2048]{1,0:T(8,128)(2,1)}, u32[]{:S(2)}, u32[]{:S(2)}) collective-permute-start(bf16[512,2048]{1,0:T(8,128)(2,1)} %pack.7.wo.w1), channel_id=1, source_target_pairs={{0,8},{8,0},{16,24},{24,16},{1,9},{9,1},{17,25},{25,17},{2,10},{10... | collective-permute-start | bytes 6291464 | tf_op jit(solution)/shard_map/ppermute | solution.py:809
  199.1 97.9 %collective-permute-start.19 = (bf16[1024,2048]{1,0:T(8,128)(2,1)}, bf16[1024,2048]{1,0:T(8,128)(2,1)}, u32[]{:S(2)}, u32[]{:S(2)}) collective-permute-start(bf16[1024,2048]{1,0:T(8,128)(2,1)} %wgrad.6), channel_id=1, source_target_pairs={{0,8},{8,0},{16,24},{24,16},{1,9},{9,1},{17,25},{25,17},{2,10},{10... | collective-permute-start | bytes 12582920 | tf_op jit(solution)/shard_map/ppermute | solution.py:809
  199.6 28.9 %collective-permute-start.15 = (bf16[1024,512]{1,0:T(8,128)(2,1)}, bf16[1024,512]{1,0:T(8,128)(2,1)}, u32[]{:S(2)}, u32[]{:S(2)}) collective-permute-start(bf16[1024,512]{1,0:T(8,128)(2,1)} %outp.4), channel_id=1, source_target_pairs={{0,1},{3,2},{4,5},{7,6},{8,9},{11,10},{12,13},{15,14},{16,17},{19,... | collective-permute-start | bytes 3145736 | tf_op jit(solution)/shard_map/ppermute | solution.py:777
  204.1 57.2 %collective-permute-start.16 = (bf16[1024,1024]{1,0:T(8,128)(2,1)}, bf16[1024,1024]{1,0:T(8,128)(2,1)}, u32[]{:S(2)}, u32[]{:S(2)}) collective-permute-start(bf16[1024,1024]{1,0:T(8,128)(2,1)} %get-tuple-element.142), channel_id=1, source_target_pairs={{4,0},{5,1},{6,2},{7,3},{12,8},{13,9},{14,10},{15,11},{20,16},{21,... | collective-permute-start | bytes 6291464 | tf_op jit(solution)/shard_map/ppermute | solution.py:865
  213.2 54.1 %collective-permute-start.17 = (bf16[1024,512]{1,0:T(8,128)(2,1)}, bf16[1024,512]{1,0:T(8,128)(2,1)}, u32[]{:S(2)}, u32[]{:S(2)}) collective-permute-start(bf16[1024,512]{1,0:T(8,128)(2,1)} %outp.5), channel_id=1, source_target_pairs={{0,1},{3,2},{4,5},{7,6},{8,9},{11,10},{12,13},{15,14},{16,17},{19,... | collective-permute-start | bytes 3145736 | tf_op jit(solution)/shard_map/ppermute | solution.py:777
  230.4 53.2 %collective-permute-start.18 = (bf16[1024,512]{1,0:T(8,128)(2,1)S(1)}, bf16[1024,512]{1,0:T(8,128)(2,1)}, u32[]{:S(2)}, u32[]{:S(2)}) collective-permute-start(bf16[1024,512]{1,0:T(8,128)(2,1)S(1)} %add_convert_fusion.15), channel_id=1, source_target_pairs={{1,2},{2,1},{5,6},{6,5},{9,10},{10,9},{13,14},{14,13},{17,18},{18,... | collective-permute-start | bytes 3145736 | tf_op jit(solution)/shard_map/ppermute | solution.py:787
  232.1 74.8 %collective-permute-start.20 = (bf16[1024,512]{1,0:T(8,128)(2,1)S(1)}, bf16[1024,512]{1,0:T(8,128)(2,1)}, u32[]{:S(2)}, u32[]{:S(2)}) collective-permute-start(bf16[1024,512]{1,0:T(8,128)(2,1)S(1)} %copy-done.16), channel_id=1, source_target_pairs={{0,1},{3,2},{4,5},{7,6},{8,9},{11,10},{12,13},{15,14},{16,17},{19,... | collective-permute-start | bytes 3145736 | tf_op jit(solution)/shard_map/ppermute | solution.py:777
  269.8 39.7 %collective-permute-start.21 = (bf16[1024,512]{1,0:T(8,128)(2,1)}, bf16[1024,512]{1,0:T(8,128)(2,1)}, u32[]{:S(2)}, u32[]{:S(2)}) collective-permute-start(bf16[1024,512]{1,0:T(8,128)(2,1)} %add_convert_fusion.14), channel_id=1, source_target_pairs={{1,2},{2,1},{5,6},{6,5},{9,10},{10,9},{13,14},{14,13},{17,18},{18,... | collective-permute-start | bytes 3145736 | tf_op jit(solution)/shard_map/ppermute | solution.py:787
  285.6 45.8 %copy-start.1 = (bf16[1024,512]{1,0:T(8,128)(2,1)}, bf16[1024,512]{1,0:T(8,128)(2,1)S(1)}, u32[]{:S(2)}) copy-start(bf16[1024,512]{1,0:T(8,128)(2,1)S(1)} %fusion.refs_0_) | copy-start | bytes 3145732
  311.4 45.6 %copy-start.2 = (bf16[1024,512]{1,0:T(8,128)(2,1)}, bf16[1024,512]{1,0:T(8,128)(2,1)S(1)}, u32[]{:S(2)}) copy-start(bf16[1024,512]{1,0:T(8,128)(2,1)S(1)} %fusion.1.refs_4_) | copy-start | bytes 3145732
  331.4 29.2 %copy-start.18 = (bf16[1024,512]{1,0:T(8,128)(2,1)S(1)}, bf16[1024,512]{1,0:T(8,128)(2,1)}, u32[]{:S(2)}) copy-start(bf16[1024,512]{1,0:T(8,128)(2,1)} %add_convert_fusion.12) | copy-start | bytes 3145732
  331.4 46.7 %collective-permute-start.26 = (bf16[1024,2048]{1,0:T(8,128)(2,1)}, bf16[1024,2048]{1,0:T(8,128)(2,1)}, u32[]{:S(2)}, u32[]{:S(2)}) collective-permute-start(bf16[1024,2048]{1,0:T(8,128)(2,1)} %wgrad.8), channel_id=1, source_target_pairs={{0,8},{8,0},{16,24},{24,16},{1,9},{9,1},{17,25},{25,17},{2,10},{10... | collective-permute-start | bytes 12582920 | tf_op jit(solution)/shard_map/ppermute | solution.py:809
  331.4 25.6 %collective-permute-start.22 = (bf16[1024,512]{1,0:T(8,128)(2,1)S(1)}, bf16[1024,512]{1,0:T(8,128)(2,1)S(1)}, u32[]{:S(2)}, u32[]{:S(2)}) collective-permute-start(bf16[1024,512]{1,0:T(8,128)(2,1)S(1)} %fusion.refs_0_), channel_id=1, source_target_pairs={{0,1},{3,2},{1,0},{2,3},{4,5},{7,6},{5,4},{6,7},{8,9},{11,10},{9,8... | collective-permute-start | bytes 3145736 | tf_op jit(solution)/shard_map/ppermute | solution.py:777
  332.0 26.8 %collective-permute-start.23 = (bf16[1024,512]{1,0:T(8,128)(2,1)}, bf16[1024,512]{1,0:T(8,128)(2,1)S(1)}, u32[]{:S(2)}, u32[]{:S(2)}) collective-permute-start(bf16[1024,512]{1,0:T(8,128)(2,1)} %add_convert_fusion.12), channel_id=1, source_target_pairs={{1,2},{2,1},{5,6},{6,5},{9,10},{10,9},{13,14},{14,13},{17,18},{18,... | collective-permute-start | bytes 3145736 | tf_op jit(solution)/shard_map/ppermute | solution.py:787
  332.8 39.6 %collective-permute-start.24 = (bf16[512,1024]{1,0:T(8,128)(2,1)}, bf16[512,1024]{1,0:T(8,128)(2,1)}, u32[]{:S(2)}, u32[]{:S(2)}) collective-permute-start(bf16[512,1024]{1,0:T(8,128)(2,1)} %get-tuple-element.166), channel_id=1, source_target_pairs={{0,16},{16,0},{8,24},{24,8},{1,17},{17,1},{9,25},{25,9},{2,18},{18... | collective-permute-start | bytes 3145736 | tf_op jit(solution)/shard_map/ppermute | solution.py:806
  333.5 39.0 %collective-permute-start.25 = (bf16[512,1024]{1,0:T(8,128)(2,1)}, bf16[512,1024]{1,0:T(8,128)(2,1)}, u32[]{:S(2)}, u32[]{:S(2)}) collective-permute-start(bf16[512,1024]{1,0:T(8,128)(2,1)} %get-tuple-element.168), channel_id=1, source_target_pairs={{0,4},{4,0},{1,5},{5,1},{2,6},{6,2},{3,7},{7,3},{8,12},{12,8},{9,1... | collective-permute-start | bytes 3145736 | tf_op jit(solution)/shard_map/ppermute | solution.py:812
  357.0 31.0 %collective-permute-start.27 = (bf16[1024,512]{1,0:T(8,128)(2,1)S(1)}, bf16[1024,512]{1,0:T(8,128)(2,1)S(1)}, u32[]{:S(2)}, u32[]{:S(2)}) collective-permute-start(bf16[1024,512]{1,0:T(8,128)(2,1)S(1)} %fusion.1.refs_4_), channel_id=1, source_target_pairs={{0,1},{3,2},{1,0},{2,3},{4,5},{7,6},{5,4},{6,7},{8,9},{11,10},{9,8... | collective-permute-start | bytes 3145736 | tf_op jit(solution)/shard_map/ppermute | solution.py:777
  358.7 32.1 %collective-permute-start.28 = (bf16[1024,512]{1,0:T(8,128)(2,1)}, bf16[1024,512]{1,0:T(8,128)(2,1)}, u32[]{:S(2)}, u32[]{:S(2)}) collective-permute-start(bf16[1024,512]{1,0:T(8,128)(2,1)} %add_convert_fusion.10), channel_id=1, source_target_pairs={{1,2},{2,1},{5,6},{6,5},{9,10},{10,9},{13,14},{14,13},{17,18},{18,... | collective-permute-start | bytes 3145736 | tf_op jit(solution)/shard_map/ppermute | solution.py:787
  361.0 49.5 %copy-start.9 = (bf16[1024,512]{1,0:T(8,128)(2,1)}, bf16[1024,512]{1,0:T(8,128)(2,1)S(1)}, u32[]{:S(2)}) copy-start(bf16[1024,512]{1,0:T(8,128)(2,1)S(1)} %fusion.2.refs_2_) | copy-start | bytes 3145732
  376.0 17.8 %collective-permute-start.29 = (bf16[256,1024]{1,0:T(8,128)(2,1)}, bf16[256,1024]{1,0:T(8,128)(2,1)S(1)}, u32[]{:S(2)}, u32[]{:S(2)}) collective-permute-start(bf16[256,1024]{1,0:T(8,128)(2,1)} %get-tuple-element.175), channel_id=1, source_target_pairs={{0,4},{4,0},{1,5},{5,1},{2,6},{6,2},{3,7},{7,3},{8,12},{12,8},{9,1... | collective-permute-start | bytes 1572872 | tf_op jit(solution)/shard_map/ppermute | solution.py:812
  377.5 16.3 %collective-permute-start.30 = (bf16[256,1024]{1,0:T(8,128)(2,1)}, bf16[256,1024]{1,0:T(8,128)(2,1)}, u32[]{:S(2)}, u32[]{:S(2)}) collective-permute-start(bf16[256,1024]{1,0:T(8,128)(2,1)} %get-tuple-element.177), channel_id=1, source_target_pairs={{0,16},{16,0},{8,24},{24,8},{1,17},{17,1},{9,25},{25,9},{2,18},{18... | collective-permute-start | bytes 1572872 | tf_op jit(solution)/shard_map/ppermute | solution.py:806
  408.5 42.9 %collective-permute-start.35 = (bf16[1024,2048]{1,0:T(8,128)(2,1)}, bf16[1024,2048]{1,0:T(8,128)(2,1)}, u32[]{:S(2)}, u32[]{:S(2)}) collective-permute-start(bf16[1024,2048]{1,0:T(8,128)(2,1)} %wgrad.10), channel_id=1, source_target_pairs={{0,8},{8,0},{16,24},{24,16},{1,9},{9,1},{17,25},{25,17},{2,10},{10... | collective-permute-start | bytes 12582920 | tf_op jit(solution)/shard_map/ppermute | solution.py:809
  408.5 25.8 %collective-permute-start.31 = (bf16[512,1024]{1,0:T(8,128)(2,1)}, bf16[512,1024]{1,0:T(8,128)(2,1)S(1)}, u32[]{:S(2)}, u32[]{:S(2)}) collective-permute-start(bf16[512,1024]{1,0:T(8,128)(2,1)} %get-tuple-element.180), channel_id=1, source_target_pairs={{0,16},{16,0},{8,24},{24,8},{1,17},{17,1},{9,25},{25,9},{2,18},{18... | collective-permute-start | bytes 3145736 | tf_op jit(solution)/shard_map/ppermute | solution.py:806
  410.0 27.3 %collective-permute-start.32 = (bf16[512,1024]{1,0:T(8,128)(2,1)}, bf16[512,1024]{1,0:T(8,128)(2,1)S(1)}, u32[]{:S(2)}, u32[]{:S(2)}) collective-permute-start(bf16[512,1024]{1,0:T(8,128)(2,1)} %get-tuple-element.182), channel_id=1, source_target_pairs={{0,4},{4,0},{1,5},{5,1},{2,6},{6,2},{3,7},{7,3},{8,12},{12,8},{9,1... | collective-permute-start | bytes 3145736 | tf_op jit(solution)/shard_map/ppermute | solution.py:812
  410.5 31.4 %collective-permute-start.33 = (bf16[1024,512]{1,0:T(8,128)(2,1)S(1)}, bf16[1024,512]{1,0:T(8,128)(2,1)}, u32[]{:S(2)}, u32[]{:S(2)}) collective-permute-start(bf16[1024,512]{1,0:T(8,128)(2,1)S(1)} %fusion.2.refs_2_), channel_id=1, source_target_pairs={{0,1},{3,2},{1,0},{2,3},{4,5},{7,6},{5,4},{6,7},{8,9},{11,10},{9,8... | collective-permute-start | bytes 3145736 | tf_op jit(solution)/shard_map/ppermute | solution.py:777
  414.4 33.5 %collective-permute-start.34 = (bf16[1024,512]{1,0:T(8,128)(2,1)}, bf16[1024,512]{1,0:T(8,128)(2,1)}, u32[]{:S(2)}, u32[]{:S(2)}) collective-permute-start(bf16[1024,512]{1,0:T(8,128)(2,1)} %add_convert_fusion.8), channel_id=1, source_target_pairs={{1,2},{2,1},{5,6},{6,5},{9,10},{10,9},{13,14},{14,13},{17,18},{18,... | collective-permute-start | bytes 3145736 | tf_op jit(solution)/shard_map/ppermute | solution.py:787
  434.3 37.5 %collective-permute-start.38 = (bf16[1024,512]{1,0:T(8,128)(2,1)}, bf16[1024,512]{1,0:T(8,128)(2,1)}, u32[]{:S(2)}, u32[]{:S(2)}) collective-permute-start(bf16[1024,512]{1,0:T(8,128)(2,1)} %fusion.3.refs_6_), channel_id=1, source_target_pairs={{0,1},{3,2},{1,0},{2,3},{4,5},{7,6},{5,4},{6,7},{8,9},{11,10},{9,8... | collective-permute-start | bytes 3145736 | tf_op jit(solution)/shard_map/ppermute | solution.py:777
  444.5 31.4 %collective-permute-start.39 = (bf16[1024,512]{1,0:T(8,128)(2,1)}, bf16[1024,512]{1,0:T(8,128)(2,1)}, u32[]{:S(2)}, u32[]{:S(2)}) collective-permute-start(bf16[1024,512]{1,0:T(8,128)(2,1)} %add_convert_fusion.6), channel_id=1, source_target_pairs={{1,2},{2,1},{5,6},{6,5},{9,10},{10,9},{13,14},{14,13},{17,18},{18,... | collective-permute-start | bytes 3145736 | tf_op jit(solution)/shard_map/ppermute | solution.py:787
  446.4 16.7 %collective-permute-start.36 = (bf16[256,1024]{1,0:T(8,128)(2,1)}, bf16[256,1024]{1,0:T(8,128)(2,1)S(1)}, u32[]{:S(2)}, u32[]{:S(2)}) collective-permute-start(bf16[256,1024]{1,0:T(8,128)(2,1)} %get-tuple-element.189), channel_id=1, source_target_pairs={{0,4},{4,0},{1,5},{5,1},{2,6},{6,2},{3,7},{7,3},{8,12},{12,8},{9,1... | collective-permute-start | bytes 1572872 | tf_op jit(solution)/shard_map/ppermute | solution.py:812
  447.9 15.7 %collective-permute-start.37 = (bf16[256,1024]{1,0:T(8,128)(2,1)S(1)}, bf16[256,1024]{1,0:T(8,128)(2,1)S(1)}, u32[]{:S(2)}, u32[]{:S(2)}) collective-permute-start(bf16[256,1024]{1,0:T(8,128)(2,1)S(1)} %copy-done.45), channel_id=1, source_target_pairs={{0,16},{16,0},{8,24},{24,8},{1,17},{17,1},{9,25},{25,9},{2,18},{18... | collective-permute-start | bytes 1572872 | tf_op jit(solution)/shard_map/ppermute | solution.py:806
  462.5 24.3 %collective-permute-start.40 = (bf16[512,1024]{1,0:T(8,128)(2,1)}, bf16[512,1024]{1,0:T(8,128)(2,1)}, u32[]{:S(2)}, u32[]{:S(2)}) collective-permute-start(bf16[512,1024]{1,0:T(8,128)(2,1)} %get-tuple-element.195), channel_id=1, source_target_pairs={{0,16},{16,0},{8,24},{24,8},{1,17},{17,1},{9,25},{25,9},{2,18},{18... | collective-permute-start | bytes 3145736 | tf_op jit(solution)/shard_map/ppermute | solution.py:806
  463.1 24.0 %collective-permute-start.41 = (bf16[512,1024]{1,0:T(8,128)(2,1)}, bf16[512,1024]{1,0:T(8,128)(2,1)}, u32[]{:S(2)}, u32[]{:S(2)}) collective-permute-start(bf16[512,1024]{1,0:T(8,128)(2,1)} %get-tuple-element.197), channel_id=1, source_target_pairs={{0,4},{4,0},{1,5},{5,1},{2,6},{6,2},{3,7},{7,3},{8,12},{12,8},{9,1... | collective-permute-start | bytes 3145736 | tf_op jit(solution)/shard_map/ppermute | solution.py:812
  463.7 35.8 %collective-permute-start.42 = (bf16[1024,512]{1,0:T(8,128)(2,1)S(1)}, bf16[1024,512]{1,0:T(8,128)(2,1)}, u32[]{:S(2)}, u32[]{:S(2)}) collective-permute-start(bf16[1024,512]{1,0:T(8,128)(2,1)S(1)} %fusion.4.refs_0_), channel_id=1, source_target_pairs={{0,1},{3,2},{1,0},{2,3},{4,5},{7,6},{5,4},{6,7},{8,9},{11,10},{9,8... | collective-permute-start | bytes 3145736 | tf_op jit(solution)/shard_map/ppermute | solution.py:777
  474.2 31.6 %collective-permute-start.43 = (bf16[1024,512]{1,0:T(8,128)(2,1)}, bf16[1024,512]{1,0:T(8,128)(2,1)}, u32[]{:S(2)}, u32[]{:S(2)}) collective-permute-start(bf16[1024,512]{1,0:T(8,128)(2,1)} %add_convert_fusion.4), channel_id=1, source_target_pairs={{1,2},{2,1},{5,6},{6,5},{9,10},{10,9},{13,14},{14,13},{17,18},{18,... | collective-permute-start | bytes 3145736 | tf_op jit(solution)/shard_map/ppermute | solution.py:787
  502.0 20.2 %collective-permute-start.46 = (bf16[1024,512]{1,0:T(8,128)(2,1)}, bf16[1024,512]{1,0:T(8,128)(2,1)}, u32[]{:S(2)}, u32[]{:S(2)}) collective-permute-start(bf16[1024,512]{1,0:T(8,128)(2,1)} %add_convert_fusion.2), channel_id=1, source_target_pairs={{1,2},{2,1},{5,6},{6,5},{9,10},{10,9},{13,14},{14,13},{17,18},{18,... | collective-permute-start | bytes 3145736 | tf_op jit(solution)/shard_map/ppermute | solution.py:787
  503.6 11.9 %collective-permute-start.44 = (bf16[256,1024]{1,0:T(8,128)(2,1)}, bf16[256,1024]{1,0:T(8,128)(2,1)S(1)}, u32[]{:S(2)}, u32[]{:S(2)}) collective-permute-start(bf16[256,1024]{1,0:T(8,128)(2,1)} %get-tuple-element.203), channel_id=1, source_target_pairs={{0,4},{4,0},{1,5},{5,1},{2,6},{6,2},{3,7},{7,3},{8,12},{12,8},{9,1... | collective-permute-start | bytes 1572872 | tf_op jit(solution)/shard_map/ppermute | solution.py:812
  504.3 12.6 %collective-permute-start.45 = (bf16[256,1024]{1,0:T(8,128)(2,1)}, bf16[256,1024]{1,0:T(8,128)(2,1)S(1)}, u32[]{:S(2)}, u32[]{:S(2)}) collective-permute-start(bf16[256,1024]{1,0:T(8,128)(2,1)} %get-tuple-element.205), channel_id=1, source_target_pairs={{0,16},{16,0},{8,24},{24,8},{1,17},{17,1},{9,25},{25,9},{2,18},{18... | collective-permute-start | bytes 1572872 | tf_op jit(solution)/shard_map/ppermute | solution.py:806
  505.7 19.6 %collective-permute-start.50 = (f32[13824]{0:T(1024)S(1)}, f32[13824]{0:T(1024)S(1)}, u32[]{:S(2)}, u32[]{:S(2)}) collective-permute-start(f32[13824]{0:T(1024)S(1)} %pad_maximum_fusion.1), channel_id=1, source_target_pairs={{0,8},{8,0},{16,24},{24,16},{1,9},{9,1},{17,25},{25,17},{2,10},{10... | collective-permute-start | bytes 165896 | tf_op jit(solution)/shard_map/ppermute | solution.py:809
  505.8 79.1 %collective-permute-start.47 = (bf16[1024,512]{1,0:T(8,128)(2,1)S(1)}, bf16[1024,512]{1,0:T(8,128)(2,1)}, u32[]{:S(2)}, u32[]{:S(2)}) collective-permute-start(bf16[1024,512]{1,0:T(8,128)(2,1)S(1)} %add_convert_fusion.3.refs_2_), channel_id=1, source_target_pairs={{1,0},{2,3},{5,4},{6,7},{9,8},{10,11},{13,12},{14,15},{17,16},{18,... | collective-permute-start | bytes 3145736 | tf_op jit(solution)/shard_map/ppermute | solution.py:777
  515.5 69.4 %collective-permute-start.48 = (bf16[1024,512]{1,0:T(8,128)(2,1)S(1)}, bf16[1024,512]{1,0:T(8,128)(2,1)}, u32[]{:S(2)}, u32[]{:S(2)}) collective-permute-start(bf16[1024,512]{1,0:T(8,128)(2,1)S(1)} %add_convert_fusion.1.refs_4_), channel_id=1, source_target_pairs={{1,0},{2,3},{5,4},{6,7},{9,8},{10,11},{13,12},{14,15},{17,16},{18,... | collective-permute-start | bytes 3145736 | tf_op jit(solution)/shard_map/ppermute | solution.py:777
  524.0 60.9 %copy-start.15 = (bf16[1024,512]{1,0:T(8,128)(2,1)}, bf16[1024,512]{1,0:T(8,128)(2,1)S(1)}, u32[]{:S(2)}) copy-start(bf16[1024,512]{1,0:T(8,128)(2,1)S(1)} %add_convert_fusion.refs_6_) | copy-start | bytes 3145732
  524.0 60.9 %collective-permute-start.49 = (bf16[1024,512]{1,0:T(8,128)(2,1)S(1)}, bf16[1024,512]{1,0:T(8,128)(2,1)}, u32[]{:S(2)}, u32[]{:S(2)}) collective-permute-start(bf16[1024,512]{1,0:T(8,128)(2,1)S(1)} %add_convert_fusion.refs_6_), channel_id=1, source_target_pairs={{1,0},{2,3},{5,4},{6,7},{9,8},{10,11},{13,12},{14,15},{17,16},{18,... | collective-permute-start | bytes 3145736 | tf_op jit(solution)/shard_map/ppermute | solution.py:777
  525.3 4.2 collective-permute-start.51
  529.6 4.2 collective-permute-start.52
  533.8 45.5 %collective-permute-start.53 = (f32[8192]{0:T(1024)S(1)}, f32[8192]{0:T(1024)S(1)}, u32[]{:S(2)}, u32[]{:S(2)}) collective-permute-start(f32[8192]{0:T(1024)S(1)} %slice.50), channel_id=1, source_target_pairs={{0,1},{1,0},{2,3},{3,2},{4,5},{5,4},{6,7},{7,6},{8,9},{9,8},{10,11... | collective-permute-start | bytes 98312 | tf_op jit(solution)/shard_map/ppermute | solution.py:874
  579.4 4.9 collective-permute-start.54
  (37 other events, 295.1 us)

commit v2 on v1

--- a/solution.py
+++ b/solution.py
@@ -19,8 +19,12 @@
 inv_sqrt_tau = 0.3989422804014327
 
 
+COST_SCALE = 20
+
+
 def cost(flops, nbytes, trans=0):
-    return pl.CostEstimate(flops=int(flops), bytes_accessed=int(nbytes), transcendentals=int(trans))
+    k = COST_SCALE
+    return pl.CostEstimate(flops=int(k * flops), bytes_accessed=int(k * nbytes), transcendentals=int(k * trans))
 
 
 def params(n, mb=60):
@@ -33,6 +37,15 @@
     return lax.dot_general(a, b, (((1,), (0,)), ((), ())), preferred_element_type=F32)
 
 
+def nn_rows(a, pieces):
+    total, at = None, 0
+    for w in pieces:
+        y = nn(a[:, at : at + w.shape[0]], w[...])
+        total = y if total is None else total + y
+        at += w.shape[0]
+    return total
+
+
 def nt(a, b):
     return lax.dot_general(a, b, (((1,), (1,)), ((), ())), preferred_element_type=F32)
 
@@ -48,7 +61,7 @@
 def row_valid(meta, row0, rows, local_len):
     slot = row0 // local_len
     pos = meta[0] * local_len + row0 % local_len + lax.broadcasted_iota(jnp.int32, (rows, 1), 0)
-    return (pos < meta[2 + NBLK + slot]).astype(F32)
+    return (pos < meta[3 + NBLK + slot]).astype(F32)
 
 
 def norm_kernel(local_len, meta, x_ref, g_ref, ga, sa, gf, sf, h1_ref, h2_ref, g_out, st_ref, gs_ref):
@@ -120,10 +133,9 @@
         out[rows, 128:] = rest.astype(BF)
 
 
-def kv_kernel(h1, wa, wb, b_ref, cosf, s1, s2, kv_ref):
-    half = wa.shape[0]
+def kv_kernel(h1, w0, w1, w2, w3, w4, w5, b_ref, cosf, s1, s2, kv_ref):
     part = lax.rem(pl.program_id(0), 2)
-    y = nn(h1[:, :half], wa[...]) + nn(h1[:, half:], wb[...]) + b_ref[...]
+    y = nn_rows(h1, (w0, w1, w2, w3, w4, w5)) + b_ref[...]
 
     @pl.when(part == 0)
     def _():
@@ -134,7 +146,7 @@
         kv_ref[...] = y.astype(BF)
 
 
-def kv_call(h1, wa, wb, b_qkv, tabs, nheads):
+def kv_call(h1, pieces, b_qkv, tabs, nheads):
     m, d = h1.shape
     local_len = tabs[0].shape[0]
 
@@ -148,8 +160,7 @@
         grid=(2 * nheads,),
         in_specs=[
             pl.BlockSpec((m, d), lambda j: (0, 0)),
-            pl.BlockSpec((d // 2, HD), src),
-            pl.BlockSpec((d // 2, HD), src),
+            *[pl.BlockSpec((p.shape[0], HD), src) for p in pieces],
             pl.BlockSpec((1, HD), src),
             tab,
             tab,
@@ -159,27 +170,30 @@
         out_shape=jax.ShapeDtypeStruct((m, 2 * nheads * HD), BF),
         compiler_params=params(1),
         cost_estimate=cost(4 * m * d * nheads * HD, 2 * (m * d + 2 * d * nheads * HD + 2 * m * nheads * HD)),
-    )(h1, wa, wb, b_qkv, *tabs)
-
-
-def qd_kernel(nheads, h1, g, wa, wb, b_ref, cosf, s1, s2, q_ref, dob_ref):
+    )(h1, *pieces, b_qkv, *tabs)
+
+
+def qd_kernel(nheads, h1, g, w0, w1, w2, w3, w4, w5, b_ref, cosf, s1, s2, q_ref, dob_ref):
     j = pl.program_id(0)
-    half = wa.shape[0]
+    pieces = (w0, w1, w2, w3, w4, w5)
 
     @pl.when(j < nheads)
     def _():
-        rotated(q_ref, nn(h1[:, :half], wa[...]) + nn(h1[:, half:], wb[...]) + b_ref[...], cosf, s1, s2)
+        rotated(q_ref, nn_rows(h1, pieces) + b_ref[...], cosf, s1, s2)
 
     @pl.when(j >= nheads)
     def _():
-        dob_ref[...] = (nn(g[:, :half], wa[...]) + nn(g[:, half:], wb[...])).astype(BF)
-
-
-def qd_call(h1, g, wa, wb, b_qkv, tabs, nheads):
+        dob_ref[...] = nn_rows(g, pieces).astype(BF)
+
+
+def qd_call(h1, g, pieces, b_qkv, tabs, nheads):
     m, d = h1.shape
     local_len = tabs[0].shape[0]
     full = pl.BlockSpec((m, d), lambda j: (0, 0))
-    w_spec = pl.BlockSpec((d // 2, HD), lambda j: (0, jnp.where(j < nheads, 3 * j, 2 * nheads + j)))
+
+    def src(j):
+        return (0, jnp.where(j < nheads, 3 * j, 2 * nheads + j))
+
     tab = pl.BlockSpec((local_len, 128), lambda j: (0, 0))
     return pl.pallas_call(
         functools.partial(qd_kernel, nheads),
@@ -188,8 +202,7 @@
         in_specs=[
             full,
             full,
-            w_spec,
-            w_spec,
+            *[pl.BlockSpec((p.shape[0], HD), src) for p in pieces],
             pl.BlockSpec((1, HD), lambda j: (0, 3 * jnp.minimum(j, nheads - 1))),
             tab,
             tab,
@@ -202,13 +215,13 @@
         out_shape=[jax.ShapeDtypeStruct((m, nheads * HD), BF)] * 2,
         compiler_params=params(1),
         cost_estimate=cost(4 * m * d * nheads * HD, 2 * (2 * m * d + 2 * d * nheads * HD + 2 * m * nheads * HD)),
-    )(h1, g, wa, wb, b_qkv, *tabs)
+    )(h1, g, *pieces, b_qkv, *tabs)
 
 
 def attn_kernel(nprev, local_len, meta, q_ref, kv_ref, pv_ref, dob_ref, cosf, s1, s2, ob_ref, dq_ref, dkv_ref, dpv_ref, sc_ref, dq_acc):
     slot = pl.program_id(0)
     ctx = meta[0]
-    length = meta[2 + NBLK + slot]
+    length = meta[3 + NBLK + slot]
     scale = 1.0 / math.sqrt(HD)
     n_vis = jnp.minimum(ctx, (length + local_len - 1) // local_len)
     q = q_ref[...]
@@ -358,147 +371,165 @@
     )(dq, dkv, rv, *tabs)
 
 
-def hidden_kernel(h2, wa, wb, b_ref, gb_ref, dg_ref):
-    half = wa.shape[0]
-    u = nn(h2[:, :half], wa[...]) + nn(h2[:, half:], wb[...]) + b_ref[...]
+def hidden_kernel(h2, w0, w1, w2, w3, w4, w5, b_ref, gb_ref, dg_ref):
+    u = nn_rows(h2, (w0, w1, w2, w3, w4, w5)) + b_ref[...]
     cdf = 0.5 * (1.0 + lax.erf(u * inv_sqrt_two))
     gb_ref[...] = (u * cdf).astype(BF)
     dg_ref[...] = (cdf + u * (jnp.exp(-0.5 * u * u) * inv_sqrt_tau)).astype(BF)
 
 
-def hidden_call(h2, wa, wb, b_in):
+def hidden_call(h2, pieces, b_in):
     m, d = h2.shape
-    f = wa.shape[1]
+    f = pieces[0].shape[1]
     t = 256
     col = pl.BlockSpec((m, t), lambda j: (0, j))
-    w_spec = pl.BlockSpec((d // 2, t), lambda j: (0, j))
+    w_specs = [pl.BlockSpec((p.shape[0], t), lambda j: (0, j)) for p in pieces]
     return pl.pallas_call(
         hidden_kernel,
         name="hidden",
         grid=(f // t,),
-        in_specs=[pl.BlockSpec((m, d), lambda j: (0, 0)), w_spec, w_spec, pl.BlockSpec((1, t), lambda j: (0, j))],
+        in_specs=[pl.BlockSpec((m, d), lambda j: (0, 0)), *w_specs, pl.BlockSpec((1, t), lambda j: (0, j))],
         out_specs=[col, col],
         out_shape=[jax.ShapeDtypeStruct((m, f), BF)] * 2,
         compiler_params=params(1),
         cost_estimate=cost(2 * m * d * f, 2 * (m * d + d * f + 2 * m * f), 2 * m * f),
-    )(h2, wa, wb, b_in)
-
-
-def dhid_kernel(g, w0, w1, w2, w3, dg_ref, du_ref, sum_ref):
-    n = w0.shape[0]
-    a = nn(g[:, :n], w0[...]) + nn(g[:, n : 2 * n], w1[...])
-    a += nn(g[:, 2 * n : 3 * n], w2[...]) + nn(g[:, 3 * n :], w3[...])
+    )(h2, *pieces, b_in)
+
+
+def dhid_kernel(g, w0, w1, w2, w3, w4, w5, dg_ref, du_ref, sum_ref):
+    a = nn_rows(g, (w0, w1, w2, w3, w4, w5))
     du = (a * dg_ref[...].astype(F32)).astype(BF)
     du_ref[...] = du
     sum_ref[...] = jnp.sum(du.astype(F32), axis=0, keepdims=True)
 
 
-def dhid_call(g, quarters, dg):
+def dhid_call(g, pieces, dg):
     m, d = g.shape
     f = dg.shape[1]
     t = 256
     col = pl.BlockSpec((m, t), lambda j: (0, j))
-    w_spec = pl.BlockSpec((d // 4, t), lambda j: (0, j))
+    w_specs = [pl.BlockSpec((p.shape[0], t), lambda j: (0, j)) for p in pieces]
     return pl.pallas_call(
         dhid_kernel,
         name="dhid",
         grid=(f // t,),
-        in_specs=[pl.BlockSpec((m, d), lambda j: (0, 0))] + [w_spec] * 4 + [col],
+        in_specs=[pl.BlockSpec((m, d), lambda j: (0, 0))] + w_specs + [col],
         out_specs=[col, pl.BlockSpec((1, t), lambda j: (0, j))],
         out_shape=[jax.ShapeDtypeStruct((m, f), BF), jax.ShapeDtypeStruct((1, f), F32)],
         compiler_params=params(1),
         cost_estimate=cost(2 * m * d * f, 2 * (m * d + d * f + 2 * m * f)),
-    )(g, *quarters, dg)
-
-
-def out_kernel(ob, gb, wp, wo, y_ref):
-    y_ref[...] = (nt(ob[...], wp[...]) + nt(gb[...], wo[...])).astype(BF)
-
-
-def out_call(ob, gb, g1, quarter, c):
+    )(g, *pieces, dg)
+
+
+def out_kernel(count, ob, gb, *refs):
+    j = pl.program_id(0)
+    ps, os, ya, yb = refs[:count], refs[count : 2 * count], refs[-2], refs[-1]
+    each = 4 // count
+    for k in range(4):
+
+        @pl.when(j == k)
+        def _():
+            y = ya if k < 2 else yb
+            y[...] = (nt(ob[...], ps[k // each][...]) + nt(gb[...], os[k // each][...])).astype(BF)
+
+
+def piece_spec(count, i, cols, at=0, prefetch=False):
+    each = 4 // count
+
+    def place(j, *_):
+        return (jnp.clip(j - i * each, 0, each - 1), at)
+
+    if prefetch:
+        return pl.BlockSpec((256, cols), lambda j, mt: place(j))
+    return pl.BlockSpec((256, cols), lambda j: place(j))
+
+
+def out_call(ob, gb, proj, out):
     m, f = gb.shape
     nf = ob.shape[1]
-    n = quarter.shape[0]
-    rows = 512
-    last = g1.shape[1] // nf - 1
-    return pl.pallas_call(
-        out_kernel,
+    count = len(out)
+    last = proj[0].shape[1] // nf - 1
+    part = jax.ShapeDtypeStruct((m, 512), BF)
+    return pl.pallas_call(
+        functools.partial(out_kernel, count),
         name="outp",
-        grid=(m // rows,),
-        in_specs=[
-            pl.BlockSpec((rows, nf), lambda i: (i, 0)),
-            pl.BlockSpec((rows, f), lambda i: (i, 0)),
-            pl.BlockSpec((n, nf), lambda i: (c % 2, last)),
-            pl.BlockSpec((n, f), lambda i: (0, 0)),
+        grid=(4,),
+        in_specs=[pl.BlockSpec((m, nf), lambda j: (0, 0)), pl.BlockSpec((m, f), lambda j: (0, 0))]
+        + [piece_spec(count, i, nf, last) for i in range(count)]
+        + [piece_spec(count, i, f) for i in range(count)],
+        out_specs=[
+            pl.BlockSpec((m, 256), lambda j: (0, jnp.minimum(j, 1))),
+            pl.BlockSpec((m, 256), lambda j: (0, jnp.maximum(j - 2, 0))),
         ],
-        out_specs=pl.BlockSpec((rows, n), lambda i: (i, 0)),
-        out_shape=jax.ShapeDtypeStruct((m, n), BF),
-        compiler_params=params(1),
-        cost_estimate=cost(2 * m * n * (f + nf), 2 * (m * f + m * nf + n * (f + nf) + m * n)),
-    )(ob, gb, g1, quarter)
-
-
-def back_kernel(c, meta, dqkv, du, w1, w2, x_ref, st_ref, ga, gf, prev, dn_ref, sums_ref):
-    i = pl.program_id(0)
-    dh1 = nt(dqkv[...], w1[...])
-    dh2 = nt(du[...], w2[...])
-    for k in range(2):
-        src = block_cols(lax.rem(meta[1 + 2 * c + k], 2) * 256)
-        dst = slice(k * 256, (k + 1) * 256)
-        a, b = dh1[:, dst], dh2[:, dst]
-        xh = (x_ref[:, src].astype(F32) - st_ref[:, 0:1]) * st_ref[:, 1:2]
-        dn_ref[:, dst] = (a * ga[:, src] + b * gf[:, src]).astype(BF)
-        for j, v in enumerate((a * xh, a, b * xh, b)):
-            part = jnp.sum(v, axis=0, keepdims=True)
-
-            @pl.when(i == 0)
-            def _():
-                sums_ref[j : j + 1, src] = part
-
-            @pl.when(i > 0)
-            def _():
-                sums_ref[j : j + 1, src] = sums_ref[j : j + 1, src] + part
-
-
-def back_call(meta, dqkv, du, g1, g2, x2, st, ga, gf, sums, c):
+        out_shape=[part, part],
+        compiler_params=params(1),
+        cost_estimate=cost(2048 * m * (f + nf), 2 * (m * f + m * nf + 1024 * (f + nf) + 1024 * m)),
+    )(ob, gb, *proj, *out)
+
+
+def back_kernel(meta, dqkv, du, w10, w11, w12, w20, w21, w22, x_ref, st_ref, ga, gf, prev, da_ref, db_ref, sums_ref):
+    j = pl.program_id(0)
+    for w1, w2, dn_ref, mine in ((w10, w20, da_ref, j < 2), (w11, w21, db_ref, j == 2), (w12, w22, db_ref, j == 3)):
+
+        @pl.when(mine)
+        def _():
+            dh1 = nt(dqkv[...], w1[...])
+            dh2 = nt(du[...], w2[...])
+            xh = (x_ref[...].astype(F32) - st_ref[:, 0:1]) * st_ref[:, 1:2]
+            dn_ref[...] = (dh1 * ga[...] + dh2 * gf[...]).astype(BF)
+            sums_ref[0:1, :] = jnp.sum(dh1 * xh, axis=0, keepdims=True)
+            sums_ref[1:2, :] = jnp.sum(dh1, axis=0, keepdims=True)
+            sums_ref[2:3, :] = jnp.sum(dh2 * xh, axis=0, keepdims=True)
+            sums_ref[3:4, :] = jnp.sum(dh2, axis=0, keepdims=True)
+
+
+def back_call(meta, dqkv, du, g1, g2, x2, st, ga, gf, sums, half):
     m, d = x2.shape
     nq = dqkv.shape[1]
     f = du.shape[1]
     n = d // 4
-    rows = 512
-
-    def absolute(r, at):
-        return pl.BlockSpec((r, n), lambda i, mt: (i if at else 0, mt[1 + 2 * c] // 2))
-
-    return pl.pallas_call(
-        functools.partial(back_kernel, c),
+
+    def absolute(rows):
+        return pl.BlockSpec((rows, 256), lambda j, mt: (0, mt[1 + 4 * half + j]))
+
+    part = jax.ShapeDtypeStruct((m, n), BF)
+    at = slice(3 * half, 3 * half + 3)
+    return pl.pallas_call(
+        back_kernel,
         name="backn",
         grid_spec=pltpu.PrefetchScalarGridSpec(
             num_scalar_prefetch=1,
-            grid=(m // rows,),
+            grid=(4,),
             in_specs=[
-                pl.BlockSpec((rows, nq), lambda i, mt: (i, 0)),
-                pl.BlockSpec((rows, f), lambda i, mt: (i, 0)),
-                pl.BlockSpec((n, nq), lambda i, mt: (c % 2, 0)),
-                pl.BlockSpec((n, f), lambda i, mt: (c % 2, 0)),
-                absolute(rows, True),
-                pl.BlockSpec((rows, 128), lambda i, mt: (i, 0)),
-                absolute(1, False),
-                absolute(1, False),
+                pl.BlockSpec((m, nq), lambda j, mt: (0, 0)),
+                pl.BlockSpec((m, f), lambda j, mt: (0, 0)),
+                pl.BlockSpec((256, nq), lambda j, mt: (jnp.minimum(j, 1), 0)),
+                pl.BlockSpec((256, nq), lambda j, mt: (0, 0)),
+                pl.BlockSpec((256, nq), lambda j, mt: (0, 0)),
+                pl.BlockSpec((256, f), lambda j, mt: (jnp.minimum(j, 1), 0)),
+                pl.BlockSpec((256, f), lambda j, mt: (0, 0)),
+                pl.BlockSpec((256, f), lambda j, mt: (0, 0)),
+                absolute(m),
+                pl.BlockSpec((m, 128), lambda j, mt: (0, 0)),
+                absolute(1),
+                absolute(1),
                 pl.BlockSpec(memory_space=pl.ANY),
             ],
-            out_specs=[pl.BlockSpec((rows, n), lambda i, mt: (i, 0)), absolute(4, False)],
+            out_specs=[
+                pl.BlockSpec((m, n // 2), lambda j, mt: (0, jnp.minimum(j, 1))),
+                pl.BlockSpec((m, n // 2), lambda j, mt: (0, jnp.maximum(j - 2, 0))),
+                absolute(4),
+            ],
         ),
-        out_shape=[jax.ShapeDtypeStruct((m, n), BF), jax.ShapeDtypeStruct((4, d), F32)],
-        input_output_aliases={9: 1},
-        compiler_params=params(1),
-        cost_estimate=cost(2 * m * n * (f + nq), 2 * (m * f + m * nq + n * (f + nq) + 2 * m * n)),
-    )(meta, dqkv, du, g1, g2, x2, st, ga, gf, sums)
-
-
-def wgrad_kernel(pairs, adds, split, *refs):
+        out_shape=[part, part, jax.ShapeDtypeStruct((4, d), F32)],
+        input_output_aliases={13: 2},
+        compiler_params=params(1),
+        cost_estimate=cost(4 * m * n * (f + nq), 2 * (m * f + m * nq + 2 * n * (f + nq) + 4 * m * n)),
+    )(meta, dqkv, du, *g1[at], *g2[at], x2, st, ga, gf, sums)
+
+
+def wgrad_kernel(pairs, adds, split, meta, *refs):
     j = pl.program_id(0)
-    half_way = sum(pairs) // 2
     start = 0
     for p, count in enumerate(pairs):
         a, b = refs[2 * p], refs[2 * p + 1]
@@ -508,29 +539,21 @@
             y = tn(a[...], b[...])
             if adds:
                 y = y + refs[2 * len(pairs)][...].astype(F32)
-            y = y.astype(BF)
             if not split:
-                refs[-1][...] = y
+                refs[-1][...] = y.astype(BF)
                 return
-            keep_x, send_x, keep_y, send_y = refs[-4:]
+            keep, send = refs[-2:]
             n = y.shape[0] // 4
-
-            @pl.when(j < half_way)
-            def _():
-                keep_x[...] = y[: 2 * n]
-                send_x[...] = y[2 * n :]
-
-            @pl.when(j >= half_way)
-            def _():
-                keep_y[:n] = y[:n]
-                send_y[:n] = y[n : 2 * n]
-                keep_y[n:] = y[2 * n : 3 * n]
-                send_y[n:] = y[3 * n :]
+            swap = meta[2 + NBLK] > 0
+            keep[:n] = y[:n].astype(BF)
+            keep[n:] = jnp.where(swap, y[2 * n : 3 * n], y[n : 2 * n]).astype(BF)
+            send[:n] = jnp.where(swap, y[n : 2 * n], y[2 * n : 3 * n]).astype(BF)
+            send[n:] = y[3 * n :].astype(BF)
 
         start += count
 
 
-def wgrad_call(*flat, half, add=None, split=False):
+def wgrad_call(meta, *flat, half, add=None, split=False):
     pairs = list(zip(flat[::2], flat[1::2]))
     m, d = pairs[0][0].shape
     t = 512
@@ -538,35 +561,31 @@
     total = sum(counts)
     in_specs, ops, start = [], [], 0
     for (a, b), c in zip(pairs, counts):
-        in_specs.append(pl.BlockSpec((m, d // 2), lambda j: (0, half)))
+        in_specs.append(pl.BlockSpec((m, d // 2), lambda j, mt: (0, half)))
         in_specs.append(
-            pl.BlockSpec((m, t), lambda j, s=start, c=c: (0, jnp.clip(j - s, 0, c - 1)))
+            pl.BlockSpec((m, t), lambda j, mt, s=start, c=c: (0, jnp.clip(j - s, 0, c - 1)))
         )
         ops += [a, b]
         start += c
-    col = pl.BlockSpec((d // 2, t), lambda j: (0, j))
+    rows = d // 4 if split else d // 2
     if add is not None:
-        in_specs.append(col)
+        in_specs.append(pl.BlockSpec((d // 2, t), lambda j, mt: (0, j)))
         ops.append(add)
-    if split:
-        h = total // 2
-        left = pl.BlockSpec((d // 4, t), lambda j: (0, jnp.minimum(j, h - 1)))
-        right = pl.BlockSpec((d // 4, t), lambda j: (0, jnp.maximum(j - h, 0)))
-        out_specs = [left, left, right, right]
-        out_shape = [jax.ShapeDtypeStruct((d // 4, h * t), BF)] * 4
-    else:
-        out_specs = col
-        out_shape = jax.ShapeDtypeStruct((d // 2, total * t), BF)
+    out_spec = pl.BlockSpec((rows, t), lambda j, mt: (0, j))
+    out_shape = jax.ShapeDtypeStruct((rows, total * t), BF)
     return pl.pallas_call(
         functools.partial(wgrad_kernel, counts, add is not None, split),
         name="wgrad",
-        grid=(total,),
-        in_specs=in_specs,
-        out_specs=out_specs,
-        out_shape=out_shape,
+        grid_spec=pltpu.PrefetchScalarGridSpec(
+            num_scalar_prefetch=1,
+            grid=(total,),
+            in_specs=in_specs,
+            out_specs=[out_spec, out_spec] if split else out_spec,
+        ),
+        out_shape=[out_shape, out_shape] if split else out_shape,
         compiler_params=params(1),
         cost_estimate=cost(m * d * total * t, 2 * (m * d // 2 * len(pairs) + m * total * t + d * total * t)),
-    )(*ops)
+    )(meta, *ops)
 
 
 def pack_kernel(*refs):
@@ -593,15 +612,14 @@
     )(*pieces)
 
 
-def half_sum_kernel(keep_x, got_x, keep_y, got_y, mid_x, send_y, mid_y, send_x):
-    n = mid_x.shape[0]
-    for keep, got, mid, send in ((keep_x, got_x, mid_x, send_y), (keep_y, got_y, mid_y, send_x)):
-        mid[...] = keep[:n].astype(F32) + got[:n].astype(F32)
-        send[...] = (keep[n:].astype(F32) + got[n:].astype(F32)).astype(BF)
-
-
-def half_sum_call(*ops):
-    rows, cols = ops[0].shape
+def half_sum_kernel(keep, got, mid, send):
+    n = mid.shape[0]
+    mid[...] = keep[:n].astype(F32) + got[:n].astype(F32)
+    send[...] = (keep[n:].astype(F32) + got[n:].astype(F32)).astype(BF)
+
+
+def half_sum_call(keep, got):
+    rows, cols = keep.shape
     t = 512
     n = rows // 2
     small = pl.BlockSpec((n, t), lambda j: (0, j))
@@ -609,36 +627,31 @@
         half_sum_kernel,
         name="hsum",
         grid=(cols // t,),
-        in_specs=[pl.BlockSpec((rows, t), lambda j: (0, j))] * 4,
-        out_specs=[small] * 4,
-        out_shape=[jax.ShapeDtypeStruct((n, cols), F32), jax.ShapeDtypeStruct((n, cols), BF)] * 2,
-        compiler_params=params(1),
-        cost_estimate=cost(8 * n * cols, 28 * n * cols),
-    )(*ops)
-
-
-def last_sum_kernel(plan, mid_x, got_y, mid_y, got_x, *outs):
+        in_specs=[pl.BlockSpec((rows, t), lambda j: (0, j))] * 2,
+        out_specs=[small] * 2,
+        out_shape=[jax.ShapeDtypeStruct((n, cols), F32), jax.ShapeDtypeStruct((n, cols), BF)],
+        compiler_params=params(1),
+        cost_estimate=cost(4 * n * cols, 14 * n * cols),
+    )(keep, got)
+
+
+def last_sum_kernel(plan, mid, got, *outs):
     j = pl.program_id(0)
-    half = sum(c for c, _ in plan) // 2
     at = 0
     for (count, turned), out in zip(plan, outs):
-        for k in range(at, at + count):
-            mid, got = (mid_x, got_y) if k < half else (mid_y, got_x)
-
-            @pl.when(j == k)
-            def _():
-                v = mid[...] + got[...].astype(F32)
-                out[...] = v.T if turned else v
+
+        @pl.when((j >= at) & (j < at + count))
+        def _():
+            v = mid[...] + got[...].astype(F32)
+            out[...] = v.T if turned else v
 
         at += count
 
 
-def last_sum_call(*ops, plan):
-    n, cols = ops[0].shape
+def last_sum_call(mid, got, plan):
+    n, cols = mid.shape
     t = 512
-    h = cols // t
-    left = pl.BlockSpec((n, t), lambda j: (0, jnp.minimum(j, h - 1)))
-    right = pl.BlockSpec((n, t), lambda j: (0, jnp.maximum(j - h, 0)))
+    block = pl.BlockSpec((n, t), lambda j: (0, j))
     out_specs, out_shape, at = [], [], 0
     for count, turned in plan:
         def place(j, at=at, count=count):
@@ -654,13 +667,13 @@
     return pl.pallas_call(
         functools.partial(last_sum_kernel, plan),
         name="lsum",
-        grid=(2 * h,),
-        in_specs=[left, left, right, right],
+        grid=(cols // t,),
+        in_specs=[block, block],
         out_specs=out_specs,
         out_shape=out_shape,
         compiler_params=params(1),
-        cost_estimate=cost(4 * n * cols, 20 * n * cols),
-    )(*ops)
+        cost_estimate=cost(2 * n * cols, 10 * n * cols),
+    )(mid, got)
 
 
 def total_of(meta, refs, c, cols):
@@ -822,38 +835,42 @@
 
     pipe = Pipe
 
-    def first_hop(self, own):
-        return self.x(own), self.y(own)
-
-    def diagonal(self, own, hop):
-        n = own.shape[0] // 2
-        return [self.x(hop[1][:n]), self.y(hop[0][n:])]
-
-    def diagonal_x(self, own, hop):
-        return [self.x(hop[1])]
-
-    def pack(self, run, own, hop, diag):
-        return run(pack_call, own, hop[1], hop[0], *diag)
-
-    def both(self, near):
-        return near, self.core(near)
-
-    def quarters_near(self, run, own, hop):
-        return self.both(run(pack_call, own, hop[1]))
-
-    def quarters_far(self, run, hop, diag):
-        return self.both(run(pack_call, hop[0], *diag))
+    def first_hop(self, own, earlier=None):
+        if earlier is None:
+            return self.x(own), self.y(own)
+        return self.x(after(own, earlier)), self.y(own)
+
+    def second_hop(self, hop, earlier=()):
+        return self.x(after(hop[1], hop[0], *earlier))
+
+    def waited(self, hop):
+        return hop
+
+    def near(self, run, own, hop):
+        v = run(pack_call, own, hop[1])
+        return v, self.core(v)
+
+    def pieces(self, near, hop, diag):
+        return near[0], hop[0], diag, near[1], self.core(hop[0]), self.core(diag)
+
+    def turn(self, v, first):
+        pairs = []
+        for dp in range(4):
+            for c in range(2):
+                to = (dp ^ 2) * 2 + c if dp % 2 != first else dp * 2 + (c ^ 1)
+                pairs.append((dp * 2 + c, to))
+        return lax.ppermute(v, ("dp", "ctx"), pairs)
 
     def scatter_cross(self, theirs):
         return self.core(theirs)
 
-    def scatter_own(self, run, pairs, got):
-        keep_x, send_x, keep_y, send_y = run(wgrad_call, *pairs, half=0, add=got, split=True)
-        return keep_x, self.x(send_x), keep_y, self.y(send_y)
+    def scatter_own(self, run, meta, pairs, got):
+        keep, send = run(wgrad_call, meta, *pairs, half=0, add=got, split=True)
+        return keep, self.turn(send, 1)
 
     def scatter_half(self, run, parts):
-        mid_x, to_y, mid_y, to_x = run(half_sum_call, *parts)
-        return mid_x, self.y(to_y), mid_y, self.x(to_x)
+        mid, send = run(half_sum_call, *parts)
+        return mid, self.turn(send, 0)
 
     def scatter_last(self, run, plan, parts):
         return run(last_sum_call, *parts, plan=plan)
@@ -864,16 +881,21 @@
     def give_back(self, dpv, dkv, slots):
         return dkv, lax.ppermute(dpv, "ctx", [(1, 0)])
 
-    def small_sum(self, group, everywhere):
-        n = group.shape[0]
-        v = jnp.concatenate([group, everywhere])
-        v = v + self.core(v)
-        v = v + self.x(v)
-        v = v + self.y(v)
-        w = v[n:]
-        w = w + lax.ppermute(w, "tensor", [(0, 1), (1, 0), (2, 3), (3, 2)])
-        w = w + lax.ppermute(w, "tensor", [(0, 2), (2, 0), (1, 3), (3, 1)])
-        return v[:n], w
+    def small_sum(self, run, v, step):
+        def add(a, b):
+            return a + b
+
+        if step == 0:
+            got = self.core(v)
+        elif step == 1:
+            got = self.x(v)
+        elif step == 2:
+            got = self.y(v)
+        elif step == 3:
+            got = lax.ppermute(v, "tensor", [(0, 1), (1, 0), (2, 3), (3, 2)])
+        else:
+            got = lax.ppermute(v, "tensor", [(0, 2), (2, 0), (1, 3), (3, 1)])
+        return lambda: run(add, v, got)
 
 
 class AnyMesh:
@@ -885,34 +907,26 @@
 
     pipe = PlainPipe
 
-    def first_hop(self, own):
+    def first_hop(self, own, earlier=None):
         return lax.all_gather(own, ("dp", "ctx"), axis=0, tiled=True)
 
-    def diagonal(self, own, hop):
+    def second_hop(self, hop, earlier=()):
         return ()
 
-    diagonal_x = diagonal
-
-    def both(self, full):
-        n = full.shape[0] // 2
-        return full[:n], full[n:]
-
-    def pack(self, run, own, hop, diag):
-        return hop
-
-    def quarters_near(self, run, own, hop):
-        n = hop.shape[0] // 4
-        return hop[:n], hop[2 * n : 3 * n]
-
-    def quarters_far(self, run, hop, diag):
-        n = hop.shape[0] // 4
-        return hop[n : 2 * n], hop[3 * n :]
+    def waited(self, hop):
+        return (hop,)
+
+    def near(self, run, own, hop):
+        return hop[:512], hop[1024:1536]
+
+    def pieces(self, near, hop, diag):
+        return near[0], hop[512:768], hop[768:1024], near[1], hop[1536:1792], hop[1792:]
 
     def scatter_cross(self, theirs):
         return theirs
 
-    def scatter_own(self, run, pairs, got):
-        full = jnp.concatenate([run(wgrad_call, *pairs, half=0), got], axis=0)
+    def scatter_own(self, run, meta, pairs, got):
+        full = jnp.concatenate([run(wgrad_call, meta, *pairs, half=0), got], axis=0)
         return lax.psum_scatter(full, ("dp", "ctx"), scatter_dimension=0, tiled=True).astype(F32)
 
     def scatter_half(self, run, parts):
@@ -937,8 +951,13 @@
         got = lax.psum_scatter(full, "ctx", scatter_dimension=1, tiled=True)
         return dkv, got.reshape(-1, cols)
 
-    def small_sum(self, group, everywhere):
-        return lax.psum(group, ("dp", "ctx")), lax.psum(everywhere, ("dp", "ctx", "tensor"))
+    def small_sum(self, run, v, step):
+        got = v
+        if step == 0:
+            got = lax.psum(v, ("dp", "ctx"))
+        elif step == 3:
+            got = lax.psum(v, "tensor")
+        return lambda: got
 
 
 def rotary_tables(positions):
@@ -960,7 +979,10 @@
     nheads = b_qkv.shape[0] // (3 * HD)
     nq = 3 * nheads * HD
     ctx = lax.axis_index("ctx")
-    meta = jnp.concatenate([ctx[None].astype(jnp.int32), comm.perm(), comm.middle()[None], lengths])
+    core = lax.axis_index("dp") % 2
+    meta = jnp.concatenate(
+        [ctx[None].astype(jnp.int32), comm.perm(), comm.middle()[None], core[None].astype(jnp.int32), lengths]
+    )
 
     run = Order()
     x2 = block_input.reshape(m, d)
@@ -972,101 +994,95 @@
 
     own1 = jnp.concatenate([w_qkv, w_proj.T], axis=1).astype(BF)
     hop1 = comm.first_hop(own1)
-    run.last = (own1,)
-    h1, h2, g, stats, g_sum = run(norm_call, meta, x2, og2, ga, sa, gf, sf, local_len)
     own2 = w_in.astype(BF)
     own3 = w_out.T.astype(BF)
-    diag1 = comm.diagonal(own1, hop1)
-    hop2 = comm.first_hop(own2)
-    near1 = comm.pack(run, own1, hop1, diag1)
-    g1 = comm.both(near1)
-    kv = run(kv_call, h1, *g1, bq, tabs, nheads)
+    run.last = (own1, own2, own3)
+    hop2 = comm.first_hop(own2, hop1[0])
+    h1, h2, g, stats, g_sum = run(norm_call, meta, x2, og2, ga, sa, gf, sf, local_len)
+    diag1 = comm.second_hop(hop1)
+    near1 = comm.near(run, own1, hop1)
+    g1 = comm.pieces(near1, hop1, diag1)
+    near2 = comm.near(run, own2, hop2)
+    kv = run(kv_call, h1, g1, bq, tabs, nheads)
     pv = comm.previous(kv, slots)
-    diag2 = comm.diagonal_x(own2, hop2)
-    hop3 = comm.first_hop(own3)
-    q, dob = run(qd_call, h1, g, *g1, bq, tabs, nheads)
-    near2 = comm.pack(run, own2, hop2, diag2)
-    g2 = comm.both(near2)
-    diag3 = comm.diagonal_x(own3, hop3)
-    gb, dg = run(hidden_call, h2, *g2, b_in.reshape(1, -1))
-    cross3 = comm.scatter_cross(run(wgrad_call, g, gb, half=1))
-    one, three = comm.quarters_near(run, own3, hop3)
+    diag2 = comm.second_hop(hop2, (kv,))
+    hop3 = comm.first_hop(own3, diag2)
+    q, dob = run(qd_call, h1, g, g1, bq, tabs, nheads)
+    near3 = comm.near(run, own3, hop3)
+    g2 = comm.pieces(near2, hop2, diag2)
+    diag3 = comm.second_hop(hop3)
     ob, dq, dkv, dpv = run(attn_call, meta, q, kv, pv, dob, tabs, nheads)
     dkv, rv = comm.give_back(dpv, dkv, slots)
+    gb, dg = run(hidden_call, after(h2, *comm.waited(hop3)), g2, b_in.reshape(1, -1))
+    g3 = comm.pieces(near3, hop3, diag3)
 
     pipe = comm.pipe(run, meta[1 + NBLK], 8)
-
-    def out_part(c, quarter):
-        return run(out_call, ob, gb, g1[c // 2], quarter, c)
-
-    pipe.send(out_part(0, one))
-    two, four = comm.quarters_far(run, hop3, diag3)
-    pipe.send(out_part(2, three))
-    pipe.send(out_part(1, two))
-    last_out = out_part(3, four)
+    ff = gb.shape[1] // 512
+    out0, out2 = run(out_call, ob, gb, (g1[0], g1[3]), (g3[0], g3[3]))
+    pipe.send(out0)
+    pipe.send(out2)
+    cross3 = comm.scatter_cross(run(wgrad_call, meta, g, gb, half=1))
+    far = (1, 2, 4, 5)
+    out1, out3 = run(out_call, ob, gb, [g1[k] for k in far], [g3[k] for k in far])
+    du, bin_sum = run(dhid_call, g, g3, dg)
+    pipe.send(after(out1, du))
     pipe.cross()
-    du, bin_sum = run(dhid_call, g, (one, two, three, four), dg)
+    state3 = comm.scatter_own(run, meta, (g, gb), cross3)
+    pipe.cross()
     dqkv, bqkv_sum = run(join_call, dq, dkv, rv, tabs, nheads)
+    pipe.send(out3)
+    gain_sums = jnp.zeros((4, d), F32)
+    dn0, dn1, gain_sums = run(back_call, meta, dqkv, du, g1, g2, x2, stats, ga, gf, gain_sums, 0)
     pipe.cross()
-    gain_sums = jnp.zeros((4, d), F32)
-    dn_parts = []
-
-    def back_part(c):
-        nonlocal gain_sums
-        part, gain_sums = run(back_call, meta, dqkv, du, g1[c // 2], g2[c // 2], x2, stats, ga, gf, gain_sums, c)
-        dn_parts.append(part)
-
-    ff = du.shape[1] // 512
-    back_part(0)
-    pipe.send(last_out)
-    back_part(1)
-    state3 = comm.scatter_own(run, (g, gb), cross3)
+    pipe.send(dn0)
+    state3 = comm.scatter_half(run, state3)
+    theirs1 = run(wgrad_call, meta, h1, dqkv, g, ob, half=1)
     pipe.cross()
-    pipe.send(dn_parts[0])
-    back_part(2)
-    cross2 = comm.scatter_cross(run(wgrad_call, h2, du, half=1))
+    pipe.send(dn1)
+    cross2 = comm.scatter_cross(run(wgrad_call, after(meta, jax.tree.leaves(state3)[-1]), h2, du, half=1))
+    dn2, dn3, gain_sums = run(back_call, meta, dqkv, du, g1, g2, x2, stats, ga, gf, gain_sums, 1)
     pipe.cross()
-    pipe.send(dn_parts[1])
-    back_part(3)
-    state3 = comm.scatter_half(run, state3)
-    state2 = comm.scatter_own(run, (h2, du), cross2)
+    pipe.send(dn2)
+    state2 = comm.scatter_own(run, meta, (h2, du), cross2)
+    (grad_out,) = comm.scatter_last(run, ((ff, True),), state3)
     pipe.cross()
-    pipe.send(dn_parts[2])
-    group, gains = comm.small_sum(
-        jnp.concatenate([g_sum.reshape(-1), bqkv_sum.reshape(-1), bin_sum.reshape(-1)]),
-        gain_sums.reshape(-1),
-    )
-    gains = gains.reshape(4, d)
-    bias_grad = group[:d]
-    (grad_out,) = comm.scatter_last(run, ((ff, True),), state3)
-    cross1 = comm.scatter_cross(run(wgrad_call, h1, dqkv, g, ob, half=1))
+    pipe.send(dn3)
     state2 = comm.scatter_half(run, state2)
     pipe.cross()
-    pipe.send(dn_parts[3])
-    state1 = comm.scatter_own(run, (h1, dqkv, g, ob), cross1)
+    pipe.send()
+    cross1 = comm.scatter_cross(after(theirs1, pipe.here[-1]))
+
+    def sums_of(order):
+        return [v for c in order for v in (pipe.here[c], pipe.sent[c])]
+
+    block_output = run(
+        rows_call, meta, x2, (b_proj + b_out).reshape(1, d), *sums_of((0, 2, 1, 3)),
+        body=functools.partial(block_out_kernel, local_len), name="bout", specs=("row", "vec") + ("part",) * 8,
+    ).reshape(slots, local_len, d)
     (grad_in,) = comm.scatter_last(run, ((ff, False),), state2)
+    state1 = comm.scatter_own(run, meta, (h1, dqkv, g, ob), cross1)
     pipe.cross()
     pipe.send()
-    state1 = comm.scatter_half(run, state1)
-    order = (0, 2, 1, 3)
-
-    def sums_of(first, order):
-        return [v for c in order for v in (pipe.here[first + c], pipe.sent[first + c])]
-
-    block_output = run(
-        rows_call, meta, x2, (b_proj + b_out).reshape(1, d), *sums_of(0, order),
-        body=functools.partial(block_out_kernel, local_len), name="bout", specs=("row", "vec") + ("part",) * 8,
-    ).reshape(slots, local_len, d)
-    pipe.cross()
+    small = jnp.concatenate([gain_sums.reshape(-1), g_sum.reshape(-1), bqkv_sum.reshape(-1), bin_sum.reshape(-1)])
+    small = after(small, pipe.here[-1])
+    for step in range(3):
+        small = comm.small_sum(run, small, step)()
+    gains = small[: 4 * d]
+    group = small[4 * d :]
+    state1 = comm.scatter_half(run, after(state1, pipe.sent[5]))
+    add = comm.small_sum(run, gains, 3)
     pipe.send()
     grad_qkv, grad_proj = comm.scatter_last(
-        run, ((nq // 512, False), (nheads * HD // 512, True)), state1
+        run, ((nq // 512, False), (nheads * HD // 512, True)), after(state1, pipe.sent[6])
     )
-    pipe.send()
+    gains = add()
+    add = comm.small_sum(run, gains, 4)
+    gains = add().reshape(4, d)
     input_grad = run(
-        rows_call, meta, x2, og2, stats, *sums_of(4, range(4)),
+        rows_call, meta, x2, og2, stats, *sums_of(range(4, 8)),
         body=functools.partial(input_grad_kernel, local_len), name="igrad", specs=("row", "row", "stat") + ("part",) * 8,
     ).reshape(slots, local_len, d)
+    bias_grad = group[:d]
     return (
         block_output,
         input_grad,

time: 606 us -> 571 us (0.942)
  waiting for transfers between devices: 194 us -> 158 us
  Pallas kernels: 273 us -> 256 us
  starting transfers between devices: 80.1 us -> 94.8 us
    ppermute x11 -> x4, waiting for transfers between devices: 75.8 us -> 7.43 us  [y(): return lax.ppermute(v, 'ctx', [(0, 1), (1, 0)])]
    ppermute x13 -> x7, waiting for transfers between devices: 32.4 us -> 67.5 us  [x(): return lax.ppermute(v, 'dp', [(0, 2), (2, 0), (1, 3), (3, 1)])]
    ppermute x2 -> x8, waiting for transfers between devices: 41.4 us -> 20.5 us  [the longest x1 16.9 us: small_sum(): got = lax.ppermute(v, 'tensor', [(0, 1), (1, 0), (2, 3), (3, 2)])]
    ppermute x2 -> x8, starting transfers between devices: 7.86 us -> 28 us  [the longest x1 18.7 us: small_sum(): got = lax.ppermute(v, 'tensor', [(0, 1), (1, 0), (2, 3), (3, 2)])]
    pallas_call x8 -> x4, Pallas kernels: 71.9 us -> 54.8 us  [the longest x2 32.3 us: back_call(): pl.pallas_call(back_kernel, name='backn', grid_spec=pltpu.PrefetchScalarG...]
    ppermute x11, waiting for transfers between devices: 22.3 us -> 35.5 us  [send(): got = lax.ppermute(v, 'tensor', pairs)]
    pallas_call x4 -> x3, Pallas kernels: 17.4 us -> 11.4 us  [pack_call(): pl.pallas_call(pack_kernel, name='pack', grid=(cols // t,), in_specs=[pl....]
    ppermute x11 -> x4, starting transfers between devices: 12.2 us -> 6.56 us  [y(): return lax.ppermute(v, 'ctx', [(0, 1), (1, 0)])]
  transfers between devices with their start and end apart: 55 -> 53, of which waited for: 15 -> 16; matrix products, arithmetic and copies ran while one was open for 7% -> 8% of each run, Pallas kernels for 36% -> 41%
where the time goes in v2:
time: 571 us; the launch traced here: 564 us
  Pallas kernels  256 us (45%)
  waiting for transfers between devices  158 us (28%)
  starting transfers between devices  94.8 us (17%)
  other arithmetic  42.6 us (7%)
  local copies, waits for them, and re-layouts  11.5 us (2%)
    ppermute x7, waiting for transfers between devices, x(): return lax.ppermute(v, 'dp', [(0, 2), (2, 0), (1, 3), (3, 1)])  67.5 us
    pallas_call x6, Pallas kernels, wgrad_call(): pl.pallas_call(functools.partial(wgrad_kernel, counts, add is not None, s...  59.6 us
    ppermute x11, waiting for transfers between devices, send(): got = lax.ppermute(v, 'tensor', pairs)  35.5 us
    pallas_call x2, Pallas kernels, back_call(): pl.pallas_call(back_kernel, name='backn', grid_spec=pltpu.PrefetchScalarG...  32.3 us
    ppermute x11, starting transfers between devices, send(): got = lax.ppermute(v, 'tensor', pairs)  31.9 us
    convert_element_type x11, other arithmetic, add_bf(): return lax.optimization_barrier((a.astype(F32) + b.astype(F32)).astype(BF))  24.7 us
    pallas_call x2, Pallas kernels, out_call(): pl.pallas_call(functools.partial(out_kernel, count), name='outp', grid=(4...  22.5 us
    pallas_call x2, Pallas kernels, rows_call(): pl.pallas_call(body, name=name, grid_spec=pltpu.PrefetchScalarGridSpec(nu...  20.8 us
  transfers between devices with their start and end apart: 53, of which 16 were waited for; matrix products, arithmetic and copies ran while one was open for 8% of the time, Pallas kernels for 41%

profile of v2, /device:TPU:0, one launch (start us, length us, event | category | flops | bytes accessed | tf_op | source)
XLA Modules:
  0.0 564.1 jit_solution(12726503169265063410)
XLA Ops:
  2.5 3.1 collective-permute-start
  7.1 2.5 copy.31
  12.2 11.9 %norm.1 = (bf16[1024,2048]{1,0:T(8,128)(2,1)}, bf16[1024,2048]{1,0:T(8,128)(2,1)}, bf16[1024,2048]{1,0:T(8,128)(2,1)}, f32[1024,128]{1,0:T(8,128)}, f32[1,2048]{1,0:T(1,128)}) custom-call(s32[13]{0:T(128)} %concatenate.10.meta, bf16[1024,2048]{1,0:T(8,128)(2,1)} %bitcast.23, bf16[1024,2048]{1,0:T(8,128)(2,1)} %bitcast.28, f32[1,2048]{1,0:T(1,128)} %bitcast.40, ...), custom_call_target="tpu_custom_call" | custom-call | flops 838860800 | bytes 419430400 | tf_op jit(solution)/shard_map/norm/pallas_call | solution.py:101
  24.0 4.7 collective-permute-done.refs_1_
  29.7 3.8 pack.3.w0.refs_0_.w10
  37.3 22.6 %collective-permute-done.3.w2.refs_1_.w12 = bf16[256,2048]{1,0:T(8,128)(2,1)} collective-permute-done((bf16[256,2048]{1,0:T(8,128)(2,1)}, bf16[256,2048]{1,0:T(8,128)(2,1)}, u32[]{:S(2)}, u32[]{:S(2)}) %collective-permute-start.3) | collective-permute-done | bytes 1048608 | tf_op jit(solution)/shard_map/ppermute | solution.py:819
  64.2 3.8 pack.4.w0.w20
  68.3 13.5 %collective-permute-done.9.w1.w21 = bf16[256,2048]{1,0:T(8,128)(2,1)} collective-permute-done((bf16[256,2048]{1,0:T(8,128)(2,1)S(1)}, bf16[256,2048]{1,0:T(8,128)(2,1)}, u32[]{:S(2)}, u32[]{:S(2)}) %collective-permute-start.9) | collective-permute-done | bytes 1048608 | tf_op jit(solution)/shard_map/ppermute | solution.py:819
  81.8 9.8 %kv.1.kv_ref = bf16[1024,1024]{1,0:T(8,128)(2,1)} custom-call(bf16[1024,2048]{1,0:T(8,128)(2,1)} %get-tuple-element.124.h1.refs_0_, bf16[512,2048]{1,0:T(8,128)(2,1)} %pack.3.w0.refs_0_.w10, bf16[256,2048]{1,0:T(8,128)(2,1)} %collective-permute-done.2.w1.refs_0_.w11, bf16[256,2048]{1,0:T(8,128)(2,1)} %collective-permute-done.3.w2.refs_1_.w12, ...), custom_call_target="tpu_custom_call" | custom-call | flops 85899345920 | bytes 209715200 | tf_op jit(solution)/shard_map/kv/pallas_call | solution.py:157
  91.7 4.1 collective-permute-start.8
  97.3 10.7 %qd.1 = (bf16[1024,512]{1,0:T(8,128)(2,1)}, bf16[1024,512]{1,0:T(8,128)(2,1)}) custom-call(bf16[1024,2048]{1,0:T(8,128)(2,1)} %get-tuple-element.124.h1.refs_0_, bf16[1024,2048]{1,0:T(8,128)(2,1)} %get-tuple-element.144.g.refs_0_.refs_2_, bf16[512,2048]{1,0:T(8,128)(2,1)} %pack.3.w0.refs_0_.w10, bf16[256,2048]{1,0:T(8,128)(2,1)} %collective-permute-done.2.w1.refs_0_.w11, ...), custom_call_target="tpu_custom_call" | custom-call | flops 85899345920 | bytes 293601280 | tf_op jit(solution)/shard_map/qd/pallas_call | solution.py:198
  108.1 3.8 pack.5.refs_2_.w0
  111.9 9.3 %collective-permute-done.10.w2.w22 = bf16[256,2048]{1,0:T(8,128)(2,1)} collective-permute-done((bf16[256,2048]{1,0:T(8,128)(2,1)S(1)}, bf16[256,2048]{1,0:T(8,128)(2,1)}, u32[]{:S(2)}, u32[]{:S(2)}) %collective-permute-start.10) | collective-permute-done | bytes 1048608 | tf_op jit(solution)/shard_map/ppermute | solution.py:819
  122.7 18.5 %collective-permute-done.8.pv_ref = bf16[1024,1024]{1,0:T(8,128)(2,1)S(1)} collective-permute-done((bf16[1024,1024]{1,0:T(8,128)(2,1)}, bf16[1024,1024]{1,0:T(8,128)(2,1)S(1)}, u32[]{:S(2)}, u32[]{:S(2)}) %collective-permute-start.8) | collective-permute-done | bytes 2097184 | tf_op jit(solution)/shard_map/ppermute | solution.py:879
  142.5 12.4 %attn.1 = (bf16[1024,512]{1,0:T(8,128)(2,1)}, bf16[1024,512]{1,0:T(8,128)(2,1)}, f32[1024,1024]{1,0:T(8,128)}, bf16[1024,1024]{1,0:T(8,128)(2,1)}) custom-call(s32[13]{0:T(128)} %concatenate.10.meta, bf16[1024,512]{1,0:T(8,128)(2,1)} %get-tuple-element.126.q_ref, bf16[1024,1024]{1,0:T(8,128)(2,1)} %kv.1.kv_ref, bf16[1024,1024]{1,0:T(8,128)(2,1)} %copy-done.33, ...), custom_call_target="tpu_custom_call" | custom-call | flops 128849018880 | bytes 209715200 | tf_op jit(solution)/shard_map/attn/pallas_call | solution.py:307
  156.0 16.4 %hidden.1 = (bf16[1024,2048]{1,0:T(8,128)(2,1)}, bf16[1024,2048]{1,0:T(8,128)(2,1)}) custom-call(bf16[1024,2048]{1,0:T(8,128)(2,1)} %get-tuple-element.136.h2.refs_0_, bf16[512,2048]{1,0:T(8,128)(2,1)} %pack.4.w0.w20, bf16[256,2048]{1,0:T(8,128)(2,1)} %collective-permute-done.9.w1.w21, bf16[256,2048]{1,0:T(8,128)(2,1)} %collective-permute-done.10.w2.w22, ...), custom_call_target="tpu_custom_call" | custom-call | flops 171798691840 | bytes 419430400 | tf_op jit(solution)/shard_map/hidden/pallas_call | solution.py:387
  173.9 10.9 %outp.2 = (bf16[1024,512]{1,0:T(8,128)(2,1)}, bf16[1024,512]{1,0:T(8,128)(2,1)}) custom-call(bf16[1024,512]{1,0:T(8,128)(2,1)} %get-tuple-element.141.ob.refs_3_, bf16[1024,2048]{1,0:T(8,128)(2,1)} %get-tuple-element.137.gb.refs_1_, bf16[512,2048]{1,0:T(8,128)(2,1)} %pack.3.w0.refs_0_.w10, bf16[512,2048]{1,0:T(8,128)(2,1)} %collective-permute-done.4.w3.refs_1_.w10, ...), custom_call_target="tpu_custom_call" | custom-call | flops 107374182400 | bytes 251658240 | tf_op jit(solution)/shard_map/outp/pallas_call | solution.py:453
  184.8 5.0 collective-permute-start.19
  189.8 7.5 %collective-permute-done.16.refs_5_.w2 = bf16[256,2048]{1,0:T(8,128)(2,1)S(1)} collective-permute-done((bf16[256,2048]{1,0:T(8,128)(2,1)}, bf16[256,2048]{1,0:T(8,128)(2,1)S(1)}, u32[]{:S(2)}, u32[]{:S(2)}) %collective-permute-start.16) | collective-permute-done | bytes 1048608 | tf_op jit(solution)/shard_map/ppermute | solution.py:819
  197.3 9.2 %wgrad.6 = bf16[1024,2048]{1,0:T(8,128)(2,1)} custom-call(s32[13]{0:T(128)} %concatenate.10.meta, bf16[1024,2048]{1,0:T(8,128)(2,1)} %get-tuple-element.144.g.refs_0_.refs_2_, bf16[1024,2048]{1,0:T(8,128)(2,1)} %get-tuple-element.137.gb.refs_1_), custom_call_target="tpu_custom_call" | custom-call | flops 85899345920 | bytes 293601280 | tf_op jit(solution)/shard_map/wgrad/pallas_call | solution.py:576
  207.0 4.5 collective-permute-start.21
  213.8 11.6 %outp.3 = (bf16[1024,512]{1,0:T(8,128)(2,1)}, bf16[1024,512]{1,0:T(8,128)(2,1)}) custom-call(bf16[1024,512]{1,0:T(8,128)(2,1)} %get-tuple-element.141.ob.refs_3_, bf16[1024,2048]{1,0:T(8,128)(2,1)} %get-tuple-element.137.gb.refs_1_, bf16[256,2048]{1,0:T(8,128)(2,1)} %collective-permute-done.2.w1.refs_0_.w11, ...), custom_call_target="tpu_custom_call" | custom-call | flops 107374182400 | bytes 251658240 | tf_op jit(solution)/shard_map/outp/pallas_call | solution.py:453
  225.5 15.2 %dhid.1 = (bf16[1024,2048]{1,0:T(8,128)(2,1)}, f32[1,2048]{1,0:T(1,128)}) custom-call(bf16[1024,2048]{1,0:T(8,128)(2,1)} %get-tuple-element.144.g.refs_0_.refs_2_, bf16[512,2048]{1,0:T(8,128)(2,1)} %pack.5.refs_2_.w0, bf16[256,2048]{1,0:T(8,128)(2,1)} %collective-permute-done.11.refs_4_.w1, bf16[256,2048]{1,0:T(8,128)(2,1)} %copy-done.36, ...), custom_call_target="tpu_custom_call" | custom-call | flops 171798691840 | bytes 419430400 | tf_op jit(solution)/shard_map/dhid/pallas_call | solution.py:412
  242.9 4.1 collective-permute-start.24
  247.0 10.0 %wgrad.7 = (bf16[512,2048]{1,0:T(8,128)(2,1)}, bf16[512,2048]{1,0:T(8,128)(2,1)}) custom-call(s32[13]{0:T(128)} %concatenate.10.meta, bf16[1024,2048]{1,0:T(8,128)(2,1)} %get-tuple-element.144.g.refs_0_.refs_2_, bf16[1024,2048]{1,0:T(8,128)(2,1)} %get-tuple-element.137.gb.refs_1_, bf16[1024,2048]{1,0:T(8,128)(2,1)} %collective-permute-done.20.refs_2_), custom_call_target="tpu_custom_call" | custom-call | flops 85899345920 | bytes 293601280 | tf_op jit(solution)/shard_map/wgrad/pallas_call | solution.py:576
  257.0 2.8 add_convert_fusion.14
  261.6 7.2 %collective-permute-done.22.rv_ref = bf16[1024,1024]{1,0:T(8,128)(2,1)} collective-permute-done((bf16[1024,1024]{1,0:T(8,128)(2,1)}, bf16[1024,1024]{1,0:T(8,128)(2,1)}, u32[]{:S(2)}, u32[]{:S(2)}) %collective-permute-start.22) | collective-permute-done | bytes 2097184 | tf_op jit(solution)/shard_map/ppermute | solution.py:882
  268.8 6.0 %join.1 = (bf16[1024,1536]{1,0:T(8,128)(2,1)}, f32[1,1536]{1,0:T(1,128)}) custom-call(bf16[1024,512]{1,0:T(8,128)(2,1)} %get-tuple-element.153.dq_ref, f32[1024,1024]{1,0:T(8,128)} %get-tuple-element.154.dkv_ref, bf16[1024,1024]{1,0:T(8,128)(2,1)} %collective-permute-done.22.rv_ref, f32[512,128]{1,0:T(8,128)} %get-tuple-element.230.cosf, ...), custom_call_target="tpu_custom_call" | custom-call | flops 314572800 | bytes 251658240 | tf_op jit(solution)/shard_map/join/pallas_call | solution.py:362
  278.3 16.0 %backn.2 = (bf16[1024,512]{1,0:T(8,128)(2,1)}, bf16[1024,512]{1,0:T(8,128)(2,1)}, f32[4,2048]{1,0:T(4,128)}) custom-call(s32[13]{0:T(128)} %concatenate.10.meta, bf16[1024,1536]{1,0:T(8,128)(2,1)} %get-tuple-element.156.dqkv.refs_1_, bf16[1024,2048]{1,0:T(8,128)(2,1)} %get-tuple-element.146.du.refs_1_, ...), custom_call_target="tpu_custom_call", output_to_operand_aliasing={{2}: (13, {})} | custom-call | flops 150323855360 | bytes 377487360 | tf_op jit(solution)/shard_map/backn/pallas_call | solution.py:497
  294.3 1.9 add_convert_fusion.12
  297.9 2.9 fusion.1.refs_4_
  300.8 3.9 collective-permute-start.30
  304.7 4.5 hsum.3
  309.1 3.2 collective-permute-start.28
  312.3 10.1 %wgrad.8 = bf16[1024,2048]{1,0:T(8,128)(2,1)} custom-call(s32[13]{0:T(128)} %concatenate.10.meta, bf16[1024,2048]{1,0:T(8,128)(2,1)} %get-tuple-element.124.h1.refs_0_, bf16[1024,1536]{1,0:T(8,128)(2,1)} %get-tuple-element.156.dqkv.refs_1_, bf16[1024,2048]{1,0:T(8,128)(2,1)} %get-tuple-element.144.g.refs_0_.refs_2_, ...), custom_call_target="tpu_custom_call" | custom-call | flops 85899345920 | bytes 335544320 | tf_op jit(solution)/shard_map/wgrad/pallas_call | solution.py:576
  322.4 2.6 add_convert_fusion.10
  326.9 2.6 fusion.2.refs_2_
  329.5 9.3 %wgrad.9 = bf16[1024,2048]{1,0:T(8,128)(2,1)} custom-call(s32[13]{0:T(128)} %concatenate.10.meta, bf16[1024,2048]{1,0:T(8,128)(2,1)} %get-tuple-element.136.h2.refs_0_, bf16[1024,2048]{1,0:T(8,128)(2,1)} %get-tuple-element.146.du.refs_1_), custom_call_target="tpu_custom_call" | custom-call | flops 85899345920 | bytes 293601280 | tf_op jit(solution)/shard_map/wgrad/pallas_call | solution.py:576
  338.7 16.3 %backn.3 = (bf16[1024,512]{1,0:T(8,128)(2,1)}, bf16[1024,512]{1,0:T(8,128)(2,1)}, f32[4,2048]{1,0:T(4,128)}) custom-call(s32[13]{0:T(128)} %concatenate.10.meta, bf16[1024,1536]{1,0:T(8,128)(2,1)} %get-tuple-element.156.dqkv.refs_1_, bf16[1024,2048]{1,0:T(8,128)(2,1)} %get-tuple-element.146.du.refs_1_, ...), custom_call_target="tpu_custom_call", output_to_operand_aliasing={{2}: (13, {})} | custom-call | flops 150323855360 | bytes 377487360 | tf_op jit(solution)/shard_map/backn/pallas_call | solution.py:497
  355.1 2.6 add_convert_fusion.8
  357.7 2.9 fusion.3.refs_6_
  360.6 10.2 %wgrad.10 = (bf16[512,2048]{1,0:T(8,128)(2,1)}, bf16[512,2048]{1,0:T(8,128)(2,1)}) custom-call(s32[13]{0:T(128)} %concatenate.10.meta, bf16[1024,2048]{1,0:T(8,128)(2,1)} %get-tuple-element.136.h2.refs_0_, bf16[1024,2048]{1,0:T(8,128)(2,1)} %get-tuple-element.146.du.refs_1_, bf16[1024,2048]{1,0:T(8,128)(2,1)} %collective-permute-done.32.refs_2_), custom_call_target="tpu_custom_call" | custom-call | flops 85899345920 | bytes 293601280 | tf_op jit(solution)/shard_map/wgrad/pallas_call | solution.py:576
  375.6 2.1 collective-permute-start.36
  377.7 4.4 lsum.3
  382.1 16.2 %collective-permute-done.33.refs_3_ = bf16[1024,512]{1,0:T(8,128)(2,1)} collective-permute-done((bf16[1024,512]{1,0:T(8,128)(2,1)S(1)}, bf16[1024,512]{1,0:T(8,128)(2,1)}, u32[]{:S(2)}, u32[]{:S(2)}) %collective-permute-start.33) | collective-permute-done | bytes 1048608 | tf_op jit(solution)/shard_map/ppermute | solution.py:790
  398.3 2.5 add_convert_fusion.6
  402.7 2.0 fusion.4.refs_0_
  404.7 4.8 hsum.4
  409.5 9.8 %collective-permute-done.36.refs_7_ = bf16[1024,512]{1,0:T(8,128)(2,1)} collective-permute-done((bf16[1024,512]{1,0:T(8,128)(2,1)}, bf16[1024,512]{1,0:T(8,128)(2,1)}, u32[]{:S(2)}, u32[]{:S(2)}) %collective-permute-start.36) | collective-permute-done | bytes 1048608 | tf_op jit(solution)/shard_map/ppermute | solution.py:790
  419.3 2.5 add_convert_fusion.4
  426.0 6.7 %collective-permute-start.40 = (bf16[1024,512]{1,0:T(8,128)(2,1)S(1)}, bf16[1024,512]{1,0:T(8,128)(2,1)S(1)}, u32[]{:S(2)}, u32[]{:S(2)}) collective-permute-start(bf16[1024,512]{1,0:T(8,128)(2,1)S(1)} %fusion.4.refs_0_), channel_id=1, source_target_pairs={{0,1},{3,2},{1,0},{2,3},{4,5},{7,6},{5,4},{6,7},{8,9},{11,10},{9,8... | collective-permute-start | bytes 3145736 | tf_op jit(solution)/shard_map/ppermute | solution.py:790
  432.6 8.8 %bout.1 = bf16[1024,2048]{1,0:T(8,128)(2,1)} custom-call(s32[13]{0:T(128)} %concatenate.10.meta, bf16[1024,2048]{1,0:T(8,128)(2,1)} %bitcast.26, f32[1,2048]{1,0:T(1,128)} %bitcast.35, bf16[1024,512]{1,0:T(8,128)(2,1)} %fusion.refs_0_, bf16[1024,512]{1,0:T(8,128)(2,1)} %collective-permute-done.27.refs_1_, bf16[1024,512]{1,0:T(8,128)(2,1)} %fusion.2.refs_2_, ...), custom_call_target="tpu_custom_call" | custom-call | flops 419430400 | bytes 335544320 | tf_op jit(solution)/shard_map/bout/pallas_call | solution.py:729
  441.4 4.0 lsum.4
  445.4 10.8 %wgrad.11 = (bf16[512,2048]{1,0:T(8,128)(2,1)}, bf16[512,2048]{1,0:T(8,128)(2,1)}) custom-call(s32[13]{0:T(128)} %concatenate.10.meta, bf16[1024,2048]{1,0:T(8,128)(2,1)} %get-tuple-element.124.h1.refs_0_, bf16[1024,1536]{1,0:T(8,128)(2,1)} %get-tuple-element.156.dqkv.refs_1_, bf16[1024,2048]{1,0:T(8,128)(2,1)} %get-tuple-element.144.g.refs_0_.refs_2_, ...), custom_call_target="tpu_custom_call" | custom-call | flops 85899345920 | bytes 335544320 | tf_op jit(solution)/shard_map/wgrad/pallas_call | solution.py:576
  460.5 2.9 add_convert_fusion.2
  469.2 14.6 %collective-permute-done.43 = f32[13824]{0:T(1024)S(1)} collective-permute-done((f32[13824]{0:T(1024)S(1)}, f32[13824]{0:T(1024)S(1)}, u32[]{:S(2)}, u32[]{:S(2)}) %collective-permute-start.43) | collective-permute-done | bytes 55328 | tf_op jit(solution)/shard_map/ppermute | solution.py:819
  485.3 2.7 collective-permute-done.44
  488.6 4.4 hsum.5
  496.4 18.7 %collective-permute-start.50 = (f32[8192]{0:T(1024)S(1)}, f32[8192]{0:T(1024)S(1)}, u32[]{:S(2)}, u32[]{:S(2)}) collective-permute-start(f32[8192]{0:T(1024)S(1)} %slice.40), channel_id=1, source_target_pairs={{0,1},{1,0},{2,3},{3,2},{4,5},{5,4},{6,7},{7,6},{8,9},{9,8},{10,11... | collective-permute-start | bytes 98312 | tf_op jit(solution)/shard_map/ppermute | solution.py:895
  515.2 9.1 %collective-permute-done.48.refs_5_ = bf16[1024,512]{1,0:T(8,128)(2,1)S(1)} collective-permute-done((bf16[1024,512]{1,0:T(8,128)(2,1)S(1)}, bf16[1024,512]{1,0:T(8,128)(2,1)S(1)}, u32[]{:S(2)}, u32[]{:S(2)}) %collective-permute-start.48) | collective-permute-done | bytes 1048608 | tf_op jit(solution)/shard_map/ppermute | solution.py:790
  524.2 4.7 lsum.5
  528.9 16.9 %collective-permute-done.50 = f32[8192]{0:T(1024)S(1)} collective-permute-done((f32[8192]{0:T(1024)S(1)}, f32[8192]{0:T(1024)S(1)}, u32[]{:S(2)}, u32[]{:S(2)}) %collective-permute-start.50) | collective-permute-done | bytes 32800 | tf_op jit(solution)/shard_map/ppermute | solution.py:895
  547.0 3.6 collective-permute-done.51
  551.2 12.0 %igrad.1 = bf16[1024,2048]{1,0:T(8,128)(2,1)} custom-call(s32[13]{0:T(128)} %concatenate.10.meta, bf16[1024,2048]{1,0:T(8,128)(2,1)} %bitcast.27, bf16[1024,2048]{1,0:T(8,128)(2,1)} %bitcast.29, f32[1024,128]{1,0:T(8,128)} %get-tuple-element.160.st_ref, bf16[1024,512]{1,0:T(8,128)(2,1)} %copy-done, bf16[1024,512]{1,0:T(8,128)(2,1)} %copy-done.2, ...), custom_call_target="tpu_custom_call" | custom-call | flops 419430400 | bytes 335544320 | tf_op jit(solution)/shard_map/igrad/pallas_call | solution.py:729
  (192 shorter events, 64.8 us)
Async XLA Ops:
  2.5 26.2 %collective-permute-start = (bf16[256,2048]{1,0:T(8,128)(2,1)S(1)}, bf16[256,2048]{1,0:T(8,128)(2,1)S(1)}, u32[]{:S(2)}, u32[]{:S(2)}) collective-permute-start(bf16[256,2048]{1,0:T(8,128)(2,1)S(1)} %pad_maximum_fusion.refs_0_), channel_id=1, source_target_pairs={{0,4},{4,0},{1,5},{5,1},{2,6},{6,2},{3,7},{7,3},{8,12},{12,8},{9,1... | collective-permute-start | bytes 3145736 | tf_op jit(solution)/shard_map/ppermute | solution.py:825
  5.6 27.9 %collective-permute-start.2 = (bf16[256,2048]{1,0:T(8,128)(2,1)S(1)}, bf16[256,2048]{1,0:T(8,128)(2,1)}, u32[]{:S(2)}, u32[]{:S(2)}) collective-permute-start(bf16[256,2048]{1,0:T(8,128)(2,1)S(1)} %pad_maximum_fusion.refs_0_), channel_id=1, source_target_pairs={{0,16},{16,0},{8,24},{24,8},{1,17},{17,1},{9,25},{25,9},{2,18},{18... | collective-permute-start | bytes 3145736 | tf_op jit(solution)/shard_map/ppermute | solution.py:819
  11.4 25.4 %copy-start.15 = (bf16[256,2048]{1,0:T(8,128)(2,1)}, bf16[256,2048]{1,0:T(8,128)(2,1)S(1)}, u32[]{:S(2)}) copy-start(bf16[256,2048]{1,0:T(8,128)(2,1)S(1)} %convert_element_type.174.refs_0_) | copy-start | bytes 3145732
  24.0 35.8 %copy-start.30 = (f32[1536]{0:T(1024)S(1)}, f32[1536]{0:T(1024)}, u32[]{:S(2)}) copy-start(f32[1536]{0:T(1024)} %param.23) | copy-start | bytes 18436
  33.4 48.4 %collective-permute-start.4 = (bf16[512,2048]{1,0:T(8,128)(2,1)}, bf16[512,2048]{1,0:T(8,128)(2,1)}, u32[]{:S(2)}, u32[]{:S(2)}) collective-permute-start(bf16[512,2048]{1,0:T(8,128)(2,1)} %pack.3.w0.refs_0_.w10), channel_id=1, source_target_pairs={{0,8},{8,0},{16,24},{24,16},{1,9},{9,1},{17,25},{25,17},{2,10},{10... | collective-permute-start | bytes 6291464 | tf_op jit(solution)/shard_map/ppermute | solution.py:822
  33.5 26.4 %collective-permute-start.3 = (bf16[256,2048]{1,0:T(8,128)(2,1)}, bf16[256,2048]{1,0:T(8,128)(2,1)}, u32[]{:S(2)}, u32[]{:S(2)}) collective-permute-start(bf16[256,2048]{1,0:T(8,128)(2,1)} %copy-done.20), channel_id=1, source_target_pairs={{0,16},{16,0},{8,24},{24,8},{1,17},{17,1},{9,25},{25,9},{2,18},{18... | collective-permute-start | bytes 3145736 | tf_op jit(solution)/shard_map/ppermute | solution.py:819
  35.2 27.2 %collective-permute-start.1 = (bf16[256,2048]{1,0:T(8,128)(2,1)S(1)}, bf16[256,2048]{1,0:T(8,128)(2,1)S(1)}, u32[]{:S(2)}, u32[]{:S(2)}) collective-permute-start(bf16[256,2048]{1,0:T(8,128)(2,1)S(1)} %convert_element_type.174.refs_0_), channel_id=1, source_target_pairs={{0,4},{4,0},{1,5},{5,1},{2,6},{6,2},{3,7},{7,3},{8,12},{12,8},{9,1... | collective-permute-start | bytes 3145736 | tf_op jit(solution)/shard_map/ppermute | solution.py:825
  36.8 31.3 %collective-permute-start.5 = (bf16[256,2048]{1,0:T(8,128)(2,1)}, bf16[256,2048]{1,0:T(8,128)(2,1)S(1)}, u32[]{:S(2)}, u32[]{:S(2)}) collective-permute-start(bf16[256,2048]{1,0:T(8,128)(2,1)} %collective-permute-done.2.w1.refs_0_.w11), channel_id=1, source_target_pairs={{0,8},{8,0},{16,24},{24,16},{1,9},{9,1},{17,25},{25,17},{2,10},{10... | collective-permute-start | bytes 3145736 | tf_op jit(solution)/shard_map/ppermute | solution.py:822
  36.8 45.1 %collective-permute-start.9 = (bf16[256,2048]{1,0:T(8,128)(2,1)S(1)}, bf16[256,2048]{1,0:T(8,128)(2,1)}, u32[]{:S(2)}, u32[]{:S(2)}) collective-permute-start(bf16[256,2048]{1,0:T(8,128)(2,1)S(1)} %convert_element_type.174.refs_0_), channel_id=1, source_target_pairs={{0,16},{16,0},{8,24},{24,8},{1,17},{17,1},{9,25},{25,9},{2,18},{18... | collective-permute-start | bytes 3145736 | tf_op jit(solution)/shard_map/ppermute | solution.py:819
  59.9 22.0 %collective-permute-start.6 = (bf16[256,2048]{1,0:T(8,128)(2,1)}, bf16[256,2048]{1,0:T(8,128)(2,1)}, u32[]{:S(2)}, u32[]{:S(2)}) collective-permute-start(bf16[256,2048]{1,0:T(8,128)(2,1)} %collective-permute-done.3.w2.refs_1_.w12), channel_id=1, source_target_pairs={{0,8},{8,0},{16,24},{24,16},{1,9},{9,1},{17,25},{25,17},{2,10},{10... | collective-permute-start | bytes 3145736 | tf_op jit(solution)/shard_map/ppermute | solution.py:822
  62.4 45.6 %collective-permute-start.7 = (bf16[256,2048]{1,0:T(8,128)(2,1)}, bf16[256,2048]{1,0:T(8,128)(2,1)}, u32[]{:S(2)}, u32[]{:S(2)}) collective-permute-start(bf16[256,2048]{1,0:T(8,128)(2,1)} %bitcast.21.refs_0_), channel_id=1, source_target_pairs={{0,4},{4,0},{1,5},{5,1},{2,6},{6,2},{3,7},{7,3},{8,12},{12,8},{9,1... | collective-permute-start | bytes 3145736 | tf_op jit(solution)/shard_map/ppermute | solution.py:825
  68.0 86.9 %collective-permute-start.12 = (bf16[512,2048]{1,0:T(8,128)(2,1)}, bf16[512,2048]{1,0:T(8,128)(2,1)}, u32[]{:S(2)}, u32[]{:S(2)}) collective-permute-start(bf16[512,2048]{1,0:T(8,128)(2,1)} %pack.4.w0.w20), channel_id=1, source_target_pairs={{0,8},{8,0},{16,24},{24,16},{1,9},{9,1},{17,25},{25,17},{2,10},{10... | collective-permute-start | bytes 6291464 | tf_op jit(solution)/shard_map/ppermute | solution.py:822
  81.8 73.2 %collective-permute-start.13 = (bf16[256,2048]{1,0:T(8,128)(2,1)}, bf16[256,2048]{1,0:T(8,128)(2,1)}, u32[]{:S(2)}, u32[]{:S(2)}) collective-permute-start(bf16[256,2048]{1,0:T(8,128)(2,1)} %collective-permute-done.9.w1.w21), channel_id=1, source_target_pairs={{0,8},{8,0},{16,24},{24,16},{1,9},{9,1},{17,25},{25,17},{2,10},{10... | collective-permute-start | bytes 3145736 | tf_op jit(solution)/shard_map/ppermute | solution.py:822
  91.7 49.5 %collective-permute-start.8 = (bf16[1024,1024]{1,0:T(8,128)(2,1)}, bf16[1024,1024]{1,0:T(8,128)(2,1)S(1)}, u32[]{:S(2)}, u32[]{:S(2)}) collective-permute-start(bf16[1024,1024]{1,0:T(8,128)(2,1)} %kv.1.kv_ref), channel_id=1, source_target_pairs={{0,4},{1,5},{2,6},{3,7},{8,12},{9,13},{10,14},{11,15},{16,20},{17,... | collective-permute-start | bytes 6291464 | tf_op jit(solution)/shard_map/ppermute | solution.py:879
  95.8 25.5 %collective-permute-start.10 = (bf16[256,2048]{1,0:T(8,128)(2,1)S(1)}, bf16[256,2048]{1,0:T(8,128)(2,1)}, u32[]{:S(2)}, u32[]{:S(2)}) collective-permute-start(bf16[256,2048]{1,0:T(8,128)(2,1)S(1)} %copy-done.22), channel_id=1, source_target_pairs={{0,16},{16,0},{8,24},{24,8},{1,17},{17,1},{9,25},{25,9},{2,18},{18... | collective-permute-start | bytes 3145736 | tf_op jit(solution)/shard_map/ppermute | solution.py:819
  111.9 62.0 %collective-permute-start.15 = (bf16[512,2048]{1,0:T(8,128)(2,1)}, bf16[512,2048]{1,0:T(8,128)(2,1)}, u32[]{:S(2)}, u32[]{:S(2)}) collective-permute-start(bf16[512,2048]{1,0:T(8,128)(2,1)} %pack.5.refs_2_.w0), channel_id=1, source_target_pairs={{0,8},{8,0},{16,24},{24,16},{1,9},{9,1},{17,25},{25,17},{2,10},{10... | collective-permute-start | bytes 6291464 | tf_op jit(solution)/shard_map/ppermute | solution.py:822
  121.2 33.7 %collective-permute-start.11 = (bf16[256,2048]{1,0:T(8,128)(2,1)}, bf16[256,2048]{1,0:T(8,128)(2,1)}, u32[]{:S(2)}, u32[]{:S(2)}) collective-permute-start(bf16[256,2048]{1,0:T(8,128)(2,1)} %bitcast.21.refs_0_), channel_id=1, source_target_pairs={{0,16},{16,0},{8,24},{24,8},{1,17},{17,1},{9,25},{25,9},{2,18},{18... | collective-permute-start | bytes 3145736 | tf_op jit(solution)/shard_map/ppermute | solution.py:819
  141.2 13.8 %collective-permute-start.14 = (bf16[256,2048]{1,0:T(8,128)(2,1)}, bf16[256,2048]{1,0:T(8,128)(2,1)S(1)}, u32[]{:S(2)}, u32[]{:S(2)}) collective-permute-start(bf16[256,2048]{1,0:T(8,128)(2,1)} %collective-permute-done.10.w2.w22), channel_id=1, source_target_pairs={{0,8},{8,0},{16,24},{24,16},{1,9},{9,1},{17,25},{25,17},{2,10},{10... | collective-permute-start | bytes 3145736 | tf_op jit(solution)/shard_map/ppermute | solution.py:822
  172.4 24.9 %collective-permute-start.16 = (bf16[256,2048]{1,0:T(8,128)(2,1)}, bf16[256,2048]{1,0:T(8,128)(2,1)S(1)}, u32[]{:S(2)}, u32[]{:S(2)}) collective-permute-start(bf16[256,2048]{1,0:T(8,128)(2,1)} %collective-permute-done.7.refs_1_), channel_id=1, source_target_pairs={{0,16},{16,0},{8,24},{24,8},{1,17},{17,1},{9,25},{25,9},{2,18},{18... | collective-permute-start | bytes 3145736 | tf_op jit(solution)/shard_map/ppermute | solution.py:819
  184.8 55.9 %collective-permute-start.19 = (bf16[1024,512]{1,0:T(8,128)(2,1)}, bf16[1024,512]{1,0:T(8,128)(2,1)}, u32[]{:S(2)}, u32[]{:S(2)}) collective-permute-start(bf16[1024,512]{1,0:T(8,128)(2,1)} %get-tuple-element.147), channel_id=1, source_target_pairs={{0,1},{3,2},{4,5},{7,6},{8,9},{11,10},{12,13},{15,14},{16,17},{19,... | collective-permute-start | bytes 3145736 | tf_op jit(solution)/shard_map/ppermute | solution.py:790
  189.7 21.8 %collective-permute-start.17 = (bf16[256,2048]{1,0:T(8,128)(2,1)}, bf16[256,2048]{1,0:T(8,128)(2,1)S(1)}, u32[]{:S(2)}, u32[]{:S(2)}) collective-permute-start(bf16[256,2048]{1,0:T(8,128)(2,1)} %collective-permute-done.11.refs_4_.w1), channel_id=1, source_target_pairs={{0,8},{8,0},{16,24},{24,16},{1,9},{9,1},{17,25},{25,17},{2,10},{10... | collective-permute-start | bytes 3145736 | tf_op jit(solution)/shard_map/ppermute | solution.py:822
  197.3 15.5 %collective-permute-start.18 = (bf16[256,2048]{1,0:T(8,128)(2,1)S(1)}, bf16[256,2048]{1,0:T(8,128)(2,1)S(1)}, u32[]{:S(2)}, u32[]{:S(2)}) collective-permute-start(bf16[256,2048]{1,0:T(8,128)(2,1)S(1)} %collective-permute-done.16.refs_5_.w2), channel_id=1, source_target_pairs={{0,8},{8,0},{16,24},{24,16},{1,9},{9,1},{17,25},{25,17},{2,10},{10... | collective-permute-start | bytes 3145736 | tf_op jit(solution)/shard_map/ppermute | solution.py:822
  206.5 40.5 %collective-permute-start.20 = (bf16[1024,2048]{1,0:T(8,128)(2,1)}, bf16[1024,2048]{1,0:T(8,128)(2,1)}, u32[]{:S(2)}, u32[]{:S(2)}) collective-permute-start(bf16[1024,2048]{1,0:T(8,128)(2,1)} %wgrad.6), channel_id=1, source_target_pairs={{0,8},{8,0},{16,24},{24,16},{1,9},{9,1},{17,25},{25,17},{2,10},{10... | collective-permute-start | bytes 12582920 | tf_op jit(solution)/shard_map/ppermute | solution.py:822
  207.0 49.9 %collective-permute-start.21 = (bf16[1024,512]{1,0:T(8,128)(2,1)}, bf16[1024,512]{1,0:T(8,128)(2,1)}, u32[]{:S(2)}, u32[]{:S(2)}) collective-permute-start(bf16[1024,512]{1,0:T(8,128)(2,1)} %get-tuple-element.152), channel_id=1, source_target_pairs={{0,1},{3,2},{4,5},{7,6},{8,9},{11,10},{12,13},{15,14},{16,17},{19,... | collective-permute-start | bytes 3145736 | tf_op jit(solution)/shard_map/ppermute | solution.py:790
  211.5 57.3 %collective-permute-start.22 = (bf16[1024,1024]{1,0:T(8,128)(2,1)}, bf16[1024,1024]{1,0:T(8,128)(2,1)}, u32[]{:S(2)}, u32[]{:S(2)}) collective-permute-start(bf16[1024,1024]{1,0:T(8,128)(2,1)} %get-tuple-element.155), channel_id=1, source_target_pairs={{4,0},{5,1},{6,2},{7,3},{12,8},{13,9},{14,10},{15,11},{20,16},{21,... | collective-permute-start | bytes 6291464 | tf_op jit(solution)/shard_map/ppermute | solution.py:882
  242.2 32.6 %collective-permute-start.23 = (bf16[1024,512]{1,0:T(8,128)(2,1)S(1)}, bf16[1024,512]{1,0:T(8,128)(2,1)S(1)}, u32[]{:S(2)}, u32[]{:S(2)}) collective-permute-start(bf16[1024,512]{1,0:T(8,128)(2,1)S(1)} %add_convert_fusion.15), channel_id=1, source_target_pairs={{1,2},{2,1},{5,6},{6,5},{9,10},{10,9},{13,14},{14,13},{17,18},{18,... | collective-permute-start | bytes 3145736 | tf_op jit(solution)/shard_map/ppermute | solution.py:800
  242.9 51.4 %collective-permute-start.24 = (bf16[1024,512]{1,0:T(8,128)(2,1)}, bf16[1024,512]{1,0:T(8,128)(2,1)}, u32[]{:S(2)}, u32[]{:S(2)}) collective-permute-start(bf16[1024,512]{1,0:T(8,128)(2,1)} %get-tuple-element.164), channel_id=1, source_target_pairs={{0,1},{3,2},{4,5},{7,6},{8,9},{11,10},{12,13},{15,14},{16,17},{19,... | collective-permute-start | bytes 3145736 | tf_op jit(solution)/shard_map/ppermute | solution.py:790
  259.8 38.1 %collective-permute-start.25 = (bf16[1024,512]{1,0:T(8,128)(2,1)}, bf16[1024,512]{1,0:T(8,128)(2,1)}, u32[]{:S(2)}, u32[]{:S(2)}) collective-permute-start(bf16[1024,512]{1,0:T(8,128)(2,1)} %add_convert_fusion.14), channel_id=1, source_target_pairs={{1,2},{2,1},{5,6},{6,5},{9,10},{10,9},{13,14},{14,13},{17,18},{18,... | collective-permute-start | bytes 3145736 | tf_op jit(solution)/shard_map/ppermute | solution.py:800
  276.2 46.2 %collective-permute-start.27 = (bf16[1024,512]{1,0:T(8,128)(2,1)}, bf16[1024,512]{1,0:T(8,128)(2,1)}, u32[]{:S(2)}, u32[]{:S(2)}) collective-permute-start(bf16[1024,512]{1,0:T(8,128)(2,1)} %fusion.refs_0_), channel_id=1, source_target_pairs={{0,1},{3,2},{1,0},{2,3},{4,5},{7,6},{5,4},{6,7},{8,9},{11,10},{9,8... | collective-permute-start | bytes 3145736 | tf_op jit(solution)/shard_map/ppermute | solution.py:790
  276.2 28.5 %collective-permute-start.26 = (bf16[512,2048]{1,0:T(8,128)(2,1)}, bf16[512,2048]{1,0:T(8,128)(2,1)}, u32[]{:S(2)}, u32[]{:S(2)}) collective-permute-start(bf16[512,2048]{1,0:T(8,128)(2,1)} %get-tuple-element.167), channel_id=1, source_target_pairs={{0,16},{4,20},{8,12},{12,8},{16,0},{20,4},{24,28},{28,24},{1,17},{... | collective-permute-start | bytes 6291464 | tf_op jit(solution)/shard_map/ppermute | solution.py:862
  296.2 30.6 %collective-permute-start.29 = (bf16[1024,512]{1,0:T(8,128)(2,1)S(1)}, bf16[1024,512]{1,0:T(8,128)(2,1)}, u32[]{:S(2)}, u32[]{:S(2)}) collective-permute-start(bf16[1024,512]{1,0:T(8,128)(2,1)S(1)} %add_convert_fusion.12), channel_id=1, source_target_pairs={{1,2},{2,1},{5,6},{6,5},{9,10},{10,9},{13,14},{14,13},{17,18},{18,... | collective-permute-start | bytes 3145736 | tf_op jit(solution)/shard_map/ppermute | solution.py:800
  300.8 54.3 %collective-permute-start.30 = (bf16[1024,512]{1,0:T(8,128)(2,1)}, bf16[1024,512]{1,0:T(8,128)(2,1)}, u32[]{:S(2)}, u32[]{:S(2)}) collective-permute-start(bf16[1024,512]{1,0:T(8,128)(2,1)} %fusion.1.refs_4_), channel_id=1, source_target_pairs={{0,1},{3,2},{1,0},{2,3},{4,5},{7,6},{5,4},{6,7},{8,9},{11,10},{9,8... | collective-permute-start | bytes 3145736 | tf_op jit(solution)/shard_map/ppermute | solution.py:790
  309.1 20.4 %collective-permute-start.28 = (bf16[256,2048]{1,0:T(8,128)(2,1)}, bf16[256,2048]{1,0:T(8,128)(2,1)S(1)}, u32[]{:S(2)}, u32[]{:S(2)}) collective-permute-start(bf16[256,2048]{1,0:T(8,128)(2,1)} %get-tuple-element.171), channel_id=1, source_target_pairs={{0,4},{4,0},{8,24},{12,28},{16,20},{20,16},{24,8},{28,12},{1,5},{5... | collective-permute-start | bytes 3145736 | tf_op jit(solution)/shard_map/ppermute | solution.py:862
  325.0 32.7 %collective-permute-start.31 = (bf16[1024,512]{1,0:T(8,128)(2,1)}, bf16[1024,512]{1,0:T(8,128)(2,1)}, u32[]{:S(2)}, u32[]{:S(2)}) collective-permute-start(bf16[1024,512]{1,0:T(8,128)(2,1)} %add_convert_fusion.10), channel_id=1, source_target_pairs={{1,2},{2,1},{5,6},{6,5},{9,10},{10,9},{13,14},{14,13},{17,18},{18,... | collective-permute-start | bytes 3145736 | tf_op jit(solution)/shard_map/ppermute | solution.py:800
  338.7 21.9 %collective-permute-start.32 = (bf16[1024,2048]{1,0:T(8,128)(2,1)}, bf16[1024,2048]{1,0:T(8,128)(2,1)}, u32[]{:S(2)}, u32[]{:S(2)}) collective-permute-start(bf16[1024,2048]{1,0:T(8,128)(2,1)} %wgrad.9), channel_id=1, source_target_pairs={{0,8},{8,0},{16,24},{24,16},{1,9},{9,1},{17,25},{25,17},{2,10},{10... | collective-permute-start | bytes 12582920 | tf_op jit(solution)/shard_map/ppermute | solution.py:822
  338.7 16.3 %copy-start.11 = (bf16[1024,512]{1,0:T(8,128)(2,1)S(1)}, bf16[1024,512]{1,0:T(8,128)(2,1)}, u32[]{:S(2)}) copy-start(bf16[1024,512]{1,0:T(8,128)(2,1)} %get-tuple-element.178) | copy-start | bytes 3145732
  370.8 33.9 %collective-permute-start.35 = (bf16[512,2048]{1,0:T(8,128)(2,1)}, bf16[512,2048]{1,0:T(8,128)(2,1)}, u32[]{:S(2)}, u32[]{:S(2)}) collective-permute-start(bf16[512,2048]{1,0:T(8,128)(2,1)} %get-tuple-element.187), channel_id=1, source_target_pairs={{0,16},{4,20},{8,12},{12,8},{16,0},{20,4},{24,28},{28,24},{1,17},{... | collective-permute-start | bytes 6291464 | tf_op jit(solution)/shard_map/ppermute | solution.py:862
  372.2 26.1 %collective-permute-start.33 = (bf16[1024,512]{1,0:T(8,128)(2,1)S(1)}, bf16[1024,512]{1,0:T(8,128)(2,1)}, u32[]{:S(2)}, u32[]{:S(2)}) collective-permute-start(bf16[1024,512]{1,0:T(8,128)(2,1)S(1)} %copy-done.8), channel_id=1, source_target_pairs={{0,1},{3,2},{1,0},{2,3},{4,5},{7,6},{5,4},{6,7},{8,9},{11,10},{9,8... | collective-permute-start | bytes 3145736 | tf_op jit(solution)/shard_map/ppermute | solution.py:790
  374.0 28.7 %collective-permute-start.34 = (bf16[1024,512]{1,0:T(8,128)(2,1)}, bf16[1024,512]{1,0:T(8,128)(2,1)}, u32[]{:S(2)}, u32[]{:S(2)}) collective-permute-start(bf16[1024,512]{1,0:T(8,128)(2,1)} %add_convert_fusion.8), channel_id=1, source_target_pairs={{1,2},{2,1},{5,6},{6,5},{9,10},{10,9},{13,14},{14,13},{17,18},{18,... | collective-permute-start | bytes 3145736 | tf_op jit(solution)/shard_map/ppermute | solution.py:800
  375.6 43.6 %collective-permute-start.36 = (bf16[1024,512]{1,0:T(8,128)(2,1)}, bf16[1024,512]{1,0:T(8,128)(2,1)}, u32[]{:S(2)}, u32[]{:S(2)}) collective-permute-start(bf16[1024,512]{1,0:T(8,128)(2,1)} %fusion.3.refs_6_), channel_id=1, source_target_pairs={{0,1},{3,2},{1,0},{2,3},{4,5},{7,6},{5,4},{6,7},{8,9},{11,10},{9,8... | collective-permute-start | bytes 3145736 | tf_op jit(solution)/shard_map/ppermute | solution.py:790
  377.7 20.6 %copy-start.7 = (bf16[1024,512]{1,0:T(8,128)(2,1)S(1)}, bf16[1024,512]{1,0:T(8,128)(2,1)}, u32[]{:S(2)}) copy-start(bf16[1024,512]{1,0:T(8,128)(2,1)} %get-tuple-element.183) | copy-start | bytes 3145732
  382.1 20.6 %copy-start.3 = (bf16[1024,512]{1,0:T(8,128)(2,1)S(1)}, bf16[1024,512]{1,0:T(8,128)(2,1)}, u32[]{:S(2)}) copy-start(bf16[1024,512]{1,0:T(8,128)(2,1)} %get-tuple-element.201) | copy-start | bytes 3145732
  400.8 21.0 %collective-permute-start.37 = (bf16[1024,512]{1,0:T(8,128)(2,1)}, bf16[1024,512]{1,0:T(8,128)(2,1)}, u32[]{:S(2)}, u32[]{:S(2)}) collective-permute-start(bf16[1024,512]{1,0:T(8,128)(2,1)} %add_convert_fusion.6), channel_id=1, source_target_pairs={{1,2},{2,1},{5,6},{6,5},{9,10},{10,9},{13,14},{14,13},{17,18},{18,... | collective-permute-start | bytes 3145736 | tf_op jit(solution)/shard_map/ppermute | solution.py:800
  404.6 21.3 %copy-start = (bf16[1024,512]{1,0:T(8,128)(2,1)}, bf16[1024,512]{1,0:T(8,128)(2,1)S(1)}, u32[]{:S(2)}) copy-start(bf16[1024,512]{1,0:T(8,128)(2,1)S(1)} %fusion.4.refs_0_) | copy-start | bytes 3145732
  423.6 35.6 %copy-start.1 = (bf16[1024,512]{1,0:T(8,128)(2,1)}, bf16[1024,512]{1,0:T(8,128)(2,1)S(1)}, u32[]{:S(2)}) copy-start(bf16[1024,512]{1,0:T(8,128)(2,1)S(1)} %add_convert_fusion.3.refs_2_) | copy-start | bytes 3145732
  423.6 21.8 %collective-permute-start.39 = (bf16[1024,2048]{1,0:T(8,128)(2,1)}, bf16[1024,2048]{1,0:T(8,128)(2,1)}, u32[]{:S(2)}, u32[]{:S(2)}) collective-permute-start(bf16[1024,2048]{1,0:T(8,128)(2,1)} %wgrad.8), channel_id=1, source_target_pairs={{0,8},{8,0},{16,24},{24,16},{1,9},{9,1},{17,25},{25,17},{2,10},{10... | collective-permute-start | bytes 12582920 | tf_op jit(solution)/shard_map/ppermute | solution.py:822
  423.7 17.7 %collective-permute-start.38 = (bf16[256,2048]{1,0:T(8,128)(2,1)}, bf16[256,2048]{1,0:T(8,128)(2,1)}, u32[]{:S(2)}, u32[]{:S(2)}) collective-permute-start(bf16[256,2048]{1,0:T(8,128)(2,1)} %get-tuple-element.197), channel_id=1, source_target_pairs={{0,4},{4,0},{8,24},{12,28},{16,20},{20,16},{24,8},{28,12},{1,5},{5... | collective-permute-start | bytes 3145736 | tf_op jit(solution)/shard_map/ppermute | solution.py:862
  426.0 34.5 %collective-permute-start.40 = (bf16[1024,512]{1,0:T(8,128)(2,1)S(1)}, bf16[1024,512]{1,0:T(8,128)(2,1)S(1)}, u32[]{:S(2)}, u32[]{:S(2)}) collective-permute-start(bf16[1024,512]{1,0:T(8,128)(2,1)S(1)} %fusion.4.refs_0_), channel_id=1, source_target_pairs={{0,1},{3,2},{1,0},{2,3},{4,5},{7,6},{5,4},{6,7},{8,9},{11,10},{9,8... | collective-permute-start | bytes 3145736 | tf_op jit(solution)/shard_map/ppermute | solution.py:790
  456.3 32.3 %collective-permute-start.45 = (bf16[512,2048]{1,0:T(8,128)(2,1)}, bf16[512,2048]{1,0:T(8,128)(2,1)}, u32[]{:S(2)}, u32[]{:S(2)}) collective-permute-start(bf16[512,2048]{1,0:T(8,128)(2,1)} %get-tuple-element.207), channel_id=1, source_target_pairs={{0,16},{4,20},{8,12},{12,8},{16,0},{20,4},{24,28},{28,24},{1,17},{... | collective-permute-start | bytes 6291464 | tf_op jit(solution)/shard_map/ppermute | solution.py:862
  457.5 7.6 %collective-permute-start.41 = (bf16[1024,512]{1,0:T(8,128)(2,1)}, bf16[1024,512]{1,0:T(8,128)(2,1)}, u32[]{:S(2)}, u32[]{:S(2)}) collective-permute-start(bf16[1024,512]{1,0:T(8,128)(2,1)} %add_convert_fusion.4), channel_id=1, source_target_pairs={{1,2},{2,1},{5,6},{6,5},{9,10},{10,9},{13,14},{14,13},{17,18},{18,... | collective-permute-start | bytes 3145736 | tf_op jit(solution)/shard_map/ppermute | solution.py:800
  459.2 29.4 %collective-permute-start.46 = (bf16[1024,512]{1,0:T(8,128)(2,1)S(1)}, bf16[1024,512]{1,0:T(8,128)(2,1)}, u32[]{:S(2)}, u32[]{:S(2)}) collective-permute-start(bf16[1024,512]{1,0:T(8,128)(2,1)S(1)} %add_convert_fusion.3.refs_2_), channel_id=1, source_target_pairs={{1,0},{2,3},{5,4},{6,7},{9,8},{10,11},{13,12},{14,15},{17,16},{18,... | collective-permute-start | bytes 3145736 | tf_op jit(solution)/shard_map/ppermute | solution.py:790
  463.4 29.9 %collective-permute-start.49 = (bf16[1024,512]{1,0:T(8,128)(2,1)}, bf16[1024,512]{1,0:T(8,128)(2,1)}, u32[]{:S(2)}, u32[]{:S(2)}) collective-permute-start(bf16[1024,512]{1,0:T(8,128)(2,1)} %add_convert_fusion.2), channel_id=1, source_target_pairs={{1,2},{2,1},{5,6},{6,5},{9,10},{10,9},{13,14},{14,13},{17,18},{18,... | collective-permute-start | bytes 3145736 | tf_op jit(solution)/shard_map/ppermute | solution.py:800
  467.0 26.0 %copy-start.9 = (bf16[1024,512]{1,0:T(8,128)(2,1)}, bf16[1024,512]{1,0:T(8,128)(2,1)S(1)}, u32[]{:S(2)}) copy-start(bf16[1024,512]{1,0:T(8,128)(2,1)S(1)} %add_convert_fusion.1.refs_4_) | copy-start | bytes 3145732
  467.0 1.3 collective-permute-start.42
  468.3 15.5 %collective-permute-start.43 = (f32[13824]{0:T(1024)S(1)}, f32[13824]{0:T(1024)S(1)}, u32[]{:S(2)}, u32[]{:S(2)}) collective-permute-start(f32[13824]{0:T(1024)S(1)} %add.118), channel_id=1, source_target_pairs={{0,16},{16,0},{8,24},{24,8},{1,17},{17,1},{9,25},{25,9},{2,18},{18... | collective-permute-start | bytes 165896 | tf_op jit(solution)/shard_map/ppermute | solution.py:819
  483.8 4.2 collective-permute-start.44
  484.0 40.2 %collective-permute-start.48 = (bf16[1024,512]{1,0:T(8,128)(2,1)S(1)}, bf16[1024,512]{1,0:T(8,128)(2,1)S(1)}, u32[]{:S(2)}, u32[]{:S(2)}) collective-permute-start(bf16[1024,512]{1,0:T(8,128)(2,1)S(1)} %add_convert_fusion.1.refs_4_), channel_id=1, source_target_pairs={{1,0},{2,3},{5,4},{6,7},{9,8},{10,11},{13,12},{14,15},{17,16},{18,... | collective-permute-start | bytes 3145736 | tf_op jit(solution)/shard_map/ppermute | solution.py:790
  492.9 31.3 %collective-permute-start.47 = (bf16[256,2048]{1,0:T(8,128)(2,1)}, bf16[256,2048]{1,0:T(8,128)(2,1)}, u32[]{:S(2)}, u32[]{:S(2)}) collective-permute-start(bf16[256,2048]{1,0:T(8,128)(2,1)} %get-tuple-element.212), channel_id=1, source_target_pairs={{0,4},{4,0},{8,24},{12,28},{16,20},{20,16},{24,8},{28,12},{1,5},{5... | collective-permute-start | bytes 3145736 | tf_op jit(solution)/shard_map/ppermute | solution.py:862
  495.1 56.1 %copy-start.14 = (bf16[1024,512]{1,0:T(8,128)(2,1)}, bf16[1024,512]{1,0:T(8,128)(2,1)S(1)}, u32[]{:S(2)}) copy-start(bf16[1024,512]{1,0:T(8,128)(2,1)S(1)} %add_convert_fusion.refs_6_) | copy-start | bytes 3145732
  495.1 56.1 %collective-permute-start.52 = (bf16[1024,512]{1,0:T(8,128)(2,1)S(1)}, bf16[1024,512]{1,0:T(8,128)(2,1)}, u32[]{:S(2)}, u32[]{:S(2)}) collective-permute-start(bf16[1024,512]{1,0:T(8,128)(2,1)S(1)} %add_convert_fusion.refs_6_), channel_id=1, source_target_pairs={{1,0},{2,3},{5,4},{6,7},{9,8},{10,11},{13,12},{14,15},{17,16},{18,... | collective-permute-start | bytes 3145736 | tf_op jit(solution)/shard_map/ppermute | solution.py:790
  496.4 49.4 %collective-permute-start.50 = (f32[8192]{0:T(1024)S(1)}, f32[8192]{0:T(1024)S(1)}, u32[]{:S(2)}, u32[]{:S(2)}) collective-permute-start(f32[8192]{0:T(1024)S(1)} %slice.40), channel_id=1, source_target_pairs={{0,1},{1,0},{2,3},{3,2},{4,5},{5,4},{6,7},{7,6},{8,9},{9,8},{10,11... | collective-permute-start | bytes 98312 | tf_op jit(solution)/shard_map/ppermute | solution.py:895
  524.2 27.0 %copy-start.17 = (bf16[1024,512]{1,0:T(8,128)(2,1)}, bf16[1024,512]{1,0:T(8,128)(2,1)S(1)}, u32[]{:S(2)}) copy-start(bf16[1024,512]{1,0:T(8,128)(2,1)S(1)} %collective-permute-done.48.refs_5_) | copy-start | bytes 3145732
  545.8 4.8 collective-permute-start.51
  546.4 16.8 %copy-start.25 = (f32[2048]{0:T(1024)}, f32[2048]{0:T(1024)S(1)}, u32[]{:S(2)}) copy-start(f32[2048]{0:T(1024)S(1)} %get-tuple-element.260) | copy-start | bytes 24580
  (28 other events, 186.1 us)

commit v3 on v2

--- a/solution.py
+++ b/solution.py
@@ -24,6 +24,7 @@
 
 def cost(flops, nbytes, trans=0):
     k = COST_SCALE
+    flops = max(flops, 300 * nbytes)
     return pl.CostEstimate(flops=int(k * flops), bytes_accessed=int(k * nbytes), transcendentals=int(k * trans))
 
 
@@ -64,7 +65,7 @@
     return (pos < meta[3 + NBLK + slot]).astype(F32)
 
 
-def norm_kernel(local_len, meta, x_ref, g_ref, ga, sa, gf, sf, h1_ref, h2_ref, g_out, st_ref, gs_ref):
+def norm_kernel(local_len, meta, x_ref, g_ref, ga, sa, h1_ref, g_out, st_ref, gs_ref):
     rows = x_ref.shape[0]
     i = pl.program_id(0)
     x = x_ref[...].astype(F32)
@@ -79,7 +80,6 @@
         dst = slice(r * 256, (r + 1) * 256)
         xh = (x_ref[:, src].astype(F32) - mean) * inv
         h1_ref[:, dst] = (xh * ga[:, src] + sa[:, src]).astype(BF)
-        h2_ref[:, dst] = (xh * gf[:, src] + sf[:, src]).astype(BF)
         gm = g_ref[:, src].astype(F32) * mask
         g_out[:, dst] = gm.astype(BF)
         part = jnp.sum(gm, axis=0, keepdims=True)
@@ -93,7 +93,34 @@
             gs_ref[:, src] = gs_ref[:, src] + part
 
 
-def norm_call(meta, x2, g2, ga, sa, gf, sf, local_len):
+def second_norm_kernel(meta, x_ref, st_ref, gf, sf, h2_ref):
+    for r in range(NBLK):
+        src = block_cols(meta[1 + r] * 256)
+        xh = (x_ref[:, src].astype(F32) - st_ref[:, 0:1]) * st_ref[:, 1:2]
+        h2_ref[:, r * 256 : (r + 1) * 256] = (xh * gf[:, src] + sf[:, src]).astype(BF)
+
+
+def second_norm_call(meta, x2, st, gf, sf):
+    m, d = x2.shape
+    rows = 256
+    row_spec = pl.BlockSpec((rows, d), lambda i, mt: (i, 0))
+    vec = pl.BlockSpec((1, d), lambda i, mt: (0, 0))
+    return pl.pallas_call(
+        second_norm_kernel,
+        name="norm2",
+        grid_spec=pltpu.PrefetchScalarGridSpec(
+            num_scalar_prefetch=1,
+            grid=(m // rows,),
+            in_specs=[row_spec, pl.BlockSpec((rows, 128), lambda i, mt: (i, 0)), vec, vec],
+            out_specs=row_spec,
+        ),
+        out_shape=jax.ShapeDtypeStruct((m, d), BF),
+        compiler_params=params(1),
+        cost_estimate=cost(5 * m * d, 4 * m * d),
+    )(meta, x2, st, gf, sf)
+
+
+def norm_call(meta, x2, g2, ga, sa, local_len):
     m, d = x2.shape
     rows = 256
     row_spec = pl.BlockSpec((rows, d), lambda i, mt: (i, 0))
@@ -104,14 +131,14 @@
         grid_spec=pltpu.PrefetchScalarGridSpec(
             num_scalar_prefetch=1,
             grid=(m // rows,),
-            in_specs=[row_spec, row_spec, vec, vec, vec, vec],
-            out_specs=[row_spec, row_spec, row_spec, pl.BlockSpec((rows, 128), lambda i, mt: (i, 0)), vec],
+            in_specs=[row_spec, row_spec, vec, vec],
+            out_specs=[row_spec, row_spec, pl.BlockSpec((rows, 128), lambda i, mt: (i, 0)), vec],
         ),
-        out_shape=[jax.ShapeDtypeStruct((m, d), BF)] * 3
+        out_shape=[jax.ShapeDtypeStruct((m, d), BF)] * 2
         + [jax.ShapeDtypeStruct((m, 128), F32), jax.ShapeDtypeStruct((1, d), F32)],
         compiler_params=params(1),
         cost_estimate=cost(20 * m * d, 10 * m * d),
-    )(meta, x2, g2, ga, sa, gf, sf)
+    )(meta, x2, g2, ga, sa)
 
 
 def rotate_tile(y, cosf, s1, s2, sign):
@@ -681,10 +708,10 @@
     return jnp.where(meta[1 + NBLK] > 0, here[:, cols].astype(F32), sent[:, cols].astype(F32))
 
 
-def block_out_kernel(local_len, meta, x_ref, b_ref, *refs):
+def block_out_kernel(local_len, first, meta, x_ref, b_ref, *refs):
     y_ref = refs[-1]
     rows = x_ref.shape[0]
-    mask = row_valid(meta, pl.program_id(0) * rows, rows, local_len)
+    mask = row_valid(meta, (first + pl.program_id(0)) * rows, rows, local_len)
     for r in range(NBLK):
         col = block_cols(meta[1 + r] * 256)
         k = r % 2 * 256
@@ -692,10 +719,10 @@
         y_ref[:, col] = (mask * (x_ref[:, col].astype(F32) + s + b_ref[:, col])).astype(BF)
 
 
-def input_grad_kernel(local_len, meta, x_ref, g_ref, st_ref, *refs):
+def input_grad_kernel(local_len, first, meta, x_ref, g_ref, st_ref, *refs):
     y_ref = refs[-1]
     rows = x_ref.shape[0]
-    mask = row_valid(meta, pl.program_id(0) * rows, rows, local_len)
+    mask = row_valid(meta, (first + pl.program_id(0)) * rows, rows, local_len)
     mean = st_ref[:, 0:1]
     inv = st_ref[:, 1:2]
     one = jnp.zeros((rows, 1), F32)
@@ -717,27 +744,35 @@
         y_ref[:, col] = (g_ref[:, col].astype(F32) * mask + inv * (dn - one - xh * two)).astype(BF)
 
 
-def rows_call(meta, *ops, body, name, specs):
+def rows_call(meta, *ops, body, name, specs, steps=None, into=None):
     rows = 256
     m, d = ops[0].shape
+    first, last = steps or (0, m // rows)
     made = {
-        "row": pl.BlockSpec((rows, d), lambda i, mt: (i, 0)),
-        "part": pl.BlockSpec((rows, d // 4), lambda i, mt: (i, 0)),
-        "stat": pl.BlockSpec((rows, 128), lambda i, mt: (i, 0)),
+        "row": pl.BlockSpec((rows, d), lambda i, mt: (first + i, 0)),
+        "part": pl.BlockSpec((rows, d // 4), lambda i, mt: (first + i, 0)),
+        "stat": pl.BlockSpec((rows, 128), lambda i, mt: (first + i, 0)),
         "vec": pl.BlockSpec((1, d), lambda i, mt: (0, 0)),
     }
-    return pl.pallas_call(
-        body,
+    in_specs = [made[s] for s in specs]
+    aliases = {}
+    if into is not None:
+        aliases = {1 + len(ops): 0}
+        in_specs.append(pl.BlockSpec(memory_space=pl.ANY))
+        ops += (into,)
+    return pl.pallas_call(
+        functools.partial(body, first),
         name=name,
         grid_spec=pltpu.PrefetchScalarGridSpec(
             num_scalar_prefetch=1,
-            grid=(m // rows,),
-            in_specs=[made[s] for s in specs],
+            grid=(last - first,),
+            in_specs=in_specs,
             out_specs=made["row"],
         ),
         out_shape=jax.ShapeDtypeStruct((m, d), BF),
-        compiler_params=params(1),
-        cost_estimate=cost(10 * m * d, 8 * m * d),
+        input_output_aliases=aliases,
+        compiler_params=params(1),
+        cost_estimate=cost(10 * (last - first) * rows * d, 8 * (last - first) * rows * d),
     )(meta, *ops)
 
 
@@ -802,7 +837,7 @@
 
 class PlainPipe:
     def __init__(self, run, middle, count):
-        self.here, self.sent = [], []
+        self.here, self.sent, self.sums = [], [], []
 
     def send(self, part=None):
         if part is not None:
@@ -850,8 +885,8 @@
         v = run(pack_call, own, hop[1])
         return v, self.core(v)
 
-    def pieces(self, near, hop, diag):
-        return near[0], hop[0], diag, near[1], self.core(hop[0]), self.core(diag)
+    def pieces(self, near, hop, diag, earlier=()):
+        return near[0], hop[0], diag, near[1], self.core(after(hop[0], *earlier[:1])), self.core(after(diag, *earlier))
 
     def turn(self, v, first):
         pairs = []
@@ -919,7 +954,7 @@
     def near(self, run, own, hop):
         return hop[:512], hop[1024:1536]
 
-    def pieces(self, near, hop, diag):
+    def pieces(self, near, hop, diag, earlier=()):
         return near[0], hop[512:768], hop[768:1024], near[1], hop[1536:1792], hop[1792:]
 
     def scatter_cross(self, theirs):
@@ -998,7 +1033,7 @@
     own3 = w_out.T.astype(BF)
     run.last = (own1, own2, own3)
     hop2 = comm.first_hop(own2, hop1[0])
-    h1, h2, g, stats, g_sum = run(norm_call, meta, x2, og2, ga, sa, gf, sf, local_len)
+    h1, g, stats, g_sum = run(norm_call, meta, x2, og2, ga, sa, local_len)
     diag1 = comm.second_hop(hop1)
     near1 = comm.near(run, own1, hop1)
     g1 = comm.pieces(near1, hop1, diag1)
@@ -1008,12 +1043,13 @@
     diag2 = comm.second_hop(hop2, (kv,))
     hop3 = comm.first_hop(own3, diag2)
     q, dob = run(qd_call, h1, g, g1, bq, tabs, nheads)
+    g2 = comm.pieces(near2, hop2, diag2, (kv, q))
+    diag3 = comm.second_hop(hop3)
+    h2 = run(second_norm_call, meta, x2, stats, gf, sf)
+    gb, dg = run(hidden_call, h2, g2, b_in.reshape(1, -1))
     near3 = comm.near(run, own3, hop3)
-    g2 = comm.pieces(near2, hop2, diag2)
-    diag3 = comm.second_hop(hop3)
     ob, dq, dkv, dpv = run(attn_call, meta, q, kv, pv, dob, tabs, nheads)
     dkv, rv = comm.give_back(dpv, dkv, slots)
-    gb, dg = run(hidden_call, after(h2, *comm.waited(hop3)), g2, b_in.reshape(1, -1))
     g3 = comm.pieces(near3, hop3, diag3)
 
     pipe = comm.pipe(run, meta[1 + NBLK], 8)
@@ -1021,12 +1057,12 @@
     out0, out2 = run(out_call, ob, gb, (g1[0], g1[3]), (g3[0], g3[3]))
     pipe.send(out0)
     pipe.send(out2)
-    cross3 = comm.scatter_cross(run(wgrad_call, meta, g, gb, half=1))
     far = (1, 2, 4, 5)
     out1, out3 = run(out_call, ob, gb, [g1[k] for k in far], [g3[k] for k in far])
+    cross3 = comm.scatter_cross(run(wgrad_call, meta, g, gb, half=1))
     du, bin_sum = run(dhid_call, g, g3, dg)
-    pipe.send(after(out1, du))
     pipe.cross()
+    pipe.send(after(out1, *pipe.sums))
     state3 = comm.scatter_own(run, meta, (g, gb), cross3)
     pipe.cross()
     dqkv, bqkv_sum = run(join_call, dq, dkv, rv, tabs, nheads)
@@ -1044,10 +1080,15 @@
     pipe.cross()
     pipe.send(dn2)
     state2 = comm.scatter_own(run, meta, (h2, du), cross2)
-    (grad_out,) = comm.scatter_last(run, ((ff, True),), state3)
     pipe.cross()
     pipe.send(dn3)
+    small = jnp.concatenate([gain_sums.reshape(-1), g_sum.reshape(-1), bqkv_sum.reshape(-1), bin_sum.reshape(-1)])
+    add = comm.small_sum(run, small, 0)
+    (grad_out,) = comm.scatter_last(run, ((ff, True),), state3)
+    small = add()
+    add = comm.small_sum(run, small, 1)
     state2 = comm.scatter_half(run, state2)
+    small = add()
     pipe.cross()
     pipe.send()
     cross1 = comm.scatter_cross(after(theirs1, pipe.here[-1]))
@@ -1055,18 +1096,18 @@
     def sums_of(order):
         return [v for c in order for v in (pipe.here[c], pipe.sent[c])]
 
-    block_output = run(
-        rows_call, meta, x2, (b_proj + b_out).reshape(1, d), *sums_of((0, 2, 1, 3)),
-        body=functools.partial(block_out_kernel, local_len), name="bout", specs=("row", "vec") + ("part",) * 8,
-    ).reshape(slots, local_len, d)
+    out_ops = (meta, x2, (b_proj + b_out).reshape(1, d), *sums_of((0, 2, 1, 3)))
+    out_half = functools.partial(
+        rows_call, body=functools.partial(block_out_kernel, local_len), name="bout", specs=("row", "vec") + ("part",) * 8
+    )
+    block_output = run(out_half, *out_ops, steps=(0, 2))
     (grad_in,) = comm.scatter_last(run, ((ff, False),), state2)
+    add = comm.small_sum(run, after(small, grad_in), 2)
     state1 = comm.scatter_own(run, meta, (h1, dqkv, g, ob), cross1)
+    small = add()
     pipe.cross()
     pipe.send()
-    small = jnp.concatenate([gain_sums.reshape(-1), g_sum.reshape(-1), bqkv_sum.reshape(-1), bin_sum.reshape(-1)])
-    small = after(small, pipe.here[-1])
-    for step in range(3):
-        small = comm.small_sum(run, small, step)()
+    block_output = run(out_half, *out_ops, steps=(2, 4), into=block_output).reshape(slots, local_len, d)
     gains = small[: 4 * d]
     group = small[4 * d :]
     state1 = comm.scatter_half(run, after(state1, pipe.sent[5]))
@@ -1077,11 +1118,11 @@
     )
     gains = add()
     add = comm.small_sum(run, gains, 4)
-    gains = add().reshape(4, d)
     input_grad = run(
         rows_call, meta, x2, og2, stats, *sums_of(range(4, 8)),
         body=functools.partial(input_grad_kernel, local_len), name="igrad", specs=("row", "row", "stat") + ("part",) * 8,
     ).reshape(slots, local_len, d)
+    gains = add().reshape(4, d)
     bias_grad = group[:d]
     return (
         block_output,

time: 571 us -> 535 us (0.937)
  waiting for transfers between devices: 158 us -> 106 us
  starting transfers between devices: 94.8 us -> 102 us
  Pallas kernels: 256 us -> 262 us
    ppermute x6, waiting for transfers between devices: 0.02 us -> 36.5 us  [turn(): return lax.ppermute(v, ('dp', 'ctx'), pairs)]
    ppermute x11, waiting for transfers between devices: 35.5 us -> 14.3 us  [send(): got = lax.ppermute(v, 'tensor', pairs)]
    ppermute x1, waiting for transfers between devices: 18.5 us -> 0.01 us  [previous(): return lax.ppermute(kv, 'ctx', [(0, 1)])]
    ppermute x1, waiting for transfers between devices: 16.9 us -> 0.01 us  [small_sum(): got = lax.ppermute(v, 'tensor', [(0, 1), (1, 0), (2, 3), (3, 2)])]
    ppermute x7, waiting for transfers between devices: 67.5 us -> 52.3 us  [x(): return lax.ppermute(v, 'dp', [(0, 2), (2, 0), (1, 3), (3, 1)])]
    ppermute x1, starting transfers between devices: 0.01 us -> 11.7 us  [small_sum(): got = lax.ppermute(v, 'tensor', [(0, 2), (2, 0), (1, 3), (3, 1)])]
    pallas_call x2 -> x4, Pallas kernels: 20.8 us -> 29.1 us  [the longest x3 22.5 us: rows_call(): pl.pallas_call(functools.partial(body, first), name=name, grid_spec=pltpu...]
    ppermute x1, waiting for transfers between devices: 7.23 us -> 0.01 us  [give_back(): return (dkv, lax.ppermute(dpv, 'ctx', [(1, 0)]))]
  transfers between devices with their start and end apart: 53 -> 53, of which waited for: 16 -> 12; matrix products, arithmetic and copies ran while one was open for 8% -> 9% of each run, Pallas kernels for 41% -> 50%
where the time goes in v3:
time: 535 us; the launch traced here: 528 us
  Pallas kernels  262 us (49%)
  waiting for transfers between devices  106 us (20%)
  starting transfers between devices  102 us (19%)
  other arithmetic  42.2 us (8%)
  local copies, waits for them, and re-layouts  14.1 us (3%)
    pallas_call x6, Pallas kernels, wgrad_call(): pl.pallas_call(functools.partial(wgrad_kernel, counts, add is not None, s...  59.5 us
    ppermute x7, waiting for transfers between devices, x(): return lax.ppermute(v, 'dp', [(0, 2), (2, 0), (1, 3), (3, 1)])  52.3 us
    ppermute x6, waiting for transfers between devices, turn(): return lax.ppermute(v, ('dp', 'ctx'), pairs)  36.5 us
    ppermute x11, starting transfers between devices, send(): got = lax.ppermute(v, 'tensor', pairs)  34.3 us
    pallas_call x2, Pallas kernels, back_call(): pl.pallas_call(back_kernel, name='backn', grid_spec=pltpu.PrefetchScalarG...  32.4 us
    pallas_call x2, Pallas kernels, out_call(): pl.pallas_call(functools.partial(out_kernel, count), name='outp', grid=(4...  22.5 us
    pallas_call x3, Pallas kernels, rows_call(): pl.pallas_call(functools.partial(body, first), name=name, grid_spec=pltpu...  22.5 us
    convert_element_type x11, other arithmetic, add_bf(): return lax.optimization_barrier((a.astype(F32) + b.astype(F32)).astype(BF))  20.8 us
  transfers between devices with their start and end apart: 53, of which 12 were waited for; matrix products, arithmetic and copies ran while one was open for 9% of the time, Pallas kernels for 50%

profile of v3, /device:TPU:0, one launch (start us, length us, event | category | flops | bytes accessed | tf_op | source)
XLA Modules:
  0.0 527.5 jit_solution(9457068509076354575)
XLA Ops:
  4.6 3.0 collective-permute-start
  10.7 2.6 copy.32
  15.4 10.5 %norm.1 = (bf16[1024,2048]{1,0:T(8,128)(2,1)}, bf16[1024,2048]{1,0:T(8,128)(2,1)}, f32[1024,128]{1,0:T(8,128)}, f32[1,2048]{1,0:T(1,128)}) custom-call(s32[13]{0:T(128)} %concatenate.10.meta, bf16[1024,2048]{1,0:T(8,128)(2,1)} %bitcast.30, bf16[1024,2048]{1,0:T(8,128)(2,1)} %bitcast.37, f32[1,2048]{1,0:T(1,128)} %bitcast.42, f32[1,2048]{1,0:T(1,128)} %bitcast.39), custom_call_target="tpu_custom_call" | custom-call | flops 125829120000 | bytes 419430400 | tf_op jit(solution)/shard_map/norm/pallas_call | solution.py:128
  27.2 1.9 fusion.5
  29.1 2.8 collective-permute-done.refs_1_
  33.9 3.8 pack.3.w0.refs_0_.w10
  38.2 18.4 %collective-permute-done.3.w2.refs_1_.w12 = bf16[256,2048]{1,0:T(8,128)(2,1)} collective-permute-done((bf16[256,2048]{1,0:T(8,128)(2,1)}, bf16[256,2048]{1,0:T(8,128)(2,1)}, u32[]{:S(2)}, u32[]{:S(2)}) %collective-permute-start.3) | collective-permute-done | bytes 1048608 | tf_op jit(solution)/shard_map/ppermute | solution.py:854
  56.6 3.9 pack.4.w0.w20
  63.8 9.8 %kv.1.kv_ref = bf16[1024,1024]{1,0:T(8,128)(2,1)} custom-call(bf16[1024,2048]{1,0:T(8,128)(2,1)} %get-tuple-element.126.h1.refs_0_, bf16[512,2048]{1,0:T(8,128)(2,1)} %pack.3.w0.refs_0_.w10, bf16[256,2048]{1,0:T(8,128)(2,1)} %copy-done.26, bf16[256,2048]{1,0:T(8,128)(2,1)} %collective-permute-done.3.w2.refs_1_.w12, bf16[512,2048]{1,0:T(8,128)(2,1)} %copy-done.24, ...), custom_call_target="tpu_custom_call" | custom-call | flops 85899345920 | bytes 209715200 | tf_op jit(solution)/shard_map/kv/pallas_call | solution.py:184
  73.6 3.9 collective-permute-start.13
  77.5 8.8 %collective-permute-done.7.w1.w21 = bf16[256,2048]{1,0:T(8,128)(2,1)S(1)} collective-permute-done((bf16[256,2048]{1,0:T(8,128)(2,1)}, bf16[256,2048]{1,0:T(8,128)(2,1)S(1)}, u32[]{:S(2)}, u32[]{:S(2)}) %collective-permute-start.7) | collective-permute-done | bytes 1048608 | tf_op jit(solution)/shard_map/ppermute | solution.py:854
  87.8 10.8 %qd.1 = (bf16[1024,512]{1,0:T(8,128)(2,1)}, bf16[1024,512]{1,0:T(8,128)(2,1)}) custom-call(bf16[1024,2048]{1,0:T(8,128)(2,1)} %get-tuple-element.126.h1.refs_0_, bf16[1024,2048]{1,0:T(8,128)(2,1)} %get-tuple-element.148.g.refs_0_.refs_2_, bf16[512,2048]{1,0:T(8,128)(2,1)} %pack.3.w0.refs_0_.w10, bf16[256,2048]{1,0:T(8,128)(2,1)} %copy-done.26, ...), custom_call_target="tpu_custom_call" | custom-call | flops 88080384000 | bytes 293601280 | tf_op jit(solution)/shard_map/qd/pallas_call | solution.py:225
  98.6 12.3 %collective-permute-done.8.w2.w22 = bf16[256,2048]{1,0:T(8,128)(2,1)} collective-permute-done((bf16[256,2048]{1,0:T(8,128)(2,1)}, bf16[256,2048]{1,0:T(8,128)(2,1)}, u32[]{:S(2)}, u32[]{:S(2)}) %collective-permute-start.8) | collective-permute-done | bytes 1048608 | tf_op jit(solution)/shard_map/ppermute | solution.py:854
  110.9 6.7 %norm2.1.h2.refs_0_ = bf16[1024,2048]{1,0:T(8,128)(2,1)} custom-call(s32[13]{0:T(128)} %concatenate.10.meta, bf16[1024,2048]{1,0:T(8,128)(2,1)} %bitcast.31, f32[1024,128]{1,0:T(8,128)} %get-tuple-element.130.st_ref, f32[1,2048]{1,0:T(1,128)} %bitcast.45, f32[1,2048]{1,0:T(1,128)} %bitcast.40), custom_call_target="tpu_custom_call" | custom-call | flops 50331648000 | bytes 167772160 | tf_op jit(solution)/shard_map/norm2/pallas_call | solution.py:108
  120.4 16.4 %hidden.1 = (bf16[1024,2048]{1,0:T(8,128)(2,1)}, bf16[1024,2048]{1,0:T(8,128)(2,1)}) custom-call(bf16[1024,2048]{1,0:T(8,128)(2,1)} %norm2.1.h2.refs_0_, bf16[512,2048]{1,0:T(8,128)(2,1)} %pack.4.w0.w20, bf16[256,2048]{1,0:T(8,128)(2,1)} %copy-done.29, bf16[256,2048]{1,0:T(8,128)(2,1)} %collective-permute-done.8.w2.w22, ...), custom_call_target="tpu_custom_call" | custom-call | flops 171798691840 | bytes 419430400 | tf_op jit(solution)/shard_map/hidden/pallas_call | solution.py:414
  136.9 3.8 pack.5.refs_2_.w0
  140.9 2.5 collective-permute-done.15.refs_4_.w1
  145.0 12.4 %attn.1 = (bf16[1024,512]{1,0:T(8,128)(2,1)}, bf16[1024,512]{1,0:T(8,128)(2,1)}, f32[1024,1024]{1,0:T(8,128)}, bf16[1024,1024]{1,0:T(8,128)(2,1)}) custom-call(s32[13]{0:T(128)} %concatenate.10.meta, bf16[1024,512]{1,0:T(8,128)(2,1)} %get-tuple-element.128.q_ref, bf16[1024,1024]{1,0:T(8,128)(2,1)} %kv.1.kv_ref, ...), custom_call_target="tpu_custom_call" | custom-call | flops 128849018880 | bytes 209715200 | tf_op jit(solution)/shard_map/attn/pallas_call | solution.py:334
  158.7 9.7 %collective-permute-done.16.refs_5_.w2 = bf16[256,2048]{1,0:T(8,128)(2,1)S(1)} collective-permute-done((bf16[256,2048]{1,0:T(8,128)(2,1)}, bf16[256,2048]{1,0:T(8,128)(2,1)S(1)}, u32[]{:S(2)}, u32[]{:S(2)}) %collective-permute-start.16) | collective-permute-done | bytes 1048608 | tf_op jit(solution)/shard_map/ppermute | solution.py:854
  169.7 10.9 %outp.2 = (bf16[1024,512]{1,0:T(8,128)(2,1)}, bf16[1024,512]{1,0:T(8,128)(2,1)}) custom-call(bf16[1024,512]{1,0:T(8,128)(2,1)} %get-tuple-element.143.ob.refs_3_, bf16[1024,2048]{1,0:T(8,128)(2,1)} %get-tuple-element.136.gb.refs_1_, bf16[512,2048]{1,0:T(8,128)(2,1)} %pack.3.w0.refs_0_.w10, bf16[512,2048]{1,0:T(8,128)(2,1)} %copy-done.24, ...), custom_call_target="tpu_custom_call" | custom-call | flops 107374182400 | bytes 251658240 | tf_op jit(solution)/shard_map/outp/pallas_call | solution.py:480
  180.6 4.7 collective-permute-start.19
  185.3 11.6 %outp.3 = (bf16[1024,512]{1,0:T(8,128)(2,1)}, bf16[1024,512]{1,0:T(8,128)(2,1)}) custom-call(bf16[1024,512]{1,0:T(8,128)(2,1)} %get-tuple-element.143.ob.refs_3_, bf16[1024,2048]{1,0:T(8,128)(2,1)} %get-tuple-element.136.gb.refs_1_, bf16[256,2048]{1,0:T(8,128)(2,1)} %copy-done.26, bf16[256,2048]{1,0:T(8,128)(2,1)} %collective-permute-done.3.w2.refs_1_.w12, ...), custom_call_target="tpu_custom_call" | custom-call | flops 107374182400 | bytes 251658240 | tf_op jit(solution)/shard_map/outp/pallas_call | solution.py:480
  196.9 9.2 %wgrad.6 = bf16[1024,2048]{1,0:T(8,128)(2,1)} custom-call(s32[13]{0:T(128)} %concatenate.10.meta, bf16[1024,2048]{1,0:T(8,128)(2,1)} %get-tuple-element.148.g.refs_0_.refs_2_, bf16[1024,2048]{1,0:T(8,128)(2,1)} %get-tuple-element.136.gb.refs_1_), custom_call_target="tpu_custom_call" | custom-call | flops 88080384000 | bytes 293601280 | tf_op jit(solution)/shard_map/wgrad/pallas_call | solution.py:603
  206.4 15.2 %dhid.1 = (bf16[1024,2048]{1,0:T(8,128)(2,1)}, f32[1,2048]{1,0:T(1,128)}) custom-call(bf16[1024,2048]{1,0:T(8,128)(2,1)} %get-tuple-element.148.g.refs_0_.refs_2_, bf16[512,2048]{1,0:T(8,128)(2,1)} %pack.5.refs_2_.w0, bf16[256,2048]{1,0:T(8,128)(2,1)} %collective-permute-done.15.refs_4_.w1, bf16[256,2048]{1,0:T(8,128)(2,1)} %copy-done.31, ...), custom_call_target="tpu_custom_call" | custom-call | flops 171798691840 | bytes 419430400 | tf_op jit(solution)/shard_map/dhid/pallas_call | solution.py:439
  222.9 2.5 add_convert_fusion.15
  227.0 3.4 collective-permute-start.24
  230.5 10.0 %wgrad.7 = (bf16[512,2048]{1,0:T(8,128)(2,1)}, bf16[512,2048]{1,0:T(8,128)(2,1)}) custom-call(s32[13]{0:T(128)} %concatenate.10.meta, bf16[1024,2048]{1,0:T(8,128)(2,1)} %get-tuple-element.148.g.refs_0_.refs_2_, bf16[1024,2048]{1,0:T(8,128)(2,1)} %get-tuple-element.136.gb.refs_1_, bf16[1024,2048]{1,0:T(8,128)(2,1)} %collective-permute-done.20.refs_2_), custom_call_target="tpu_custom_call" | custom-call | flops 88080384000 | bytes 293601280 | tf_op jit(solution)/shard_map/wgrad/pallas_call | solution.py:603
  240.5 5.8 %collective-permute-done.21 = bf16[1024,512]{1,0:T(8,128)(2,1)S(1)} collective-permute-done((bf16[1024,512]{1,0:T(8,128)(2,1)S(1)}, bf16[1024,512]{1,0:T(8,128)(2,1)S(1)}, u32[]{:S(2)}, u32[]{:S(2)}) %collective-permute-start.21) | collective-permute-done | bytes 1048608 | tf_op jit(solution)/shard_map/ppermute | solution.py:825
  247.6 2.0 collective-permute-start.25
  249.6 6.0 %join.1 = (bf16[1024,1536]{1,0:T(8,128)(2,1)}, f32[1,1536]{1,0:T(1,128)}) custom-call(bf16[1024,512]{1,0:T(8,128)(2,1)} %get-tuple-element.158.dq_ref, f32[1024,1024]{1,0:T(8,128)} %get-tuple-element.159.dkv_ref, bf16[1024,1024]{1,0:T(8,128)(2,1)} %collective-permute-done.22.rv_ref, f32[512,128]{1,0:T(8,128)} %get-tuple-element.234.cosf, ...), custom_call_target="tpu_custom_call" | custom-call | flops 75497472000 | bytes 251658240 | tf_op jit(solution)/shard_map/join/pallas_call | solution.py:389
  255.7 2.9 fusion.refs_0_
  258.6 4.4 collective-permute-start.28
  265.1 16.0 %backn.2 = (bf16[1024,512]{1,0:T(8,128)(2,1)}, bf16[1024,512]{1,0:T(8,128)(2,1)}, f32[4,2048]{1,0:T(4,128)}) custom-call(s32[13]{0:T(128)} %concatenate.10.meta, bf16[1024,1536]{1,0:T(8,128)(2,1)} %get-tuple-element.161.dqkv.refs_1_, bf16[1024,2048]{1,0:T(8,128)(2,1)} %get-tuple-element.150.du.refs_1_, ...), custom_call_target="tpu_custom_call", output_to_operand_aliasing={{2}: (13, {})} | custom-call | flops 150323855360 | bytes 377487360 | tf_op jit(solution)/shard_map/backn/pallas_call | solution.py:524
  281.2 2.9 add_convert_fusion.12
  286.3 2.9 fusion.1.refs_4_
  290.0 4.4 hsum.3
  295.0 10.2 %wgrad.8 = bf16[1024,2048]{1,0:T(8,128)(2,1)} custom-call(s32[13]{0:T(128)} %concatenate.10.meta, bf16[1024,2048]{1,0:T(8,128)(2,1)} %get-tuple-element.126.h1.refs_0_, bf16[1024,1536]{1,0:T(8,128)(2,1)} %get-tuple-element.161.dqkv.refs_1_, bf16[1024,2048]{1,0:T(8,128)(2,1)} %get-tuple-element.148.g.refs_0_.refs_2_, ...), custom_call_target="tpu_custom_call" | custom-call | flops 100663296000 | bytes 335544320 | tf_op jit(solution)/shard_map/wgrad/pallas_call | solution.py:603
  305.2 2.6 add_convert_fusion.10
  309.6 2.9 fusion.2.refs_2_
  312.5 2.0 collective-permute-start.33
  314.5 9.2 %wgrad.9 = bf16[1024,2048]{1,0:T(8,128)(2,1)} custom-call(s32[13]{0:T(128)} %concatenate.10.meta, bf16[1024,2048]{1,0:T(8,128)(2,1)} %norm2.1.h2.refs_0_, bf16[1024,2048]{1,0:T(8,128)(2,1)} %get-tuple-element.150.du.refs_1_), custom_call_target="tpu_custom_call" | custom-call | flops 88080384000 | bytes 293601280 | tf_op jit(solution)/shard_map/wgrad/pallas_call | solution.py:603
  323.7 16.4 %backn.3 = (bf16[1024,512]{1,0:T(8,128)(2,1)}, bf16[1024,512]{1,0:T(8,128)(2,1)}, f32[4,2048]{1,0:T(4,128)}) custom-call(s32[13]{0:T(128)} %concatenate.10.meta, bf16[1024,1536]{1,0:T(8,128)(2,1)} %get-tuple-element.161.dqkv.refs_1_, bf16[1024,2048]{1,0:T(8,128)(2,1)} %get-tuple-element.150.du.refs_1_, ...), custom_call_target="tpu_custom_call", output_to_operand_aliasing={{2}: (13, {})} | custom-call | flops 150323855360 | bytes 377487360 | tf_op jit(solution)/shard_map/backn/pallas_call | solution.py:524
  343.5 2.9 fusion.3.refs_6_
  346.5 1.9 collective-permute-start.38
  348.5 10.1 %wgrad.10 = (bf16[512,2048]{1,0:T(8,128)(2,1)}, bf16[512,2048]{1,0:T(8,128)(2,1)}) custom-call(s32[13]{0:T(128)} %concatenate.10.meta, bf16[1024,2048]{1,0:T(8,128)(2,1)} %norm2.1.h2.refs_0_, bf16[1024,2048]{1,0:T(8,128)(2,1)} %get-tuple-element.150.du.refs_1_, bf16[1024,2048]{1,0:T(8,128)(2,1)} %collective-permute-done.32.refs_2_), custom_call_target="tpu_custom_call" | custom-call | flops 88080384000 | bytes 293601280 | tf_op jit(solution)/shard_map/wgrad/pallas_call | solution.py:603
  360.2 2.6 fusion.4.refs_0_
  363.5 4.3 lsum.3
  370.0 12.0 %collective-permute-start.43 = (bf16[1024,512]{1,0:T(8,128)(2,1)}, bf16[1024,512]{1,0:T(8,128)(2,1)}, u32[]{:S(2)}, u32[]{:S(2)}) collective-permute-start(bf16[1024,512]{1,0:T(8,128)(2,1)} %fusion.4.refs_0_), channel_id=1, source_target_pairs={{0,1},{3,2},{1,0},{2,3},{4,5},{7,6},{5,4},{6,7},{8,9},{11,10},{9,8... | collective-permute-start | bytes 3145736 | tf_op jit(solution)/shard_map/ppermute | solution.py:825
  382.0 7.8 %collective-permute-done.36.got = bf16[512,2048]{1,0:T(8,128)(2,1)} collective-permute-done((bf16[512,2048]{1,0:T(8,128)(2,1)}, bf16[512,2048]{1,0:T(8,128)(2,1)}, u32[]{:S(2)}, u32[]{:S(2)}) %collective-permute-start.36) | collective-permute-done | bytes 2097184 | tf_op jit(solution)/shard_map/ppermute | solution.py:897
  389.8 4.4 hsum.4
  394.2 2.5 add_convert_fusion.4
  399.3 1.9 collective-permute-start.44
  402.7 5.3 %bout.2.refs_8_ = bf16[1024,2048]{1,0:T(8,128)(2,1)} custom-call(s32[13]{0:T(128)} %concatenate.10.meta, bf16[1024,2048]{1,0:T(8,128)(2,1)} %bitcast.34, f32[1,2048]{1,0:T(1,128)} %bitcast.28, bf16[1024,512]{1,0:T(8,128)(2,1)} %fusion.refs_0_, bf16[1024,512]{1,0:T(8,128)(2,1)} %collective-permute-done.28.refs_1_, bf16[1024,512]{1,0:T(8,128)(2,1)} %fusion.2.refs_2_, ...), custom_call_target="tpu_custom_call" | custom-call | flops 50331648000 | bytes 167772160 | tf_op jit(solution)/shard_map/bout/pallas_call | solution.py:763
  408.0 8.1 %collective-permute-done.40.got = bf16[256,2048]{1,0:T(8,128)(2,1)S(1)} collective-permute-done((bf16[256,2048]{1,0:T(8,128)(2,1)S(1)}, bf16[256,2048]{1,0:T(8,128)(2,1)S(1)}, u32[]{:S(2)}, u32[]{:S(2)}) %collective-permute-start.40) | collective-permute-done | bytes 1048608 | tf_op jit(solution)/shard_map/ppermute | solution.py:897
  417.2 4.0 lsum.4
  422.5 10.8 %wgrad.11 = (bf16[512,2048]{1,0:T(8,128)(2,1)}, bf16[512,2048]{1,0:T(8,128)(2,1)}) custom-call(s32[13]{0:T(128)} %concatenate.10.meta, bf16[1024,2048]{1,0:T(8,128)(2,1)} %get-tuple-element.126.h1.refs_0_, bf16[1024,1536]{1,0:T(8,128)(2,1)} %get-tuple-element.161.dqkv.refs_1_, bf16[1024,2048]{1,0:T(8,128)(2,1)} %get-tuple-element.148.g.refs_0_.refs_2_, ...), custom_call_target="tpu_custom_call" | custom-call | flops 100663296000 | bytes 335544320 | tf_op jit(solution)/shard_map/wgrad/pallas_call | solution.py:603
  439.4 5.2 bout.3
  444.6 20.5 %collective-permute-done.45.got = bf16[512,2048]{1,0:T(8,128)(2,1)} collective-permute-done((bf16[512,2048]{1,0:T(8,128)(2,1)}, bf16[512,2048]{1,0:T(8,128)(2,1)}, u32[]{:S(2)}, u32[]{:S(2)}) %collective-permute-start.45) | collective-permute-done | bytes 2097184 | tf_op jit(solution)/shard_map/ppermute | solution.py:897
  465.2 4.4 hsum.5
  470.8 14.6 %collective-permute-start.50 = (f32[8192]{0:T(1024)S(1)}, f32[8192]{0:T(1024)S(1)}, u32[]{:S(2)}, u32[]{:S(2)}) collective-permute-start(f32[8192]{0:T(1024)S(1)} %slice.40), channel_id=1, source_target_pairs={{0,1},{1,0},{2,3},{3,2},{4,5},{5,4},{6,7},{7,6},{8,9},{9,8},{10,11... | collective-permute-start | bytes 98312 | tf_op jit(solution)/shard_map/ppermute | solution.py:930
  488.6 4.3 lsum.5
  492.9 11.7 %collective-permute-start.52 = (f32[8192]{0:T(1024)S(1)}, f32[8192]{0:T(1024)S(1)}, u32[]{:S(2)}, u32[]{:S(2)}) collective-permute-start(f32[8192]{0:T(1024)S(1)} %add.122), channel_id=1, source_target_pairs={{0,2},{2,0},{1,3},{3,1},{4,6},{6,4},{5,7},{7,5},{8,10},{10,8},{9,1... | collective-permute-start | bytes 98312 | tf_op jit(solution)/shard_map/ppermute | solution.py:932
  504.6 8.5 %collective-permute-done.51.refs_7_ = bf16[1024,512]{1,0:T(8,128)(2,1)S(1)} collective-permute-done((bf16[1024,512]{1,0:T(8,128)(2,1)}, bf16[1024,512]{1,0:T(8,128)(2,1)S(1)}, u32[]{:S(2)}, u32[]{:S(2)}) %collective-permute-start.51) | collective-permute-done | bytes 1048608 | tf_op jit(solution)/shard_map/ppermute | solution.py:825
  514.1 12.0 %igrad.1 = bf16[1024,2048]{1,0:T(8,128)(2,1)} custom-call(s32[13]{0:T(128)} %concatenate.10.meta, bf16[1024,2048]{1,0:T(8,128)(2,1)} %bitcast.36, bf16[1024,2048]{1,0:T(8,128)(2,1)} %bitcast.38, f32[1024,128]{1,0:T(8,128)} %get-tuple-element.130.st_ref, bf16[1024,512]{1,0:T(8,128)(2,1)} %fusion.4.refs_0_, bf16[1024,512]{1,0:T(8,128)(2,1)} %collective-permute-done.43.refs_1_, ...), custom_call_target="tpu_custom_call" | custom-call | flops 100663296000 | bytes 335544320 | tf_op jit(solution)/shard_map/igrad/pallas_call | solution.py:763
  (186 shorter events, 64.2 us)
Async XLA Ops:
  4.6 27.3 %collective-permute-start = (bf16[256,2048]{1,0:T(8,128)(2,1)}, bf16[256,2048]{1,0:T(8,128)(2,1)}, u32[]{:S(2)}, u32[]{:S(2)}) collective-permute-start(bf16[256,2048]{1,0:T(8,128)(2,1)} %pad_maximum_fusion.refs_0_), channel_id=1, source_target_pairs={{0,4},{4,0},{1,5},{5,1},{2,6},{6,2},{3,7},{7,3},{8,12},{12,8},{9,1... | collective-permute-start | bytes 3145736 | tf_op jit(solution)/shard_map/ppermute | solution.py:860
  7.6 24.8 %collective-permute-start.2 = (bf16[256,2048]{1,0:T(8,128)(2,1)}, bf16[256,2048]{1,0:T(8,128)(2,1)S(1)}, u32[]{:S(2)}, u32[]{:S(2)}) collective-permute-start(bf16[256,2048]{1,0:T(8,128)(2,1)} %pad_maximum_fusion.refs_0_), channel_id=1, source_target_pairs={{0,16},{16,0},{8,24},{24,8},{1,17},{17,1},{9,25},{25,9},{2,18},{18... | collective-permute-start | bytes 3145736 | tf_op jit(solution)/shard_map/ppermute | solution.py:854
  10.2 46.4 %collective-permute-start.1 = (bf16[256,2048]{1,0:T(8,128)(2,1)}, bf16[256,2048]{1,0:T(8,128)(2,1)}, u32[]{:S(2)}, u32[]{:S(2)}) collective-permute-start(bf16[256,2048]{1,0:T(8,128)(2,1)} %convert_element_type.174.refs_0_), channel_id=1, source_target_pairs={{0,4},{4,0},{1,5},{5,1},{2,6},{6,2},{3,7},{7,3},{8,12},{12,8},{9,1... | collective-permute-start | bytes 3145736 | tf_op jit(solution)/shard_map/ppermute | solution.py:860
  13.3 123.6 %collective-permute-start.12 = (bf16[256,2048]{1,0:T(8,128)(2,1)}, bf16[256,2048]{1,0:T(8,128)(2,1)}, u32[]{:S(2)}, u32[]{:S(2)}) collective-permute-start(bf16[256,2048]{1,0:T(8,128)(2,1)} %bitcast.21.refs_0_), channel_id=1, source_target_pairs={{0,4},{4,0},{1,5},{5,1},{2,6},{6,2},{3,7},{7,3},{8,12},{12,8},{9,1... | collective-permute-start | bytes 3145736 | tf_op jit(solution)/shard_map/ppermute | solution.py:860
  15.4 11.1 %copy-start.19 = (f32[2048]{0:T(1024)S(1)}, f32[2048]{0:T(1024)}, u32[]{:S(2)}) copy-start(f32[2048]{0:T(1024)} %param.25) | copy-start | bytes 24580
  15.4 11.1 %copy-start.20 = (f32[2048]{0:T(1024)S(1)}, f32[2048]{0:T(1024)}, u32[]{:S(2)}) copy-start(f32[2048]{0:T(1024)} %param.29) | copy-start | bytes 24580
  32.4 24.2 %collective-permute-start.3 = (bf16[256,2048]{1,0:T(8,128)(2,1)}, bf16[256,2048]{1,0:T(8,128)(2,1)}, u32[]{:S(2)}, u32[]{:S(2)}) collective-permute-start(bf16[256,2048]{1,0:T(8,128)(2,1)} %collective-permute-done.refs_1_), channel_id=1, source_target_pairs={{0,16},{16,0},{8,24},{24,8},{1,17},{17,1},{9,25},{25,9},{2,18},{18... | collective-permute-start | bytes 3145736 | tf_op jit(solution)/shard_map/ppermute | solution.py:854
  37.7 24.8 %collective-permute-start.4 = (bf16[512,2048]{1,0:T(8,128)(2,1)}, bf16[512,2048]{1,0:T(8,128)(2,1)S(1)}, u32[]{:S(2)}, u32[]{:S(2)}) collective-permute-start(bf16[512,2048]{1,0:T(8,128)(2,1)} %pack.3.w0.refs_0_.w10), channel_id=1, source_target_pairs={{0,8},{8,0},{16,24},{24,16},{1,9},{9,1},{17,25},{25,17},{2,10},{10... | collective-permute-start | bytes 6291464 | tf_op jit(solution)/shard_map/ppermute | solution.py:857
  37.7 23.3 %collective-permute-start.5 = (bf16[256,2048]{1,0:T(8,128)(2,1)S(1)}, bf16[256,2048]{1,0:T(8,128)(2,1)}, u32[]{:S(2)}, u32[]{:S(2)}) collective-permute-start(bf16[256,2048]{1,0:T(8,128)(2,1)S(1)} %collective-permute-done.2.w1.refs_0_.w11), channel_id=1, source_target_pairs={{0,8},{8,0},{16,24},{24,16},{1,9},{9,1},{17,25},{25,17},{2,10},{10... | collective-permute-start | bytes 3145736 | tf_op jit(solution)/shard_map/ppermute | solution.py:857
  56.6 5.9 %collective-permute-start.6 = (bf16[256,2048]{1,0:T(8,128)(2,1)}, bf16[256,2048]{1,0:T(8,128)(2,1)}, u32[]{:S(2)}, u32[]{:S(2)}) collective-permute-start(bf16[256,2048]{1,0:T(8,128)(2,1)} %collective-permute-done.3.w2.refs_1_.w12), channel_id=1, source_target_pairs={{0,8},{8,0},{16,24},{24,16},{1,9},{9,1},{17,25},{25,17},{2,10},{10... | collective-permute-start | bytes 3145736 | tf_op jit(solution)/shard_map/ppermute | solution.py:857
  60.5 57.1 %collective-permute-start.9 = (bf16[512,2048]{1,0:T(8,128)(2,1)}, bf16[512,2048]{1,0:T(8,128)(2,1)}, u32[]{:S(2)}, u32[]{:S(2)}) collective-permute-start(bf16[512,2048]{1,0:T(8,128)(2,1)} %pack.4.w0.w20), channel_id=1, source_target_pairs={{0,8},{8,0},{16,24},{24,16},{1,9},{9,1},{17,25},{25,17},{2,10},{10... | collective-permute-start | bytes 6291464 | tf_op jit(solution)/shard_map/ppermute | solution.py:857
  61.0 25.3 %collective-permute-start.7 = (bf16[256,2048]{1,0:T(8,128)(2,1)}, bf16[256,2048]{1,0:T(8,128)(2,1)S(1)}, u32[]{:S(2)}, u32[]{:S(2)}) collective-permute-start(bf16[256,2048]{1,0:T(8,128)(2,1)} %convert_element_type.174.refs_0_), channel_id=1, source_target_pairs={{0,16},{16,0},{8,24},{24,8},{1,17},{17,1},{9,25},{25,9},{2,18},{18... | collective-permute-start | bytes 3145736 | tf_op jit(solution)/shard_map/ppermute | solution.py:854
  73.6 71.4 %collective-permute-start.13 = (bf16[1024,1024]{1,0:T(8,128)(2,1)}, bf16[1024,1024]{1,0:T(8,128)(2,1)}, u32[]{:S(2)}, u32[]{:S(2)}) collective-permute-start(bf16[1024,1024]{1,0:T(8,128)(2,1)} %kv.1.kv_ref), channel_id=1, source_target_pairs={{0,4},{1,5},{2,6},{3,7},{8,12},{9,13},{10,14},{11,15},{16,20},{17,... | collective-permute-start | bytes 6291464 | tf_op jit(solution)/shard_map/ppermute | solution.py:914
  86.3 12.3 %copy-start.29 = (bf16[256,2048]{1,0:T(8,128)(2,1)}, bf16[256,2048]{1,0:T(8,128)(2,1)S(1)}, u32[]{:S(2)}) copy-start(bf16[256,2048]{1,0:T(8,128)(2,1)S(1)} %collective-permute-done.7.w1.w21) | copy-start | bytes 3145732
  86.3 24.6 %collective-permute-start.8 = (bf16[256,2048]{1,0:T(8,128)(2,1)}, bf16[256,2048]{1,0:T(8,128)(2,1)}, u32[]{:S(2)}, u32[]{:S(2)}) collective-permute-start(bf16[256,2048]{1,0:T(8,128)(2,1)} %collective-permute-done.1.refs_1_), channel_id=1, source_target_pairs={{0,16},{16,0},{8,24},{24,8},{1,17},{17,1},{9,25},{25,9},{2,18},{18... | collective-permute-start | bytes 3145736 | tf_op jit(solution)/shard_map/ppermute | solution.py:854
  87.8 31.3 %collective-permute-start.10 = (bf16[256,2048]{1,0:T(8,128)(2,1)S(1)}, bf16[256,2048]{1,0:T(8,128)(2,1)S(1)}, u32[]{:S(2)}, u32[]{:S(2)}) collective-permute-start(bf16[256,2048]{1,0:T(8,128)(2,1)S(1)} %collective-permute-done.7.w1.w21), channel_id=1, source_target_pairs={{0,8},{8,0},{16,24},{24,16},{1,9},{9,1},{17,25},{25,17},{2,10},{10... | collective-permute-start | bytes 3145736 | tf_op jit(solution)/shard_map/ppermute | solution.py:857
  110.9 8.2 %collective-permute-start.11 = (bf16[256,2048]{1,0:T(8,128)(2,1)}, bf16[256,2048]{1,0:T(8,128)(2,1)S(1)}, u32[]{:S(2)}, u32[]{:S(2)}) collective-permute-start(bf16[256,2048]{1,0:T(8,128)(2,1)} %collective-permute-done.8.w2.w22), channel_id=1, source_target_pairs={{0,8},{8,0},{16,24},{24,16},{1,9},{9,1},{17,25},{25,17},{2,10},{10... | collective-permute-start | bytes 3145736 | tf_op jit(solution)/shard_map/ppermute | solution.py:857
  117.6 25.9 %collective-permute-start.15 = (bf16[256,2048]{1,0:T(8,128)(2,1)}, bf16[256,2048]{1,0:T(8,128)(2,1)}, u32[]{:S(2)}, u32[]{:S(2)}) collective-permute-start(bf16[256,2048]{1,0:T(8,128)(2,1)} %bitcast.21.refs_0_), channel_id=1, source_target_pairs={{0,16},{16,0},{8,24},{24,8},{1,17},{17,1},{9,25},{25,9},{2,18},{18... | collective-permute-start | bytes 3145736 | tf_op jit(solution)/shard_map/ppermute | solution.py:854
  140.7 27.7 %collective-permute-start.14 = (bf16[512,2048]{1,0:T(8,128)(2,1)}, bf16[512,2048]{1,0:T(8,128)(2,1)S(1)}, u32[]{:S(2)}, u32[]{:S(2)}) collective-permute-start(bf16[512,2048]{1,0:T(8,128)(2,1)} %pack.5.refs_2_.w0), channel_id=1, source_target_pairs={{0,8},{8,0},{16,24},{24,16},{1,9},{9,1},{17,25},{25,17},{2,10},{10... | collective-permute-start | bytes 6291464 | tf_op jit(solution)/shard_map/ppermute | solution.py:857
  143.5 24.9 %collective-permute-start.16 = (bf16[256,2048]{1,0:T(8,128)(2,1)}, bf16[256,2048]{1,0:T(8,128)(2,1)S(1)}, u32[]{:S(2)}, u32[]{:S(2)}) collective-permute-start(bf16[256,2048]{1,0:T(8,128)(2,1)} %collective-permute-done.12.refs_1_), channel_id=1, source_target_pairs={{0,16},{16,0},{8,24},{24,8},{1,17},{17,1},{9,25},{25,9},{2,18},{18... | collective-permute-start | bytes 3145736 | tf_op jit(solution)/shard_map/ppermute | solution.py:854
  157.3 28.0 %collective-permute-start.17 = (bf16[256,2048]{1,0:T(8,128)(2,1)}, bf16[256,2048]{1,0:T(8,128)(2,1)}, u32[]{:S(2)}, u32[]{:S(2)}) collective-permute-start(bf16[256,2048]{1,0:T(8,128)(2,1)} %collective-permute-done.15.refs_4_.w1), channel_id=1, source_target_pairs={{0,8},{8,0},{16,24},{24,16},{1,9},{9,1},{17,25},{25,17},{2,10},{10... | collective-permute-start | bytes 3145736 | tf_op jit(solution)/shard_map/ppermute | solution.py:857
  157.4 92.2 %collective-permute-start.22 = (bf16[1024,1024]{1,0:T(8,128)(2,1)}, bf16[1024,1024]{1,0:T(8,128)(2,1)}, u32[]{:S(2)}, u32[]{:S(2)}) collective-permute-start(bf16[1024,1024]{1,0:T(8,128)(2,1)} %get-tuple-element.160), channel_id=1, source_target_pairs={{4,0},{5,1},{6,2},{7,3},{12,8},{13,9},{14,10},{15,11},{20,16},{21,... | collective-permute-start | bytes 6291464 | tf_op jit(solution)/shard_map/ppermute | solution.py:917
  168.4 12.3 %copy-start.31 = (bf16[256,2048]{1,0:T(8,128)(2,1)}, bf16[256,2048]{1,0:T(8,128)(2,1)S(1)}, u32[]{:S(2)}) copy-start(bf16[256,2048]{1,0:T(8,128)(2,1)S(1)} %collective-permute-done.16.refs_5_.w2) | copy-start | bytes 3145732
  168.4 16.9 %collective-permute-start.18 = (bf16[256,2048]{1,0:T(8,128)(2,1)S(1)}, bf16[256,2048]{1,0:T(8,128)(2,1)}, u32[]{:S(2)}, u32[]{:S(2)}) collective-permute-start(bf16[256,2048]{1,0:T(8,128)(2,1)S(1)} %collective-permute-done.16.refs_5_.w2), channel_id=1, source_target_pairs={{0,8},{8,0},{16,24},{24,16},{1,9},{9,1},{17,25},{25,17},{2,10},{10... | collective-permute-start | bytes 3145736 | tf_op jit(solution)/shard_map/ppermute | solution.py:857
  180.6 42.3 %collective-permute-start.19 = (bf16[1024,512]{1,0:T(8,128)(2,1)}, bf16[1024,512]{1,0:T(8,128)(2,1)}, u32[]{:S(2)}, u32[]{:S(2)}) collective-permute-start(bf16[1024,512]{1,0:T(8,128)(2,1)} %get-tuple-element.151), channel_id=1, source_target_pairs={{0,1},{3,2},{4,5},{7,6},{8,9},{11,10},{12,13},{15,14},{16,17},{19,... | collective-permute-start | bytes 3145736 | tf_op jit(solution)/shard_map/ppermute | solution.py:825
  206.2 24.3 %collective-permute-start.20 = (bf16[1024,2048]{1,0:T(8,128)(2,1)}, bf16[1024,2048]{1,0:T(8,128)(2,1)}, u32[]{:S(2)}, u32[]{:S(2)}) collective-permute-start(bf16[1024,2048]{1,0:T(8,128)(2,1)} %wgrad.6), channel_id=1, source_target_pairs={{0,8},{8,0},{16,24},{24,16},{1,9},{9,1},{17,25},{25,17},{2,10},{10... | collective-permute-start | bytes 12582920 | tf_op jit(solution)/shard_map/ppermute | solution.py:857
  206.4 15.2 %copy-start.12 = (bf16[1024,512]{1,0:T(8,128)(2,1)S(1)}, bf16[1024,512]{1,0:T(8,128)(2,1)}, u32[]{:S(2)}) copy-start(bf16[1024,512]{1,0:T(8,128)(2,1)} %get-tuple-element.155) | copy-start | bytes 3145732
  206.4 16.5 %copy-start.13 = (bf16[1024,512]{1,0:T(8,128)(2,1)S(1)}, bf16[1024,512]{1,0:T(8,128)(2,1)}, u32[]{:S(2)}) copy-start(bf16[1024,512]{1,0:T(8,128)(2,1)} %get-tuple-element.151) | copy-start | bytes 3145732
  221.5 24.8 %collective-permute-start.21 = (bf16[1024,512]{1,0:T(8,128)(2,1)S(1)}, bf16[1024,512]{1,0:T(8,128)(2,1)S(1)}, u32[]{:S(2)}, u32[]{:S(2)}) collective-permute-start(bf16[1024,512]{1,0:T(8,128)(2,1)S(1)} %copy-done.12), channel_id=1, source_target_pairs={{0,1},{3,2},{4,5},{7,6},{8,9},{11,10},{12,13},{15,14},{16,17},{19,... | collective-permute-start | bytes 3145736 | tf_op jit(solution)/shard_map/ppermute | solution.py:825
  225.4 30.3 %collective-permute-start.23 = (bf16[1024,512]{1,0:T(8,128)(2,1)}, bf16[1024,512]{1,0:T(8,128)(2,1)}, u32[]{:S(2)}, u32[]{:S(2)}) collective-permute-start(bf16[1024,512]{1,0:T(8,128)(2,1)} %add_convert_fusion.15), channel_id=1, source_target_pairs={{1,2},{2,1},{5,6},{6,5},{9,10},{10,9},{13,14},{14,13},{17,18},{18,... | collective-permute-start | bytes 3145736 | tf_op jit(solution)/shard_map/ppermute | solution.py:835
  227.0 54.1 %collective-permute-start.24 = (bf16[1024,512]{1,0:T(8,128)(2,1)}, bf16[1024,512]{1,0:T(8,128)(2,1)}, u32[]{:S(2)}, u32[]{:S(2)}) collective-permute-start(bf16[1024,512]{1,0:T(8,128)(2,1)} %get-tuple-element.166), channel_id=1, source_target_pairs={{0,1},{3,2},{4,5},{7,6},{8,9},{11,10},{12,13},{15,14},{16,17},{19,... | collective-permute-start | bytes 3145736 | tf_op jit(solution)/shard_map/ppermute | solution.py:825
  247.6 38.7 %collective-permute-start.25 = (bf16[1024,512]{1,0:T(8,128)(2,1)}, bf16[1024,512]{1,0:T(8,128)(2,1)}, u32[]{:S(2)}, u32[]{:S(2)}) collective-permute-start(bf16[1024,512]{1,0:T(8,128)(2,1)} %add_convert_fusion.14), channel_id=1, source_target_pairs={{1,2},{2,1},{5,6},{6,5},{9,10},{10,9},{13,14},{14,13},{17,18},{18,... | collective-permute-start | bytes 3145736 | tf_op jit(solution)/shard_map/ppermute | solution.py:835
  258.6 46.5 %collective-permute-start.28 = (bf16[1024,512]{1,0:T(8,128)(2,1)}, bf16[1024,512]{1,0:T(8,128)(2,1)}, u32[]{:S(2)}, u32[]{:S(2)}) collective-permute-start(bf16[1024,512]{1,0:T(8,128)(2,1)} %fusion.refs_0_), channel_id=1, source_target_pairs={{0,1},{3,2},{1,0},{2,3},{4,5},{7,6},{5,4},{6,7},{8,9},{11,10},{9,8... | collective-permute-start | bytes 3145736 | tf_op jit(solution)/shard_map/ppermute | solution.py:825
  263.0 27.0 %collective-permute-start.26 = (bf16[512,2048]{1,0:T(8,128)(2,1)}, bf16[512,2048]{1,0:T(8,128)(2,1)}, u32[]{:S(2)}, u32[]{:S(2)}) collective-permute-start(bf16[512,2048]{1,0:T(8,128)(2,1)} %get-tuple-element.169), channel_id=1, source_target_pairs={{0,16},{4,20},{8,12},{12,8},{16,0},{20,4},{24,28},{28,24},{1,17},{... | collective-permute-start | bytes 6291464 | tf_op jit(solution)/shard_map/ppermute | solution.py:897
  284.0 25.5 %collective-permute-start.29 = (bf16[1024,512]{1,0:T(8,128)(2,1)}, bf16[1024,512]{1,0:T(8,128)(2,1)}, u32[]{:S(2)}, u32[]{:S(2)}) collective-permute-start(bf16[1024,512]{1,0:T(8,128)(2,1)} %add_convert_fusion.12), channel_id=1, source_target_pairs={{1,2},{2,1},{5,6},{6,5},{9,10},{10,9},{13,14},{14,13},{17,18},{18,... | collective-permute-start | bytes 3145736 | tf_op jit(solution)/shard_map/ppermute | solution.py:835
  289.2 50.8 %collective-permute-start.30 = (bf16[1024,512]{1,0:T(8,128)(2,1)}, bf16[1024,512]{1,0:T(8,128)(2,1)}, u32[]{:S(2)}, u32[]{:S(2)}) collective-permute-start(bf16[1024,512]{1,0:T(8,128)(2,1)} %fusion.1.refs_4_), channel_id=1, source_target_pairs={{0,1},{3,2},{1,0},{2,3},{4,5},{7,6},{5,4},{6,7},{8,9},{11,10},{9,8... | collective-permute-start | bytes 3145736 | tf_op jit(solution)/shard_map/ppermute | solution.py:825
  294.4 10.8 %copy-start.3 = (bf16[1024,512]{1,0:T(8,128)(2,1)S(1)}, bf16[1024,512]{1,0:T(8,128)(2,1)}, u32[]{:S(2)}) copy-start(bf16[1024,512]{1,0:T(8,128)(2,1)} %get-tuple-element.174) | copy-start | bytes 3145732
  294.4 20.2 %collective-permute-start.27 = (bf16[256,2048]{1,0:T(8,128)(2,1)}, bf16[256,2048]{1,0:T(8,128)(2,1)S(1)}, u32[]{:S(2)}, u32[]{:S(2)}) collective-permute-start(bf16[256,2048]{1,0:T(8,128)(2,1)} %get-tuple-element.170), channel_id=1, source_target_pairs={{0,4},{4,0},{8,24},{12,28},{16,20},{20,16},{24,8},{28,12},{1,5},{5... | collective-permute-start | bytes 3145736 | tf_op jit(solution)/shard_map/ppermute | solution.py:897
  307.7 35.8 %collective-permute-start.31 = (bf16[1024,512]{1,0:T(8,128)(2,1)}, bf16[1024,512]{1,0:T(8,128)(2,1)}, u32[]{:S(2)}, u32[]{:S(2)}) collective-permute-start(bf16[1024,512]{1,0:T(8,128)(2,1)} %add_convert_fusion.10), channel_id=1, source_target_pairs={{1,2},{2,1},{5,6},{6,5},{9,10},{10,9},{13,14},{14,13},{17,18},{18,... | collective-permute-start | bytes 3145736 | tf_op jit(solution)/shard_map/ppermute | solution.py:835
  312.5 46.1 %collective-permute-start.33 = (bf16[1024,512]{1,0:T(8,128)(2,1)}, bf16[1024,512]{1,0:T(8,128)(2,1)}, u32[]{:S(2)}, u32[]{:S(2)}) collective-permute-start(bf16[1024,512]{1,0:T(8,128)(2,1)} %fusion.2.refs_2_), channel_id=1, source_target_pairs={{0,1},{3,2},{1,0},{2,3},{4,5},{7,6},{5,4},{6,7},{8,9},{11,10},{9,8... | collective-permute-start | bytes 3145736 | tf_op jit(solution)/shard_map/ppermute | solution.py:825
  323.7 24.8 %collective-permute-start.32 = (bf16[1024,2048]{1,0:T(8,128)(2,1)}, bf16[1024,2048]{1,0:T(8,128)(2,1)}, u32[]{:S(2)}, u32[]{:S(2)}) collective-permute-start(bf16[1024,2048]{1,0:T(8,128)(2,1)} %wgrad.9), channel_id=1, source_target_pairs={{0,8},{8,0},{16,24},{24,16},{1,9},{9,1},{17,25},{25,17},{2,10},{10... | collective-permute-start | bytes 12582920 | tf_op jit(solution)/shard_map/ppermute | solution.py:857
  323.7 16.4 %copy-start.9 = (bf16[1024,512]{1,0:T(8,128)(2,1)S(1)}, bf16[1024,512]{1,0:T(8,128)(2,1)}, u32[]{:S(2)}) copy-start(bf16[1024,512]{1,0:T(8,128)(2,1)} %get-tuple-element.185) | copy-start | bytes 3145732
  341.7 18.5 %collective-permute-start.34 = (bf16[1024,512]{1,0:T(8,128)(2,1)S(1)}, bf16[1024,512]{1,0:T(8,128)(2,1)}, u32[]{:S(2)}, u32[]{:S(2)}) collective-permute-start(bf16[1024,512]{1,0:T(8,128)(2,1)S(1)} %add_convert_fusion.8), channel_id=1, source_target_pairs={{1,2},{2,1},{5,6},{6,5},{9,10},{10,9},{13,14},{14,13},{17,18},{18,... | collective-permute-start | bytes 3145736 | tf_op jit(solution)/shard_map/ppermute | solution.py:835
  346.5 47.7 %collective-permute-start.38 = (bf16[1024,512]{1,0:T(8,128)(2,1)}, bf16[1024,512]{1,0:T(8,128)(2,1)}, u32[]{:S(2)}, u32[]{:S(2)}) collective-permute-start(bf16[1024,512]{1,0:T(8,128)(2,1)} %fusion.3.refs_6_), channel_id=1, source_target_pairs={{0,1},{3,2},{1,0},{2,3},{4,5},{7,6},{5,4},{6,7},{8,9},{11,10},{9,8... | collective-permute-start | bytes 3145736 | tf_op jit(solution)/shard_map/ppermute | solution.py:825
  348.4 19.4 %collective-permute-start.35 = (f32[13824]{0:T(1024)S(1)}, f32[13824]{0:T(1024)S(1)}, u32[]{:S(2)}, u32[]{:S(2)}) collective-permute-start(f32[13824]{0:T(1024)S(1)} %pad_maximum_fusion.1), channel_id=1, source_target_pairs={{0,8},{8,0},{16,24},{24,16},{1,9},{9,1},{17,25},{25,17},{2,10},{10... | collective-permute-start | bytes 165896 | tf_op jit(solution)/shard_map/ppermute | solution.py:857
  362.9 27.0 %collective-permute-start.36 = (bf16[512,2048]{1,0:T(8,128)(2,1)}, bf16[512,2048]{1,0:T(8,128)(2,1)}, u32[]{:S(2)}, u32[]{:S(2)}) collective-permute-start(bf16[512,2048]{1,0:T(8,128)(2,1)} %get-tuple-element.195), channel_id=1, source_target_pairs={{0,16},{4,20},{8,12},{12,8},{16,0},{20,4},{24,28},{28,24},{1,17},{... | collective-permute-start | bytes 6291464 | tf_op jit(solution)/shard_map/ppermute | solution.py:897
  367.8 26.4 %copy-start.7 = (bf16[1024,512]{1,0:T(8,128)(2,1)S(1)}, bf16[1024,512]{1,0:T(8,128)(2,1)}, u32[]{:S(2)}) copy-start(bf16[1024,512]{1,0:T(8,128)(2,1)} %get-tuple-element.198) | copy-start | bytes 3145732
  367.8 26.4 %collective-permute-start.37 = (f32[13824]{0:T(1024)S(1)}, f32[13824]{0:T(1024)S(1)}, u32[]{:S(2)}, u32[]{:S(2)}) collective-permute-start(f32[13824]{0:T(1024)S(1)} %add.113), channel_id=1, source_target_pairs={{0,16},{16,0},{8,24},{24,8},{1,17},{17,1},{9,25},{25,9},{2,18},{18... | collective-permute-start | bytes 165896 | tf_op jit(solution)/shard_map/ppermute | solution.py:854
  369.2 27.5 %collective-permute-start.39 = (bf16[1024,512]{1,0:T(8,128)(2,1)S(1)}, bf16[1024,512]{1,0:T(8,128)(2,1)S(1)}, u32[]{:S(2)}, u32[]{:S(2)}) collective-permute-start(bf16[1024,512]{1,0:T(8,128)(2,1)S(1)} %add_convert_fusion.6), channel_id=1, source_target_pairs={{1,2},{2,1},{5,6},{6,5},{9,10},{10,9},{13,14},{14,13},{17,18},{18,... | collective-permute-start | bytes 3145736 | tf_op jit(solution)/shard_map/ppermute | solution.py:835
  370.0 63.4 %collective-permute-start.43 = (bf16[1024,512]{1,0:T(8,128)(2,1)}, bf16[1024,512]{1,0:T(8,128)(2,1)}, u32[]{:S(2)}, u32[]{:S(2)}) collective-permute-start(bf16[1024,512]{1,0:T(8,128)(2,1)} %fusion.4.refs_0_), channel_id=1, source_target_pairs={{0,1},{3,2},{1,0},{2,3},{4,5},{7,6},{5,4},{6,7},{8,9},{11,10},{9,8... | collective-permute-start | bytes 3145736 | tf_op jit(solution)/shard_map/ppermute | solution.py:825
  398.0 46.6 %collective-permute-start.46 = (bf16[1024,512]{1,0:T(8,128)(2,1)}, bf16[1024,512]{1,0:T(8,128)(2,1)}, u32[]{:S(2)}, u32[]{:S(2)}) collective-permute-start(bf16[1024,512]{1,0:T(8,128)(2,1)} %add_convert_fusion.3.refs_2_), channel_id=1, source_target_pairs={{1,0},{2,3},{5,4},{6,7},{9,8},{10,11},{13,12},{14,15},{17,16},{18,... | collective-permute-start | bytes 3145736 | tf_op jit(solution)/shard_map/ppermute | solution.py:825
  399.3 36.3 %collective-permute-start.44 = (bf16[1024,512]{1,0:T(8,128)(2,1)}, bf16[1024,512]{1,0:T(8,128)(2,1)}, u32[]{:S(2)}, u32[]{:S(2)}) collective-permute-start(bf16[1024,512]{1,0:T(8,128)(2,1)} %add_convert_fusion.4), channel_id=1, source_target_pairs={{1,2},{2,1},{5,6},{6,5},{9,10},{10,9},{13,14},{14,13},{17,18},{18,... | collective-permute-start | bytes 3145736 | tf_op jit(solution)/shard_map/ppermute | solution.py:835
  401.2 21.3 %collective-permute-start.41 = (bf16[1024,2048]{1,0:T(8,128)(2,1)}, bf16[1024,2048]{1,0:T(8,128)(2,1)}, u32[]{:S(2)}, u32[]{:S(2)}) collective-permute-start(bf16[1024,2048]{1,0:T(8,128)(2,1)} %wgrad.8), channel_id=1, source_target_pairs={{0,8},{8,0},{16,24},{24,16},{1,9},{9,1},{17,25},{25,17},{2,10},{10... | collective-permute-start | bytes 12582920 | tf_op jit(solution)/shard_map/ppermute | solution.py:857
  401.3 14.9 %collective-permute-start.40 = (bf16[256,2048]{1,0:T(8,128)(2,1)S(1)}, bf16[256,2048]{1,0:T(8,128)(2,1)S(1)}, u32[]{:S(2)}, u32[]{:S(2)}) collective-permute-start(bf16[256,2048]{1,0:T(8,128)(2,1)S(1)} %copy-done.32), channel_id=1, source_target_pairs={{0,4},{4,0},{8,24},{12,28},{16,20},{20,16},{24,8},{28,12},{1,5},{5... | collective-permute-start | bytes 3145736 | tf_op jit(solution)/shard_map/ppermute | solution.py:897
  421.1 12.3 %copy-start.1 = (bf16[1024,512]{1,0:T(8,128)(2,1)S(1)}, bf16[1024,512]{1,0:T(8,128)(2,1)}, u32[]{:S(2)}) copy-start(bf16[1024,512]{1,0:T(8,128)(2,1)} %get-tuple-element.208) | copy-start | bytes 3145732
  421.1 12.2 %collective-permute-start.42 = (f32[13824]{0:T(1024)S(1)}, f32[13824]{0:T(1024)S(1)}, u32[]{:S(2)}, u32[]{:S(2)}) collective-permute-start(f32[13824]{0:T(1024)S(1)} %add.114), channel_id=1, source_target_pairs={{0,4},{4,0},{1,5},{5,1},{2,6},{6,2},{3,7},{7,3},{8,12},{12,8},{9,1... | collective-permute-start | bytes 165896 | tf_op jit(solution)/shard_map/ppermute | solution.py:860
  434.9 51.1 %collective-permute-start.49 = (bf16[1024,512]{1,0:T(8,128)(2,1)S(1)}, bf16[1024,512]{1,0:T(8,128)(2,1)S(1)}, u32[]{:S(2)}, u32[]{:S(2)}) collective-permute-start(bf16[1024,512]{1,0:T(8,128)(2,1)S(1)} %add_convert_fusion.2), channel_id=1, source_target_pairs={{1,2},{2,1},{5,6},{6,5},{9,10},{10,9},{13,14},{14,13},{17,18},{18,... | collective-permute-start | bytes 3145736 | tf_op jit(solution)/shard_map/ppermute | solution.py:835
  437.5 51.1 %collective-permute-start.48 = (bf16[1024,512]{1,0:T(8,128)(2,1)S(1)}, bf16[1024,512]{1,0:T(8,128)(2,1)}, u32[]{:S(2)}, u32[]{:S(2)}) collective-permute-start(bf16[1024,512]{1,0:T(8,128)(2,1)S(1)} %add_convert_fusion.1.refs_4_), channel_id=1, source_target_pairs={{1,0},{2,3},{5,4},{6,7},{9,8},{10,11},{13,12},{14,15},{17,16},{18,... | collective-permute-start | bytes 3145736 | tf_op jit(solution)/shard_map/ppermute | solution.py:825
  438.8 26.4 %collective-permute-start.45 = (bf16[512,2048]{1,0:T(8,128)(2,1)}, bf16[512,2048]{1,0:T(8,128)(2,1)}, u32[]{:S(2)}, u32[]{:S(2)}) collective-permute-start(bf16[512,2048]{1,0:T(8,128)(2,1)} %get-tuple-element.211), channel_id=1, source_target_pairs={{0,16},{4,20},{8,12},{12,8},{16,0},{20,4},{24,28},{28,24},{1,17},{... | collective-permute-start | bytes 6291464 | tf_op jit(solution)/shard_map/ppermute | solution.py:897
  469.5 19.0 %collective-permute-start.47 = (bf16[256,2048]{1,0:T(8,128)(2,1)}, bf16[256,2048]{1,0:T(8,128)(2,1)}, u32[]{:S(2)}, u32[]{:S(2)}) collective-permute-start(bf16[256,2048]{1,0:T(8,128)(2,1)} %get-tuple-element.216), channel_id=1, source_target_pairs={{0,4},{4,0},{8,24},{12,28},{16,20},{20,16},{24,8},{28,12},{1,5},{5... | collective-permute-start | bytes 3145736 | tf_op jit(solution)/shard_map/ppermute | solution.py:897
  470.8 22.1 %collective-permute-start.50 = (f32[8192]{0:T(1024)S(1)}, f32[8192]{0:T(1024)S(1)}, u32[]{:S(2)}, u32[]{:S(2)}) collective-permute-start(f32[8192]{0:T(1024)S(1)} %slice.40), channel_id=1, source_target_pairs={{0,1},{1,0},{2,3},{3,2},{4,5},{5,4},{6,7},{7,6},{8,9},{9,8},{10,11... | collective-permute-start | bytes 98312 | tf_op jit(solution)/shard_map/ppermute | solution.py:930
  486.0 40.7 %copy-start.16 = (f32[2048]{0:T(1024)}, f32[2048]{0:T(1024)S(1)}, u32[]{:S(2)}) copy-start(f32[2048]{0:T(1024)S(1)} %get-tuple-element.264) | copy-start | bytes 24580
  487.3 25.8 %collective-permute-start.51 = (bf16[1024,512]{1,0:T(8,128)(2,1)}, bf16[1024,512]{1,0:T(8,128)(2,1)S(1)}, u32[]{:S(2)}, u32[]{:S(2)}) collective-permute-start(bf16[1024,512]{1,0:T(8,128)(2,1)} %add_convert_fusion.refs_6_), channel_id=1, source_target_pairs={{1,0},{2,3},{5,4},{6,7},{9,8},{10,11},{13,12},{14,15},{17,16},{18,... | collective-permute-start | bytes 3145736 | tf_op jit(solution)/shard_map/ppermute | solution.py:825
  492.9 33.2 %collective-permute-start.52 = (f32[8192]{0:T(1024)S(1)}, f32[8192]{0:T(1024)S(1)}, u32[]{:S(2)}, u32[]{:S(2)}) collective-permute-start(f32[8192]{0:T(1024)S(1)} %add.122), channel_id=1, source_target_pairs={{0,2},{2,0},{1,3},{3,1},{4,6},{6,4},{5,7},{7,5},{8,10},{10,8},{9,1... | collective-permute-start | bytes 98312 | tf_op jit(solution)/shard_map/ppermute | solution.py:932
  (24 other events, 118.8 us)

commit v4 on v3

--- a/solution.py
+++ b/solution.py
@@ -22,8 +22,7 @@
 COST_SCALE = 20
 
 
-def cost(flops, nbytes, trans=0):
-    k = COST_SCALE
+def cost(flops, nbytes, trans=0, k=COST_SCALE):
     flops = max(flops, 300 * nbytes)
     return pl.CostEstimate(flops=int(k * flops), bytes_accessed=int(k * nbytes), transcendentals=int(k * trans))
 
@@ -471,7 +470,7 @@
     return pl.BlockSpec((256, cols), lambda j: place(j))
 
 
-def out_call(ob, gb, proj, out):
+def out_call(ob, gb, proj, out, scale=COST_SCALE):
     m, f = gb.shape
     nf = ob.shape[1]
     count = len(out)
@@ -490,7 +489,7 @@
         ],
         out_shape=[part, part],
         compiler_params=params(1),
-        cost_estimate=cost(2048 * m * (f + nf), 2 * (m * f + m * nf + 1024 * (f + nf) + 1024 * m)),
+        cost_estimate=cost(2048 * m * (f + nf), 2 * (m * f + m * nf + 1024 * (f + nf) + 1024 * m), k=scale),
     )(ob, gb, *proj, *out)
 
 
@@ -881,6 +880,9 @@
     def waited(self, hop):
         return hop
 
+    def near_pieces(self, near):
+        return near
+
     def near(self, run, own, hop):
         v = run(pack_call, own, hop[1])
         return v, self.core(v)
@@ -950,6 +952,9 @@
 
     def waited(self, hop):
         return (hop,)
+
+    def near_pieces(self, near):
+        return near
 
     def near(self, run, own, hop):
         return hop[:512], hop[1024:1536]
@@ -1050,16 +1055,17 @@
     near3 = comm.near(run, own3, hop3)
     ob, dq, dkv, dpv = run(attn_call, meta, q, kv, pv, dob, tabs, nheads)
     dkv, rv = comm.give_back(dpv, dkv, slots)
-    g3 = comm.pieces(near3, hop3, diag3)
+    g3 = comm.near_pieces(near3)
 
     pipe = comm.pipe(run, meta[1 + NBLK], 8)
     ff = gb.shape[1] // 512
-    out0, out2 = run(out_call, ob, gb, (g1[0], g1[3]), (g3[0], g3[3]))
+    out0, out2 = run(out_call, ob, gb, (g1[0], g1[3]), g3, 0.01)
     pipe.send(out0)
     pipe.send(out2)
+    g3 = comm.pieces(near3, hop3, diag3, (ob, out0))
+    cross3 = comm.scatter_cross(run(wgrad_call, meta, g, gb, half=1))
     far = (1, 2, 4, 5)
     out1, out3 = run(out_call, ob, gb, [g1[k] for k in far], [g3[k] for k in far])
-    cross3 = comm.scatter_cross(run(wgrad_call, meta, g, gb, half=1))
     du, bin_sum = run(dhid_call, g, g3, dg)
     pipe.cross()
     pipe.send(after(out1, *pipe.sums))
@@ -1080,18 +1086,17 @@
     pipe.cross()
     pipe.send(dn2)
     state2 = comm.scatter_own(run, meta, (h2, du), cross2)
+    (grad_out,) = comm.scatter_last(run, ((ff, True),), state3)
     pipe.cross()
     pipe.send(dn3)
     small = jnp.concatenate([gain_sums.reshape(-1), g_sum.reshape(-1), bqkv_sum.reshape(-1), bin_sum.reshape(-1)])
     add = comm.small_sum(run, small, 0)
-    (grad_out,) = comm.scatter_last(run, ((ff, True),), state3)
-    small = add()
-    add = comm.small_sum(run, small, 1)
-    state2 = comm.scatter_half(run, state2)
-    small = add()
     pipe.cross()
     pipe.send()
     cross1 = comm.scatter_cross(after(theirs1, pipe.here[-1]))
+    state2 = comm.scatter_half(run, state2)
+    small = add()
+    add = comm.small_sum(run, small, 1)
 
     def sums_of(order):
         return [v for c in order for v in (pipe.here[c], pipe.sent[c])]
@@ -1101,13 +1106,14 @@
         rows_call, body=functools.partial(block_out_kernel, local_len), name="bout", specs=("row", "vec") + ("part",) * 8
     )
     block_output = run(out_half, *out_ops, steps=(0, 2))
+    small = add()
+    pipe.cross()
+    pipe.send()
     (grad_in,) = comm.scatter_last(run, ((ff, False),), state2)
     add = comm.small_sum(run, after(small, grad_in), 2)
     state1 = comm.scatter_own(run, meta, (h1, dqkv, g, ob), cross1)
+    block_output = run(out_half, *out_ops, steps=(2, 4), into=block_output).reshape(slots, local_len, d)
     small = add()
-    pipe.cross()
-    pipe.send()
-    block_output = run(out_half, *out_ops, steps=(2, 4), into=block_output).reshape(slots, local_len, d)
     gains = small[: 4 * d]
     group = small[4 * d :]
     state1 = comm.scatter_half(run, after(state1, pipe.sent[5]))

time: 535 us -> 513 us (0.959)
  waiting for transfers between devices: 106 us -> 80.2 us
  other arithmetic: 42.2 us -> 48.4 us
    ppermute x6, waiting for transfers between devices: 36.5 us -> 19 us  [turn(): return lax.ppermute(v, ('dp', 'ctx'), pairs)]
    ppermute x11, starting transfers between devices: 34.3 us -> 21.5 us  [send(): got = lax.ppermute(v, 'tensor', pairs)]
    ppermute x7, waiting for transfers between devices: 52.3 us -> 42.6 us  [x(): return lax.ppermute(v, 'dp', [(0, 2), (2, 0), (1, 3), (3, 1)])]
    ppermute x6, starting transfers between devices: 5.5 us -> 13.5 us  [turn(): return lax.ppermute(v, ('dp', 'ctx'), pairs)]
    unnamed x74 -> x68, local copies, waits for them, and re-layouts: 10.5 us -> 12.7 us
  transfers between devices with their start and end apart: 53 -> 53, of which waited for: 12 -> 12; matrix products, arithmetic and copies ran while one was open for 9% -> 10% of each run, Pallas kernels for 50% -> 52%
where the time goes in v4:
time: 513 us; the launch traced here: 506 us
  Pallas kernels  261 us (51%)
  starting transfers between devices  98.1 us (19%)
  waiting for transfers between devices  80.2 us (16%)
  other arithmetic  48.4 us (9%)
  local copies, waits for them, and re-layouts  16.4 us (3%)
    pallas_call x6, Pallas kernels, wgrad_call(): pl.pallas_call(functools.partial(wgrad_kernel, counts, add is not None, s...  59.4 us
    ppermute x7, waiting for transfers between devices, x(): return lax.ppermute(v, 'dp', [(0, 2), (2, 0), (1, 3), (3, 1)])  42.6 us
    pallas_call x2, Pallas kernels, back_call(): pl.pallas_call(back_kernel, name='backn', grid_spec=pltpu.PrefetchScalarG...  32.3 us
    convert_element_type x11, other arithmetic, add_bf(): return lax.optimization_barrier((a.astype(F32) + b.astype(F32)).astype(BF))  25.8 us
    pallas_call x2, Pallas kernels, out_call(): pl.pallas_call(functools.partial(out_kernel, count), name='outp', grid=(4...  22.6 us
    pallas_call x3, Pallas kernels, rows_call(): pl.pallas_call(functools.partial(body, first), name=name, grid_spec=pltpu...  22.4 us
    ppermute x11, starting transfers between devices, send(): got = lax.ppermute(v, 'tensor', pairs)  21.5 us
    ppermute x6, waiting for transfers between devices, turn(): return lax.ppermute(v, ('dp', 'ctx'), pairs)  19 us
  transfers between devices with their start and end apart: 53, of which 12 were waited for; matrix products, arithmetic and copies ran while one was open for 10% of the time, Pallas kernels for 52%

profile of v4, /device:TPU:0, one launch (start us, length us, event | category | flops | bytes accessed | tf_op | source)
XLA Modules:
  0.0 505.8 jit_solution(13598315944211635148)
XLA Ops:
  4.6 3.0 collective-permute-start
  10.7 2.6 copy.32
  15.4 10.5 %norm.1 = (bf16[1024,2048]{1,0:T(8,128)(2,1)}, bf16[1024,2048]{1,0:T(8,128)(2,1)}, f32[1024,128]{1,0:T(8,128)}, f32[1,2048]{1,0:T(1,128)}) custom-call(s32[13]{0:T(128)} %concatenate.10.meta, bf16[1024,2048]{1,0:T(8,128)(2,1)} %bitcast.30, bf16[1024,2048]{1,0:T(8,128)(2,1)} %bitcast.37, f32[1,2048]{1,0:T(1,128)} %bitcast.42, f32[1,2048]{1,0:T(1,128)} %bitcast.39), custom_call_target="tpu_custom_call" | custom-call | flops 125829120000 | bytes 419430400 | tf_op jit(solution)/shard_map/norm/pallas_call | solution.py:127
  26.6 1.9 fusion.5
  28.5 3.4 collective-permute-done.refs_1_
  33.9 3.8 pack.3.w0.refs_0_.w10
  38.2 18.4 %collective-permute-done.3.w2.refs_1_.w12 = bf16[256,2048]{1,0:T(8,128)(2,1)} collective-permute-done((bf16[256,2048]{1,0:T(8,128)(2,1)}, bf16[256,2048]{1,0:T(8,128)(2,1)}, u32[]{:S(2)}, u32[]{:S(2)}) %collective-permute-start.3) | collective-permute-done | bytes 1048608 | tf_op jit(solution)/shard_map/ppermute | solution.py:853
  56.6 3.8 pack.4.w0.w20
  63.8 9.8 %kv.1.kv_ref = bf16[1024,1024]{1,0:T(8,128)(2,1)} custom-call(bf16[1024,2048]{1,0:T(8,128)(2,1)} %get-tuple-element.128.h1.refs_0_, bf16[512,2048]{1,0:T(8,128)(2,1)} %pack.3.w0.refs_0_.w10, bf16[256,2048]{1,0:T(8,128)(2,1)} %copy-done.23, bf16[256,2048]{1,0:T(8,128)(2,1)} %collective-permute-done.3.w2.refs_1_.w12, bf16[512,2048]{1,0:T(8,128)(2,1)} %copy-done.9, ...), custom_call_target="tpu_custom_call" | custom-call | flops 85899345920 | bytes 209715200 | tf_op jit(solution)/shard_map/kv/pallas_call | solution.py:183
  73.5 3.9 collective-permute-start.13
  77.5 8.8 %collective-permute-done.7.w1.w21 = bf16[256,2048]{1,0:T(8,128)(2,1)S(1)} collective-permute-done((bf16[256,2048]{1,0:T(8,128)(2,1)}, bf16[256,2048]{1,0:T(8,128)(2,1)S(1)}, u32[]{:S(2)}, u32[]{:S(2)}) %collective-permute-start.7) | collective-permute-done | bytes 1048608 | tf_op jit(solution)/shard_map/ppermute | solution.py:853
  87.8 10.7 %qd.1 = (bf16[1024,512]{1,0:T(8,128)(2,1)}, bf16[1024,512]{1,0:T(8,128)(2,1)}) custom-call(bf16[1024,2048]{1,0:T(8,128)(2,1)} %get-tuple-element.128.h1.refs_0_, bf16[1024,2048]{1,0:T(8,128)(2,1)} %get-tuple-element.153.g.refs_0_.refs_2_, bf16[512,2048]{1,0:T(8,128)(2,1)} %pack.3.w0.refs_0_.w10, bf16[256,2048]{1,0:T(8,128)(2,1)} %copy-done.23, ...), custom_call_target="tpu_custom_call" | custom-call | flops 88080384000 | bytes 293601280 | tf_op jit(solution)/shard_map/qd/pallas_call | solution.py:224
  98.5 12.4 %collective-permute-done.8.w2.w22 = bf16[256,2048]{1,0:T(8,128)(2,1)} collective-permute-done((bf16[256,2048]{1,0:T(8,128)(2,1)}, bf16[256,2048]{1,0:T(8,128)(2,1)}, u32[]{:S(2)}, u32[]{:S(2)}) %collective-permute-start.8) | collective-permute-done | bytes 1048608 | tf_op jit(solution)/shard_map/ppermute | solution.py:853
  110.9 6.7 %norm2.1.h2.refs_0_ = bf16[1024,2048]{1,0:T(8,128)(2,1)} custom-call(s32[13]{0:T(128)} %concatenate.10.meta, bf16[1024,2048]{1,0:T(8,128)(2,1)} %bitcast.31, f32[1024,128]{1,0:T(8,128)} %get-tuple-element.132.st_ref, f32[1,2048]{1,0:T(1,128)} %bitcast.45, f32[1,2048]{1,0:T(1,128)} %bitcast.40), custom_call_target="tpu_custom_call" | custom-call | flops 50331648000 | bytes 167772160 | tf_op jit(solution)/shard_map/norm2/pallas_call | solution.py:107
  120.4 16.4 %hidden.1 = (bf16[1024,2048]{1,0:T(8,128)(2,1)}, bf16[1024,2048]{1,0:T(8,128)(2,1)}) custom-call(bf16[1024,2048]{1,0:T(8,128)(2,1)} %norm2.1.h2.refs_0_, bf16[512,2048]{1,0:T(8,128)(2,1)} %pack.4.w0.w20, bf16[256,2048]{1,0:T(8,128)(2,1)} %copy-done.26, bf16[256,2048]{1,0:T(8,128)(2,1)} %collective-permute-done.8.w2.w22, ...), custom_call_target="tpu_custom_call" | custom-call | flops 171798691840 | bytes 419430400 | tf_op jit(solution)/shard_map/hidden/pallas_call | solution.py:413
  136.9 3.9 pack.5.refs_2_.w0
  141.0 2.5 collective-permute-done.15.refs_4_.w1
  144.9 12.4 %attn.1 = (bf16[1024,512]{1,0:T(8,128)(2,1)}, bf16[1024,512]{1,0:T(8,128)(2,1)}, f32[1024,1024]{1,0:T(8,128)}, bf16[1024,1024]{1,0:T(8,128)(2,1)}) custom-call(s32[13]{0:T(128)} %concatenate.10.meta, bf16[1024,512]{1,0:T(8,128)(2,1)} %get-tuple-element.130.q_ref, bf16[1024,1024]{1,0:T(8,128)(2,1)} %kv.1.kv_ref, ...), custom_call_target="tpu_custom_call" | custom-call | flops 128849018880 | bytes 209715200 | tf_op jit(solution)/shard_map/attn/pallas_call | solution.py:333
  160.0 10.9 %outp.2 = (bf16[1024,512]{1,0:T(8,128)(2,1)}, bf16[1024,512]{1,0:T(8,128)(2,1)}) custom-call(bf16[1024,512]{1,0:T(8,128)(2,1)} %get-tuple-element.146.ob.refs_3_, bf16[1024,2048]{1,0:T(8,128)(2,1)} %get-tuple-element.138.gb.refs_1_, bf16[512,2048]{1,0:T(8,128)(2,1)} %pack.3.w0.refs_0_.w10, bf16[512,2048]{1,0:T(8,128)(2,1)} %copy-done.9, ...), custom_call_target="tpu_custom_call" | custom-call | flops 53687092 | bytes 125829 | tf_op jit(solution)/shard_map/outp/pallas_call | solution.py:479
  170.9 4.6 collective-permute-start.19
  175.8 9.2 %wgrad.6 = bf16[1024,2048]{1,0:T(8,128)(2,1)} custom-call(s32[13]{0:T(128)} %concatenate.10.meta, bf16[1024,2048]{1,0:T(8,128)(2,1)} %get-tuple-element.153.g.refs_0_.refs_2_, bf16[1024,2048]{1,0:T(8,128)(2,1)} %get-tuple-element.138.gb.refs_1_), custom_call_target="tpu_custom_call" | custom-call | flops 88080384000 | bytes 293601280 | tf_op jit(solution)/shard_map/wgrad/pallas_call | solution.py:602
  185.4 2.3 collective-permute-start.21
  188.7 11.7 %outp.3 = (bf16[1024,512]{1,0:T(8,128)(2,1)}, bf16[1024,512]{1,0:T(8,128)(2,1)}) custom-call(bf16[1024,512]{1,0:T(8,128)(2,1)} %get-tuple-element.146.ob.refs_3_, bf16[1024,2048]{1,0:T(8,128)(2,1)} %get-tuple-element.138.gb.refs_1_, bf16[256,2048]{1,0:T(8,128)(2,1)} %copy-done.23, bf16[256,2048]{1,0:T(8,128)(2,1)} %collective-permute-done.3.w2.refs_1_.w12, ...), custom_call_target="tpu_custom_call" | custom-call | flops 107374182400 | bytes 251658240 | tf_op jit(solution)/shard_map/outp/pallas_call | solution.py:479
  200.4 15.1 %dhid.1 = (bf16[1024,2048]{1,0:T(8,128)(2,1)}, f32[1,2048]{1,0:T(1,128)}) custom-call(bf16[1024,2048]{1,0:T(8,128)(2,1)} %get-tuple-element.153.g.refs_0_.refs_2_, bf16[512,2048]{1,0:T(8,128)(2,1)} %pack.5.refs_2_.w0, bf16[256,2048]{1,0:T(8,128)(2,1)} %collective-permute-done.15.refs_4_.w1, bf16[256,2048]{1,0:T(8,128)(2,1)} %copy-done.28, ...), custom_call_target="tpu_custom_call" | custom-call | flops 171798691840 | bytes 419430400 | tf_op jit(solution)/shard_map/dhid/pallas_call | solution.py:438
  215.5 2.5 add_convert_fusion.15
  219.6 2.3 collective-permute-start.24
  221.9 10.0 %wgrad.7 = (bf16[512,2048]{1,0:T(8,128)(2,1)}, bf16[512,2048]{1,0:T(8,128)(2,1)}) custom-call(s32[13]{0:T(128)} %concatenate.10.meta, bf16[1024,2048]{1,0:T(8,128)(2,1)} %get-tuple-element.153.g.refs_0_.refs_2_, bf16[1024,2048]{1,0:T(8,128)(2,1)} %get-tuple-element.138.gb.refs_1_, bf16[1024,2048]{1,0:T(8,128)(2,1)} %collective-permute-done.20.refs_2_), custom_call_target="tpu_custom_call" | custom-call | flops 88080384000 | bytes 293601280 | tf_op jit(solution)/shard_map/wgrad/pallas_call | solution.py:602
  232.0 2.8 add_convert_fusion.14
  234.8 2.0 collective-permute-start.25
  236.8 6.0 %join.1 = (bf16[1024,1536]{1,0:T(8,128)(2,1)}, f32[1,1536]{1,0:T(1,128)}) custom-call(bf16[1024,512]{1,0:T(8,128)(2,1)} %get-tuple-element.163.dq_ref, f32[1024,1024]{1,0:T(8,128)} %get-tuple-element.164.dkv_ref, bf16[1024,1024]{1,0:T(8,128)(2,1)} %collective-permute-done.22.rv_ref, f32[512,128]{1,0:T(8,128)} %get-tuple-element.238.cosf, ...), custom_call_target="tpu_custom_call" | custom-call | flops 75497472000 | bytes 251658240 | tf_op jit(solution)/shard_map/join/pallas_call | solution.py:388
  242.9 2.9 fusion.refs_0_
  247.7 16.0 %backn.2 = (bf16[1024,512]{1,0:T(8,128)(2,1)}, bf16[1024,512]{1,0:T(8,128)(2,1)}, f32[4,2048]{1,0:T(4,128)}) custom-call(s32[13]{0:T(128)} %concatenate.10.meta, bf16[1024,1536]{1,0:T(8,128)(2,1)} %get-tuple-element.166.dqkv.refs_1_, bf16[1024,2048]{1,0:T(8,128)(2,1)} %get-tuple-element.155.du.refs_1_, ...), custom_call_target="tpu_custom_call", output_to_operand_aliasing={{2}: (13, {})} | custom-call | flops 150323855360 | bytes 377487360 | tf_op jit(solution)/shard_map/backn/pallas_call | solution.py:523
  263.7 2.9 add_convert_fusion.12
  268.2 3.0 fusion.1.refs_4_
  271.2 3.1 collective-permute-start.30
  274.3 4.4 hsum.3
  278.6 9.6 %collective-permute-start.28 = (bf16[256,2048]{1,0:T(8,128)(2,1)}, bf16[256,2048]{1,0:T(8,128)(2,1)S(1)}, u32[]{:S(2)}, u32[]{:S(2)}) collective-permute-start(bf16[256,2048]{1,0:T(8,128)(2,1)} %get-tuple-element.177), channel_id=1, source_target_pairs={{0,4},{4,0},{8,24},{12,28},{16,20},{20,16},{24,8},{28,12},{1,5},{5... | collective-permute-start | bytes 3145736 | tf_op jit(solution)/shard_map/ppermute | solution.py:899
  288.3 10.2 %wgrad.8 = bf16[1024,2048]{1,0:T(8,128)(2,1)} custom-call(s32[13]{0:T(128)} %concatenate.10.meta, bf16[1024,2048]{1,0:T(8,128)(2,1)} %get-tuple-element.128.h1.refs_0_, bf16[1024,1536]{1,0:T(8,128)(2,1)} %get-tuple-element.166.dqkv.refs_1_, bf16[1024,2048]{1,0:T(8,128)(2,1)} %get-tuple-element.153.g.refs_0_.refs_2_, ...), custom_call_target="tpu_custom_call" | custom-call | flops 100663296000 | bytes 335544320 | tf_op jit(solution)/shard_map/wgrad/pallas_call | solution.py:602
  298.5 2.6 add_convert_fusion.10
  302.9 2.9 fusion.2.refs_2_
  307.6 9.2 %wgrad.9 = bf16[1024,2048]{1,0:T(8,128)(2,1)} custom-call(s32[13]{0:T(128)} %concatenate.10.meta, bf16[1024,2048]{1,0:T(8,128)(2,1)} %norm2.1.h2.refs_0_, bf16[1024,2048]{1,0:T(8,128)(2,1)} %get-tuple-element.155.du.refs_1_), custom_call_target="tpu_custom_call" | custom-call | flops 88080384000 | bytes 293601280 | tf_op jit(solution)/shard_map/wgrad/pallas_call | solution.py:602
  316.7 16.3 %backn.3 = (bf16[1024,512]{1,0:T(8,128)(2,1)}, bf16[1024,512]{1,0:T(8,128)(2,1)}, f32[4,2048]{1,0:T(4,128)}) custom-call(s32[13]{0:T(128)} %concatenate.10.meta, bf16[1024,1536]{1,0:T(8,128)(2,1)} %get-tuple-element.166.dqkv.refs_1_, bf16[1024,2048]{1,0:T(8,128)(2,1)} %get-tuple-element.155.du.refs_1_, ...), custom_call_target="tpu_custom_call", output_to_operand_aliasing={{2}: (13, {})} | custom-call | flops 150323855360 | bytes 377487360 | tf_op jit(solution)/shard_map/backn/pallas_call | solution.py:523
  333.1 2.5 add_convert_fusion.8
  337.3 2.9 fusion.3.refs_6_
  341.2 10.0 %wgrad.10 = (bf16[512,2048]{1,0:T(8,128)(2,1)}, bf16[512,2048]{1,0:T(8,128)(2,1)}) custom-call(s32[13]{0:T(128)} %concatenate.10.meta, bf16[1024,2048]{1,0:T(8,128)(2,1)} %norm2.1.h2.refs_0_, bf16[1024,2048]{1,0:T(8,128)(2,1)} %get-tuple-element.155.du.refs_1_, bf16[1024,2048]{1,0:T(8,128)(2,1)} %collective-permute-done.32.refs_2_), custom_call_target="tpu_custom_call" | custom-call | flops 88080384000 | bytes 293601280 | tf_op jit(solution)/shard_map/wgrad/pallas_call | solution.py:602
  352.8 4.3 lsum.3
  357.2 2.6 add_convert_fusion.6
  362.2 2.9 fusion.4.refs_0_
  369.4 2.8 add_convert_fusion.3.refs_2_
  372.5 5.1 %collective-permute-done.37.got = bf16[512,2048]{1,0:T(8,128)(2,1)} collective-permute-done((bf16[512,2048]{1,0:T(8,128)(2,1)}, bf16[512,2048]{1,0:T(8,128)(2,1)}, u32[]{:S(2)}, u32[]{:S(2)}) %collective-permute-start.37) | collective-permute-done | bytes 2097184 | tf_op jit(solution)/shard_map/ppermute | solution.py:899
  377.5 4.4 hsum.4
  383.8 5.3 %bout.2.refs_8_ = bf16[1024,2048]{1,0:T(8,128)(2,1)} custom-call(s32[13]{0:T(128)} %concatenate.10.meta, bf16[1024,2048]{1,0:T(8,128)(2,1)} %bitcast.34, f32[1,2048]{1,0:T(1,128)} %bitcast.28, bf16[1024,512]{1,0:T(8,128)(2,1)} %fusion.refs_0_, bf16[1024,512]{1,0:T(8,128)(2,1)} %collective-permute-done.27.refs_1_, bf16[1024,512]{1,0:T(8,128)(2,1)} %fusion.2.refs_2_, ...), custom_call_target="tpu_custom_call" | custom-call | flops 50331648000 | bytes 167772160 | tf_op jit(solution)/shard_map/bout/pallas_call | solution.py:762
  391.1 2.5 add_convert_fusion.2
  398.8 4.0 lsum.4
  403.6 10.8 %wgrad.11 = (bf16[512,2048]{1,0:T(8,128)(2,1)}, bf16[512,2048]{1,0:T(8,128)(2,1)}) custom-call(s32[13]{0:T(128)} %concatenate.10.meta, bf16[1024,2048]{1,0:T(8,128)(2,1)} %get-tuple-element.128.h1.refs_0_, bf16[1024,1536]{1,0:T(8,128)(2,1)} %get-tuple-element.166.dqkv.refs_1_, bf16[1024,2048]{1,0:T(8,128)(2,1)} %get-tuple-element.153.g.refs_0_.refs_2_, ...), custom_call_target="tpu_custom_call" | custom-call | flops 100663296000 | bytes 335544320 | tf_op jit(solution)/shard_map/wgrad/pallas_call | solution.py:602
  414.8 5.1 %bout.3 = bf16[1024,2048]{1,0:T(8,128)(2,1)} custom-call(s32[13]{0:T(128)} %concatenate.10.meta, bf16[1024,2048]{1,0:T(8,128)(2,1)} %bitcast.35, f32[1,2048]{1,0:T(1,128)} %bitcast.29, bf16[1024,512]{1,0:T(8,128)(2,1)} %fusion.refs_0_, bf16[1024,512]{1,0:T(8,128)(2,1)} %collective-permute-done.27.refs_1_, ...), custom_call_target="tpu_custom_call", output_to_operand_aliasing={{}: (11, {})} | custom-call | flops 50331648000 | bytes 167772160 | tf_op jit(solution)/shard_map/bout/pallas_call | solution.py:762
  420.7 7.1 %collective-permute-done.46.refs_3_ = bf16[1024,512]{1,0:T(8,128)(2,1)} collective-permute-done((bf16[1024,512]{1,0:T(8,128)(2,1)}, bf16[1024,512]{1,0:T(8,128)(2,1)}, u32[]{:S(2)}, u32[]{:S(2)}) %collective-permute-start.46) | collective-permute-done | bytes 1048608 | tf_op jit(solution)/shard_map/ppermute | solution.py:824
  427.8 12.9 %collective-permute-done.45.got = bf16[512,2048]{1,0:T(8,128)(2,1)S(1)} collective-permute-done((bf16[512,2048]{1,0:T(8,128)(2,1)}, bf16[512,2048]{1,0:T(8,128)(2,1)S(1)}, u32[]{:S(2)}, u32[]{:S(2)}) %collective-permute-start.45) | collective-permute-done | bytes 2097184 | tf_op jit(solution)/shard_map/ppermute | solution.py:899
  442.0 4.4 hsum.5
  448.1 15.2 %collective-permute-start.50 = (f32[8192]{0:T(1024)S(1)}, f32[8192]{0:T(1024)S(1)}, u32[]{:S(2)}, u32[]{:S(2)}) collective-permute-start(f32[8192]{0:T(1024)S(1)} %slice.40), channel_id=1, source_target_pairs={{0,1},{1,0},{2,3},{3,2},{4,5},{5,4},{6,7},{7,6},{8,9},{9,8},{10,11... | collective-permute-start | bytes 98312 | tf_op jit(solution)/shard_map/ppermute | solution.py:932
  468.0 4.3 lsum.5
  472.3 11.1 %collective-permute-start.52 = (f32[8192]{0:T(1024)S(1)}, f32[8192]{0:T(1024)S(1)}, u32[]{:S(2)}, u32[]{:S(2)}) collective-permute-start(f32[8192]{0:T(1024)S(1)} %add.122), channel_id=1, source_target_pairs={{0,2},{2,0},{1,3},{3,1},{4,6},{6,4},{5,7},{7,5},{8,10},{10,8},{9,1... | collective-permute-start | bytes 98312 | tf_op jit(solution)/shard_map/ppermute | solution.py:934
  483.4 7.9 %collective-permute-done.51.refs_7_ = bf16[1024,512]{1,0:T(8,128)(2,1)S(1)} collective-permute-done((bf16[1024,512]{1,0:T(8,128)(2,1)S(1)}, bf16[1024,512]{1,0:T(8,128)(2,1)S(1)}, u32[]{:S(2)}, u32[]{:S(2)}) %collective-permute-start.51) | collective-permute-done | bytes 1048608 | tf_op jit(solution)/shard_map/ppermute | solution.py:824
  492.4 12.0 %igrad.1 = bf16[1024,2048]{1,0:T(8,128)(2,1)} custom-call(s32[13]{0:T(128)} %concatenate.10.meta, bf16[1024,2048]{1,0:T(8,128)(2,1)} %bitcast.36, bf16[1024,2048]{1,0:T(8,128)(2,1)} %bitcast.38, f32[1024,128]{1,0:T(8,128)} %get-tuple-element.132.st_ref, bf16[1024,512]{1,0:T(8,128)(2,1)} %fusion.4.refs_0_, bf16[1024,512]{1,0:T(8,128)(2,1)} %collective-permute-done.40.refs_1_, ...), custom_call_target="tpu_custom_call" | custom-call | flops 100663296000 | bytes 335544320 | tf_op jit(solution)/shard_map/igrad/pallas_call | solution.py:762
  (180 shorter events, 67.1 us)
Async XLA Ops:
  0.6 8.4 %copy-start.8 = (f32[256,2048]{1,0:T(8,128)S(1)}, f32[256,2048]{1,0:T(8,128)}, u32[]{:S(2)}) copy-start(f32[256,2048]{1,0:T(8,128)} %param.26) | copy-start | bytes 6291460
  4.6 27.3 %collective-permute-start = (bf16[256,2048]{1,0:T(8,128)(2,1)}, bf16[256,2048]{1,0:T(8,128)(2,1)}, u32[]{:S(2)}, u32[]{:S(2)}) collective-permute-start(bf16[256,2048]{1,0:T(8,128)(2,1)} %pad_maximum_fusion.refs_0_), channel_id=1, source_target_pairs={{0,4},{4,0},{1,5},{5,1},{2,6},{6,2},{3,7},{7,3},{8,12},{12,8},{9,1... | collective-permute-start | bytes 3145736 | tf_op jit(solution)/shard_map/ppermute | solution.py:859
  7.6 24.8 %collective-permute-start.2 = (bf16[256,2048]{1,0:T(8,128)(2,1)}, bf16[256,2048]{1,0:T(8,128)(2,1)S(1)}, u32[]{:S(2)}, u32[]{:S(2)}) collective-permute-start(bf16[256,2048]{1,0:T(8,128)(2,1)} %pad_maximum_fusion.refs_0_), channel_id=1, source_target_pairs={{0,16},{16,0},{8,24},{24,8},{1,17},{17,1},{9,25},{25,9},{2,18},{18... | collective-permute-start | bytes 3145736 | tf_op jit(solution)/shard_map/ppermute | solution.py:853
  10.2 46.4 %collective-permute-start.1 = (bf16[256,2048]{1,0:T(8,128)(2,1)}, bf16[256,2048]{1,0:T(8,128)(2,1)}, u32[]{:S(2)}, u32[]{:S(2)}) collective-permute-start(bf16[256,2048]{1,0:T(8,128)(2,1)} %convert_element_type.174.refs_0_), channel_id=1, source_target_pairs={{0,4},{4,0},{1,5},{5,1},{2,6},{6,2},{3,7},{7,3},{8,12},{12,8},{9,1... | collective-permute-start | bytes 3145736 | tf_op jit(solution)/shard_map/ppermute | solution.py:859
  13.3 123.6 %collective-permute-start.12 = (bf16[256,2048]{1,0:T(8,128)(2,1)}, bf16[256,2048]{1,0:T(8,128)(2,1)}, u32[]{:S(2)}, u32[]{:S(2)}) collective-permute-start(bf16[256,2048]{1,0:T(8,128)(2,1)} %bitcast.21.refs_0_), channel_id=1, source_target_pairs={{0,4},{4,0},{1,5},{5,1},{2,6},{6,2},{3,7},{7,3},{8,12},{12,8},{9,1... | collective-permute-start | bytes 3145736 | tf_op jit(solution)/shard_map/ppermute | solution.py:859
  15.4 10.5 %copy-start.19 = (f32[1536]{0:T(1024)S(1)}, f32[1536]{0:T(1024)}, u32[]{:S(2)}) copy-start(f32[1536]{0:T(1024)} %param.23) | copy-start | bytes 18436
  32.4 24.2 %collective-permute-start.3 = (bf16[256,2048]{1,0:T(8,128)(2,1)}, bf16[256,2048]{1,0:T(8,128)(2,1)}, u32[]{:S(2)}, u32[]{:S(2)}) collective-permute-start(bf16[256,2048]{1,0:T(8,128)(2,1)} %collective-permute-done.refs_1_), channel_id=1, source_target_pairs={{0,16},{16,0},{8,24},{24,8},{1,17},{17,1},{9,25},{25,9},{2,18},{18... | collective-permute-start | bytes 3145736 | tf_op jit(solution)/shard_map/ppermute | solution.py:853
  37.7 24.8 %collective-permute-start.4 = (bf16[512,2048]{1,0:T(8,128)(2,1)}, bf16[512,2048]{1,0:T(8,128)(2,1)S(1)}, u32[]{:S(2)}, u32[]{:S(2)}) collective-permute-start(bf16[512,2048]{1,0:T(8,128)(2,1)} %pack.3.w0.refs_0_.w10), channel_id=1, source_target_pairs={{0,8},{8,0},{16,24},{24,16},{1,9},{9,1},{17,25},{25,17},{2,10},{10... | collective-permute-start | bytes 6291464 | tf_op jit(solution)/shard_map/ppermute | solution.py:856
  37.7 23.3 %collective-permute-start.5 = (bf16[256,2048]{1,0:T(8,128)(2,1)S(1)}, bf16[256,2048]{1,0:T(8,128)(2,1)}, u32[]{:S(2)}, u32[]{:S(2)}) collective-permute-start(bf16[256,2048]{1,0:T(8,128)(2,1)S(1)} %collective-permute-done.2.w1.refs_0_.w11), channel_id=1, source_target_pairs={{0,8},{8,0},{16,24},{24,16},{1,9},{9,1},{17,25},{25,17},{2,10},{10... | collective-permute-start | bytes 3145736 | tf_op jit(solution)/shard_map/ppermute | solution.py:856
  56.6 5.8 %collective-permute-start.6 = (bf16[256,2048]{1,0:T(8,128)(2,1)}, bf16[256,2048]{1,0:T(8,128)(2,1)}, u32[]{:S(2)}, u32[]{:S(2)}) collective-permute-start(bf16[256,2048]{1,0:T(8,128)(2,1)} %collective-permute-done.3.w2.refs_1_.w12), channel_id=1, source_target_pairs={{0,8},{8,0},{16,24},{24,16},{1,9},{9,1},{17,25},{25,17},{2,10},{10... | collective-permute-start | bytes 3145736 | tf_op jit(solution)/shard_map/ppermute | solution.py:856
  60.4 57.1 %collective-permute-start.9 = (bf16[512,2048]{1,0:T(8,128)(2,1)}, bf16[512,2048]{1,0:T(8,128)(2,1)}, u32[]{:S(2)}, u32[]{:S(2)}) collective-permute-start(bf16[512,2048]{1,0:T(8,128)(2,1)} %pack.4.w0.w20), channel_id=1, source_target_pairs={{0,8},{8,0},{16,24},{24,16},{1,9},{9,1},{17,25},{25,17},{2,10},{10... | collective-permute-start | bytes 6291464 | tf_op jit(solution)/shard_map/ppermute | solution.py:856
  61.0 25.3 %collective-permute-start.7 = (bf16[256,2048]{1,0:T(8,128)(2,1)}, bf16[256,2048]{1,0:T(8,128)(2,1)S(1)}, u32[]{:S(2)}, u32[]{:S(2)}) collective-permute-start(bf16[256,2048]{1,0:T(8,128)(2,1)} %convert_element_type.174.refs_0_), channel_id=1, source_target_pairs={{0,16},{16,0},{8,24},{24,8},{1,17},{17,1},{9,25},{25,9},{2,18},{18... | collective-permute-start | bytes 3145736 | tf_op jit(solution)/shard_map/ppermute | solution.py:853
  73.5 71.4 %collective-permute-start.13 = (bf16[1024,1024]{1,0:T(8,128)(2,1)}, bf16[1024,1024]{1,0:T(8,128)(2,1)}, u32[]{:S(2)}, u32[]{:S(2)}) collective-permute-start(bf16[1024,1024]{1,0:T(8,128)(2,1)} %kv.1.kv_ref), channel_id=1, source_target_pairs={{0,4},{1,5},{2,6},{3,7},{8,12},{9,13},{10,14},{11,15},{16,20},{17,... | collective-permute-start | bytes 6291464 | tf_op jit(solution)/shard_map/ppermute | solution.py:916
  86.3 12.2 %copy-start.26 = (bf16[256,2048]{1,0:T(8,128)(2,1)}, bf16[256,2048]{1,0:T(8,128)(2,1)S(1)}, u32[]{:S(2)}) copy-start(bf16[256,2048]{1,0:T(8,128)(2,1)S(1)} %collective-permute-done.7.w1.w21) | copy-start | bytes 3145732
  86.3 24.6 %collective-permute-start.8 = (bf16[256,2048]{1,0:T(8,128)(2,1)}, bf16[256,2048]{1,0:T(8,128)(2,1)}, u32[]{:S(2)}, u32[]{:S(2)}) collective-permute-start(bf16[256,2048]{1,0:T(8,128)(2,1)} %collective-permute-done.1.refs_1_), channel_id=1, source_target_pairs={{0,16},{16,0},{8,24},{24,8},{1,17},{17,1},{9,25},{25,9},{2,18},{18... | collective-permute-start | bytes 3145736 | tf_op jit(solution)/shard_map/ppermute | solution.py:853
  87.8 31.3 %collective-permute-start.10 = (bf16[256,2048]{1,0:T(8,128)(2,1)S(1)}, bf16[256,2048]{1,0:T(8,128)(2,1)S(1)}, u32[]{:S(2)}, u32[]{:S(2)}) collective-permute-start(bf16[256,2048]{1,0:T(8,128)(2,1)S(1)} %collective-permute-done.7.w1.w21), channel_id=1, source_target_pairs={{0,8},{8,0},{16,24},{24,16},{1,9},{9,1},{17,25},{25,17},{2,10},{10... | collective-permute-start | bytes 3145736 | tf_op jit(solution)/shard_map/ppermute | solution.py:856
  110.9 8.2 %collective-permute-start.11 = (bf16[256,2048]{1,0:T(8,128)(2,1)}, bf16[256,2048]{1,0:T(8,128)(2,1)S(1)}, u32[]{:S(2)}, u32[]{:S(2)}) collective-permute-start(bf16[256,2048]{1,0:T(8,128)(2,1)} %collective-permute-done.8.w2.w22), channel_id=1, source_target_pairs={{0,8},{8,0},{16,24},{24,16},{1,9},{9,1},{17,25},{25,17},{2,10},{10... | collective-permute-start | bytes 3145736 | tf_op jit(solution)/shard_map/ppermute | solution.py:856
  117.6 25.9 %collective-permute-start.15 = (bf16[256,2048]{1,0:T(8,128)(2,1)}, bf16[256,2048]{1,0:T(8,128)(2,1)}, u32[]{:S(2)}, u32[]{:S(2)}) collective-permute-start(bf16[256,2048]{1,0:T(8,128)(2,1)} %bitcast.21.refs_0_), channel_id=1, source_target_pairs={{0,16},{16,0},{8,24},{24,8},{1,17},{17,1},{9,25},{25,9},{2,18},{18... | collective-permute-start | bytes 3145736 | tf_op jit(solution)/shard_map/ppermute | solution.py:853
  140.8 18.0 %collective-permute-start.14 = (bf16[512,2048]{1,0:T(8,128)(2,1)}, bf16[512,2048]{1,0:T(8,128)(2,1)S(1)}, u32[]{:S(2)}, u32[]{:S(2)}) collective-permute-start(bf16[512,2048]{1,0:T(8,128)(2,1)} %pack.5.refs_2_.w0), channel_id=1, source_target_pairs={{0,8},{8,0},{16,24},{24,16},{1,9},{9,1},{17,25},{25,17},{2,10},{10... | collective-permute-start | bytes 6291464 | tf_op jit(solution)/shard_map/ppermute | solution.py:856
  143.4 32.1 %collective-permute-start.16 = (bf16[256,2048]{1,0:T(8,128)(2,1)}, bf16[256,2048]{1,0:T(8,128)(2,1)S(1)}, u32[]{:S(2)}, u32[]{:S(2)}) collective-permute-start(bf16[256,2048]{1,0:T(8,128)(2,1)} %collective-permute-done.12.refs_1_), channel_id=1, source_target_pairs={{0,16},{16,0},{8,24},{24,8},{1,17},{17,1},{9,25},{25,9},{2,18},{18... | collective-permute-start | bytes 3145736 | tf_op jit(solution)/shard_map/ppermute | solution.py:853
  157.3 28.0 %collective-permute-start.17 = (bf16[256,2048]{1,0:T(8,128)(2,1)}, bf16[256,2048]{1,0:T(8,128)(2,1)}, u32[]{:S(2)}, u32[]{:S(2)}) collective-permute-start(bf16[256,2048]{1,0:T(8,128)(2,1)} %collective-permute-done.15.refs_4_.w1), channel_id=1, source_target_pairs={{0,8},{8,0},{16,24},{24,16},{1,9},{9,1},{17,25},{25,17},{2,10},{10... | collective-permute-start | bytes 3145736 | tf_op jit(solution)/shard_map/ppermute | solution.py:856
  157.4 79.4 %collective-permute-start.22 = (bf16[1024,1024]{1,0:T(8,128)(2,1)}, bf16[1024,1024]{1,0:T(8,128)(2,1)}, u32[]{:S(2)}, u32[]{:S(2)}) collective-permute-start(bf16[1024,1024]{1,0:T(8,128)(2,1)} %get-tuple-element.165), channel_id=1, source_target_pairs={{4,0},{5,1},{6,2},{7,3},{12,8},{13,9},{14,10},{15,11},{20,16},{21,... | collective-permute-start | bytes 6291464 | tf_op jit(solution)/shard_map/ppermute | solution.py:919
  170.9 44.6 %collective-permute-start.19 = (bf16[1024,512]{1,0:T(8,128)(2,1)}, bf16[1024,512]{1,0:T(8,128)(2,1)}, u32[]{:S(2)}, u32[]{:S(2)}) collective-permute-start(bf16[1024,512]{1,0:T(8,128)(2,1)} %get-tuple-element.156), channel_id=1, source_target_pairs={{0,1},{3,2},{4,5},{7,6},{8,9},{11,10},{12,13},{15,14},{16,17},{19,... | collective-permute-start | bytes 3145736 | tf_op jit(solution)/shard_map/ppermute | solution.py:824
  175.5 9.5 %copy-start.28 = (bf16[256,2048]{1,0:T(8,128)(2,1)}, bf16[256,2048]{1,0:T(8,128)(2,1)S(1)}, u32[]{:S(2)}) copy-start(bf16[256,2048]{1,0:T(8,128)(2,1)S(1)} %collective-permute-done.16.refs_5_.w2) | copy-start | bytes 3145732
  175.6 12.1 %collective-permute-start.18 = (bf16[256,2048]{1,0:T(8,128)(2,1)S(1)}, bf16[256,2048]{1,0:T(8,128)(2,1)S(1)}, u32[]{:S(2)}, u32[]{:S(2)}) collective-permute-start(bf16[256,2048]{1,0:T(8,128)(2,1)S(1)} %collective-permute-done.16.refs_5_.w2), channel_id=1, source_target_pairs={{0,8},{8,0},{16,24},{24,16},{1,9},{9,1},{17,25},{25,17},{2,10},{10... | collective-permute-start | bytes 3145736 | tf_op jit(solution)/shard_map/ppermute | solution.py:856
  185.0 36.9 %collective-permute-start.20 = (bf16[1024,2048]{1,0:T(8,128)(2,1)}, bf16[1024,2048]{1,0:T(8,128)(2,1)}, u32[]{:S(2)}, u32[]{:S(2)}) collective-permute-start(bf16[1024,2048]{1,0:T(8,128)(2,1)} %wgrad.6), channel_id=1, source_target_pairs={{0,8},{8,0},{16,24},{24,16},{1,9},{9,1},{17,25},{25,17},{2,10},{10... | collective-permute-start | bytes 12582920 | tf_op jit(solution)/shard_map/ppermute | solution.py:856
  185.4 46.6 %collective-permute-start.21 = (bf16[1024,512]{1,0:T(8,128)(2,1)}, bf16[1024,512]{1,0:T(8,128)(2,1)}, u32[]{:S(2)}, u32[]{:S(2)}) collective-permute-start(bf16[1024,512]{1,0:T(8,128)(2,1)} %get-tuple-element.160), channel_id=1, source_target_pairs={{0,1},{3,2},{4,5},{7,6},{8,9},{11,10},{12,13},{15,14},{16,17},{19,... | collective-permute-start | bytes 3145736 | tf_op jit(solution)/shard_map/ppermute | solution.py:824
  200.4 15.2 %copy-start.11 = (bf16[1024,512]{1,0:T(8,128)(2,1)S(1)}, bf16[1024,512]{1,0:T(8,128)(2,1)}, u32[]{:S(2)}) copy-start(bf16[1024,512]{1,0:T(8,128)(2,1)} %get-tuple-element.156) | copy-start | bytes 3145732
  218.0 24.9 %collective-permute-start.23 = (bf16[1024,512]{1,0:T(8,128)(2,1)}, bf16[1024,512]{1,0:T(8,128)(2,1)}, u32[]{:S(2)}, u32[]{:S(2)}) collective-permute-start(bf16[1024,512]{1,0:T(8,128)(2,1)} %add_convert_fusion.15), channel_id=1, source_target_pairs={{1,2},{2,1},{5,6},{6,5},{9,10},{10,9},{13,14},{14,13},{17,18},{18,... | collective-permute-start | bytes 3145736 | tf_op jit(solution)/shard_map/ppermute | solution.py:834
  219.6 44.1 %collective-permute-start.24 = (bf16[1024,512]{1,0:T(8,128)(2,1)}, bf16[1024,512]{1,0:T(8,128)(2,1)}, u32[]{:S(2)}, u32[]{:S(2)}) collective-permute-start(bf16[1024,512]{1,0:T(8,128)(2,1)} %get-tuple-element.170), channel_id=1, source_target_pairs={{0,1},{3,2},{4,5},{7,6},{8,9},{11,10},{12,13},{15,14},{16,17},{19,... | collective-permute-start | bytes 3145736 | tf_op jit(solution)/shard_map/ppermute | solution.py:824
  234.8 33.4 %collective-permute-start.25 = (bf16[1024,512]{1,0:T(8,128)(2,1)}, bf16[1024,512]{1,0:T(8,128)(2,1)}, u32[]{:S(2)}, u32[]{:S(2)}) collective-permute-start(bf16[1024,512]{1,0:T(8,128)(2,1)} %add_convert_fusion.14), channel_id=1, source_target_pairs={{1,2},{2,1},{5,6},{6,5},{9,10},{10,9},{13,14},{14,13},{17,18},{18,... | collective-permute-start | bytes 3145736 | tf_op jit(solution)/shard_map/ppermute | solution.py:834
  236.8 6.0 %copy-start.1 = (bf16[1024,512]{1,0:T(8,128)(2,1)S(1)}, bf16[1024,512]{1,0:T(8,128)(2,1)}, u32[]{:S(2)}) copy-start(bf16[1024,512]{1,0:T(8,128)(2,1)} %get-tuple-element.176) | copy-start | bytes 3145732
  245.8 52.6 %collective-permute-start.27 = (bf16[1024,512]{1,0:T(8,128)(2,1)}, bf16[1024,512]{1,0:T(8,128)(2,1)}, u32[]{:S(2)}, u32[]{:S(2)}) collective-permute-start(bf16[1024,512]{1,0:T(8,128)(2,1)} %fusion.refs_0_), channel_id=1, source_target_pairs={{0,1},{3,2},{1,0},{2,3},{4,5},{7,6},{5,4},{6,7},{8,9},{11,10},{9,8... | collective-permute-start | bytes 3145736 | tf_op jit(solution)/shard_map/ppermute | solution.py:824
  246.6 27.7 %collective-permute-start.26 = (bf16[512,2048]{1,0:T(8,128)(2,1)}, bf16[512,2048]{1,0:T(8,128)(2,1)}, u32[]{:S(2)}, u32[]{:S(2)}) collective-permute-start(bf16[512,2048]{1,0:T(8,128)(2,1)} %get-tuple-element.173), channel_id=1, source_target_pairs={{0,16},{4,20},{8,12},{12,8},{16,0},{20,4},{24,28},{28,24},{1,17},{... | collective-permute-start | bytes 6291464 | tf_op jit(solution)/shard_map/ppermute | solution.py:899
  266.6 36.3 %collective-permute-start.29 = (bf16[1024,512]{1,0:T(8,128)(2,1)}, bf16[1024,512]{1,0:T(8,128)(2,1)}, u32[]{:S(2)}, u32[]{:S(2)}) collective-permute-start(bf16[1024,512]{1,0:T(8,128)(2,1)} %add_convert_fusion.12), channel_id=1, source_target_pairs={{1,2},{2,1},{5,6},{6,5},{9,10},{10,9},{13,14},{14,13},{17,18},{18,... | collective-permute-start | bytes 3145736 | tf_op jit(solution)/shard_map/ppermute | solution.py:834
  271.2 61.9 %collective-permute-start.30 = (bf16[1024,512]{1,0:T(8,128)(2,1)}, bf16[1024,512]{1,0:T(8,128)(2,1)}, u32[]{:S(2)}, u32[]{:S(2)}) collective-permute-start(bf16[1024,512]{1,0:T(8,128)(2,1)} %fusion.1.refs_4_), channel_id=1, source_target_pairs={{0,1},{3,2},{1,0},{2,3},{4,5},{7,6},{5,4},{6,7},{8,9},{11,10},{9,8... | collective-permute-start | bytes 3145736 | tf_op jit(solution)/shard_map/ppermute | solution.py:824
  278.6 19.8 %copy-start.2 = (bf16[1024,512]{1,0:T(8,128)(2,1)S(1)}, bf16[1024,512]{1,0:T(8,128)(2,1)}, u32[]{:S(2)}) copy-start(bf16[1024,512]{1,0:T(8,128)(2,1)} %get-tuple-element.176) | copy-start | bytes 3145732
  278.6 28.9 %collective-permute-start.28 = (bf16[256,2048]{1,0:T(8,128)(2,1)}, bf16[256,2048]{1,0:T(8,128)(2,1)S(1)}, u32[]{:S(2)}, u32[]{:S(2)}) collective-permute-start(bf16[256,2048]{1,0:T(8,128)(2,1)} %get-tuple-element.177), channel_id=1, source_target_pairs={{0,4},{4,0},{8,24},{12,28},{16,20},{20,16},{24,8},{28,12},{1,5},{5... | collective-permute-start | bytes 3145736 | tf_op jit(solution)/shard_map/ppermute | solution.py:899
  301.0 36.3 %collective-permute-start.31 = (bf16[1024,512]{1,0:T(8,128)(2,1)}, bf16[1024,512]{1,0:T(8,128)(2,1)}, u32[]{:S(2)}, u32[]{:S(2)}) collective-permute-start(bf16[1024,512]{1,0:T(8,128)(2,1)} %add_convert_fusion.10), channel_id=1, source_target_pairs={{1,2},{2,1},{5,6},{6,5},{9,10},{10,9},{13,14},{14,13},{17,18},{18,... | collective-permute-start | bytes 3145736 | tf_op jit(solution)/shard_map/ppermute | solution.py:834
  305.8 51.4 %collective-permute-start.33 = (bf16[1024,512]{1,0:T(8,128)(2,1)}, bf16[1024,512]{1,0:T(8,128)(2,1)}, u32[]{:S(2)}, u32[]{:S(2)}) collective-permute-start(bf16[1024,512]{1,0:T(8,128)(2,1)} %fusion.2.refs_2_), channel_id=1, source_target_pairs={{0,1},{3,2},{1,0},{2,3},{4,5},{7,6},{5,4},{6,7},{8,9},{11,10},{9,8... | collective-permute-start | bytes 3145736 | tf_op jit(solution)/shard_map/ppermute | solution.py:824
  307.6 9.2 %copy-start.27 = (bf16[256,2048]{1,0:T(8,128)(2,1)}, bf16[256,2048]{1,0:T(8,128)(2,1)S(1)}, u32[]{:S(2)}) copy-start(bf16[256,2048]{1,0:T(8,128)(2,1)S(1)} %collective-permute-done.28.got) | copy-start | bytes 3145732
  316.7 24.5 %collective-permute-start.32 = (bf16[1024,2048]{1,0:T(8,128)(2,1)}, bf16[1024,2048]{1,0:T(8,128)(2,1)}, u32[]{:S(2)}, u32[]{:S(2)}) collective-permute-start(bf16[1024,2048]{1,0:T(8,128)(2,1)} %wgrad.9), channel_id=1, source_target_pairs={{0,8},{8,0},{16,24},{24,16},{1,9},{9,1},{17,25},{25,17},{2,10},{10... | collective-permute-start | bytes 12582920 | tf_op jit(solution)/shard_map/ppermute | solution.py:856
  316.7 16.4 %copy-start.7 = (bf16[1024,512]{1,0:T(8,128)(2,1)S(1)}, bf16[1024,512]{1,0:T(8,128)(2,1)}, u32[]{:S(2)}) copy-start(bf16[1024,512]{1,0:T(8,128)(2,1)} %get-tuple-element.185) | copy-start | bytes 3145732
  335.7 26.5 %collective-permute-start.34 = (bf16[1024,512]{1,0:T(8,128)(2,1)}, bf16[1024,512]{1,0:T(8,128)(2,1)}, u32[]{:S(2)}, u32[]{:S(2)}) collective-permute-start(bf16[1024,512]{1,0:T(8,128)(2,1)} %add_convert_fusion.8), channel_id=1, source_target_pairs={{1,2},{2,1},{5,6},{6,5},{9,10},{10,9},{13,14},{14,13},{17,18},{18,... | collective-permute-start | bytes 3145736 | tf_op jit(solution)/shard_map/ppermute | solution.py:834
  340.2 26.7 %collective-permute-start.35 = (bf16[1024,512]{1,0:T(8,128)(2,1)}, bf16[1024,512]{1,0:T(8,128)(2,1)}, u32[]{:S(2)}, u32[]{:S(2)}) collective-permute-start(bf16[1024,512]{1,0:T(8,128)(2,1)} %fusion.3.refs_6_), channel_id=1, source_target_pairs={{0,1},{3,2},{1,0},{2,3},{4,5},{7,6},{5,4},{6,7},{8,9},{11,10},{9,8... | collective-permute-start | bytes 3145736 | tf_op jit(solution)/shard_map/ppermute | solution.py:824
  351.2 26.4 %collective-permute-start.37 = (bf16[512,2048]{1,0:T(8,128)(2,1)}, bf16[512,2048]{1,0:T(8,128)(2,1)}, u32[]{:S(2)}, u32[]{:S(2)}) collective-permute-start(bf16[512,2048]{1,0:T(8,128)(2,1)} %get-tuple-element.196), channel_id=1, source_target_pairs={{0,16},{4,20},{8,12},{12,8},{16,0},{20,4},{24,28},{28,24},{1,17},{... | collective-permute-start | bytes 6291464 | tf_op jit(solution)/shard_map/ppermute | solution.py:899
  359.7 9.7 %collective-permute-start.36 = (bf16[1024,512]{1,0:T(8,128)(2,1)}, bf16[1024,512]{1,0:T(8,128)(2,1)}, u32[]{:S(2)}, u32[]{:S(2)}) collective-permute-start(bf16[1024,512]{1,0:T(8,128)(2,1)} %add_convert_fusion.6), channel_id=1, source_target_pairs={{1,2},{2,1},{5,6},{6,5},{9,10},{10,9},{13,14},{14,13},{17,18},{18,... | collective-permute-start | bytes 3145736 | tf_op jit(solution)/shard_map/ppermute | solution.py:834
  362.1 19.9 %collective-permute-start.38 = (f32[13824]{0:T(1024)S(1)}, f32[13824]{0:T(1024)S(1)}, u32[]{:S(2)}, u32[]{:S(2)}) collective-permute-start(f32[13824]{0:T(1024)S(1)} %pad_maximum_fusion.1), channel_id=1, source_target_pairs={{0,8},{8,0},{16,24},{24,16},{1,9},{9,1},{17,25},{25,17},{2,10},{10... | collective-permute-start | bytes 165896 | tf_op jit(solution)/shard_map/ppermute | solution.py:856
  365.1 26.0 %collective-permute-start.40 = (bf16[1024,512]{1,0:T(8,128)(2,1)}, bf16[1024,512]{1,0:T(8,128)(2,1)}, u32[]{:S(2)}, u32[]{:S(2)}) collective-permute-start(bf16[1024,512]{1,0:T(8,128)(2,1)} %fusion.4.refs_0_), channel_id=1, source_target_pairs={{0,1},{3,2},{1,0},{2,3},{4,5},{7,6},{5,4},{6,7},{8,9},{11,10},{9,8... | collective-permute-start | bytes 3145736 | tf_op jit(solution)/shard_map/ppermute | solution.py:824
  368.5 26.7 %collective-permute-start.41 = (bf16[1024,512]{1,0:T(8,128)(2,1)S(1)}, bf16[1024,512]{1,0:T(8,128)(2,1)S(1)}, u32[]{:S(2)}, u32[]{:S(2)}) collective-permute-start(bf16[1024,512]{1,0:T(8,128)(2,1)S(1)} %add_convert_fusion.4), channel_id=1, source_target_pairs={{1,2},{2,1},{5,6},{6,5},{9,10},{10,9},{13,14},{14,13},{17,18},{18,... | collective-permute-start | bytes 3145736 | tf_op jit(solution)/shard_map/ppermute | solution.py:834
  372.3 31.3 %collective-permute-start.43 = (bf16[1024,2048]{1,0:T(8,128)(2,1)}, bf16[1024,2048]{1,0:T(8,128)(2,1)}, u32[]{:S(2)}, u32[]{:S(2)}) collective-permute-start(bf16[1024,2048]{1,0:T(8,128)(2,1)} %wgrad.8), channel_id=1, source_target_pairs={{0,8},{8,0},{16,24},{24,16},{1,9},{9,1},{17,25},{25,17},{2,10},{10... | collective-permute-start | bytes 12582920 | tf_op jit(solution)/shard_map/ppermute | solution.py:856
  382.0 7.1 %collective-permute-start.39 = (f32[13824]{0:T(1024)S(1)}, f32[13824]{0:T(1024)S(1)}, u32[]{:S(2)}, u32[]{:S(2)}) collective-permute-start(f32[13824]{0:T(1024)S(1)} %add.115), channel_id=1, source_target_pairs={{0,16},{16,0},{8,24},{24,8},{1,17},{17,1},{9,25},{25,9},{2,18},{18... | collective-permute-start | bytes 165896 | tf_op jit(solution)/shard_map/ppermute | solution.py:853
  383.7 15.1 %collective-permute-start.42 = (bf16[256,2048]{1,0:T(8,128)(2,1)}, bf16[256,2048]{1,0:T(8,128)(2,1)}, u32[]{:S(2)}, u32[]{:S(2)}) collective-permute-start(bf16[256,2048]{1,0:T(8,128)(2,1)} %get-tuple-element.208), channel_id=1, source_target_pairs={{0,4},{4,0},{8,24},{12,28},{16,20},{20,16},{24,8},{28,12},{1,5},{5... | collective-permute-start | bytes 3145736 | tf_op jit(solution)/shard_map/ppermute | solution.py:899
  389.1 38.7 %collective-permute-start.46 = (bf16[1024,512]{1,0:T(8,128)(2,1)}, bf16[1024,512]{1,0:T(8,128)(2,1)}, u32[]{:S(2)}, u32[]{:S(2)}) collective-permute-start(bf16[1024,512]{1,0:T(8,128)(2,1)} %add_convert_fusion.3.refs_2_), channel_id=1, source_target_pairs={{1,0},{2,3},{5,4},{6,7},{9,8},{10,11},{13,12},{14,15},{17,16},{18,... | collective-permute-start | bytes 3145736 | tf_op jit(solution)/shard_map/ppermute | solution.py:824
  393.6 70.3 %collective-permute-start.49 = (bf16[1024,512]{1,0:T(8,128)(2,1)}, bf16[1024,512]{1,0:T(8,128)(2,1)}, u32[]{:S(2)}, u32[]{:S(2)}) collective-permute-start(bf16[1024,512]{1,0:T(8,128)(2,1)} %add_convert_fusion.2), channel_id=1, source_target_pairs={{1,2},{2,1},{5,6},{6,5},{9,10},{10,9},{13,14},{14,13},{17,18},{18,... | collective-permute-start | bytes 3145736 | tf_op jit(solution)/shard_map/ppermute | solution.py:834
  396.5 70.6 %collective-permute-start.48 = (bf16[1024,512]{1,0:T(8,128)(2,1)}, bf16[1024,512]{1,0:T(8,128)(2,1)}, u32[]{:S(2)}, u32[]{:S(2)}) collective-permute-start(bf16[1024,512]{1,0:T(8,128)(2,1)} %add_convert_fusion.1.refs_4_), channel_id=1, source_target_pairs={{1,0},{2,3},{5,4},{6,7},{9,8},{10,11},{13,12},{14,15},{17,16},{18,... | collective-permute-start | bytes 3145736 | tf_op jit(solution)/shard_map/ppermute | solution.py:824
  402.7 17.2 %collective-permute-start.44 = (f32[13824]{0:T(1024)}, f32[13824]{0:T(1024)}, u32[]{:S(2)}, u32[]{:S(2)}) collective-permute-start(f32[13824]{0:T(1024)} %add.117), channel_id=1, source_target_pairs={{0,4},{4,0},{1,5},{5,1},{2,6},{6,2},{3,7},{7,3},{8,12},{12,8},{9,1... | collective-permute-start | bytes 165896 | tf_op jit(solution)/shard_map/ppermute | solution.py:859
  414.4 26.2 %collective-permute-start.45 = (bf16[512,2048]{1,0:T(8,128)(2,1)}, bf16[512,2048]{1,0:T(8,128)(2,1)S(1)}, u32[]{:S(2)}, u32[]{:S(2)}) collective-permute-start(bf16[512,2048]{1,0:T(8,128)(2,1)} %get-tuple-element.215), channel_id=1, source_target_pairs={{0,16},{4,20},{8,12},{12,8},{16,0},{20,4},{24,28},{28,24},{1,17},{... | collective-permute-start | bytes 6291464 | tf_op jit(solution)/shard_map/ppermute | solution.py:899
  446.3 20.7 %collective-permute-start.47 = (bf16[256,2048]{1,0:T(8,128)(2,1)}, bf16[256,2048]{1,0:T(8,128)(2,1)S(1)}, u32[]{:S(2)}, u32[]{:S(2)}) collective-permute-start(bf16[256,2048]{1,0:T(8,128)(2,1)} %get-tuple-element.220), channel_id=1, source_target_pairs={{0,4},{4,0},{8,24},{12,28},{16,20},{20,16},{24,8},{28,12},{1,5},{5... | collective-permute-start | bytes 3145736 | tf_op jit(solution)/shard_map/ppermute | solution.py:899
  448.1 24.2 %collective-permute-start.50 = (f32[8192]{0:T(1024)S(1)}, f32[8192]{0:T(1024)S(1)}, u32[]{:S(2)}, u32[]{:S(2)}) collective-permute-start(f32[8192]{0:T(1024)S(1)} %slice.40), channel_id=1, source_target_pairs={{0,1},{1,0},{2,3},{3,2},{4,5},{5,4},{6,7},{7,6},{8,9},{9,8},{10,11... | collective-permute-start | bytes 98312 | tf_op jit(solution)/shard_map/ppermute | solution.py:932
  463.9 41.1 %copy-start.14 = (f32[2048]{0:T(1024)}, f32[2048]{0:T(1024)S(1)}, u32[]{:S(2)}) copy-start(f32[2048]{0:T(1024)S(1)} %get-tuple-element.268) | copy-start | bytes 24580
  465.7 6.6 %copy-start.12 = (bf16[1024,512]{1,0:T(8,128)(2,1)}, bf16[1024,512]{1,0:T(8,128)(2,1)S(1)}, u32[]{:S(2)}) copy-start(bf16[1024,512]{1,0:T(8,128)(2,1)S(1)} %add_convert_fusion.refs_6_) | copy-start | bytes 3145732
  465.7 25.6 %collective-permute-start.51 = (bf16[1024,512]{1,0:T(8,128)(2,1)S(1)}, bf16[1024,512]{1,0:T(8,128)(2,1)S(1)}, u32[]{:S(2)}, u32[]{:S(2)}) collective-permute-start(bf16[1024,512]{1,0:T(8,128)(2,1)S(1)} %add_convert_fusion.refs_6_), channel_id=1, source_target_pairs={{1,0},{2,3},{5,4},{6,7},{9,8},{10,11},{13,12},{14,15},{17,16},{18,... | collective-permute-start | bytes 3145736 | tf_op jit(solution)/shard_map/ppermute | solution.py:824
  472.3 32.0 %collective-permute-start.52 = (f32[8192]{0:T(1024)S(1)}, f32[8192]{0:T(1024)S(1)}, u32[]{:S(2)}, u32[]{:S(2)}) collective-permute-start(f32[8192]{0:T(1024)S(1)} %add.122), channel_id=1, source_target_pairs={{0,2},{2,0},{1,3},{3,1},{4,6},{6,4},{5,7},{7,5},{8,10},{10,8},{9,1... | collective-permute-start | bytes 98312 | tf_op jit(solution)/shard_map/ppermute | solution.py:934
  (21 other events, 71.8 us)

commit v5 on v4

--- a/solution.py
+++ b/solution.py
@@ -702,20 +702,28 @@
     )(mid, got)
 
 
-def total_of(meta, refs, c, cols):
-    here, sent = refs[2 * c], refs[2 * c + 1]
-    return jnp.where(meta[1 + NBLK] > 0, here[:, cols].astype(F32), sent[:, cols].astype(F32))
+def by_role(meta, refs, body):
+    @pl.when(meta[1 + NBLK] > 0)
+    def _():
+        body(refs[0::2])
+
+    @pl.when(meta[1 + NBLK] == 0)
+    def _():
+        body(refs[1::2])
 
 
 def block_out_kernel(local_len, first, meta, x_ref, b_ref, *refs):
     y_ref = refs[-1]
     rows = x_ref.shape[0]
     mask = row_valid(meta, (first + pl.program_id(0)) * rows, rows, local_len)
-    for r in range(NBLK):
-        col = block_cols(meta[1 + r] * 256)
-        k = r % 2 * 256
-        s = total_of(meta, refs, r // 2, slice(k, k + 256))
-        y_ref[:, col] = (mask * (x_ref[:, col].astype(F32) + s + b_ref[:, col])).astype(BF)
+
+    def body(parts):
+        for r in range(NBLK):
+            col = block_cols(meta[1 + r] * 256)
+            s = parts[r // 2][:, r % 2 * 256 : r % 2 * 256 + 256].astype(F32)
+            y_ref[:, col] = (mask * (x_ref[:, col].astype(F32) + s + b_ref[:, col])).astype(BF)
+
+    by_role(meta, refs[:8], body)
 
 
 def input_grad_kernel(local_len, first, meta, x_ref, g_ref, st_ref, *refs):
@@ -724,23 +732,28 @@
     mask = row_valid(meta, (first + pl.program_id(0)) * rows, rows, local_len)
     mean = st_ref[:, 0:1]
     inv = st_ref[:, 1:2]
-    one = jnp.zeros((rows, 1), F32)
-    two = jnp.zeros((rows, 1), F32)
-    for r in range(NBLK):
-        col = block_cols(meta[1 + r] * 256)
-        k = r % 2 * 256
-        dn = total_of(meta, refs, r // 2, slice(k, k + 256))
-        one += jnp.sum(dn, axis=1, keepdims=True)
-        two += jnp.sum(dn * ((x_ref[:, col].astype(F32) - mean) * inv), axis=1, keepdims=True)
     d = x_ref.shape[1]
-    one = one / d
-    two = two / d
-    for r in range(NBLK):
-        col = block_cols(meta[1 + r] * 256)
-        k = r % 2 * 256
-        dn = total_of(meta, refs, r // 2, slice(k, k + 256))
-        xh = (x_ref[:, col].astype(F32) - mean) * inv
-        y_ref[:, col] = (g_ref[:, col].astype(F32) * mask + inv * (dn - one - xh * two)).astype(BF)
+
+    def body(parts):
+        def dn_of(r):
+            return parts[r // 2][:, r % 2 * 256 : r % 2 * 256 + 256].astype(F32)
+
+        one = jnp.zeros((rows, 256), F32)
+        two = jnp.zeros((rows, 256), F32)
+        for r in range(NBLK):
+            dn = dn_of(r)
+            one += dn
+            two += dn * (x_ref[:, block_cols(meta[1 + r] * 256)].astype(F32) - mean)
+        one = jnp.sum(one, axis=1, keepdims=True) / d
+        two = jnp.sum(two, axis=1, keepdims=True) * inv / d
+        slope = inv * inv * two
+        shift = slope * mean - inv * one
+        for r in range(NBLK):
+            col = block_cols(meta[1 + r] * 256)
+            y = g_ref[:, col].astype(F32) * mask + inv * dn_of(r)
+            y_ref[:, col] = (y + (shift - slope * x_ref[:, col].astype(F32))).astype(BF)
+
+    by_role(meta, refs[:8], body)
 
 
 def rows_call(meta, *ops, body, name, specs, steps=None, into=None):
@@ -1078,19 +1091,19 @@
     pipe.cross()
     pipe.send(dn0)
     state3 = comm.scatter_half(run, state3)
-    theirs1 = run(wgrad_call, meta, h1, dqkv, g, ob, half=1)
     pipe.cross()
     pipe.send(dn1)
-    cross2 = comm.scatter_cross(run(wgrad_call, after(meta, jax.tree.leaves(state3)[-1]), h2, du, half=1))
     dn2, dn3, gain_sums = run(back_call, meta, dqkv, du, g1, g2, x2, stats, ga, gf, gain_sums, 1)
     pipe.cross()
     pipe.send(dn2)
+    cross2 = comm.scatter_cross(run(wgrad_call, after(meta, jax.tree.leaves(state3)[-1]), h2, du, half=1))
+    theirs1 = run(wgrad_call, meta, h1, dqkv, g, ob, half=1)
+    pipe.cross()
+    pipe.send(dn3)
     state2 = comm.scatter_own(run, meta, (h2, du), cross2)
     (grad_out,) = comm.scatter_last(run, ((ff, True),), state3)
-    pipe.cross()
-    pipe.send(dn3)
     small = jnp.concatenate([gain_sums.reshape(-1), g_sum.reshape(-1), bqkv_sum.reshape(-1), bin_sum.reshape(-1)])
-    add = comm.small_sum(run, small, 0)
+    add = comm.small_sum(run, after(small, grad_out), 0)
     pipe.cross()
     pipe.send()
     cross1 = comm.scatter_cross(after(theirs1, pipe.here[-1]))
@@ -1117,11 +1130,11 @@
     gains = small[: 4 * d]
     group = small[4 * d :]
     state1 = comm.scatter_half(run, after(state1, pipe.sent[5]))
-    add = comm.small_sum(run, gains, 3)
     pipe.send()
     grad_qkv, grad_proj = comm.scatter_last(
         run, ((nq // 512, False), (nheads * HD // 512, True)), after(state1, pipe.sent[6])
     )
+    add = comm.small_sum(run, after(gains, grad_qkv), 3)
     gains = add()
     add = comm.small_sum(run, gains, 4)
     input_grad = run(

time: 513 us -> 516 us (level)
  waiting for transfers between devices: 80.2 us -> 95.1 us
  starting transfers between devices: 98.1 us -> 90 us
    ppermute x6, waiting for transfers between devices: 19 us -> 46.9 us  [turn(): return lax.ppermute(v, ('dp', 'ctx'), pairs)]
    ppermute x11, waiting for transfers between devices: 15.1 us -> 0.03 us  [send(): got = lax.ppermute(v, 'tensor', pairs)]
    ppermute x1, starting transfers between devices: 11.1 us -> 1.01 us  [small_sum(): got = lax.ppermute(v, 'tensor', [(0, 2), (2, 0), (1, 3), (3, 1)])]
    ppermute x1, starting transfers between devices: 15.2 us -> 5.42 us  [small_sum(): got = lax.ppermute(v, 'tensor', [(0, 1), (1, 0), (2, 3), (3, 2)])]
    ppermute x6, starting transfers between devices: 13.5 us -> 21.2 us  [turn(): return lax.ppermute(v, ('dp', 'ctx'), pairs)]
    unnamed x68 -> x74, local copies, waits for them, and re-layouts: 12.7 us -> 12.7 us
  transfers between devices with their start and end apart: 53 -> 53, of which waited for: 12 -> 11; matrix products, arithmetic and copies ran while one was open for 10% -> 10% of each run, Pallas kernels for 52% -> 51%
where the time goes in v5:
time: 516 us; the launch traced here: 509 us
  Pallas kernels  260 us (50%)
  waiting for transfers between devices  95.1 us (18%)
  starting transfers between devices  90 us (17%)
  other arithmetic  45.9 us (9%)
  local copies, waits for them, and re-layouts  16.4 us (3%)
    pallas_call x6, Pallas kernels, wgrad_call(): pl.pallas_call(functools.partial(wgrad_kernel, counts, add is not None, s...  59.4 us
    ppermute x6, waiting for transfers between devices, turn(): return lax.ppermute(v, ('dp', 'ctx'), pairs)  46.9 us
    ppermute x7, waiting for transfers between devices, x(): return lax.ppermute(v, 'dp', [(0, 2), (2, 0), (1, 3), (3, 1)])  42.7 us
    pallas_call x2, Pallas kernels, back_call(): pl.pallas_call(back_kernel, name='backn', grid_spec=pltpu.PrefetchScalarG...  32.4 us
    ppermute x11, starting transfers between devices, send(): got = lax.ppermute(v, 'tensor', pairs)  26.5 us
    convert_element_type x11, other arithmetic, add_bf(): return lax.optimization_barrier((a.astype(F32) + b.astype(F32)).astype(BF))  23.5 us
    pallas_call x2, Pallas kernels, out_call(): pl.pallas_call(functools.partial(out_kernel, count), name='outp', grid=(4...  22.5 us
    ppermute x6, starting transfers between devices, turn(): return lax.ppermute(v, ('dp', 'ctx'), pairs)  21.2 us
  transfers between devices with their start and end apart: 53, of which 11 were waited for; matrix products, arithmetic and copies ran while one was open for 10% of the time, Pallas kernels for 51%

profile of v5, /device:TPU:0, one launch (start us, length us, event | category | flops | bytes accessed | tf_op | source)
XLA Modules:
  0.0 508.6 jit_solution(11174681709512852991)
XLA Ops:
  4.6 3.0 collective-permute-start
  10.7 2.6 copy.32
  15.4 10.5 %norm.1 = (bf16[1024,2048]{1,0:T(8,128)(2,1)}, bf16[1024,2048]{1,0:T(8,128)(2,1)}, f32[1024,128]{1,0:T(8,128)}, f32[1,2048]{1,0:T(1,128)}) custom-call(s32[13]{0:T(128)} %concatenate.10.meta, bf16[1024,2048]{1,0:T(8,128)(2,1)} %bitcast.30, bf16[1024,2048]{1,0:T(8,128)(2,1)} %bitcast.37, f32[1,2048]{1,0:T(1,128)} %bitcast.42, f32[1,2048]{1,0:T(1,128)} %bitcast.39), custom_call_target="tpu_custom_call" | custom-call | flops 125829120000 | bytes 419430400 | tf_op jit(solution)/shard_map/norm/pallas_call | solution.py:127
  27.2 1.9 fusion.5
  29.1 2.8 collective-permute-done.refs_1_
  33.9 3.8 pack.3.w0.refs_0_.w10
  38.2 18.4 %collective-permute-done.3.w2.refs_1_.w12 = bf16[256,2048]{1,0:T(8,128)(2,1)} collective-permute-done((bf16[256,2048]{1,0:T(8,128)(2,1)}, bf16[256,2048]{1,0:T(8,128)(2,1)}, u32[]{:S(2)}, u32[]{:S(2)}) %collective-permute-start.3) | collective-permute-done | bytes 1048608 | tf_op jit(solution)/shard_map/ppermute | solution.py:866
  56.6 3.9 pack.4.w0.w20
  63.8 9.8 %kv.1.kv_ref = bf16[1024,1024]{1,0:T(8,128)(2,1)} custom-call(bf16[1024,2048]{1,0:T(8,128)(2,1)} %get-tuple-element.130.h1.refs_0_, bf16[512,2048]{1,0:T(8,128)(2,1)} %pack.3.w0.refs_0_.w10, bf16[256,2048]{1,0:T(8,128)(2,1)} %copy-done.27, bf16[256,2048]{1,0:T(8,128)(2,1)} %collective-permute-done.3.w2.refs_1_.w12, bf16[512,2048]{1,0:T(8,128)(2,1)} %copy-done.11, ...), custom_call_target="tpu_custom_call" | custom-call | flops 85899345920 | bytes 209715200 | tf_op jit(solution)/shard_map/kv/pallas_call | solution.py:183
  73.6 3.9 collective-permute-start.13
  77.5 8.8 %collective-permute-done.7.w1.w21 = bf16[256,2048]{1,0:T(8,128)(2,1)S(1)} collective-permute-done((bf16[256,2048]{1,0:T(8,128)(2,1)}, bf16[256,2048]{1,0:T(8,128)(2,1)S(1)}, u32[]{:S(2)}, u32[]{:S(2)}) %collective-permute-start.7) | collective-permute-done | bytes 1048608 | tf_op jit(solution)/shard_map/ppermute | solution.py:866
  87.8 10.7 %qd.1 = (bf16[1024,512]{1,0:T(8,128)(2,1)}, bf16[1024,512]{1,0:T(8,128)(2,1)}) custom-call(bf16[1024,2048]{1,0:T(8,128)(2,1)} %get-tuple-element.130.h1.refs_0_, bf16[1024,2048]{1,0:T(8,128)(2,1)} %get-tuple-element.154.g.refs_0_.refs_2_, bf16[512,2048]{1,0:T(8,128)(2,1)} %pack.3.w0.refs_0_.w10, bf16[256,2048]{1,0:T(8,128)(2,1)} %copy-done.27, ...), custom_call_target="tpu_custom_call" | custom-call | flops 88080384000 | bytes 293601280 | tf_op jit(solution)/shard_map/qd/pallas_call | solution.py:224
  98.5 12.4 %collective-permute-done.8.w2.w22 = bf16[256,2048]{1,0:T(8,128)(2,1)} collective-permute-done((bf16[256,2048]{1,0:T(8,128)(2,1)}, bf16[256,2048]{1,0:T(8,128)(2,1)}, u32[]{:S(2)}, u32[]{:S(2)}) %collective-permute-start.8) | collective-permute-done | bytes 1048608 | tf_op jit(solution)/shard_map/ppermute | solution.py:866
  110.9 6.7 %norm2.1.h2.refs_0_ = bf16[1024,2048]{1,0:T(8,128)(2,1)} custom-call(s32[13]{0:T(128)} %concatenate.10.meta, bf16[1024,2048]{1,0:T(8,128)(2,1)} %bitcast.31, f32[1024,128]{1,0:T(8,128)} %get-tuple-element.134.st_ref, f32[1,2048]{1,0:T(1,128)} %bitcast.45, f32[1,2048]{1,0:T(1,128)} %bitcast.40), custom_call_target="tpu_custom_call" | custom-call | flops 50331648000 | bytes 167772160 | tf_op jit(solution)/shard_map/norm2/pallas_call | solution.py:107
  120.4 16.4 %hidden.1 = (bf16[1024,2048]{1,0:T(8,128)(2,1)}, bf16[1024,2048]{1,0:T(8,128)(2,1)}) custom-call(bf16[1024,2048]{1,0:T(8,128)(2,1)} %norm2.1.h2.refs_0_, bf16[512,2048]{1,0:T(8,128)(2,1)} %pack.4.w0.w20, bf16[256,2048]{1,0:T(8,128)(2,1)} %copy-done.30, bf16[256,2048]{1,0:T(8,128)(2,1)} %collective-permute-done.8.w2.w22, ...), custom_call_target="tpu_custom_call" | custom-call | flops 171798691840 | bytes 419430400 | tf_op jit(solution)/shard_map/hidden/pallas_call | solution.py:413
  136.9 3.8 pack.5.refs_2_.w0
  140.9 2.5 collective-permute-done.15.refs_4_.w1
  145.0 12.4 %attn.1 = (bf16[1024,512]{1,0:T(8,128)(2,1)}, bf16[1024,512]{1,0:T(8,128)(2,1)}, f32[1024,1024]{1,0:T(8,128)}, bf16[1024,1024]{1,0:T(8,128)(2,1)}) custom-call(s32[13]{0:T(128)} %concatenate.10.meta, bf16[1024,512]{1,0:T(8,128)(2,1)} %get-tuple-element.132.q_ref, bf16[1024,1024]{1,0:T(8,128)(2,1)} %kv.1.kv_ref, ...), custom_call_target="tpu_custom_call" | custom-call | flops 128849018880 | bytes 209715200 | tf_op jit(solution)/shard_map/attn/pallas_call | solution.py:333
  160.0 10.9 %outp.2 = (bf16[1024,512]{1,0:T(8,128)(2,1)}, bf16[1024,512]{1,0:T(8,128)(2,1)}) custom-call(bf16[1024,512]{1,0:T(8,128)(2,1)} %get-tuple-element.148.ob.refs_3_, bf16[1024,2048]{1,0:T(8,128)(2,1)} %get-tuple-element.140.gb.refs_1_, bf16[512,2048]{1,0:T(8,128)(2,1)} %pack.3.w0.refs_0_.w10, bf16[512,2048]{1,0:T(8,128)(2,1)} %copy-done.11, ...), custom_call_target="tpu_custom_call" | custom-call | flops 53687092 | bytes 125829 | tf_op jit(solution)/shard_map/outp/pallas_call | solution.py:479
  170.9 4.6 collective-permute-start.19
  175.8 9.2 %wgrad.6 = bf16[1024,2048]{1,0:T(8,128)(2,1)} custom-call(s32[13]{0:T(128)} %concatenate.10.meta, bf16[1024,2048]{1,0:T(8,128)(2,1)} %get-tuple-element.154.g.refs_0_.refs_2_, bf16[1024,2048]{1,0:T(8,128)(2,1)} %get-tuple-element.140.gb.refs_1_), custom_call_target="tpu_custom_call" | custom-call | flops 88080384000 | bytes 293601280 | tf_op jit(solution)/shard_map/wgrad/pallas_call | solution.py:602
  185.3 2.3 collective-permute-start.21
  188.7 11.6 %outp.3 = (bf16[1024,512]{1,0:T(8,128)(2,1)}, bf16[1024,512]{1,0:T(8,128)(2,1)}) custom-call(bf16[1024,512]{1,0:T(8,128)(2,1)} %get-tuple-element.148.ob.refs_3_, bf16[1024,2048]{1,0:T(8,128)(2,1)} %get-tuple-element.140.gb.refs_1_, bf16[256,2048]{1,0:T(8,128)(2,1)} %copy-done.27, bf16[256,2048]{1,0:T(8,128)(2,1)} %collective-permute-done.3.w2.refs_1_.w12, ...), custom_call_target="tpu_custom_call" | custom-call | flops 107374182400 | bytes 251658240 | tf_op jit(solution)/shard_map/outp/pallas_call | solution.py:479
  200.3 15.1 %dhid.1 = (bf16[1024,2048]{1,0:T(8,128)(2,1)}, f32[1,2048]{1,0:T(1,128)}) custom-call(bf16[1024,2048]{1,0:T(8,128)(2,1)} %get-tuple-element.154.g.refs_0_.refs_2_, bf16[512,2048]{1,0:T(8,128)(2,1)} %pack.5.refs_2_.w0, bf16[256,2048]{1,0:T(8,128)(2,1)} %collective-permute-done.15.refs_4_.w1, bf16[256,2048]{1,0:T(8,128)(2,1)} %copy-done.31, ...), custom_call_target="tpu_custom_call" | custom-call | flops 171798691840 | bytes 419430400 | tf_op jit(solution)/shard_map/dhid/pallas_call | solution.py:438
  215.4 2.5 add_convert_fusion.15
  219.5 2.3 collective-permute-start.24
  221.8 10.0 %wgrad.7 = (bf16[512,2048]{1,0:T(8,128)(2,1)}, bf16[512,2048]{1,0:T(8,128)(2,1)}) custom-call(s32[13]{0:T(128)} %concatenate.10.meta, bf16[1024,2048]{1,0:T(8,128)(2,1)} %get-tuple-element.154.g.refs_0_.refs_2_, bf16[1024,2048]{1,0:T(8,128)(2,1)} %get-tuple-element.140.gb.refs_1_, bf16[1024,2048]{1,0:T(8,128)(2,1)} %collective-permute-done.20.refs_2_), custom_call_target="tpu_custom_call" | custom-call | flops 88080384000 | bytes 293601280 | tf_op jit(solution)/shard_map/wgrad/pallas_call | solution.py:602
  231.9 2.8 add_convert_fusion.14
  234.7 2.0 collective-permute-start.25
  236.7 6.0 %join.1 = (bf16[1024,1536]{1,0:T(8,128)(2,1)}, f32[1,1536]{1,0:T(1,128)}) custom-call(bf16[1024,512]{1,0:T(8,128)(2,1)} %get-tuple-element.163.dq_ref, f32[1024,1024]{1,0:T(8,128)} %get-tuple-element.164.dkv_ref, bf16[1024,1024]{1,0:T(8,128)(2,1)} %collective-permute-done.22.rv_ref, f32[512,128]{1,0:T(8,128)} %get-tuple-element.242.cosf, ...), custom_call_target="tpu_custom_call" | custom-call | flops 75497472000 | bytes 251658240 | tf_op jit(solution)/shard_map/join/pallas_call | solution.py:388
  242.8 2.9 fusion.refs_0_
  247.7 16.0 %backn.2 = (bf16[1024,512]{1,0:T(8,128)(2,1)}, bf16[1024,512]{1,0:T(8,128)(2,1)}, f32[4,2048]{1,0:T(4,128)}) custom-call(s32[13]{0:T(128)} %concatenate.10.meta, bf16[1024,1536]{1,0:T(8,128)(2,1)} %get-tuple-element.166.dqkv.refs_1_, bf16[1024,2048]{1,0:T(8,128)(2,1)} %get-tuple-element.156.du.refs_1_, ...), custom_call_target="tpu_custom_call", output_to_operand_aliasing={{2}: (13, {})} | custom-call | flops 150323855360 | bytes 377487360 | tf_op jit(solution)/shard_map/backn/pallas_call | solution.py:523
  263.7 1.9 add_convert_fusion.12
  267.0 3.0 fusion.1.refs_4_
  269.9 4.0 collective-permute-start.29
  274.0 4.4 hsum.3
  278.4 2.6 add_convert_fusion.10
  284.2 4.4 collective-permute-start.32
  288.6 17.2 %collective-permute-start.30 = (bf16[256,2048]{1,0:T(8,128)(2,1)}, bf16[256,2048]{1,0:T(8,128)(2,1)}, u32[]{:S(2)}, u32[]{:S(2)}) collective-permute-start(bf16[256,2048]{1,0:T(8,128)(2,1)} %get-tuple-element.184), channel_id=1, source_target_pairs={{0,4},{4,0},{8,24},{12,28},{16,20},{20,16},{24,8},{28,12},{1,5},{5... | collective-permute-start | bytes 3145736 | tf_op jit(solution)/shard_map/ppermute | solution.py:912
  305.8 16.4 %backn.3 = (bf16[1024,512]{1,0:T(8,128)(2,1)}, bf16[1024,512]{1,0:T(8,128)(2,1)}, f32[4,2048]{1,0:T(4,128)}) custom-call(s32[13]{0:T(128)} %concatenate.10.meta, bf16[1024,1536]{1,0:T(8,128)(2,1)} %get-tuple-element.166.dqkv.refs_1_, bf16[1024,2048]{1,0:T(8,128)(2,1)} %get-tuple-element.156.du.refs_1_, ...), custom_call_target="tpu_custom_call", output_to_operand_aliasing={{2}: (13, {})} | custom-call | flops 150323855360 | bytes 377487360 | tf_op jit(solution)/shard_map/backn/pallas_call | solution.py:523
  322.3 2.6 add_convert_fusion.8
  327.2 3.0 fusion.3.refs_6_
  330.2 9.2 %wgrad.8 = bf16[1024,2048]{1,0:T(8,128)(2,1)} custom-call(s32[13]{0:T(128)} %concatenate.10.meta, bf16[1024,2048]{1,0:T(8,128)(2,1)} %norm2.1.h2.refs_0_, bf16[1024,2048]{1,0:T(8,128)(2,1)} %get-tuple-element.156.du.refs_1_), custom_call_target="tpu_custom_call" | custom-call | flops 88080384000 | bytes 293601280 | tf_op jit(solution)/shard_map/wgrad/pallas_call | solution.py:602
  339.3 1.8 collective-permute-start.35
  341.2 10.2 %wgrad.9 = bf16[1024,2048]{1,0:T(8,128)(2,1)} custom-call(s32[13]{0:T(128)} %concatenate.10.meta, bf16[1024,2048]{1,0:T(8,128)(2,1)} %get-tuple-element.130.h1.refs_0_, bf16[1024,1536]{1,0:T(8,128)(2,1)} %get-tuple-element.166.dqkv.refs_1_, bf16[1024,2048]{1,0:T(8,128)(2,1)} %get-tuple-element.154.g.refs_0_.refs_2_, ...), custom_call_target="tpu_custom_call" | custom-call | flops 100663296000 | bytes 335544320 | tf_op jit(solution)/shard_map/wgrad/pallas_call | solution.py:602
  354.8 3.0 fusion.4.refs_0_
  357.8 2.0 collective-permute-start.40
  359.8 10.0 %wgrad.10 = (bf16[512,2048]{1,0:T(8,128)(2,1)}, bf16[512,2048]{1,0:T(8,128)(2,1)}) custom-call(s32[13]{0:T(128)} %concatenate.10.meta, bf16[1024,2048]{1,0:T(8,128)(2,1)} %norm2.1.h2.refs_0_, bf16[1024,2048]{1,0:T(8,128)(2,1)} %get-tuple-element.156.du.refs_1_, bf16[1024,2048]{1,0:T(8,128)(2,1)} %collective-permute-done.34.refs_2_), custom_call_target="tpu_custom_call" | custom-call | flops 88080384000 | bytes 293601280 | tf_op jit(solution)/shard_map/wgrad/pallas_call | solution.py:602
  371.3 4.3 lsum.3
  377.1 2.5 add_convert_fusion.3.refs_2_
  380.9 15.2 %collective-permute-done.37.got = bf16[512,2048]{1,0:T(8,128)(2,1)} collective-permute-done((bf16[512,2048]{1,0:T(8,128)(2,1)}, bf16[512,2048]{1,0:T(8,128)(2,1)}, u32[]{:S(2)}, u32[]{:S(2)}) %collective-permute-start.37) | collective-permute-done | bytes 2097184 | tf_op jit(solution)/shard_map/ppermute | solution.py:912
  396.1 4.4 hsum.4
  402.1 5.0 bout.2.refs_8_
  409.1 2.5 add_convert_fusion.2
  417.2 4.0 lsum.4
  421.8 10.8 %wgrad.11 = (bf16[512,2048]{1,0:T(8,128)(2,1)}, bf16[512,2048]{1,0:T(8,128)(2,1)}) custom-call(s32[13]{0:T(128)} %concatenate.10.meta, bf16[1024,2048]{1,0:T(8,128)(2,1)} %get-tuple-element.130.h1.refs_0_, bf16[1024,1536]{1,0:T(8,128)(2,1)} %get-tuple-element.166.dqkv.refs_1_, bf16[1024,2048]{1,0:T(8,128)(2,1)} %get-tuple-element.154.g.refs_0_.refs_2_, ...), custom_call_target="tpu_custom_call" | custom-call | flops 100663296000 | bytes 335544320 | tf_op jit(solution)/shard_map/wgrad/pallas_call | solution.py:602
  433.1 4.8 bout.3
  438.8 20.0 %collective-permute-done.45.got = bf16[512,2048]{1,0:T(8,128)(2,1)S(1)} collective-permute-done((bf16[512,2048]{1,0:T(8,128)(2,1)}, bf16[512,2048]{1,0:T(8,128)(2,1)S(1)}, u32[]{:S(2)}, u32[]{:S(2)}) %collective-permute-start.45) | collective-permute-done | bytes 2097184 | tf_op jit(solution)/shard_map/ppermute | solution.py:912
  460.2 4.4 hsum.5
  469.4 10.2 %collective-permute-done.47.got = bf16[256,2048]{1,0:T(8,128)(2,1)S(1)} collective-permute-done((bf16[256,2048]{1,0:T(8,128)(2,1)}, bf16[256,2048]{1,0:T(8,128)(2,1)S(1)}, u32[]{:S(2)}, u32[]{:S(2)}) %collective-permute-start.47) | collective-permute-done | bytes 1048608 | tf_op jit(solution)/shard_map/ppermute | solution.py:912
  480.5 4.3 lsum.5
  484.8 5.4 %collective-permute-start.50 = (f32[8192]{0:T(1024)S(1)}, f32[8192]{0:T(1024)S(1)}, u32[]{:S(2)}, u32[]{:S(2)}) collective-permute-start(f32[8192]{0:T(1024)S(1)} %slice.40), channel_id=1, source_target_pairs={{0,1},{1,0},{2,3},{3,2},{4,5},{5,4},{6,7},{7,6},{8,9},{9,8},{10,11... | collective-permute-start | bytes 98312 | tf_op jit(solution)/shard_map/ppermute | solution.py:945
  491.4 2.6 collective-permute-done.50
  496.1 11.1 %igrad.1 = bf16[1024,2048]{1,0:T(8,128)(2,1)} custom-call(s32[13]{0:T(128)} %concatenate.10.meta, bf16[1024,2048]{1,0:T(8,128)(2,1)} %bitcast.36, bf16[1024,2048]{1,0:T(8,128)(2,1)} %bitcast.38, f32[1024,128]{1,0:T(8,128)} %get-tuple-element.134.st_ref, bf16[1024,512]{1,0:T(8,128)(2,1)} %fusion.4.refs_0_, bf16[1024,512]{1,0:T(8,128)(2,1)} %collective-permute-done.40.refs_1_, ...), custom_call_target="tpu_custom_call" | custom-call | flops 100663296000 | bytes 335544320 | tf_op jit(solution)/shard_map/igrad/pallas_call | solution.py:775
  (186 shorter events, 67.5 us)
Async XLA Ops:
  4.6 27.3 %collective-permute-start = (bf16[256,2048]{1,0:T(8,128)(2,1)}, bf16[256,2048]{1,0:T(8,128)(2,1)}, u32[]{:S(2)}, u32[]{:S(2)}) collective-permute-start(bf16[256,2048]{1,0:T(8,128)(2,1)} %pad_maximum_fusion.refs_0_), channel_id=1, source_target_pairs={{0,4},{4,0},{1,5},{5,1},{2,6},{6,2},{3,7},{7,3},{8,12},{12,8},{9,1... | collective-permute-start | bytes 3145736 | tf_op jit(solution)/shard_map/ppermute | solution.py:872
  7.6 24.8 %collective-permute-start.2 = (bf16[256,2048]{1,0:T(8,128)(2,1)}, bf16[256,2048]{1,0:T(8,128)(2,1)S(1)}, u32[]{:S(2)}, u32[]{:S(2)}) collective-permute-start(bf16[256,2048]{1,0:T(8,128)(2,1)} %pad_maximum_fusion.refs_0_), channel_id=1, source_target_pairs={{0,16},{16,0},{8,24},{24,8},{1,17},{17,1},{9,25},{25,9},{2,18},{18... | collective-permute-start | bytes 3145736 | tf_op jit(solution)/shard_map/ppermute | solution.py:866
  10.2 46.4 %collective-permute-start.1 = (bf16[256,2048]{1,0:T(8,128)(2,1)}, bf16[256,2048]{1,0:T(8,128)(2,1)}, u32[]{:S(2)}, u32[]{:S(2)}) collective-permute-start(bf16[256,2048]{1,0:T(8,128)(2,1)} %convert_element_type.174.refs_0_), channel_id=1, source_target_pairs={{0,4},{4,0},{1,5},{5,1},{2,6},{6,2},{3,7},{7,3},{8,12},{12,8},{9,1... | collective-permute-start | bytes 3145736 | tf_op jit(solution)/shard_map/ppermute | solution.py:872
  13.3 123.6 %collective-permute-start.12 = (bf16[256,2048]{1,0:T(8,128)(2,1)}, bf16[256,2048]{1,0:T(8,128)(2,1)}, u32[]{:S(2)}, u32[]{:S(2)}) collective-permute-start(bf16[256,2048]{1,0:T(8,128)(2,1)} %bitcast.21.refs_0_), channel_id=1, source_target_pairs={{0,4},{4,0},{1,5},{5,1},{2,6},{6,2},{3,7},{7,3},{8,12},{12,8},{9,1... | collective-permute-start | bytes 3145736 | tf_op jit(solution)/shard_map/ppermute | solution.py:872
  15.4 10.5 %copy-start.23 = (f32[1536]{0:T(1024)S(1)}, f32[1536]{0:T(1024)}, u32[]{:S(2)}) copy-start(f32[1536]{0:T(1024)} %param.23) | copy-start | bytes 18436
  15.4 11.1 %copy-start.21 = (f32[2048]{0:T(1024)S(1)}, f32[2048]{0:T(1024)}, u32[]{:S(2)}) copy-start(f32[2048]{0:T(1024)} %param.25) | copy-start | bytes 24580
  15.4 11.1 %copy-start.22 = (f32[2048]{0:T(1024)S(1)}, f32[2048]{0:T(1024)}, u32[]{:S(2)}) copy-start(f32[2048]{0:T(1024)} %param.29) | copy-start | bytes 24580
  32.4 24.2 %collective-permute-start.3 = (bf16[256,2048]{1,0:T(8,128)(2,1)}, bf16[256,2048]{1,0:T(8,128)(2,1)}, u32[]{:S(2)}, u32[]{:S(2)}) collective-permute-start(bf16[256,2048]{1,0:T(8,128)(2,1)} %collective-permute-done.refs_1_), channel_id=1, source_target_pairs={{0,16},{16,0},{8,24},{24,8},{1,17},{17,1},{9,25},{25,9},{2,18},{18... | collective-permute-start | bytes 3145736 | tf_op jit(solution)/shard_map/ppermute | solution.py:866
  37.7 24.8 %collective-permute-start.4 = (bf16[512,2048]{1,0:T(8,128)(2,1)}, bf16[512,2048]{1,0:T(8,128)(2,1)S(1)}, u32[]{:S(2)}, u32[]{:S(2)}) collective-permute-start(bf16[512,2048]{1,0:T(8,128)(2,1)} %pack.3.w0.refs_0_.w10), channel_id=1, source_target_pairs={{0,8},{8,0},{16,24},{24,16},{1,9},{9,1},{17,25},{25,17},{2,10},{10... | collective-permute-start | bytes 6291464 | tf_op jit(solution)/shard_map/ppermute | solution.py:869
  37.7 23.3 %collective-permute-start.5 = (bf16[256,2048]{1,0:T(8,128)(2,1)S(1)}, bf16[256,2048]{1,0:T(8,128)(2,1)}, u32[]{:S(2)}, u32[]{:S(2)}) collective-permute-start(bf16[256,2048]{1,0:T(8,128)(2,1)S(1)} %collective-permute-done.2.w1.refs_0_.w11), channel_id=1, source_target_pairs={{0,8},{8,0},{16,24},{24,16},{1,9},{9,1},{17,25},{25,17},{2,10},{10... | collective-permute-start | bytes 3145736 | tf_op jit(solution)/shard_map/ppermute | solution.py:869
  56.6 5.9 %collective-permute-start.6 = (bf16[256,2048]{1,0:T(8,128)(2,1)}, bf16[256,2048]{1,0:T(8,128)(2,1)}, u32[]{:S(2)}, u32[]{:S(2)}) collective-permute-start(bf16[256,2048]{1,0:T(8,128)(2,1)} %collective-permute-done.3.w2.refs_1_.w12), channel_id=1, source_target_pairs={{0,8},{8,0},{16,24},{24,16},{1,9},{9,1},{17,25},{25,17},{2,10},{10... | collective-permute-start | bytes 3145736 | tf_op jit(solution)/shard_map/ppermute | solution.py:869
  60.5 57.1 %collective-permute-start.9 = (bf16[512,2048]{1,0:T(8,128)(2,1)}, bf16[512,2048]{1,0:T(8,128)(2,1)}, u32[]{:S(2)}, u32[]{:S(2)}) collective-permute-start(bf16[512,2048]{1,0:T(8,128)(2,1)} %pack.4.w0.w20), channel_id=1, source_target_pairs={{0,8},{8,0},{16,24},{24,16},{1,9},{9,1},{17,25},{25,17},{2,10},{10... | collective-permute-start | bytes 6291464 | tf_op jit(solution)/shard_map/ppermute | solution.py:869
  61.0 25.3 %collective-permute-start.7 = (bf16[256,2048]{1,0:T(8,128)(2,1)}, bf16[256,2048]{1,0:T(8,128)(2,1)S(1)}, u32[]{:S(2)}, u32[]{:S(2)}) collective-permute-start(bf16[256,2048]{1,0:T(8,128)(2,1)} %convert_element_type.174.refs_0_), channel_id=1, source_target_pairs={{0,16},{16,0},{8,24},{24,8},{1,17},{17,1},{9,25},{25,9},{2,18},{18... | collective-permute-start | bytes 3145736 | tf_op jit(solution)/shard_map/ppermute | solution.py:866
  73.6 71.4 %collective-permute-start.13 = (bf16[1024,1024]{1,0:T(8,128)(2,1)}, bf16[1024,1024]{1,0:T(8,128)(2,1)}, u32[]{:S(2)}, u32[]{:S(2)}) collective-permute-start(bf16[1024,1024]{1,0:T(8,128)(2,1)} %kv.1.kv_ref), channel_id=1, source_target_pairs={{0,4},{1,5},{2,6},{3,7},{8,12},{9,13},{10,14},{11,15},{16,20},{17,... | collective-permute-start | bytes 6291464 | tf_op jit(solution)/shard_map/ppermute | solution.py:929
  86.3 12.2 %copy-start.30 = (bf16[256,2048]{1,0:T(8,128)(2,1)}, bf16[256,2048]{1,0:T(8,128)(2,1)S(1)}, u32[]{:S(2)}) copy-start(bf16[256,2048]{1,0:T(8,128)(2,1)S(1)} %collective-permute-done.7.w1.w21) | copy-start | bytes 3145732
  86.3 24.6 %collective-permute-start.8 = (bf16[256,2048]{1,0:T(8,128)(2,1)}, bf16[256,2048]{1,0:T(8,128)(2,1)}, u32[]{:S(2)}, u32[]{:S(2)}) collective-permute-start(bf16[256,2048]{1,0:T(8,128)(2,1)} %collective-permute-done.1.refs_1_), channel_id=1, source_target_pairs={{0,16},{16,0},{8,24},{24,8},{1,17},{17,1},{9,25},{25,9},{2,18},{18... | collective-permute-start | bytes 3145736 | tf_op jit(solution)/shard_map/ppermute | solution.py:866
  87.8 31.3 %collective-permute-start.10 = (bf16[256,2048]{1,0:T(8,128)(2,1)S(1)}, bf16[256,2048]{1,0:T(8,128)(2,1)S(1)}, u32[]{:S(2)}, u32[]{:S(2)}) collective-permute-start(bf16[256,2048]{1,0:T(8,128)(2,1)S(1)} %collective-permute-done.7.w1.w21), channel_id=1, source_target_pairs={{0,8},{8,0},{16,24},{24,16},{1,9},{9,1},{17,25},{25,17},{2,10},{10... | collective-permute-start | bytes 3145736 | tf_op jit(solution)/shard_map/ppermute | solution.py:869
  110.9 8.2 %collective-permute-start.11 = (bf16[256,2048]{1,0:T(8,128)(2,1)}, bf16[256,2048]{1,0:T(8,128)(2,1)S(1)}, u32[]{:S(2)}, u32[]{:S(2)}) collective-permute-start(bf16[256,2048]{1,0:T(8,128)(2,1)} %collective-permute-done.8.w2.w22), channel_id=1, source_target_pairs={{0,8},{8,0},{16,24},{24,16},{1,9},{9,1},{17,25},{25,17},{2,10},{10... | collective-permute-start | bytes 3145736 | tf_op jit(solution)/shard_map/ppermute | solution.py:869
  117.6 25.9 %collective-permute-start.15 = (bf16[256,2048]{1,0:T(8,128)(2,1)}, bf16[256,2048]{1,0:T(8,128)(2,1)}, u32[]{:S(2)}, u32[]{:S(2)}) collective-permute-start(bf16[256,2048]{1,0:T(8,128)(2,1)} %bitcast.21.refs_0_), channel_id=1, source_target_pairs={{0,16},{16,0},{8,24},{24,8},{1,17},{17,1},{9,25},{25,9},{2,18},{18... | collective-permute-start | bytes 3145736 | tf_op jit(solution)/shard_map/ppermute | solution.py:866
  140.7 18.0 %collective-permute-start.14 = (bf16[512,2048]{1,0:T(8,128)(2,1)}, bf16[512,2048]{1,0:T(8,128)(2,1)S(1)}, u32[]{:S(2)}, u32[]{:S(2)}) collective-permute-start(bf16[512,2048]{1,0:T(8,128)(2,1)} %pack.5.refs_2_.w0), channel_id=1, source_target_pairs={{0,8},{8,0},{16,24},{24,16},{1,9},{9,1},{17,25},{25,17},{2,10},{10... | collective-permute-start | bytes 6291464 | tf_op jit(solution)/shard_map/ppermute | solution.py:869
  143.5 32.1 %collective-permute-start.16 = (bf16[256,2048]{1,0:T(8,128)(2,1)}, bf16[256,2048]{1,0:T(8,128)(2,1)S(1)}, u32[]{:S(2)}, u32[]{:S(2)}) collective-permute-start(bf16[256,2048]{1,0:T(8,128)(2,1)} %collective-permute-done.12.refs_1_), channel_id=1, source_target_pairs={{0,16},{16,0},{8,24},{24,8},{1,17},{17,1},{9,25},{25,9},{2,18},{18... | collective-permute-start | bytes 3145736 | tf_op jit(solution)/shard_map/ppermute | solution.py:866
  157.3 28.0 %collective-permute-start.17 = (bf16[256,2048]{1,0:T(8,128)(2,1)}, bf16[256,2048]{1,0:T(8,128)(2,1)}, u32[]{:S(2)}, u32[]{:S(2)}) collective-permute-start(bf16[256,2048]{1,0:T(8,128)(2,1)} %collective-permute-done.15.refs_4_.w1), channel_id=1, source_target_pairs={{0,8},{8,0},{16,24},{24,16},{1,9},{9,1},{17,25},{25,17},{2,10},{10... | collective-permute-start | bytes 3145736 | tf_op jit(solution)/shard_map/ppermute | solution.py:869
  157.4 79.3 %collective-permute-start.22 = (bf16[1024,1024]{1,0:T(8,128)(2,1)}, bf16[1024,1024]{1,0:T(8,128)(2,1)}, u32[]{:S(2)}, u32[]{:S(2)}) collective-permute-start(bf16[1024,1024]{1,0:T(8,128)(2,1)} %get-tuple-element.165), channel_id=1, source_target_pairs={{4,0},{5,1},{6,2},{7,3},{12,8},{13,9},{14,10},{15,11},{20,16},{21,... | collective-permute-start | bytes 6291464 | tf_op jit(solution)/shard_map/ppermute | solution.py:932
  170.9 44.5 %collective-permute-start.19 = (bf16[1024,512]{1,0:T(8,128)(2,1)}, bf16[1024,512]{1,0:T(8,128)(2,1)}, u32[]{:S(2)}, u32[]{:S(2)}) collective-permute-start(bf16[1024,512]{1,0:T(8,128)(2,1)} %get-tuple-element.157), channel_id=1, source_target_pairs={{0,1},{3,2},{4,5},{7,6},{8,9},{11,10},{12,13},{15,14},{16,17},{19,... | collective-permute-start | bytes 3145736 | tf_op jit(solution)/shard_map/ppermute | solution.py:837
  175.5 9.5 %copy-start.31 = (bf16[256,2048]{1,0:T(8,128)(2,1)}, bf16[256,2048]{1,0:T(8,128)(2,1)S(1)}, u32[]{:S(2)}) copy-start(bf16[256,2048]{1,0:T(8,128)(2,1)S(1)} %collective-permute-done.16.refs_5_.w2) | copy-start | bytes 3145732
  175.5 12.1 %collective-permute-start.18 = (bf16[256,2048]{1,0:T(8,128)(2,1)S(1)}, bf16[256,2048]{1,0:T(8,128)(2,1)S(1)}, u32[]{:S(2)}, u32[]{:S(2)}) collective-permute-start(bf16[256,2048]{1,0:T(8,128)(2,1)S(1)} %collective-permute-done.16.refs_5_.w2), channel_id=1, source_target_pairs={{0,8},{8,0},{16,24},{24,16},{1,9},{9,1},{17,25},{25,17},{2,10},{10... | collective-permute-start | bytes 3145736 | tf_op jit(solution)/shard_map/ppermute | solution.py:869
  185.1 36.7 %collective-permute-start.20 = (bf16[1024,2048]{1,0:T(8,128)(2,1)}, bf16[1024,2048]{1,0:T(8,128)(2,1)}, u32[]{:S(2)}, u32[]{:S(2)}) collective-permute-start(bf16[1024,2048]{1,0:T(8,128)(2,1)} %wgrad.6), channel_id=1, source_target_pairs={{0,8},{8,0},{16,24},{24,16},{1,9},{9,1},{17,25},{25,17},{2,10},{10... | collective-permute-start | bytes 12582920 | tf_op jit(solution)/shard_map/ppermute | solution.py:869
  185.3 46.5 %collective-permute-start.21 = (bf16[1024,512]{1,0:T(8,128)(2,1)}, bf16[1024,512]{1,0:T(8,128)(2,1)}, u32[]{:S(2)}, u32[]{:S(2)}) collective-permute-start(bf16[1024,512]{1,0:T(8,128)(2,1)} %get-tuple-element.162), channel_id=1, source_target_pairs={{0,1},{3,2},{4,5},{7,6},{8,9},{11,10},{12,13},{15,14},{16,17},{19,... | collective-permute-start | bytes 3145736 | tf_op jit(solution)/shard_map/ppermute | solution.py:837
  200.3 15.1 %copy-start.14 = (bf16[1024,512]{1,0:T(8,128)(2,1)S(1)}, bf16[1024,512]{1,0:T(8,128)(2,1)}, u32[]{:S(2)}) copy-start(bf16[1024,512]{1,0:T(8,128)(2,1)} %get-tuple-element.157) | copy-start | bytes 3145732
  217.9 24.8 %collective-permute-start.23 = (bf16[1024,512]{1,0:T(8,128)(2,1)}, bf16[1024,512]{1,0:T(8,128)(2,1)}, u32[]{:S(2)}, u32[]{:S(2)}) collective-permute-start(bf16[1024,512]{1,0:T(8,128)(2,1)} %add_convert_fusion.15), channel_id=1, source_target_pairs={{1,2},{2,1},{5,6},{6,5},{9,10},{10,9},{13,14},{14,13},{17,18},{18,... | collective-permute-start | bytes 3145736 | tf_op jit(solution)/shard_map/ppermute | solution.py:847
  219.5 44.2 %collective-permute-start.24 = (bf16[1024,512]{1,0:T(8,128)(2,1)}, bf16[1024,512]{1,0:T(8,128)(2,1)}, u32[]{:S(2)}, u32[]{:S(2)}) collective-permute-start(bf16[1024,512]{1,0:T(8,128)(2,1)} %get-tuple-element.172), channel_id=1, source_target_pairs={{0,1},{3,2},{4,5},{7,6},{8,9},{11,10},{12,13},{15,14},{16,17},{19,... | collective-permute-start | bytes 3145736 | tf_op jit(solution)/shard_map/ppermute | solution.py:837
  234.7 32.3 %collective-permute-start.25 = (bf16[1024,512]{1,0:T(8,128)(2,1)}, bf16[1024,512]{1,0:T(8,128)(2,1)}, u32[]{:S(2)}, u32[]{:S(2)}) collective-permute-start(bf16[1024,512]{1,0:T(8,128)(2,1)} %add_convert_fusion.14), channel_id=1, source_target_pairs={{1,2},{2,1},{5,6},{6,5},{9,10},{10,9},{13,14},{14,13},{17,18},{18,... | collective-permute-start | bytes 3145736 | tf_op jit(solution)/shard_map/ppermute | solution.py:847
  245.7 32.7 %collective-permute-start.27 = (bf16[1024,512]{1,0:T(8,128)(2,1)}, bf16[1024,512]{1,0:T(8,128)(2,1)}, u32[]{:S(2)}, u32[]{:S(2)}) collective-permute-start(bf16[1024,512]{1,0:T(8,128)(2,1)} %fusion.refs_0_), channel_id=1, source_target_pairs={{0,1},{3,2},{1,0},{2,3},{4,5},{7,6},{5,4},{6,7},{8,9},{11,10},{9,8... | collective-permute-start | bytes 3145736 | tf_op jit(solution)/shard_map/ppermute | solution.py:837
  246.5 27.4 %collective-permute-start.26 = (bf16[512,2048]{1,0:T(8,128)(2,1)}, bf16[512,2048]{1,0:T(8,128)(2,1)}, u32[]{:S(2)}, u32[]{:S(2)}) collective-permute-start(bf16[512,2048]{1,0:T(8,128)(2,1)} %get-tuple-element.175), channel_id=1, source_target_pairs={{0,16},{4,20},{8,12},{12,8},{16,0},{20,4},{24,28},{28,24},{1,17},{... | collective-permute-start | bytes 6291464 | tf_op jit(solution)/shard_map/ppermute | solution.py:912
  265.6 17.1 %collective-permute-start.28 = (bf16[1024,512]{1,0:T(8,128)(2,1)S(1)}, bf16[1024,512]{1,0:T(8,128)(2,1)S(1)}, u32[]{:S(2)}, u32[]{:S(2)}) collective-permute-start(bf16[1024,512]{1,0:T(8,128)(2,1)S(1)} %add_convert_fusion.12), channel_id=1, source_target_pairs={{1,2},{2,1},{5,6},{6,5},{9,10},{10,9},{13,14},{14,13},{17,18},{18,... | collective-permute-start | bytes 3145736 | tf_op jit(solution)/shard_map/ppermute | solution.py:847
  269.9 8.4 %copy-start.3 = (bf16[1024,512]{1,0:T(8,128)(2,1)S(1)}, bf16[1024,512]{1,0:T(8,128)(2,1)}, u32[]{:S(2)}) copy-start(bf16[1024,512]{1,0:T(8,128)(2,1)} %get-tuple-element.177) | copy-start | bytes 3145732
  269.9 52.4 %collective-permute-start.29 = (bf16[1024,512]{1,0:T(8,128)(2,1)}, bf16[1024,512]{1,0:T(8,128)(2,1)}, u32[]{:S(2)}, u32[]{:S(2)}) collective-permute-start(bf16[1024,512]{1,0:T(8,128)(2,1)} %fusion.1.refs_4_), channel_id=1, source_target_pairs={{0,1},{3,2},{1,0},{2,3},{4,5},{7,6},{5,4},{6,7},{8,9},{11,10},{9,8... | collective-permute-start | bytes 3145736 | tf_op jit(solution)/shard_map/ppermute | solution.py:837
  281.0 46.3 %collective-permute-start.31 = (bf16[1024,512]{1,0:T(8,128)(2,1)}, bf16[1024,512]{1,0:T(8,128)(2,1)}, u32[]{:S(2)}, u32[]{:S(2)}) collective-permute-start(bf16[1024,512]{1,0:T(8,128)(2,1)} %add_convert_fusion.10), channel_id=1, source_target_pairs={{1,2},{2,1},{5,6},{6,5},{9,10},{10,9},{13,14},{14,13},{17,18},{18,... | collective-permute-start | bytes 3145736 | tf_op jit(solution)/shard_map/ppermute | solution.py:847
  284.2 67.2 %collective-permute-start.32 = (bf16[1024,512]{1,0:T(8,128)(2,1)}, bf16[1024,512]{1,0:T(8,128)(2,1)}, u32[]{:S(2)}, u32[]{:S(2)}) collective-permute-start(bf16[1024,512]{1,0:T(8,128)(2,1)} %fusion.2.refs_2_), channel_id=1, source_target_pairs={{0,1},{3,2},{1,0},{2,3},{4,5},{7,6},{5,4},{6,7},{8,9},{11,10},{9,8... | collective-permute-start | bytes 3145736 | tf_op jit(solution)/shard_map/ppermute | solution.py:837
  288.6 41.6 %collective-permute-start.30 = (bf16[256,2048]{1,0:T(8,128)(2,1)}, bf16[256,2048]{1,0:T(8,128)(2,1)}, u32[]{:S(2)}, u32[]{:S(2)}) collective-permute-start(bf16[256,2048]{1,0:T(8,128)(2,1)} %get-tuple-element.184), channel_id=1, source_target_pairs={{0,4},{4,0},{8,24},{12,28},{16,20},{20,16},{24,8},{28,12},{1,5},{5... | collective-permute-start | bytes 3145736 | tf_op jit(solution)/shard_map/ppermute | solution.py:912
  305.8 16.5 %copy-start.9 = (bf16[1024,512]{1,0:T(8,128)(2,1)S(1)}, bf16[1024,512]{1,0:T(8,128)(2,1)}, u32[]{:S(2)}) copy-start(bf16[1024,512]{1,0:T(8,128)(2,1)} %get-tuple-element.183) | copy-start | bytes 3145732
  324.9 29.9 %collective-permute-start.33 = (bf16[1024,512]{1,0:T(8,128)(2,1)}, bf16[1024,512]{1,0:T(8,128)(2,1)}, u32[]{:S(2)}, u32[]{:S(2)}) collective-permute-start(bf16[1024,512]{1,0:T(8,128)(2,1)} %add_convert_fusion.8), channel_id=1, source_target_pairs={{1,2},{2,1},{5,6},{6,5},{9,10},{10,9},{13,14},{14,13},{17,18},{18,... | collective-permute-start | bytes 3145736 | tf_op jit(solution)/shard_map/ppermute | solution.py:847
  339.3 12.0 %copy-start.5 = (bf16[1024,512]{1,0:T(8,128)(2,1)S(1)}, bf16[1024,512]{1,0:T(8,128)(2,1)}, u32[]{:S(2)}) copy-start(bf16[1024,512]{1,0:T(8,128)(2,1)} %get-tuple-element.189) | copy-start | bytes 3145732
  339.3 20.5 %collective-permute-start.34 = (bf16[1024,2048]{1,0:T(8,128)(2,1)}, bf16[1024,2048]{1,0:T(8,128)(2,1)}, u32[]{:S(2)}, u32[]{:S(2)}) collective-permute-start(bf16[1024,2048]{1,0:T(8,128)(2,1)} %wgrad.8), channel_id=1, source_target_pairs={{0,8},{8,0},{16,24},{24,16},{1,9},{9,1},{17,25},{25,17},{2,10},{10... | collective-permute-start | bytes 12582920 | tf_op jit(solution)/shard_map/ppermute | solution.py:869
  339.3 36.2 %collective-permute-start.35 = (bf16[1024,512]{1,0:T(8,128)(2,1)}, bf16[1024,512]{1,0:T(8,128)(2,1)}, u32[]{:S(2)}, u32[]{:S(2)}) collective-permute-start(bf16[1024,512]{1,0:T(8,128)(2,1)} %fusion.3.refs_6_), channel_id=1, source_target_pairs={{0,1},{3,2},{1,0},{2,3},{4,5},{7,6},{5,4},{6,7},{8,9},{11,10},{9,8... | collective-permute-start | bytes 3145736 | tf_op jit(solution)/shard_map/ppermute | solution.py:837
  353.0 24.1 %collective-permute-start.36 = (bf16[1024,512]{1,0:T(8,128)(2,1)S(1)}, bf16[1024,512]{1,0:T(8,128)(2,1)}, u32[]{:S(2)}, u32[]{:S(2)}) collective-permute-start(bf16[1024,512]{1,0:T(8,128)(2,1)S(1)} %add_convert_fusion.6), channel_id=1, source_target_pairs={{1,2},{2,1},{5,6},{6,5},{9,10},{10,9},{13,14},{14,13},{17,18},{18,... | collective-permute-start | bytes 3145736 | tf_op jit(solution)/shard_map/ppermute | solution.py:847
  357.8 51.3 %collective-permute-start.40 = (bf16[1024,512]{1,0:T(8,128)(2,1)}, bf16[1024,512]{1,0:T(8,128)(2,1)}, u32[]{:S(2)}, u32[]{:S(2)}) collective-permute-start(bf16[1024,512]{1,0:T(8,128)(2,1)} %fusion.4.refs_0_), channel_id=1, source_target_pairs={{0,1},{3,2},{1,0},{2,3},{4,5},{7,6},{5,4},{6,7},{8,9},{11,10},{9,8... | collective-permute-start | bytes 3145736 | tf_op jit(solution)/shard_map/ppermute | solution.py:837
  369.8 26.4 %collective-permute-start.37 = (bf16[512,2048]{1,0:T(8,128)(2,1)}, bf16[512,2048]{1,0:T(8,128)(2,1)}, u32[]{:S(2)}, u32[]{:S(2)}) collective-permute-start(bf16[512,2048]{1,0:T(8,128)(2,1)} %get-tuple-element.198), channel_id=1, source_target_pairs={{0,16},{4,20},{8,12},{12,8},{16,0},{20,4},{24,28},{28,24},{1,17},{... | collective-permute-start | bytes 6291464 | tf_op jit(solution)/shard_map/ppermute | solution.py:912
  379.6 33.7 %collective-permute-start.41 = (bf16[1024,512]{1,0:T(8,128)(2,1)S(1)}, bf16[1024,512]{1,0:T(8,128)(2,1)S(1)}, u32[]{:S(2)}, u32[]{:S(2)}) collective-permute-start(bf16[1024,512]{1,0:T(8,128)(2,1)S(1)} %add_convert_fusion.4), channel_id=1, source_target_pairs={{1,2},{2,1},{5,6},{6,5},{9,10},{10,9},{13,14},{14,13},{17,18},{18,... | collective-permute-start | bytes 3145736 | tf_op jit(solution)/shard_map/ppermute | solution.py:847
  380.3 41.5 %collective-permute-start.43 = (bf16[1024,2048]{1,0:T(8,128)(2,1)}, bf16[1024,2048]{1,0:T(8,128)(2,1)}, u32[]{:S(2)}, u32[]{:S(2)}) collective-permute-start(bf16[1024,2048]{1,0:T(8,128)(2,1)} %wgrad.9), channel_id=1, source_target_pairs={{0,8},{8,0},{16,24},{24,16},{1,9},{9,1},{17,25},{25,17},{2,10},{10... | collective-permute-start | bytes 12582920 | tf_op jit(solution)/shard_map/ppermute | solution.py:869
  380.4 20.2 %collective-permute-start.38 = (f32[13824]{0:T(1024)S(1)}, f32[13824]{0:T(1024)S(1)}, u32[]{:S(2)}, u32[]{:S(2)}) collective-permute-start(f32[13824]{0:T(1024)S(1)} %copy-done.15), channel_id=1, source_target_pairs={{0,8},{8,0},{16,24},{24,16},{1,9},{9,1},{17,25},{25,17},{2,10},{10... | collective-permute-start | bytes 165896 | tf_op jit(solution)/shard_map/ppermute | solution.py:869
  400.6 6.6 %collective-permute-start.39 = (f32[13824]{0:T(1024)S(1)}, f32[13824]{0:T(1024)S(1)}, u32[]{:S(2)}, u32[]{:S(2)}) collective-permute-start(f32[13824]{0:T(1024)S(1)} %add.115), channel_id=1, source_target_pairs={{0,16},{16,0},{8,24},{24,8},{1,17},{17,1},{9,25},{25,9},{2,18},{18... | collective-permute-start | bytes 165896 | tf_op jit(solution)/shard_map/ppermute | solution.py:866
  402.1 15.1 %collective-permute-start.42 = (bf16[256,2048]{1,0:T(8,128)(2,1)}, bf16[256,2048]{1,0:T(8,128)(2,1)}, u32[]{:S(2)}, u32[]{:S(2)}) collective-permute-start(bf16[256,2048]{1,0:T(8,128)(2,1)} %get-tuple-element.211), channel_id=1, source_target_pairs={{0,4},{4,0},{8,24},{12,28},{16,20},{20,16},{24,8},{28,12},{1,5},{5... | collective-permute-start | bytes 3145736 | tf_op jit(solution)/shard_map/ppermute | solution.py:912
  407.1 31.7 %collective-permute-start.46 = (bf16[1024,512]{1,0:T(8,128)(2,1)}, bf16[1024,512]{1,0:T(8,128)(2,1)}, u32[]{:S(2)}, u32[]{:S(2)}) collective-permute-start(bf16[1024,512]{1,0:T(8,128)(2,1)} %add_convert_fusion.3.refs_2_), channel_id=1, source_target_pairs={{1,0},{2,3},{5,4},{6,7},{9,8},{10,11},{13,12},{14,15},{17,16},{18,... | collective-permute-start | bytes 3145736 | tf_op jit(solution)/shard_map/ppermute | solution.py:837
  411.6 54.4 %collective-permute-start.49 = (bf16[1024,512]{1,0:T(8,128)(2,1)}, bf16[1024,512]{1,0:T(8,128)(2,1)}, u32[]{:S(2)}, u32[]{:S(2)}) collective-permute-start(bf16[1024,512]{1,0:T(8,128)(2,1)} %add_convert_fusion.2), channel_id=1, source_target_pairs={{1,2},{2,1},{5,6},{6,5},{9,10},{10,9},{13,14},{14,13},{17,18},{18,... | collective-permute-start | bytes 3145736 | tf_op jit(solution)/shard_map/ppermute | solution.py:847
  414.5 54.9 %collective-permute-start.48 = (bf16[1024,512]{1,0:T(8,128)(2,1)}, bf16[1024,512]{1,0:T(8,128)(2,1)}, u32[]{:S(2)}, u32[]{:S(2)}) collective-permute-start(bf16[1024,512]{1,0:T(8,128)(2,1)} %add_convert_fusion.1.refs_4_), channel_id=1, source_target_pairs={{1,0},{2,3},{5,4},{6,7},{9,8},{10,11},{13,12},{14,15},{17,16},{18,... | collective-permute-start | bytes 3145736 | tf_op jit(solution)/shard_map/ppermute | solution.py:837
  421.2 16.8 %collective-permute-start.44 = (f32[13824]{0:T(1024)}, f32[13824]{0:T(1024)}, u32[]{:S(2)}, u32[]{:S(2)}) collective-permute-start(f32[13824]{0:T(1024)} %add.117), channel_id=1, source_target_pairs={{0,4},{4,0},{1,5},{5,1},{2,6},{6,2},{3,7},{7,3},{8,12},{12,8},{9,1... | collective-permute-start | bytes 165896 | tf_op jit(solution)/shard_map/ppermute | solution.py:872
  432.6 26.2 %collective-permute-start.45 = (bf16[512,2048]{1,0:T(8,128)(2,1)}, bf16[512,2048]{1,0:T(8,128)(2,1)S(1)}, u32[]{:S(2)}, u32[]{:S(2)}) collective-permute-start(bf16[512,2048]{1,0:T(8,128)(2,1)} %get-tuple-element.218), channel_id=1, source_target_pairs={{0,16},{4,20},{8,12},{12,8},{16,0},{20,4},{24,28},{28,24},{1,17},{... | collective-permute-start | bytes 6291464 | tf_op jit(solution)/shard_map/ppermute | solution.py:912
  464.5 15.0 %collective-permute-start.47 = (bf16[256,2048]{1,0:T(8,128)(2,1)}, bf16[256,2048]{1,0:T(8,128)(2,1)S(1)}, u32[]{:S(2)}, u32[]{:S(2)}) collective-permute-start(bf16[256,2048]{1,0:T(8,128)(2,1)} %get-tuple-element.223), channel_id=1, source_target_pairs={{0,4},{4,0},{8,24},{12,28},{16,20},{20,16},{24,8},{28,12},{1,5},{5... | collective-permute-start | bytes 3145736 | tf_op jit(solution)/shard_map/ppermute | solution.py:912
  467.8 17.0 %copy-start.13 = (bf16[1024,512]{1,0:T(8,128)(2,1)}, bf16[1024,512]{1,0:T(8,128)(2,1)S(1)}, u32[]{:S(2)}) copy-start(bf16[1024,512]{1,0:T(8,128)(2,1)S(1)} %add_convert_fusion.refs_6_) | copy-start | bytes 3145732
  467.8 27.2 %collective-permute-start.51 = (bf16[1024,512]{1,0:T(8,128)(2,1)S(1)}, bf16[1024,512]{1,0:T(8,128)(2,1)S(1)}, u32[]{:S(2)}, u32[]{:S(2)}) collective-permute-start(bf16[1024,512]{1,0:T(8,128)(2,1)S(1)} %add_convert_fusion.refs_6_), channel_id=1, source_target_pairs={{1,0},{2,3},{5,4},{6,7},{9,8},{10,11},{13,12},{14,15},{17,16},{18,... | collective-permute-start | bytes 3145736 | tf_op jit(solution)/shard_map/ppermute | solution.py:837
  484.8 9.2 %collective-permute-start.50 = (f32[8192]{0:T(1024)S(1)}, f32[8192]{0:T(1024)S(1)}, u32[]{:S(2)}, u32[]{:S(2)}) collective-permute-start(f32[8192]{0:T(1024)S(1)} %slice.40), channel_id=1, source_target_pairs={{0,1},{1,0},{2,3},{3,2},{4,5},{5,4},{6,7},{7,6},{8,9},{9,8},{10,11... | collective-permute-start | bytes 98312 | tf_op jit(solution)/shard_map/ppermute | solution.py:945
  490.8 16.9 %copy-start.18 = (f32[2048]{0:T(1024)}, f32[2048]{0:T(1024)S(1)}, u32[]{:S(2)}) copy-start(f32[2048]{0:T(1024)S(1)} %get-tuple-element.272) | copy-start | bytes 24580
  494.0 13.1 %collective-permute-start.52 = (f32[8192]{0:T(1024)S(1)}, f32[8192]{0:T(1024)S(1)}, u32[]{:S(2)}, u32[]{:S(2)}) collective-permute-start(f32[8192]{0:T(1024)S(1)} %add.122), channel_id=1, source_target_pairs={{0,2},{2,0},{1,3},{3,1},{4,6},{6,4},{5,7},{7,5},{8,10},{10,8},{9,1... | collective-permute-start | bytes 98312 | tf_op jit(solution)/shard_map/ppermute | solution.py:947
  (24 other events, 85.5 us)

commit v6 on v5

--- a/solution.py
+++ b/solution.py
@@ -1087,12 +1087,12 @@
     dqkv, bqkv_sum = run(join_call, dq, dkv, rv, tabs, nheads)
     pipe.send(out3)
     gain_sums = jnp.zeros((4, d), F32)
+    pipe.cross()
     dn0, dn1, gain_sums = run(back_call, meta, dqkv, du, g1, g2, x2, stats, ga, gf, gain_sums, 0)
-    pipe.cross()
     pipe.send(dn0)
-    state3 = comm.scatter_half(run, state3)
     pipe.cross()
     pipe.send(dn1)
+    state3 = comm.scatter_half(run, state3)
     dn2, dn3, gain_sums = run(back_call, meta, dqkv, du, g1, g2, x2, stats, ga, gf, gain_sums, 1)
     pipe.cross()
     pipe.send(dn2)
@@ -1129,18 +1129,16 @@
     small = add()
     gains = small[: 4 * d]
     group = small[4 * d :]
+    pipe.send()
     state1 = comm.scatter_half(run, after(state1, pipe.sent[5]))
-    pipe.send()
-    grad_qkv, grad_proj = comm.scatter_last(
-        run, ((nq // 512, False), (nheads * HD // 512, True)), after(state1, pipe.sent[6])
-    )
-    add = comm.small_sum(run, after(gains, grad_qkv), 3)
-    gains = add()
-    add = comm.small_sum(run, gains, 4)
+    add = comm.small_sum(run, after(gains, *jax.tree.leaves(state1)[:1]), 3)
     input_grad = run(
         rows_call, meta, x2, og2, stats, *sums_of(range(4, 8)),
         body=functools.partial(input_grad_kernel, local_len), name="igrad", specs=("row", "row", "stat") + ("part",) * 8,
     ).reshape(slots, local_len, d)
+    gains = add()
+    add = comm.small_sum(run, gains, 4)
+    grad_qkv, grad_proj = comm.scatter_last(run, ((nq // 512, False), (nheads * HD // 512, True)), state1)
     gains = add().reshape(4, d)
     bias_grad = group[:d]
     return (

time: 516 us -> 504 us (0.977)
  waiting for transfers between devices: 95.1 us -> 87.2 us
  starting transfers between devices: 90 us -> 83.8 us
    ppermute x6, waiting for transfers between devices: 46.9 us -> 32 us  [turn(): return lax.ppermute(v, ('dp', 'ctx'), pairs)]
    ppermute x11, waiting for transfers between devices: 0.03 us -> 9.6 us  [send(): got = lax.ppermute(v, 'tensor', pairs)]
    ppermute x6, starting transfers between devices: 21.2 us -> 12.7 us  [turn(): return lax.ppermute(v, ('dp', 'ctx'), pairs)]
    unnamed x74 -> x70, local copies, waits for them, and re-layouts: 12.7 us -> 11.7 us
  transfers between devices with their start and end apart: 53 -> 53, of which waited for: 11 -> 10; matrix products, arithmetic and copies ran while one was open for 10% -> 10% of each run, Pallas kernels for 51% -> 52%
where the time goes in v6:
time: 504 us; the launch traced here: 497 us
  Pallas kernels  260 us (52%)
  waiting for transfers between devices  87.2 us (17%)
  starting transfers between devices  83.8 us (17%)
  other arithmetic  48.7 us (10%)
  local copies, waits for them, and re-layouts  15.4 us (3%)
    pallas_call x6, Pallas kernels, wgrad_call(): pl.pallas_call(functools.partial(wgrad_kernel, counts, add is not None, s...  59.5 us
    ppermute x7, waiting for transfers between devices, x(): return lax.ppermute(v, 'dp', [(0, 2), (2, 0), (1, 3), (3, 1)])  42.7 us
    pallas_call x2, Pallas kernels, back_call(): pl.pallas_call(back_kernel, name='backn', grid_spec=pltpu.PrefetchScalarG...  32.3 us
    ppermute x6, waiting for transfers between devices, turn(): return lax.ppermute(v, ('dp', 'ctx'), pairs)  32 us
    ppermute x11, starting transfers between devices, send(): got = lax.ppermute(v, 'tensor', pairs)  30.2 us
    convert_element_type x11, other arithmetic, add_bf(): return lax.optimization_barrier((a.astype(F32) + b.astype(F32)).astype(BF))  24.4 us
    pallas_call x2, Pallas kernels, out_call(): pl.pallas_call(functools.partial(out_kernel, count), name='outp', grid=(4...  22.6 us
    pallas_call x3, Pallas kernels, rows_call(): pl.pallas_call(functools.partial(body, first), name=name, grid_spec=pltpu...  20.8 us
  transfers between devices with their start and end apart: 53, of which 10 were waited for; matrix products, arithmetic and copies ran while one was open for 10% of the time, Pallas kernels for 52%

profile of v6, /device:TPU:0, one launch (start us, length us, event | category | flops | bytes accessed | tf_op | source)
XLA Modules:
  0.0 496.6 jit_solution(13304445092567754812)
XLA Ops:
  4.6 3.0 collective-permute-start
  10.7 2.6 copy.32
  15.4 10.5 %norm.1 = (bf16[1024,2048]{1,0:T(8,128)(2,1)}, bf16[1024,2048]{1,0:T(8,128)(2,1)}, f32[1024,128]{1,0:T(8,128)}, f32[1,2048]{1,0:T(1,128)}) custom-call(s32[13]{0:T(128)} %concatenate.10.meta, bf16[1024,2048]{1,0:T(8,128)(2,1)} %bitcast.30, bf16[1024,2048]{1,0:T(8,128)(2,1)} %bitcast.37, f32[1,2048]{1,0:T(1,128)} %bitcast.42, f32[1,2048]{1,0:T(1,128)} %bitcast.39), custom_call_target="tpu_custom_call" | custom-call | flops 125829120000 | bytes 419430400 | tf_op jit(solution)/shard_map/norm/pallas_call | solution.py:127
  27.2 1.9 fusion.5
  29.1 2.8 collective-permute-done.refs_1_
  33.9 3.8 pack.3.w0.refs_0_.w10
  38.2 18.4 %collective-permute-done.3.w2.refs_1_.w12 = bf16[256,2048]{1,0:T(8,128)(2,1)} collective-permute-done((bf16[256,2048]{1,0:T(8,128)(2,1)}, bf16[256,2048]{1,0:T(8,128)(2,1)}, u32[]{:S(2)}, u32[]{:S(2)}) %collective-permute-start.3) | collective-permute-done | bytes 1048608 | tf_op jit(solution)/shard_map/ppermute | solution.py:866
  56.6 3.9 pack.4.w0.w20
  63.8 9.8 %kv.1.kv_ref = bf16[1024,1024]{1,0:T(8,128)(2,1)} custom-call(bf16[1024,2048]{1,0:T(8,128)(2,1)} %get-tuple-element.128.h1.refs_0_, bf16[512,2048]{1,0:T(8,128)(2,1)} %pack.3.w0.refs_0_.w10, bf16[256,2048]{1,0:T(8,128)(2,1)} %copy-done.26, bf16[256,2048]{1,0:T(8,128)(2,1)} %collective-permute-done.3.w2.refs_1_.w12, bf16[512,2048]{1,0:T(8,128)(2,1)} %copy-done.10, ...), custom_call_target="tpu_custom_call" | custom-call | flops 85899345920 | bytes 209715200 | tf_op jit(solution)/shard_map/kv/pallas_call | solution.py:183
  73.6 3.9 collective-permute-start.13
  77.5 8.8 %collective-permute-done.7.w1.w21 = bf16[256,2048]{1,0:T(8,128)(2,1)S(1)} collective-permute-done((bf16[256,2048]{1,0:T(8,128)(2,1)}, bf16[256,2048]{1,0:T(8,128)(2,1)S(1)}, u32[]{:S(2)}, u32[]{:S(2)}) %collective-permute-start.7) | collective-permute-done | bytes 1048608 | tf_op jit(solution)/shard_map/ppermute | solution.py:866
  87.8 10.7 %qd.1 = (bf16[1024,512]{1,0:T(8,128)(2,1)}, bf16[1024,512]{1,0:T(8,128)(2,1)}) custom-call(bf16[1024,2048]{1,0:T(8,128)(2,1)} %get-tuple-element.128.h1.refs_0_, bf16[1024,2048]{1,0:T(8,128)(2,1)} %get-tuple-element.152.g.refs_0_.refs_2_, bf16[512,2048]{1,0:T(8,128)(2,1)} %pack.3.w0.refs_0_.w10, bf16[256,2048]{1,0:T(8,128)(2,1)} %copy-done.26, ...), custom_call_target="tpu_custom_call" | custom-call | flops 88080384000 | bytes 293601280 | tf_op jit(solution)/shard_map/qd/pallas_call | solution.py:224
  98.5 12.4 %collective-permute-done.8.w2.w22 = bf16[256,2048]{1,0:T(8,128)(2,1)} collective-permute-done((bf16[256,2048]{1,0:T(8,128)(2,1)}, bf16[256,2048]{1,0:T(8,128)(2,1)}, u32[]{:S(2)}, u32[]{:S(2)}) %collective-permute-start.8) | collective-permute-done | bytes 1048608 | tf_op jit(solution)/shard_map/ppermute | solution.py:866
  110.9 6.7 %norm2.1.h2.refs_0_ = bf16[1024,2048]{1,0:T(8,128)(2,1)} custom-call(s32[13]{0:T(128)} %concatenate.10.meta, bf16[1024,2048]{1,0:T(8,128)(2,1)} %bitcast.31, f32[1024,128]{1,0:T(8,128)} %get-tuple-element.132.st_ref, f32[1,2048]{1,0:T(1,128)} %bitcast.45, f32[1,2048]{1,0:T(1,128)} %bitcast.40), custom_call_target="tpu_custom_call" | custom-call | flops 50331648000 | bytes 167772160 | tf_op jit(solution)/shard_map/norm2/pallas_call | solution.py:107
  120.5 16.4 %hidden.1 = (bf16[1024,2048]{1,0:T(8,128)(2,1)}, bf16[1024,2048]{1,0:T(8,128)(2,1)}) custom-call(bf16[1024,2048]{1,0:T(8,128)(2,1)} %norm2.1.h2.refs_0_, bf16[512,2048]{1,0:T(8,128)(2,1)} %pack.4.w0.w20, bf16[256,2048]{1,0:T(8,128)(2,1)} %copy-done.29, bf16[256,2048]{1,0:T(8,128)(2,1)} %collective-permute-done.8.w2.w22, ...), custom_call_target="tpu_custom_call" | custom-call | flops 171798691840 | bytes 419430400 | tf_op jit(solution)/shard_map/hidden/pallas_call | solution.py:413
  136.9 3.8 pack.5.refs_2_.w0
  140.9 2.5 collective-permute-done.15.refs_4_.w1
  145.0 12.4 %attn.1 = (bf16[1024,512]{1,0:T(8,128)(2,1)}, bf16[1024,512]{1,0:T(8,128)(2,1)}, f32[1024,1024]{1,0:T(8,128)}, bf16[1024,1024]{1,0:T(8,128)(2,1)}) custom-call(s32[13]{0:T(128)} %concatenate.10.meta, bf16[1024,512]{1,0:T(8,128)(2,1)} %get-tuple-element.130.q_ref, bf16[1024,1024]{1,0:T(8,128)(2,1)} %kv.1.kv_ref, ...), custom_call_target="tpu_custom_call" | custom-call | flops 128849018880 | bytes 209715200 | tf_op jit(solution)/shard_map/attn/pallas_call | solution.py:333
  160.0 10.9 %outp.2 = (bf16[1024,512]{1,0:T(8,128)(2,1)}, bf16[1024,512]{1,0:T(8,128)(2,1)}) custom-call(bf16[1024,512]{1,0:T(8,128)(2,1)} %get-tuple-element.146.ob.refs_3_, bf16[1024,2048]{1,0:T(8,128)(2,1)} %get-tuple-element.138.gb.refs_1_, bf16[512,2048]{1,0:T(8,128)(2,1)} %pack.3.w0.refs_0_.w10, bf16[512,2048]{1,0:T(8,128)(2,1)} %copy-done.10, ...), custom_call_target="tpu_custom_call" | custom-call | flops 53687092 | bytes 125829 | tf_op jit(solution)/shard_map/outp/pallas_call | solution.py:479
  170.9 4.8 collective-permute-start.19
  176.0 9.2 %wgrad.6 = bf16[1024,2048]{1,0:T(8,128)(2,1)} custom-call(s32[13]{0:T(128)} %concatenate.10.meta, bf16[1024,2048]{1,0:T(8,128)(2,1)} %get-tuple-element.152.g.refs_0_.refs_2_, bf16[1024,2048]{1,0:T(8,128)(2,1)} %get-tuple-element.138.gb.refs_1_), custom_call_target="tpu_custom_call" | custom-call | flops 88080384000 | bytes 293601280 | tf_op jit(solution)/shard_map/wgrad/pallas_call | solution.py:602
  185.6 2.3 collective-permute-start.21
  188.9 11.7 %outp.3 = (bf16[1024,512]{1,0:T(8,128)(2,1)}, bf16[1024,512]{1,0:T(8,128)(2,1)}) custom-call(bf16[1024,512]{1,0:T(8,128)(2,1)} %get-tuple-element.146.ob.refs_3_, bf16[1024,2048]{1,0:T(8,128)(2,1)} %get-tuple-element.138.gb.refs_1_, bf16[256,2048]{1,0:T(8,128)(2,1)} %copy-done.26, bf16[256,2048]{1,0:T(8,128)(2,1)} %collective-permute-done.3.w2.refs_1_.w12, ...), custom_call_target="tpu_custom_call" | custom-call | flops 107374182400 | bytes 251658240 | tf_op jit(solution)/shard_map/outp/pallas_call | solution.py:479
  200.6 15.1 %dhid.1 = (bf16[1024,2048]{1,0:T(8,128)(2,1)}, f32[1,2048]{1,0:T(1,128)}) custom-call(bf16[1024,2048]{1,0:T(8,128)(2,1)} %get-tuple-element.152.g.refs_0_.refs_2_, bf16[512,2048]{1,0:T(8,128)(2,1)} %pack.5.refs_2_.w0, bf16[256,2048]{1,0:T(8,128)(2,1)} %collective-permute-done.15.refs_4_.w1, bf16[256,2048]{1,0:T(8,128)(2,1)} %copy-done.30, ...), custom_call_target="tpu_custom_call" | custom-call | flops 171798691840 | bytes 419430400 | tf_op jit(solution)/shard_map/dhid/pallas_call | solution.py:438
  215.7 2.5 add_convert_fusion.15
  219.8 2.3 collective-permute-start.24
  222.1 10.0 %wgrad.7 = (bf16[512,2048]{1,0:T(8,128)(2,1)}, bf16[512,2048]{1,0:T(8,128)(2,1)}) custom-call(s32[13]{0:T(128)} %concatenate.10.meta, bf16[1024,2048]{1,0:T(8,128)(2,1)} %get-tuple-element.152.g.refs_0_.refs_2_, bf16[1024,2048]{1,0:T(8,128)(2,1)} %get-tuple-element.138.gb.refs_1_, bf16[1024,2048]{1,0:T(8,128)(2,1)} %collective-permute-done.20.refs_2_), custom_call_target="tpu_custom_call" | custom-call | flops 88080384000 | bytes 293601280 | tf_op jit(solution)/shard_map/wgrad/pallas_call | solution.py:602
  232.1 2.8 add_convert_fusion.14
  236.6 6.0 %join.1 = (bf16[1024,1536]{1,0:T(8,128)(2,1)}, f32[1,1536]{1,0:T(1,128)}) custom-call(bf16[1024,512]{1,0:T(8,128)(2,1)} %get-tuple-element.162.dq_ref, f32[1024,1024]{1,0:T(8,128)} %get-tuple-element.163.dkv_ref, bf16[1024,1024]{1,0:T(8,128)(2,1)} %collective-permute-done.22.rv_ref, f32[512,128]{1,0:T(8,128)} %get-tuple-element.238.cosf, ...), custom_call_target="tpu_custom_call" | custom-call | flops 75497472000 | bytes 251658240 | tf_op jit(solution)/shard_map/join/pallas_call | solution.py:388
  242.6 2.9 fusion.refs_0_
  246.8 2.8 add_convert_fusion.12
  252.4 16.0 %backn.2 = (bf16[1024,512]{1,0:T(8,128)(2,1)}, bf16[1024,512]{1,0:T(8,128)(2,1)}, f32[4,2048]{1,0:T(4,128)}) custom-call(s32[13]{0:T(128)} %concatenate.10.meta, bf16[1024,1536]{1,0:T(8,128)(2,1)} %get-tuple-element.165.dqkv.refs_1_, bf16[1024,2048]{1,0:T(8,128)(2,1)} %get-tuple-element.154.du.refs_1_, ...), custom_call_target="tpu_custom_call", output_to_operand_aliasing={{2}: (13, {})} | custom-call | flops 150323855360 | bytes 377487360 | tf_op jit(solution)/shard_map/backn/pallas_call | solution.py:523
  269.1 3.3 fusion.1.refs_4_
  272.5 2.3 collective-permute-start.29
  274.8 2.5 add_convert_fusion.10
  279.0 3.0 fusion.2.refs_2_
  282.0 9.3 %collective-permute-start.32 = (bf16[1024,512]{1,0:T(8,128)(2,1)}, bf16[1024,512]{1,0:T(8,128)(2,1)}, u32[]{:S(2)}, u32[]{:S(2)}) collective-permute-start(bf16[1024,512]{1,0:T(8,128)(2,1)} %fusion.2.refs_2_), channel_id=1, source_target_pairs={{0,1},{3,2},{1,0},{2,3},{4,5},{7,6},{5,4},{6,7},{8,9},{11,10},{9,8... | collective-permute-start | bytes 3145736 | tf_op jit(solution)/shard_map/ppermute | solution.py:837
  291.3 4.4 hsum.3
  295.7 10.1 %collective-permute-start.30 = (bf16[256,2048]{1,0:T(8,128)(2,1)}, bf16[256,2048]{1,0:T(8,128)(2,1)}, u32[]{:S(2)}, u32[]{:S(2)}) collective-permute-start(bf16[256,2048]{1,0:T(8,128)(2,1)} %get-tuple-element.182), channel_id=1, source_target_pairs={{0,4},{4,0},{8,24},{12,28},{16,20},{20,16},{24,8},{28,12},{1,5},{5... | collective-permute-start | bytes 3145736 | tf_op jit(solution)/shard_map/ppermute | solution.py:912
  305.8 16.2 %backn.3 = (bf16[1024,512]{1,0:T(8,128)(2,1)}, bf16[1024,512]{1,0:T(8,128)(2,1)}, f32[4,2048]{1,0:T(4,128)}) custom-call(s32[13]{0:T(128)} %concatenate.10.meta, bf16[1024,1536]{1,0:T(8,128)(2,1)} %get-tuple-element.165.dqkv.refs_1_, bf16[1024,2048]{1,0:T(8,128)(2,1)} %get-tuple-element.154.du.refs_1_, ...), custom_call_target="tpu_custom_call", output_to_operand_aliasing={{2}: (13, {})} | custom-call | flops 150323855360 | bytes 377487360 | tf_op jit(solution)/shard_map/backn/pallas_call | solution.py:523
  322.1 2.6 add_convert_fusion.8
  326.4 3.0 fusion.3.refs_6_
  331.8 9.2 %wgrad.8 = bf16[1024,2048]{1,0:T(8,128)(2,1)} custom-call(s32[13]{0:T(128)} %concatenate.10.meta, bf16[1024,2048]{1,0:T(8,128)(2,1)} %norm2.1.h2.refs_0_, bf16[1024,2048]{1,0:T(8,128)(2,1)} %get-tuple-element.154.du.refs_1_), custom_call_target="tpu_custom_call" | custom-call | flops 88080384000 | bytes 293601280 | tf_op jit(solution)/shard_map/wgrad/pallas_call | solution.py:602
  341.0 10.3 %wgrad.9 = bf16[1024,2048]{1,0:T(8,128)(2,1)} custom-call(s32[13]{0:T(128)} %concatenate.10.meta, bf16[1024,2048]{1,0:T(8,128)(2,1)} %get-tuple-element.128.h1.refs_0_, bf16[1024,1536]{1,0:T(8,128)(2,1)} %get-tuple-element.165.dqkv.refs_1_, bf16[1024,2048]{1,0:T(8,128)(2,1)} %get-tuple-element.152.g.refs_0_.refs_2_, ...), custom_call_target="tpu_custom_call" | custom-call | flops 100663296000 | bytes 335544320 | tf_op jit(solution)/shard_map/wgrad/pallas_call | solution.py:602
  352.9 1.8 collective-permute-start.36
  354.7 2.9 fusion.4.refs_0_
  357.7 2.0 collective-permute-start.40
  359.7 10.0 %wgrad.10 = (bf16[512,2048]{1,0:T(8,128)(2,1)}, bf16[512,2048]{1,0:T(8,128)(2,1)}) custom-call(s32[13]{0:T(128)} %concatenate.10.meta, bf16[1024,2048]{1,0:T(8,128)(2,1)} %norm2.1.h2.refs_0_, bf16[1024,2048]{1,0:T(8,128)(2,1)} %get-tuple-element.154.du.refs_1_, bf16[1024,2048]{1,0:T(8,128)(2,1)} %collective-permute-done.34.refs_2_), custom_call_target="tpu_custom_call" | custom-call | flops 88080384000 | bytes 293601280 | tf_op jit(solution)/shard_map/wgrad/pallas_call | solution.py:602
  370.3 4.3 lsum.3
  377.0 2.5 add_convert_fusion.3.refs_2_
  380.0 16.1 %collective-permute-done.37.got = bf16[512,2048]{1,0:T(8,128)(2,1)} collective-permute-done((bf16[512,2048]{1,0:T(8,128)(2,1)}, bf16[512,2048]{1,0:T(8,128)(2,1)}, u32[]{:S(2)}, u32[]{:S(2)}) %collective-permute-start.37) | collective-permute-done | bytes 2097184 | tf_op jit(solution)/shard_map/ppermute | solution.py:912
  396.0 4.5 hsum.4
  401.2 5.0 bout.2.refs_8_
  408.1 2.5 add_convert_fusion.2
  416.3 4.0 lsum.4
  420.9 10.8 %wgrad.11 = (bf16[512,2048]{1,0:T(8,128)(2,1)}, bf16[512,2048]{1,0:T(8,128)(2,1)}) custom-call(s32[13]{0:T(128)} %concatenate.10.meta, bf16[1024,2048]{1,0:T(8,128)(2,1)} %get-tuple-element.128.h1.refs_0_, bf16[1024,1536]{1,0:T(8,128)(2,1)} %get-tuple-element.165.dqkv.refs_1_, bf16[1024,2048]{1,0:T(8,128)(2,1)} %get-tuple-element.152.g.refs_0_.refs_2_, ...), custom_call_target="tpu_custom_call" | custom-call | flops 100663296000 | bytes 335544320 | tf_op jit(solution)/shard_map/wgrad/pallas_call | solution.py:602
  433.1 4.8 bout.3
  439.4 1.8 add_convert_fusion.refs_6_
  443.4 14.5 %collective-permute-done.44.got = bf16[512,2048]{1,0:T(8,128)(2,1)S(1)} collective-permute-done((bf16[512,2048]{1,0:T(8,128)(2,1)}, bf16[512,2048]{1,0:T(8,128)(2,1)S(1)}, u32[]{:S(2)}, u32[]{:S(2)}) %collective-permute-start.44) | collective-permute-done | bytes 2097184 | tf_op jit(solution)/shard_map/ppermute | solution.py:912
  459.3 4.5 hsum.5
  463.7 5.3 %collective-permute-start.50 = (f32[8192]{0:T(1024)S(1)}, f32[8192]{0:T(1024)S(1)}, u32[]{:S(2)}, u32[]{:S(2)}) collective-permute-start(f32[8192]{0:T(1024)S(1)} %slice.40), channel_id=1, source_target_pairs={{0,1},{1,0},{2,3},{3,2},{4,5},{5,4},{6,7},{7,6},{8,9},{9,8},{10,11... | collective-permute-start | bytes 98312 | tf_op jit(solution)/shard_map/ppermute | solution.py:945
  469.0 9.6 %collective-permute-done.49.refs_7_ = bf16[1024,512]{1,0:T(8,128)(2,1)} collective-permute-done((bf16[1024,512]{1,0:T(8,128)(2,1)S(1)}, bf16[1024,512]{1,0:T(8,128)(2,1)}, u32[]{:S(2)}, u32[]{:S(2)}) %collective-permute-start.49) | collective-permute-done | bytes 1048608 | tf_op jit(solution)/shard_map/ppermute | solution.py:837
  478.6 11.1 %igrad.1 = bf16[1024,2048]{1,0:T(8,128)(2,1)} custom-call(s32[13]{0:T(128)} %concatenate.10.meta, bf16[1024,2048]{1,0:T(8,128)(2,1)} %bitcast.36, bf16[1024,2048]{1,0:T(8,128)(2,1)} %bitcast.38, f32[1024,128]{1,0:T(8,128)} %get-tuple-element.132.st_ref, bf16[1024,512]{1,0:T(8,128)(2,1)} %fusion.4.refs_0_, bf16[1024,512]{1,0:T(8,128)(2,1)} %collective-permute-done.40.refs_1_, ...), custom_call_target="tpu_custom_call" | custom-call | flops 100663296000 | bytes 335544320 | tf_op jit(solution)/shard_map/igrad/pallas_call | solution.py:775
  490.8 4.3 lsum.5
  (182 shorter events, 63.2 us)
Async XLA Ops:
  0.6 8.4 %copy-start.9 = (f32[256,2048]{1,0:T(8,128)S(1)}, f32[256,2048]{1,0:T(8,128)}, u32[]{:S(2)}) copy-start(f32[256,2048]{1,0:T(8,128)} %param.26) | copy-start | bytes 6291460
  4.6 27.3 %collective-permute-start = (bf16[256,2048]{1,0:T(8,128)(2,1)}, bf16[256,2048]{1,0:T(8,128)(2,1)}, u32[]{:S(2)}, u32[]{:S(2)}) collective-permute-start(bf16[256,2048]{1,0:T(8,128)(2,1)} %pad_maximum_fusion.refs_0_), channel_id=1, source_target_pairs={{0,4},{4,0},{1,5},{5,1},{2,6},{6,2},{3,7},{7,3},{8,12},{12,8},{9,1... | collective-permute-start | bytes 3145736 | tf_op jit(solution)/shard_map/ppermute | solution.py:872
  7.6 24.8 %collective-permute-start.2 = (bf16[256,2048]{1,0:T(8,128)(2,1)}, bf16[256,2048]{1,0:T(8,128)(2,1)S(1)}, u32[]{:S(2)}, u32[]{:S(2)}) collective-permute-start(bf16[256,2048]{1,0:T(8,128)(2,1)} %pad_maximum_fusion.refs_0_), channel_id=1, source_target_pairs={{0,16},{16,0},{8,24},{24,8},{1,17},{17,1},{9,25},{25,9},{2,18},{18... | collective-permute-start | bytes 3145736 | tf_op jit(solution)/shard_map/ppermute | solution.py:866
  10.2 46.4 %collective-permute-start.1 = (bf16[256,2048]{1,0:T(8,128)(2,1)}, bf16[256,2048]{1,0:T(8,128)(2,1)}, u32[]{:S(2)}, u32[]{:S(2)}) collective-permute-start(bf16[256,2048]{1,0:T(8,128)(2,1)} %convert_element_type.174.refs_0_), channel_id=1, source_target_pairs={{0,4},{4,0},{1,5},{5,1},{2,6},{6,2},{3,7},{7,3},{8,12},{12,8},{9,1... | collective-permute-start | bytes 3145736 | tf_op jit(solution)/shard_map/ppermute | solution.py:872
  13.3 123.6 %collective-permute-start.12 = (bf16[256,2048]{1,0:T(8,128)(2,1)}, bf16[256,2048]{1,0:T(8,128)(2,1)}, u32[]{:S(2)}, u32[]{:S(2)}) collective-permute-start(bf16[256,2048]{1,0:T(8,128)(2,1)} %bitcast.21.refs_0_), channel_id=1, source_target_pairs={{0,4},{4,0},{1,5},{5,1},{2,6},{6,2},{3,7},{7,3},{8,12},{12,8},{9,1... | collective-permute-start | bytes 3145736 | tf_op jit(solution)/shard_map/ppermute | solution.py:872
  15.4 10.5 %copy-start.22 = (f32[1536]{0:T(1024)S(1)}, f32[1536]{0:T(1024)}, u32[]{:S(2)}) copy-start(f32[1536]{0:T(1024)} %param.23) | copy-start | bytes 18436
  15.4 11.1 %copy-start.20 = (f32[2048]{0:T(1024)S(1)}, f32[2048]{0:T(1024)}, u32[]{:S(2)}) copy-start(f32[2048]{0:T(1024)} %param.25) | copy-start | bytes 24580
  15.4 11.1 %copy-start.21 = (f32[2048]{0:T(1024)S(1)}, f32[2048]{0:T(1024)}, u32[]{:S(2)}) copy-start(f32[2048]{0:T(1024)} %param.29) | copy-start | bytes 24580
  32.4 24.2 %collective-permute-start.3 = (bf16[256,2048]{1,0:T(8,128)(2,1)}, bf16[256,2048]{1,0:T(8,128)(2,1)}, u32[]{:S(2)}, u32[]{:S(2)}) collective-permute-start(bf16[256,2048]{1,0:T(8,128)(2,1)} %collective-permute-done.refs_1_), channel_id=1, source_target_pairs={{0,16},{16,0},{8,24},{24,8},{1,17},{17,1},{9,25},{25,9},{2,18},{18... | collective-permute-start | bytes 3145736 | tf_op jit(solution)/shard_map/ppermute | solution.py:866
  37.7 24.8 %collective-permute-start.4 = (bf16[512,2048]{1,0:T(8,128)(2,1)}, bf16[512,2048]{1,0:T(8,128)(2,1)S(1)}, u32[]{:S(2)}, u32[]{:S(2)}) collective-permute-start(bf16[512,2048]{1,0:T(8,128)(2,1)} %pack.3.w0.refs_0_.w10), channel_id=1, source_target_pairs={{0,8},{8,0},{16,24},{24,16},{1,9},{9,1},{17,25},{25,17},{2,10},{10... | collective-permute-start | bytes 6291464 | tf_op jit(solution)/shard_map/ppermute | solution.py:869
  37.7 23.3 %collective-permute-start.5 = (bf16[256,2048]{1,0:T(8,128)(2,1)S(1)}, bf16[256,2048]{1,0:T(8,128)(2,1)}, u32[]{:S(2)}, u32[]{:S(2)}) collective-permute-start(bf16[256,2048]{1,0:T(8,128)(2,1)S(1)} %collective-permute-done.2.w1.refs_0_.w11), channel_id=1, source_target_pairs={{0,8},{8,0},{16,24},{24,16},{1,9},{9,1},{17,25},{25,17},{2,10},{10... | collective-permute-start | bytes 3145736 | tf_op jit(solution)/shard_map/ppermute | solution.py:869
  56.6 5.9 %collective-permute-start.6 = (bf16[256,2048]{1,0:T(8,128)(2,1)}, bf16[256,2048]{1,0:T(8,128)(2,1)}, u32[]{:S(2)}, u32[]{:S(2)}) collective-permute-start(bf16[256,2048]{1,0:T(8,128)(2,1)} %collective-permute-done.3.w2.refs_1_.w12), channel_id=1, source_target_pairs={{0,8},{8,0},{16,24},{24,16},{1,9},{9,1},{17,25},{25,17},{2,10},{10... | collective-permute-start | bytes 3145736 | tf_op jit(solution)/shard_map/ppermute | solution.py:869
  60.5 57.1 %collective-permute-start.9 = (bf16[512,2048]{1,0:T(8,128)(2,1)}, bf16[512,2048]{1,0:T(8,128)(2,1)}, u32[]{:S(2)}, u32[]{:S(2)}) collective-permute-start(bf16[512,2048]{1,0:T(8,128)(2,1)} %pack.4.w0.w20), channel_id=1, source_target_pairs={{0,8},{8,0},{16,24},{24,16},{1,9},{9,1},{17,25},{25,17},{2,10},{10... | collective-permute-start | bytes 6291464 | tf_op jit(solution)/shard_map/ppermute | solution.py:869
  61.0 25.3 %collective-permute-start.7 = (bf16[256,2048]{1,0:T(8,128)(2,1)}, bf16[256,2048]{1,0:T(8,128)(2,1)S(1)}, u32[]{:S(2)}, u32[]{:S(2)}) collective-permute-start(bf16[256,2048]{1,0:T(8,128)(2,1)} %convert_element_type.174.refs_0_), channel_id=1, source_target_pairs={{0,16},{16,0},{8,24},{24,8},{1,17},{17,1},{9,25},{25,9},{2,18},{18... | collective-permute-start | bytes 3145736 | tf_op jit(solution)/shard_map/ppermute | solution.py:866
  73.6 71.4 %collective-permute-start.13 = (bf16[1024,1024]{1,0:T(8,128)(2,1)}, bf16[1024,1024]{1,0:T(8,128)(2,1)}, u32[]{:S(2)}, u32[]{:S(2)}) collective-permute-start(bf16[1024,1024]{1,0:T(8,128)(2,1)} %kv.1.kv_ref), channel_id=1, source_target_pairs={{0,4},{1,5},{2,6},{3,7},{8,12},{9,13},{10,14},{11,15},{16,20},{17,... | collective-permute-start | bytes 6291464 | tf_op jit(solution)/shard_map/ppermute | solution.py:929
  86.3 12.2 %copy-start.29 = (bf16[256,2048]{1,0:T(8,128)(2,1)}, bf16[256,2048]{1,0:T(8,128)(2,1)S(1)}, u32[]{:S(2)}) copy-start(bf16[256,2048]{1,0:T(8,128)(2,1)S(1)} %collective-permute-done.7.w1.w21) | copy-start | bytes 3145732
  86.3 24.6 %collective-permute-start.8 = (bf16[256,2048]{1,0:T(8,128)(2,1)}, bf16[256,2048]{1,0:T(8,128)(2,1)}, u32[]{:S(2)}, u32[]{:S(2)}) collective-permute-start(bf16[256,2048]{1,0:T(8,128)(2,1)} %collective-permute-done.1.refs_1_), channel_id=1, source_target_pairs={{0,16},{16,0},{8,24},{24,8},{1,17},{17,1},{9,25},{25,9},{2,18},{18... | collective-permute-start | bytes 3145736 | tf_op jit(solution)/shard_map/ppermute | solution.py:866
  87.8 31.3 %collective-permute-start.10 = (bf16[256,2048]{1,0:T(8,128)(2,1)S(1)}, bf16[256,2048]{1,0:T(8,128)(2,1)S(1)}, u32[]{:S(2)}, u32[]{:S(2)}) collective-permute-start(bf16[256,2048]{1,0:T(8,128)(2,1)S(1)} %collective-permute-done.7.w1.w21), channel_id=1, source_target_pairs={{0,8},{8,0},{16,24},{24,16},{1,9},{9,1},{17,25},{25,17},{2,10},{10... | collective-permute-start | bytes 3145736 | tf_op jit(solution)/shard_map/ppermute | solution.py:869
  110.9 8.2 %collective-permute-start.11 = (bf16[256,2048]{1,0:T(8,128)(2,1)}, bf16[256,2048]{1,0:T(8,128)(2,1)S(1)}, u32[]{:S(2)}, u32[]{:S(2)}) collective-permute-start(bf16[256,2048]{1,0:T(8,128)(2,1)} %collective-permute-done.8.w2.w22), channel_id=1, source_target_pairs={{0,8},{8,0},{16,24},{24,16},{1,9},{9,1},{17,25},{25,17},{2,10},{10... | collective-permute-start | bytes 3145736 | tf_op jit(solution)/shard_map/ppermute | solution.py:869
  117.6 25.9 %collective-permute-start.15 = (bf16[256,2048]{1,0:T(8,128)(2,1)}, bf16[256,2048]{1,0:T(8,128)(2,1)}, u32[]{:S(2)}, u32[]{:S(2)}) collective-permute-start(bf16[256,2048]{1,0:T(8,128)(2,1)} %bitcast.21.refs_0_), channel_id=1, source_target_pairs={{0,16},{16,0},{8,24},{24,8},{1,17},{17,1},{9,25},{25,9},{2,18},{18... | collective-permute-start | bytes 3145736 | tf_op jit(solution)/shard_map/ppermute | solution.py:866
  140.7 18.0 %collective-permute-start.14 = (bf16[512,2048]{1,0:T(8,128)(2,1)}, bf16[512,2048]{1,0:T(8,128)(2,1)S(1)}, u32[]{:S(2)}, u32[]{:S(2)}) collective-permute-start(bf16[512,2048]{1,0:T(8,128)(2,1)} %pack.5.refs_2_.w0), channel_id=1, source_target_pairs={{0,8},{8,0},{16,24},{24,16},{1,9},{9,1},{17,25},{25,17},{2,10},{10... | collective-permute-start | bytes 6291464 | tf_op jit(solution)/shard_map/ppermute | solution.py:869
  143.5 32.3 %collective-permute-start.16 = (bf16[256,2048]{1,0:T(8,128)(2,1)}, bf16[256,2048]{1,0:T(8,128)(2,1)S(1)}, u32[]{:S(2)}, u32[]{:S(2)}) collective-permute-start(bf16[256,2048]{1,0:T(8,128)(2,1)} %collective-permute-done.12.refs_1_), channel_id=1, source_target_pairs={{0,16},{16,0},{8,24},{24,8},{1,17},{17,1},{9,25},{25,9},{2,18},{18... | collective-permute-start | bytes 3145736 | tf_op jit(solution)/shard_map/ppermute | solution.py:866
  157.3 28.2 %collective-permute-start.17 = (bf16[256,2048]{1,0:T(8,128)(2,1)}, bf16[256,2048]{1,0:T(8,128)(2,1)}, u32[]{:S(2)}, u32[]{:S(2)}) collective-permute-start(bf16[256,2048]{1,0:T(8,128)(2,1)} %collective-permute-done.15.refs_4_.w1), channel_id=1, source_target_pairs={{0,8},{8,0},{16,24},{24,16},{1,9},{9,1},{17,25},{25,17},{2,10},{10... | collective-permute-start | bytes 3145736 | tf_op jit(solution)/shard_map/ppermute | solution.py:869
  157.4 79.2 %collective-permute-start.22 = (bf16[1024,1024]{1,0:T(8,128)(2,1)}, bf16[1024,1024]{1,0:T(8,128)(2,1)}, u32[]{:S(2)}, u32[]{:S(2)}) collective-permute-start(bf16[1024,1024]{1,0:T(8,128)(2,1)} %get-tuple-element.164), channel_id=1, source_target_pairs={{4,0},{5,1},{6,2},{7,3},{12,8},{13,9},{14,10},{15,11},{20,16},{21,... | collective-permute-start | bytes 6291464 | tf_op jit(solution)/shard_map/ppermute | solution.py:932
  170.9 44.7 %collective-permute-start.19 = (bf16[1024,512]{1,0:T(8,128)(2,1)}, bf16[1024,512]{1,0:T(8,128)(2,1)}, u32[]{:S(2)}, u32[]{:S(2)}) collective-permute-start(bf16[1024,512]{1,0:T(8,128)(2,1)} %get-tuple-element.155), channel_id=1, source_target_pairs={{0,1},{3,2},{4,5},{7,6},{8,9},{11,10},{12,13},{15,14},{16,17},{19,... | collective-permute-start | bytes 3145736 | tf_op jit(solution)/shard_map/ppermute | solution.py:837
  175.8 9.5 %copy-start.30 = (bf16[256,2048]{1,0:T(8,128)(2,1)}, bf16[256,2048]{1,0:T(8,128)(2,1)S(1)}, u32[]{:S(2)}) copy-start(bf16[256,2048]{1,0:T(8,128)(2,1)S(1)} %collective-permute-done.16.refs_5_.w2) | copy-start | bytes 3145732
  175.8 12.1 %collective-permute-start.18 = (bf16[256,2048]{1,0:T(8,128)(2,1)S(1)}, bf16[256,2048]{1,0:T(8,128)(2,1)S(1)}, u32[]{:S(2)}, u32[]{:S(2)}) collective-permute-start(bf16[256,2048]{1,0:T(8,128)(2,1)S(1)} %collective-permute-done.16.refs_5_.w2), channel_id=1, source_target_pairs={{0,8},{8,0},{16,24},{24,16},{1,9},{9,1},{17,25},{25,17},{2,10},{10... | collective-permute-start | bytes 3145736 | tf_op jit(solution)/shard_map/ppermute | solution.py:869
  185.2 36.8 %collective-permute-start.20 = (bf16[1024,2048]{1,0:T(8,128)(2,1)}, bf16[1024,2048]{1,0:T(8,128)(2,1)}, u32[]{:S(2)}, u32[]{:S(2)}) collective-permute-start(bf16[1024,2048]{1,0:T(8,128)(2,1)} %wgrad.6), channel_id=1, source_target_pairs={{0,8},{8,0},{16,24},{24,16},{1,9},{9,1},{17,25},{25,17},{2,10},{10... | collective-permute-start | bytes 12582920 | tf_op jit(solution)/shard_map/ppermute | solution.py:869
  185.6 46.6 %collective-permute-start.21 = (bf16[1024,512]{1,0:T(8,128)(2,1)}, bf16[1024,512]{1,0:T(8,128)(2,1)}, u32[]{:S(2)}, u32[]{:S(2)}) collective-permute-start(bf16[1024,512]{1,0:T(8,128)(2,1)} %get-tuple-element.161), channel_id=1, source_target_pairs={{0,1},{3,2},{4,5},{7,6},{8,9},{11,10},{12,13},{15,14},{16,17},{19,... | collective-permute-start | bytes 3145736 | tf_op jit(solution)/shard_map/ppermute | solution.py:837
  200.6 15.1 %copy-start.12 = (bf16[1024,512]{1,0:T(8,128)(2,1)S(1)}, bf16[1024,512]{1,0:T(8,128)(2,1)}, u32[]{:S(2)}) copy-start(bf16[1024,512]{1,0:T(8,128)(2,1)} %get-tuple-element.155) | copy-start | bytes 3145732
  218.2 24.4 %collective-permute-start.23 = (bf16[1024,512]{1,0:T(8,128)(2,1)}, bf16[1024,512]{1,0:T(8,128)(2,1)}, u32[]{:S(2)}, u32[]{:S(2)}) collective-permute-start(bf16[1024,512]{1,0:T(8,128)(2,1)} %add_convert_fusion.15), channel_id=1, source_target_pairs={{1,2},{2,1},{5,6},{6,5},{9,10},{10,9},{13,14},{14,13},{17,18},{18,... | collective-permute-start | bytes 3145736 | tf_op jit(solution)/shard_map/ppermute | solution.py:847
  219.8 27.0 %collective-permute-start.24 = (bf16[1024,512]{1,0:T(8,128)(2,1)}, bf16[1024,512]{1,0:T(8,128)(2,1)}, u32[]{:S(2)}, u32[]{:S(2)}) collective-permute-start(bf16[1024,512]{1,0:T(8,128)(2,1)} %get-tuple-element.168), channel_id=1, source_target_pairs={{0,1},{3,2},{4,5},{7,6},{8,9},{11,10},{12,13},{15,14},{16,17},{19,... | collective-permute-start | bytes 3145736 | tf_op jit(solution)/shard_map/ppermute | solution.py:837
  234.9 34.2 %collective-permute-start.25 = (bf16[1024,512]{1,0:T(8,128)(2,1)}, bf16[1024,512]{1,0:T(8,128)(2,1)}, u32[]{:S(2)}, u32[]{:S(2)}) collective-permute-start(bf16[1024,512]{1,0:T(8,128)(2,1)} %add_convert_fusion.14), channel_id=1, source_target_pairs={{1,2},{2,1},{5,6},{6,5},{9,10},{10,9},{13,14},{14,13},{17,18},{18,... | collective-permute-start | bytes 3145736 | tf_op jit(solution)/shard_map/ppermute | solution.py:847
  245.6 29.2 %collective-permute-start.26 = (bf16[1024,512]{1,0:T(8,128)(2,1)}, bf16[1024,512]{1,0:T(8,128)(2,1)}, u32[]{:S(2)}, u32[]{:S(2)}) collective-permute-start(bf16[1024,512]{1,0:T(8,128)(2,1)} %fusion.refs_0_), channel_id=1, source_target_pairs={{0,1},{3,2},{1,0},{2,3},{4,5},{7,6},{5,4},{6,7},{8,9},{11,10},{9,8... | collective-permute-start | bytes 3145736 | tf_op jit(solution)/shard_map/ppermute | solution.py:837
  249.6 29.4 %collective-permute-start.27 = (bf16[1024,512]{1,0:T(8,128)(2,1)}, bf16[1024,512]{1,0:T(8,128)(2,1)}, u32[]{:S(2)}, u32[]{:S(2)}) collective-permute-start(bf16[1024,512]{1,0:T(8,128)(2,1)} %add_convert_fusion.12), channel_id=1, source_target_pairs={{1,2},{2,1},{5,6},{6,5},{9,10},{10,9},{13,14},{14,13},{17,18},{18,... | collective-permute-start | bytes 3145736 | tf_op jit(solution)/shard_map/ppermute | solution.py:847
  251.3 40.0 %collective-permute-start.28 = (bf16[512,2048]{1,0:T(8,128)(2,1)}, bf16[512,2048]{1,0:T(8,128)(2,1)}, u32[]{:S(2)}, u32[]{:S(2)}) collective-permute-start(bf16[512,2048]{1,0:T(8,128)(2,1)} %get-tuple-element.176), channel_id=1, source_target_pairs={{0,16},{4,20},{8,12},{12,8},{16,0},{20,4},{24,28},{28,24},{1,17},{... | collective-permute-start | bytes 6291464 | tf_op jit(solution)/shard_map/ppermute | solution.py:912
  252.4 16.1 %copy-start.23 = (f32[1,1536]{1,0:T(1,128)S(1)}, f32[1,1536]{1,0:T(1,128)}, u32[]{:S(2)}) copy-start(f32[1,1536]{1,0:T(1,128)} %get-tuple-element.200) | copy-start | bytes 18436
  272.5 49.6 %collective-permute-start.29 = (bf16[1024,512]{1,0:T(8,128)(2,1)}, bf16[1024,512]{1,0:T(8,128)(2,1)}, u32[]{:S(2)}, u32[]{:S(2)}) collective-permute-start(bf16[1024,512]{1,0:T(8,128)(2,1)} %fusion.1.refs_4_), channel_id=1, source_target_pairs={{0,1},{3,2},{1,0},{2,3},{4,5},{7,6},{5,4},{6,7},{8,9},{11,10},{9,8... | collective-permute-start | bytes 3145736 | tf_op jit(solution)/shard_map/ppermute | solution.py:837
  277.2 49.1 %collective-permute-start.31 = (bf16[1024,512]{1,0:T(8,128)(2,1)}, bf16[1024,512]{1,0:T(8,128)(2,1)}, u32[]{:S(2)}, u32[]{:S(2)}) collective-permute-start(bf16[1024,512]{1,0:T(8,128)(2,1)} %add_convert_fusion.10), channel_id=1, source_target_pairs={{1,2},{2,1},{5,6},{6,5},{9,10},{10,9},{13,14},{14,13},{17,18},{18,... | collective-permute-start | bytes 3145736 | tf_op jit(solution)/shard_map/ppermute | solution.py:847
  282.0 69.2 %collective-permute-start.32 = (bf16[1024,512]{1,0:T(8,128)(2,1)}, bf16[1024,512]{1,0:T(8,128)(2,1)}, u32[]{:S(2)}, u32[]{:S(2)}) collective-permute-start(bf16[1024,512]{1,0:T(8,128)(2,1)} %fusion.2.refs_2_), channel_id=1, source_target_pairs={{0,1},{3,2},{1,0},{2,3},{4,5},{7,6},{5,4},{6,7},{8,9},{11,10},{9,8... | collective-permute-start | bytes 3145736 | tf_op jit(solution)/shard_map/ppermute | solution.py:837
  295.7 36.1 %collective-permute-start.30 = (bf16[256,2048]{1,0:T(8,128)(2,1)}, bf16[256,2048]{1,0:T(8,128)(2,1)}, u32[]{:S(2)}, u32[]{:S(2)}) collective-permute-start(bf16[256,2048]{1,0:T(8,128)(2,1)} %get-tuple-element.182), channel_id=1, source_target_pairs={{0,4},{4,0},{8,24},{12,28},{16,20},{20,16},{24,8},{28,12},{1,5},{5... | collective-permute-start | bytes 3145736 | tf_op jit(solution)/shard_map/ppermute | solution.py:912
  305.8 16.3 %copy-start.8 = (bf16[1024,512]{1,0:T(8,128)(2,1)S(1)}, bf16[1024,512]{1,0:T(8,128)(2,1)}, u32[]{:S(2)}) copy-start(bf16[1024,512]{1,0:T(8,128)(2,1)} %get-tuple-element.181) | copy-start | bytes 3145732
  324.7 30.1 %collective-permute-start.33 = (bf16[1024,512]{1,0:T(8,128)(2,1)}, bf16[1024,512]{1,0:T(8,128)(2,1)}, u32[]{:S(2)}, u32[]{:S(2)}) collective-permute-start(bf16[1024,512]{1,0:T(8,128)(2,1)} %add_convert_fusion.8), channel_id=1, source_target_pairs={{1,2},{2,1},{5,6},{6,5},{9,10},{10,9},{13,14},{14,13},{17,18},{18,... | collective-permute-start | bytes 3145736 | tf_op jit(solution)/shard_map/ppermute | solution.py:847
  329.3 45.2 %collective-permute-start.35 = (bf16[1024,512]{1,0:T(8,128)(2,1)}, bf16[1024,512]{1,0:T(8,128)(2,1)}, u32[]{:S(2)}, u32[]{:S(2)}) collective-permute-start(bf16[1024,512]{1,0:T(8,128)(2,1)} %fusion.3.refs_6_), channel_id=1, source_target_pairs={{0,1},{3,2},{1,0},{2,3},{4,5},{7,6},{5,4},{6,7},{8,9},{11,10},{9,8... | collective-permute-start | bytes 3145736 | tf_op jit(solution)/shard_map/ppermute | solution.py:837
  341.0 10.3 %copy-start.5 = (bf16[1024,512]{1,0:T(8,128)(2,1)S(1)}, bf16[1024,512]{1,0:T(8,128)(2,1)}, u32[]{:S(2)}) copy-start(bf16[1024,512]{1,0:T(8,128)(2,1)} %get-tuple-element.187) | copy-start | bytes 3145732
  341.0 18.8 %collective-permute-start.34 = (bf16[1024,2048]{1,0:T(8,128)(2,1)}, bf16[1024,2048]{1,0:T(8,128)(2,1)}, u32[]{:S(2)}, u32[]{:S(2)}) collective-permute-start(bf16[1024,2048]{1,0:T(8,128)(2,1)} %wgrad.8), channel_id=1, source_target_pairs={{0,8},{8,0},{16,24},{24,16},{1,9},{9,1},{17,25},{25,17},{2,10},{10... | collective-permute-start | bytes 12582920 | tf_op jit(solution)/shard_map/ppermute | solution.py:869
  352.9 24.1 %collective-permute-start.36 = (bf16[1024,512]{1,0:T(8,128)(2,1)S(1)}, bf16[1024,512]{1,0:T(8,128)(2,1)}, u32[]{:S(2)}, u32[]{:S(2)}) collective-permute-start(bf16[1024,512]{1,0:T(8,128)(2,1)S(1)} %add_convert_fusion.6), channel_id=1, source_target_pairs={{1,2},{2,1},{5,6},{6,5},{9,10},{10,9},{13,14},{14,13},{17,18},{18,... | collective-permute-start | bytes 3145736 | tf_op jit(solution)/shard_map/ppermute | solution.py:847
  357.7 50.4 %collective-permute-start.40 = (bf16[1024,512]{1,0:T(8,128)(2,1)}, bf16[1024,512]{1,0:T(8,128)(2,1)}, u32[]{:S(2)}, u32[]{:S(2)}) collective-permute-start(bf16[1024,512]{1,0:T(8,128)(2,1)} %fusion.4.refs_0_), channel_id=1, source_target_pairs={{0,1},{3,2},{1,0},{2,3},{4,5},{7,6},{5,4},{6,7},{8,9},{11,10},{9,8... | collective-permute-start | bytes 3145736 | tf_op jit(solution)/shard_map/ppermute | solution.py:837
  369.7 26.4 %collective-permute-start.37 = (bf16[512,2048]{1,0:T(8,128)(2,1)}, bf16[512,2048]{1,0:T(8,128)(2,1)}, u32[]{:S(2)}, u32[]{:S(2)}) collective-permute-start(bf16[512,2048]{1,0:T(8,128)(2,1)} %get-tuple-element.196), channel_id=1, source_target_pairs={{0,16},{4,20},{8,12},{12,8},{16,0},{20,4},{24,28},{28,24},{1,17},{... | collective-permute-start | bytes 6291464 | tf_op jit(solution)/shard_map/ppermute | solution.py:912
  376.1 36.2 %collective-permute-start.41 = (bf16[1024,512]{1,0:T(8,128)(2,1)S(1)}, bf16[1024,512]{1,0:T(8,128)(2,1)S(1)}, u32[]{:S(2)}, u32[]{:S(2)}) collective-permute-start(bf16[1024,512]{1,0:T(8,128)(2,1)S(1)} %add_convert_fusion.4), channel_id=1, source_target_pairs={{1,2},{2,1},{5,6},{6,5},{9,10},{10,9},{13,14},{14,13},{17,18},{18,... | collective-permute-start | bytes 3145736 | tf_op jit(solution)/shard_map/ppermute | solution.py:847
  379.5 21.1 %collective-permute-start.38 = (f32[13824]{0:T(1024)S(1)}, f32[13824]{0:T(1024)S(1)}, u32[]{:S(2)}, u32[]{:S(2)}) collective-permute-start(f32[13824]{0:T(1024)S(1)} %copy-done.14), channel_id=1, source_target_pairs={{0,8},{8,0},{16,24},{24,16},{1,9},{9,1},{17,25},{25,17},{2,10},{10... | collective-permute-start | bytes 165896 | tf_op jit(solution)/shard_map/ppermute | solution.py:869
  379.5 41.4 %collective-permute-start.43 = (bf16[1024,2048]{1,0:T(8,128)(2,1)}, bf16[1024,2048]{1,0:T(8,128)(2,1)}, u32[]{:S(2)}, u32[]{:S(2)}) collective-permute-start(bf16[1024,2048]{1,0:T(8,128)(2,1)} %wgrad.9), channel_id=1, source_target_pairs={{0,8},{8,0},{16,24},{24,16},{1,9},{9,1},{17,25},{25,17},{2,10},{10... | collective-permute-start | bytes 12582920 | tf_op jit(solution)/shard_map/ppermute | solution.py:869
  400.5 5.6 %collective-permute-start.39 = (f32[13824]{0:T(1024)S(1)}, f32[13824]{0:T(1024)S(1)}, u32[]{:S(2)}, u32[]{:S(2)}) collective-permute-start(f32[13824]{0:T(1024)S(1)} %add.115), channel_id=1, source_target_pairs={{0,16},{16,0},{8,24},{24,8},{1,17},{17,1},{9,25},{25,9},{2,18},{18... | collective-permute-start | bytes 165896 | tf_op jit(solution)/shard_map/ppermute | solution.py:866
  401.2 15.1 %collective-permute-start.42 = (bf16[256,2048]{1,0:T(8,128)(2,1)}, bf16[256,2048]{1,0:T(8,128)(2,1)}, u32[]{:S(2)}, u32[]{:S(2)}) collective-permute-start(bf16[256,2048]{1,0:T(8,128)(2,1)} %get-tuple-element.209), channel_id=1, source_target_pairs={{0,4},{4,0},{8,24},{12,28},{16,20},{20,16},{24,8},{28,12},{1,5},{5... | collective-permute-start | bytes 3145736 | tf_op jit(solution)/shard_map/ppermute | solution.py:912
  406.2 37.3 %collective-permute-start.45 = (bf16[1024,512]{1,0:T(8,128)(2,1)}, bf16[1024,512]{1,0:T(8,128)(2,1)}, u32[]{:S(2)}, u32[]{:S(2)}) collective-permute-start(bf16[1024,512]{1,0:T(8,128)(2,1)} %add_convert_fusion.3.refs_2_), channel_id=1, source_target_pairs={{1,0},{2,3},{5,4},{6,7},{9,8},{10,11},{13,12},{14,15},{17,16},{18,... | collective-permute-start | bytes 3145736 | tf_op jit(solution)/shard_map/ppermute | solution.py:837
  410.6 28.8 %collective-permute-start.47 = (bf16[1024,512]{1,0:T(8,128)(2,1)}, bf16[1024,512]{1,0:T(8,128)(2,1)}, u32[]{:S(2)}, u32[]{:S(2)}) collective-permute-start(bf16[1024,512]{1,0:T(8,128)(2,1)} %add_convert_fusion.2), channel_id=1, source_target_pairs={{1,2},{2,1},{5,6},{6,5},{9,10},{10,9},{13,14},{14,13},{17,18},{18,... | collective-permute-start | bytes 3145736 | tf_op jit(solution)/shard_map/ppermute | solution.py:847
  413.6 55.4 %collective-permute-start.48 = (bf16[1024,512]{1,0:T(8,128)(2,1)}, bf16[1024,512]{1,0:T(8,128)(2,1)}, u32[]{:S(2)}, u32[]{:S(2)}) collective-permute-start(bf16[1024,512]{1,0:T(8,128)(2,1)} %add_convert_fusion.1.refs_4_), channel_id=1, source_target_pairs={{1,0},{2,3},{5,4},{6,7},{9,8},{10,11},{13,12},{14,15},{17,16},{18,... | collective-permute-start | bytes 3145736 | tf_op jit(solution)/shard_map/ppermute | solution.py:837
  420.3 17.7 %collective-permute-start.46 = (f32[13824]{0:T(1024)}, f32[13824]{0:T(1024)}, u32[]{:S(2)}, u32[]{:S(2)}) collective-permute-start(f32[13824]{0:T(1024)} %add.117), channel_id=1, source_target_pairs={{0,4},{4,0},{1,5},{5,1},{2,6},{6,2},{3,7},{7,3},{8,12},{12,8},{9,1... | collective-permute-start | bytes 165896 | tf_op jit(solution)/shard_map/ppermute | solution.py:872
  431.7 26.2 %collective-permute-start.44 = (bf16[512,2048]{1,0:T(8,128)(2,1)}, bf16[512,2048]{1,0:T(8,128)(2,1)S(1)}, u32[]{:S(2)}, u32[]{:S(2)}) collective-permute-start(bf16[512,2048]{1,0:T(8,128)(2,1)} %get-tuple-element.214), channel_id=1, source_target_pairs={{0,16},{4,20},{8,12},{12,8},{16,0},{20,4},{24,28},{28,24},{1,17},{... | collective-permute-start | bytes 6291464 | tf_op jit(solution)/shard_map/ppermute | solution.py:912
  441.3 22.5 %copy-start.13 = (bf16[1024,512]{1,0:T(8,128)(2,1)}, bf16[1024,512]{1,0:T(8,128)(2,1)S(1)}, u32[]{:S(2)}) copy-start(bf16[1024,512]{1,0:T(8,128)(2,1)S(1)} %add_convert_fusion.refs_6_) | copy-start | bytes 3145732
  441.3 37.3 %collective-permute-start.49 = (bf16[1024,512]{1,0:T(8,128)(2,1)S(1)}, bf16[1024,512]{1,0:T(8,128)(2,1)}, u32[]{:S(2)}, u32[]{:S(2)}) collective-permute-start(bf16[1024,512]{1,0:T(8,128)(2,1)S(1)} %add_convert_fusion.refs_6_), channel_id=1, source_target_pairs={{1,0},{2,3},{5,4},{6,7},{9,8},{10,11},{13,12},{14,15},{17,16},{18,... | collective-permute-start | bytes 3145736 | tf_op jit(solution)/shard_map/ppermute | solution.py:837
  463.7 25.9 %collective-permute-start.50 = (f32[8192]{0:T(1024)S(1)}, f32[8192]{0:T(1024)S(1)}, u32[]{:S(2)}, u32[]{:S(2)}) collective-permute-start(f32[8192]{0:T(1024)S(1)} %slice.40), channel_id=1, source_target_pairs={{0,1},{1,0},{2,3},{3,2},{4,5},{5,4},{6,7},{7,6},{8,9},{9,8},{10,11... | collective-permute-start | bytes 98312 | tf_op jit(solution)/shard_map/ppermute | solution.py:945
  469.0 20.8 %collective-permute-start.51 = (bf16[256,2048]{1,0:T(8,128)(2,1)}, bf16[256,2048]{1,0:T(8,128)(2,1)S(1)}, u32[]{:S(2)}, u32[]{:S(2)}) collective-permute-start(bf16[256,2048]{1,0:T(8,128)(2,1)} %get-tuple-element.226), channel_id=1, source_target_pairs={{0,4},{4,0},{8,24},{12,28},{16,20},{20,16},{24,8},{28,12},{1,5},{5... | collective-permute-start | bytes 3145736 | tf_op jit(solution)/shard_map/ppermute | solution.py:912
  489.7 5.4 %collective-permute-start.52 = (f32[8192]{0:T(1024)S(1)}, f32[8192]{0:T(1024)S(1)}, u32[]{:S(2)}, u32[]{:S(2)}) collective-permute-start(f32[8192]{0:T(1024)S(1)} %add.122), channel_id=1, source_target_pairs={{0,2},{2,0},{1,3},{3,1},{4,6},{6,4},{5,7},{7,5},{8,10},{10,8},{9,1... | collective-permute-start | bytes 98312 | tf_op jit(solution)/shard_map/ppermute | solution.py:947
  (22 other events, 84.2 us)

commit v7 on v6

--- a/solution.py
+++ b/solution.py
@@ -19,7 +19,7 @@
 inv_sqrt_tau = 0.3989422804014327
 
 
-COST_SCALE = 20
+COST_SCALE = 100
 
 
 def cost(flops, nbytes, trans=0, k=COST_SCALE):
@@ -1096,20 +1096,24 @@
     dn2, dn3, gain_sums = run(back_call, meta, dqkv, du, g1, g2, x2, stats, ga, gf, gain_sums, 1)
     pipe.cross()
     pipe.send(dn2)
+    small = jnp.concatenate([gain_sums.reshape(-1), g_sum.reshape(-1), bqkv_sum.reshape(-1), bin_sum.reshape(-1)])
+    add = comm.small_sum(run, small, 0)
     cross2 = comm.scatter_cross(run(wgrad_call, after(meta, jax.tree.leaves(state3)[-1]), h2, du, half=1))
+    small = add()
+    add = comm.small_sum(run, small, 1)
     theirs1 = run(wgrad_call, meta, h1, dqkv, g, ob, half=1)
+    small = add()
     pipe.cross()
     pipe.send(dn3)
     state2 = comm.scatter_own(run, meta, (h2, du), cross2)
+    cross1 = comm.scatter_cross(after(theirs1, *jax.tree.leaves(state2)[:1]))
     (grad_out,) = comm.scatter_last(run, ((ff, True),), state3)
-    small = jnp.concatenate([gain_sums.reshape(-1), g_sum.reshape(-1), bqkv_sum.reshape(-1), bin_sum.reshape(-1)])
-    add = comm.small_sum(run, after(small, grad_out), 0)
     pipe.cross()
     pipe.send()
-    cross1 = comm.scatter_cross(after(theirs1, pipe.here[-1]))
+    state1 = comm.scatter_own(run, meta, (h1, dqkv, g, ob), cross1)
+    pipe.cross()
+    pipe.send()
     state2 = comm.scatter_half(run, state2)
-    small = add()
-    add = comm.small_sum(run, small, 1)
 
     def sums_of(order):
         return [v for c in order for v in (pipe.here[c], pipe.sent[c])]
@@ -1119,18 +1123,14 @@
         rows_call, body=functools.partial(block_out_kernel, local_len), name="bout", specs=("row", "vec") + ("part",) * 8
     )
     block_output = run(out_half, *out_ops, steps=(0, 2))
-    small = add()
-    pipe.cross()
+    (grad_in,) = comm.scatter_last(run, ((ff, False),), state2)
+    block_output = run(out_half, *out_ops, steps=(2, 4), into=block_output).reshape(slots, local_len, d)
     pipe.send()
-    (grad_in,) = comm.scatter_last(run, ((ff, False),), state2)
-    add = comm.small_sum(run, after(small, grad_in), 2)
-    state1 = comm.scatter_own(run, meta, (h1, dqkv, g, ob), cross1)
-    block_output = run(out_half, *out_ops, steps=(2, 4), into=block_output).reshape(slots, local_len, d)
+    add = comm.small_sum(run, after(small, pipe.sent[5], pipe.here[-1], *jax.tree.leaves(state1)[-1:]), 2)
+    state1 = comm.scatter_half(run, state1)
     small = add()
     gains = small[: 4 * d]
     group = small[4 * d :]
-    pipe.send()
-    state1 = comm.scatter_half(run, after(state1, pipe.sent[5]))
     add = comm.small_sum(run, after(gains, *jax.tree.leaves(state1)[:1]), 3)
     input_grad = run(
         rows_call, meta, x2, og2, stats, *sums_of(range(4, 8)),

time: 504 us -> 505 us (level)
  other arithmetic: 48.7 us -> 57.9 us
  waiting for transfers between devices: 87.2 us -> 81.3 us
    ppermute x6, waiting for transfers between devices: 32 us -> 22.8 us  [turn(): return lax.ppermute(v, ('dp', 'ctx'), pairs)]
    unnamed x70 -> x52, local copies, waits for them, and re-layouts: 11.7 us -> 6.32 us
  transfers between devices with their start and end apart: 53 -> 53, of which waited for: 10 -> 11; matrix products, arithmetic and copies ran while one was open for 10% -> 12% of each run, Pallas kernels for 52% -> 52%
where the time goes in v7:
time: 505 us; the launch traced here: 497 us
  Pallas kernels  261 us (52%)
  starting transfers between devices  84 us (17%)
  waiting for transfers between devices  81.3 us (16%)
  other arithmetic  57.9 us (11%)
  local copies, waits for them, and re-layouts  12 us (2%)
    pallas_call x6, Pallas kernels, wgrad_call(): pl.pallas_call(functools.partial(wgrad_kernel, counts, add is not None, s...  59.7 us
    ppermute x7, waiting for transfers between devices, x(): return lax.ppermute(v, 'dp', [(0, 2), (2, 0), (1, 3), (3, 1)])  44.1 us
    pallas_call x2, Pallas kernels, back_call(): pl.pallas_call(back_kernel, name='backn', grid_spec=pltpu.PrefetchScalarG...  32.5 us
    ppermute x11, starting transfers between devices, send(): got = lax.ppermute(v, 'tensor', pairs)  29.8 us
    convert_element_type x11, other arithmetic, add_bf(): return lax.optimization_barrier((a.astype(F32) + b.astype(F32)).astype(BF))  29.1 us
    ppermute x6, waiting for transfers between devices, turn(): return lax.ppermute(v, ('dp', 'ctx'), pairs)  22.8 us
    pallas_call x2, Pallas kernels, out_call(): pl.pallas_call(functools.partial(out_kernel, count), name='outp', grid=(4...  22.5 us
    pallas_call x3, Pallas kernels, rows_call(): pl.pallas_call(functools.partial(body, first), name=name, grid_spec=pltpu...  20.7 us
  transfers between devices with their start and end apart: 53, of which 11 were waited for; matrix products, arithmetic and copies ran while one was open for 12% of the time, Pallas kernels for 52%

profile of v7, /device:TPU:0, one launch (start us, length us, event | category | flops | bytes accessed | tf_op | source)
XLA Modules:
  0.0 497.0 jit_solution(17931663635814301837)
XLA Ops:
  4.6 3.0 collective-permute-start
  10.7 2.5 copy.32
  15.4 10.5 %norm.1 = (bf16[1024,2048]{1,0:T(8,128)(2,1)}, bf16[1024,2048]{1,0:T(8,128)(2,1)}, f32[1024,128]{1,0:T(8,128)}, f32[1,2048]{1,0:T(1,128)}) custom-call(s32[13]{0:T(128)} %concatenate.10.meta, bf16[1024,2048]{1,0:T(8,128)(2,1)} %bitcast.30, bf16[1024,2048]{1,0:T(8,128)(2,1)} %bitcast.37, f32[1,2048]{1,0:T(1,128)} %bitcast.42, f32[1,2048]{1,0:T(1,128)} %bitcast.39), custom_call_target="tpu_custom_call" | custom-call | flops 629145600000 | bytes 2097152000 | tf_op jit(solution)/shard_map/norm/pallas_call | solution.py:127
  29.0 2.9 collective-permute-done.refs_1_
  34.0 3.8 pack.3.w0.refs_0_.w10
  38.3 18.3 %collective-permute-done.3.w2.refs_1_.w12 = bf16[256,2048]{1,0:T(8,128)(2,1)} collective-permute-done((bf16[256,2048]{1,0:T(8,128)(2,1)}, bf16[256,2048]{1,0:T(8,128)(2,1)}, u32[]{:S(2)}, u32[]{:S(2)}) %collective-permute-start.3) | collective-permute-done | bytes 1048608 | tf_op jit(solution)/shard_map/ppermute | solution.py:866
  56.6 3.8 pack.4.w0.w20
  63.8 9.8 %kv.1.kv_ref = bf16[1024,1024]{1,0:T(8,128)(2,1)} custom-call(bf16[1024,2048]{1,0:T(8,128)(2,1)} %get-tuple-element.125.h1.refs_0_, bf16[512,2048]{1,0:T(8,128)(2,1)} %pack.3.w0.refs_0_.w10, bf16[256,2048]{1,0:T(8,128)(2,1)} %collective-permute-done.2.w1.refs_0_.w11, bf16[256,2048]{1,0:T(8,128)(2,1)} %collective-permute-done.3.w2.refs_1_.w12, ...), custom_call_target="tpu_custom_call" | custom-call | flops 429496729600 | bytes 1048576000 | tf_op jit(solution)/shard_map/kv/pallas_call | solution.py:183
  73.5 3.9 collective-permute-start.13
  77.5 8.9 %collective-permute-done.7.w1.w21 = bf16[256,2048]{1,0:T(8,128)(2,1)} collective-permute-done((bf16[256,2048]{1,0:T(8,128)(2,1)}, bf16[256,2048]{1,0:T(8,128)(2,1)}, u32[]{:S(2)}, u32[]{:S(2)}) %collective-permute-start.7) | collective-permute-done | bytes 1048608 | tf_op jit(solution)/shard_map/ppermute | solution.py:866
  87.9 10.8 %qd.1 = (bf16[1024,512]{1,0:T(8,128)(2,1)}, bf16[1024,512]{1,0:T(8,128)(2,1)}) custom-call(bf16[1024,2048]{1,0:T(8,128)(2,1)} %get-tuple-element.125.h1.refs_0_, bf16[1024,2048]{1,0:T(8,128)(2,1)} %get-tuple-element.149.g.refs_0_.refs_2_, bf16[512,2048]{1,0:T(8,128)(2,1)} %pack.3.w0.refs_0_.w10, bf16[256,2048]{1,0:T(8,128)(2,1)} %collective-permute-done.2.w1.refs_0_.w11, ...), custom_call_target="tpu_custom_call" | custom-call | flops 440401920000 | bytes 1468006400 | tf_op jit(solution)/shard_map/qd/pallas_call | solution.py:224
  98.7 12.4 %collective-permute-done.8.w2.w22 = bf16[256,2048]{1,0:T(8,128)(2,1)} collective-permute-done((bf16[256,2048]{1,0:T(8,128)(2,1)}, bf16[256,2048]{1,0:T(8,128)(2,1)}, u32[]{:S(2)}, u32[]{:S(2)}) %collective-permute-start.8) | collective-permute-done | bytes 1048608 | tf_op jit(solution)/shard_map/ppermute | solution.py:866
  111.0 6.7 %norm2.1.h2.refs_0_ = bf16[1024,2048]{1,0:T(8,128)(2,1)} custom-call(s32[13]{0:T(128)} %concatenate.10.meta, bf16[1024,2048]{1,0:T(8,128)(2,1)} %bitcast.31, f32[1024,128]{1,0:T(8,128)} %get-tuple-element.129.st_ref, f32[1,2048]{1,0:T(1,128)} %bitcast.45, f32[1,2048]{1,0:T(1,128)} %bitcast.40), custom_call_target="tpu_custom_call" | custom-call | flops 251658240000 | bytes 838860800 | tf_op jit(solution)/shard_map/norm2/pallas_call | solution.py:107
  119.2 16.5 %hidden.1 = (bf16[1024,2048]{1,0:T(8,128)(2,1)}, bf16[1024,2048]{1,0:T(8,128)(2,1)}) custom-call(bf16[1024,2048]{1,0:T(8,128)(2,1)} %norm2.1.h2.refs_0_, bf16[512,2048]{1,0:T(8,128)(2,1)} %pack.4.w0.w20, bf16[256,2048]{1,0:T(8,128)(2,1)} %collective-permute-done.7.w1.w21, bf16[256,2048]{1,0:T(8,128)(2,1)} %collective-permute-done.8.w2.w22, ...), custom_call_target="tpu_custom_call" | custom-call | flops 858993459200 | bytes 2097152000 | tf_op jit(solution)/shard_map/hidden/pallas_call | solution.py:413
  135.7 3.8 pack.5.refs_2_.w0
  139.8 3.8 collective-permute-done.15.refs_4_.w1
  145.1 12.5 %attn.1 = (bf16[1024,512]{1,0:T(8,128)(2,1)}, bf16[1024,512]{1,0:T(8,128)(2,1)}, f32[1024,1024]{1,0:T(8,128)}, bf16[1024,1024]{1,0:T(8,128)(2,1)}) custom-call(s32[13]{0:T(128)} %concatenate.10.meta, bf16[1024,512]{1,0:T(8,128)(2,1)} %get-tuple-element.127.q_ref, bf16[1024,1024]{1,0:T(8,128)(2,1)} %kv.1.kv_ref, ...), custom_call_target="tpu_custom_call" | custom-call | flops 644245094400 | bytes 1048576000 | tf_op jit(solution)/shard_map/attn/pallas_call | solution.py:333
  159.0 10.9 %outp.2 = (bf16[1024,512]{1,0:T(8,128)(2,1)}, bf16[1024,512]{1,0:T(8,128)(2,1)}) custom-call(bf16[1024,512]{1,0:T(8,128)(2,1)} %get-tuple-element.143.ob.refs_3_, bf16[1024,2048]{1,0:T(8,128)(2,1)} %get-tuple-element.135.gb.refs_1_, bf16[512,2048]{1,0:T(8,128)(2,1)} %pack.3.w0.refs_0_.w10, bf16[512,2048]{1,0:T(8,128)(2,1)} %copy-done.10, ...), custom_call_target="tpu_custom_call" | custom-call | flops 53687092 | bytes 125829 | tf_op jit(solution)/shard_map/outp/pallas_call | solution.py:479
  169.9 4.8 collective-permute-start.19
  175.0 9.2 %wgrad.6 = bf16[1024,2048]{1,0:T(8,128)(2,1)} custom-call(s32[13]{0:T(128)} %concatenate.10.meta, bf16[1024,2048]{1,0:T(8,128)(2,1)} %get-tuple-element.149.g.refs_0_.refs_2_, bf16[1024,2048]{1,0:T(8,128)(2,1)} %get-tuple-element.135.gb.refs_1_), custom_call_target="tpu_custom_call" | custom-call | flops 440401920000 | bytes 1468006400 | tf_op jit(solution)/shard_map/wgrad/pallas_call | solution.py:602
  184.5 2.3 collective-permute-start.21
  186.8 11.6 %outp.3 = (bf16[1024,512]{1,0:T(8,128)(2,1)}, bf16[1024,512]{1,0:T(8,128)(2,1)}) custom-call(bf16[1024,512]{1,0:T(8,128)(2,1)} %get-tuple-element.143.ob.refs_3_, bf16[1024,2048]{1,0:T(8,128)(2,1)} %get-tuple-element.135.gb.refs_1_, bf16[256,2048]{1,0:T(8,128)(2,1)} %collective-permute-done.2.w1.refs_0_.w11, ...), custom_call_target="tpu_custom_call" | custom-call | flops 536870912000 | bytes 1258291200 | tf_op jit(solution)/shard_map/outp/pallas_call | solution.py:479
  198.5 15.2 %dhid.1 = (bf16[1024,2048]{1,0:T(8,128)(2,1)}, f32[1,2048]{1,0:T(1,128)}) custom-call(bf16[1024,2048]{1,0:T(8,128)(2,1)} %get-tuple-element.149.g.refs_0_.refs_2_, bf16[512,2048]{1,0:T(8,128)(2,1)} %pack.5.refs_2_.w0, bf16[256,2048]{1,0:T(8,128)(2,1)} %collective-permute-done.15.refs_4_.w1, bf16[256,2048]{1,0:T(8,128)(2,1)} %collective-permute-done.16.refs_5_.w2, ...), custom_call_target="tpu_custom_call" | custom-call | flops 858993459200 | bytes 2097152000 | tf_op jit(solution)/shard_map/dhid/pallas_call | solution.py:438
  213.6 2.5 add_convert_fusion.15
  217.8 2.3 collective-permute-start.24
  220.0 10.0 %wgrad.7 = (bf16[512,2048]{1,0:T(8,128)(2,1)}, bf16[512,2048]{1,0:T(8,128)(2,1)}) custom-call(s32[13]{0:T(128)} %concatenate.10.meta, bf16[1024,2048]{1,0:T(8,128)(2,1)} %get-tuple-element.149.g.refs_0_.refs_2_, bf16[1024,2048]{1,0:T(8,128)(2,1)} %get-tuple-element.135.gb.refs_1_, bf16[1024,2048]{1,0:T(8,128)(2,1)} %collective-permute-done.20.refs_2_), custom_call_target="tpu_custom_call" | custom-call | flops 440401920000 | bytes 1468006400 | tf_op jit(solution)/shard_map/wgrad/pallas_call | solution.py:602
  230.1 2.8 add_convert_fusion.14
  234.6 6.0 %join.1 = (bf16[1024,1536]{1,0:T(8,128)(2,1)}, f32[1,1536]{1,0:T(1,128)}) custom-call(bf16[1024,512]{1,0:T(8,128)(2,1)} %get-tuple-element.159.dq_ref, f32[1024,1024]{1,0:T(8,128)} %get-tuple-element.160.dkv_ref, bf16[1024,1024]{1,0:T(8,128)(2,1)} %collective-permute-done.22.rv_ref, f32[512,128]{1,0:T(8,128)} %get-tuple-element.232.cosf, ...), custom_call_target="tpu_custom_call" | custom-call | flops 377487360000 | bytes 1258291200 | tf_op jit(solution)/shard_map/join/pallas_call | solution.py:388
  240.6 3.0 fusion.refs_0_
  244.8 2.8 add_convert_fusion.12
  250.4 16.2 %backn.2 = (bf16[1024,512]{1,0:T(8,128)(2,1)}, bf16[1024,512]{1,0:T(8,128)(2,1)}, f32[4,2048]{1,0:T(4,128)}) custom-call(s32[13]{0:T(128)} %concatenate.10.meta, bf16[1024,1536]{1,0:T(8,128)(2,1)} %get-tuple-element.162.dqkv.refs_1_, bf16[1024,2048]{1,0:T(8,128)(2,1)} %get-tuple-element.151.du.refs_1_, ...), custom_call_target="tpu_custom_call", output_to_operand_aliasing={{2}: (13, {})} | custom-call | flops 751619276800 | bytes 1887436800 | tf_op jit(solution)/shard_map/backn/pallas_call | solution.py:523
  267.2 3.3 fusion.1.refs_4_
  270.5 2.3 collective-permute-start.29
  272.9 2.5 add_convert_fusion.10
  277.2 2.9 fusion.2.refs_2_
  280.1 9.1 %collective-permute-start.34 = (bf16[1024,512]{1,0:T(8,128)(2,1)}, bf16[1024,512]{1,0:T(8,128)(2,1)}, u32[]{:S(2)}, u32[]{:S(2)}) collective-permute-start(bf16[1024,512]{1,0:T(8,128)(2,1)} %fusion.2.refs_2_), channel_id=1, source_target_pairs={{0,1},{3,2},{1,0},{2,3},{4,5},{7,6},{5,4},{6,7},{8,9},{11,10},{9,8... | collective-permute-start | bytes 3145736 | tf_op jit(solution)/shard_map/ppermute | solution.py:837
  289.2 4.4 hsum.3
  293.6 10.0 %collective-permute-start.30 = (bf16[256,2048]{1,0:T(8,128)(2,1)}, bf16[256,2048]{1,0:T(8,128)(2,1)}, u32[]{:S(2)}, u32[]{:S(2)}) collective-permute-start(bf16[256,2048]{1,0:T(8,128)(2,1)} %get-tuple-element.183), channel_id=1, source_target_pairs={{0,4},{4,0},{8,24},{12,28},{16,20},{20,16},{24,8},{28,12},{1,5},{5... | collective-permute-start | bytes 3145736 | tf_op jit(solution)/shard_map/ppermute | solution.py:912
  303.6 16.3 %backn.3 = (bf16[1024,512]{1,0:T(8,128)(2,1)}, bf16[1024,512]{1,0:T(8,128)(2,1)}, f32[4,2048]{1,0:T(4,128)}) custom-call(s32[13]{0:T(128)} %concatenate.10.meta, bf16[1024,1536]{1,0:T(8,128)(2,1)} %get-tuple-element.162.dqkv.refs_1_, bf16[1024,2048]{1,0:T(8,128)(2,1)} %get-tuple-element.151.du.refs_1_, ...), custom_call_target="tpu_custom_call", output_to_operand_aliasing={{2}: (13, {})} | custom-call | flops 751619276800 | bytes 1887436800 | tf_op jit(solution)/shard_map/backn/pallas_call | solution.py:523
  320.0 2.6 add_convert_fusion.8
  324.4 2.9 fusion.3.refs_6_
  329.8 9.2 %wgrad.8 = bf16[1024,2048]{1,0:T(8,128)(2,1)} custom-call(s32[13]{0:T(128)} %concatenate.10.meta, bf16[1024,2048]{1,0:T(8,128)(2,1)} %norm2.1.h2.refs_0_, bf16[1024,2048]{1,0:T(8,128)(2,1)} %get-tuple-element.151.du.refs_1_), custom_call_target="tpu_custom_call" | custom-call | flops 440401920000 | bytes 1468006400 | tf_op jit(solution)/shard_map/wgrad/pallas_call | solution.py:602
  341.2 10.2 %wgrad.9 = bf16[1024,2048]{1,0:T(8,128)(2,1)} custom-call(s32[13]{0:T(128)} %concatenate.10.meta, bf16[1024,2048]{1,0:T(8,128)(2,1)} %get-tuple-element.125.h1.refs_0_, bf16[1024,1536]{1,0:T(8,128)(2,1)} %get-tuple-element.162.dqkv.refs_1_, bf16[1024,2048]{1,0:T(8,128)(2,1)} %get-tuple-element.149.g.refs_0_.refs_2_, ...), custom_call_target="tpu_custom_call" | custom-call | flops 503316480000 | bytes 1677721600 | tf_op jit(solution)/shard_map/wgrad/pallas_call | solution.py:602
  353.0 2.5 add_convert_fusion.6
  357.3 2.9 fusion.4.refs_0_
  362.3 10.0 %wgrad.10 = (bf16[512,2048]{1,0:T(8,128)(2,1)}, bf16[512,2048]{1,0:T(8,128)(2,1)}) custom-call(s32[13]{0:T(128)} %concatenate.10.meta, bf16[1024,2048]{1,0:T(8,128)(2,1)} %norm2.1.h2.refs_0_, bf16[1024,2048]{1,0:T(8,128)(2,1)} %get-tuple-element.151.du.refs_1_, bf16[1024,2048]{1,0:T(8,128)(2,1)} %collective-permute-done.36.refs_2_), custom_call_target="tpu_custom_call" | custom-call | flops 440401920000 | bytes 1468006400 | tf_op jit(solution)/shard_map/wgrad/pallas_call | solution.py:602
  372.3 4.4 lsum.3
  376.6 2.5 add_convert_fusion.4
  380.9 2.8 add_convert_fusion.3.refs_2_
  386.4 11.0 %wgrad.11 = (bf16[512,2048]{1,0:T(8,128)(2,1)}, bf16[512,2048]{1,0:T(8,128)(2,1)}) custom-call(s32[13]{0:T(128)} %concatenate.10.meta, bf16[1024,2048]{1,0:T(8,128)(2,1)} %get-tuple-element.125.h1.refs_0_, bf16[1024,1536]{1,0:T(8,128)(2,1)} %get-tuple-element.162.dqkv.refs_1_, bf16[1024,2048]{1,0:T(8,128)(2,1)} %get-tuple-element.149.g.refs_0_.refs_2_, ...), custom_call_target="tpu_custom_call" | custom-call | flops 503316480000 | bytes 1677721600 | tf_op jit(solution)/shard_map/wgrad/pallas_call | solution.py:602
  397.4 2.5 add_convert_fusion.2
  401.6 2.8 add_convert_fusion.1.refs_4_
  405.7 5.7 %collective-permute-done.42.got = bf16[512,2048]{1,0:T(8,128)(2,1)} collective-permute-done((bf16[512,2048]{1,0:T(8,128)(2,1)}, bf16[512,2048]{1,0:T(8,128)(2,1)}, u32[]{:S(2)}, u32[]{:S(2)}) %collective-permute-start.42) | collective-permute-done | bytes 2097184 | tf_op jit(solution)/shard_map/ppermute | solution.py:912
  411.4 4.4 hsum.4
  415.8 4.8 bout.2.refs_8_
  422.0 15.5 %collective-permute-done.43.got = bf16[256,2048]{1,0:T(8,128)(2,1)} collective-permute-done((bf16[256,2048]{1,0:T(8,128)(2,1)}, bf16[256,2048]{1,0:T(8,128)(2,1)}, u32[]{:S(2)}, u32[]{:S(2)}) %collective-permute-start.43) | collective-permute-done | bytes 1048608 | tf_op jit(solution)/shard_map/ppermute | solution.py:912
  437.5 4.0 lsum.4
  441.5 4.8 bout.3
  446.3 2.8 add_convert_fusion.refs_6_
  452.3 4.5 hsum.5
  460.6 3.3 collective-permute-start.50
  463.9 10.7 %collective-permute-done.49.refs_7_ = bf16[1024,512]{1,0:T(8,128)(2,1)} collective-permute-done((bf16[1024,512]{1,0:T(8,128)(2,1)}, bf16[1024,512]{1,0:T(8,128)(2,1)}, u32[]{:S(2)}, u32[]{:S(2)}) %collective-permute-start.49) | collective-permute-done | bytes 1048608 | tf_op jit(solution)/shard_map/ppermute | solution.py:837
  474.6 11.1 %igrad.1 = bf16[1024,2048]{1,0:T(8,128)(2,1)} custom-call(s32[13]{0:T(128)} %concatenate.10.meta, bf16[1024,2048]{1,0:T(8,128)(2,1)} %bitcast.36, bf16[1024,2048]{1,0:T(8,128)(2,1)} %bitcast.38, f32[1024,128]{1,0:T(8,128)} %get-tuple-element.129.st_ref, bf16[1024,512]{1,0:T(8,128)(2,1)} %fusion.4.refs_0_, bf16[1024,512]{1,0:T(8,128)(2,1)} %collective-permute-done.40.refs_1_, ...), custom_call_target="tpu_custom_call" | custom-call | flops 503316480000 | bytes 1677721600 | tf_op jit(solution)/shard_map/igrad/pallas_call | solution.py:775
  489.7 4.3 lsum.5
  (164 shorter events, 69.2 us)
Async XLA Ops:
  0.6 8.4 %copy-start.9 = (f32[256,2048]{1,0:T(8,128)S(1)}, f32[256,2048]{1,0:T(8,128)}, u32[]{:S(2)}) copy-start(f32[256,2048]{1,0:T(8,128)} %param.26) | copy-start | bytes 6291460
  4.6 27.3 %collective-permute-start = (bf16[256,2048]{1,0:T(8,128)(2,1)}, bf16[256,2048]{1,0:T(8,128)(2,1)}, u32[]{:S(2)}, u32[]{:S(2)}) collective-permute-start(bf16[256,2048]{1,0:T(8,128)(2,1)} %pad_maximum_fusion.refs_0_), channel_id=1, source_target_pairs={{0,4},{4,0},{1,5},{5,1},{2,6},{6,2},{3,7},{7,3},{8,12},{12,8},{9,1... | collective-permute-start | bytes 3145736 | tf_op jit(solution)/shard_map/ppermute | solution.py:872
  7.6 24.9 %collective-permute-start.2 = (bf16[256,2048]{1,0:T(8,128)(2,1)}, bf16[256,2048]{1,0:T(8,128)(2,1)}, u32[]{:S(2)}, u32[]{:S(2)}) collective-permute-start(bf16[256,2048]{1,0:T(8,128)(2,1)} %pad_maximum_fusion.refs_0_), channel_id=1, source_target_pairs={{0,16},{16,0},{8,24},{24,8},{1,17},{17,1},{9,25},{25,9},{2,18},{18... | collective-permute-start | bytes 3145736 | tf_op jit(solution)/shard_map/ppermute | solution.py:866
  10.2 46.4 %collective-permute-start.1 = (bf16[256,2048]{1,0:T(8,128)(2,1)}, bf16[256,2048]{1,0:T(8,128)(2,1)}, u32[]{:S(2)}, u32[]{:S(2)}) collective-permute-start(bf16[256,2048]{1,0:T(8,128)(2,1)} %convert_element_type.174.refs_0_), channel_id=1, source_target_pairs={{0,4},{4,0},{1,5},{5,1},{2,6},{6,2},{3,7},{7,3},{8,12},{12,8},{9,1... | collective-permute-start | bytes 3145736 | tf_op jit(solution)/shard_map/ppermute | solution.py:872
  13.3 122.4 %collective-permute-start.12 = (bf16[256,2048]{1,0:T(8,128)(2,1)}, bf16[256,2048]{1,0:T(8,128)(2,1)}, u32[]{:S(2)}, u32[]{:S(2)}) collective-permute-start(bf16[256,2048]{1,0:T(8,128)(2,1)} %bitcast.21.refs_0_), channel_id=1, source_target_pairs={{0,4},{4,0},{1,5},{5,1},{2,6},{6,2},{3,7},{7,3},{8,12},{12,8},{9,1... | collective-permute-start | bytes 3145736 | tf_op jit(solution)/shard_map/ppermute | solution.py:872
  15.4 10.5 %copy-start.20 = (f32[1536]{0:T(1024)S(1)}, f32[1536]{0:T(1024)}, u32[]{:S(2)}) copy-start(f32[1536]{0:T(1024)} %param.23) | copy-start | bytes 18436
  15.4 11.1 %copy-start.18 = (f32[2048]{0:T(1024)S(1)}, f32[2048]{0:T(1024)}, u32[]{:S(2)}) copy-start(f32[2048]{0:T(1024)} %param.25) | copy-start | bytes 24580
  15.4 11.1 %copy-start.19 = (f32[2048]{0:T(1024)S(1)}, f32[2048]{0:T(1024)}, u32[]{:S(2)}) copy-start(f32[2048]{0:T(1024)} %param.29) | copy-start | bytes 24580
  32.5 24.1 %collective-permute-start.3 = (bf16[256,2048]{1,0:T(8,128)(2,1)}, bf16[256,2048]{1,0:T(8,128)(2,1)}, u32[]{:S(2)}, u32[]{:S(2)}) collective-permute-start(bf16[256,2048]{1,0:T(8,128)(2,1)} %collective-permute-done.refs_1_), channel_id=1, source_target_pairs={{0,16},{16,0},{8,24},{24,8},{1,17},{17,1},{9,25},{25,9},{2,18},{18... | collective-permute-start | bytes 3145736 | tf_op jit(solution)/shard_map/ppermute | solution.py:866
  37.8 24.7 %collective-permute-start.4 = (bf16[512,2048]{1,0:T(8,128)(2,1)}, bf16[512,2048]{1,0:T(8,128)(2,1)S(1)}, u32[]{:S(2)}, u32[]{:S(2)}) collective-permute-start(bf16[512,2048]{1,0:T(8,128)(2,1)} %pack.3.w0.refs_0_.w10), channel_id=1, source_target_pairs={{0,8},{8,0},{16,24},{24,16},{1,9},{9,1},{17,25},{25,17},{2,10},{10... | collective-permute-start | bytes 6291464 | tf_op jit(solution)/shard_map/ppermute | solution.py:869
  37.8 23.2 %collective-permute-start.5 = (bf16[256,2048]{1,0:T(8,128)(2,1)}, bf16[256,2048]{1,0:T(8,128)(2,1)S(1)}, u32[]{:S(2)}, u32[]{:S(2)}) collective-permute-start(bf16[256,2048]{1,0:T(8,128)(2,1)} %collective-permute-done.2.w1.refs_0_.w11), channel_id=1, source_target_pairs={{0,8},{8,0},{16,24},{24,16},{1,9},{9,1},{17,25},{25,17},{2,10},{10... | collective-permute-start | bytes 3145736 | tf_op jit(solution)/shard_map/ppermute | solution.py:869
  56.6 5.8 %collective-permute-start.6 = (bf16[256,2048]{1,0:T(8,128)(2,1)}, bf16[256,2048]{1,0:T(8,128)(2,1)}, u32[]{:S(2)}, u32[]{:S(2)}) collective-permute-start(bf16[256,2048]{1,0:T(8,128)(2,1)} %collective-permute-done.3.w2.refs_1_.w12), channel_id=1, source_target_pairs={{0,8},{8,0},{16,24},{24,16},{1,9},{9,1},{17,25},{25,17},{2,10},{10... | collective-permute-start | bytes 3145736 | tf_op jit(solution)/shard_map/ppermute | solution.py:869
  60.4 57.3 %collective-permute-start.9 = (bf16[512,2048]{1,0:T(8,128)(2,1)}, bf16[512,2048]{1,0:T(8,128)(2,1)}, u32[]{:S(2)}, u32[]{:S(2)}) collective-permute-start(bf16[512,2048]{1,0:T(8,128)(2,1)} %pack.4.w0.w20), channel_id=1, source_target_pairs={{0,8},{8,0},{16,24},{24,16},{1,9},{9,1},{17,25},{25,17},{2,10},{10... | collective-permute-start | bytes 6291464 | tf_op jit(solution)/shard_map/ppermute | solution.py:869
  61.0 25.5 %collective-permute-start.7 = (bf16[256,2048]{1,0:T(8,128)(2,1)}, bf16[256,2048]{1,0:T(8,128)(2,1)}, u32[]{:S(2)}, u32[]{:S(2)}) collective-permute-start(bf16[256,2048]{1,0:T(8,128)(2,1)} %convert_element_type.174.refs_0_), channel_id=1, source_target_pairs={{0,16},{16,0},{8,24},{24,8},{1,17},{17,1},{9,25},{25,9},{2,18},{18... | collective-permute-start | bytes 3145736 | tf_op jit(solution)/shard_map/ppermute | solution.py:866
  73.5 71.5 %collective-permute-start.13 = (bf16[1024,1024]{1,0:T(8,128)(2,1)}, bf16[1024,1024]{1,0:T(8,128)(2,1)}, u32[]{:S(2)}, u32[]{:S(2)}) collective-permute-start(bf16[1024,1024]{1,0:T(8,128)(2,1)} %kv.1.kv_ref), channel_id=1, source_target_pairs={{0,4},{1,5},{2,6},{3,7},{8,12},{9,13},{10,14},{11,15},{16,20},{17,... | collective-permute-start | bytes 6291464 | tf_op jit(solution)/shard_map/ppermute | solution.py:929
  86.4 24.6 %collective-permute-start.8 = (bf16[256,2048]{1,0:T(8,128)(2,1)}, bf16[256,2048]{1,0:T(8,128)(2,1)}, u32[]{:S(2)}, u32[]{:S(2)}) collective-permute-start(bf16[256,2048]{1,0:T(8,128)(2,1)} %collective-permute-done.1.refs_1_), channel_id=1, source_target_pairs={{0,16},{16,0},{8,24},{24,8},{1,17},{17,1},{9,25},{25,9},{2,18},{18... | collective-permute-start | bytes 3145736 | tf_op jit(solution)/shard_map/ppermute | solution.py:866
  87.9 31.3 %collective-permute-start.10 = (bf16[256,2048]{1,0:T(8,128)(2,1)}, bf16[256,2048]{1,0:T(8,128)(2,1)}, u32[]{:S(2)}, u32[]{:S(2)}) collective-permute-start(bf16[256,2048]{1,0:T(8,128)(2,1)} %collective-permute-done.7.w1.w21), channel_id=1, source_target_pairs={{0,8},{8,0},{16,24},{24,16},{1,9},{9,1},{17,25},{25,17},{2,10},{10... | collective-permute-start | bytes 3145736 | tf_op jit(solution)/shard_map/ppermute | solution.py:869
  111.0 8.2 %collective-permute-start.11 = (bf16[256,2048]{1,0:T(8,128)(2,1)}, bf16[256,2048]{1,0:T(8,128)(2,1)}, u32[]{:S(2)}, u32[]{:S(2)}) collective-permute-start(bf16[256,2048]{1,0:T(8,128)(2,1)} %collective-permute-done.8.w2.w22), channel_id=1, source_target_pairs={{0,8},{8,0},{16,24},{24,16},{1,9},{9,1},{17,25},{25,17},{2,10},{10... | collective-permute-start | bytes 3145736 | tf_op jit(solution)/shard_map/ppermute | solution.py:869
  117.7 25.9 %collective-permute-start.15 = (bf16[256,2048]{1,0:T(8,128)(2,1)}, bf16[256,2048]{1,0:T(8,128)(2,1)}, u32[]{:S(2)}, u32[]{:S(2)}) collective-permute-start(bf16[256,2048]{1,0:T(8,128)(2,1)} %bitcast.21.refs_0_), channel_id=1, source_target_pairs={{0,16},{16,0},{8,24},{24,8},{1,17},{17,1},{9,25},{25,9},{2,18},{18... | collective-permute-start | bytes 3145736 | tf_op jit(solution)/shard_map/ppermute | solution.py:866
  139.5 19.4 %collective-permute-start.14 = (bf16[512,2048]{1,0:T(8,128)(2,1)}, bf16[512,2048]{1,0:T(8,128)(2,1)}, u32[]{:S(2)}, u32[]{:S(2)}) collective-permute-start(bf16[512,2048]{1,0:T(8,128)(2,1)} %pack.5.refs_2_.w0), channel_id=1, source_target_pairs={{0,8},{8,0},{16,24},{24,16},{1,9},{9,1},{17,25},{25,17},{2,10},{10... | collective-permute-start | bytes 6291464 | tf_op jit(solution)/shard_map/ppermute | solution.py:869
  143.6 31.1 %collective-permute-start.16 = (bf16[256,2048]{1,0:T(8,128)(2,1)}, bf16[256,2048]{1,0:T(8,128)(2,1)}, u32[]{:S(2)}, u32[]{:S(2)}) collective-permute-start(bf16[256,2048]{1,0:T(8,128)(2,1)} %collective-permute-done.12.refs_1_), channel_id=1, source_target_pairs={{0,16},{16,0},{8,24},{24,8},{1,17},{17,1},{9,25},{25,9},{2,18},{18... | collective-permute-start | bytes 3145736 | tf_op jit(solution)/shard_map/ppermute | solution.py:866
  157.6 26.9 %collective-permute-start.17 = (bf16[256,2048]{1,0:T(8,128)(2,1)}, bf16[256,2048]{1,0:T(8,128)(2,1)}, u32[]{:S(2)}, u32[]{:S(2)}) collective-permute-start(bf16[256,2048]{1,0:T(8,128)(2,1)} %collective-permute-done.15.refs_4_.w1), channel_id=1, source_target_pairs={{0,8},{8,0},{16,24},{24,16},{1,9},{9,1},{17,25},{25,17},{2,10},{10... | collective-permute-start | bytes 3145736 | tf_op jit(solution)/shard_map/ppermute | solution.py:869
  157.6 76.9 %collective-permute-start.22 = (bf16[1024,1024]{1,0:T(8,128)(2,1)}, bf16[1024,1024]{1,0:T(8,128)(2,1)}, u32[]{:S(2)}, u32[]{:S(2)}) collective-permute-start(bf16[1024,1024]{1,0:T(8,128)(2,1)} %get-tuple-element.161), channel_id=1, source_target_pairs={{4,0},{5,1},{6,2},{7,3},{12,8},{13,9},{14,10},{15,11},{20,16},{21,... | collective-permute-start | bytes 6291464 | tf_op jit(solution)/shard_map/ppermute | solution.py:932
  169.9 43.8 %collective-permute-start.19 = (bf16[1024,512]{1,0:T(8,128)(2,1)}, bf16[1024,512]{1,0:T(8,128)(2,1)}, u32[]{:S(2)}, u32[]{:S(2)}) collective-permute-start(bf16[1024,512]{1,0:T(8,128)(2,1)} %get-tuple-element.152), channel_id=1, source_target_pairs={{0,1},{3,2},{4,5},{7,6},{8,9},{11,10},{12,13},{15,14},{16,17},{19,... | collective-permute-start | bytes 3145736 | tf_op jit(solution)/shard_map/ppermute | solution.py:837
  174.7 12.1 %collective-permute-start.18 = (bf16[256,2048]{1,0:T(8,128)(2,1)}, bf16[256,2048]{1,0:T(8,128)(2,1)}, u32[]{:S(2)}, u32[]{:S(2)}) collective-permute-start(bf16[256,2048]{1,0:T(8,128)(2,1)} %collective-permute-done.16.refs_5_.w2), channel_id=1, source_target_pairs={{0,8},{8,0},{16,24},{24,16},{1,9},{9,1},{17,25},{25,17},{2,10},{10... | collective-permute-start | bytes 3145736 | tf_op jit(solution)/shard_map/ppermute | solution.py:869
  184.2 35.8 %collective-permute-start.20 = (bf16[1024,2048]{1,0:T(8,128)(2,1)}, bf16[1024,2048]{1,0:T(8,128)(2,1)}, u32[]{:S(2)}, u32[]{:S(2)}) collective-permute-start(bf16[1024,2048]{1,0:T(8,128)(2,1)} %wgrad.6), channel_id=1, source_target_pairs={{0,8},{8,0},{16,24},{24,16},{1,9},{9,1},{17,25},{25,17},{2,10},{10... | collective-permute-start | bytes 12582920 | tf_op jit(solution)/shard_map/ppermute | solution.py:869
  184.5 45.6 %collective-permute-start.21 = (bf16[1024,512]{1,0:T(8,128)(2,1)}, bf16[1024,512]{1,0:T(8,128)(2,1)}, u32[]{:S(2)}, u32[]{:S(2)}) collective-permute-start(bf16[1024,512]{1,0:T(8,128)(2,1)} %get-tuple-element.158), channel_id=1, source_target_pairs={{0,1},{3,2},{4,5},{7,6},{8,9},{11,10},{12,13},{15,14},{16,17},{19,... | collective-permute-start | bytes 3145736 | tf_op jit(solution)/shard_map/ppermute | solution.py:837
  198.5 15.2 %copy-start.11 = (bf16[1024,512]{1,0:T(8,128)(2,1)S(1)}, bf16[1024,512]{1,0:T(8,128)(2,1)}, u32[]{:S(2)}) copy-start(bf16[1024,512]{1,0:T(8,128)(2,1)} %get-tuple-element.152) | copy-start | bytes 3145732
  216.1 24.4 %collective-permute-start.23 = (bf16[1024,512]{1,0:T(8,128)(2,1)}, bf16[1024,512]{1,0:T(8,128)(2,1)}, u32[]{:S(2)}, u32[]{:S(2)}) collective-permute-start(bf16[1024,512]{1,0:T(8,128)(2,1)} %add_convert_fusion.15), channel_id=1, source_target_pairs={{1,2},{2,1},{5,6},{6,5},{9,10},{10,9},{13,14},{14,13},{17,18},{18,... | collective-permute-start | bytes 3145736 | tf_op jit(solution)/shard_map/ppermute | solution.py:847
  217.8 27.0 %collective-permute-start.24 = (bf16[1024,512]{1,0:T(8,128)(2,1)}, bf16[1024,512]{1,0:T(8,128)(2,1)}, u32[]{:S(2)}, u32[]{:S(2)}) collective-permute-start(bf16[1024,512]{1,0:T(8,128)(2,1)} %get-tuple-element.165), channel_id=1, source_target_pairs={{0,1},{3,2},{4,5},{7,6},{8,9},{11,10},{12,13},{15,14},{16,17},{19,... | collective-permute-start | bytes 3145736 | tf_op jit(solution)/shard_map/ppermute | solution.py:837
  232.9 34.3 %collective-permute-start.25 = (bf16[1024,512]{1,0:T(8,128)(2,1)}, bf16[1024,512]{1,0:T(8,128)(2,1)}, u32[]{:S(2)}, u32[]{:S(2)}) collective-permute-start(bf16[1024,512]{1,0:T(8,128)(2,1)} %add_convert_fusion.14), channel_id=1, source_target_pairs={{1,2},{2,1},{5,6},{6,5},{9,10},{10,9},{13,14},{14,13},{17,18},{18,... | collective-permute-start | bytes 3145736 | tf_op jit(solution)/shard_map/ppermute | solution.py:847
  243.6 29.3 %collective-permute-start.26 = (bf16[1024,512]{1,0:T(8,128)(2,1)}, bf16[1024,512]{1,0:T(8,128)(2,1)}, u32[]{:S(2)}, u32[]{:S(2)}) collective-permute-start(bf16[1024,512]{1,0:T(8,128)(2,1)} %fusion.refs_0_), channel_id=1, source_target_pairs={{0,1},{3,2},{1,0},{2,3},{4,5},{7,6},{5,4},{6,7},{8,9},{11,10},{9,8... | collective-permute-start | bytes 3145736 | tf_op jit(solution)/shard_map/ppermute | solution.py:837
  247.6 29.6 %collective-permute-start.27 = (bf16[1024,512]{1,0:T(8,128)(2,1)}, bf16[1024,512]{1,0:T(8,128)(2,1)}, u32[]{:S(2)}, u32[]{:S(2)}) collective-permute-start(bf16[1024,512]{1,0:T(8,128)(2,1)} %add_convert_fusion.12), channel_id=1, source_target_pairs={{1,2},{2,1},{5,6},{6,5},{9,10},{10,9},{13,14},{14,13},{17,18},{18,... | collective-permute-start | bytes 3145736 | tf_op jit(solution)/shard_map/ppermute | solution.py:847
  249.3 40.0 %collective-permute-start.28 = (bf16[512,2048]{1,0:T(8,128)(2,1)}, bf16[512,2048]{1,0:T(8,128)(2,1)}, u32[]{:S(2)}, u32[]{:S(2)}) collective-permute-start(bf16[512,2048]{1,0:T(8,128)(2,1)} %get-tuple-element.173), channel_id=1, source_target_pairs={{0,16},{4,20},{8,12},{12,8},{16,0},{20,4},{24,28},{28,24},{1,17},{... | collective-permute-start | bytes 6291464 | tf_op jit(solution)/shard_map/ppermute | solution.py:912
  250.4 16.2 %copy-start.21 = (f32[1,1536]{1,0:T(1,128)S(1)}, f32[1,1536]{1,0:T(1,128)}, u32[]{:S(2)}) copy-start(f32[1,1536]{1,0:T(1,128)} %get-tuple-element.181) | copy-start | bytes 18436
  270.5 6.7 %copy-start.2 = (bf16[1024,512]{1,0:T(8,128)(2,1)S(1)}, bf16[1024,512]{1,0:T(8,128)(2,1)}, u32[]{:S(2)}) copy-start(bf16[1024,512]{1,0:T(8,128)(2,1)} %get-tuple-element.190) | copy-start | bytes 3145732
  270.5 49.4 %collective-permute-start.29 = (bf16[1024,512]{1,0:T(8,128)(2,1)}, bf16[1024,512]{1,0:T(8,128)(2,1)}, u32[]{:S(2)}, u32[]{:S(2)}) collective-permute-start(bf16[1024,512]{1,0:T(8,128)(2,1)} %fusion.1.refs_4_), channel_id=1, source_target_pairs={{0,1},{3,2},{1,0},{2,3},{4,5},{7,6},{5,4},{6,7},{8,9},{11,10},{9,8... | collective-permute-start | bytes 3145736 | tf_op jit(solution)/shard_map/ppermute | solution.py:837
  275.4 49.0 %collective-permute-start.31 = (bf16[1024,512]{1,0:T(8,128)(2,1)}, bf16[1024,512]{1,0:T(8,128)(2,1)}, u32[]{:S(2)}, u32[]{:S(2)}) collective-permute-start(bf16[1024,512]{1,0:T(8,128)(2,1)} %add_convert_fusion.10), channel_id=1, source_target_pairs={{1,2},{2,1},{5,6},{6,5},{9,10},{10,9},{13,14},{14,13},{17,18},{18,... | collective-permute-start | bytes 3145736 | tf_op jit(solution)/shard_map/ppermute | solution.py:847
  280.1 72.8 %collective-permute-start.34 = (bf16[1024,512]{1,0:T(8,128)(2,1)}, bf16[1024,512]{1,0:T(8,128)(2,1)}, u32[]{:S(2)}, u32[]{:S(2)}) collective-permute-start(bf16[1024,512]{1,0:T(8,128)(2,1)} %fusion.2.refs_2_), channel_id=1, source_target_pairs={{0,1},{3,2},{1,0},{2,3},{4,5},{7,6},{5,4},{6,7},{8,9},{11,10},{9,8... | collective-permute-start | bytes 3145736 | tf_op jit(solution)/shard_map/ppermute | solution.py:837
  293.6 36.2 %collective-permute-start.30 = (bf16[256,2048]{1,0:T(8,128)(2,1)}, bf16[256,2048]{1,0:T(8,128)(2,1)}, u32[]{:S(2)}, u32[]{:S(2)}) collective-permute-start(bf16[256,2048]{1,0:T(8,128)(2,1)} %get-tuple-element.183), channel_id=1, source_target_pairs={{0,4},{4,0},{8,24},{12,28},{16,20},{20,16},{24,8},{28,12},{1,5},{5... | collective-permute-start | bytes 3145736 | tf_op jit(solution)/shard_map/ppermute | solution.py:912
  303.6 16.3 %copy-start.8 = (bf16[1024,512]{1,0:T(8,128)(2,1)S(1)}, bf16[1024,512]{1,0:T(8,128)(2,1)}, u32[]{:S(2)}) copy-start(bf16[1024,512]{1,0:T(8,128)(2,1)} %get-tuple-element.178) | copy-start | bytes 3145732
  322.6 34.8 %collective-permute-start.35 = (bf16[1024,512]{1,0:T(8,128)(2,1)}, bf16[1024,512]{1,0:T(8,128)(2,1)}, u32[]{:S(2)}, u32[]{:S(2)}) collective-permute-start(bf16[1024,512]{1,0:T(8,128)(2,1)} %add_convert_fusion.8), channel_id=1, source_target_pairs={{1,2},{2,1},{5,6},{6,5},{9,10},{10,9},{13,14},{14,13},{17,18},{18,... | collective-permute-start | bytes 3145736 | tf_op jit(solution)/shard_map/ppermute | solution.py:847
  328.0 11.1 %collective-permute-start.32 = (f32[13824]{0:T(1024)}, f32[13824]{0:T(1024)}, u32[]{:S(2)}, u32[]{:S(2)}) collective-permute-start(f32[13824]{0:T(1024)} %pad_maximum_fusion.1), channel_id=1, source_target_pairs={{0,8},{8,0},{16,24},{24,16},{1,9},{9,1},{17,25},{25,17},{2,10},{10... | collective-permute-start | bytes 165896 | tf_op jit(solution)/shard_map/ppermute | solution.py:869
  328.0 48.7 %collective-permute-start.37 = (bf16[1024,512]{1,0:T(8,128)(2,1)}, bf16[1024,512]{1,0:T(8,128)(2,1)}, u32[]{:S(2)}, u32[]{:S(2)}) collective-permute-start(bf16[1024,512]{1,0:T(8,128)(2,1)} %fusion.3.refs_6_), channel_id=1, source_target_pairs={{0,1},{3,2},{1,0},{2,3},{4,5},{7,6},{5,4},{6,7},{8,9},{11,10},{9,8... | collective-permute-start | bytes 3145736 | tf_op jit(solution)/shard_map/ppermute | solution.py:837
  340.5 10.9 %collective-permute-start.33 = (f32[13824]{0:T(1024)}, f32[13824]{0:T(1024)}, u32[]{:S(2)}, u32[]{:S(2)}) collective-permute-start(f32[13824]{0:T(1024)} %add.111), channel_id=1, source_target_pairs={{0,16},{16,0},{8,24},{24,8},{1,17},{17,1},{9,25},{25,9},{2,18},{18... | collective-permute-start | bytes 165896 | tf_op jit(solution)/shard_map/ppermute | solution.py:866
  341.2 21.1 %collective-permute-start.36 = (bf16[1024,2048]{1,0:T(8,128)(2,1)}, bf16[1024,2048]{1,0:T(8,128)(2,1)}, u32[]{:S(2)}, u32[]{:S(2)}) collective-permute-start(bf16[1024,2048]{1,0:T(8,128)(2,1)} %wgrad.8), channel_id=1, source_target_pairs={{0,8},{8,0},{16,24},{24,16},{1,9},{9,1},{17,25},{25,17},{2,10},{10... | collective-permute-start | bytes 12582920 | tf_op jit(solution)/shard_map/ppermute | solution.py:869
  341.2 11.8 %copy-start.3 = (bf16[1024,512]{1,0:T(8,128)(2,1)S(1)}, bf16[1024,512]{1,0:T(8,128)(2,1)}, u32[]{:S(2)}) copy-start(bf16[1024,512]{1,0:T(8,128)(2,1)} %get-tuple-element.190) | copy-start | bytes 3145732
  355.4 25.4 %collective-permute-start.38 = (bf16[1024,512]{1,0:T(8,128)(2,1)}, bf16[1024,512]{1,0:T(8,128)(2,1)}, u32[]{:S(2)}, u32[]{:S(2)}) collective-permute-start(bf16[1024,512]{1,0:T(8,128)(2,1)} %add_convert_fusion.6), channel_id=1, source_target_pairs={{1,2},{2,1},{5,6},{6,5},{9,10},{10,9},{13,14},{14,13},{17,18},{18,... | collective-permute-start | bytes 3145736 | tf_op jit(solution)/shard_map/ppermute | solution.py:847
  360.3 37.2 %collective-permute-start.40 = (bf16[1024,512]{1,0:T(8,128)(2,1)}, bf16[1024,512]{1,0:T(8,128)(2,1)}, u32[]{:S(2)}, u32[]{:S(2)}) collective-permute-start(bf16[1024,512]{1,0:T(8,128)(2,1)} %fusion.4.refs_0_), channel_id=1, source_target_pairs={{0,1},{3,2},{1,0},{2,3},{4,5},{7,6},{5,4},{6,7},{8,9},{11,10},{9,8... | collective-permute-start | bytes 3145736 | tf_op jit(solution)/shard_map/ppermute | solution.py:837
  372.3 14.2 %collective-permute-start.39 = (bf16[1024,2048]{1,0:T(8,128)(2,1)}, bf16[1024,2048]{1,0:T(8,128)(2,1)}, u32[]{:S(2)}, u32[]{:S(2)}) collective-permute-start(bf16[1024,2048]{1,0:T(8,128)(2,1)} %wgrad.9), channel_id=1, source_target_pairs={{0,8},{8,0},{16,24},{24,16},{1,9},{9,1},{17,25},{25,17},{2,10},{10... | collective-permute-start | bytes 12582920 | tf_op jit(solution)/shard_map/ppermute | solution.py:869
  379.2 22.4 %collective-permute-start.41 = (bf16[1024,512]{1,0:T(8,128)(2,1)}, bf16[1024,512]{1,0:T(8,128)(2,1)}, u32[]{:S(2)}, u32[]{:S(2)}) collective-permute-start(bf16[1024,512]{1,0:T(8,128)(2,1)} %add_convert_fusion.4), channel_id=1, source_target_pairs={{1,2},{2,1},{5,6},{6,5},{9,10},{10,9},{13,14},{14,13},{17,18},{18,... | collective-permute-start | bytes 3145736 | tf_op jit(solution)/shard_map/ppermute | solution.py:847
  383.7 66.7 %collective-permute-start.44 = (bf16[1024,512]{1,0:T(8,128)(2,1)}, bf16[1024,512]{1,0:T(8,128)(2,1)}, u32[]{:S(2)}, u32[]{:S(2)}) collective-permute-start(bf16[1024,512]{1,0:T(8,128)(2,1)} %add_convert_fusion.3.refs_2_), channel_id=1, source_target_pairs={{1,0},{2,3},{5,4},{6,7},{9,8},{10,11},{13,12},{14,15},{17,16},{18,... | collective-permute-start | bytes 3145736 | tf_op jit(solution)/shard_map/ppermute | solution.py:837
  384.9 26.4 %collective-permute-start.42 = (bf16[512,2048]{1,0:T(8,128)(2,1)}, bf16[512,2048]{1,0:T(8,128)(2,1)}, u32[]{:S(2)}, u32[]{:S(2)}) collective-permute-start(bf16[512,2048]{1,0:T(8,128)(2,1)} %get-tuple-element.204), channel_id=1, source_target_pairs={{0,16},{4,20},{8,12},{12,8},{16,0},{20,4},{24,28},{28,24},{1,17},{... | collective-permute-start | bytes 6291464 | tf_op jit(solution)/shard_map/ppermute | solution.py:912
  386.4 11.0 %copy-start.1 = (bf16[1024,512]{1,0:T(8,128)(2,1)S(1)}, bf16[1024,512]{1,0:T(8,128)(2,1)}, u32[]{:S(2)}) copy-start(bf16[1024,512]{1,0:T(8,128)(2,1)} %get-tuple-element.201) | copy-start | bytes 3145732
  399.9 46.4 %collective-permute-start.45 = (bf16[1024,512]{1,0:T(8,128)(2,1)}, bf16[1024,512]{1,0:T(8,128)(2,1)}, u32[]{:S(2)}, u32[]{:S(2)}) collective-permute-start(bf16[1024,512]{1,0:T(8,128)(2,1)} %add_convert_fusion.2), channel_id=1, source_target_pairs={{1,2},{2,1},{5,6},{6,5},{9,10},{10,9},{13,14},{14,13},{17,18},{18,... | collective-permute-start | bytes 3145736 | tf_op jit(solution)/shard_map/ppermute | solution.py:847
  404.4 59.6 %collective-permute-start.48 = (bf16[1024,512]{1,0:T(8,128)(2,1)}, bf16[1024,512]{1,0:T(8,128)(2,1)}, u32[]{:S(2)}, u32[]{:S(2)}) collective-permute-start(bf16[1024,512]{1,0:T(8,128)(2,1)} %add_convert_fusion.1.refs_4_), channel_id=1, source_target_pairs={{1,0},{2,3},{5,4},{6,7},{9,8},{10,11},{13,12},{14,15},{17,16},{18,... | collective-permute-start | bytes 3145736 | tf_op jit(solution)/shard_map/ppermute | solution.py:837
  415.8 21.7 %collective-permute-start.43 = (bf16[256,2048]{1,0:T(8,128)(2,1)}, bf16[256,2048]{1,0:T(8,128)(2,1)}, u32[]{:S(2)}, u32[]{:S(2)}) collective-permute-start(bf16[256,2048]{1,0:T(8,128)(2,1)} %get-tuple-element.208), channel_id=1, source_target_pairs={{0,4},{4,0},{8,24},{12,28},{16,20},{20,16},{24,8},{28,12},{1,5},{5... | collective-permute-start | bytes 3145736 | tf_op jit(solution)/shard_map/ppermute | solution.py:912
  420.6 31.4 %collective-permute-start.46 = (bf16[512,2048]{1,0:T(8,128)(2,1)}, bf16[512,2048]{1,0:T(8,128)(2,1)}, u32[]{:S(2)}, u32[]{:S(2)}) collective-permute-start(bf16[512,2048]{1,0:T(8,128)(2,1)} %get-tuple-element.211), channel_id=1, source_target_pairs={{0,16},{4,20},{8,12},{12,8},{16,0},{20,4},{24,28},{28,24},{1,17},{... | collective-permute-start | bytes 6291464 | tf_op jit(solution)/shard_map/ppermute | solution.py:912
  449.1 25.5 %collective-permute-start.49 = (bf16[1024,512]{1,0:T(8,128)(2,1)}, bf16[1024,512]{1,0:T(8,128)(2,1)}, u32[]{:S(2)}, u32[]{:S(2)}) collective-permute-start(bf16[1024,512]{1,0:T(8,128)(2,1)} %add_convert_fusion.refs_6_), channel_id=1, source_target_pairs={{1,0},{2,3},{5,4},{6,7},{9,8},{10,11},{13,12},{14,15},{17,16},{18,... | collective-permute-start | bytes 3145736 | tf_op jit(solution)/shard_map/ppermute | solution.py:837
  452.0 6.5 %collective-permute-start.47 = (f32[13824]{0:T(1024)}, f32[13824]{0:T(1024)}, u32[]{:S(2)}, u32[]{:S(2)}) collective-permute-start(f32[13824]{0:T(1024)} %add.112), channel_id=1, source_target_pairs={{0,4},{4,0},{1,5},{5,1},{2,6},{6,2},{3,7},{7,3},{8,12},{12,8},{9,1... | collective-permute-start | bytes 165896 | tf_op jit(solution)/shard_map/ppermute | solution.py:872
  456.8 32.9 %collective-permute-start.51 = (bf16[256,2048]{1,0:T(8,128)(2,1)}, bf16[256,2048]{1,0:T(8,128)(2,1)}, u32[]{:S(2)}, u32[]{:S(2)}) collective-permute-start(bf16[256,2048]{1,0:T(8,128)(2,1)} %get-tuple-element.220), channel_id=1, source_target_pairs={{0,4},{4,0},{8,24},{12,28},{16,20},{20,16},{24,8},{28,12},{1,5},{5... | collective-permute-start | bytes 3145736 | tf_op jit(solution)/shard_map/ppermute | solution.py:912
  460.6 27.7 %collective-permute-start.50 = (f32[8192]{0:T(1024)}, f32[8192]{0:T(1024)}, u32[]{:S(2)}, u32[]{:S(2)}) collective-permute-start(f32[8192]{0:T(1024)} %slice.40), channel_id=1, source_target_pairs={{0,1},{1,0},{2,3},{3,2},{4,5},{5,4},{6,7},{7,6},{8,9},{9,8},{10,11... | collective-permute-start | bytes 98312 | tf_op jit(solution)/shard_map/ppermute | solution.py:945
  489.7 5.1 %collective-permute-start.52 = (f32[8192]{0:T(1024)}, f32[8192]{0:T(1024)}, u32[]{:S(2)}, u32[]{:S(2)}) collective-permute-start(f32[8192]{0:T(1024)} %add.122), channel_id=1, source_target_pairs={{0,2},{2,0},{1,3},{3,1},{4,6},{6,4},{5,7},{7,5},{8,10},{10,8},{9,1... | collective-permute-start | bytes 98312 | tf_op jit(solution)/shard_map/ppermute | solution.py:947
  489.7 6.5 %copy-start.15 = (f32[2048]{0:T(1024)S(1)}, f32[2048]{0:T(1024)}, u32[]{:S(2)}) copy-start(f32[2048]{0:T(1024)} %get-tuple-element.262) | copy-start | bytes 24580
  (13 other events, 53.5 us)

commit v8 on v7

--- a/solution.py
+++ b/solution.py
@@ -674,7 +674,7 @@
         at += count
 
 
-def last_sum_call(mid, got, plan):
+def last_sum_call(mid, got, plan, scale):
     n, cols = mid.shape
     t = 512
     block = pl.BlockSpec((n, t), lambda j: (0, j))
@@ -698,7 +698,7 @@
         out_specs=out_specs,
         out_shape=out_shape,
         compiler_params=params(1),
-        cost_estimate=cost(2 * n * cols, 10 * n * cols),
+        cost_estimate=cost(2 * n * cols, 10 * n * cols, k=scale),
     )(mid, got)
 
 
@@ -756,7 +756,7 @@
     by_role(meta, refs[:8], body)
 
 
-def rows_call(meta, *ops, body, name, specs, steps=None, into=None):
+def rows_call(meta, *ops, body, name, specs, steps=None, into=None, scale=COST_SCALE):
     rows = 256
     m, d = ops[0].shape
     first, last = steps or (0, m // rows)
@@ -784,7 +784,7 @@
         out_shape=jax.ShapeDtypeStruct((m, d), BF),
         input_output_aliases=aliases,
         compiler_params=params(1),
-        cost_estimate=cost(10 * (last - first) * rows * d, 8 * (last - first) * rows * d),
+        cost_estimate=cost(10 * (last - first) * rows * d, 8 * (last - first) * rows * d, k=scale),
     )(meta, *ops)
 
 
@@ -922,8 +922,8 @@
         mid, send = run(half_sum_call, *parts)
         return mid, self.turn(send, 0)
 
-    def scatter_last(self, run, plan, parts):
-        return run(last_sum_call, *parts, plan=plan)
+    def scatter_last(self, run, plan, parts, scale=COST_SCALE):
+        return run(last_sum_call, *parts, plan=plan, scale=scale)
 
     def previous(self, kv, slots):
         return lax.ppermute(kv, "ctx", [(0, 1)])
@@ -985,7 +985,7 @@
     def scatter_half(self, run, parts):
         return parts
 
-    def scatter_last(self, run, plan, parts):
+    def scatter_last(self, run, plan, parts, scale=None):
         outs, at = [], 0
         for count, turned in plan:
             v = parts[:, at * 512 : (at + count) * 512]
@@ -1079,11 +1079,11 @@
     cross3 = comm.scatter_cross(run(wgrad_call, meta, g, gb, half=1))
     far = (1, 2, 4, 5)
     out1, out3 = run(out_call, ob, gb, [g1[k] for k in far], [g3[k] for k in far])
+    pipe.cross()
+    pipe.send(after(out1, *pipe.sums))
     du, bin_sum = run(dhid_call, g, g3, dg)
     pipe.cross()
-    pipe.send(after(out1, *pipe.sums))
     state3 = comm.scatter_own(run, meta, (g, gb), cross3)
-    pipe.cross()
     dqkv, bqkv_sum = run(join_call, dq, dkv, rv, tabs, nheads)
     pipe.send(out3)
     gain_sums = jnp.zeros((4, d), F32)
@@ -1123,9 +1123,9 @@
         rows_call, body=functools.partial(block_out_kernel, local_len), name="bout", specs=("row", "vec") + ("part",) * 8
     )
     block_output = run(out_half, *out_ops, steps=(0, 2))
-    (grad_in,) = comm.scatter_last(run, ((ff, False),), state2)
-    block_output = run(out_half, *out_ops, steps=(2, 4), into=block_output).reshape(slots, local_len, d)
+    block_output = run(out_half, *out_ops, steps=(2, 4), into=block_output, scale=0.01).reshape(slots, local_len, d)
     pipe.send()
+    (grad_in,) = comm.scatter_last(run, ((ff, False),), state2, 0.01)
     add = comm.small_sum(run, after(small, pipe.sent[5], pipe.here[-1], *jax.tree.leaves(state1)[-1:]), 2)
     state1 = comm.scatter_half(run, state1)
     small = add()

time: 505 us -> 496 us (0.982)
    ppermute x11, waiting for transfers between devices: 10.7 us -> 5.11 us  [send(): got = lax.ppermute(v, 'tensor', pairs)]
  transfers between devices with their start and end apart: 53 -> 53, of which waited for: 11 -> 11; matrix products, arithmetic and copies ran while one was open for 12% -> 13% of each run, Pallas kernels for 52% -> 53%
where the time goes in v8:
time: 496 us; the launch traced here: 488 us
  Pallas kernels  261 us (53%)
  starting transfers between devices  79.7 us (16%)
  waiting for transfers between devices  76.9 us (16%)
  other arithmetic  57.8 us (12%)
  local copies, waits for them, and re-layouts  12 us (2%)
    pallas_call x6, Pallas kernels, wgrad_call(): pl.pallas_call(functools.partial(wgrad_kernel, counts, add is not None, s...  59.7 us
    ppermute x7, waiting for transfers between devices, x(): return lax.ppermute(v, 'dp', [(0, 2), (2, 0), (1, 3), (3, 1)])  44 us
    pallas_call x2, Pallas kernels, back_call(): pl.pallas_call(back_kernel, name='backn', grid_spec=pltpu.PrefetchScalarG...  32.5 us
    convert_element_type x11, other arithmetic, add_bf(): return lax.optimization_barrier((a.astype(F32) + b.astype(F32)).astype(BF))  29 us
    ppermute x11, starting transfers between devices, send(): got = lax.ppermute(v, 'tensor', pairs)  26.1 us
    ppermute x6, waiting for transfers between devices, turn(): return lax.ppermute(v, ('dp', 'ctx'), pairs)  24.8 us
    pallas_call x2, Pallas kernels, out_call(): pl.pallas_call(functools.partial(out_kernel, count), name='outp', grid=(4...  22.6 us
    pallas_call x3, Pallas kernels, rows_call(): pl.pallas_call(functools.partial(body, first), name=name, grid_spec=pltpu...  20.8 us
  transfers between devices with their start and end apart: 53, of which 11 were waited for; matrix products, arithmetic and copies ran while one was open for 13% of the time, Pallas kernels for 53%

profile of v8, /device:TPU:0, one launch (start us, length us, event | category | flops | bytes accessed | tf_op | source)
XLA Modules:
  0.0 488.2 jit_solution(4157966673624132233)
XLA Ops:
  4.6 3.0 collective-permute-start
  10.7 2.5 copy.32
  15.4 10.5 %norm.1 = (bf16[1024,2048]{1,0:T(8,128)(2,1)}, bf16[1024,2048]{1,0:T(8,128)(2,1)}, f32[1024,128]{1,0:T(8,128)}, f32[1,2048]{1,0:T(1,128)}) custom-call(s32[13]{0:T(128)} %concatenate.10.meta, bf16[1024,2048]{1,0:T(8,128)(2,1)} %bitcast.23, bf16[1024,2048]{1,0:T(8,128)(2,1)} %bitcast.38, f32[1,2048]{1,0:T(1,128)} %bitcast.43, f32[1,2048]{1,0:T(1,128)} %bitcast.40), custom_call_target="tpu_custom_call" | custom-call | flops 629145600000 | bytes 2097152000 | tf_op jit(solution)/shard_map/norm/pallas_call | solution.py:127
  29.0 2.9 collective-permute-done.refs_1_
  34.0 3.8 pack.3.w0.refs_0_.w10
  38.3 18.3 %collective-permute-done.3.w2.refs_1_.w12 = bf16[256,2048]{1,0:T(8,128)(2,1)} collective-permute-done((bf16[256,2048]{1,0:T(8,128)(2,1)}, bf16[256,2048]{1,0:T(8,128)(2,1)}, u32[]{:S(2)}, u32[]{:S(2)}) %collective-permute-start.3) | collective-permute-done | bytes 1048608 | tf_op jit(solution)/shard_map/ppermute | solution.py:866
  56.6 3.8 pack.4.w0.w20
  63.8 9.8 %kv.1.kv_ref = bf16[1024,1024]{1,0:T(8,128)(2,1)} custom-call(bf16[1024,2048]{1,0:T(8,128)(2,1)} %get-tuple-element.125.h1.refs_0_, bf16[512,2048]{1,0:T(8,128)(2,1)} %pack.3.w0.refs_0_.w10, bf16[256,2048]{1,0:T(8,128)(2,1)} %collective-permute-done.2.w1.refs_0_.w11, bf16[256,2048]{1,0:T(8,128)(2,1)} %collective-permute-done.3.w2.refs_1_.w12, ...), custom_call_target="tpu_custom_call" | custom-call | flops 429496729600 | bytes 1048576000 | tf_op jit(solution)/shard_map/kv/pallas_call | solution.py:183
  73.5 3.9 collective-permute-start.13
  77.5 8.9 %collective-permute-done.7.w1.w21 = bf16[256,2048]{1,0:T(8,128)(2,1)} collective-permute-done((bf16[256,2048]{1,0:T(8,128)(2,1)}, bf16[256,2048]{1,0:T(8,128)(2,1)}, u32[]{:S(2)}, u32[]{:S(2)}) %collective-permute-start.7) | collective-permute-done | bytes 1048608 | tf_op jit(solution)/shard_map/ppermute | solution.py:866
  87.9 10.8 %qd.1 = (bf16[1024,512]{1,0:T(8,128)(2,1)}, bf16[1024,512]{1,0:T(8,128)(2,1)}) custom-call(bf16[1024,2048]{1,0:T(8,128)(2,1)} %get-tuple-element.125.h1.refs_0_, bf16[1024,2048]{1,0:T(8,128)(2,1)} %get-tuple-element.153.g.refs_0_.refs_2_, bf16[512,2048]{1,0:T(8,128)(2,1)} %pack.3.w0.refs_0_.w10, bf16[256,2048]{1,0:T(8,128)(2,1)} %collective-permute-done.2.w1.refs_0_.w11, ...), custom_call_target="tpu_custom_call" | custom-call | flops 440401920000 | bytes 1468006400 | tf_op jit(solution)/shard_map/qd/pallas_call | solution.py:224
  98.7 12.3 %collective-permute-done.8.w2.w22 = bf16[256,2048]{1,0:T(8,128)(2,1)} collective-permute-done((bf16[256,2048]{1,0:T(8,128)(2,1)}, bf16[256,2048]{1,0:T(8,128)(2,1)}, u32[]{:S(2)}, u32[]{:S(2)}) %collective-permute-start.8) | collective-permute-done | bytes 1048608 | tf_op jit(solution)/shard_map/ppermute | solution.py:866
  111.0 6.7 %norm2.1.h2.refs_0_ = bf16[1024,2048]{1,0:T(8,128)(2,1)} custom-call(s32[13]{0:T(128)} %concatenate.10.meta, bf16[1024,2048]{1,0:T(8,128)(2,1)} %bitcast.24, f32[1024,128]{1,0:T(8,128)} %get-tuple-element.129.st_ref, f32[1,2048]{1,0:T(1,128)} %bitcast.46, f32[1,2048]{1,0:T(1,128)} %bitcast.41), custom_call_target="tpu_custom_call" | custom-call | flops 251658240000 | bytes 838860800 | tf_op jit(solution)/shard_map/norm2/pallas_call | solution.py:107
  119.2 16.5 %hidden.1 = (bf16[1024,2048]{1,0:T(8,128)(2,1)}, bf16[1024,2048]{1,0:T(8,128)(2,1)}) custom-call(bf16[1024,2048]{1,0:T(8,128)(2,1)} %norm2.1.h2.refs_0_, bf16[512,2048]{1,0:T(8,128)(2,1)} %pack.4.w0.w20, bf16[256,2048]{1,0:T(8,128)(2,1)} %collective-permute-done.7.w1.w21, bf16[256,2048]{1,0:T(8,128)(2,1)} %collective-permute-done.8.w2.w22, ...), custom_call_target="tpu_custom_call" | custom-call | flops 858993459200 | bytes 2097152000 | tf_op jit(solution)/shard_map/hidden/pallas_call | solution.py:413
  135.7 3.8 pack.5.refs_2_.w0
  139.8 3.8 collective-permute-done.15.refs_4_.w1
  145.1 12.5 %attn.1 = (bf16[1024,512]{1,0:T(8,128)(2,1)}, bf16[1024,512]{1,0:T(8,128)(2,1)}, f32[1024,1024]{1,0:T(8,128)}, bf16[1024,1024]{1,0:T(8,128)(2,1)}) custom-call(s32[13]{0:T(128)} %concatenate.10.meta, bf16[1024,512]{1,0:T(8,128)(2,1)} %get-tuple-element.127.q_ref, bf16[1024,1024]{1,0:T(8,128)(2,1)} %kv.1.kv_ref, ...), custom_call_target="tpu_custom_call" | custom-call | flops 644245094400 | bytes 1048576000 | tf_op jit(solution)/shard_map/attn/pallas_call | solution.py:333
  159.0 10.9 %outp.2 = (bf16[1024,512]{1,0:T(8,128)(2,1)}, bf16[1024,512]{1,0:T(8,128)(2,1)}) custom-call(bf16[1024,512]{1,0:T(8,128)(2,1)} %get-tuple-element.143.ob.refs_3_, bf16[1024,2048]{1,0:T(8,128)(2,1)} %get-tuple-element.135.gb.refs_1_, bf16[512,2048]{1,0:T(8,128)(2,1)} %pack.3.w0.refs_0_.w10, bf16[512,2048]{1,0:T(8,128)(2,1)} %copy-done.10, ...), custom_call_target="tpu_custom_call" | custom-call | flops 53687092 | bytes 125829 | tf_op jit(solution)/shard_map/outp/pallas_call | solution.py:479
  169.9 4.9 %collective-permute-start.19 = (bf16[1024,512]{1,0:T(8,128)(2,1)}, bf16[1024,512]{1,0:T(8,128)(2,1)}, u32[]{:S(2)}, u32[]{:S(2)}) collective-permute-start(bf16[1024,512]{1,0:T(8,128)(2,1)} %get-tuple-element.149), channel_id=1, source_target_pairs={{0,1},{3,2},{4,5},{7,6},{8,9},{11,10},{12,13},{15,14},{16,17},{19,... | collective-permute-start | bytes 3145736 | tf_op jit(solution)/shard_map/ppermute | solution.py:837
  175.1 9.2 %wgrad.6 = bf16[1024,2048]{1,0:T(8,128)(2,1)} custom-call(s32[13]{0:T(128)} %concatenate.10.meta, bf16[1024,2048]{1,0:T(8,128)(2,1)} %get-tuple-element.153.g.refs_0_.refs_2_, bf16[1024,2048]{1,0:T(8,128)(2,1)} %get-tuple-element.135.gb.refs_1_), custom_call_target="tpu_custom_call" | custom-call | flops 440401920000 | bytes 1468006400 | tf_op jit(solution)/shard_map/wgrad/pallas_call | solution.py:602
  184.6 2.3 collective-permute-start.20
  186.9 11.7 %outp.3 = (bf16[1024,512]{1,0:T(8,128)(2,1)}, bf16[1024,512]{1,0:T(8,128)(2,1)}) custom-call(bf16[1024,512]{1,0:T(8,128)(2,1)} %get-tuple-element.143.ob.refs_3_, bf16[1024,2048]{1,0:T(8,128)(2,1)} %get-tuple-element.135.gb.refs_1_, bf16[256,2048]{1,0:T(8,128)(2,1)} %collective-permute-done.2.w1.refs_0_.w11, ...), custom_call_target="tpu_custom_call" | custom-call | flops 536870912000 | bytes 1258291200 | tf_op jit(solution)/shard_map/outp/pallas_call | solution.py:479
  198.6 2.5 add_convert_fusion.15
  202.8 15.1 %dhid.1 = (bf16[1024,2048]{1,0:T(8,128)(2,1)}, f32[1,2048]{1,0:T(1,128)}) custom-call(bf16[1024,2048]{1,0:T(8,128)(2,1)} %get-tuple-element.153.g.refs_0_.refs_2_, bf16[512,2048]{1,0:T(8,128)(2,1)} %pack.5.refs_2_.w0, bf16[256,2048]{1,0:T(8,128)(2,1)} %collective-permute-done.15.refs_4_.w1, bf16[256,2048]{1,0:T(8,128)(2,1)} %collective-permute-done.16.refs_5_.w2, ...), custom_call_target="tpu_custom_call" | custom-call | flops 858993459200 | bytes 2097152000 | tf_op jit(solution)/shard_map/dhid/pallas_call | solution.py:438
  219.2 2.8 add_convert_fusion.14
  223.6 7.3 %collective-permute-start.24 = (bf16[1024,512]{1,0:T(8,128)(2,1)}, bf16[1024,512]{1,0:T(8,128)(2,1)}, u32[]{:S(2)}, u32[]{:S(2)}) collective-permute-start(bf16[1024,512]{1,0:T(8,128)(2,1)} %get-tuple-element.165), channel_id=1, source_target_pairs={{0,1},{3,2},{4,5},{7,6},{8,9},{11,10},{12,13},{15,14},{16,17},{19,... | collective-permute-start | bytes 3145736 | tf_op jit(solution)/shard_map/ppermute | solution.py:837
  231.0 10.1 %wgrad.7 = (bf16[512,2048]{1,0:T(8,128)(2,1)}, bf16[512,2048]{1,0:T(8,128)(2,1)}) custom-call(s32[13]{0:T(128)} %concatenate.10.meta, bf16[1024,2048]{1,0:T(8,128)(2,1)} %get-tuple-element.153.g.refs_0_.refs_2_, bf16[1024,2048]{1,0:T(8,128)(2,1)} %get-tuple-element.135.gb.refs_1_, bf16[1024,2048]{1,0:T(8,128)(2,1)} %collective-permute-done.21.refs_2_), custom_call_target="tpu_custom_call" | custom-call | flops 440401920000 | bytes 1468006400 | tf_op jit(solution)/shard_map/wgrad/pallas_call | solution.py:602
  241.0 6.0 %join.1 = (bf16[1024,1536]{1,0:T(8,128)(2,1)}, f32[1,1536]{1,0:T(1,128)}) custom-call(bf16[1024,512]{1,0:T(8,128)(2,1)} %get-tuple-element.159.dq_ref, f32[1024,1024]{1,0:T(8,128)} %get-tuple-element.160.dkv_ref, bf16[1024,1024]{1,0:T(8,128)(2,1)} %collective-permute-done.22.rv_ref, f32[512,128]{1,0:T(8,128)} %get-tuple-element.232.cosf, ...), custom_call_target="tpu_custom_call" | custom-call | flops 377487360000 | bytes 1258291200 | tf_op jit(solution)/shard_map/join/pallas_call | solution.py:388
  247.1 2.9 fusion.refs_0_
  250.0 3.8 collective-permute-done.24
  253.7 2.8 add_convert_fusion.12
  259.3 16.2 %backn.2 = (bf16[1024,512]{1,0:T(8,128)(2,1)}, bf16[1024,512]{1,0:T(8,128)(2,1)}, f32[4,2048]{1,0:T(4,128)}) custom-call(s32[13]{0:T(128)} %concatenate.10.meta, bf16[1024,1536]{1,0:T(8,128)(2,1)} %get-tuple-element.162.dqkv.refs_1_, bf16[1024,2048]{1,0:T(8,128)(2,1)} %get-tuple-element.155.du.refs_1_, ...), custom_call_target="tpu_custom_call", output_to_operand_aliasing={{2}: (13, {})} | custom-call | flops 751619276800 | bytes 1887436800 | tf_op jit(solution)/shard_map/backn/pallas_call | solution.py:523
  275.5 3.3 fusion.1.refs_4_
  278.8 3.0 collective-permute-start.29
  282.4 2.5 add_convert_fusion.10
  286.7 2.9 fusion.2.refs_2_
  291.5 4.4 hsum.3
  295.9 9.4 %collective-permute-start.30 = (bf16[256,2048]{1,0:T(8,128)(2,1)}, bf16[256,2048]{1,0:T(8,128)(2,1)}, u32[]{:S(2)}, u32[]{:S(2)}) collective-permute-start(bf16[256,2048]{1,0:T(8,128)(2,1)} %get-tuple-element.183), channel_id=1, source_target_pairs={{0,4},{4,0},{8,24},{12,28},{16,20},{20,16},{24,8},{28,12},{1,5},{5... | collective-permute-start | bytes 3145736 | tf_op jit(solution)/shard_map/ppermute | solution.py:912
  305.3 16.3 %backn.3 = (bf16[1024,512]{1,0:T(8,128)(2,1)}, bf16[1024,512]{1,0:T(8,128)(2,1)}, f32[4,2048]{1,0:T(4,128)}) custom-call(s32[13]{0:T(128)} %concatenate.10.meta, bf16[1024,1536]{1,0:T(8,128)(2,1)} %get-tuple-element.162.dqkv.refs_1_, bf16[1024,2048]{1,0:T(8,128)(2,1)} %get-tuple-element.155.du.refs_1_, ...), custom_call_target="tpu_custom_call", output_to_operand_aliasing={{2}: (13, {})} | custom-call | flops 751619276800 | bytes 1887436800 | tf_op jit(solution)/shard_map/backn/pallas_call | solution.py:523
  321.6 2.6 add_convert_fusion.8
  326.0 2.9 fusion.3.refs_6_
  331.6 9.2 %wgrad.8 = bf16[1024,2048]{1,0:T(8,128)(2,1)} custom-call(s32[13]{0:T(128)} %concatenate.10.meta, bf16[1024,2048]{1,0:T(8,128)(2,1)} %norm2.1.h2.refs_0_, bf16[1024,2048]{1,0:T(8,128)(2,1)} %get-tuple-element.155.du.refs_1_), custom_call_target="tpu_custom_call" | custom-call | flops 440401920000 | bytes 1468006400 | tf_op jit(solution)/shard_map/wgrad/pallas_call | solution.py:602
  343.9 10.2 %wgrad.9 = bf16[1024,2048]{1,0:T(8,128)(2,1)} custom-call(s32[13]{0:T(128)} %concatenate.10.meta, bf16[1024,2048]{1,0:T(8,128)(2,1)} %get-tuple-element.125.h1.refs_0_, bf16[1024,1536]{1,0:T(8,128)(2,1)} %get-tuple-element.162.dqkv.refs_1_, bf16[1024,2048]{1,0:T(8,128)(2,1)} %get-tuple-element.153.g.refs_0_.refs_2_, ...), custom_call_target="tpu_custom_call" | custom-call | flops 503316480000 | bytes 1677721600 | tf_op jit(solution)/shard_map/wgrad/pallas_call | solution.py:602
  355.7 2.5 add_convert_fusion.6
  360.1 2.9 fusion.4.refs_0_
  364.0 10.0 %wgrad.10 = (bf16[512,2048]{1,0:T(8,128)(2,1)}, bf16[512,2048]{1,0:T(8,128)(2,1)}) custom-call(s32[13]{0:T(128)} %concatenate.10.meta, bf16[1024,2048]{1,0:T(8,128)(2,1)} %norm2.1.h2.refs_0_, bf16[1024,2048]{1,0:T(8,128)(2,1)} %get-tuple-element.155.du.refs_1_, bf16[1024,2048]{1,0:T(8,128)(2,1)} %collective-permute-done.36.refs_2_), custom_call_target="tpu_custom_call" | custom-call | flops 440401920000 | bytes 1468006400 | tf_op jit(solution)/shard_map/wgrad/pallas_call | solution.py:602
  373.9 4.4 lsum.3
  378.3 2.5 add_convert_fusion.4
  382.5 2.8 add_convert_fusion.3.refs_2_
  387.1 11.0 %wgrad.11 = (bf16[512,2048]{1,0:T(8,128)(2,1)}, bf16[512,2048]{1,0:T(8,128)(2,1)}) custom-call(s32[13]{0:T(128)} %concatenate.10.meta, bf16[1024,2048]{1,0:T(8,128)(2,1)} %get-tuple-element.125.h1.refs_0_, bf16[1024,1536]{1,0:T(8,128)(2,1)} %get-tuple-element.162.dqkv.refs_1_, bf16[1024,2048]{1,0:T(8,128)(2,1)} %get-tuple-element.153.g.refs_0_.refs_2_, ...), custom_call_target="tpu_custom_call" | custom-call | flops 503316480000 | bytes 1677721600 | tf_op jit(solution)/shard_map/wgrad/pallas_call | solution.py:602
  398.1 2.5 add_convert_fusion.2
  402.2 2.8 add_convert_fusion.1.refs_4_
  406.4 6.7 %collective-permute-done.42.got = bf16[512,2048]{1,0:T(8,128)(2,1)} collective-permute-done((bf16[512,2048]{1,0:T(8,128)(2,1)}, bf16[512,2048]{1,0:T(8,128)(2,1)}, u32[]{:S(2)}, u32[]{:S(2)}) %collective-permute-start.42) | collective-permute-done | bytes 2097184 | tf_op jit(solution)/shard_map/ppermute | solution.py:912
  413.0 4.4 hsum.4
  417.9 4.8 bout.2.refs_8_
  422.7 4.9 bout.3
  427.5 2.8 add_convert_fusion.refs_6_
  431.6 12.1 %collective-permute-done.46.got = bf16[256,2048]{1,0:T(8,128)(2,1)} collective-permute-done((bf16[256,2048]{1,0:T(8,128)(2,1)}, bf16[256,2048]{1,0:T(8,128)(2,1)}, u32[]{:S(2)}, u32[]{:S(2)}) %collective-permute-start.46) | collective-permute-done | bytes 1048608 | tf_op jit(solution)/shard_map/ppermute | solution.py:912
  443.8 4.0 lsum.4
  447.7 5.9 %collective-permute-done.45.got = bf16[512,2048]{1,0:T(8,128)(2,1)} collective-permute-done((bf16[512,2048]{1,0:T(8,128)(2,1)}, bf16[512,2048]{1,0:T(8,128)(2,1)}, u32[]{:S(2)}, u32[]{:S(2)}) %collective-permute-start.45) | collective-permute-done | bytes 2097184 | tf_op jit(solution)/shard_map/ppermute | solution.py:912
  454.0 4.5 hsum.5
  462.3 3.4 collective-permute-start.50
  465.7 11.1 %igrad.1 = bf16[1024,2048]{1,0:T(8,128)(2,1)} custom-call(s32[13]{0:T(128)} %concatenate.10.meta, bf16[1024,2048]{1,0:T(8,128)(2,1)} %bitcast.29, bf16[1024,2048]{1,0:T(8,128)(2,1)} %bitcast.39, f32[1024,128]{1,0:T(8,128)} %get-tuple-element.129.st_ref, bf16[1024,512]{1,0:T(8,128)(2,1)} %fusion.4.refs_0_, bf16[1024,512]{1,0:T(8,128)(2,1)} %collective-permute-done.40.refs_1_, ...), custom_call_target="tpu_custom_call" | custom-call | flops 503316480000 | bytes 1677721600 | tf_op jit(solution)/shard_map/igrad/pallas_call | solution.py:775
  481.7 4.3 lsum.5
  (164 shorter events, 67.7 us)
Async XLA Ops:
  0.6 8.4 %copy-start.9 = (f32[256,2048]{1,0:T(8,128)S(1)}, f32[256,2048]{1,0:T(8,128)}, u32[]{:S(2)}) copy-start(f32[256,2048]{1,0:T(8,128)} %param.26) | copy-start | bytes 6291460
  4.6 27.3 %collective-permute-start = (bf16[256,2048]{1,0:T(8,128)(2,1)}, bf16[256,2048]{1,0:T(8,128)(2,1)}, u32[]{:S(2)}, u32[]{:S(2)}) collective-permute-start(bf16[256,2048]{1,0:T(8,128)(2,1)} %pad_maximum_fusion.refs_0_), channel_id=1, source_target_pairs={{0,4},{4,0},{1,5},{5,1},{2,6},{6,2},{3,7},{7,3},{8,12},{12,8},{9,1... | collective-permute-start | bytes 3145736 | tf_op jit(solution)/shard_map/ppermute | solution.py:872
  7.6 24.9 %collective-permute-start.2 = (bf16[256,2048]{1,0:T(8,128)(2,1)}, bf16[256,2048]{1,0:T(8,128)(2,1)}, u32[]{:S(2)}, u32[]{:S(2)}) collective-permute-start(bf16[256,2048]{1,0:T(8,128)(2,1)} %pad_maximum_fusion.refs_0_), channel_id=1, source_target_pairs={{0,16},{16,0},{8,24},{24,8},{1,17},{17,1},{9,25},{25,9},{2,18},{18... | collective-permute-start | bytes 3145736 | tf_op jit(solution)/shard_map/ppermute | solution.py:866
  10.2 46.4 %collective-permute-start.1 = (bf16[256,2048]{1,0:T(8,128)(2,1)}, bf16[256,2048]{1,0:T(8,128)(2,1)}, u32[]{:S(2)}, u32[]{:S(2)}) collective-permute-start(bf16[256,2048]{1,0:T(8,128)(2,1)} %convert_element_type.174.refs_0_), channel_id=1, source_target_pairs={{0,4},{4,0},{1,5},{5,1},{2,6},{6,2},{3,7},{7,3},{8,12},{12,8},{9,1... | collective-permute-start | bytes 3145736 | tf_op jit(solution)/shard_map/ppermute | solution.py:872
  13.3 122.4 %collective-permute-start.12 = (bf16[256,2048]{1,0:T(8,128)(2,1)}, bf16[256,2048]{1,0:T(8,128)(2,1)}, u32[]{:S(2)}, u32[]{:S(2)}) collective-permute-start(bf16[256,2048]{1,0:T(8,128)(2,1)} %bitcast.21.refs_0_), channel_id=1, source_target_pairs={{0,4},{4,0},{1,5},{5,1},{2,6},{6,2},{3,7},{7,3},{8,12},{12,8},{9,1... | collective-permute-start | bytes 3145736 | tf_op jit(solution)/shard_map/ppermute | solution.py:872
  15.4 10.5 %copy-start.20 = (f32[1536]{0:T(1024)S(1)}, f32[1536]{0:T(1024)}, u32[]{:S(2)}) copy-start(f32[1536]{0:T(1024)} %param.23) | copy-start | bytes 18436
  15.4 11.1 %copy-start.18 = (f32[2048]{0:T(1024)S(1)}, f32[2048]{0:T(1024)}, u32[]{:S(2)}) copy-start(f32[2048]{0:T(1024)} %param.25) | copy-start | bytes 24580
  15.4 11.1 %copy-start.19 = (f32[2048]{0:T(1024)S(1)}, f32[2048]{0:T(1024)}, u32[]{:S(2)}) copy-start(f32[2048]{0:T(1024)} %param.29) | copy-start | bytes 24580
  32.5 24.1 %collective-permute-start.3 = (bf16[256,2048]{1,0:T(8,128)(2,1)}, bf16[256,2048]{1,0:T(8,128)(2,1)}, u32[]{:S(2)}, u32[]{:S(2)}) collective-permute-start(bf16[256,2048]{1,0:T(8,128)(2,1)} %collective-permute-done.refs_1_), channel_id=1, source_target_pairs={{0,16},{16,0},{8,24},{24,8},{1,17},{17,1},{9,25},{25,9},{2,18},{18... | collective-permute-start | bytes 3145736 | tf_op jit(solution)/shard_map/ppermute | solution.py:866
  37.8 24.7 %collective-permute-start.4 = (bf16[512,2048]{1,0:T(8,128)(2,1)}, bf16[512,2048]{1,0:T(8,128)(2,1)S(1)}, u32[]{:S(2)}, u32[]{:S(2)}) collective-permute-start(bf16[512,2048]{1,0:T(8,128)(2,1)} %pack.3.w0.refs_0_.w10), channel_id=1, source_target_pairs={{0,8},{8,0},{16,24},{24,16},{1,9},{9,1},{17,25},{25,17},{2,10},{10... | collective-permute-start | bytes 6291464 | tf_op jit(solution)/shard_map/ppermute | solution.py:869
  37.8 23.2 %collective-permute-start.5 = (bf16[256,2048]{1,0:T(8,128)(2,1)}, bf16[256,2048]{1,0:T(8,128)(2,1)S(1)}, u32[]{:S(2)}, u32[]{:S(2)}) collective-permute-start(bf16[256,2048]{1,0:T(8,128)(2,1)} %collective-permute-done.2.w1.refs_0_.w11), channel_id=1, source_target_pairs={{0,8},{8,0},{16,24},{24,16},{1,9},{9,1},{17,25},{25,17},{2,10},{10... | collective-permute-start | bytes 3145736 | tf_op jit(solution)/shard_map/ppermute | solution.py:869
  56.6 5.8 %collective-permute-start.6 = (bf16[256,2048]{1,0:T(8,128)(2,1)}, bf16[256,2048]{1,0:T(8,128)(2,1)}, u32[]{:S(2)}, u32[]{:S(2)}) collective-permute-start(bf16[256,2048]{1,0:T(8,128)(2,1)} %collective-permute-done.3.w2.refs_1_.w12), channel_id=1, source_target_pairs={{0,8},{8,0},{16,24},{24,16},{1,9},{9,1},{17,25},{25,17},{2,10},{10... | collective-permute-start | bytes 3145736 | tf_op jit(solution)/shard_map/ppermute | solution.py:869
  60.4 57.3 %collective-permute-start.9 = (bf16[512,2048]{1,0:T(8,128)(2,1)}, bf16[512,2048]{1,0:T(8,128)(2,1)}, u32[]{:S(2)}, u32[]{:S(2)}) collective-permute-start(bf16[512,2048]{1,0:T(8,128)(2,1)} %pack.4.w0.w20), channel_id=1, source_target_pairs={{0,8},{8,0},{16,24},{24,16},{1,9},{9,1},{17,25},{25,17},{2,10},{10... | collective-permute-start | bytes 6291464 | tf_op jit(solution)/shard_map/ppermute | solution.py:869
  61.0 25.5 %collective-permute-start.7 = (bf16[256,2048]{1,0:T(8,128)(2,1)}, bf16[256,2048]{1,0:T(8,128)(2,1)}, u32[]{:S(2)}, u32[]{:S(2)}) collective-permute-start(bf16[256,2048]{1,0:T(8,128)(2,1)} %convert_element_type.174.refs_0_), channel_id=1, source_target_pairs={{0,16},{16,0},{8,24},{24,8},{1,17},{17,1},{9,25},{25,9},{2,18},{18... | collective-permute-start | bytes 3145736 | tf_op jit(solution)/shard_map/ppermute | solution.py:866
  73.5 71.5 %collective-permute-start.13 = (bf16[1024,1024]{1,0:T(8,128)(2,1)}, bf16[1024,1024]{1,0:T(8,128)(2,1)}, u32[]{:S(2)}, u32[]{:S(2)}) collective-permute-start(bf16[1024,1024]{1,0:T(8,128)(2,1)} %kv.1.kv_ref), channel_id=1, source_target_pairs={{0,4},{1,5},{2,6},{3,7},{8,12},{9,13},{10,14},{11,15},{16,20},{17,... | collective-permute-start | bytes 6291464 | tf_op jit(solution)/shard_map/ppermute | solution.py:929
  86.4 24.6 %collective-permute-start.8 = (bf16[256,2048]{1,0:T(8,128)(2,1)}, bf16[256,2048]{1,0:T(8,128)(2,1)}, u32[]{:S(2)}, u32[]{:S(2)}) collective-permute-start(bf16[256,2048]{1,0:T(8,128)(2,1)} %collective-permute-done.1.refs_1_), channel_id=1, source_target_pairs={{0,16},{16,0},{8,24},{24,8},{1,17},{17,1},{9,25},{25,9},{2,18},{18... | collective-permute-start | bytes 3145736 | tf_op jit(solution)/shard_map/ppermute | solution.py:866
  87.9 31.3 %collective-permute-start.10 = (bf16[256,2048]{1,0:T(8,128)(2,1)}, bf16[256,2048]{1,0:T(8,128)(2,1)}, u32[]{:S(2)}, u32[]{:S(2)}) collective-permute-start(bf16[256,2048]{1,0:T(8,128)(2,1)} %collective-permute-done.7.w1.w21), channel_id=1, source_target_pairs={{0,8},{8,0},{16,24},{24,16},{1,9},{9,1},{17,25},{25,17},{2,10},{10... | collective-permute-start | bytes 3145736 | tf_op jit(solution)/shard_map/ppermute | solution.py:869
  111.0 8.2 %collective-permute-start.11 = (bf16[256,2048]{1,0:T(8,128)(2,1)}, bf16[256,2048]{1,0:T(8,128)(2,1)}, u32[]{:S(2)}, u32[]{:S(2)}) collective-permute-start(bf16[256,2048]{1,0:T(8,128)(2,1)} %collective-permute-done.8.w2.w22), channel_id=1, source_target_pairs={{0,8},{8,0},{16,24},{24,16},{1,9},{9,1},{17,25},{25,17},{2,10},{10... | collective-permute-start | bytes 3145736 | tf_op jit(solution)/shard_map/ppermute | solution.py:869
  117.7 25.9 %collective-permute-start.15 = (bf16[256,2048]{1,0:T(8,128)(2,1)}, bf16[256,2048]{1,0:T(8,128)(2,1)}, u32[]{:S(2)}, u32[]{:S(2)}) collective-permute-start(bf16[256,2048]{1,0:T(8,128)(2,1)} %bitcast.21.refs_0_), channel_id=1, source_target_pairs={{0,16},{16,0},{8,24},{24,8},{1,17},{17,1},{9,25},{25,9},{2,18},{18... | collective-permute-start | bytes 3145736 | tf_op jit(solution)/shard_map/ppermute | solution.py:866
  139.5 19.4 %collective-permute-start.14 = (bf16[512,2048]{1,0:T(8,128)(2,1)}, bf16[512,2048]{1,0:T(8,128)(2,1)}, u32[]{:S(2)}, u32[]{:S(2)}) collective-permute-start(bf16[512,2048]{1,0:T(8,128)(2,1)} %pack.5.refs_2_.w0), channel_id=1, source_target_pairs={{0,8},{8,0},{16,24},{24,16},{1,9},{9,1},{17,25},{25,17},{2,10},{10... | collective-permute-start | bytes 6291464 | tf_op jit(solution)/shard_map/ppermute | solution.py:869
  143.6 31.2 %collective-permute-start.16 = (bf16[256,2048]{1,0:T(8,128)(2,1)}, bf16[256,2048]{1,0:T(8,128)(2,1)}, u32[]{:S(2)}, u32[]{:S(2)}) collective-permute-start(bf16[256,2048]{1,0:T(8,128)(2,1)} %collective-permute-done.12.refs_1_), channel_id=1, source_target_pairs={{0,16},{16,0},{8,24},{24,8},{1,17},{17,1},{9,25},{25,9},{2,18},{18... | collective-permute-start | bytes 3145736 | tf_op jit(solution)/shard_map/ppermute | solution.py:866
  157.6 27.0 %collective-permute-start.17 = (bf16[256,2048]{1,0:T(8,128)(2,1)}, bf16[256,2048]{1,0:T(8,128)(2,1)}, u32[]{:S(2)}, u32[]{:S(2)}) collective-permute-start(bf16[256,2048]{1,0:T(8,128)(2,1)} %collective-permute-done.15.refs_4_.w1), channel_id=1, source_target_pairs={{0,8},{8,0},{16,24},{24,16},{1,9},{9,1},{17,25},{25,17},{2,10},{10... | collective-permute-start | bytes 3145736 | tf_op jit(solution)/shard_map/ppermute | solution.py:869
  157.6 83.4 %collective-permute-start.22 = (bf16[1024,1024]{1,0:T(8,128)(2,1)}, bf16[1024,1024]{1,0:T(8,128)(2,1)}, u32[]{:S(2)}, u32[]{:S(2)}) collective-permute-start(bf16[1024,1024]{1,0:T(8,128)(2,1)} %get-tuple-element.161), channel_id=1, source_target_pairs={{4,0},{5,1},{6,2},{7,3},{12,8},{13,9},{14,10},{15,11},{20,16},{21,... | collective-permute-start | bytes 6291464 | tf_op jit(solution)/shard_map/ppermute | solution.py:932
  169.9 28.7 %collective-permute-start.19 = (bf16[1024,512]{1,0:T(8,128)(2,1)}, bf16[1024,512]{1,0:T(8,128)(2,1)}, u32[]{:S(2)}, u32[]{:S(2)}) collective-permute-start(bf16[1024,512]{1,0:T(8,128)(2,1)} %get-tuple-element.149), channel_id=1, source_target_pairs={{0,1},{3,2},{4,5},{7,6},{8,9},{11,10},{12,13},{15,14},{16,17},{19,... | collective-permute-start | bytes 3145736 | tf_op jit(solution)/shard_map/ppermute | solution.py:837
  174.8 12.0 %collective-permute-start.18 = (bf16[256,2048]{1,0:T(8,128)(2,1)}, bf16[256,2048]{1,0:T(8,128)(2,1)}, u32[]{:S(2)}, u32[]{:S(2)}) collective-permute-start(bf16[256,2048]{1,0:T(8,128)(2,1)} %collective-permute-done.16.refs_5_.w2), channel_id=1, source_target_pairs={{0,8},{8,0},{16,24},{24,16},{1,9},{9,1},{17,25},{25,17},{2,10},{10... | collective-permute-start | bytes 3145736 | tf_op jit(solution)/shard_map/ppermute | solution.py:869
  184.3 46.6 %collective-permute-start.21 = (bf16[1024,2048]{1,0:T(8,128)(2,1)}, bf16[1024,2048]{1,0:T(8,128)(2,1)}, u32[]{:S(2)}, u32[]{:S(2)}) collective-permute-start(bf16[1024,2048]{1,0:T(8,128)(2,1)} %wgrad.6), channel_id=1, source_target_pairs={{0,8},{8,0},{16,24},{24,16},{1,9},{9,1},{17,25},{25,17},{2,10},{10... | collective-permute-start | bytes 12582920 | tf_op jit(solution)/shard_map/ppermute | solution.py:869
  184.6 34.6 %collective-permute-start.20 = (bf16[1024,512]{1,0:T(8,128)(2,1)}, bf16[1024,512]{1,0:T(8,128)(2,1)}, u32[]{:S(2)}, u32[]{:S(2)}) collective-permute-start(bf16[1024,512]{1,0:T(8,128)(2,1)} %get-tuple-element.156), channel_id=1, source_target_pairs={{0,1},{3,2},{4,5},{7,6},{8,9},{11,10},{12,13},{15,14},{16,17},{19,... | collective-permute-start | bytes 3145736 | tf_op jit(solution)/shard_map/ppermute | solution.py:837
  186.9 11.7 %copy-start.11 = (bf16[1024,512]{1,0:T(8,128)(2,1)S(1)}, bf16[1024,512]{1,0:T(8,128)(2,1)}, u32[]{:S(2)}) copy-start(bf16[1024,512]{1,0:T(8,128)(2,1)} %get-tuple-element.149) | copy-start | bytes 3145732
  201.1 46.0 %collective-permute-start.23 = (bf16[1024,512]{1,0:T(8,128)(2,1)}, bf16[1024,512]{1,0:T(8,128)(2,1)}, u32[]{:S(2)}, u32[]{:S(2)}) collective-permute-start(bf16[1024,512]{1,0:T(8,128)(2,1)} %add_convert_fusion.15), channel_id=1, source_target_pairs={{1,2},{2,1},{5,6},{6,5},{9,10},{10,9},{13,14},{14,13},{17,18},{18,... | collective-permute-start | bytes 3145736 | tf_op jit(solution)/shard_map/ppermute | solution.py:847
  222.0 53.5 %collective-permute-start.25 = (bf16[1024,512]{1,0:T(8,128)(2,1)}, bf16[1024,512]{1,0:T(8,128)(2,1)}, u32[]{:S(2)}, u32[]{:S(2)}) collective-permute-start(bf16[1024,512]{1,0:T(8,128)(2,1)} %add_convert_fusion.14), channel_id=1, source_target_pairs={{1,2},{2,1},{5,6},{6,5},{9,10},{10,9},{13,14},{14,13},{17,18},{18,... | collective-permute-start | bytes 3145736 | tf_op jit(solution)/shard_map/ppermute | solution.py:847
  223.6 30.1 %collective-permute-start.24 = (bf16[1024,512]{1,0:T(8,128)(2,1)}, bf16[1024,512]{1,0:T(8,128)(2,1)}, u32[]{:S(2)}, u32[]{:S(2)}) collective-permute-start(bf16[1024,512]{1,0:T(8,128)(2,1)} %get-tuple-element.165), channel_id=1, source_target_pairs={{0,1},{3,2},{4,5},{7,6},{8,9},{11,10},{12,13},{15,14},{16,17},{19,... | collective-permute-start | bytes 3145736 | tf_op jit(solution)/shard_map/ppermute | solution.py:837
  250.0 32.4 %collective-permute-start.26 = (bf16[1024,512]{1,0:T(8,128)(2,1)}, bf16[1024,512]{1,0:T(8,128)(2,1)}, u32[]{:S(2)}, u32[]{:S(2)}) collective-permute-start(bf16[1024,512]{1,0:T(8,128)(2,1)} %fusion.refs_0_), channel_id=1, source_target_pairs={{0,1},{3,2},{1,0},{2,3},{4,5},{7,6},{5,4},{6,7},{8,9},{11,10},{9,8... | collective-permute-start | bytes 3145736 | tf_op jit(solution)/shard_map/ppermute | solution.py:837
  256.5 30.2 %collective-permute-start.27 = (bf16[1024,512]{1,0:T(8,128)(2,1)}, bf16[1024,512]{1,0:T(8,128)(2,1)}, u32[]{:S(2)}, u32[]{:S(2)}) collective-permute-start(bf16[1024,512]{1,0:T(8,128)(2,1)} %add_convert_fusion.12), channel_id=1, source_target_pairs={{1,2},{2,1},{5,6},{6,5},{9,10},{10,9},{13,14},{14,13},{17,18},{18,... | collective-permute-start | bytes 3145736 | tf_op jit(solution)/shard_map/ppermute | solution.py:847
  258.1 33.4 %collective-permute-start.28 = (bf16[512,2048]{1,0:T(8,128)(2,1)}, bf16[512,2048]{1,0:T(8,128)(2,1)}, u32[]{:S(2)}, u32[]{:S(2)}) collective-permute-start(bf16[512,2048]{1,0:T(8,128)(2,1)} %get-tuple-element.173), channel_id=1, source_target_pairs={{0,16},{4,20},{8,12},{12,8},{16,0},{20,4},{24,28},{28,24},{1,17},{... | collective-permute-start | bytes 6291464 | tf_op jit(solution)/shard_map/ppermute | solution.py:912
  275.4 6.3 %copy-start.21 = (f32[1,1536]{1,0:T(1,128)S(1)}, f32[1,1536]{1,0:T(1,128)}, u32[]{:S(2)}) copy-start(f32[1,1536]{1,0:T(1,128)} %get-tuple-element.181) | copy-start | bytes 18436
  275.5 7.0 %copy-start.5 = (bf16[1024,512]{1,0:T(8,128)(2,1)S(1)}, bf16[1024,512]{1,0:T(8,128)(2,1)}, u32[]{:S(2)}) copy-start(bf16[1024,512]{1,0:T(8,128)(2,1)} %get-tuple-element.169) | copy-start | bytes 3145732
  278.8 7.9 %copy-start.2 = (bf16[1024,512]{1,0:T(8,128)(2,1)S(1)}, bf16[1024,512]{1,0:T(8,128)(2,1)}, u32[]{:S(2)}) copy-start(bf16[1024,512]{1,0:T(8,128)(2,1)} %get-tuple-element.190) | copy-start | bytes 3145732
  278.8 42.8 %collective-permute-start.29 = (bf16[1024,512]{1,0:T(8,128)(2,1)}, bf16[1024,512]{1,0:T(8,128)(2,1)}, u32[]{:S(2)}, u32[]{:S(2)}) collective-permute-start(bf16[1024,512]{1,0:T(8,128)(2,1)} %fusion.1.refs_4_), channel_id=1, source_target_pairs={{0,1},{3,2},{1,0},{2,3},{4,5},{7,6},{5,4},{6,7},{8,9},{11,10},{9,8... | collective-permute-start | bytes 3145736 | tf_op jit(solution)/shard_map/ppermute | solution.py:837
  284.9 41.1 %collective-permute-start.31 = (bf16[1024,512]{1,0:T(8,128)(2,1)}, bf16[1024,512]{1,0:T(8,128)(2,1)}, u32[]{:S(2)}, u32[]{:S(2)}) collective-permute-start(bf16[1024,512]{1,0:T(8,128)(2,1)} %add_convert_fusion.10), channel_id=1, source_target_pairs={{1,2},{2,1},{5,6},{6,5},{9,10},{10,9},{13,14},{14,13},{17,18},{18,... | collective-permute-start | bytes 3145736 | tf_op jit(solution)/shard_map/ppermute | solution.py:847
  289.6 66.1 %collective-permute-start.34 = (bf16[1024,512]{1,0:T(8,128)(2,1)}, bf16[1024,512]{1,0:T(8,128)(2,1)}, u32[]{:S(2)}, u32[]{:S(2)}) collective-permute-start(bf16[1024,512]{1,0:T(8,128)(2,1)} %fusion.2.refs_2_), channel_id=1, source_target_pairs={{0,1},{3,2},{1,0},{2,3},{4,5},{7,6},{5,4},{6,7},{8,9},{11,10},{9,8... | collective-permute-start | bytes 3145736 | tf_op jit(solution)/shard_map/ppermute | solution.py:837
  295.9 35.7 %collective-permute-start.30 = (bf16[256,2048]{1,0:T(8,128)(2,1)}, bf16[256,2048]{1,0:T(8,128)(2,1)}, u32[]{:S(2)}, u32[]{:S(2)}) collective-permute-start(bf16[256,2048]{1,0:T(8,128)(2,1)} %get-tuple-element.183), channel_id=1, source_target_pairs={{0,4},{4,0},{8,24},{12,28},{16,20},{20,16},{24,8},{28,12},{1,5},{5... | collective-permute-start | bytes 3145736 | tf_op jit(solution)/shard_map/ppermute | solution.py:912
  305.3 16.3 %copy-start.8 = (bf16[1024,512]{1,0:T(8,128)(2,1)S(1)}, bf16[1024,512]{1,0:T(8,128)(2,1)}, u32[]{:S(2)}) copy-start(bf16[1024,512]{1,0:T(8,128)(2,1)} %get-tuple-element.178) | copy-start | bytes 3145732
  324.2 35.9 %collective-permute-start.35 = (bf16[1024,512]{1,0:T(8,128)(2,1)}, bf16[1024,512]{1,0:T(8,128)(2,1)}, u32[]{:S(2)}, u32[]{:S(2)}) collective-permute-start(bf16[1024,512]{1,0:T(8,128)(2,1)} %add_convert_fusion.8), channel_id=1, source_target_pairs={{1,2},{2,1},{5,6},{6,5},{9,10},{10,9},{13,14},{14,13},{17,18},{18,... | collective-permute-start | bytes 3145736 | tf_op jit(solution)/shard_map/ppermute | solution.py:847
  329.6 11.2 %collective-permute-start.32 = (f32[13824]{0:T(1024)}, f32[13824]{0:T(1024)}, u32[]{:S(2)}, u32[]{:S(2)}) collective-permute-start(f32[13824]{0:T(1024)} %pad_maximum_fusion.1), channel_id=1, source_target_pairs={{0,8},{8,0},{16,24},{24,16},{1,9},{9,1},{17,25},{25,17},{2,10},{10... | collective-permute-start | bytes 165896 | tf_op jit(solution)/shard_map/ppermute | solution.py:869
  329.6 48.7 %collective-permute-start.37 = (bf16[1024,512]{1,0:T(8,128)(2,1)}, bf16[1024,512]{1,0:T(8,128)(2,1)}, u32[]{:S(2)}, u32[]{:S(2)}) collective-permute-start(bf16[1024,512]{1,0:T(8,128)(2,1)} %fusion.3.refs_6_), channel_id=1, source_target_pairs={{0,1},{3,2},{1,0},{2,3},{4,5},{7,6},{5,4},{6,7},{8,9},{11,10},{9,8... | collective-permute-start | bytes 3145736 | tf_op jit(solution)/shard_map/ppermute | solution.py:837
  342.3 11.8 %collective-permute-start.33 = (f32[13824]{0:T(1024)}, f32[13824]{0:T(1024)}, u32[]{:S(2)}, u32[]{:S(2)}) collective-permute-start(f32[13824]{0:T(1024)} %add.111), channel_id=1, source_target_pairs={{0,16},{16,0},{8,24},{24,8},{1,17},{17,1},{9,25},{25,9},{2,18},{18... | collective-permute-start | bytes 165896 | tf_op jit(solution)/shard_map/ppermute | solution.py:866
  343.9 20.1 %collective-permute-start.36 = (bf16[1024,2048]{1,0:T(8,128)(2,1)}, bf16[1024,2048]{1,0:T(8,128)(2,1)}, u32[]{:S(2)}, u32[]{:S(2)}) collective-permute-start(bf16[1024,2048]{1,0:T(8,128)(2,1)} %wgrad.8), channel_id=1, source_target_pairs={{0,8},{8,0},{16,24},{24,16},{1,9},{9,1},{17,25},{25,17},{2,10},{10... | collective-permute-start | bytes 12582920 | tf_op jit(solution)/shard_map/ppermute | solution.py:869
  343.9 11.8 %copy-start.3 = (bf16[1024,512]{1,0:T(8,128)(2,1)S(1)}, bf16[1024,512]{1,0:T(8,128)(2,1)}, u32[]{:S(2)}) copy-start(bf16[1024,512]{1,0:T(8,128)(2,1)} %get-tuple-element.190) | copy-start | bytes 3145732
  358.2 24.3 %collective-permute-start.38 = (bf16[1024,512]{1,0:T(8,128)(2,1)}, bf16[1024,512]{1,0:T(8,128)(2,1)}, u32[]{:S(2)}, u32[]{:S(2)}) collective-permute-start(bf16[1024,512]{1,0:T(8,128)(2,1)} %add_convert_fusion.6), channel_id=1, source_target_pairs={{1,2},{2,1},{5,6},{6,5},{9,10},{10,9},{13,14},{14,13},{17,18},{18,... | collective-permute-start | bytes 3145736 | tf_op jit(solution)/shard_map/ppermute | solution.py:847
  363.0 35.1 %collective-permute-start.40 = (bf16[1024,512]{1,0:T(8,128)(2,1)}, bf16[1024,512]{1,0:T(8,128)(2,1)}, u32[]{:S(2)}, u32[]{:S(2)}) collective-permute-start(bf16[1024,512]{1,0:T(8,128)(2,1)} %fusion.4.refs_0_), channel_id=1, source_target_pairs={{0,1},{3,2},{1,0},{2,3},{4,5},{7,6},{5,4},{6,7},{8,9},{11,10},{9,8... | collective-permute-start | bytes 3145736 | tf_op jit(solution)/shard_map/ppermute | solution.py:837
  373.9 13.2 %collective-permute-start.39 = (bf16[1024,2048]{1,0:T(8,128)(2,1)}, bf16[1024,2048]{1,0:T(8,128)(2,1)}, u32[]{:S(2)}, u32[]{:S(2)}) collective-permute-start(bf16[1024,2048]{1,0:T(8,128)(2,1)} %wgrad.9), channel_id=1, source_target_pairs={{0,8},{8,0},{16,24},{24,16},{1,9},{9,1},{17,25},{25,17},{2,10},{10... | collective-permute-start | bytes 12582920 | tf_op jit(solution)/shard_map/ppermute | solution.py:869
  380.8 21.4 %collective-permute-start.41 = (bf16[1024,512]{1,0:T(8,128)(2,1)}, bf16[1024,512]{1,0:T(8,128)(2,1)}, u32[]{:S(2)}, u32[]{:S(2)}) collective-permute-start(bf16[1024,512]{1,0:T(8,128)(2,1)} %add_convert_fusion.4), channel_id=1, source_target_pairs={{1,2},{2,1},{5,6},{6,5},{9,10},{10,9},{13,14},{14,13},{17,18},{18,... | collective-permute-start | bytes 3145736 | tf_op jit(solution)/shard_map/ppermute | solution.py:847
  385.3 62.4 %collective-permute-start.43 = (bf16[1024,512]{1,0:T(8,128)(2,1)}, bf16[1024,512]{1,0:T(8,128)(2,1)}, u32[]{:S(2)}, u32[]{:S(2)}) collective-permute-start(bf16[1024,512]{1,0:T(8,128)(2,1)} %add_convert_fusion.3.refs_2_), channel_id=1, source_target_pairs={{1,0},{2,3},{5,4},{6,7},{9,8},{10,11},{13,12},{14,15},{17,16},{18,... | collective-permute-start | bytes 3145736 | tf_op jit(solution)/shard_map/ppermute | solution.py:837
  386.6 26.4 %collective-permute-start.42 = (bf16[512,2048]{1,0:T(8,128)(2,1)}, bf16[512,2048]{1,0:T(8,128)(2,1)}, u32[]{:S(2)}, u32[]{:S(2)}) collective-permute-start(bf16[512,2048]{1,0:T(8,128)(2,1)} %get-tuple-element.204), channel_id=1, source_target_pairs={{0,16},{4,20},{8,12},{12,8},{16,0},{20,4},{24,28},{28,24},{1,17},{... | collective-permute-start | bytes 6291464 | tf_op jit(solution)/shard_map/ppermute | solution.py:912
  387.1 11.0 %copy-start.1 = (bf16[1024,512]{1,0:T(8,128)(2,1)S(1)}, bf16[1024,512]{1,0:T(8,128)(2,1)}, u32[]{:S(2)}) copy-start(bf16[1024,512]{1,0:T(8,128)(2,1)} %get-tuple-element.201) | copy-start | bytes 3145732
  400.6 27.0 %collective-permute-start.44 = (bf16[1024,512]{1,0:T(8,128)(2,1)}, bf16[1024,512]{1,0:T(8,128)(2,1)}, u32[]{:S(2)}, u32[]{:S(2)}) collective-permute-start(bf16[1024,512]{1,0:T(8,128)(2,1)} %add_convert_fusion.2), channel_id=1, source_target_pairs={{1,2},{2,1},{5,6},{6,5},{9,10},{10,9},{13,14},{14,13},{17,18},{18,... | collective-permute-start | bytes 3145736 | tf_op jit(solution)/shard_map/ppermute | solution.py:847
  405.1 60.6 %collective-permute-start.48 = (bf16[1024,512]{1,0:T(8,128)(2,1)}, bf16[1024,512]{1,0:T(8,128)(2,1)}, u32[]{:S(2)}, u32[]{:S(2)}) collective-permute-start(bf16[1024,512]{1,0:T(8,128)(2,1)} %add_convert_fusion.1.refs_4_), channel_id=1, source_target_pairs={{1,0},{2,3},{5,4},{6,7},{9,8},{10,11},{13,12},{14,15},{17,16},{18,... | collective-permute-start | bytes 3145736 | tf_op jit(solution)/shard_map/ppermute | solution.py:837
  417.4 26.3 %collective-permute-start.46 = (bf16[256,2048]{1,0:T(8,128)(2,1)}, bf16[256,2048]{1,0:T(8,128)(2,1)}, u32[]{:S(2)}, u32[]{:S(2)}) collective-permute-start(bf16[256,2048]{1,0:T(8,128)(2,1)} %get-tuple-element.212), channel_id=1, source_target_pairs={{0,4},{4,0},{8,24},{12,28},{16,20},{20,16},{24,8},{28,12},{1,5},{5... | collective-permute-start | bytes 3145736 | tf_op jit(solution)/shard_map/ppermute | solution.py:912
  417.4 36.2 %collective-permute-start.45 = (bf16[512,2048]{1,0:T(8,128)(2,1)}, bf16[512,2048]{1,0:T(8,128)(2,1)}, u32[]{:S(2)}, u32[]{:S(2)}) collective-permute-start(bf16[512,2048]{1,0:T(8,128)(2,1)} %get-tuple-element.209), channel_id=1, source_target_pairs={{0,16},{4,20},{8,12},{12,8},{16,0},{20,4},{24,28},{28,24},{1,17},{... | collective-permute-start | bytes 6291464 | tf_op jit(solution)/shard_map/ppermute | solution.py:912
  430.3 35.3 %collective-permute-start.49 = (bf16[1024,512]{1,0:T(8,128)(2,1)}, bf16[1024,512]{1,0:T(8,128)(2,1)}, u32[]{:S(2)}, u32[]{:S(2)}) collective-permute-start(bf16[1024,512]{1,0:T(8,128)(2,1)} %add_convert_fusion.refs_6_), channel_id=1, source_target_pairs={{1,0},{2,3},{5,4},{6,7},{9,8},{10,11},{13,12},{14,15},{17,16},{18,... | collective-permute-start | bytes 3145736 | tf_op jit(solution)/shard_map/ppermute | solution.py:837
  453.7 6.5 %collective-permute-start.47 = (f32[13824]{0:T(1024)}, f32[13824]{0:T(1024)}, u32[]{:S(2)}, u32[]{:S(2)}) collective-permute-start(f32[13824]{0:T(1024)} %add.112), channel_id=1, source_target_pairs={{0,4},{4,0},{1,5},{5,1},{2,6},{6,2},{3,7},{7,3},{8,12},{12,8},{9,1... | collective-permute-start | bytes 165896 | tf_op jit(solution)/shard_map/ppermute | solution.py:872
  458.4 23.2 %collective-permute-start.51 = (bf16[256,2048]{1,0:T(8,128)(2,1)}, bf16[256,2048]{1,0:T(8,128)(2,1)}, u32[]{:S(2)}, u32[]{:S(2)}) collective-permute-start(bf16[256,2048]{1,0:T(8,128)(2,1)} %get-tuple-element.220), channel_id=1, source_target_pairs={{0,4},{4,0},{8,24},{12,28},{16,20},{20,16},{24,8},{28,12},{1,5},{5... | collective-permute-start | bytes 3145736 | tf_op jit(solution)/shard_map/ppermute | solution.py:912
  462.3 17.1 %collective-permute-start.50 = (f32[8192]{0:T(1024)}, f32[8192]{0:T(1024)}, u32[]{:S(2)}, u32[]{:S(2)}) collective-permute-start(f32[8192]{0:T(1024)} %slice.40), channel_id=1, source_target_pairs={{0,1},{1,0},{2,3},{3,2},{4,5},{5,4},{6,7},{7,6},{8,9},{9,8},{10,11... | collective-permute-start | bytes 98312 | tf_op jit(solution)/shard_map/ppermute | solution.py:945
  480.7 5.3 %collective-permute-start.52 = (f32[8192]{0:T(1024)}, f32[8192]{0:T(1024)}, u32[]{:S(2)}, u32[]{:S(2)}) collective-permute-start(f32[8192]{0:T(1024)} %add.122), channel_id=1, source_target_pairs={{0,2},{2,0},{1,3},{3,1},{4,6},{6,4},{5,7},{7,5},{8,10},{10,8},{9,1... | collective-permute-start | bytes 98312 | tf_op jit(solution)/shard_map/ppermute | solution.py:947
  (13 other events, 53.5 us)

commit v9 on v8

--- a/solution.py
+++ b/solution.py
@@ -27,7 +27,7 @@
     return pl.CostEstimate(flops=int(k * flops), bytes_accessed=int(k * nbytes), transcendentals=int(k * trans))
 
 
-def params(n, mb=60):
+def params(n, mb=30):
     return pltpu.CompilerParams(
         dimension_semantics=("arbitrary",) * n, vmem_limit_bytes=int(mb * 1024 * 1024)
     )
@@ -349,7 +349,7 @@
             jax.ShapeDtypeStruct((m, 2 * nheads * HD), F32),
             jax.ShapeDtypeStruct((nprev * m, 2 * nheads * HD), BF),
         ],
-        compiler_params=params(2),
+        compiler_params=params(2, 30 if nprev == 1 else 60),
         cost_estimate=cost(12 * m * nheads * HD * (nprev + 1) * local_len, 20 * m * nheads * HD, m * nheads * (nprev + 1) * local_len),
     )(meta, q, kv, pv, dob, *tabs)
 

time: 496 us -> 489 us (0.986)
  Pallas kernels: 261 us -> 211 us
  local copies, waits for them, and re-layouts: 12 us -> 41.5 us
  waiting for transfers between devices: 76.9 us -> 85 us
    unnamed x52 -> x192, local copies, waits for them, and re-layouts: 6.33 us -> 37.6 us
    pallas_call x6, Pallas kernels: 59.7 us -> 46.8 us  [wgrad_call(): pl.pallas_call(functools.partial(wgrad_kernel, counts, add is not None, s...]
    pallas_call x2, Pallas kernels: 32.5 us -> 23.7 us  [back_call(): pl.pallas_call(back_kernel, name='backn', grid_spec=pltpu.PrefetchScalarG...]
    ppermute x7, waiting for transfers between devices: 44 us -> 50.5 us  [x(): return lax.ppermute(v, 'dp', [(0, 2), (2, 0), (1, 3), (3, 1)])]
  transfers between devices with their start and end apart: 53 -> 53, of which waited for: 11 -> 12; matrix products, arithmetic and copies ran while one was open for 13% -> 13% of each run, Pallas kernels for 53% -> 44%
where the time goes in v9:
time: 489 us; the launch traced here: 482 us
  Pallas kernels  211 us (43%)
  waiting for transfers between devices  85 us (17%)
  starting transfers between devices  83.4 us (17%)
  other arithmetic  59.3 us (12%)
  local copies, waits for them, and re-layouts  41.5 us (8%)
    ppermute x7, waiting for transfers between devices, x(): return lax.ppermute(v, 'dp', [(0, 2), (2, 0), (1, 3), (3, 1)])  50.5 us
    pallas_call x6, Pallas kernels, wgrad_call(): pl.pallas_call(functools.partial(wgrad_kernel, counts, add is not None, s...  46.8 us
    unnamed x192, local copies, waits for them, and re-layouts  37.6 us
    convert_element_type x11, other arithmetic, add_bf(): return lax.optimization_barrier((a.astype(F32) + b.astype(F32)).astype(BF))  30.1 us
    ppermute x11, starting transfers between devices, send(): got = lax.ppermute(v, 'tensor', pairs)  28.6 us
    pallas_call x2, Pallas kernels, back_call(): pl.pallas_call(back_kernel, name='backn', grid_spec=pltpu.PrefetchScalarG...  23.7 us
    ppermute x6, waiting for transfers between devices, turn(): return lax.ppermute(v, ('dp', 'ctx'), pairs)  22.9 us
    pallas_call x2, Pallas kernels, out_call(): pl.pallas_call(functools.partial(out_kernel, count), name='outp', grid=(4...  18.8 us
  transfers between devices with their start and end apart: 53, of which 12 were waited for; matrix products, arithmetic and copies ran while one was open for 13% of the time, Pallas kernels for 44%

profile of v9, /device:TPU:0, one launch (start us, length us, event | category | flops | bytes accessed | tf_op | source)
XLA Modules:
  0.0 482.1 jit_solution(2732660733548497787)
XLA Ops:
  4.6 3.0 collective-permute-start
  10.7 2.6 copy.32
  19.3 6.3 %norm.1 = (bf16[1024,2048]{1,0:T(8,128)(2,1)S(1)}, bf16[1024,2048]{1,0:T(8,128)(2,1)S(1)}, f32[1024,128]{1,0:T(8,128)S(1)}, f32[1,2048]{1,0:T(1,128)S(1)}) custom-call(s32[13]{0:T(128)S(1)} %concatenate.10.meta, bf16[1024,2048]{1,0:T(8,128)(2,1)S(1)} %bitcast.23, bf16[1024,2048]{1,0:T(8,128)(2,1)S(1)} %bitcast.35, f32[1,2048]{1,0:T(1,128)S(1)} %bitcast.40, ...), custom_call_target="tpu_custom_call" | custom-call | flops 629145600000 | bytes 2097152000 | tf_op jit(solution)/shard_map/norm/pallas_call | solution.py:127
  34.0 2.4 pack.3.w0.refs_0_.w10
  37.0 19.4 %collective-permute-done.3.w2.refs_1_.w12 = bf16[256,2048]{1,0:T(8,128)(2,1)S(1)} collective-permute-done((bf16[256,2048]{1,0:T(8,128)(2,1)}, bf16[256,2048]{1,0:T(8,128)(2,1)S(1)}, u32[]{:S(2)}, u32[]{:S(2)}) %collective-permute-start.3) | collective-permute-done | bytes 1048608 | tf_op jit(solution)/shard_map/ppermute | solution.py:866
  56.5 4.2 pack.4.w0.w20
  62.4 8.6 %kv.1.kv_ref = bf16[1024,1024]{1,0:T(8,128)(2,1)} custom-call(bf16[1024,2048]{1,0:T(8,128)(2,1)S(1)} %copy-done.60, bf16[512,2048]{1,0:T(8,128)(2,1)S(1)} %pack.3.w0.refs_0_.w10, bf16[256,2048]{1,0:T(8,128)(2,1)} %collective-permute-done.2.w1.refs_0_.w11, bf16[256,2048]{1,0:T(8,128)(2,1)S(1)} %collective-permute-done.3.w2.refs_1_.w12, ...), custom_call_target="tpu_custom_call" | custom-call | flops 429496729600 | bytes 1048576000 | tf_op jit(solution)/shard_map/kv/pallas_call | solution.py:183
  71.0 4.0 collective-permute-start.13
  75.0 11.6 %collective-permute-done.7.w1.w21 = bf16[256,2048]{1,0:T(8,128)(2,1)} collective-permute-done((bf16[256,2048]{1,0:T(8,128)(2,1)}, bf16[256,2048]{1,0:T(8,128)(2,1)}, u32[]{:S(2)}, u32[]{:S(2)}) %collective-permute-start.7) | collective-permute-done | bytes 1048608 | tf_op jit(solution)/shard_map/ppermute | solution.py:866
  90.4 6.8 %qd.1 = (bf16[1024,512]{1,0:T(8,128)(2,1)S(1)}, bf16[1024,512]{1,0:T(8,128)(2,1)S(1)}) custom-call(bf16[1024,2048]{1,0:T(8,128)(2,1)S(1)} %copy-done.61, bf16[1024,2048]{1,0:T(8,128)(2,1)S(1)} %copy-done.69, bf16[512,2048]{1,0:T(8,128)(2,1)S(1)} %pack.3.w0.refs_0_.w10, bf16[256,2048]{1,0:T(8,128)(2,1)} %collective-permute-done.2.w1.refs_0_.w11, ...), custom_call_target="tpu_custom_call" | custom-call | flops 440401920000 | bytes 1468006400 | tf_op jit(solution)/shard_map/qd/pallas_call | solution.py:224
  97.3 14.3 %collective-permute-done.8.w2.w22 = bf16[256,2048]{1,0:T(8,128)(2,1)} collective-permute-done((bf16[256,2048]{1,0:T(8,128)(2,1)}, bf16[256,2048]{1,0:T(8,128)(2,1)}, u32[]{:S(2)}, u32[]{:S(2)}) %collective-permute-start.8) | collective-permute-done | bytes 1048608 | tf_op jit(solution)/shard_map/ppermute | solution.py:866
  111.6 3.3 norm2.1.h2.refs_0_
  116.5 14.7 %hidden.1 = (bf16[1024,2048]{1,0:T(8,128)(2,1)S(1)}, bf16[1024,2048]{1,0:T(8,128)(2,1)S(1)}) custom-call(bf16[1024,2048]{1,0:T(8,128)(2,1)S(1)} %norm2.1.h2.refs_0_, bf16[512,2048]{1,0:T(8,128)(2,1)} %pack.4.w0.w20, bf16[256,2048]{1,0:T(8,128)(2,1)} %collective-permute-done.7.w1.w21, bf16[256,2048]{1,0:T(8,128)(2,1)} %collective-permute-done.8.w2.w22, ...), custom_call_target="tpu_custom_call" | custom-call | flops 858993459200 | bytes 2097152000 | tf_op jit(solution)/shard_map/hidden/pallas_call | solution.py:413
  131.2 4.8 pack.5.refs_2_.w0
  136.3 4.5 collective-permute-done.15.refs_4_.w1
  142.4 12.2 %attn.1 = (bf16[1024,512]{1,0:T(8,128)(2,1)S(1)}, bf16[1024,512]{1,0:T(8,128)(2,1)S(1)}, f32[1024,1024]{1,0:T(8,128)S(1)}, bf16[1024,1024]{1,0:T(8,128)(2,1)}) custom-call(s32[13]{0:T(128)S(1)} %concatenate.10.meta, bf16[1024,512]{1,0:T(8,128)(2,1)S(1)} %get-tuple-element.127.q_ref, bf16[1024,1024]{1,0:T(8,128)(2,1)} %kv.1.kv_ref, ...), custom_call_target="tpu_custom_call" | custom-call | flops 644245094400 | bytes 1048576000 | tf_op jit(solution)/shard_map/attn/pallas_call | solution.py:333
  156.4 9.2 %outp.2 = (bf16[1024,512]{1,0:T(8,128)(2,1)}, bf16[1024,512]{1,0:T(8,128)(2,1)}) custom-call(bf16[1024,512]{1,0:T(8,128)(2,1)S(1)} %get-tuple-element.143.ob.refs_3_, bf16[1024,2048]{1,0:T(8,128)(2,1)S(1)} %get-tuple-element.135.gb.refs_1_, bf16[512,2048]{1,0:T(8,128)(2,1)S(1)} %copy-done.18, bf16[512,2048]{1,0:T(8,128)(2,1)S(1)} %copy-done.15, ...), custom_call_target="tpu_custom_call" | custom-call | flops 53687092 | bytes 125829 | tf_op jit(solution)/shard_map/outp/pallas_call | solution.py:479
  165.6 4.4 collective-permute-start.19
  170.3 7.3 %wgrad.6 = bf16[1024,2048]{1,0:T(8,128)(2,1)} custom-call(s32[13]{0:T(128)S(1)} %concatenate.10.meta, bf16[1024,2048]{1,0:T(8,128)(2,1)S(1)} %copy-done.70, bf16[1024,2048]{1,0:T(8,128)(2,1)S(1)} %get-tuple-element.135.gb.refs_1_), custom_call_target="tpu_custom_call" | custom-call | flops 440401920000 | bytes 1468006400 | tf_op jit(solution)/shard_map/wgrad/pallas_call | solution.py:602
  177.8 2.3 collective-permute-start.20
  180.2 9.6 %outp.3 = (bf16[1024,512]{1,0:T(8,128)(2,1)}, bf16[1024,512]{1,0:T(8,128)(2,1)S(1)}) custom-call(bf16[1024,512]{1,0:T(8,128)(2,1)S(1)} %get-tuple-element.143.ob.refs_3_, bf16[1024,2048]{1,0:T(8,128)(2,1)S(1)} %get-tuple-element.135.gb.refs_1_, bf16[256,2048]{1,0:T(8,128)(2,1)} %collective-permute-done.2.w1.refs_0_.w11, bf16[256,2048]{1,0:T(8,128)(2,1)S(1)} %copy-done.44, ...), custom_call_target="tpu_custom_call" | custom-call | flops 536870912000 | bytes 1258291200 | tf_op jit(solution)/shard_map/outp/pallas_call | solution.py:479
  189.7 3.2 collective-permute-done.19
  192.9 2.8 add_convert_fusion.15
  201.8 12.3 %dhid.1 = (bf16[1024,2048]{1,0:T(8,128)(2,1)S(1)}, f32[1,2048]{1,0:T(1,128)S(1)}) custom-call(bf16[1024,2048]{1,0:T(8,128)(2,1)S(1)} %copy-done.71, bf16[512,2048]{1,0:T(8,128)(2,1)} %pack.5.refs_2_.w0, bf16[256,2048]{1,0:T(8,128)(2,1)} %collective-permute-done.15.refs_4_.w1, bf16[256,2048]{1,0:T(8,128)(2,1)} %collective-permute-done.16.refs_5_.w2, ...), custom_call_target="tpu_custom_call" | custom-call | flops 858993459200 | bytes 2097152000 | tf_op jit(solution)/shard_map/dhid/pallas_call | solution.py:438
  216.2 2.8 add_convert_fusion.14
  220.7 8.4 %collective-permute-start.24 = (bf16[1024,512]{1,0:T(8,128)(2,1)}, bf16[1024,512]{1,0:T(8,128)(2,1)}, u32[]{:S(2)}, u32[]{:S(2)}) collective-permute-start(bf16[1024,512]{1,0:T(8,128)(2,1)} %get-tuple-element.165), channel_id=1, source_target_pairs={{0,1},{3,2},{4,5},{7,6},{8,9},{11,10},{12,13},{15,14},{16,17},{19,... | collective-permute-start | bytes 3145736 | tf_op jit(solution)/shard_map/ppermute | solution.py:837
  229.1 8.3 %wgrad.7 = (bf16[512,2048]{1,0:T(8,128)(2,1)S(1)}, bf16[512,2048]{1,0:T(8,128)(2,1)}) custom-call(s32[13]{0:T(128)S(1)} %concatenate.10.meta, bf16[1024,2048]{1,0:T(8,128)(2,1)S(1)} %copy-done.71, bf16[1024,2048]{1,0:T(8,128)(2,1)S(1)} %get-tuple-element.135.gb.refs_1_, bf16[1024,2048]{1,0:T(8,128)(2,1)} %collective-permute-done.21.refs_2_), custom_call_target="tpu_custom_call" | custom-call | flops 440401920000 | bytes 1468006400 | tf_op jit(solution)/shard_map/wgrad/pallas_call | solution.py:602
  237.4 3.8 join.1
  241.3 4.1 fusion.refs_0_
  245.5 5.9 %collective-permute-done.24 = bf16[1024,512]{1,0:T(8,128)(2,1)} collective-permute-done((bf16[1024,512]{1,0:T(8,128)(2,1)}, bf16[1024,512]{1,0:T(8,128)(2,1)}, u32[]{:S(2)}, u32[]{:S(2)}) %collective-permute-start.24) | collective-permute-done | bytes 1048608 | tf_op jit(solution)/shard_map/ppermute | solution.py:837
  251.5 2.8 add_convert_fusion.12
  258.7 11.9 %backn.2 = (bf16[1024,512]{1,0:T(8,128)(2,1)S(1)}, bf16[1024,512]{1,0:T(8,128)(2,1)S(1)}, f32[4,2048]{1,0:T(4,128)S(1)}) custom-call(s32[13]{0:T(128)S(1)} %copy-done.34, bf16[1024,1536]{1,0:T(8,128)(2,1)S(1)} %get-tuple-element.162.dqkv.refs_1_, bf16[1024,2048]{1,0:T(8,128)(2,1)S(1)} %copy-done.75, ...), custom_call_target="tpu_custom_call", output_to_operand_aliasing={{2}: (13, {})} | custom-call | flops 751619276800 | bytes 1887436800 | tf_op jit(solution)/shard_map/backn/pallas_call | solution.py:523
  270.7 3.7 fusion.1.refs_4_
  274.4 4.4 collective-permute-start.29
  279.4 2.5 add_convert_fusion.10
  283.7 3.1 fusion.2.refs_2_
  287.7 4.9 %hsum.3 = (f32[256,2048]{1,0:T(8,128)S(1)}, bf16[256,2048]{1,0:T(8,128)(2,1)}) custom-call(bf16[512,2048]{1,0:T(8,128)(2,1)S(1)} %copy-done.58, bf16[512,2048]{1,0:T(8,128)(2,1)} %collective-permute-done.28.got), custom_call_target="tpu_custom_call" | custom-call | flops 220200960000 | bytes 734003200 | tf_op jit(solution)/shard_map/hsum/pallas_call | solution.py:652
  292.6 9.7 %collective-permute-start.30 = (bf16[256,2048]{1,0:T(8,128)(2,1)}, bf16[256,2048]{1,0:T(8,128)(2,1)}, u32[]{:S(2)}, u32[]{:S(2)}) collective-permute-start(bf16[256,2048]{1,0:T(8,128)(2,1)} %get-tuple-element.183), channel_id=1, source_target_pairs={{0,4},{4,0},{8,24},{12,28},{16,20},{20,16},{24,8},{28,12},{1,5},{5... | collective-permute-start | bytes 3145736 | tf_op jit(solution)/shard_map/ppermute | solution.py:912
  302.3 11.8 %backn.3 = (bf16[1024,512]{1,0:T(8,128)(2,1)S(1)}, bf16[1024,512]{1,0:T(8,128)(2,1)S(1)}, f32[4,2048]{1,0:T(4,128)S(1)}) custom-call(s32[13]{0:T(128)S(1)} %copy-done.35, bf16[1024,1536]{1,0:T(8,128)(2,1)S(1)} %copy-done.65, bf16[1024,2048]{1,0:T(8,128)(2,1)S(1)} %copy-done.76, bf16[512,2048]{1,0:T(8,128)(2,1)S(1)} %copy-done.16, ...), custom_call_target="tpu_custom_call", output_to_operand_aliasing={{2}: (13, {})} | custom-call | flops 751619276800 | bytes 1887436800 | tf_op jit(solution)/shard_map/backn/pallas_call | solution.py:523
  314.2 3.2 add_convert_fusion.8
  319.2 2.9 fusion.3.refs_6_
  327.1 7.3 %wgrad.8 = bf16[1024,2048]{1,0:T(8,128)(2,1)} custom-call(s32[13]{0:T(128)S(1)} %copy-done.35, bf16[1024,2048]{1,0:T(8,128)(2,1)S(1)} %copy-done.55, bf16[1024,2048]{1,0:T(8,128)(2,1)S(1)} %copy-done.77), custom_call_target="tpu_custom_call" | custom-call | flops 440401920000 | bytes 1468006400 | tf_op jit(solution)/shard_map/wgrad/pallas_call | solution.py:602
  341.8 7.3 %wgrad.9 = bf16[1024,2048]{1,0:T(8,128)(2,1)} custom-call(s32[13]{0:T(128)S(1)} %copy-done.35, bf16[1024,2048]{1,0:T(8,128)(2,1)S(1)} %copy-done.62, bf16[1024,1536]{1,0:T(8,128)(2,1)S(1)} %copy-done.66, bf16[1024,2048]{1,0:T(8,128)(2,1)S(1)} %copy-done.72, bf16[1024,512]{1,0:T(8,128)(2,1)S(1)} %copy-done.21), custom_call_target="tpu_custom_call" | custom-call | flops 503316480000 | bytes 1677721600 | tf_op jit(solution)/shard_map/wgrad/pallas_call | solution.py:602
  350.6 2.5 add_convert_fusion.6
  354.9 3.1 fusion.4.refs_0_
  362.4 8.3 %wgrad.10 = (bf16[512,2048]{1,0:T(8,128)(2,1)S(1)}, bf16[512,2048]{1,0:T(8,128)(2,1)}) custom-call(s32[13]{0:T(128)S(1)} %copy-done.35, bf16[1024,2048]{1,0:T(8,128)(2,1)S(1)} %copy-done.56, bf16[1024,2048]{1,0:T(8,128)(2,1)S(1)} %copy-done.78, bf16[1024,2048]{1,0:T(8,128)(2,1)} %collective-permute-done.36.refs_2_), custom_call_target="tpu_custom_call" | custom-call | flops 440401920000 | bytes 1468006400 | tf_op jit(solution)/shard_map/wgrad/pallas_call | solution.py:602
  370.7 4.1 lsum.3
  374.7 2.5 add_convert_fusion.4
  379.0 2.8 add_convert_fusion.3.refs_2_
  388.1 8.3 %wgrad.11 = (bf16[512,2048]{1,0:T(8,128)(2,1)S(1)}, bf16[512,2048]{1,0:T(8,128)(2,1)}) custom-call(s32[13]{0:T(128)S(1)} %copy-done.35, bf16[1024,2048]{1,0:T(8,128)(2,1)S(1)} %copy-done.63, bf16[1024,1536]{1,0:T(8,128)(2,1)S(1)} %copy-done.67, bf16[1024,2048]{1,0:T(8,128)(2,1)S(1)} %copy-done.73, bf16[1024,512]{1,0:T(8,128)(2,1)S(1)} %copy-done.21, ...), custom_call_target="tpu_custom_call" | custom-call | flops 503316480000 | bytes 1677721600 | tf_op jit(solution)/shard_map/wgrad/pallas_call | solution.py:602
  396.4 2.6 add_convert_fusion.2
  400.6 2.8 add_convert_fusion.1.refs_4_
  404.6 4.9 %collective-permute-done.42.got = bf16[512,2048]{1,0:T(8,128)(2,1)} collective-permute-done((bf16[512,2048]{1,0:T(8,128)(2,1)}, bf16[512,2048]{1,0:T(8,128)(2,1)}, u32[]{:S(2)}, u32[]{:S(2)}) %collective-permute-start.42) | collective-permute-done | bytes 2097184 | tf_op jit(solution)/shard_map/ppermute | solution.py:912
  409.5 3.9 hsum.4
  415.5 4.1 bout.2.refs_8_
  419.6 4.1 bout.3
  423.7 2.8 add_convert_fusion.refs_6_
  428.0 11.7 %collective-permute-done.46.got = bf16[256,2048]{1,0:T(8,128)(2,1)} collective-permute-done((bf16[256,2048]{1,0:T(8,128)(2,1)}, bf16[256,2048]{1,0:T(8,128)(2,1)}, u32[]{:S(2)}, u32[]{:S(2)}) %collective-permute-start.46) | collective-permute-done | bytes 1048608 | tf_op jit(solution)/shard_map/ppermute | solution.py:912
  439.8 3.7 lsum.4
  443.4 6.2 %collective-permute-done.45.got = bf16[512,2048]{1,0:T(8,128)(2,1)} collective-permute-done((bf16[512,2048]{1,0:T(8,128)(2,1)}, bf16[512,2048]{1,0:T(8,128)(2,1)}, u32[]{:S(2)}, u32[]{:S(2)}) %collective-permute-start.45) | collective-permute-done | bytes 2097184 | tf_op jit(solution)/shard_map/ppermute | solution.py:912
  451.3 4.1 hsum.5
  457.9 3.3 collective-permute-start.50
  461.2 9.4 %igrad.1 = bf16[1024,2048]{1,0:T(8,128)(2,1)} custom-call(s32[13]{0:T(128)S(1)} %copy-done.35, bf16[1024,2048]{1,0:T(8,128)(2,1)S(1)} %bitcast.29, bf16[1024,2048]{1,0:T(8,128)(2,1)S(1)} %bitcast.36, f32[1024,128]{1,0:T(8,128)S(1)} %copy-done.81, bf16[1024,512]{1,0:T(8,128)(2,1)} %fusion.4.refs_0_, bf16[1024,512]{1,0:T(8,128)(2,1)} %collective-permute-done.40.refs_1_, ...), custom_call_target="tpu_custom_call" | custom-call | flops 503316480000 | bytes 1677721600 | tf_op jit(solution)/shard_map/igrad/pallas_call | solution.py:775
  474.6 4.0 lsum.5
  (304 shorter events, 98.1 us)
Async XLA Ops:
  4.6 27.3 %collective-permute-start = (bf16[256,2048]{1,0:T(8,128)(2,1)}, bf16[256,2048]{1,0:T(8,128)(2,1)}, u32[]{:S(2)}, u32[]{:S(2)}) collective-permute-start(bf16[256,2048]{1,0:T(8,128)(2,1)} %pad_maximum_fusion.refs_0_), channel_id=1, source_target_pairs={{0,4},{4,0},{1,5},{5,1},{2,6},{6,2},{3,7},{7,3},{8,12},{12,8},{9,1... | collective-permute-start | bytes 3145736 | tf_op jit(solution)/shard_map/ppermute | solution.py:872
  7.6 24.9 %collective-permute-start.2 = (bf16[256,2048]{1,0:T(8,128)(2,1)}, bf16[256,2048]{1,0:T(8,128)(2,1)}, u32[]{:S(2)}, u32[]{:S(2)}) collective-permute-start(bf16[256,2048]{1,0:T(8,128)(2,1)} %pad_maximum_fusion.refs_0_), channel_id=1, source_target_pairs={{0,16},{16,0},{8,24},{24,8},{1,17},{17,1},{9,25},{25,9},{2,18},{18... | collective-permute-start | bytes 3145736 | tf_op jit(solution)/shard_map/ppermute | solution.py:866
  10.2 46.3 %collective-permute-start.1 = (bf16[256,2048]{1,0:T(8,128)(2,1)}, bf16[256,2048]{1,0:T(8,128)(2,1)}, u32[]{:S(2)}, u32[]{:S(2)}) collective-permute-start(bf16[256,2048]{1,0:T(8,128)(2,1)} %convert_element_type.174.refs_0_), channel_id=1, source_target_pairs={{0,4},{4,0},{1,5},{5,1},{2,6},{6,2},{3,7},{7,3},{8,12},{12,8},{9,1... | collective-permute-start | bytes 3145736 | tf_op jit(solution)/shard_map/ppermute | solution.py:872
  13.3 117.9 %collective-permute-start.12 = (bf16[256,2048]{1,0:T(8,128)(2,1)}, bf16[256,2048]{1,0:T(8,128)(2,1)}, u32[]{:S(2)}, u32[]{:S(2)}) collective-permute-start(bf16[256,2048]{1,0:T(8,128)(2,1)} %bitcast.21.refs_0_), channel_id=1, source_target_pairs={{0,4},{4,0},{1,5},{5,1},{2,6},{6,2},{3,7},{7,3},{8,12},{12,8},{9,1... | collective-permute-start | bytes 3145736 | tf_op jit(solution)/shard_map/ppermute | solution.py:872
  14.9 214.1 %copy-start.33 = (s32[13]{0:T(128)}, s32[13]{0:T(128)S(1)}, u32[]{:S(2)}) copy-start(s32[13]{0:T(128)S(1)} %concatenate.10.meta) | copy-start | bytes 160
  29.6 226.9 %copy-start.79 = (f32[1024,128]{1,0:T(8,128)}, f32[1024,128]{1,0:T(8,128)S(1)}, u32[]{:S(2)}) copy-start(f32[1024,128]{1,0:T(8,128)S(1)} %get-tuple-element.129.st_ref) | copy-start | bytes 1572868
  30.7 57.4 %copy-start.22 = (f32[512,128]{1,0:T(8,128)}, f32[512,128]{1,0:T(8,128)S(1)}, u32[]{:S(2)}) copy-start(f32[512,128]{1,0:T(8,128)S(1)} %get-tuple-element.230.s2) | copy-start | bytes 786436
  30.8 57.4 %copy-start.25 = (f32[512,128]{1,0:T(8,128)}, f32[512,128]{1,0:T(8,128)S(1)}, u32[]{:S(2)}) copy-start(f32[512,128]{1,0:T(8,128)S(1)} %get-tuple-element.231.s1) | copy-start | bytes 786436
  30.8 57.4 %copy-start.28 = (f32[512,128]{1,0:T(8,128)}, f32[512,128]{1,0:T(8,128)S(1)}, u32[]{:S(2)}) copy-start(f32[512,128]{1,0:T(8,128)S(1)} %get-tuple-element.232.cosf) | copy-start | bytes 786436
  32.5 24.0 %collective-permute-start.3 = (bf16[256,2048]{1,0:T(8,128)(2,1)}, bf16[256,2048]{1,0:T(8,128)(2,1)S(1)}, u32[]{:S(2)}, u32[]{:S(2)}) collective-permute-start(bf16[256,2048]{1,0:T(8,128)(2,1)} %collective-permute-done.refs_1_), channel_id=1, source_target_pairs={{0,16},{16,0},{8,24},{24,8},{1,17},{17,1},{9,25},{25,9},{2,18},{18... | collective-permute-start | bytes 3145736 | tf_op jit(solution)/shard_map/ppermute | solution.py:866
  36.4 51.7 %copy-start.17 = (bf16[512,2048]{1,0:T(8,128)(2,1)}, bf16[512,2048]{1,0:T(8,128)(2,1)S(1)}, u32[]{:S(2)}) copy-start(bf16[512,2048]{1,0:T(8,128)(2,1)S(1)} %pack.3.w0.refs_0_.w10) | copy-start | bytes 6291460
  36.5 25.9 %copy-start.60 = (bf16[1024,2048]{1,0:T(8,128)(2,1)S(1)}, bf16[1024,2048]{1,0:T(8,128)(2,1)}, u32[]{:S(2)}) copy-start(bf16[1024,2048]{1,0:T(8,128)(2,1)} %copy-done.59) | copy-start | bytes 12582916
  36.5 25.9 %collective-permute-start.4 = (bf16[512,2048]{1,0:T(8,128)(2,1)S(1)}, bf16[512,2048]{1,0:T(8,128)(2,1)S(1)}, u32[]{:S(2)}, u32[]{:S(2)}) collective-permute-start(bf16[512,2048]{1,0:T(8,128)(2,1)S(1)} %pack.3.w0.refs_0_.w10), channel_id=1, source_target_pairs={{0,8},{8,0},{16,24},{24,16},{1,9},{9,1},{17,25},{25,17},{2,10},{10... | collective-permute-start | bytes 6291464 | tf_op jit(solution)/shard_map/ppermute | solution.py:869
  36.5 24.3 %collective-permute-start.5 = (bf16[256,2048]{1,0:T(8,128)(2,1)}, bf16[256,2048]{1,0:T(8,128)(2,1)S(1)}, u32[]{:S(2)}, u32[]{:S(2)}) collective-permute-start(bf16[256,2048]{1,0:T(8,128)(2,1)} %collective-permute-done.2.w1.refs_0_.w11), channel_id=1, source_target_pairs={{0,8},{8,0},{16,24},{24,16},{1,9},{9,1},{17,25},{25,17},{2,10},{10... | collective-permute-start | bytes 3145736 | tf_op jit(solution)/shard_map/ppermute | solution.py:869
  56.5 31.7 %copy-start.43 = (bf16[256,2048]{1,0:T(8,128)(2,1)}, bf16[256,2048]{1,0:T(8,128)(2,1)S(1)}, u32[]{:S(2)}) copy-start(bf16[256,2048]{1,0:T(8,128)(2,1)S(1)} %collective-permute-done.3.w2.refs_1_.w12) | copy-start | bytes 3145732
  56.5 5.9 %collective-permute-start.6 = (bf16[256,2048]{1,0:T(8,128)(2,1)S(1)}, bf16[256,2048]{1,0:T(8,128)(2,1)S(1)}, u32[]{:S(2)}, u32[]{:S(2)}) collective-permute-start(bf16[256,2048]{1,0:T(8,128)(2,1)S(1)} %collective-permute-done.3.w2.refs_1_.w12), channel_id=1, source_target_pairs={{0,8},{8,0},{16,24},{24,16},{1,9},{9,1},{17,25},{25,17},{2,10},{10... | collective-permute-start | bytes 3145736 | tf_op jit(solution)/shard_map/ppermute | solution.py:869
  60.7 54.2 %collective-permute-start.9 = (bf16[512,2048]{1,0:T(8,128)(2,1)}, bf16[512,2048]{1,0:T(8,128)(2,1)}, u32[]{:S(2)}, u32[]{:S(2)}) collective-permute-start(bf16[512,2048]{1,0:T(8,128)(2,1)} %pack.4.w0.w20), channel_id=1, source_target_pairs={{0,8},{8,0},{16,24},{24,16},{1,9},{9,1},{17,25},{25,17},{2,10},{10... | collective-permute-start | bytes 6291464 | tf_op jit(solution)/shard_map/ppermute | solution.py:869
  60.9 119.3 %copy-start.38 = (bf16[256,2048]{1,0:T(8,128)(2,1)}, bf16[256,2048]{1,0:T(8,128)(2,1)S(1)}, u32[]{:S(2)}) copy-start(bf16[256,2048]{1,0:T(8,128)(2,1)S(1)} %collective-permute-done.5.w4.refs_2_.w11) | copy-start | bytes 3145732
  60.9 25.8 %collective-permute-start.7 = (bf16[256,2048]{1,0:T(8,128)(2,1)}, bf16[256,2048]{1,0:T(8,128)(2,1)}, u32[]{:S(2)}, u32[]{:S(2)}) collective-permute-start(bf16[256,2048]{1,0:T(8,128)(2,1)} %convert_element_type.174.refs_0_), channel_id=1, source_target_pairs={{0,16},{16,0},{8,24},{24,8},{1,17},{17,1},{9,25},{25,9},{2,18},{18... | collective-permute-start | bytes 3145736 | tf_op jit(solution)/shard_map/ppermute | solution.py:866
  71.0 71.3 %collective-permute-start.13 = (bf16[1024,1024]{1,0:T(8,128)(2,1)}, bf16[1024,1024]{1,0:T(8,128)(2,1)}, u32[]{:S(2)}, u32[]{:S(2)}) collective-permute-start(bf16[1024,1024]{1,0:T(8,128)(2,1)} %kv.1.kv_ref), channel_id=1, source_target_pairs={{0,4},{1,5},{2,6},{3,7},{8,12},{9,13},{10,14},{11,15},{16,20},{17,... | collective-permute-start | bytes 6291464 | tf_op jit(solution)/shard_map/ppermute | solution.py:929
  86.6 24.9 %collective-permute-start.8 = (bf16[256,2048]{1,0:T(8,128)(2,1)}, bf16[256,2048]{1,0:T(8,128)(2,1)}, u32[]{:S(2)}, u32[]{:S(2)}) collective-permute-start(bf16[256,2048]{1,0:T(8,128)(2,1)} %collective-permute-done.1.refs_1_), channel_id=1, source_target_pairs={{0,16},{16,0},{8,24},{24,8},{1,17},{17,1},{9,25},{25,9},{2,18},{18... | collective-permute-start | bytes 3145736 | tf_op jit(solution)/shard_map/ppermute | solution.py:866
  88.1 28.3 %collective-permute-start.10 = (bf16[256,2048]{1,0:T(8,128)(2,1)}, bf16[256,2048]{1,0:T(8,128)(2,1)}, u32[]{:S(2)}, u32[]{:S(2)}) collective-permute-start(bf16[256,2048]{1,0:T(8,128)(2,1)} %collective-permute-done.7.w1.w21), channel_id=1, source_target_pairs={{0,8},{8,0},{16,24},{24,16},{1,9},{9,1},{17,25},{25,17},{2,10},{10... | collective-permute-start | bytes 3145736 | tf_op jit(solution)/shard_map/ppermute | solution.py:869
  111.6 4.9 %collective-permute-start.11 = (bf16[256,2048]{1,0:T(8,128)(2,1)}, bf16[256,2048]{1,0:T(8,128)(2,1)}, u32[]{:S(2)}, u32[]{:S(2)}) collective-permute-start(bf16[256,2048]{1,0:T(8,128)(2,1)} %collective-permute-done.8.w2.w22), channel_id=1, source_target_pairs={{0,8},{8,0},{16,24},{24,16},{1,9},{9,1},{17,25},{25,17},{2,10},{10... | collective-permute-start | bytes 3145736 | tf_op jit(solution)/shard_map/ppermute | solution.py:869
  114.9 25.9 %collective-permute-start.15 = (bf16[256,2048]{1,0:T(8,128)(2,1)}, bf16[256,2048]{1,0:T(8,128)(2,1)}, u32[]{:S(2)}, u32[]{:S(2)}) collective-permute-start(bf16[256,2048]{1,0:T(8,128)(2,1)} %bitcast.21.refs_0_), channel_id=1, source_target_pairs={{0,16},{16,0},{8,24},{24,8},{1,17},{17,1},{9,25},{25,9},{2,18},{18... | collective-permute-start | bytes 3145736 | tf_op jit(solution)/shard_map/ppermute | solution.py:866
  136.0 20.3 %collective-permute-start.14 = (bf16[512,2048]{1,0:T(8,128)(2,1)}, bf16[512,2048]{1,0:T(8,128)(2,1)}, u32[]{:S(2)}, u32[]{:S(2)}) collective-permute-start(bf16[512,2048]{1,0:T(8,128)(2,1)} %pack.5.refs_2_.w0), channel_id=1, source_target_pairs={{0,8},{8,0},{16,24},{24,16},{1,9},{9,1},{17,25},{25,17},{2,10},{10... | collective-permute-start | bytes 6291464 | tf_op jit(solution)/shard_map/ppermute | solution.py:869
  140.8 29.2 %collective-permute-start.16 = (bf16[256,2048]{1,0:T(8,128)(2,1)}, bf16[256,2048]{1,0:T(8,128)(2,1)}, u32[]{:S(2)}, u32[]{:S(2)}) collective-permute-start(bf16[256,2048]{1,0:T(8,128)(2,1)} %collective-permute-done.12.refs_1_), channel_id=1, source_target_pairs={{0,16},{16,0},{8,24},{24,8},{1,17},{17,1},{9,25},{25,9},{2,18},{18... | collective-permute-start | bytes 3145736 | tf_op jit(solution)/shard_map/ppermute | solution.py:866
  154.6 23.3 %collective-permute-start.17 = (bf16[256,2048]{1,0:T(8,128)(2,1)}, bf16[256,2048]{1,0:T(8,128)(2,1)}, u32[]{:S(2)}, u32[]{:S(2)}) collective-permute-start(bf16[256,2048]{1,0:T(8,128)(2,1)} %collective-permute-done.15.refs_4_.w1), channel_id=1, source_target_pairs={{0,8},{8,0},{16,24},{24,16},{1,9},{9,1},{17,25},{25,17},{2,10},{10... | collective-permute-start | bytes 3145736 | tf_op jit(solution)/shard_map/ppermute | solution.py:869
  154.6 82.8 %collective-permute-start.22 = (bf16[1024,1024]{1,0:T(8,128)(2,1)}, bf16[1024,1024]{1,0:T(8,128)(2,1)}, u32[]{:S(2)}, u32[]{:S(2)}) collective-permute-start(bf16[1024,1024]{1,0:T(8,128)(2,1)} %get-tuple-element.161), channel_id=1, source_target_pairs={{4,0},{5,1},{6,2},{7,3},{12,8},{13,9},{14,10},{15,11},{20,16},{21,... | collective-permute-start | bytes 6291464 | tf_op jit(solution)/shard_map/ppermute | solution.py:932
  165.6 27.3 %collective-permute-start.19 = (bf16[1024,512]{1,0:T(8,128)(2,1)}, bf16[1024,512]{1,0:T(8,128)(2,1)}, u32[]{:S(2)}, u32[]{:S(2)}) collective-permute-start(bf16[1024,512]{1,0:T(8,128)(2,1)} %get-tuple-element.149), channel_id=1, source_target_pairs={{0,1},{3,2},{4,5},{7,6},{8,9},{11,10},{12,13},{15,14},{16,17},{19,... | collective-permute-start | bytes 3145736 | tf_op jit(solution)/shard_map/ppermute | solution.py:837
  170.1 10.1 %collective-permute-start.18 = (bf16[256,2048]{1,0:T(8,128)(2,1)}, bf16[256,2048]{1,0:T(8,128)(2,1)}, u32[]{:S(2)}, u32[]{:S(2)}) collective-permute-start(bf16[256,2048]{1,0:T(8,128)(2,1)} %collective-permute-done.16.refs_5_.w2), channel_id=1, source_target_pairs={{0,8},{8,0},{16,24},{24,16},{1,9},{9,1},{17,25},{25,17},{2,10},{10... | collective-permute-start | bytes 3145736 | tf_op jit(solution)/shard_map/ppermute | solution.py:869
  177.5 51.5 %collective-permute-start.21 = (bf16[1024,2048]{1,0:T(8,128)(2,1)}, bf16[1024,2048]{1,0:T(8,128)(2,1)}, u32[]{:S(2)}, u32[]{:S(2)}) collective-permute-start(bf16[1024,2048]{1,0:T(8,128)(2,1)} %wgrad.6), channel_id=1, source_target_pairs={{0,8},{8,0},{16,24},{24,16},{1,9},{9,1},{17,25},{25,17},{2,10},{10... | collective-permute-start | bytes 12582920 | tf_op jit(solution)/shard_map/ppermute | solution.py:869
  177.8 38.3 %collective-permute-start.20 = (bf16[1024,512]{1,0:T(8,128)(2,1)}, bf16[1024,512]{1,0:T(8,128)(2,1)}, u32[]{:S(2)}, u32[]{:S(2)}) collective-permute-start(bf16[1024,512]{1,0:T(8,128)(2,1)} %get-tuple-element.156), channel_id=1, source_target_pairs={{0,1},{3,2},{4,5},{7,6},{8,9},{11,10},{12,13},{15,14},{16,17},{19,... | collective-permute-start | bytes 3145736 | tf_op jit(solution)/shard_map/ppermute | solution.py:837
  189.7 51.5 %copy-start.4 = (bf16[1024,512]{1,0:T(8,128)(2,1)}, bf16[1024,512]{1,0:T(8,128)(2,1)S(1)}, u32[]{:S(2)}) copy-start(bf16[1024,512]{1,0:T(8,128)(2,1)S(1)} %get-tuple-element.169) | copy-start | bytes 3145732
  195.8 45.5 %collective-permute-start.23 = (bf16[1024,512]{1,0:T(8,128)(2,1)}, bf16[1024,512]{1,0:T(8,128)(2,1)}, u32[]{:S(2)}, u32[]{:S(2)}) collective-permute-start(bf16[1024,512]{1,0:T(8,128)(2,1)} %add_convert_fusion.15), channel_id=1, source_target_pairs={{1,2},{2,1},{5,6},{6,5},{9,10},{10,9},{13,14},{14,13},{17,18},{18,... | collective-permute-start | bytes 3145736 | tf_op jit(solution)/shard_map/ppermute | solution.py:847
  219.0 51.7 %collective-permute-start.25 = (bf16[1024,512]{1,0:T(8,128)(2,1)}, bf16[1024,512]{1,0:T(8,128)(2,1)}, u32[]{:S(2)}, u32[]{:S(2)}) collective-permute-start(bf16[1024,512]{1,0:T(8,128)(2,1)} %add_convert_fusion.14), channel_id=1, source_target_pairs={{1,2},{2,1},{5,6},{6,5},{9,10},{10,9},{13,14},{14,13},{17,18},{18,... | collective-permute-start | bytes 3145736 | tf_op jit(solution)/shard_map/ppermute | solution.py:847
  220.7 30.8 %collective-permute-start.24 = (bf16[1024,512]{1,0:T(8,128)(2,1)}, bf16[1024,512]{1,0:T(8,128)(2,1)}, u32[]{:S(2)}, u32[]{:S(2)}) collective-permute-start(bf16[1024,512]{1,0:T(8,128)(2,1)} %get-tuple-element.165), channel_id=1, source_target_pairs={{0,1},{3,2},{4,5},{7,6},{8,9},{11,10},{12,13},{15,14},{16,17},{19,... | collective-permute-start | bytes 3145736 | tf_op jit(solution)/shard_map/ppermute | solution.py:837
  245.4 33.9 %collective-permute-start.26 = (bf16[1024,512]{1,0:T(8,128)(2,1)}, bf16[1024,512]{1,0:T(8,128)(2,1)}, u32[]{:S(2)}, u32[]{:S(2)}) collective-permute-start(bf16[1024,512]{1,0:T(8,128)(2,1)} %fusion.refs_0_), channel_id=1, source_target_pairs={{0,1},{3,2},{1,0},{2,3},{4,5},{7,6},{5,4},{6,7},{8,9},{11,10},{9,8... | collective-permute-start | bytes 3145736 | tf_op jit(solution)/shard_map/ppermute | solution.py:837
  254.3 29.4 %collective-permute-start.27 = (bf16[1024,512]{1,0:T(8,128)(2,1)}, bf16[1024,512]{1,0:T(8,128)(2,1)}, u32[]{:S(2)}, u32[]{:S(2)}) collective-permute-start(bf16[1024,512]{1,0:T(8,128)(2,1)} %add_convert_fusion.12), channel_id=1, source_target_pairs={{1,2},{2,1},{5,6},{6,5},{9,10},{10,9},{13,14},{14,13},{17,18},{18,... | collective-permute-start | bytes 3145736 | tf_op jit(solution)/shard_map/ppermute | solution.py:847
  255.9 31.6 %collective-permute-start.28 = (bf16[512,2048]{1,0:T(8,128)(2,1)}, bf16[512,2048]{1,0:T(8,128)(2,1)}, u32[]{:S(2)}, u32[]{:S(2)}) collective-permute-start(bf16[512,2048]{1,0:T(8,128)(2,1)} %get-tuple-element.173), channel_id=1, source_target_pairs={{0,16},{4,20},{8,12},{12,8},{16,0},{20,4},{24,28},{28,24},{1,17},{... | collective-permute-start | bytes 6291464 | tf_op jit(solution)/shard_map/ppermute | solution.py:912
  274.4 39.8 %collective-permute-start.29 = (bf16[1024,512]{1,0:T(8,128)(2,1)}, bf16[1024,512]{1,0:T(8,128)(2,1)}, u32[]{:S(2)}, u32[]{:S(2)}) collective-permute-start(bf16[1024,512]{1,0:T(8,128)(2,1)} %fusion.1.refs_4_), channel_id=1, source_target_pairs={{0,1},{3,2},{1,0},{2,3},{4,5},{7,6},{5,4},{6,7},{8,9},{11,10},{9,8... | collective-permute-start | bytes 3145736 | tf_op jit(solution)/shard_map/ppermute | solution.py:837
  281.9 37.3 %collective-permute-start.31 = (bf16[1024,512]{1,0:T(8,128)(2,1)}, bf16[1024,512]{1,0:T(8,128)(2,1)}, u32[]{:S(2)}, u32[]{:S(2)}) collective-permute-start(bf16[1024,512]{1,0:T(8,128)(2,1)} %add_convert_fusion.10), channel_id=1, source_target_pairs={{1,2},{2,1},{5,6},{6,5},{9,10},{10,9},{13,14},{14,13},{17,18},{18,... | collective-permute-start | bytes 3145736 | tf_op jit(solution)/shard_map/ppermute | solution.py:847
  286.8 63.8 %collective-permute-start.34 = (bf16[1024,512]{1,0:T(8,128)(2,1)}, bf16[1024,512]{1,0:T(8,128)(2,1)}, u32[]{:S(2)}, u32[]{:S(2)}) collective-permute-start(bf16[1024,512]{1,0:T(8,128)(2,1)} %fusion.2.refs_2_), channel_id=1, source_target_pairs={{0,1},{3,2},{1,0},{2,3},{4,5},{7,6},{5,4},{6,7},{8,9},{11,10},{9,8... | collective-permute-start | bytes 3145736 | tf_op jit(solution)/shard_map/ppermute | solution.py:837
  292.6 32.4 %collective-permute-start.30 = (bf16[256,2048]{1,0:T(8,128)(2,1)}, bf16[256,2048]{1,0:T(8,128)(2,1)}, u32[]{:S(2)}, u32[]{:S(2)}) collective-permute-start(bf16[256,2048]{1,0:T(8,128)(2,1)} %get-tuple-element.183), channel_id=1, source_target_pairs={{0,4},{4,0},{8,24},{12,28},{16,20},{20,16},{24,8},{28,12},{1,5},{5... | collective-permute-start | bytes 3145736 | tf_op jit(solution)/shard_map/ppermute | solution.py:912
  314.1 40.8 %copy-start = (bf16[1024,512]{1,0:T(8,128)(2,1)}, bf16[1024,512]{1,0:T(8,128)(2,1)S(1)}, u32[]{:S(2)}) copy-start(bf16[1024,512]{1,0:T(8,128)(2,1)S(1)} %get-tuple-element.201) | copy-start | bytes 3145732
  317.4 37.5 %collective-permute-start.35 = (bf16[1024,512]{1,0:T(8,128)(2,1)}, bf16[1024,512]{1,0:T(8,128)(2,1)}, u32[]{:S(2)}, u32[]{:S(2)}) collective-permute-start(bf16[1024,512]{1,0:T(8,128)(2,1)} %add_convert_fusion.8), channel_id=1, source_target_pairs={{1,2},{2,1},{5,6},{6,5},{9,10},{10,9},{13,14},{14,13},{17,18},{18,... | collective-permute-start | bytes 3145736 | tf_op jit(solution)/shard_map/ppermute | solution.py:847
  322.8 11.6 %collective-permute-start.32 = (f32[13824]{0:T(1024)}, f32[13824]{0:T(1024)}, u32[]{:S(2)}, u32[]{:S(2)}) collective-permute-start(f32[13824]{0:T(1024)} %pad_maximum_fusion.1), channel_id=1, source_target_pairs={{0,8},{8,0},{16,24},{24,16},{1,9},{9,1},{17,25},{25,17},{2,10},{10... | collective-permute-start | bytes 165896 | tf_op jit(solution)/shard_map/ppermute | solution.py:869
  322.8 51.9 %collective-permute-start.37 = (bf16[1024,512]{1,0:T(8,128)(2,1)}, bf16[1024,512]{1,0:T(8,128)(2,1)}, u32[]{:S(2)}, u32[]{:S(2)}) collective-permute-start(bf16[1024,512]{1,0:T(8,128)(2,1)} %fusion.3.refs_6_), channel_id=1, source_target_pairs={{0,1},{3,2},{1,0},{2,3},{4,5},{7,6},{5,4},{6,7},{8,9},{11,10},{9,8... | collective-permute-start | bytes 3145736 | tf_op jit(solution)/shard_map/ppermute | solution.py:837
  335.9 13.2 %collective-permute-start.33 = (f32[13824]{0:T(1024)}, f32[13824]{0:T(1024)}, u32[]{:S(2)}, u32[]{:S(2)}) collective-permute-start(f32[13824]{0:T(1024)} %add.111), channel_id=1, source_target_pairs={{0,16},{16,0},{8,24},{24,8},{1,17},{17,1},{9,25},{25,9},{2,18},{18... | collective-permute-start | bytes 165896 | tf_op jit(solution)/shard_map/ppermute | solution.py:866
  337.4 22.8 %collective-permute-start.36 = (bf16[1024,2048]{1,0:T(8,128)(2,1)}, bf16[1024,2048]{1,0:T(8,128)(2,1)}, u32[]{:S(2)}, u32[]{:S(2)}) collective-permute-start(bf16[1024,2048]{1,0:T(8,128)(2,1)} %wgrad.8), channel_id=1, source_target_pairs={{0,8},{8,0},{16,24},{24,16},{1,9},{9,1},{17,25},{25,17},{2,10},{10... | collective-permute-start | bytes 12582920 | tf_op jit(solution)/shard_map/ppermute | solution.py:869
  353.1 25.9 %collective-permute-start.38 = (bf16[1024,512]{1,0:T(8,128)(2,1)}, bf16[1024,512]{1,0:T(8,128)(2,1)}, u32[]{:S(2)}, u32[]{:S(2)}) collective-permute-start(bf16[1024,512]{1,0:T(8,128)(2,1)} %add_convert_fusion.6), channel_id=1, source_target_pairs={{1,2},{2,1},{5,6},{6,5},{9,10},{10,9},{13,14},{14,13},{17,18},{18,... | collective-permute-start | bytes 3145736 | tf_op jit(solution)/shard_map/ppermute | solution.py:847
  358.1 38.3 %collective-permute-start.40 = (bf16[1024,512]{1,0:T(8,128)(2,1)}, bf16[1024,512]{1,0:T(8,128)(2,1)}, u32[]{:S(2)}, u32[]{:S(2)}) collective-permute-start(bf16[1024,512]{1,0:T(8,128)(2,1)} %fusion.4.refs_0_), channel_id=1, source_target_pairs={{0,1},{3,2},{1,0},{2,3},{4,5},{7,6},{5,4},{6,7},{8,9},{11,10},{9,8... | collective-permute-start | bytes 3145736 | tf_op jit(solution)/shard_map/ppermute | solution.py:837
  370.7 13.0 %collective-permute-start.39 = (bf16[1024,2048]{1,0:T(8,128)(2,1)}, bf16[1024,2048]{1,0:T(8,128)(2,1)}, u32[]{:S(2)}, u32[]{:S(2)}) collective-permute-start(bf16[1024,2048]{1,0:T(8,128)(2,1)} %wgrad.9), channel_id=1, source_target_pairs={{0,8},{8,0},{16,24},{24,16},{1,9},{9,1},{17,25},{25,17},{2,10},{10... | collective-permute-start | bytes 12582920 | tf_op jit(solution)/shard_map/ppermute | solution.py:869
  377.2 23.3 %collective-permute-start.41 = (bf16[1024,512]{1,0:T(8,128)(2,1)}, bf16[1024,512]{1,0:T(8,128)(2,1)}, u32[]{:S(2)}, u32[]{:S(2)}) collective-permute-start(bf16[1024,512]{1,0:T(8,128)(2,1)} %add_convert_fusion.4), channel_id=1, source_target_pairs={{1,2},{2,1},{5,6},{6,5},{9,10},{10,9},{13,14},{14,13},{17,18},{18,... | collective-permute-start | bytes 3145736 | tf_op jit(solution)/shard_map/ppermute | solution.py:847
  381.8 61.6 %collective-permute-start.43 = (bf16[1024,512]{1,0:T(8,128)(2,1)}, bf16[1024,512]{1,0:T(8,128)(2,1)}, u32[]{:S(2)}, u32[]{:S(2)}) collective-permute-start(bf16[1024,512]{1,0:T(8,128)(2,1)} %add_convert_fusion.3.refs_2_), channel_id=1, source_target_pairs={{1,0},{2,3},{5,4},{6,7},{9,8},{10,11},{13,12},{14,15},{17,16},{18,... | collective-permute-start | bytes 3145736 | tf_op jit(solution)/shard_map/ppermute | solution.py:837
  383.1 26.4 %collective-permute-start.42 = (bf16[512,2048]{1,0:T(8,128)(2,1)}, bf16[512,2048]{1,0:T(8,128)(2,1)}, u32[]{:S(2)}, u32[]{:S(2)}) collective-permute-start(bf16[512,2048]{1,0:T(8,128)(2,1)} %get-tuple-element.204), channel_id=1, source_target_pairs={{0,16},{4,20},{8,12},{12,8},{16,0},{20,4},{24,28},{28,24},{1,17},{... | collective-permute-start | bytes 6291464 | tf_op jit(solution)/shard_map/ppermute | solution.py:912
  398.9 24.8 %collective-permute-start.44 = (bf16[1024,512]{1,0:T(8,128)(2,1)}, bf16[1024,512]{1,0:T(8,128)(2,1)}, u32[]{:S(2)}, u32[]{:S(2)}) collective-permute-start(bf16[1024,512]{1,0:T(8,128)(2,1)} %add_convert_fusion.2), channel_id=1, source_target_pairs={{1,2},{2,1},{5,6},{6,5},{9,10},{10,9},{13,14},{14,13},{17,18},{18,... | collective-permute-start | bytes 3145736 | tf_op jit(solution)/shard_map/ppermute | solution.py:847
  403.4 57.8 %collective-permute-start.48 = (bf16[1024,512]{1,0:T(8,128)(2,1)}, bf16[1024,512]{1,0:T(8,128)(2,1)}, u32[]{:S(2)}, u32[]{:S(2)}) collective-permute-start(bf16[1024,512]{1,0:T(8,128)(2,1)} %add_convert_fusion.1.refs_4_), channel_id=1, source_target_pairs={{1,0},{2,3},{5,4},{6,7},{9,8},{10,11},{13,12},{14,15},{17,16},{18,... | collective-permute-start | bytes 3145736 | tf_op jit(solution)/shard_map/ppermute | solution.py:837
  413.4 26.3 %collective-permute-start.46 = (bf16[256,2048]{1,0:T(8,128)(2,1)}, bf16[256,2048]{1,0:T(8,128)(2,1)}, u32[]{:S(2)}, u32[]{:S(2)}) collective-permute-start(bf16[256,2048]{1,0:T(8,128)(2,1)} %get-tuple-element.212), channel_id=1, source_target_pairs={{0,4},{4,0},{8,24},{12,28},{16,20},{20,16},{24,8},{28,12},{1,5},{5... | collective-permute-start | bytes 3145736 | tf_op jit(solution)/shard_map/ppermute | solution.py:912
  415.0 34.7 %collective-permute-start.45 = (bf16[512,2048]{1,0:T(8,128)(2,1)}, bf16[512,2048]{1,0:T(8,128)(2,1)}, u32[]{:S(2)}, u32[]{:S(2)}) collective-permute-start(bf16[512,2048]{1,0:T(8,128)(2,1)} %get-tuple-element.209), channel_id=1, source_target_pairs={{0,16},{4,20},{8,12},{12,8},{16,0},{20,4},{24,28},{28,24},{1,17},{... | collective-permute-start | bytes 6291464 | tf_op jit(solution)/shard_map/ppermute | solution.py:912
  426.5 34.7 %collective-permute-start.49 = (bf16[1024,512]{1,0:T(8,128)(2,1)}, bf16[1024,512]{1,0:T(8,128)(2,1)}, u32[]{:S(2)}, u32[]{:S(2)}) collective-permute-start(bf16[1024,512]{1,0:T(8,128)(2,1)} %add_convert_fusion.refs_6_), channel_id=1, source_target_pairs={{1,0},{2,3},{5,4},{6,7},{9,8},{10,11},{13,12},{14,15},{17,16},{18,... | collective-permute-start | bytes 3145736 | tf_op jit(solution)/shard_map/ppermute | solution.py:837
  449.7 6.1 %collective-permute-start.47 = (f32[13824]{0:T(1024)}, f32[13824]{0:T(1024)}, u32[]{:S(2)}, u32[]{:S(2)}) collective-permute-start(f32[13824]{0:T(1024)} %add.112), channel_id=1, source_target_pairs={{0,4},{4,0},{1,5},{5,1},{2,6},{6,2},{3,7},{7,3},{8,12},{12,8},{9,1... | collective-permute-start | bytes 165896 | tf_op jit(solution)/shard_map/ppermute | solution.py:872
  455.4 19.2 %collective-permute-start.51 = (bf16[256,2048]{1,0:T(8,128)(2,1)}, bf16[256,2048]{1,0:T(8,128)(2,1)}, u32[]{:S(2)}, u32[]{:S(2)}) collective-permute-start(bf16[256,2048]{1,0:T(8,128)(2,1)} %get-tuple-element.220), channel_id=1, source_target_pairs={{0,4},{4,0},{8,24},{12,28},{16,20},{20,16},{24,8},{28,12},{1,5},{5... | collective-permute-start | bytes 3145736 | tf_op jit(solution)/shard_map/ppermute | solution.py:912
  457.9 15.3 %collective-permute-start.50 = (f32[8192]{0:T(1024)}, f32[8192]{0:T(1024)}, u32[]{:S(2)}, u32[]{:S(2)}) collective-permute-start(f32[8192]{0:T(1024)} %slice.40), channel_id=1, source_target_pairs={{0,1},{1,0},{2,3},{3,2},{4,5},{5,4},{6,7},{7,6},{8,9},{9,8},{10,11... | collective-permute-start | bytes 98312 | tf_op jit(solution)/shard_map/ppermute | solution.py:945
  474.6 5.3 %collective-permute-start.52 = (f32[8192]{0:T(1024)}, f32[8192]{0:T(1024)}, u32[]{:S(2)}, u32[]{:S(2)}) collective-permute-start(f32[8192]{0:T(1024)} %add.122), channel_id=1, source_target_pairs={{0,2},{2,0},{1,3},{3,1},{4,6},{6,4},{5,7},{7,5},{8,10},{10,8},{9,1... | collective-permute-start | bytes 98312 | tf_op jit(solution)/shard_map/ppermute | solution.py:947
  (83 other events, 815.1 us)

commit v10 on v9

--- a/solution.py
+++ b/solution.py
@@ -27,7 +27,7 @@
     return pl.CostEstimate(flops=int(k * flops), bytes_accessed=int(k * nbytes), transcendentals=int(k * trans))
 
 
-def params(n, mb=30):
+def params(n, mb=21):
     return pltpu.CompilerParams(
         dimension_semantics=("arbitrary",) * n, vmem_limit_bytes=int(mb * 1024 * 1024)
     )
@@ -349,7 +349,7 @@
             jax.ShapeDtypeStruct((m, 2 * nheads * HD), F32),
             jax.ShapeDtypeStruct((nprev * m, 2 * nheads * HD), BF),
         ],
-        compiler_params=params(2, 30 if nprev == 1 else 60),
+        compiler_params=params(2, 21 if nprev == 1 else 60),
         cost_estimate=cost(12 * m * nheads * HD * (nprev + 1) * local_len, 20 * m * nheads * HD, m * nheads * (nprev + 1) * local_len),
     )(meta, q, kv, pv, dob, *tabs)
 

time: 489 us -> 479 us (0.980)
  local copies, waits for them, and re-layouts: 41.5 us -> 22 us
  waiting for transfers between devices: 85 us -> 95.1 us
    unnamed x192 -> x174, local copies, waits for them, and re-layouts: 37.6 us -> 18 us
  transfers between devices with their start and end apart: 53 -> 53, of which waited for: 12 -> 13; matrix products, arithmetic and copies ran while one was open for 13% -> 13% of each run, Pallas kernels for 44% -> 44%
where the time goes in v10:
time: 479 us; the launch traced here: 472 us
  Pallas kernels  210 us (44%)
  waiting for transfers between devices  95.1 us (20%)
  starting transfers between devices  83.7 us (17%)
  other arithmetic  59.2 us (12%)
  local copies, waits for them, and re-layouts  22 us (5%)
    ppermute x7, waiting for transfers between devices, x(): return lax.ppermute(v, 'dp', [(0, 2), (2, 0), (1, 3), (3, 1)])  53.6 us
    pallas_call x6, Pallas kernels, wgrad_call(): pl.pallas_call(functools.partial(wgrad_kernel, counts, add is not None, s...  46.8 us
    convert_element_type x11, other arithmetic, add_bf(): return lax.optimization_barrier((a.astype(F32) + b.astype(F32)).astype(BF))  30.1 us
    ppermute x6, waiting for transfers between devices, turn(): return lax.ppermute(v, ('dp', 'ctx'), pairs)  27.1 us
    ppermute x11, starting transfers between devices, send(): got = lax.ppermute(v, 'tensor', pairs)  26.9 us
    pallas_call x2, Pallas kernels, back_call(): pl.pallas_call(back_kernel, name='backn', grid_spec=pltpu.PrefetchScalarG...  23.6 us
    pallas_call x2, Pallas kernels, out_call(): pl.pallas_call(functools.partial(out_kernel, count), name='outp', grid=(4...  18.8 us
    unnamed x174, local copies, waits for them, and re-layouts  18 us
  transfers between devices with their start and end apart: 53, of which 13 were waited for; matrix products, arithmetic and copies ran while one was open for 13% of the time, Pallas kernels for 44%

profile of v10, /device:TPU:0, one launch (start us, length us, event | category | flops | bytes accessed | tf_op | source)
XLA Modules:
  0.0 471.8 jit_solution(13413163768768150722)
XLA Ops:
  4.6 3.0 collective-permute-start
  10.7 2.5 copy.32
  19.3 6.3 %norm.1 = (bf16[1024,2048]{1,0:T(8,128)(2,1)S(1)}, bf16[1024,2048]{1,0:T(8,128)(2,1)S(1)}, f32[1024,128]{1,0:T(8,128)S(1)}, f32[1,2048]{1,0:T(1,128)S(1)}) custom-call(s32[13]{0:T(128)S(1)} %concatenate.10.meta, bf16[1024,2048]{1,0:T(8,128)(2,1)S(1)} %bitcast.23, bf16[1024,2048]{1,0:T(8,128)(2,1)S(1)} %bitcast.35, f32[1,2048]{1,0:T(1,128)S(1)} %bitcast.40, ...), custom_call_target="tpu_custom_call" | custom-call | flops 629145600000 | bytes 2097152000 | tf_op jit(solution)/shard_map/norm/pallas_call | solution.py:127
  34.0 2.4 pack.3.w0.refs_0_.w10
  37.0 19.4 %collective-permute-done.3.w2.refs_1_.w12 = bf16[256,2048]{1,0:T(8,128)(2,1)S(1)} collective-permute-done((bf16[256,2048]{1,0:T(8,128)(2,1)}, bf16[256,2048]{1,0:T(8,128)(2,1)S(1)}, u32[]{:S(2)}, u32[]{:S(2)}) %collective-permute-start.3) | collective-permute-done | bytes 1048608 | tf_op jit(solution)/shard_map/ppermute | solution.py:866
  56.5 4.3 pack.4.w0.w20
  62.4 8.6 %kv.1.kv_ref = bf16[1024,1024]{1,0:T(8,128)(2,1)} custom-call(bf16[1024,2048]{1,0:T(8,128)(2,1)S(1)} %copy-done.60, bf16[512,2048]{1,0:T(8,128)(2,1)S(1)} %pack.3.w0.refs_0_.w10, bf16[256,2048]{1,0:T(8,128)(2,1)} %collective-permute-done.2.w1.refs_0_.w11, bf16[256,2048]{1,0:T(8,128)(2,1)S(1)} %collective-permute-done.3.w2.refs_1_.w12, ...), custom_call_target="tpu_custom_call" | custom-call | flops 429496729600 | bytes 1048576000 | tf_op jit(solution)/shard_map/kv/pallas_call | solution.py:183
  71.0 4.0 collective-permute-start.13
  75.0 11.7 %collective-permute-done.7.w1.w21 = bf16[256,2048]{1,0:T(8,128)(2,1)} collective-permute-done((bf16[256,2048]{1,0:T(8,128)(2,1)}, bf16[256,2048]{1,0:T(8,128)(2,1)}, u32[]{:S(2)}, u32[]{:S(2)}) %collective-permute-start.7) | collective-permute-done | bytes 1048608 | tf_op jit(solution)/shard_map/ppermute | solution.py:866
  88.3 6.9 %qd.1 = (bf16[1024,512]{1,0:T(8,128)(2,1)S(1)}, bf16[1024,512]{1,0:T(8,128)(2,1)S(1)}) custom-call(bf16[1024,2048]{1,0:T(8,128)(2,1)S(1)} %copy-done.60, bf16[1024,2048]{1,0:T(8,128)(2,1)S(1)} %copy-done.67, bf16[512,2048]{1,0:T(8,128)(2,1)S(1)} %pack.3.w0.refs_0_.w10, bf16[256,2048]{1,0:T(8,128)(2,1)} %collective-permute-done.2.w1.refs_0_.w11, ...), custom_call_target="tpu_custom_call" | custom-call | flops 440401920000 | bytes 1468006400 | tf_op jit(solution)/shard_map/qd/pallas_call | solution.py:224
  95.1 16.4 %collective-permute-done.8.w2.w22 = bf16[256,2048]{1,0:T(8,128)(2,1)} collective-permute-done((bf16[256,2048]{1,0:T(8,128)(2,1)}, bf16[256,2048]{1,0:T(8,128)(2,1)}, u32[]{:S(2)}, u32[]{:S(2)}) %collective-permute-start.8) | collective-permute-done | bytes 1048608 | tf_op jit(solution)/shard_map/ppermute | solution.py:866
  111.6 3.3 norm2.1.h2.refs_0_
  116.5 14.7 %hidden.1 = (bf16[1024,2048]{1,0:T(8,128)(2,1)S(1)}, bf16[1024,2048]{1,0:T(8,128)(2,1)S(1)}) custom-call(bf16[1024,2048]{1,0:T(8,128)(2,1)S(1)} %norm2.1.h2.refs_0_, bf16[512,2048]{1,0:T(8,128)(2,1)} %pack.4.w0.w20, bf16[256,2048]{1,0:T(8,128)(2,1)} %collective-permute-done.7.w1.w21, bf16[256,2048]{1,0:T(8,128)(2,1)} %collective-permute-done.8.w2.w22, ...), custom_call_target="tpu_custom_call" | custom-call | flops 858993459200 | bytes 2097152000 | tf_op jit(solution)/shard_map/hidden/pallas_call | solution.py:413
  131.2 4.0 pack.5.refs_2_.w0
  135.5 5.4 %collective-permute-done.15.refs_4_.w1 = bf16[256,2048]{1,0:T(8,128)(2,1)} collective-permute-done((bf16[256,2048]{1,0:T(8,128)(2,1)}, bf16[256,2048]{1,0:T(8,128)(2,1)}, u32[]{:S(2)}, u32[]{:S(2)}) %collective-permute-start.15) | collective-permute-done | bytes 1048608 | tf_op jit(solution)/shard_map/ppermute | solution.py:866
  142.4 12.2 %attn.1 = (bf16[1024,512]{1,0:T(8,128)(2,1)S(1)}, bf16[1024,512]{1,0:T(8,128)(2,1)S(1)}, f32[1024,1024]{1,0:T(8,128)S(1)}, bf16[1024,1024]{1,0:T(8,128)(2,1)}) custom-call(s32[13]{0:T(128)S(1)} %concatenate.10.meta, bf16[1024,512]{1,0:T(8,128)(2,1)S(1)} %get-tuple-element.127.q_ref, bf16[1024,1024]{1,0:T(8,128)(2,1)} %kv.1.kv_ref, ...), custom_call_target="tpu_custom_call" | custom-call | flops 644245094400 | bytes 1048576000 | tf_op jit(solution)/shard_map/attn/pallas_call | solution.py:333
  156.4 9.1 %outp.2 = (bf16[1024,512]{1,0:T(8,128)(2,1)}, bf16[1024,512]{1,0:T(8,128)(2,1)}) custom-call(bf16[1024,512]{1,0:T(8,128)(2,1)S(1)} %get-tuple-element.143.ob.refs_3_, bf16[1024,2048]{1,0:T(8,128)(2,1)S(1)} %get-tuple-element.135.gb.refs_1_, bf16[512,2048]{1,0:T(8,128)(2,1)S(1)} %copy-done.18, bf16[512,2048]{1,0:T(8,128)(2,1)S(1)} %copy-done.15, ...), custom_call_target="tpu_custom_call" | custom-call | flops 53687092 | bytes 125829 | tf_op jit(solution)/shard_map/outp/pallas_call | solution.py:479
  165.5 4.5 collective-permute-start.19
  170.2 7.3 %wgrad.6 = bf16[1024,2048]{1,0:T(8,128)(2,1)} custom-call(s32[13]{0:T(128)S(1)} %concatenate.10.meta, bf16[1024,2048]{1,0:T(8,128)(2,1)S(1)} %copy-done.68, bf16[1024,2048]{1,0:T(8,128)(2,1)S(1)} %get-tuple-element.135.gb.refs_1_), custom_call_target="tpu_custom_call" | custom-call | flops 440401920000 | bytes 1468006400 | tf_op jit(solution)/shard_map/wgrad/pallas_call | solution.py:602
  180.1 9.6 %outp.3 = (bf16[1024,512]{1,0:T(8,128)(2,1)}, bf16[1024,512]{1,0:T(8,128)(2,1)S(1)}) custom-call(bf16[1024,512]{1,0:T(8,128)(2,1)S(1)} %get-tuple-element.143.ob.refs_3_, bf16[1024,2048]{1,0:T(8,128)(2,1)S(1)} %get-tuple-element.135.gb.refs_1_, bf16[256,2048]{1,0:T(8,128)(2,1)} %collective-permute-done.2.w1.refs_0_.w11, bf16[256,2048]{1,0:T(8,128)(2,1)S(1)} %copy-done.44, ...), custom_call_target="tpu_custom_call" | custom-call | flops 536870912000 | bytes 1258291200 | tf_op jit(solution)/shard_map/outp/pallas_call | solution.py:479
  189.7 3.1 collective-permute-done.19
  192.9 2.8 add_convert_fusion.15
  199.5 12.3 %dhid.1 = (bf16[1024,2048]{1,0:T(8,128)(2,1)S(1)}, f32[1,2048]{1,0:T(1,128)S(1)}) custom-call(bf16[1024,2048]{1,0:T(8,128)(2,1)S(1)} %copy-done.69, bf16[512,2048]{1,0:T(8,128)(2,1)} %pack.5.refs_2_.w0, bf16[256,2048]{1,0:T(8,128)(2,1)} %collective-permute-done.15.refs_4_.w1, bf16[256,2048]{1,0:T(8,128)(2,1)} %collective-permute-done.16.refs_5_.w2, ...), custom_call_target="tpu_custom_call" | custom-call | flops 858993459200 | bytes 2097152000 | tf_op jit(solution)/shard_map/dhid/pallas_call | solution.py:438
  211.9 2.9 collective-permute-done.20
  214.8 2.8 add_convert_fusion.14
  219.3 7.5 %collective-permute-start.24 = (bf16[1024,512]{1,0:T(8,128)(2,1)}, bf16[1024,512]{1,0:T(8,128)(2,1)}, u32[]{:S(2)}, u32[]{:S(2)}) collective-permute-start(bf16[1024,512]{1,0:T(8,128)(2,1)} %get-tuple-element.165), channel_id=1, source_target_pairs={{0,1},{3,2},{4,5},{7,6},{8,9},{11,10},{12,13},{15,14},{16,17},{19,... | collective-permute-start | bytes 3145736 | tf_op jit(solution)/shard_map/ppermute | solution.py:837
  226.9 8.3 %wgrad.7 = (bf16[512,2048]{1,0:T(8,128)(2,1)S(1)}, bf16[512,2048]{1,0:T(8,128)(2,1)}) custom-call(s32[13]{0:T(128)S(1)} %concatenate.10.meta, bf16[1024,2048]{1,0:T(8,128)(2,1)S(1)} %copy-done.69, bf16[1024,2048]{1,0:T(8,128)(2,1)S(1)} %get-tuple-element.135.gb.refs_1_, bf16[1024,2048]{1,0:T(8,128)(2,1)} %collective-permute-done.21.refs_2_), custom_call_target="tpu_custom_call" | custom-call | flops 440401920000 | bytes 1468006400 | tf_op jit(solution)/shard_map/wgrad/pallas_call | solution.py:602
  235.3 3.8 join.1
  239.1 4.1 fusion.refs_0_
  243.3 6.0 %collective-permute-done.24 = bf16[1024,512]{1,0:T(8,128)(2,1)} collective-permute-done((bf16[1024,512]{1,0:T(8,128)(2,1)}, bf16[1024,512]{1,0:T(8,128)(2,1)}, u32[]{:S(2)}, u32[]{:S(2)}) %collective-permute-start.24) | collective-permute-done | bytes 1048608 | tf_op jit(solution)/shard_map/ppermute | solution.py:837
  249.4 2.8 add_convert_fusion.12
  254.4 11.8 %backn.2 = (bf16[1024,512]{1,0:T(8,128)(2,1)S(1)}, bf16[1024,512]{1,0:T(8,128)(2,1)S(1)}, f32[4,2048]{1,0:T(4,128)S(1)}) custom-call(s32[13]{0:T(128)S(1)} %copy-done.34, bf16[1024,1536]{1,0:T(8,128)(2,1)S(1)} %get-tuple-element.162.dqkv.refs_1_, bf16[1024,2048]{1,0:T(8,128)(2,1)S(1)} %get-tuple-element.155.du.refs_1_, ...), custom_call_target="tpu_custom_call", output_to_operand_aliasing={{2}: (13, {})} | custom-call | flops 751619276800 | bytes 1887436800 | tf_op jit(solution)/shard_map/backn/pallas_call | solution.py:523
  266.3 3.7 fusion.1.refs_4_
  270.0 3.5 collective-permute-start.29
  274.1 2.5 add_convert_fusion.10
  278.5 3.1 fusion.2.refs_2_
  283.3 4.8 %hsum.3 = (f32[256,2048]{1,0:T(8,128)S(1)}, bf16[256,2048]{1,0:T(8,128)(2,1)}) custom-call(bf16[512,2048]{1,0:T(8,128)(2,1)S(1)} %copy-done.58, bf16[512,2048]{1,0:T(8,128)(2,1)} %collective-permute-done.28.got), custom_call_target="tpu_custom_call" | custom-call | flops 220200960000 | bytes 734003200 | tf_op jit(solution)/shard_map/hsum/pallas_call | solution.py:652
  288.1 9.7 %collective-permute-start.30 = (bf16[256,2048]{1,0:T(8,128)(2,1)}, bf16[256,2048]{1,0:T(8,128)(2,1)}, u32[]{:S(2)}, u32[]{:S(2)}) collective-permute-start(bf16[256,2048]{1,0:T(8,128)(2,1)} %get-tuple-element.183), channel_id=1, source_target_pairs={{0,4},{4,0},{8,24},{12,28},{16,20},{20,16},{24,8},{28,12},{1,5},{5... | collective-permute-start | bytes 3145736 | tf_op jit(solution)/shard_map/ppermute | solution.py:912
  297.8 11.8 %backn.3 = (bf16[1024,512]{1,0:T(8,128)(2,1)S(1)}, bf16[1024,512]{1,0:T(8,128)(2,1)S(1)}, f32[4,2048]{1,0:T(4,128)S(1)}) custom-call(s32[13]{0:T(128)S(1)} %copy-done.35, bf16[1024,1536]{1,0:T(8,128)(2,1)S(1)} %copy-done.63, bf16[1024,2048]{1,0:T(8,128)(2,1)S(1)} %copy-done.72, bf16[512,2048]{1,0:T(8,128)(2,1)S(1)} %copy-done.16, ...), custom_call_target="tpu_custom_call", output_to_operand_aliasing={{2}: (13, {})} | custom-call | flops 751619276800 | bytes 1887436800 | tf_op jit(solution)/shard_map/backn/pallas_call | solution.py:523
  309.7 3.2 add_convert_fusion.8
  314.7 2.9 fusion.3.refs_6_
  322.7 7.3 %wgrad.8 = bf16[1024,2048]{1,0:T(8,128)(2,1)} custom-call(s32[13]{0:T(128)S(1)} %copy-done.35, bf16[1024,2048]{1,0:T(8,128)(2,1)S(1)} %copy-done.55, bf16[1024,2048]{1,0:T(8,128)(2,1)S(1)} %copy-done.73), custom_call_target="tpu_custom_call" | custom-call | flops 440401920000 | bytes 1468006400 | tf_op jit(solution)/shard_map/wgrad/pallas_call | solution.py:602
  333.0 7.3 %wgrad.9 = bf16[1024,2048]{1,0:T(8,128)(2,1)} custom-call(s32[13]{0:T(128)S(1)} %copy-done.35, bf16[1024,2048]{1,0:T(8,128)(2,1)S(1)} %copy-done.61, bf16[1024,1536]{1,0:T(8,128)(2,1)S(1)} %copy-done.64, bf16[1024,2048]{1,0:T(8,128)(2,1)S(1)} %copy-done.70, bf16[1024,512]{1,0:T(8,128)(2,1)S(1)} %copy-done.21), custom_call_target="tpu_custom_call" | custom-call | flops 503316480000 | bytes 1677721600 | tf_op jit(solution)/shard_map/wgrad/pallas_call | solution.py:602
  341.8 2.5 add_convert_fusion.6
  346.2 3.1 fusion.4.refs_0_
  350.5 8.3 %wgrad.10 = (bf16[512,2048]{1,0:T(8,128)(2,1)S(1)}, bf16[512,2048]{1,0:T(8,128)(2,1)}) custom-call(s32[13]{0:T(128)S(1)} %copy-done.35, bf16[1024,2048]{1,0:T(8,128)(2,1)S(1)} %copy-done.56, bf16[1024,2048]{1,0:T(8,128)(2,1)S(1)} %copy-done.73, bf16[1024,2048]{1,0:T(8,128)(2,1)} %collective-permute-done.36.refs_2_), custom_call_target="tpu_custom_call" | custom-call | flops 440401920000 | bytes 1468006400 | tf_op jit(solution)/shard_map/wgrad/pallas_call | solution.py:602
  358.8 4.1 lsum.3
  362.9 2.5 add_convert_fusion.4
  367.2 2.8 add_convert_fusion.3.refs_2_
  372.0 8.3 %wgrad.11 = (bf16[512,2048]{1,0:T(8,128)(2,1)S(1)}, bf16[512,2048]{1,0:T(8,128)(2,1)}) custom-call(s32[13]{0:T(128)S(1)} %copy-done.35, bf16[1024,2048]{1,0:T(8,128)(2,1)S(1)} %copy-done.61, bf16[1024,1536]{1,0:T(8,128)(2,1)S(1)} %copy-done.65, bf16[1024,2048]{1,0:T(8,128)(2,1)S(1)} %copy-done.70, bf16[1024,512]{1,0:T(8,128)(2,1)S(1)} %copy-done.21, ...), custom_call_target="tpu_custom_call" | custom-call | flops 503316480000 | bytes 1677721600 | tf_op jit(solution)/shard_map/wgrad/pallas_call | solution.py:602
  380.2 2.5 add_convert_fusion.2
  384.4 2.8 add_convert_fusion.1.refs_4_
  388.6 9.2 %collective-permute-done.42.got = bf16[512,2048]{1,0:T(8,128)(2,1)} collective-permute-done((bf16[512,2048]{1,0:T(8,128)(2,1)}, bf16[512,2048]{1,0:T(8,128)(2,1)}, u32[]{:S(2)}, u32[]{:S(2)}) %collective-permute-start.42) | collective-permute-done | bytes 2097184 | tf_op jit(solution)/shard_map/ppermute | solution.py:912
  397.7 3.9 hsum.4
  403.9 4.1 bout.2.refs_8_
  407.9 4.1 bout.3
  412.0 2.8 add_convert_fusion.refs_6_
  416.4 11.6 %collective-permute-done.46.got = bf16[256,2048]{1,0:T(8,128)(2,1)} collective-permute-done((bf16[256,2048]{1,0:T(8,128)(2,1)}, bf16[256,2048]{1,0:T(8,128)(2,1)}, u32[]{:S(2)}, u32[]{:S(2)}) %collective-permute-start.46) | collective-permute-done | bytes 1048608 | tf_op jit(solution)/shard_map/ppermute | solution.py:912
  428.0 3.7 lsum.4
  431.6 6.2 %collective-permute-done.45.got = bf16[512,2048]{1,0:T(8,128)(2,1)} collective-permute-done((bf16[512,2048]{1,0:T(8,128)(2,1)}, bf16[512,2048]{1,0:T(8,128)(2,1)}, u32[]{:S(2)}, u32[]{:S(2)}) %collective-permute-start.45) | collective-permute-done | bytes 2097184 | tf_op jit(solution)/shard_map/ppermute | solution.py:912
  439.6 4.0 hsum.5
  446.1 4.8 %collective-permute-start.50 = (f32[8192]{0:T(1024)}, f32[8192]{0:T(1024)}, u32[]{:S(2)}, u32[]{:S(2)}) collective-permute-start(f32[8192]{0:T(1024)} %slice.40), channel_id=1, source_target_pairs={{0,1},{1,0},{2,3},{3,2},{4,5},{5,4},{6,7},{7,6},{8,9},{9,8},{10,11... | collective-permute-start | bytes 98312 | tf_op jit(solution)/shard_map/ppermute | solution.py:945
  450.9 9.4 %igrad.1 = bf16[1024,2048]{1,0:T(8,128)(2,1)} custom-call(s32[13]{0:T(128)S(1)} %copy-done.35, bf16[1024,2048]{1,0:T(8,128)(2,1)S(1)} %bitcast.29, bf16[1024,2048]{1,0:T(8,128)(2,1)S(1)} %bitcast.36, f32[1024,128]{1,0:T(8,128)S(1)} %copy-done.76, bf16[1024,512]{1,0:T(8,128)(2,1)} %fusion.4.refs_0_, bf16[1024,512]{1,0:T(8,128)(2,1)} %collective-permute-done.40.refs_1_, ...), custom_call_target="tpu_custom_call" | custom-call | flops 503316480000 | bytes 1677721600 | tf_op jit(solution)/shard_map/igrad/pallas_call | solution.py:775
  464.4 4.0 lsum.5
  (286 shorter events, 81.4 us)
Async XLA Ops:
  4.6 27.3 %collective-permute-start = (bf16[256,2048]{1,0:T(8,128)(2,1)}, bf16[256,2048]{1,0:T(8,128)(2,1)}, u32[]{:S(2)}, u32[]{:S(2)}) collective-permute-start(bf16[256,2048]{1,0:T(8,128)(2,1)} %pad_maximum_fusion.refs_0_), channel_id=1, source_target_pairs={{0,4},{4,0},{1,5},{5,1},{2,6},{6,2},{3,7},{7,3},{8,12},{12,8},{9,1... | collective-permute-start | bytes 3145736 | tf_op jit(solution)/shard_map/ppermute | solution.py:872
  7.6 24.9 %collective-permute-start.2 = (bf16[256,2048]{1,0:T(8,128)(2,1)}, bf16[256,2048]{1,0:T(8,128)(2,1)}, u32[]{:S(2)}, u32[]{:S(2)}) collective-permute-start(bf16[256,2048]{1,0:T(8,128)(2,1)} %pad_maximum_fusion.refs_0_), channel_id=1, source_target_pairs={{0,16},{16,0},{8,24},{24,8},{1,17},{17,1},{9,25},{25,9},{2,18},{18... | collective-permute-start | bytes 3145736 | tf_op jit(solution)/shard_map/ppermute | solution.py:866
  10.2 46.3 %collective-permute-start.1 = (bf16[256,2048]{1,0:T(8,128)(2,1)}, bf16[256,2048]{1,0:T(8,128)(2,1)}, u32[]{:S(2)}, u32[]{:S(2)}) collective-permute-start(bf16[256,2048]{1,0:T(8,128)(2,1)} %convert_element_type.174.refs_0_), channel_id=1, source_target_pairs={{0,4},{4,0},{1,5},{5,1},{2,6},{6,2},{3,7},{7,3},{8,12},{12,8},{9,1... | collective-permute-start | bytes 3145736 | tf_op jit(solution)/shard_map/ppermute | solution.py:872
  13.2 118.0 %collective-permute-start.12 = (bf16[256,2048]{1,0:T(8,128)(2,1)}, bf16[256,2048]{1,0:T(8,128)(2,1)}, u32[]{:S(2)}, u32[]{:S(2)}) collective-permute-start(bf16[256,2048]{1,0:T(8,128)(2,1)} %bitcast.21.refs_0_), channel_id=1, source_target_pairs={{0,4},{4,0},{1,5},{5,1},{2,6},{6,2},{3,7},{7,3},{8,12},{12,8},{9,1... | collective-permute-start | bytes 3145736 | tf_op jit(solution)/shard_map/ppermute | solution.py:872
  14.9 212.0 %copy-start.33 = (s32[13]{0:T(128)}, s32[13]{0:T(128)S(1)}, u32[]{:S(2)}) copy-start(s32[13]{0:T(128)S(1)} %concatenate.10.meta) | copy-start | bytes 160
  29.6 224.8 %copy-start.74 = (f32[1024,128]{1,0:T(8,128)}, f32[1024,128]{1,0:T(8,128)S(1)}, u32[]{:S(2)}) copy-start(f32[1024,128]{1,0:T(8,128)S(1)} %get-tuple-element.129.st_ref) | copy-start | bytes 1572868
  30.7 57.4 %copy-start.22 = (f32[512,128]{1,0:T(8,128)}, f32[512,128]{1,0:T(8,128)S(1)}, u32[]{:S(2)}) copy-start(f32[512,128]{1,0:T(8,128)S(1)} %get-tuple-element.230.s2) | copy-start | bytes 786436
  30.7 57.4 %copy-start.25 = (f32[512,128]{1,0:T(8,128)}, f32[512,128]{1,0:T(8,128)S(1)}, u32[]{:S(2)}) copy-start(f32[512,128]{1,0:T(8,128)S(1)} %get-tuple-element.231.s1) | copy-start | bytes 786436
  30.7 57.4 %copy-start.28 = (f32[512,128]{1,0:T(8,128)}, f32[512,128]{1,0:T(8,128)S(1)}, u32[]{:S(2)}) copy-start(f32[512,128]{1,0:T(8,128)S(1)} %get-tuple-element.232.cosf) | copy-start | bytes 786436
  32.5 24.0 %collective-permute-start.3 = (bf16[256,2048]{1,0:T(8,128)(2,1)}, bf16[256,2048]{1,0:T(8,128)(2,1)S(1)}, u32[]{:S(2)}, u32[]{:S(2)}) collective-permute-start(bf16[256,2048]{1,0:T(8,128)(2,1)} %collective-permute-done.refs_1_), channel_id=1, source_target_pairs={{0,16},{16,0},{8,24},{24,8},{1,17},{17,1},{9,25},{25,9},{2,18},{18... | collective-permute-start | bytes 3145736 | tf_op jit(solution)/shard_map/ppermute | solution.py:866
  36.4 51.7 %copy-start.17 = (bf16[512,2048]{1,0:T(8,128)(2,1)}, bf16[512,2048]{1,0:T(8,128)(2,1)S(1)}, u32[]{:S(2)}) copy-start(bf16[512,2048]{1,0:T(8,128)(2,1)S(1)} %pack.3.w0.refs_0_.w10) | copy-start | bytes 6291460
  36.5 25.9 %collective-permute-start.4 = (bf16[512,2048]{1,0:T(8,128)(2,1)S(1)}, bf16[512,2048]{1,0:T(8,128)(2,1)S(1)}, u32[]{:S(2)}, u32[]{:S(2)}) collective-permute-start(bf16[512,2048]{1,0:T(8,128)(2,1)S(1)} %pack.3.w0.refs_0_.w10), channel_id=1, source_target_pairs={{0,8},{8,0},{16,24},{24,16},{1,9},{9,1},{17,25},{25,17},{2,10},{10... | collective-permute-start | bytes 6291464 | tf_op jit(solution)/shard_map/ppermute | solution.py:869
  36.5 24.3 %collective-permute-start.5 = (bf16[256,2048]{1,0:T(8,128)(2,1)}, bf16[256,2048]{1,0:T(8,128)(2,1)S(1)}, u32[]{:S(2)}, u32[]{:S(2)}) collective-permute-start(bf16[256,2048]{1,0:T(8,128)(2,1)} %collective-permute-done.2.w1.refs_0_.w11), channel_id=1, source_target_pairs={{0,8},{8,0},{16,24},{24,16},{1,9},{9,1},{17,25},{25,17},{2,10},{10... | collective-permute-start | bytes 3145736 | tf_op jit(solution)/shard_map/ppermute | solution.py:869
  56.5 31.7 %copy-start.43 = (bf16[256,2048]{1,0:T(8,128)(2,1)}, bf16[256,2048]{1,0:T(8,128)(2,1)S(1)}, u32[]{:S(2)}) copy-start(bf16[256,2048]{1,0:T(8,128)(2,1)S(1)} %collective-permute-done.3.w2.refs_1_.w12) | copy-start | bytes 3145732
  56.5 5.9 %collective-permute-start.6 = (bf16[256,2048]{1,0:T(8,128)(2,1)S(1)}, bf16[256,2048]{1,0:T(8,128)(2,1)S(1)}, u32[]{:S(2)}, u32[]{:S(2)}) collective-permute-start(bf16[256,2048]{1,0:T(8,128)(2,1)S(1)} %collective-permute-done.3.w2.refs_1_.w12), channel_id=1, source_target_pairs={{0,8},{8,0},{16,24},{24,16},{1,9},{9,1},{17,25},{25,17},{2,10},{10... | collective-permute-start | bytes 3145736 | tf_op jit(solution)/shard_map/ppermute | solution.py:869
  60.8 54.1 %collective-permute-start.9 = (bf16[512,2048]{1,0:T(8,128)(2,1)}, bf16[512,2048]{1,0:T(8,128)(2,1)}, u32[]{:S(2)}, u32[]{:S(2)}) collective-permute-start(bf16[512,2048]{1,0:T(8,128)(2,1)} %pack.4.w0.w20), channel_id=1, source_target_pairs={{0,8},{8,0},{16,24},{24,16},{1,9},{9,1},{17,25},{25,17},{2,10},{10... | collective-permute-start | bytes 6291464 | tf_op jit(solution)/shard_map/ppermute | solution.py:869
  60.9 119.2 %copy-start.38 = (bf16[256,2048]{1,0:T(8,128)(2,1)}, bf16[256,2048]{1,0:T(8,128)(2,1)S(1)}, u32[]{:S(2)}) copy-start(bf16[256,2048]{1,0:T(8,128)(2,1)S(1)} %collective-permute-done.5.w4.refs_2_.w11) | copy-start | bytes 3145732
  60.9 25.8 %collective-permute-start.7 = (bf16[256,2048]{1,0:T(8,128)(2,1)}, bf16[256,2048]{1,0:T(8,128)(2,1)}, u32[]{:S(2)}, u32[]{:S(2)}) collective-permute-start(bf16[256,2048]{1,0:T(8,128)(2,1)} %convert_element_type.174.refs_0_), channel_id=1, source_target_pairs={{0,16},{16,0},{8,24},{24,8},{1,17},{17,1},{9,25},{25,9},{2,18},{18... | collective-permute-start | bytes 3145736 | tf_op jit(solution)/shard_map/ppermute | solution.py:866
  71.0 71.3 %collective-permute-start.13 = (bf16[1024,1024]{1,0:T(8,128)(2,1)}, bf16[1024,1024]{1,0:T(8,128)(2,1)}, u32[]{:S(2)}, u32[]{:S(2)}) collective-permute-start(bf16[1024,1024]{1,0:T(8,128)(2,1)} %kv.1.kv_ref), channel_id=1, source_target_pairs={{0,4},{1,5},{2,6},{3,7},{8,12},{9,13},{10,14},{11,15},{16,20},{17,... | collective-permute-start | bytes 6291464 | tf_op jit(solution)/shard_map/ppermute | solution.py:929
  86.7 24.9 %collective-permute-start.8 = (bf16[256,2048]{1,0:T(8,128)(2,1)}, bf16[256,2048]{1,0:T(8,128)(2,1)}, u32[]{:S(2)}, u32[]{:S(2)}) collective-permute-start(bf16[256,2048]{1,0:T(8,128)(2,1)} %collective-permute-done.1.refs_1_), channel_id=1, source_target_pairs={{0,16},{16,0},{8,24},{24,8},{1,17},{17,1},{9,25},{25,9},{2,18},{18... | collective-permute-start | bytes 3145736 | tf_op jit(solution)/shard_map/ppermute | solution.py:866
  88.2 28.3 %collective-permute-start.10 = (bf16[256,2048]{1,0:T(8,128)(2,1)}, bf16[256,2048]{1,0:T(8,128)(2,1)}, u32[]{:S(2)}, u32[]{:S(2)}) collective-permute-start(bf16[256,2048]{1,0:T(8,128)(2,1)} %collective-permute-done.7.w1.w21), channel_id=1, source_target_pairs={{0,8},{8,0},{16,24},{24,16},{1,9},{9,1},{17,25},{25,17},{2,10},{10... | collective-permute-start | bytes 3145736 | tf_op jit(solution)/shard_map/ppermute | solution.py:869
  111.6 4.9 %collective-permute-start.11 = (bf16[256,2048]{1,0:T(8,128)(2,1)}, bf16[256,2048]{1,0:T(8,128)(2,1)}, u32[]{:S(2)}, u32[]{:S(2)}) collective-permute-start(bf16[256,2048]{1,0:T(8,128)(2,1)} %collective-permute-done.8.w2.w22), channel_id=1, source_target_pairs={{0,8},{8,0},{16,24},{24,16},{1,9},{9,1},{17,25},{25,17},{2,10},{10... | collective-permute-start | bytes 3145736 | tf_op jit(solution)/shard_map/ppermute | solution.py:869
  114.9 25.9 %collective-permute-start.15 = (bf16[256,2048]{1,0:T(8,128)(2,1)}, bf16[256,2048]{1,0:T(8,128)(2,1)}, u32[]{:S(2)}, u32[]{:S(2)}) collective-permute-start(bf16[256,2048]{1,0:T(8,128)(2,1)} %bitcast.21.refs_0_), channel_id=1, source_target_pairs={{0,16},{16,0},{8,24},{24,8},{1,17},{17,1},{9,25},{25,9},{2,18},{18... | collective-permute-start | bytes 3145736 | tf_op jit(solution)/shard_map/ppermute | solution.py:866
  135.2 21.2 %collective-permute-start.14 = (bf16[512,2048]{1,0:T(8,128)(2,1)}, bf16[512,2048]{1,0:T(8,128)(2,1)}, u32[]{:S(2)}, u32[]{:S(2)}) collective-permute-start(bf16[512,2048]{1,0:T(8,128)(2,1)} %pack.5.refs_2_.w0), channel_id=1, source_target_pairs={{0,8},{8,0},{16,24},{24,16},{1,9},{9,1},{17,25},{25,17},{2,10},{10... | collective-permute-start | bytes 6291464 | tf_op jit(solution)/shard_map/ppermute | solution.py:869
  140.8 29.2 %collective-permute-start.16 = (bf16[256,2048]{1,0:T(8,128)(2,1)}, bf16[256,2048]{1,0:T(8,128)(2,1)}, u32[]{:S(2)}, u32[]{:S(2)}) collective-permute-start(bf16[256,2048]{1,0:T(8,128)(2,1)} %collective-permute-done.12.refs_1_), channel_id=1, source_target_pairs={{0,16},{16,0},{8,24},{24,8},{1,17},{17,1},{9,25},{25,9},{2,18},{18... | collective-permute-start | bytes 3145736 | tf_op jit(solution)/shard_map/ppermute | solution.py:866
  154.6 23.2 %collective-permute-start.17 = (bf16[256,2048]{1,0:T(8,128)(2,1)}, bf16[256,2048]{1,0:T(8,128)(2,1)}, u32[]{:S(2)}, u32[]{:S(2)}) collective-permute-start(bf16[256,2048]{1,0:T(8,128)(2,1)} %collective-permute-done.15.refs_4_.w1), channel_id=1, source_target_pairs={{0,8},{8,0},{16,24},{24,16},{1,9},{9,1},{17,25},{25,17},{2,10},{10... | collective-permute-start | bytes 3145736 | tf_op jit(solution)/shard_map/ppermute | solution.py:869
  154.6 80.6 %collective-permute-start.22 = (bf16[1024,1024]{1,0:T(8,128)(2,1)}, bf16[1024,1024]{1,0:T(8,128)(2,1)}, u32[]{:S(2)}, u32[]{:S(2)}) collective-permute-start(bf16[1024,1024]{1,0:T(8,128)(2,1)} %get-tuple-element.161), channel_id=1, source_target_pairs={{4,0},{5,1},{6,2},{7,3},{12,8},{13,9},{14,10},{15,11},{20,16},{21,... | collective-permute-start | bytes 6291464 | tf_op jit(solution)/shard_map/ppermute | solution.py:932
  165.5 27.3 %collective-permute-start.19 = (bf16[1024,512]{1,0:T(8,128)(2,1)}, bf16[1024,512]{1,0:T(8,128)(2,1)}, u32[]{:S(2)}, u32[]{:S(2)}) collective-permute-start(bf16[1024,512]{1,0:T(8,128)(2,1)} %get-tuple-element.149), channel_id=1, source_target_pairs={{0,1},{3,2},{4,5},{7,6},{8,9},{11,10},{12,13},{15,14},{16,17},{19,... | collective-permute-start | bytes 3145736 | tf_op jit(solution)/shard_map/ppermute | solution.py:837
  170.0 10.1 %collective-permute-start.18 = (bf16[256,2048]{1,0:T(8,128)(2,1)}, bf16[256,2048]{1,0:T(8,128)(2,1)}, u32[]{:S(2)}, u32[]{:S(2)}) collective-permute-start(bf16[256,2048]{1,0:T(8,128)(2,1)} %collective-permute-done.16.refs_5_.w2), channel_id=1, source_target_pairs={{0,8},{8,0},{16,24},{24,16},{1,9},{9,1},{17,25},{25,17},{2,10},{10... | collective-permute-start | bytes 3145736 | tf_op jit(solution)/shard_map/ppermute | solution.py:869
  177.5 49.4 %collective-permute-start.21 = (bf16[1024,2048]{1,0:T(8,128)(2,1)}, bf16[1024,2048]{1,0:T(8,128)(2,1)}, u32[]{:S(2)}, u32[]{:S(2)}) collective-permute-start(bf16[1024,2048]{1,0:T(8,128)(2,1)} %wgrad.6), channel_id=1, source_target_pairs={{0,8},{8,0},{16,24},{24,16},{1,9},{9,1},{17,25},{25,17},{2,10},{10... | collective-permute-start | bytes 12582920 | tf_op jit(solution)/shard_map/ppermute | solution.py:869
  177.8 37.0 %collective-permute-start.20 = (bf16[1024,512]{1,0:T(8,128)(2,1)}, bf16[1024,512]{1,0:T(8,128)(2,1)}, u32[]{:S(2)}, u32[]{:S(2)}) collective-permute-start(bf16[1024,512]{1,0:T(8,128)(2,1)} %get-tuple-element.156), channel_id=1, source_target_pairs={{0,1},{3,2},{4,5},{7,6},{8,9},{11,10},{12,13},{15,14},{16,17},{19,... | collective-permute-start | bytes 3145736 | tf_op jit(solution)/shard_map/ppermute | solution.py:837
  189.7 49.4 %copy-start.4 = (bf16[1024,512]{1,0:T(8,128)(2,1)}, bf16[1024,512]{1,0:T(8,128)(2,1)S(1)}, u32[]{:S(2)}) copy-start(bf16[1024,512]{1,0:T(8,128)(2,1)S(1)} %get-tuple-element.169) | copy-start | bytes 3145732
  195.7 43.4 %collective-permute-start.23 = (bf16[1024,512]{1,0:T(8,128)(2,1)}, bf16[1024,512]{1,0:T(8,128)(2,1)}, u32[]{:S(2)}, u32[]{:S(2)}) collective-permute-start(bf16[1024,512]{1,0:T(8,128)(2,1)} %add_convert_fusion.15), channel_id=1, source_target_pairs={{1,2},{2,1},{5,6},{6,5},{9,10},{10,9},{13,14},{14,13},{17,18},{18,... | collective-permute-start | bytes 3145736 | tf_op jit(solution)/shard_map/ppermute | solution.py:847
  211.9 42.5 %copy-start.71 = (bf16[1024,2048]{1,0:T(8,128)(2,1)}, bf16[1024,2048]{1,0:T(8,128)(2,1)S(1)}, u32[]{:S(2)}) copy-start(bf16[1024,2048]{1,0:T(8,128)(2,1)S(1)} %get-tuple-element.155.du.refs_1_) | copy-start | bytes 12582916
  217.6 48.6 %collective-permute-start.25 = (bf16[1024,512]{1,0:T(8,128)(2,1)}, bf16[1024,512]{1,0:T(8,128)(2,1)}, u32[]{:S(2)}, u32[]{:S(2)}) collective-permute-start(bf16[1024,512]{1,0:T(8,128)(2,1)} %add_convert_fusion.14), channel_id=1, source_target_pairs={{1,2},{2,1},{5,6},{6,5},{9,10},{10,9},{13,14},{14,13},{17,18},{18,... | collective-permute-start | bytes 3145736 | tf_op jit(solution)/shard_map/ppermute | solution.py:847
  219.3 30.0 %collective-permute-start.24 = (bf16[1024,512]{1,0:T(8,128)(2,1)}, bf16[1024,512]{1,0:T(8,128)(2,1)}, u32[]{:S(2)}, u32[]{:S(2)}) collective-permute-start(bf16[1024,512]{1,0:T(8,128)(2,1)} %get-tuple-element.165), channel_id=1, source_target_pairs={{0,1},{3,2},{4,5},{7,6},{8,9},{11,10},{12,13},{15,14},{16,17},{19,... | collective-permute-start | bytes 3145736 | tf_op jit(solution)/shard_map/ppermute | solution.py:837
  243.3 30.9 %collective-permute-start.26 = (bf16[1024,512]{1,0:T(8,128)(2,1)}, bf16[1024,512]{1,0:T(8,128)(2,1)}, u32[]{:S(2)}, u32[]{:S(2)}) collective-permute-start(bf16[1024,512]{1,0:T(8,128)(2,1)} %fusion.refs_0_), channel_id=1, source_target_pairs={{0,1},{3,2},{1,0},{2,3},{4,5},{7,6},{5,4},{6,7},{8,9},{11,10},{9,8... | collective-permute-start | bytes 3145736 | tf_op jit(solution)/shard_map/ppermute | solution.py:837
  252.2 26.3 %collective-permute-start.27 = (bf16[1024,512]{1,0:T(8,128)(2,1)}, bf16[1024,512]{1,0:T(8,128)(2,1)}, u32[]{:S(2)}, u32[]{:S(2)}) collective-permute-start(bf16[1024,512]{1,0:T(8,128)(2,1)} %add_convert_fusion.12), channel_id=1, source_target_pairs={{1,2},{2,1},{5,6},{6,5},{9,10},{10,9},{13,14},{14,13},{17,18},{18,... | collective-permute-start | bytes 3145736 | tf_op jit(solution)/shard_map/ppermute | solution.py:847
  253.8 29.3 %collective-permute-start.28 = (bf16[512,2048]{1,0:T(8,128)(2,1)}, bf16[512,2048]{1,0:T(8,128)(2,1)}, u32[]{:S(2)}, u32[]{:S(2)}) collective-permute-start(bf16[512,2048]{1,0:T(8,128)(2,1)} %get-tuple-element.173), channel_id=1, source_target_pairs={{0,16},{4,20},{8,12},{12,8},{16,0},{20,4},{24,28},{28,24},{1,17},{... | collective-permute-start | bytes 6291464 | tf_op jit(solution)/shard_map/ppermute | solution.py:912
  270.0 39.7 %collective-permute-start.29 = (bf16[1024,512]{1,0:T(8,128)(2,1)}, bf16[1024,512]{1,0:T(8,128)(2,1)}, u32[]{:S(2)}, u32[]{:S(2)}) collective-permute-start(bf16[1024,512]{1,0:T(8,128)(2,1)} %fusion.1.refs_4_), channel_id=1, source_target_pairs={{0,1},{3,2},{1,0},{2,3},{4,5},{7,6},{5,4},{6,7},{8,9},{11,10},{9,8... | collective-permute-start | bytes 3145736 | tf_op jit(solution)/shard_map/ppermute | solution.py:837
  276.6 38.0 %collective-permute-start.31 = (bf16[1024,512]{1,0:T(8,128)(2,1)}, bf16[1024,512]{1,0:T(8,128)(2,1)}, u32[]{:S(2)}, u32[]{:S(2)}) collective-permute-start(bf16[1024,512]{1,0:T(8,128)(2,1)} %add_convert_fusion.10), channel_id=1, source_target_pairs={{1,2},{2,1},{5,6},{6,5},{9,10},{10,9},{13,14},{14,13},{17,18},{18,... | collective-permute-start | bytes 3145736 | tf_op jit(solution)/shard_map/ppermute | solution.py:847
  281.6 60.2 %collective-permute-start.34 = (bf16[1024,512]{1,0:T(8,128)(2,1)}, bf16[1024,512]{1,0:T(8,128)(2,1)}, u32[]{:S(2)}, u32[]{:S(2)}) collective-permute-start(bf16[1024,512]{1,0:T(8,128)(2,1)} %fusion.2.refs_2_), channel_id=1, source_target_pairs={{0,1},{3,2},{1,0},{2,3},{4,5},{7,6},{5,4},{6,7},{8,9},{11,10},{9,8... | collective-permute-start | bytes 3145736 | tf_op jit(solution)/shard_map/ppermute | solution.py:837
  288.1 32.4 %collective-permute-start.30 = (bf16[256,2048]{1,0:T(8,128)(2,1)}, bf16[256,2048]{1,0:T(8,128)(2,1)}, u32[]{:S(2)}, u32[]{:S(2)}) collective-permute-start(bf16[256,2048]{1,0:T(8,128)(2,1)} %get-tuple-element.183), channel_id=1, source_target_pairs={{0,4},{4,0},{8,24},{12,28},{16,20},{20,16},{24,8},{28,12},{1,5},{5... | collective-permute-start | bytes 3145736 | tf_op jit(solution)/shard_map/ppermute | solution.py:912
  309.6 36.6 %copy-start = (bf16[1024,512]{1,0:T(8,128)(2,1)}, bf16[1024,512]{1,0:T(8,128)(2,1)S(1)}, u32[]{:S(2)}) copy-start(bf16[1024,512]{1,0:T(8,128)(2,1)S(1)} %get-tuple-element.201) | copy-start | bytes 3145732
  312.9 33.3 %collective-permute-start.35 = (bf16[1024,512]{1,0:T(8,128)(2,1)}, bf16[1024,512]{1,0:T(8,128)(2,1)}, u32[]{:S(2)}, u32[]{:S(2)}) collective-permute-start(bf16[1024,512]{1,0:T(8,128)(2,1)} %add_convert_fusion.8), channel_id=1, source_target_pairs={{1,2},{2,1},{5,6},{6,5},{9,10},{10,9},{13,14},{14,13},{17,18},{18,... | collective-permute-start | bytes 3145736 | tf_op jit(solution)/shard_map/ppermute | solution.py:847
  318.3 11.8 %collective-permute-start.32 = (f32[13824]{0:T(1024)}, f32[13824]{0:T(1024)}, u32[]{:S(2)}, u32[]{:S(2)}) collective-permute-start(f32[13824]{0:T(1024)} %pad_maximum_fusion.1), channel_id=1, source_target_pairs={{0,8},{8,0},{16,24},{24,16},{1,9},{9,1},{17,25},{25,17},{2,10},{10... | collective-permute-start | bytes 165896 | tf_op jit(solution)/shard_map/ppermute | solution.py:869
  318.3 44.6 %collective-permute-start.37 = (bf16[1024,512]{1,0:T(8,128)(2,1)}, bf16[1024,512]{1,0:T(8,128)(2,1)}, u32[]{:S(2)}, u32[]{:S(2)}) collective-permute-start(bf16[1024,512]{1,0:T(8,128)(2,1)} %fusion.3.refs_6_), channel_id=1, source_target_pairs={{0,1},{3,2},{1,0},{2,3},{4,5},{7,6},{5,4},{6,7},{8,9},{11,10},{9,8... | collective-permute-start | bytes 3145736 | tf_op jit(solution)/shard_map/ppermute | solution.py:837
  331.5 8.8 %collective-permute-start.33 = (f32[13824]{0:T(1024)}, f32[13824]{0:T(1024)}, u32[]{:S(2)}, u32[]{:S(2)}) collective-permute-start(f32[13824]{0:T(1024)} %add.111), channel_id=1, source_target_pairs={{0,16},{16,0},{8,24},{24,8},{1,17},{17,1},{9,25},{25,9},{2,18},{18... | collective-permute-start | bytes 165896 | tf_op jit(solution)/shard_map/ppermute | solution.py:866
  333.0 17.5 %collective-permute-start.36 = (bf16[1024,2048]{1,0:T(8,128)(2,1)}, bf16[1024,2048]{1,0:T(8,128)(2,1)}, u32[]{:S(2)}, u32[]{:S(2)}) collective-permute-start(bf16[1024,2048]{1,0:T(8,128)(2,1)} %wgrad.8), channel_id=1, source_target_pairs={{0,8},{8,0},{16,24},{24,16},{1,9},{9,1},{17,25},{25,17},{2,10},{10... | collective-permute-start | bytes 12582920 | tf_op jit(solution)/shard_map/ppermute | solution.py:869
  344.3 22.9 %collective-permute-start.38 = (bf16[1024,512]{1,0:T(8,128)(2,1)}, bf16[1024,512]{1,0:T(8,128)(2,1)}, u32[]{:S(2)}, u32[]{:S(2)}) collective-permute-start(bf16[1024,512]{1,0:T(8,128)(2,1)} %add_convert_fusion.6), channel_id=1, source_target_pairs={{1,2},{2,1},{5,6},{6,5},{9,10},{10,9},{13,14},{14,13},{17,18},{18,... | collective-permute-start | bytes 3145736 | tf_op jit(solution)/shard_map/ppermute | solution.py:847
  349.4 30.9 %collective-permute-start.40 = (bf16[1024,512]{1,0:T(8,128)(2,1)}, bf16[1024,512]{1,0:T(8,128)(2,1)}, u32[]{:S(2)}, u32[]{:S(2)}) collective-permute-start(bf16[1024,512]{1,0:T(8,128)(2,1)} %fusion.4.refs_0_), channel_id=1, source_target_pairs={{0,1},{3,2},{1,0},{2,3},{4,5},{7,6},{5,4},{6,7},{8,9},{11,10},{9,8... | collective-permute-start | bytes 3145736 | tf_op jit(solution)/shard_map/ppermute | solution.py:837
  358.8 13.1 %collective-permute-start.39 = (bf16[1024,2048]{1,0:T(8,128)(2,1)}, bf16[1024,2048]{1,0:T(8,128)(2,1)}, u32[]{:S(2)}, u32[]{:S(2)}) collective-permute-start(bf16[1024,2048]{1,0:T(8,128)(2,1)} %wgrad.9), channel_id=1, source_target_pairs={{0,8},{8,0},{16,24},{24,16},{1,9},{9,1},{17,25},{25,17},{2,10},{10... | collective-permute-start | bytes 12582920 | tf_op jit(solution)/shard_map/ppermute | solution.py:869
  365.4 19.0 %collective-permute-start.41 = (bf16[1024,512]{1,0:T(8,128)(2,1)}, bf16[1024,512]{1,0:T(8,128)(2,1)}, u32[]{:S(2)}, u32[]{:S(2)}) collective-permute-start(bf16[1024,512]{1,0:T(8,128)(2,1)} %add_convert_fusion.4), channel_id=1, source_target_pairs={{1,2},{2,1},{5,6},{6,5},{9,10},{10,9},{13,14},{14,13},{17,18},{18,... | collective-permute-start | bytes 3145736 | tf_op jit(solution)/shard_map/ppermute | solution.py:847
  370.0 61.6 %collective-permute-start.43 = (bf16[1024,512]{1,0:T(8,128)(2,1)}, bf16[1024,512]{1,0:T(8,128)(2,1)}, u32[]{:S(2)}, u32[]{:S(2)}) collective-permute-start(bf16[1024,512]{1,0:T(8,128)(2,1)} %add_convert_fusion.3.refs_2_), channel_id=1, source_target_pairs={{1,0},{2,3},{5,4},{6,7},{9,8},{10,11},{13,12},{14,15},{17,16},{18,... | collective-permute-start | bytes 3145736 | tf_op jit(solution)/shard_map/ppermute | solution.py:837
  371.3 26.4 %collective-permute-start.42 = (bf16[512,2048]{1,0:T(8,128)(2,1)}, bf16[512,2048]{1,0:T(8,128)(2,1)}, u32[]{:S(2)}, u32[]{:S(2)}) collective-permute-start(bf16[512,2048]{1,0:T(8,128)(2,1)} %get-tuple-element.204), channel_id=1, source_target_pairs={{0,16},{4,20},{8,12},{12,8},{16,0},{20,4},{24,28},{28,24},{1,17},{... | collective-permute-start | bytes 6291464 | tf_op jit(solution)/shard_map/ppermute | solution.py:912
  382.7 29.3 %collective-permute-start.44 = (bf16[1024,512]{1,0:T(8,128)(2,1)}, bf16[1024,512]{1,0:T(8,128)(2,1)}, u32[]{:S(2)}, u32[]{:S(2)}) collective-permute-start(bf16[1024,512]{1,0:T(8,128)(2,1)} %add_convert_fusion.2), channel_id=1, source_target_pairs={{1,2},{2,1},{5,6},{6,5},{9,10},{10,9},{13,14},{14,13},{17,18},{18,... | collective-permute-start | bytes 3145736 | tf_op jit(solution)/shard_map/ppermute | solution.py:847
  387.3 63.6 %collective-permute-start.48 = (bf16[1024,512]{1,0:T(8,128)(2,1)}, bf16[1024,512]{1,0:T(8,128)(2,1)}, u32[]{:S(2)}, u32[]{:S(2)}) collective-permute-start(bf16[1024,512]{1,0:T(8,128)(2,1)} %add_convert_fusion.1.refs_4_), channel_id=1, source_target_pairs={{1,0},{2,3},{5,4},{6,7},{9,8},{10,11},{13,12},{14,15},{17,16},{18,... | collective-permute-start | bytes 3145736 | tf_op jit(solution)/shard_map/ppermute | solution.py:837
  401.6 26.3 %collective-permute-start.46 = (bf16[256,2048]{1,0:T(8,128)(2,1)}, bf16[256,2048]{1,0:T(8,128)(2,1)}, u32[]{:S(2)}, u32[]{:S(2)}) collective-permute-start(bf16[256,2048]{1,0:T(8,128)(2,1)} %get-tuple-element.212), channel_id=1, source_target_pairs={{0,4},{4,0},{8,24},{12,28},{16,20},{20,16},{24,8},{28,12},{1,5},{5... | collective-permute-start | bytes 3145736 | tf_op jit(solution)/shard_map/ppermute | solution.py:912
  403.3 34.6 %collective-permute-start.45 = (bf16[512,2048]{1,0:T(8,128)(2,1)}, bf16[512,2048]{1,0:T(8,128)(2,1)}, u32[]{:S(2)}, u32[]{:S(2)}) collective-permute-start(bf16[512,2048]{1,0:T(8,128)(2,1)} %get-tuple-element.209), channel_id=1, source_target_pairs={{0,16},{4,20},{8,12},{12,8},{16,0},{20,4},{24,28},{28,24},{1,17},{... | collective-permute-start | bytes 6291464 | tf_op jit(solution)/shard_map/ppermute | solution.py:912
  414.8 36.0 %collective-permute-start.49 = (bf16[1024,512]{1,0:T(8,128)(2,1)}, bf16[1024,512]{1,0:T(8,128)(2,1)}, u32[]{:S(2)}, u32[]{:S(2)}) collective-permute-start(bf16[1024,512]{1,0:T(8,128)(2,1)} %add_convert_fusion.refs_6_), channel_id=1, source_target_pairs={{1,0},{2,3},{5,4},{6,7},{9,8},{10,11},{13,12},{14,15},{17,16},{18,... | collective-permute-start | bytes 3145736 | tf_op jit(solution)/shard_map/ppermute | solution.py:837
  437.9 6.1 %collective-permute-start.47 = (f32[13824]{0:T(1024)}, f32[13824]{0:T(1024)}, u32[]{:S(2)}, u32[]{:S(2)}) collective-permute-start(f32[13824]{0:T(1024)} %add.112), channel_id=1, source_target_pairs={{0,4},{4,0},{1,5},{5,1},{2,6},{6,2},{3,7},{7,3},{8,12},{12,8},{9,1... | collective-permute-start | bytes 165896 | tf_op jit(solution)/shard_map/ppermute | solution.py:872
  443.6 20.8 %collective-permute-start.51 = (bf16[256,2048]{1,0:T(8,128)(2,1)}, bf16[256,2048]{1,0:T(8,128)(2,1)}, u32[]{:S(2)}, u32[]{:S(2)}) collective-permute-start(bf16[256,2048]{1,0:T(8,128)(2,1)} %get-tuple-element.220), channel_id=1, source_target_pairs={{0,4},{4,0},{8,24},{12,28},{16,20},{20,16},{24,8},{28,12},{1,5},{5... | collective-permute-start | bytes 3145736 | tf_op jit(solution)/shard_map/ppermute | solution.py:912
  446.1 16.8 %collective-permute-start.50 = (f32[8192]{0:T(1024)}, f32[8192]{0:T(1024)}, u32[]{:S(2)}, u32[]{:S(2)}) collective-permute-start(f32[8192]{0:T(1024)} %slice.40), channel_id=1, source_target_pairs={{0,1},{1,0},{2,3},{3,2},{4,5},{5,4},{6,7},{7,6},{8,9},{9,8},{10,11... | collective-permute-start | bytes 98312 | tf_op jit(solution)/shard_map/ppermute | solution.py:945
  464.2 5.3 %collective-permute-start.52 = (f32[8192]{0:T(1024)}, f32[8192]{0:T(1024)}, u32[]{:S(2)}, u32[]{:S(2)}) collective-permute-start(f32[8192]{0:T(1024)} %add.122), channel_id=1, source_target_pairs={{0,2},{2,0},{1,3},{3,1},{4,6},{6,4},{5,7},{7,5},{8,10},{10,8},{9,1... | collective-permute-start | bytes 98312 | tf_op jit(solution)/shard_map/ppermute | solution.py:947
  (74 other events, 815.0 us)

commit v11 on v10

--- a/solution.py
+++ b/solution.py
@@ -27,7 +27,7 @@
     return pl.CostEstimate(flops=int(k * flops), bytes_accessed=int(k * nbytes), transcendentals=int(k * trans))
 
 
-def params(n, mb=21):
+def params(n, mb=18):
     return pltpu.CompilerParams(
         dimension_semantics=("arbitrary",) * n, vmem_limit_bytes=int(mb * 1024 * 1024)
     )
@@ -349,7 +349,7 @@
             jax.ShapeDtypeStruct((m, 2 * nheads * HD), F32),
             jax.ShapeDtypeStruct((nprev * m, 2 * nheads * HD), BF),
         ],
-        compiler_params=params(2, 21 if nprev == 1 else 60),
+        compiler_params=params(2, 18 if nprev == 1 else 60),
         cost_estimate=cost(12 * m * nheads * HD * (nprev + 1) * local_len, 20 * m * nheads * HD, m * nheads * (nprev + 1) * local_len),
     )(meta, q, kv, pv, dob, *tabs)
 

time: 479 us -> 477 us (level)
  waiting for transfers between devices: 95.1 us -> 88.7 us
    unnamed x174 -> x178, local copies, waits for them, and re-layouts: 18 us -> 22.1 us
  transfers between devices with their start and end apart: 53 -> 53, of which waited for: 13 -> 13; matrix products, arithmetic and copies ran while one was open for 13% -> 13% of each run, Pallas kernels for 44% -> 45%
where the time goes in v11:
time: 477 us; the launch traced here: 470 us
  Pallas kernels  210 us (44%)
  waiting for transfers between devices  88.7 us (19%)
  starting transfers between devices  83.2 us (17%)
  other arithmetic  59.4 us (12%)
  local copies, waits for them, and re-layouts  26.1 us (5%)
    ppermute x7, waiting for transfers between devices, x(): return lax.ppermute(v, 'dp', [(0, 2), (2, 0), (1, 3), (3, 1)])  53.5 us
    pallas_call x6, Pallas kernels, wgrad_call(): pl.pallas_call(functools.partial(wgrad_kernel, counts, add is not None, s...  46.8 us
    convert_element_type x11, other arithmetic, add_bf(): return lax.optimization_barrier((a.astype(F32) + b.astype(F32)).astype(BF))  30.2 us
    ppermute x11, starting transfers between devices, send(): got = lax.ppermute(v, 'tensor', pairs)  26.8 us
    pallas_call x2, Pallas kernels, back_call(): pl.pallas_call(back_kernel, name='backn', grid_spec=pltpu.PrefetchScalarG...  23.7 us
    ppermute x6, waiting for transfers between devices, turn(): return lax.ppermute(v, ('dp', 'ctx'), pairs)  23 us
    unnamed x178, local copies, waits for them, and re-layouts  22.1 us
    pallas_call x2, Pallas kernels, out_call(): pl.pallas_call(functools.partial(out_kernel, count), name='outp', grid=(4...  18.9 us
  transfers between devices with their start and end apart: 53, of which 13 were waited for; matrix products, arithmetic and copies ran while one was open for 13% of the time, Pallas kernels for 45%

profile of v11, /device:TPU:0, one launch (start us, length us, event | category | flops | bytes accessed | tf_op | source)
XLA Modules:
  0.0 469.8 jit_solution(16072738228000778402)
XLA Ops:
  4.6 3.0 collective-permute-start
  10.7 2.6 copy.32
  19.3 6.3 %norm.1 = (bf16[1024,2048]{1,0:T(8,128)(2,1)S(1)}, bf16[1024,2048]{1,0:T(8,128)(2,1)S(1)}, f32[1024,128]{1,0:T(8,128)S(1)}, f32[1,2048]{1,0:T(1,128)S(1)}) custom-call(s32[13]{0:T(128)S(1)} %concatenate.10.meta, bf16[1024,2048]{1,0:T(8,128)(2,1)S(1)} %bitcast.23, bf16[1024,2048]{1,0:T(8,128)(2,1)S(1)} %bitcast.35, f32[1,2048]{1,0:T(1,128)S(1)} %bitcast.40, ...), custom_call_target="tpu_custom_call" | custom-call | flops 629145600000 | bytes 2097152000 | tf_op jit(solution)/shard_map/norm/pallas_call | solution.py:127
  34.0 2.4 pack.3.w0.refs_0_.w10
  37.0 19.4 %collective-permute-done.3.w2.refs_1_.w12 = bf16[256,2048]{1,0:T(8,128)(2,1)S(1)} collective-permute-done((bf16[256,2048]{1,0:T(8,128)(2,1)}, bf16[256,2048]{1,0:T(8,128)(2,1)S(1)}, u32[]{:S(2)}, u32[]{:S(2)}) %collective-permute-start.3) | collective-permute-done | bytes 1048608 | tf_op jit(solution)/shard_map/ppermute | solution.py:866
  56.5 4.2 pack.4.w0.w20
  62.4 8.5 %kv.1.kv_ref = bf16[1024,1024]{1,0:T(8,128)(2,1)} custom-call(bf16[1024,2048]{1,0:T(8,128)(2,1)S(1)} %copy-done.60, bf16[512,2048]{1,0:T(8,128)(2,1)S(1)} %pack.3.w0.refs_0_.w10, bf16[256,2048]{1,0:T(8,128)(2,1)} %collective-permute-done.2.w1.refs_0_.w11, bf16[256,2048]{1,0:T(8,128)(2,1)S(1)} %collective-permute-done.3.w2.refs_1_.w12, ...), custom_call_target="tpu_custom_call" | custom-call | flops 429496729600 | bytes 1048576000 | tf_op jit(solution)/shard_map/kv/pallas_call | solution.py:183
  70.9 4.0 collective-permute-start.13
  74.9 11.7 %collective-permute-done.7.w1.w21 = bf16[256,2048]{1,0:T(8,128)(2,1)} collective-permute-done((bf16[256,2048]{1,0:T(8,128)(2,1)}, bf16[256,2048]{1,0:T(8,128)(2,1)}, u32[]{:S(2)}, u32[]{:S(2)}) %collective-permute-start.7) | collective-permute-done | bytes 1048608 | tf_op jit(solution)/shard_map/ppermute | solution.py:866
  88.2 6.9 %qd.1 = (bf16[1024,512]{1,0:T(8,128)(2,1)S(1)}, bf16[1024,512]{1,0:T(8,128)(2,1)S(1)}) custom-call(bf16[1024,2048]{1,0:T(8,128)(2,1)S(1)} %copy-done.60, bf16[1024,2048]{1,0:T(8,128)(2,1)S(1)} %copy-done.68, bf16[512,2048]{1,0:T(8,128)(2,1)S(1)} %pack.3.w0.refs_0_.w10, bf16[256,2048]{1,0:T(8,128)(2,1)} %collective-permute-done.2.w1.refs_0_.w11, ...), custom_call_target="tpu_custom_call" | custom-call | flops 440401920000 | bytes 1468006400 | tf_op jit(solution)/shard_map/qd/pallas_call | solution.py:224
  95.1 16.4 %collective-permute-done.8.w2.w22 = bf16[256,2048]{1,0:T(8,128)(2,1)} collective-permute-done((bf16[256,2048]{1,0:T(8,128)(2,1)}, bf16[256,2048]{1,0:T(8,128)(2,1)}, u32[]{:S(2)}, u32[]{:S(2)}) %collective-permute-start.8) | collective-permute-done | bytes 1048608 | tf_op jit(solution)/shard_map/ppermute | solution.py:866
  111.6 3.2 norm2.1.h2.refs_0_
  116.4 14.7 %hidden.1 = (bf16[1024,2048]{1,0:T(8,128)(2,1)S(1)}, bf16[1024,2048]{1,0:T(8,128)(2,1)S(1)}) custom-call(bf16[1024,2048]{1,0:T(8,128)(2,1)S(1)} %norm2.1.h2.refs_0_, bf16[512,2048]{1,0:T(8,128)(2,1)} %pack.4.w0.w20, bf16[256,2048]{1,0:T(8,128)(2,1)} %collective-permute-done.7.w1.w21, bf16[256,2048]{1,0:T(8,128)(2,1)} %collective-permute-done.8.w2.w22, ...), custom_call_target="tpu_custom_call" | custom-call | flops 858993459200 | bytes 2097152000 | tf_op jit(solution)/shard_map/hidden/pallas_call | solution.py:413
  131.2 4.0 pack.5.refs_2_.w0
  135.5 5.3 %collective-permute-done.15.refs_4_.w1 = bf16[256,2048]{1,0:T(8,128)(2,1)} collective-permute-done((bf16[256,2048]{1,0:T(8,128)(2,1)}, bf16[256,2048]{1,0:T(8,128)(2,1)}, u32[]{:S(2)}, u32[]{:S(2)}) %collective-permute-start.15) | collective-permute-done | bytes 1048608 | tf_op jit(solution)/shard_map/ppermute | solution.py:866
  142.3 12.3 %attn.1 = (bf16[1024,512]{1,0:T(8,128)(2,1)S(1)}, bf16[1024,512]{1,0:T(8,128)(2,1)S(1)}, f32[1024,1024]{1,0:T(8,128)S(1)}, bf16[1024,1024]{1,0:T(8,128)(2,1)}) custom-call(s32[13]{0:T(128)S(1)} %concatenate.10.meta, bf16[1024,512]{1,0:T(8,128)(2,1)S(1)} %get-tuple-element.127.q_ref, bf16[1024,1024]{1,0:T(8,128)(2,1)} %kv.1.kv_ref, ...), custom_call_target="tpu_custom_call" | custom-call | flops 644245094400 | bytes 1048576000 | tf_op jit(solution)/shard_map/attn/pallas_call | solution.py:333
  156.4 9.2 %outp.2 = (bf16[1024,512]{1,0:T(8,128)(2,1)}, bf16[1024,512]{1,0:T(8,128)(2,1)}) custom-call(bf16[1024,512]{1,0:T(8,128)(2,1)S(1)} %get-tuple-element.143.ob.refs_3_, bf16[1024,2048]{1,0:T(8,128)(2,1)S(1)} %get-tuple-element.135.gb.refs_1_, bf16[512,2048]{1,0:T(8,128)(2,1)S(1)} %copy-done.18, bf16[512,2048]{1,0:T(8,128)(2,1)S(1)} %copy-done.15, ...), custom_call_target="tpu_custom_call" | custom-call | flops 53687092 | bytes 125829 | tf_op jit(solution)/shard_map/outp/pallas_call | solution.py:479
  165.7 4.5 collective-permute-start.19
  170.5 7.3 %wgrad.6 = bf16[1024,2048]{1,0:T(8,128)(2,1)} custom-call(s32[13]{0:T(128)S(1)} %concatenate.10.meta, bf16[1024,2048]{1,0:T(8,128)(2,1)S(1)} %copy-done.69, bf16[1024,2048]{1,0:T(8,128)(2,1)S(1)} %get-tuple-element.135.gb.refs_1_), custom_call_target="tpu_custom_call" | custom-call | flops 440401920000 | bytes 1468006400 | tf_op jit(solution)/shard_map/wgrad/pallas_call | solution.py:602
  180.2 9.7 %outp.3 = (bf16[1024,512]{1,0:T(8,128)(2,1)}, bf16[1024,512]{1,0:T(8,128)(2,1)S(1)}) custom-call(bf16[1024,512]{1,0:T(8,128)(2,1)S(1)} %get-tuple-element.143.ob.refs_3_, bf16[1024,2048]{1,0:T(8,128)(2,1)S(1)} %get-tuple-element.135.gb.refs_1_, bf16[256,2048]{1,0:T(8,128)(2,1)} %collective-permute-done.2.w1.refs_0_.w11, bf16[256,2048]{1,0:T(8,128)(2,1)S(1)} %copy-done.44, ...), custom_call_target="tpu_custom_call" | custom-call | flops 536870912000 | bytes 1258291200 | tf_op jit(solution)/shard_map/outp/pallas_call | solution.py:479
  190.0 3.0 collective-permute-done.19
  193.0 2.8 add_convert_fusion.15
  199.6 12.4 %dhid.1 = (bf16[1024,2048]{1,0:T(8,128)(2,1)S(1)}, f32[1,2048]{1,0:T(1,128)S(1)}) custom-call(bf16[1024,2048]{1,0:T(8,128)(2,1)S(1)} %copy-done.70, bf16[512,2048]{1,0:T(8,128)(2,1)} %pack.5.refs_2_.w0, bf16[256,2048]{1,0:T(8,128)(2,1)} %collective-permute-done.15.refs_4_.w1, bf16[256,2048]{1,0:T(8,128)(2,1)} %collective-permute-done.16.refs_5_.w2, ...), custom_call_target="tpu_custom_call" | custom-call | flops 858993459200 | bytes 2097152000 | tf_op jit(solution)/shard_map/dhid/pallas_call | solution.py:438
  212.0 3.0 collective-permute-done.20
  215.1 2.8 add_convert_fusion.14
  219.5 7.6 %collective-permute-start.24 = (bf16[1024,512]{1,0:T(8,128)(2,1)}, bf16[1024,512]{1,0:T(8,128)(2,1)}, u32[]{:S(2)}, u32[]{:S(2)}) collective-permute-start(bf16[1024,512]{1,0:T(8,128)(2,1)} %get-tuple-element.165), channel_id=1, source_target_pairs={{0,1},{3,2},{4,5},{7,6},{8,9},{11,10},{12,13},{15,14},{16,17},{19,... | collective-permute-start | bytes 3145736 | tf_op jit(solution)/shard_map/ppermute | solution.py:837
  229.3 8.3 %wgrad.7 = (bf16[512,2048]{1,0:T(8,128)(2,1)S(1)}, bf16[512,2048]{1,0:T(8,128)(2,1)}) custom-call(s32[13]{0:T(128)S(1)} %concatenate.10.meta, bf16[1024,2048]{1,0:T(8,128)(2,1)S(1)} %copy-done.71, bf16[1024,2048]{1,0:T(8,128)(2,1)S(1)} %get-tuple-element.135.gb.refs_1_, bf16[1024,2048]{1,0:T(8,128)(2,1)} %collective-permute-done.21.refs_2_), custom_call_target="tpu_custom_call" | custom-call | flops 440401920000 | bytes 1468006400 | tf_op jit(solution)/shard_map/wgrad/pallas_call | solution.py:602
  237.6 3.9 join.1
  241.6 4.1 fusion.refs_0_
  245.8 3.8 collective-permute-done.24
  249.6 2.8 add_convert_fusion.12
  254.7 11.9 %backn.2 = (bf16[1024,512]{1,0:T(8,128)(2,1)S(1)}, bf16[1024,512]{1,0:T(8,128)(2,1)S(1)}, f32[4,2048]{1,0:T(4,128)S(1)}) custom-call(s32[13]{0:T(128)S(1)} %copy-done.34, bf16[1024,1536]{1,0:T(8,128)(2,1)S(1)} %get-tuple-element.162.dqkv.refs_1_, bf16[1024,2048]{1,0:T(8,128)(2,1)S(1)} %get-tuple-element.155.du.refs_1_, ...), custom_call_target="tpu_custom_call", output_to_operand_aliasing={{2}: (13, {})} | custom-call | flops 751619276800 | bytes 1887436800 | tf_op jit(solution)/shard_map/backn/pallas_call | solution.py:523
  266.6 3.7 fusion.1.refs_4_
  270.3 3.4 collective-permute-start.29
  274.4 2.5 add_convert_fusion.10
  278.8 3.1 fusion.2.refs_2_
  283.6 4.8 %hsum.3 = (f32[256,2048]{1,0:T(8,128)S(1)}, bf16[256,2048]{1,0:T(8,128)(2,1)}) custom-call(bf16[512,2048]{1,0:T(8,128)(2,1)S(1)} %copy-done.58, bf16[512,2048]{1,0:T(8,128)(2,1)} %collective-permute-done.28.got), custom_call_target="tpu_custom_call" | custom-call | flops 220200960000 | bytes 734003200 | tf_op jit(solution)/shard_map/hsum/pallas_call | solution.py:652
  288.4 9.6 %collective-permute-start.30 = (bf16[256,2048]{1,0:T(8,128)(2,1)}, bf16[256,2048]{1,0:T(8,128)(2,1)}, u32[]{:S(2)}, u32[]{:S(2)}) collective-permute-start(bf16[256,2048]{1,0:T(8,128)(2,1)} %get-tuple-element.183), channel_id=1, source_target_pairs={{0,4},{4,0},{8,24},{12,28},{16,20},{20,16},{24,8},{28,12},{1,5},{5... | collective-permute-start | bytes 3145736 | tf_op jit(solution)/shard_map/ppermute | solution.py:912
  298.0 11.8 %backn.3 = (bf16[1024,512]{1,0:T(8,128)(2,1)S(1)}, bf16[1024,512]{1,0:T(8,128)(2,1)S(1)}, f32[4,2048]{1,0:T(4,128)S(1)}) custom-call(s32[13]{0:T(128)S(1)} %copy-done.35, bf16[1024,1536]{1,0:T(8,128)(2,1)S(1)} %copy-done.64, bf16[1024,2048]{1,0:T(8,128)(2,1)S(1)} %copy-done.75, bf16[512,2048]{1,0:T(8,128)(2,1)S(1)} %copy-done.16, ...), custom_call_target="tpu_custom_call", output_to_operand_aliasing={{2}: (13, {})} | custom-call | flops 751619276800 | bytes 1887436800 | tf_op jit(solution)/shard_map/backn/pallas_call | solution.py:523
  309.9 3.2 add_convert_fusion.8
  315.0 3.0 fusion.3.refs_6_
  320.7 7.3 %wgrad.8 = bf16[1024,2048]{1,0:T(8,128)(2,1)} custom-call(s32[13]{0:T(128)S(1)} %copy-done.35, bf16[1024,2048]{1,0:T(8,128)(2,1)S(1)} %copy-done.55, bf16[1024,2048]{1,0:T(8,128)(2,1)S(1)} %copy-done.75), custom_call_target="tpu_custom_call" | custom-call | flops 440401920000 | bytes 1468006400 | tf_op jit(solution)/shard_map/wgrad/pallas_call | solution.py:602
  331.0 7.4 %wgrad.9 = bf16[1024,2048]{1,0:T(8,128)(2,1)} custom-call(s32[13]{0:T(128)S(1)} %copy-done.35, bf16[1024,2048]{1,0:T(8,128)(2,1)S(1)} %copy-done.61, bf16[1024,1536]{1,0:T(8,128)(2,1)S(1)} %copy-done.65, bf16[1024,2048]{1,0:T(8,128)(2,1)S(1)} %copy-done.72, bf16[1024,512]{1,0:T(8,128)(2,1)S(1)} %copy-done.21), custom_call_target="tpu_custom_call" | custom-call | flops 503316480000 | bytes 1677721600 | tf_op jit(solution)/shard_map/wgrad/pallas_call | solution.py:602
  339.9 2.5 add_convert_fusion.6
  344.3 3.1 fusion.4.refs_0_
  348.7 8.3 %wgrad.10 = (bf16[512,2048]{1,0:T(8,128)(2,1)S(1)}, bf16[512,2048]{1,0:T(8,128)(2,1)}) custom-call(s32[13]{0:T(128)S(1)} %copy-done.35, bf16[1024,2048]{1,0:T(8,128)(2,1)S(1)} %copy-done.56, bf16[1024,2048]{1,0:T(8,128)(2,1)S(1)} %copy-done.75, bf16[1024,2048]{1,0:T(8,128)(2,1)} %collective-permute-done.36.refs_2_), custom_call_target="tpu_custom_call" | custom-call | flops 440401920000 | bytes 1468006400 | tf_op jit(solution)/shard_map/wgrad/pallas_call | solution.py:602
  357.0 4.1 lsum.3
  361.1 2.6 add_convert_fusion.4
  365.5 2.8 add_convert_fusion.3.refs_2_
  374.2 8.3 %wgrad.11 = (bf16[512,2048]{1,0:T(8,128)(2,1)S(1)}, bf16[512,2048]{1,0:T(8,128)(2,1)}) custom-call(s32[13]{0:T(128)S(1)} %copy-done.35, bf16[1024,2048]{1,0:T(8,128)(2,1)S(1)} %copy-done.62, bf16[1024,1536]{1,0:T(8,128)(2,1)S(1)} %copy-done.66, bf16[1024,2048]{1,0:T(8,128)(2,1)S(1)} %copy-done.73, bf16[1024,512]{1,0:T(8,128)(2,1)S(1)} %copy-done.21, ...), custom_call_target="tpu_custom_call" | custom-call | flops 503316480000 | bytes 1677721600 | tf_op jit(solution)/shard_map/wgrad/pallas_call | solution.py:602
  382.5 2.6 add_convert_fusion.2
  386.7 2.8 add_convert_fusion.1.refs_4_
  390.8 5.1 %collective-permute-done.42.got = bf16[512,2048]{1,0:T(8,128)(2,1)} collective-permute-done((bf16[512,2048]{1,0:T(8,128)(2,1)}, bf16[512,2048]{1,0:T(8,128)(2,1)}, u32[]{:S(2)}, u32[]{:S(2)}) %collective-permute-start.42) | collective-permute-done | bytes 2097184 | tf_op jit(solution)/shard_map/ppermute | solution.py:912
  396.0 3.9 hsum.4
  402.1 4.1 bout.2.refs_8_
  406.1 4.1 bout.3
  410.2 2.8 add_convert_fusion.refs_6_
  414.6 11.6 %collective-permute-done.46.got = bf16[256,2048]{1,0:T(8,128)(2,1)} collective-permute-done((bf16[256,2048]{1,0:T(8,128)(2,1)}, bf16[256,2048]{1,0:T(8,128)(2,1)}, u32[]{:S(2)}, u32[]{:S(2)}) %collective-permute-start.46) | collective-permute-done | bytes 1048608 | tf_op jit(solution)/shard_map/ppermute | solution.py:912
  426.2 3.7 lsum.4
  429.9 6.2 %collective-permute-done.45.got = bf16[512,2048]{1,0:T(8,128)(2,1)} collective-permute-done((bf16[512,2048]{1,0:T(8,128)(2,1)}, bf16[512,2048]{1,0:T(8,128)(2,1)}, u32[]{:S(2)}, u32[]{:S(2)}) %collective-permute-start.45) | collective-permute-done | bytes 2097184 | tf_op jit(solution)/shard_map/ppermute | solution.py:912
  437.8 4.1 hsum.5
  444.3 4.6 collective-permute-start.50
  448.9 9.4 %igrad.1 = bf16[1024,2048]{1,0:T(8,128)(2,1)} custom-call(s32[13]{0:T(128)S(1)} %copy-done.35, bf16[1024,2048]{1,0:T(8,128)(2,1)S(1)} %bitcast.29, bf16[1024,2048]{1,0:T(8,128)(2,1)S(1)} %bitcast.36, f32[1024,128]{1,0:T(8,128)S(1)} %copy-done.78, bf16[1024,512]{1,0:T(8,128)(2,1)} %fusion.4.refs_0_, bf16[1024,512]{1,0:T(8,128)(2,1)} %collective-permute-done.40.refs_1_, ...), custom_call_target="tpu_custom_call" | custom-call | flops 503316480000 | bytes 1677721600 | tf_op jit(solution)/shard_map/igrad/pallas_call | solution.py:775
  462.5 4.0 lsum.5
  (290 shorter events, 85.2 us)
Async XLA Ops:
  4.6 27.3 %collective-permute-start = (bf16[256,2048]{1,0:T(8,128)(2,1)}, bf16[256,2048]{1,0:T(8,128)(2,1)}, u32[]{:S(2)}, u32[]{:S(2)}) collective-permute-start(bf16[256,2048]{1,0:T(8,128)(2,1)} %pad_maximum_fusion.refs_0_), channel_id=1, source_target_pairs={{0,4},{4,0},{1,5},{5,1},{2,6},{6,2},{3,7},{7,3},{8,12},{12,8},{9,1... | collective-permute-start | bytes 3145736 | tf_op jit(solution)/shard_map/ppermute | solution.py:872
  7.6 24.9 %collective-permute-start.2 = (bf16[256,2048]{1,0:T(8,128)(2,1)}, bf16[256,2048]{1,0:T(8,128)(2,1)}, u32[]{:S(2)}, u32[]{:S(2)}) collective-permute-start(bf16[256,2048]{1,0:T(8,128)(2,1)} %pad_maximum_fusion.refs_0_), channel_id=1, source_target_pairs={{0,16},{16,0},{8,24},{24,8},{1,17},{17,1},{9,25},{25,9},{2,18},{18... | collective-permute-start | bytes 3145736 | tf_op jit(solution)/shard_map/ppermute | solution.py:866
  10.2 46.3 %collective-permute-start.1 = (bf16[256,2048]{1,0:T(8,128)(2,1)}, bf16[256,2048]{1,0:T(8,128)(2,1)}, u32[]{:S(2)}, u32[]{:S(2)}) collective-permute-start(bf16[256,2048]{1,0:T(8,128)(2,1)} %convert_element_type.174.refs_0_), channel_id=1, source_target_pairs={{0,4},{4,0},{1,5},{5,1},{2,6},{6,2},{3,7},{7,3},{8,12},{12,8},{9,1... | collective-permute-start | bytes 3145736 | tf_op jit(solution)/shard_map/ppermute | solution.py:872
  13.3 117.9 %collective-permute-start.12 = (bf16[256,2048]{1,0:T(8,128)(2,1)}, bf16[256,2048]{1,0:T(8,128)(2,1)}, u32[]{:S(2)}, u32[]{:S(2)}) collective-permute-start(bf16[256,2048]{1,0:T(8,128)(2,1)} %bitcast.21.refs_0_), channel_id=1, source_target_pairs={{0,4},{4,0},{1,5},{5,1},{2,6},{6,2},{3,7},{7,3},{8,12},{12,8},{9,1... | collective-permute-start | bytes 3145736 | tf_op jit(solution)/shard_map/ppermute | solution.py:872
  14.9 212.2 %copy-start.33 = (s32[13]{0:T(128)}, s32[13]{0:T(128)S(1)}, u32[]{:S(2)}) copy-start(s32[13]{0:T(128)S(1)} %concatenate.10.meta) | copy-start | bytes 160
  29.6 225.0 %copy-start.76 = (f32[1024,128]{1,0:T(8,128)}, f32[1024,128]{1,0:T(8,128)S(1)}, u32[]{:S(2)}) copy-start(f32[1024,128]{1,0:T(8,128)S(1)} %get-tuple-element.129.st_ref) | copy-start | bytes 1572868
  30.8 57.4 %copy-start.22 = (f32[512,128]{1,0:T(8,128)}, f32[512,128]{1,0:T(8,128)S(1)}, u32[]{:S(2)}) copy-start(f32[512,128]{1,0:T(8,128)S(1)} %get-tuple-element.230.s2) | copy-start | bytes 786436
  30.8 57.3 %copy-start.25 = (f32[512,128]{1,0:T(8,128)}, f32[512,128]{1,0:T(8,128)S(1)}, u32[]{:S(2)}) copy-start(f32[512,128]{1,0:T(8,128)S(1)} %get-tuple-element.231.s1) | copy-start | bytes 786436
  30.8 57.3 %copy-start.28 = (f32[512,128]{1,0:T(8,128)}, f32[512,128]{1,0:T(8,128)S(1)}, u32[]{:S(2)}) copy-start(f32[512,128]{1,0:T(8,128)S(1)} %get-tuple-element.232.cosf) | copy-start | bytes 786436
  32.5 24.0 %collective-permute-start.3 = (bf16[256,2048]{1,0:T(8,128)(2,1)}, bf16[256,2048]{1,0:T(8,128)(2,1)S(1)}, u32[]{:S(2)}, u32[]{:S(2)}) collective-permute-start(bf16[256,2048]{1,0:T(8,128)(2,1)} %collective-permute-done.refs_1_), channel_id=1, source_target_pairs={{0,16},{16,0},{8,24},{24,8},{1,17},{17,1},{9,25},{25,9},{2,18},{18... | collective-permute-start | bytes 3145736 | tf_op jit(solution)/shard_map/ppermute | solution.py:866
  36.4 51.7 %copy-start.17 = (bf16[512,2048]{1,0:T(8,128)(2,1)}, bf16[512,2048]{1,0:T(8,128)(2,1)S(1)}, u32[]{:S(2)}) copy-start(bf16[512,2048]{1,0:T(8,128)(2,1)S(1)} %pack.3.w0.refs_0_.w10) | copy-start | bytes 6291460
  36.5 25.9 %collective-permute-start.4 = (bf16[512,2048]{1,0:T(8,128)(2,1)S(1)}, bf16[512,2048]{1,0:T(8,128)(2,1)S(1)}, u32[]{:S(2)}, u32[]{:S(2)}) collective-permute-start(bf16[512,2048]{1,0:T(8,128)(2,1)S(1)} %pack.3.w0.refs_0_.w10), channel_id=1, source_target_pairs={{0,8},{8,0},{16,24},{24,16},{1,9},{9,1},{17,25},{25,17},{2,10},{10... | collective-permute-start | bytes 6291464 | tf_op jit(solution)/shard_map/ppermute | solution.py:869
  36.5 24.3 %collective-permute-start.5 = (bf16[256,2048]{1,0:T(8,128)(2,1)}, bf16[256,2048]{1,0:T(8,128)(2,1)S(1)}, u32[]{:S(2)}, u32[]{:S(2)}) collective-permute-start(bf16[256,2048]{1,0:T(8,128)(2,1)} %collective-permute-done.2.w1.refs_0_.w11), channel_id=1, source_target_pairs={{0,8},{8,0},{16,24},{24,16},{1,9},{9,1},{17,25},{25,17},{2,10},{10... | collective-permute-start | bytes 3145736 | tf_op jit(solution)/shard_map/ppermute | solution.py:869
  56.5 31.6 %copy-start.43 = (bf16[256,2048]{1,0:T(8,128)(2,1)}, bf16[256,2048]{1,0:T(8,128)(2,1)S(1)}, u32[]{:S(2)}) copy-start(bf16[256,2048]{1,0:T(8,128)(2,1)S(1)} %collective-permute-done.3.w2.refs_1_.w12) | copy-start | bytes 3145732
  56.5 5.8 %collective-permute-start.6 = (bf16[256,2048]{1,0:T(8,128)(2,1)S(1)}, bf16[256,2048]{1,0:T(8,128)(2,1)S(1)}, u32[]{:S(2)}, u32[]{:S(2)}) collective-permute-start(bf16[256,2048]{1,0:T(8,128)(2,1)S(1)} %collective-permute-done.3.w2.refs_1_.w12), channel_id=1, source_target_pairs={{0,8},{8,0},{16,24},{24,16},{1,9},{9,1},{17,25},{25,17},{2,10},{10... | collective-permute-start | bytes 3145736 | tf_op jit(solution)/shard_map/ppermute | solution.py:869
  60.7 54.1 %collective-permute-start.9 = (bf16[512,2048]{1,0:T(8,128)(2,1)}, bf16[512,2048]{1,0:T(8,128)(2,1)}, u32[]{:S(2)}, u32[]{:S(2)}) collective-permute-start(bf16[512,2048]{1,0:T(8,128)(2,1)} %pack.4.w0.w20), channel_id=1, source_target_pairs={{0,8},{8,0},{16,24},{24,16},{1,9},{9,1},{17,25},{25,17},{2,10},{10... | collective-permute-start | bytes 6291464 | tf_op jit(solution)/shard_map/ppermute | solution.py:869
  60.8 119.4 %copy-start.38 = (bf16[256,2048]{1,0:T(8,128)(2,1)}, bf16[256,2048]{1,0:T(8,128)(2,1)S(1)}, u32[]{:S(2)}) copy-start(bf16[256,2048]{1,0:T(8,128)(2,1)S(1)} %collective-permute-done.5.w4.refs_2_.w11) | copy-start | bytes 3145732
  60.8 25.8 %collective-permute-start.7 = (bf16[256,2048]{1,0:T(8,128)(2,1)}, bf16[256,2048]{1,0:T(8,128)(2,1)}, u32[]{:S(2)}, u32[]{:S(2)}) collective-permute-start(bf16[256,2048]{1,0:T(8,128)(2,1)} %convert_element_type.174.refs_0_), channel_id=1, source_target_pairs={{0,16},{16,0},{8,24},{24,8},{1,17},{17,1},{9,25},{25,9},{2,18},{18... | collective-permute-start | bytes 3145736 | tf_op jit(solution)/shard_map/ppermute | solution.py:866
  70.9 71.4 %collective-permute-start.13 = (bf16[1024,1024]{1,0:T(8,128)(2,1)}, bf16[1024,1024]{1,0:T(8,128)(2,1)}, u32[]{:S(2)}, u32[]{:S(2)}) collective-permute-start(bf16[1024,1024]{1,0:T(8,128)(2,1)} %kv.1.kv_ref), channel_id=1, source_target_pairs={{0,4},{1,5},{2,6},{3,7},{8,12},{9,13},{10,14},{11,15},{16,20},{17,... | collective-permute-start | bytes 6291464 | tf_op jit(solution)/shard_map/ppermute | solution.py:929
  86.6 24.9 %collective-permute-start.8 = (bf16[256,2048]{1,0:T(8,128)(2,1)}, bf16[256,2048]{1,0:T(8,128)(2,1)}, u32[]{:S(2)}, u32[]{:S(2)}) collective-permute-start(bf16[256,2048]{1,0:T(8,128)(2,1)} %collective-permute-done.1.refs_1_), channel_id=1, source_target_pairs={{0,16},{16,0},{8,24},{24,8},{1,17},{17,1},{9,25},{25,9},{2,18},{18... | collective-permute-start | bytes 3145736 | tf_op jit(solution)/shard_map/ppermute | solution.py:866
  88.1 28.3 %collective-permute-start.10 = (bf16[256,2048]{1,0:T(8,128)(2,1)}, bf16[256,2048]{1,0:T(8,128)(2,1)}, u32[]{:S(2)}, u32[]{:S(2)}) collective-permute-start(bf16[256,2048]{1,0:T(8,128)(2,1)} %collective-permute-done.7.w1.w21), channel_id=1, source_target_pairs={{0,8},{8,0},{16,24},{24,16},{1,9},{9,1},{17,25},{25,17},{2,10},{10... | collective-permute-start | bytes 3145736 | tf_op jit(solution)/shard_map/ppermute | solution.py:869
  111.5 4.9 %collective-permute-start.11 = (bf16[256,2048]{1,0:T(8,128)(2,1)}, bf16[256,2048]{1,0:T(8,128)(2,1)}, u32[]{:S(2)}, u32[]{:S(2)}) collective-permute-start(bf16[256,2048]{1,0:T(8,128)(2,1)} %collective-permute-done.8.w2.w22), channel_id=1, source_target_pairs={{0,8},{8,0},{16,24},{24,16},{1,9},{9,1},{17,25},{25,17},{2,10},{10... | collective-permute-start | bytes 3145736 | tf_op jit(solution)/shard_map/ppermute | solution.py:869
  114.8 26.0 %collective-permute-start.15 = (bf16[256,2048]{1,0:T(8,128)(2,1)}, bf16[256,2048]{1,0:T(8,128)(2,1)}, u32[]{:S(2)}, u32[]{:S(2)}) collective-permute-start(bf16[256,2048]{1,0:T(8,128)(2,1)} %bitcast.21.refs_0_), channel_id=1, source_target_pairs={{0,16},{16,0},{8,24},{24,8},{1,17},{17,1},{9,25},{25,9},{2,18},{18... | collective-permute-start | bytes 3145736 | tf_op jit(solution)/shard_map/ppermute | solution.py:866
  135.2 21.2 %collective-permute-start.14 = (bf16[512,2048]{1,0:T(8,128)(2,1)}, bf16[512,2048]{1,0:T(8,128)(2,1)}, u32[]{:S(2)}, u32[]{:S(2)}) collective-permute-start(bf16[512,2048]{1,0:T(8,128)(2,1)} %pack.5.refs_2_.w0), channel_id=1, source_target_pairs={{0,8},{8,0},{16,24},{24,16},{1,9},{9,1},{17,25},{25,17},{2,10},{10... | collective-permute-start | bytes 6291464 | tf_op jit(solution)/shard_map/ppermute | solution.py:869
  140.8 29.4 %collective-permute-start.16 = (bf16[256,2048]{1,0:T(8,128)(2,1)}, bf16[256,2048]{1,0:T(8,128)(2,1)}, u32[]{:S(2)}, u32[]{:S(2)}) collective-permute-start(bf16[256,2048]{1,0:T(8,128)(2,1)} %collective-permute-done.12.refs_1_), channel_id=1, source_target_pairs={{0,16},{16,0},{8,24},{24,8},{1,17},{17,1},{9,25},{25,9},{2,18},{18... | collective-permute-start | bytes 3145736 | tf_op jit(solution)/shard_map/ppermute | solution.py:866
  154.6 23.3 %collective-permute-start.17 = (bf16[256,2048]{1,0:T(8,128)(2,1)}, bf16[256,2048]{1,0:T(8,128)(2,1)}, u32[]{:S(2)}, u32[]{:S(2)}) collective-permute-start(bf16[256,2048]{1,0:T(8,128)(2,1)} %collective-permute-done.15.refs_4_.w1), channel_id=1, source_target_pairs={{0,8},{8,0},{16,24},{24,16},{1,9},{9,1},{17,25},{25,17},{2,10},{10... | collective-permute-start | bytes 3145736 | tf_op jit(solution)/shard_map/ppermute | solution.py:869
  154.6 83.0 %collective-permute-start.22 = (bf16[1024,1024]{1,0:T(8,128)(2,1)}, bf16[1024,1024]{1,0:T(8,128)(2,1)}, u32[]{:S(2)}, u32[]{:S(2)}) collective-permute-start(bf16[1024,1024]{1,0:T(8,128)(2,1)} %get-tuple-element.161), channel_id=1, source_target_pairs={{4,0},{5,1},{6,2},{7,3},{12,8},{13,9},{14,10},{15,11},{20,16},{21,... | collective-permute-start | bytes 6291464 | tf_op jit(solution)/shard_map/ppermute | solution.py:932
  165.7 27.3 %collective-permute-start.19 = (bf16[1024,512]{1,0:T(8,128)(2,1)}, bf16[1024,512]{1,0:T(8,128)(2,1)}, u32[]{:S(2)}, u32[]{:S(2)}) collective-permute-start(bf16[1024,512]{1,0:T(8,128)(2,1)} %get-tuple-element.149), channel_id=1, source_target_pairs={{0,1},{3,2},{4,5},{7,6},{8,9},{11,10},{12,13},{15,14},{16,17},{19,... | collective-permute-start | bytes 3145736 | tf_op jit(solution)/shard_map/ppermute | solution.py:837
  170.2 10.1 %collective-permute-start.18 = (bf16[256,2048]{1,0:T(8,128)(2,1)}, bf16[256,2048]{1,0:T(8,128)(2,1)}, u32[]{:S(2)}, u32[]{:S(2)}) collective-permute-start(bf16[256,2048]{1,0:T(8,128)(2,1)} %collective-permute-done.16.refs_5_.w2), channel_id=1, source_target_pairs={{0,8},{8,0},{16,24},{24,16},{1,9},{9,1},{17,25},{25,17},{2,10},{10... | collective-permute-start | bytes 3145736 | tf_op jit(solution)/shard_map/ppermute | solution.py:869
  177.7 49.4 %collective-permute-start.21 = (bf16[1024,2048]{1,0:T(8,128)(2,1)}, bf16[1024,2048]{1,0:T(8,128)(2,1)}, u32[]{:S(2)}, u32[]{:S(2)}) collective-permute-start(bf16[1024,2048]{1,0:T(8,128)(2,1)} %wgrad.6), channel_id=1, source_target_pairs={{0,8},{8,0},{16,24},{24,16},{1,9},{9,1},{17,25},{25,17},{2,10},{10... | collective-permute-start | bytes 12582920 | tf_op jit(solution)/shard_map/ppermute | solution.py:869
  177.9 37.1 %collective-permute-start.20 = (bf16[1024,512]{1,0:T(8,128)(2,1)}, bf16[1024,512]{1,0:T(8,128)(2,1)}, u32[]{:S(2)}, u32[]{:S(2)}) collective-permute-start(bf16[1024,512]{1,0:T(8,128)(2,1)} %get-tuple-element.156), channel_id=1, source_target_pairs={{0,1},{3,2},{4,5},{7,6},{8,9},{11,10},{12,13},{15,14},{16,17},{19,... | collective-permute-start | bytes 3145736 | tf_op jit(solution)/shard_map/ppermute | solution.py:837
  189.9 51.6 %copy-start.4 = (bf16[1024,512]{1,0:T(8,128)(2,1)}, bf16[1024,512]{1,0:T(8,128)(2,1)S(1)}, u32[]{:S(2)}) copy-start(bf16[1024,512]{1,0:T(8,128)(2,1)S(1)} %get-tuple-element.169) | copy-start | bytes 3145732
  195.8 45.8 %collective-permute-start.23 = (bf16[1024,512]{1,0:T(8,128)(2,1)}, bf16[1024,512]{1,0:T(8,128)(2,1)}, u32[]{:S(2)}, u32[]{:S(2)}) collective-permute-start(bf16[1024,512]{1,0:T(8,128)(2,1)} %add_convert_fusion.15), channel_id=1, source_target_pairs={{1,2},{2,1},{5,6},{6,5},{9,10},{10,9},{13,14},{14,13},{17,18},{18,... | collective-permute-start | bytes 3145736 | tf_op jit(solution)/shard_map/ppermute | solution.py:847
  212.0 42.6 %copy-start.74 = (bf16[1024,2048]{1,0:T(8,128)(2,1)}, bf16[1024,2048]{1,0:T(8,128)(2,1)S(1)}, u32[]{:S(2)}) copy-start(bf16[1024,2048]{1,0:T(8,128)(2,1)S(1)} %get-tuple-element.155.du.refs_1_) | copy-start | bytes 12582916
  217.8 48.8 %collective-permute-start.25 = (bf16[1024,512]{1,0:T(8,128)(2,1)}, bf16[1024,512]{1,0:T(8,128)(2,1)}, u32[]{:S(2)}, u32[]{:S(2)}) collective-permute-start(bf16[1024,512]{1,0:T(8,128)(2,1)} %add_convert_fusion.14), channel_id=1, source_target_pairs={{1,2},{2,1},{5,6},{6,5},{9,10},{10,9},{13,14},{14,13},{17,18},{18,... | collective-permute-start | bytes 3145736 | tf_op jit(solution)/shard_map/ppermute | solution.py:847
  219.5 30.1 %collective-permute-start.24 = (bf16[1024,512]{1,0:T(8,128)(2,1)}, bf16[1024,512]{1,0:T(8,128)(2,1)}, u32[]{:S(2)}, u32[]{:S(2)}) collective-permute-start(bf16[1024,512]{1,0:T(8,128)(2,1)} %get-tuple-element.165), channel_id=1, source_target_pairs={{0,1},{3,2},{4,5},{7,6},{8,9},{11,10},{12,13},{15,14},{16,17},{19,... | collective-permute-start | bytes 3145736 | tf_op jit(solution)/shard_map/ppermute | solution.py:837
  245.7 28.7 %collective-permute-start.26 = (bf16[1024,512]{1,0:T(8,128)(2,1)}, bf16[1024,512]{1,0:T(8,128)(2,1)}, u32[]{:S(2)}, u32[]{:S(2)}) collective-permute-start(bf16[1024,512]{1,0:T(8,128)(2,1)} %fusion.refs_0_), channel_id=1, source_target_pairs={{0,1},{3,2},{1,0},{2,3},{4,5},{7,6},{5,4},{6,7},{8,9},{11,10},{9,8... | collective-permute-start | bytes 3145736 | tf_op jit(solution)/shard_map/ppermute | solution.py:837
  252.4 26.4 %collective-permute-start.27 = (bf16[1024,512]{1,0:T(8,128)(2,1)}, bf16[1024,512]{1,0:T(8,128)(2,1)}, u32[]{:S(2)}, u32[]{:S(2)}) collective-permute-start(bf16[1024,512]{1,0:T(8,128)(2,1)} %add_convert_fusion.12), channel_id=1, source_target_pairs={{1,2},{2,1},{5,6},{6,5},{9,10},{10,9},{13,14},{14,13},{17,18},{18,... | collective-permute-start | bytes 3145736 | tf_op jit(solution)/shard_map/ppermute | solution.py:847
  254.1 29.4 %collective-permute-start.28 = (bf16[512,2048]{1,0:T(8,128)(2,1)}, bf16[512,2048]{1,0:T(8,128)(2,1)}, u32[]{:S(2)}, u32[]{:S(2)}) collective-permute-start(bf16[512,2048]{1,0:T(8,128)(2,1)} %get-tuple-element.173), channel_id=1, source_target_pairs={{0,16},{4,20},{8,12},{12,8},{16,0},{20,4},{24,28},{28,24},{1,17},{... | collective-permute-start | bytes 6291464 | tf_op jit(solution)/shard_map/ppermute | solution.py:912
  270.3 39.6 %collective-permute-start.29 = (bf16[1024,512]{1,0:T(8,128)(2,1)}, bf16[1024,512]{1,0:T(8,128)(2,1)}, u32[]{:S(2)}, u32[]{:S(2)}) collective-permute-start(bf16[1024,512]{1,0:T(8,128)(2,1)} %fusion.1.refs_4_), channel_id=1, source_target_pairs={{0,1},{3,2},{1,0},{2,3},{4,5},{7,6},{5,4},{6,7},{8,9},{11,10},{9,8... | collective-permute-start | bytes 3145736 | tf_op jit(solution)/shard_map/ppermute | solution.py:837
  276.9 38.1 %collective-permute-start.31 = (bf16[1024,512]{1,0:T(8,128)(2,1)}, bf16[1024,512]{1,0:T(8,128)(2,1)}, u32[]{:S(2)}, u32[]{:S(2)}) collective-permute-start(bf16[1024,512]{1,0:T(8,128)(2,1)} %add_convert_fusion.10), channel_id=1, source_target_pairs={{1,2},{2,1},{5,6},{6,5},{9,10},{10,9},{13,14},{14,13},{17,18},{18,... | collective-permute-start | bytes 3145736 | tf_op jit(solution)/shard_map/ppermute | solution.py:847
  281.9 58.0 %collective-permute-start.34 = (bf16[1024,512]{1,0:T(8,128)(2,1)}, bf16[1024,512]{1,0:T(8,128)(2,1)}, u32[]{:S(2)}, u32[]{:S(2)}) collective-permute-start(bf16[1024,512]{1,0:T(8,128)(2,1)} %fusion.2.refs_2_), channel_id=1, source_target_pairs={{0,1},{3,2},{1,0},{2,3},{4,5},{7,6},{5,4},{6,7},{8,9},{11,10},{9,8... | collective-permute-start | bytes 3145736 | tf_op jit(solution)/shard_map/ppermute | solution.py:837
  288.4 32.3 %collective-permute-start.30 = (bf16[256,2048]{1,0:T(8,128)(2,1)}, bf16[256,2048]{1,0:T(8,128)(2,1)}, u32[]{:S(2)}, u32[]{:S(2)}) collective-permute-start(bf16[256,2048]{1,0:T(8,128)(2,1)} %get-tuple-element.183), channel_id=1, source_target_pairs={{0,4},{4,0},{8,24},{12,28},{16,20},{20,16},{24,8},{28,12},{1,5},{5... | collective-permute-start | bytes 3145736 | tf_op jit(solution)/shard_map/ppermute | solution.py:912
  309.9 34.4 %copy-start = (bf16[1024,512]{1,0:T(8,128)(2,1)}, bf16[1024,512]{1,0:T(8,128)(2,1)S(1)}, u32[]{:S(2)}) copy-start(bf16[1024,512]{1,0:T(8,128)(2,1)S(1)} %get-tuple-element.201) | copy-start | bytes 3145732
  313.2 31.1 %collective-permute-start.35 = (bf16[1024,512]{1,0:T(8,128)(2,1)}, bf16[1024,512]{1,0:T(8,128)(2,1)}, u32[]{:S(2)}, u32[]{:S(2)}) collective-permute-start(bf16[1024,512]{1,0:T(8,128)(2,1)} %add_convert_fusion.8), channel_id=1, source_target_pairs={{1,2},{2,1},{5,6},{6,5},{9,10},{10,9},{13,14},{14,13},{17,18},{18,... | collective-permute-start | bytes 3145736 | tf_op jit(solution)/shard_map/ppermute | solution.py:847
  318.7 9.4 %collective-permute-start.32 = (f32[13824]{0:T(1024)}, f32[13824]{0:T(1024)}, u32[]{:S(2)}, u32[]{:S(2)}) collective-permute-start(f32[13824]{0:T(1024)} %pad_maximum_fusion.1), channel_id=1, source_target_pairs={{0,8},{8,0},{16,24},{24,16},{1,9},{9,1},{17,25},{25,17},{2,10},{10... | collective-permute-start | bytes 165896 | tf_op jit(solution)/shard_map/ppermute | solution.py:869
  318.7 42.4 %collective-permute-start.37 = (bf16[1024,512]{1,0:T(8,128)(2,1)}, bf16[1024,512]{1,0:T(8,128)(2,1)}, u32[]{:S(2)}, u32[]{:S(2)}) collective-permute-start(bf16[1024,512]{1,0:T(8,128)(2,1)} %fusion.3.refs_6_), channel_id=1, source_target_pairs={{0,1},{3,2},{1,0},{2,3},{4,5},{7,6},{5,4},{6,7},{8,9},{11,10},{9,8... | collective-permute-start | bytes 3145736 | tf_op jit(solution)/shard_map/ppermute | solution.py:837
  329.5 8.9 %collective-permute-start.33 = (f32[13824]{0:T(1024)}, f32[13824]{0:T(1024)}, u32[]{:S(2)}, u32[]{:S(2)}) collective-permute-start(f32[13824]{0:T(1024)} %add.111), channel_id=1, source_target_pairs={{0,16},{16,0},{8,24},{24,8},{1,17},{17,1},{9,25},{25,9},{2,18},{18... | collective-permute-start | bytes 165896 | tf_op jit(solution)/shard_map/ppermute | solution.py:866
  331.0 17.7 %collective-permute-start.36 = (bf16[1024,2048]{1,0:T(8,128)(2,1)}, bf16[1024,2048]{1,0:T(8,128)(2,1)}, u32[]{:S(2)}, u32[]{:S(2)}) collective-permute-start(bf16[1024,2048]{1,0:T(8,128)(2,1)} %wgrad.8), channel_id=1, source_target_pairs={{0,8},{8,0},{16,24},{24,16},{1,9},{9,1},{17,25},{25,17},{2,10},{10... | collective-permute-start | bytes 12582920 | tf_op jit(solution)/shard_map/ppermute | solution.py:869
  342.4 23.0 %collective-permute-start.38 = (bf16[1024,512]{1,0:T(8,128)(2,1)}, bf16[1024,512]{1,0:T(8,128)(2,1)}, u32[]{:S(2)}, u32[]{:S(2)}) collective-permute-start(bf16[1024,512]{1,0:T(8,128)(2,1)} %add_convert_fusion.6), channel_id=1, source_target_pairs={{1,2},{2,1},{5,6},{6,5},{9,10},{10,9},{13,14},{14,13},{17,18},{18,... | collective-permute-start | bytes 3145736 | tf_op jit(solution)/shard_map/ppermute | solution.py:847
  347.5 35.0 %collective-permute-start.40 = (bf16[1024,512]{1,0:T(8,128)(2,1)}, bf16[1024,512]{1,0:T(8,128)(2,1)}, u32[]{:S(2)}, u32[]{:S(2)}) collective-permute-start(bf16[1024,512]{1,0:T(8,128)(2,1)} %fusion.4.refs_0_), channel_id=1, source_target_pairs={{0,1},{3,2},{1,0},{2,3},{4,5},{7,6},{5,4},{6,7},{8,9},{11,10},{9,8... | collective-permute-start | bytes 3145736 | tf_op jit(solution)/shard_map/ppermute | solution.py:837
  357.0 13.2 %collective-permute-start.39 = (bf16[1024,2048]{1,0:T(8,128)(2,1)}, bf16[1024,2048]{1,0:T(8,128)(2,1)}, u32[]{:S(2)}, u32[]{:S(2)}) collective-permute-start(bf16[1024,2048]{1,0:T(8,128)(2,1)} %wgrad.9), channel_id=1, source_target_pairs={{0,8},{8,0},{16,24},{24,16},{1,9},{9,1},{17,25},{25,17},{2,10},{10... | collective-permute-start | bytes 12582920 | tf_op jit(solution)/shard_map/ppermute | solution.py:869
  363.7 23.0 %collective-permute-start.41 = (bf16[1024,512]{1,0:T(8,128)(2,1)}, bf16[1024,512]{1,0:T(8,128)(2,1)}, u32[]{:S(2)}, u32[]{:S(2)}) collective-permute-start(bf16[1024,512]{1,0:T(8,128)(2,1)} %add_convert_fusion.4), channel_id=1, source_target_pairs={{1,2},{2,1},{5,6},{6,5},{9,10},{10,9},{13,14},{14,13},{17,18},{18,... | collective-permute-start | bytes 3145736 | tf_op jit(solution)/shard_map/ppermute | solution.py:847
  368.3 61.6 %collective-permute-start.43 = (bf16[1024,512]{1,0:T(8,128)(2,1)}, bf16[1024,512]{1,0:T(8,128)(2,1)}, u32[]{:S(2)}, u32[]{:S(2)}) collective-permute-start(bf16[1024,512]{1,0:T(8,128)(2,1)} %add_convert_fusion.3.refs_2_), channel_id=1, source_target_pairs={{1,0},{2,3},{5,4},{6,7},{9,8},{10,11},{13,12},{14,15},{17,16},{18,... | collective-permute-start | bytes 3145736 | tf_op jit(solution)/shard_map/ppermute | solution.py:837
  369.5 26.4 %collective-permute-start.42 = (bf16[512,2048]{1,0:T(8,128)(2,1)}, bf16[512,2048]{1,0:T(8,128)(2,1)}, u32[]{:S(2)}, u32[]{:S(2)}) collective-permute-start(bf16[512,2048]{1,0:T(8,128)(2,1)} %get-tuple-element.204), channel_id=1, source_target_pairs={{0,16},{4,20},{8,12},{12,8},{16,0},{20,4},{24,28},{28,24},{1,17},{... | collective-permute-start | bytes 6291464 | tf_op jit(solution)/shard_map/ppermute | solution.py:912
  385.1 25.1 %collective-permute-start.44 = (bf16[1024,512]{1,0:T(8,128)(2,1)}, bf16[1024,512]{1,0:T(8,128)(2,1)}, u32[]{:S(2)}, u32[]{:S(2)}) collective-permute-start(bf16[1024,512]{1,0:T(8,128)(2,1)} %add_convert_fusion.2), channel_id=1, source_target_pairs={{1,2},{2,1},{5,6},{6,5},{9,10},{10,9},{13,14},{14,13},{17,18},{18,... | collective-permute-start | bytes 3145736 | tf_op jit(solution)/shard_map/ppermute | solution.py:847
  389.5 59.4 %collective-permute-start.48 = (bf16[1024,512]{1,0:T(8,128)(2,1)}, bf16[1024,512]{1,0:T(8,128)(2,1)}, u32[]{:S(2)}, u32[]{:S(2)}) collective-permute-start(bf16[1024,512]{1,0:T(8,128)(2,1)} %add_convert_fusion.1.refs_4_), channel_id=1, source_target_pairs={{1,0},{2,3},{5,4},{6,7},{9,8},{10,11},{13,12},{14,15},{17,16},{18,... | collective-permute-start | bytes 3145736 | tf_op jit(solution)/shard_map/ppermute | solution.py:837
  399.9 26.3 %collective-permute-start.46 = (bf16[256,2048]{1,0:T(8,128)(2,1)}, bf16[256,2048]{1,0:T(8,128)(2,1)}, u32[]{:S(2)}, u32[]{:S(2)}) collective-permute-start(bf16[256,2048]{1,0:T(8,128)(2,1)} %get-tuple-element.212), channel_id=1, source_target_pairs={{0,4},{4,0},{8,24},{12,28},{16,20},{20,16},{24,8},{28,12},{1,5},{5... | collective-permute-start | bytes 3145736 | tf_op jit(solution)/shard_map/ppermute | solution.py:912
  401.5 34.6 %collective-permute-start.45 = (bf16[512,2048]{1,0:T(8,128)(2,1)}, bf16[512,2048]{1,0:T(8,128)(2,1)}, u32[]{:S(2)}, u32[]{:S(2)}) collective-permute-start(bf16[512,2048]{1,0:T(8,128)(2,1)} %get-tuple-element.209), channel_id=1, source_target_pairs={{0,16},{4,20},{8,12},{12,8},{16,0},{20,4},{24,28},{28,24},{1,17},{... | collective-permute-start | bytes 6291464 | tf_op jit(solution)/shard_map/ppermute | solution.py:912
  413.0 35.9 %collective-permute-start.49 = (bf16[1024,512]{1,0:T(8,128)(2,1)}, bf16[1024,512]{1,0:T(8,128)(2,1)}, u32[]{:S(2)}, u32[]{:S(2)}) collective-permute-start(bf16[1024,512]{1,0:T(8,128)(2,1)} %add_convert_fusion.refs_6_), channel_id=1, source_target_pairs={{1,0},{2,3},{5,4},{6,7},{9,8},{10,11},{13,12},{14,15},{17,16},{18,... | collective-permute-start | bytes 3145736 | tf_op jit(solution)/shard_map/ppermute | solution.py:837
  436.1 6.1 %collective-permute-start.47 = (f32[13824]{0:T(1024)}, f32[13824]{0:T(1024)}, u32[]{:S(2)}, u32[]{:S(2)}) collective-permute-start(f32[13824]{0:T(1024)} %add.112), channel_id=1, source_target_pairs={{0,4},{4,0},{1,5},{5,1},{2,6},{6,2},{3,7},{7,3},{8,12},{12,8},{9,1... | collective-permute-start | bytes 165896 | tf_op jit(solution)/shard_map/ppermute | solution.py:872
  441.9 20.6 %collective-permute-start.51 = (bf16[256,2048]{1,0:T(8,128)(2,1)}, bf16[256,2048]{1,0:T(8,128)(2,1)}, u32[]{:S(2)}, u32[]{:S(2)}) collective-permute-start(bf16[256,2048]{1,0:T(8,128)(2,1)} %get-tuple-element.220), channel_id=1, source_target_pairs={{0,4},{4,0},{8,24},{12,28},{16,20},{20,16},{24,8},{28,12},{1,5},{5... | collective-permute-start | bytes 3145736 | tf_op jit(solution)/shard_map/ppermute | solution.py:912
  444.3 16.6 %collective-permute-start.50 = (f32[8192]{0:T(1024)}, f32[8192]{0:T(1024)}, u32[]{:S(2)}, u32[]{:S(2)}) collective-permute-start(f32[8192]{0:T(1024)} %slice.40), channel_id=1, source_target_pairs={{0,1},{1,0},{2,3},{3,2},{4,5},{5,4},{6,7},{7,6},{8,9},{9,8},{10,11... | collective-permute-start | bytes 98312 | tf_op jit(solution)/shard_map/ppermute | solution.py:945
  462.3 5.2 %collective-permute-start.52 = (f32[8192]{0:T(1024)}, f32[8192]{0:T(1024)}, u32[]{:S(2)}, u32[]{:S(2)}) collective-permute-start(f32[8192]{0:T(1024)} %add.122), channel_id=1, source_target_pairs={{0,2},{2,0},{1,3},{3,1},{4,6},{6,4},{5,7},{7,5},{8,10},{10,8},{9,1... | collective-permute-start | bytes 98312 | tf_op jit(solution)/shard_map/ppermute | solution.py:947
  (76 other events, 807.3 us)
